TPU v7x, 32 devices: a whole 2x2x4 slice. The times are simulated.
32 devices in a mesh: fsdp: 4 (over z), ctx: 2 (over x), tp: 4 (over y, core).
Axes of the slice: x: 2, y: 2, z: 4, core: 2. Of those that a mesh axis runs over, the one named last changes fastest.
Arguments:
- layer_input: bfloat16 [8192, 4096], P(('fsdp', 'ctx'), 'tp'), may hold values from -6 to 6
- attn_gain: bfloat16 [4096], P('tp'), may hold values from 0.099609375 to 1.8984375
- qkv_weight: bfloat16 [4096, 3, 4096], P('fsdp', None, 'tp'), may hold values from -1 to 1
- out_weight: bfloat16 [4096, 4096], P('tp', 'fsdp'), may hold values from -0.75 to 0.75
- ffn_gain: bfloat16 [4096], P('tp'), may hold values from 0.099609375 to 1.8984375
- gate_up_weight: bfloat16 [4096, 2, 11008], P('fsdp', None, 'tp'), may hold values from -0.09375 to 0.09375
- down_weight: bfloat16 [11008, 4096], P('tp', 'fsdp'), may hold values from -0.0546875 to 0.0546875
- cotangent: bfloat16 [8192, 4096], P(('fsdp', 'ctx'), 'tp'), may hold values from -6 to 6
Outputs:
- layer_output: bfloat16 [8192, 4096], P(('fsdp', 'ctx'), 'tp')
- grad_input: float32 [8192, 4096], P(('fsdp', 'ctx'), 'tp')
- grad_attn_gain: float32 [4096], P('tp')
- grad_qkv: float32 [4096, 3, 4096], P(('fsdp', 'ctx'), None, 'tp')
- grad_out_weight: float32 [4096, 4096], P('tp', ('fsdp', 'ctx'))
- grad_ffn_gain: float32 [4096], P('tp')
- grad_gate_up: float32 [4096, 2, 11008], P(('fsdp', 'ctx'), None, 'tp')
- grad_down: float32 [11008, 4096], P('tp', ('fsdp', 'ctx'))
All inputs are finite; a program needn't handle non-finite values.
Results may differ from a plain program's by a relative error of at most 0.018.
Values may be sent and summed in bfloat16 or wider, within the bound.
No kernel may reach another device: no remote copies, remote signals or barrier semaphores. Data moves between devices by JAX's collectives and lax.ppermute only.
A program may use at most 384 MiB of HBM per device.

v0:
```python
import math

import jax
import jax.numpy as jnp
from jax import lax
from jax.sharding import PartitionSpec as P

D = 4096
HD = 128


rms_epsilon = 1e-05
masked_score = -1e30


def rotate(values, positions, direction):
    half_width = HD // 2
    inv_freq = jnp.exp(-math.log(10000.0) * jnp.arange(half_width, dtype=jnp.float32) * 2.0 / HD)
    angles = positions.astype(jnp.float32)[:, None] * inv_freq[None, :]
    cosine = jnp.cos(angles)[:, None, :]
    sine_table = direction * jnp.sin(angles)[:, None, :]
    shaped = values.reshape(values.shape[0], -1, 2, half_width)
    lower_half = shaped[:, :, 0, :]
    upper_half = shaped[:, :, 1, :]
    turned = jnp.stack(
        [
            lower_half * cosine - upper_half * sine_table,
            upper_half * cosine + lower_half * sine_table,
        ],
        axis=2,
    )
    return turned.reshape(values.shape)


def row_total(values):
    return lax.psum(values, "tp")


def full_rows(values):
    return lax.all_gather(values, "tp", axis=1, tiled=True)


def shard_sum(values):
    return lax.psum_scatter(values, "tp", scatter_dimension=1, tiled=True)


def to_heads(values):
    return lax.all_to_all(values, "ctx", split_axis=2, concat_axis=0, tiled=True)


def to_tokens(values):
    return lax.all_to_all(values, "ctx", split_axis=0, concat_axis=2, tiled=True)


def contract_rows(left, right):
    return lax.dot_general(
        left, right, (((0,), (0,)), ((), ())), preferred_element_type=jnp.float32
    )


def contract_cols(left, right):
    return lax.dot_general(
        left, right, (((1,), (1,)), ((), ())), preferred_element_type=jnp.float32
    )


def in_proj(full_input, weight):
    row_count = full_input.shape[0]
    flat_cols = weight.shape[1] * weight.shape[2]
    shard_piece = lax.all_gather(weight, "fsdp", axis=0, tiled=True)
    running = jnp.dot(
        full_input,
        shard_piece.reshape(shard_piece.shape[0], flat_cols),
        preferred_element_type=jnp.float32,
    )
    return running.reshape(row_count, weight.shape[1], weight.shape[2])


def in_proj_back(grads, weight):
    flat_grads = grads.reshape(grads.shape[0], -1)
    shard_piece = lax.all_gather(weight, "fsdp", axis=0, tiled=True)
    return contract_cols(flat_grads, shard_piece.reshape(shard_piece.shape[0], -1))


def out_proj(inner, weight):
    return jnp.dot(
        inner,
        lax.all_gather(weight, "fsdp", axis=1, tiled=True),
        preferred_element_type=jnp.float32,
    )


def out_proj_back(full_grad, weight):
    return contract_cols(full_grad, lax.all_gather(weight, "fsdp", axis=1, tiled=True))


def reduce_grads(first_grad, second_grad):
    reduced = (
        lax.psum_scatter(
            first_grad.astype(jnp.bfloat16), ("fsdp", "ctx"), scatter_dimension=0, tiled=True
        ).astype(jnp.float32),
        lax.psum_scatter(
            second_grad.astype(jnp.bfloat16), ("fsdp", "ctx"), scatter_dimension=0, tiled=True
        ).astype(jnp.float32),
    )
    return reduced


def score_block(query_heads, key_heads, first_row, block_len):
    query_block = lax.dynamic_slice_in_dim(query_heads, first_row, block_len, 0)
    scores = jnp.einsum("qhd,khd->hqk", query_block, key_heads, preferred_element_type=jnp.float32)
    scores = scores * (1.0 / math.sqrt(HD))
    key_index = jnp.arange(key_heads.shape[0], dtype=jnp.int32)
    query_index = first_row + jnp.arange(block_len, dtype=jnp.int32)
    allowed = key_index[None, :] <= query_index[:, None]
    return (query_block, jnp.where(allowed[None, :, :], scores, masked_score))


def attend_forward(qkv_heads):
    seq_len = qkv_heads.shape[0]
    head_count = qkv_heads.shape[2] // HD
    block_len = min(512, seq_len)
    block_count = seq_len // block_len
    query_heads = qkv_heads[:, 0].reshape(seq_len, head_count, HD)
    key_heads = qkv_heads[:, 1].reshape(seq_len, head_count, HD)
    value_heads = qkv_heads[:, 2].reshape(seq_len, head_count, HD)

    def one_block(block_index):
        query_block, scores = score_block(
            query_heads, key_heads, block_index * block_len, block_len
        )
        row_max = jnp.max(scores, axis=-1, keepdims=True)
        expo_vals = jnp.exp(scores - row_max)
        row_sums = jnp.sum(expo_vals, axis=-1, keepdims=True)
        soft = (expo_vals / row_sums).astype(jnp.bfloat16)
        mixed = jnp.einsum("hqk,khd->qhd", soft, value_heads, preferred_element_type=jnp.float32)
        return (mixed.astype(jnp.bfloat16), (row_max + jnp.log(row_sums))[:, :, 0])

    head_outs, log_norms = lax.map(one_block, jnp.arange(block_count, dtype=jnp.int32))
    return (head_outs.reshape(seq_len, 1, head_count * HD), log_norms)


def attend_backward(qkv_heads, log_norms, grad_out):
    seq_len = qkv_heads.shape[0]
    head_count = qkv_heads.shape[2] // HD
    block_len = min(512, seq_len)
    block_count = seq_len // block_len
    score_scale = 1.0 / math.sqrt(HD)
    query_heads = qkv_heads[:, 0].reshape(seq_len, head_count, HD)
    key_heads = qkv_heads[:, 1].reshape(seq_len, head_count, HD)
    value_heads = qkv_heads[:, 2].reshape(seq_len, head_count, HD)
    grad_heads = grad_out.reshape(seq_len, head_count, HD)

    def one_block(running_grads, block_item):
        block_index, block_norms = block_item
        first_row = block_index * block_len
        query_block, scores = score_block(query_heads, key_heads, first_row, block_len)
        probs_full = jnp.exp(scores - block_norms[:, :, None])
        soft = probs_full.astype(jnp.bfloat16)
        grad_block = lax.dynamic_slice_in_dim(grad_heads, first_row, block_len, 0)
        grad_probs = jnp.einsum(
            "qhd,khd->hqk", grad_block, value_heads, preferred_element_type=jnp.float32
        )
        weighted = jnp.sum(probs_full * grad_probs, axis=-1, keepdims=True)
        grad_scores = (probs_full * (grad_probs - weighted)).astype(jnp.bfloat16)
        query_grad = (
            jnp.einsum("hqk,khd->qhd", grad_scores, key_heads, preferred_element_type=jnp.float32)
            * score_scale
        )
        key_grad = (
            running_grads[0]
            + jnp.einsum(
                "hqk,qhd->khd", grad_scores, query_block, preferred_element_type=jnp.float32
            )
            * score_scale
        )
        value_grad = running_grads[1] + jnp.einsum(
            "hqk,qhd->khd", soft, grad_block, preferred_element_type=jnp.float32
        )
        return ((key_grad, value_grad), query_grad)

    zero_grads = jnp.zeros((seq_len, head_count, HD), jnp.float32)
    key_value, query_grads = lax.scan(
        one_block, (zero_grads, zero_grads), (jnp.arange(block_count, dtype=jnp.int32), log_norms)
    )
    flat_width = head_count * HD
    return (
        query_grads.reshape(seq_len, flat_width),
        key_value[0].reshape(seq_len, flat_width),
        key_value[1].reshape(seq_len, flat_width),
    )


def body(
    layer_input, attn_gain, qkv_weight, out_weight, ffn_gain, gate_up_weight, down_weight, cotangent
):
    row_count = layer_input.shape[0]
    input_float = layer_input.astype(jnp.float32)
    attn_scale = attn_gain.astype(jnp.float32)
    ffn_scale = ffn_gain.astype(jnp.float32)
    rms_one = lax.rsqrt(row_total(jnp.sum(input_float * input_float, axis=-1)) / D + rms_epsilon)[
        :, None
    ]
    normed_attn = (input_float * rms_one * attn_scale).astype(jnp.bfloat16)
    attn_full = full_rows(normed_attn)
    proj = in_proj(attn_full, qkv_weight)
    positions = lax.axis_index("ctx") * row_count + jnp.arange(row_count, dtype=jnp.int32)
    qkv_local = jnp.stack(
        [rotate(proj[:, 0], positions, 1.0), rotate(proj[:, 1], positions, 1.0), proj[:, 2]], axis=1
    ).astype(jnp.bfloat16)
    qkv_heads = to_heads(qkv_local)
    seq_len = qkv_heads.shape[0]
    head_outs, log_norms = attend_forward(qkv_heads)
    attn_tokens = to_tokens(head_outs)[:, 0, :]
    resid = input_float + shard_sum(out_proj(attn_tokens, out_weight))
    rms_two = lax.rsqrt(row_total(jnp.sum(resid * resid, axis=-1)) / D + rms_epsilon)[:, None]
    normed_ffn = (resid * rms_two * ffn_scale).astype(jnp.bfloat16)
    ffn_full = full_rows(normed_ffn)
    gate_up = in_proj(ffn_full, gate_up_weight)
    gate = gate_up[:, 0]
    up_value = gate_up[:, 1]
    sigma = jax.nn.sigmoid(gate)
    hidden = (gate * sigma * up_value).astype(jnp.bfloat16)
    layer_output = (resid + shard_sum(out_proj(hidden, down_weight))).astype(jnp.bfloat16)
    cotan_full = full_rows(cotangent)
    grad_hidden = out_proj_back(cotan_full, down_weight)
    down_grad_t = contract_rows(cotan_full, hidden)
    grad_gu = jnp.stack(
        [grad_hidden * up_value * sigma * (1.0 + gate * (1.0 - sigma)), grad_hidden * gate * sigma],
        axis=1,
    ).astype(jnp.bfloat16)
    grad_nffn = shard_sum(in_proj_back(grad_gu, gate_up_weight))
    gate_up_grad = contract_rows(ffn_full, grad_gu.reshape(row_count, -1)).reshape(D, 2, -1)
    ffn_reduced = reduce_grads(gate_up_grad, down_grad_t)
    ffn_term = grad_nffn * ffn_scale
    ffn_dot = row_total(jnp.sum(ffn_term * resid, axis=-1))[:, None]
    grad_resid = (
        cotangent.astype(jnp.float32) + rms_two * ffn_term - resid * rms_two**3 * ffn_dot / D
    )
    ffn_gain_part = jnp.sum(grad_nffn * resid * rms_two, axis=0)
    grad_branch = grad_resid.astype(jnp.bfloat16)
    branch_full = full_rows(grad_branch)
    grad_attn_tokens = out_proj_back(branch_full, out_weight).astype(jnp.bfloat16)
    out_grad_t = contract_rows(branch_full, attn_tokens)
    grad_out_heads = to_heads(grad_attn_tokens[:, None, :])
    query_grad, key_grad, value_grad = attend_backward(qkv_heads, log_norms, grad_out_heads)
    all_positions = jnp.arange(seq_len, dtype=jnp.int32)
    grad_proj_heads = jnp.stack(
        [
            rotate(query_grad, all_positions, -1.0),
            rotate(key_grad, all_positions, -1.0),
            value_grad,
        ],
        axis=1,
    ).astype(jnp.bfloat16)
    grad_proj = to_tokens(grad_proj_heads)
    grad_nattn = shard_sum(in_proj_back(grad_proj, qkv_weight))
    qkv_grad = contract_rows(attn_full, grad_proj.reshape(row_count, -1)).reshape(D, 3, -1)
    attn_reduced = reduce_grads(qkv_grad, out_grad_t)
    attn_term = grad_nattn * attn_scale
    attn_dot = row_total(jnp.sum(attn_term * input_float, axis=-1))[:, None]
    grad_input = grad_resid + rms_one * attn_term - input_float * rms_one**3 * attn_dot / D
    attn_gain_part = jnp.sum(grad_nattn * input_float * rms_one, axis=0)
    gain_grads = lax.psum((attn_gain_part, ffn_gain_part), ("fsdp", "ctx"))
    return (
        layer_output,
        grad_input,
        gain_grads[0],
        attn_reduced[0],
        attn_reduced[1].T,
        gain_grads[1],
        ffn_reduced[0],
        ffn_reduced[1].T,
    )


def solution(mesh):
    return jax.shard_map(
        body,
        mesh=mesh,
        in_specs=(
            P(("fsdp", "ctx"), "tp"),
            P("tp"),
            P("fsdp", None, "tp"),
            P("tp", "fsdp"),
            P("tp"),
            P("fsdp", None, "tp"),
            P("tp", "fsdp"),
            P(("fsdp", "ctx"), "tp"),
        ),
        out_specs=(
            P(("fsdp", "ctx"), "tp"),
            P(("fsdp", "ctx"), "tp"),
            P("tp"),
            P(("fsdp", "ctx"), None, "tp"),
            P("tp", ("fsdp", "ctx")),
            P("tp"),
            P(("fsdp", "ctx"), None, "tp"),
            P("tp", ("fsdp", "ctx")),
        ),
        check_vma=False,
    )
```

profile of v0, /device:TPU:0, one launch (start us, length us, event | category | flops | bytes accessed | tf_op | source)
XLA Modules:
  0.0 4552.9 jit_solution(1638973924265543728)
XLA Ops:
  23.1 8.7 copy.70
  33.3 48.4 %all-gather.9.cloned.1.call-done = bf16[1024,4096]{1,0:T(8,128)(2,1)} async-done(((bf16[1024,1024]{1,0:T(8,128)(2,1)}), bf16[1024,4096]{1,0:T(8,128)(2,1)}) %all-gather.9.cloned.1.call-update) | async-done | bytes 8388624 | tf_op jit(solution)/shard_map/all_gather | solution.py:40
  81.8 427.4 %all-gather.11.cloned.1.call-done = bf16[4096,3,1024]{0,2,1:T(8,128)(2,1)} async-done(((bf16[1024,3,1024]{0,2,1:T(8,128)(2,1)}), bf16[4096,3,1024]{0,2,1:T(8,128)(2,1)}) %all-gather.11.cloned.1.call-update) | async-done | bytes 25165840 | tf_op jit(solution)/shard_map/all_gather | solution.py:70
  509.1 32.0 fusion.29
  550.8 11.6 copy.71
  570.2 92.0 %all-to-all-done = bf16[1024,3,1024]{0,1,2:T(4,128)(2,1)} async-done(((bf16[1024,3,1024]{0,1,2:T(4,128)(2,1)}), bf16[1024,3,1024]{0,1,2:T(4,128)(2,1)}, u32[]{:S(2)}, u32[]{:S(2)}) %all-to-all-start) | async-done | bytes 6291488 | tf_op jit(solution)/shard_map/all_to_all | solution.py:48
  662.2 8.7 copy.72
  670.9 8.9 copy.73
  705.8 72.8 %while.27 = (s32[]{:T(128)}, bf16[4,512,4,128]{3,2,1,0:T(4,128)(2,1)}, f32[4,4,512]{2,1,0:T(4,128)}, s32[4]{0:T(128)S(1)}, bf16[2048,4,128]{2,0,1:T(8,128)(2,1)}...) while((s32[]{:T(128)}, ...), condition=%wide.region_5.6_spmd, body=%wide.region_2.5_spmd.sunk | while | flops 2199124480 | bytes 69275856 | solution.py:139
  778.6 12.7 reshape.256
  791.9 15.4 reduce
  811.1 28.5 all_to_all.63
  847.8 16.2 fusion.52
  864.7 122.9 %reduce-scatter.9.cloned.1.call-done = f32[1024,1024]{1,0:T(8,128)} async-done(((f32[1024,4096]{1,0:T(8,128)}), f32[1024,1024]{1,0:T(8,128)}) %reduce-scatter.9.cloned.1.call-update) | async-done | bytes 4194320 | tf_op jit(solution)/shard_map/reduce_scatter | solution.py:44
  1006.4 733.5 %all-gather.17.cloned.1.call-done = bf16[4096,2,2752]{0,2,1:T(8,128)(2,1)} async-done(((bf16[1024,2,2752]{0,2,1:T(8,128)(2,1)}), bf16[4096,2,2752]{0,2,1:T(8,128)(2,1)}) %all-gather.17.cloned.1.call-update) | async-done | bytes 45088784 | tf_op jit(solution)/shard_map/all_gather | solution.py:70
  1739.9 58.6 %all-gather.15.cloned.1.call-done = bf16[1024,4096]{1,0:T(8,128)(2,1)} async-done(((bf16[1024,1024]{1,0:T(8,128)(2,1)}), bf16[1024,4096]{1,0:T(8,128)(2,1)}) %all-gather.15.cloned.1.call-update) | async-done | bytes 8388624 | tf_op jit(solution)/shard_map/all_gather | solution.py:40
  1798.5 55.8 %fusion.27 = f32[1024,2,2752]{0,2,1:T(8,128)} fusion(bf16[4096,2,2752]{0,2,1:T(8,128)(2,1)} %all-gather.17.cloned.1.call-done, bf16[1024,4096]{1,0:T(8,128)(2,1)} %all-gather.15.cloned.1.call-done), kind=kOutput, calls=%fused_computation.41 | convolution fusion | flops 46170898432 | bytes 76021760 | tf_op jit(solution)/shard_map/dot_general | solution.py:71
  1858.4 384.2 %all-gather.19.cloned.1.call-done = bf16[2752,4096]{1,0:T(8,128)(2,1)} async-done(((bf16[2752,1024]{1,0:T(8,128)(2,1)}), bf16[2752,4096]{1,0:T(8,128)(2,1)}) %all-gather.19.cloned.1.call-update) | async-done | bytes 22544400 | tf_op jit(solution)/shard_map/all_gather | solution.py:88
  2242.7 36.9 multiply_bitcast_fusion.1
  2279.5 58.5 %convolution_bitcast_fusion = f32[1024,4096]{1,0:T(8,128)} fusion(bf16[4096,2,2752]{0,2,1:T(8,128)(2,1)} %all-gather.17.cloned.1.call-done, bf16[1024,1,2752]{0,2,1:T(8,128)(2,1)} %get-tuple-element.270, bf16[1024,1,2752]{0,2,1:T(8,128)(2,1)} %get-tuple-element.269), kind=kOutput, calls=%fused_computation.63 | convolution fusion | flops 46176534528 | bytes 73138176 | tf_op jit(solution)/shard_map/dot_general | solution.py:62
  2338.1 12.0 multiply_convert_fusion.1
  2353.5 31.8 fusion.53
  2385.4 77.3 %reduce-scatter.13.cloned.1.call-done = f32[1024,1024]{1,0:T(8,128)} async-done(((f32[1024,4096]{1,0:T(8,128)}), f32[1024,1024]{1,0:T(8,128)}) %reduce-scatter.13.cloned.1.call-update) | async-done | bytes 4194320 | tf_op jit(solution)/shard_map/reduce_scatter | solution.py:44
  2473.5 117.8 %reduce-scatter.11.cloned.1.call-done = f32[1024,1024]{1,0:T(8,128)} async-done(((f32[1024,4096]{1,0:T(8,128)}), f32[1024,1024]{1,0:T(8,128)}) %reduce-scatter.11.cloned.1.call-update) | async-done | bytes 4194320 | tf_op jit(solution)/shard_map/reduce_scatter | solution.py:44
  2598.8 31.1 fusion.31
  2633.2 23.9 all-gather.23.cloned.1.call-done
  2657.2 13.7 convert_bitcast_fusion.2
  2678.4 13.0 reduce.1
  2697.8 15.1 convolution_convert_fusion.3
  2712.9 24.9 all-to-all-done.2
  2753.4 356.6 %while.28 = (s32[]{:T(128)}, f32[2048,4,128]{0,2,1:T(8,128)}, f32[2048,4,128]{0,2,1:T(8,128)}, f32[4,512,4,128]{1,0,3,2:T(4,128)}, s32[4]{0:T(128)S(1)}, /*index...) while((s32[]{:T(128)}, f32[2048,4,128]{0,2,1:T(8,128)}, ...), condition=%wide.region_15.16_spmd.clone, body=%wide.region_13.15_spmd.clone.sunk | while | flops 5438175744 | bytes 199291264 | solution.py:183
  2755.1 9.5 fusion.112
  2767.1 12.6 multiply_reduce_fusion.5
  2779.8 15.6 multiply_convert_fusion.4
  2802.9 11.4 bitcast_add_fusion.5
  2820.0 21.1 dynamic_update_slice.20
  2842.3 9.3 fusion.112
  2854.2 12.8 multiply_reduce_fusion.5
  2867.0 15.1 multiply_convert_fusion.4
  2882.1 9.1 bitcast_add_fusion.4
  2891.3 12.4 bitcast_add_fusion.5
  2909.4 21.0 dynamic_update_slice.20
  2931.7 9.4 fusion.112
  2943.7 12.6 multiply_reduce_fusion.5
  2956.3 15.4 multiply_convert_fusion.4
  2971.8 8.9 bitcast_add_fusion.4
  2980.7 12.8 bitcast_add_fusion.5
  2999.2 21.1 dynamic_update_slice.20
  3021.5 9.3 fusion.112
  3033.4 12.8 multiply_reduce_fusion.5
  3046.2 15.4 multiply_convert_fusion.4
  3061.6 8.7 bitcast_add_fusion.4
  3070.3 12.8 bitcast_add_fusion.5
  3088.8 21.1 dynamic_update_slice.20
  3127.4 14.1 copy.90
  3141.5 103.2 %all_to_all.64 = bf16[2048,3,512]{2,1,0:T(4,128)(2,1)} all-to-all(bf16[2048,3,512]{2,1,0:T(4,128)(2,1)} %copy.90), channel_id=1, replica_groups=mesh['fsdp'=4,'ctx'=2,'tp'=4] {'ctx'}, dimensions={0} | all-to-all | bytes 12582912 | tf_op jit(solution)/shard_map/all_to_all | solution.py:52
  3244.7 13.0 copy.91
  3257.6 33.8 fusion.54
  3291.5 55.4 %convolution_convert_fusion = bf16[4096,2,2752]{0,2,1:T(8,128)(2,1)} fusion(bf16[1024,4096]{1,0:T(8,128)(2,1)} %all-gather.15.cloned.1.call-done, bf16[1024,1,2752]{0,2,1:T(8,128)(2,1)} %get-tuple-element.270, bf16[1024,1,2752]{0,2,1:T(8,128)(2,1)} %get-tuple-element.269), kind=kOutput, calls=%fused_computation.43 | convolution fusion | flops 46215987200 | bytes 64749568 | tf_op jit(solution)/shard_map/dot_general | solution.py:56
  3347.0 34.7 convolution_convert_fusion.2
  3392.7 25.0 reduce-scatter.15.cloned.1.call-done
  3421.2 22.7 all-reduce
  3455.5 677.6 %reduce-scatter.21.cloned.1.call-done = bf16[512,2,2752]{0,2,1:T(8,128)(2,1)} async-done(((bf16[4096,2,2752]{0,2,1:T(8,128)(2,1)}), bf16[512,2,2752]{0,2,1:T(8,128)(2,1)}) %reduce-scatter.21.cloned.1.call-update) | async-done | bytes 5636112 | tf_op jit(solution)/shard_map/reduce_scatter | solution.py:99
  4141.7 398.9 %reduce-scatter.17.cloned.1.call-done = bf16[512,3,1024]{2,0,1:T(8,128)(2,1)} async-done(((bf16[4096,3,1024]{2,0,1:T(8,128)(2,1)}), bf16[512,3,1024]{2,0,1:T(8,128)(2,1)}) %reduce-scatter.17.cloned.1.call-update) | async-done | bytes 3145744 | tf_op jit(solution)/shard_map/reduce_scatter | solution.py:99
  (259 shorter events, 322.0 us)
Async XLA Ops:
  7.2 74.6 %all-gather.9.cloned.1.call-start = ((), (), s32[]{:S(2)}) async-start(), calls=%async_computation.12 | async-start | bytes 10485760 | tf_op jit(solution)/shard_map/all_gather | solution.py:40
  7.9 15.1 copy-start.19
  19.0 0.6 copy-start.17
  23.0 486.1 %all-gather.11.cloned.1.call-start = ((), (), s32[]{:S(2)}) async-start(), calls=%async_computation.13 | async-start | bytes 31457280 | tf_op jit(solution)/shard_map/all_gather | solution.py:70
  545.9 1.6 copy-start.9
  562.4 99.9 %all-to-all-start = ((bf16[1024,3,1024]{0,1,2:T(4,128)(2,1)}), bf16[1024,3,1024]{0,1,2:T(4,128)(2,1)}, u32[]{:S(2)}, u32[]{:S(2)}) async-start(bf16[1024,3,1024]{0,1,2:T(4,128)(2,1)} %copy.71), calls=%async_computation | async-start | bytes 16777216 | tf_op jit(solution)/shard_map/all_to_all | solution.py:48
  569.4 278.4 %all-gather.13.cloned.1.call-start = ((), (), s32[]{:S(2)}) async-start(), calls=%async_computation.14 | async-start | bytes 10485760 | tf_op jit(solution)/shard_map/all_gather | solution.py:88
  570.2 417.4 %reduce-scatter.9.cloned.1.call-start = ((), (), s32[]{:S(2)}) async-start(), calls=%async_computation.15 | async-start | bytes 20971520 | tf_op jit(solution)/shard_map/reduce_scatter | solution.py:44
  712.1 4.4 copy-start.2
  730.3 4.4 copy-start.2
  748.5 4.4 copy-start.2
  766.7 4.4 copy-start.2
  778.6 28.8 copy-start
  864.0 0.7 copy-start.26
  864.0 123.6 %copy-start.6 = (bf16[1024,1024]{1,0:T(8,128)(2,1)S(1)}, bf16[1024,1024]{1,0:T(8,128)(2,1)}, u32[]{:S(2)}) copy-start(bf16[1024,1024]{1,0:T(8,128)(2,1)} %param.12) | copy-start | bytes 6291460
  864.1 875.8 %all-gather.17.cloned.1.call-start = ((), (), s32[]{:S(2)}) async-start(), calls=%async_computation.17 | async-start | bytes 56360960 | tf_op jit(solution)/shard_map/all_gather | solution.py:70
  864.6 933.8 %all-gather.15.cloned.1.call-start = ((), (), s32[]{:S(2)}) async-start(), calls=%async_computation.16 | async-start | bytes 10485760 | tf_op jit(solution)/shard_map/all_gather | solution.py:40
  864.7 134.0 %copy-start.15 = (f32[1024]{0:T(1024)}, f32[1024]{0:T(1024)S(1)}, u32[]{:S(2)}) copy-start(f32[1024]{0:T(1024)S(1)} %convert_element_type.111) | copy-start | bytes 12292
  998.7 0.6 copy-start.13
  1004.9 853.6 %all-gather.21.cloned.1.call-start = ((), (), s32[]{:S(2)}) async-start(), calls=%async_computation.20 | async-start | bytes 10485760 | tf_op jit(solution)/shard_map/all_gather | solution.py:40
  1005.6 1237.0 %all-gather.19.cloned.1.call-start = ((), (), s32[]{:S(2)}) async-start(), calls=%async_computation.18 | async-start | bytes 28180480 | tf_op jit(solution)/shard_map/all_gather | solution.py:88
  1006.4 1456.3 %reduce-scatter.13.cloned.1.call-start = ((), (), s32[]{:S(2)}) async-start(), calls=%async_computation.21 | async-start | bytes 20971520 | tf_op jit(solution)/shard_map/reduce_scatter | solution.py:44
  2338.1 253.2 %reduce-scatter.11.cloned.1.call-start = ((), (), s32[]{:S(2)}) async-start(), calls=%async_computation.19 | async-start | bytes 20971520 | tf_op jit(solution)/shard_map/reduce_scatter | solution.py:44
  2350.1 3.4 copy-start.10
  2385.3 77.4 %copy-start.14 = (f32[1024]{0:T(1024)S(1)}, f32[1024]{0:T(1024)}, u32[]{:S(2)}) copy-start(f32[1024]{0:T(1024)} %copy-done.13) | copy-start | bytes 12292
  2385.3 77.4 %copy-start.16 = (f32[1024]{0:T(1024)S(1)}, f32[1024]{0:T(1024)}, u32[]{:S(2)}) copy-start(f32[1024]{0:T(1024)} %copy-done.15) | copy-start | bytes 12292
  2385.3 206.0 %copy-start.8 = (bf16[1024,1024]{1,0:T(8,128)(2,1)S(1)}, bf16[1024,1024]{1,0:T(8,128)(2,1)}, u32[]{:S(2)}) copy-start(bf16[1024,1024]{1,0:T(8,128)(2,1)} %param.19) | copy-start | bytes 6291460
  2385.3 206.0 %copy-start.22 = (f32[1024]{0:T(1024)S(1)}, f32[1024]{0:T(1024)}, u32[]{:S(2)}) copy-start(f32[1024]{0:T(1024)} %get-tuple-element.295) | copy-start | bytes 12292
  2385.3 271.8 %all-gather.23.cloned.1.call-start = ((), (), s32[]{:S(2)}) async-start(), calls=%async_computation.22 | async-start | bytes 10485760 | tf_op jit(solution)/shard_map/all_gather | solution.py:40
  2598.7 783.0 %reduce-scatter.23.cloned.1.call-start = ((), (), s32[]{:S(2)}) async-start(), calls=%async_computation.27 | async-start | bytes 25362432 | tf_op jit(solution)/shard_map/reduce_scatter | solution.py:102
  2629.9 0.6 copy-start.25
  2694.0 43.8 all-to-all-start.2
  2697.8 689.1 %reduce-scatter.19.cloned.1.call-start = ((), (), s32[]{:S(2)}) async-start(), calls=%async_computation.25 | async-start | bytes 9437184 | tf_op jit(solution)/shard_map/reduce_scatter | solution.py:102
  2712.9 704.8 %reduce-scatter.15.cloned.1.call-start = ((), (), s32[]{:S(2)}) async-start(), calls=%async_computation.23 | async-start | bytes 20971520 | tf_op jit(solution)/shard_map/reduce_scatter | solution.py:44
  2745.3 8.1 copy-start.1
  2755.1 12.1 copy-start.3
  2767.1 12.7 copy-start.4
  2795.4 7.4 copy-start.5
  2795.4 18.9 slice-start
  2802.9 11.4 slice-start.1
  2842.3 11.9 copy-start.3
  2854.2 12.8 copy-start.4
  2882.1 9.1 copy-start.5
  2882.1 21.6 slice-start
  2891.3 12.4 slice-start.1
  2931.7 12.0 copy-start.3
  2943.7 12.6 copy-start.4
  2971.8 8.9 copy-start.5
  2971.8 21.7 slice-start
  2980.7 12.8 slice-start.1
  3021.5 11.9 copy-start.3
  3033.4 12.8 copy-start.4
  3061.6 8.7 copy-start.5
  3061.6 21.5 slice-start
  3070.3 12.8 slice-start.1
  3112.5 6.2 copy-start.11
  3112.6 6.2 copy-start.12
  3291.4 841.8 %reduce-scatter.21.cloned.1.call-start = ((), (), s32[]{:S(2)}) async-start(), calls=%async_computation.26 | async-start | bytes 50724864 | tf_op jit(solution)/shard_map/reduce_scatter | solution.py:99
  3346.9 1193.7 %reduce-scatter.17.cloned.1.call-start = ((), (), s32[]{:S(2)}) async-start(), calls=%async_computation.24 | async-start | bytes 28311552 | tf_op jit(solution)/shard_map/reduce_scatter | solution.py:99
  3386.8 30.9 copy-start.7
  3386.8 30.9 copy-start.18
  3386.8 30.9 copy-start.20
  3392.7 28.5 copy-start.23
  3392.7 57.3 %copy-start.21 = (f32[1024]{0:T(1024)S(1)}, f32[1024]{0:T(1024)}, u32[]{:S(2)}) copy-start(f32[1024]{0:T(1024)} %get-tuple-element.293) | copy-start | bytes 12292
  (1 other events, 0.5 us)
Sparse Core Ops, SparseCore 0:
  23.1 58.5 all-gather.8
  83.9 425.1 all-gather.10
  571.8 148.3 all-gather.12
  864.2 123.3 reduce-scatter.8
  989.1 750.7 all-gather.16
  1741.9 56.4 all-gather.14
  1800.1 58.2 all-gather.20
  1860.1 382.5 all-gather.18
  2338.2 124.4 reduce-scatter.12
  2465.1 126.1 reduce-scatter.10
  2598.8 58.2 all-gather.22
  2661.5 366.1 reduce-scatter.22
  3031.4 148.1 reduce-scatter.18
  3291.5 126.0 reduce-scatter.14
  3421.5 711.6 reduce-scatter.20
  4136.9 403.6 reduce-scatter.16
where the time goes:
time: 4570 us; the launch traced here: 4550 us
  waiting for transfers between devices  3220 us (70%)
  matrix products  640 us (14%)
  local copies, waits for them, and re-layouts  272 us (6%)
  other arithmetic  209 us (5%)
  blocking collectives  180 us (4%)
    all_gather x2, waiting for transfers between devices, in_proj(): shard_piece = lax.all_gather(weight, 'fsdp', axis=0, tiled=True)  1160 us
    reduce_scatter x2, waiting for transfers between devices, reduce_grads(): lax.psum_scatter(first_grad.astype(jnp.bfloat16), ('fsdp', 'ctx'), scatte...  1080 us
    all_gather x2, waiting for transfers between devices, out_proj(): lax.all_gather(weight, 'fsdp', axis=1, tiled=True)  384 us
    reduce_scatter x4, waiting for transfers between devices, shard_sum(): return lax.psum_scatter(values, 'tp', scatter_dimension=1, tiled=True)  343 us
    dot_general x4, matrix products, contract_cols(): lax.dot_general(left, right, (((1,), (1,)), ((), ())), preferred_element_...  143 us
    dot_general x4, matrix products, contract_rows(): lax.dot_general(left, right, (((0,), (0,)), ((), ())), preferred_element_...  136 us
    all_gather x4, waiting for transfers between devices, full_rows(): return lax.all_gather(values, 'tp', axis=1, tiled=True)  135 us
    all_to_all x2, blocking collectives, to_tokens(): lax.all_to_all(values, 'ctx', split_axis=0, concat_axis=2, tiled=True)  132 us
  transfers between devices with their start and end apart: 18, of which 15 were waited for; matrix products, arithmetic and copies ran while one was open for 20% of the time, Pallas kernels for 0%

commit v1 on v0

v1 whole, which is shorter than its diff:
```python
import math

import jax
import jax.numpy as jnp
from jax import lax
from jax.sharding import PartitionSpec as P

D = 4096
HD = 128

rms_epsilon = 1e-05
masked_score = -1e30
BF = jnp.bfloat16
F32 = jnp.float32


def rotate(values, positions, direction):
    half_width = HD // 2
    inv_freq = jnp.exp(-math.log(10000.0) * jnp.arange(half_width, dtype=F32) * 2.0 / HD)
    angles = positions.astype(F32)[:, None] * inv_freq[None, :]
    cosine = jnp.cos(angles)[:, None, :]
    sine_table = direction * jnp.sin(angles)[:, None, :]
    shaped = values.reshape(values.shape[0], -1, 2, half_width)
    lower_half = shaped[:, :, 0, :]
    upper_half = shaped[:, :, 1, :]
    turned = jnp.stack(
        [
            lower_half * cosine - upper_half * sine_table,
            upper_half * cosine + lower_half * sine_table,
        ],
        axis=2,
    )
    return turned.reshape(values.shape)


def row_total(values):
    return lax.psum(values, "tp")


def swap(values, axis, bit):
    count = lax.axis_size(axis)
    step = 1 << bit
    return lax.ppermute(values, axis, [(i, i ^ step) for i in range(count)])


def bit_of(axis, bit):
    return (lax.axis_index(axis) >> bit) & 1


def tp_bits():
    return range(lax.axis_size("tp").bit_length() - 1)


def in_order(bit, mine, other):
    first = lax.select(jnp.broadcast_to(bit == 0, mine.shape), mine, other)
    second = lax.select(jnp.broadcast_to(bit == 0, mine.shape), other, mine)
    return first, second


def gather_rows(values):
    rows, cols = values.shape
    high_bits = [b for b in reversed(tp_bits()) if b > 0]
    plans = (
        [("ctx", 0)] + [("tp", b) for b in high_bits] + [("tp", 0)],
        [("tp", b) for b in high_bits] + [("ctx", 0)] + [("tp", 0)],
    )
    pieces = []
    for index, plan in enumerate(plans):
        part = values[index * (rows // 2) : (index + 1) * (rows // 2)]
        blocks = {(): part}
        ctx_parts = [[part]]
        for axis, bit in plan:
            if axis == "ctx":
                mine = jnp.concatenate(ctx_parts[0], axis=1)
                other = swap(mine, "ctx", 0)
                first, second = in_order(lax.axis_index("ctx"), mine, other)
                width = ctx_parts[0][0].shape[1]
                ctx_parts = [
                    [full[:, i : i + width] for i in range(0, full.shape[1], width)]
                    for full in (first, second)
                ]
            else:
                mine = jnp.stack([jnp.concatenate(p, axis=1) for p in ctx_parts])
                other = swap(mine, "tp", bit)
                first, second = in_order(bit_of("tp", bit), mine, other)
                grown = []
                for c in range(len(ctx_parts)):
                    line = []
                    for i in range(len(ctx_parts[c])):
                        line.append(first[c][:, i * cols : (i + 1) * cols])
                        line.append(second[c][:, i * cols : (i + 1) * cols])
                    grown.append(line)
                ctx_parts = grown
        pieces.append([jnp.concatenate(p, axis=1) for p in ctx_parts])
    ordered = []
    for c in range(len(pieces[0])):
        ordered += [pieces[0][c], pieces[1][c]]
    return jnp.concatenate(ordered, axis=0)


def scatter_rows(block_of):
    count = lax.axis_size("tp")
    mine = bit_of("tp", 0)
    half = count // 2
    send = jnp.stack([block_of(2 * i + (1 - mine)) for i in range(half)]).astype(BF)
    got = swap(send, "tp", 0)
    keep = jnp.stack([block_of(2 * i + mine) for i in range(half)])
    total = (keep + got.astype(F32)).astype(BF)
    ctx_count = lax.axis_size("ctx")
    rows = total.shape[1] // ctx_count
    total = total.reshape(half, ctx_count, 2, rows // 2, total.shape[2])
    high_bits = [b for b in reversed(tp_bits()) if b > 0]
    me_ctx = lax.axis_index("ctx")
    done = []
    for index in range(2):
        part = total[:, :, index].astype(F32)
        plan = [("tp", b) for b in high_bits]
        plan = [("ctx", 0)] + plan if index == 0 else plan + [("ctx", 0)]
        for axis, bit in plan:
            if axis == "ctx":
                other = lax.dynamic_index_in_dim(part, 1 - me_ctx, 1, keepdims=True)
                own = lax.dynamic_index_in_dim(part, me_ctx, 1, keepdims=True)
                part = own + swap(other.astype(BF), "ctx", 0).astype(F32)
            else:
                b = bit_of("tp", bit)
                split = part.reshape((2, part.shape[0] // 2) + part.shape[1:])
                other = lax.dynamic_index_in_dim(split, 1 - b, 0, keepdims=False)
                own = lax.dynamic_index_in_dim(split, b, 0, keepdims=False)
                part = own + swap(other.astype(BF), "tp", bit).astype(F32)
        done.append(part[0, 0])
    return jnp.concatenate(done, axis=0)


def contract_rows(left, right):
    return lax.dot_general(
        left, right, (((0,), (0,)), ((), ())), preferred_element_type=F32
    )


def contract_cols(left, right):
    return lax.dot_general(
        left, right, (((1,), (1,)), ((), ())), preferred_element_type=F32
    )


def dot(left, right):
    return jnp.dot(left, right, preferred_element_type=F32)


def ctx_half(weight, axis):
    count = lax.axis_size("ctx")
    size = weight.shape[axis] // count
    return lax.dynamic_slice_in_dim(weight, lax.axis_index("ctx") * size, size, axis)


def after(value, token):
    value, _ = lax.optimization_barrier((value, token))
    return value


def owners(grad):
    return lax.psum_scatter(grad, "fsdp", scatter_dimension=0, tiled=False)


def trade_ctx(block, axis):
    size = block.shape[axis] // 2
    me = lax.axis_index("ctx")
    own = lax.dynamic_slice_in_dim(block, me * size, size, axis)
    give = lax.dynamic_slice_in_dim(block, (1 - me) * size, size, axis)
    got = swap(give, "ctx", 0)
    return in_order(me, own, got)


def score_block(query_heads, key_heads, first_row, block_len):
    query_block = lax.dynamic_slice_in_dim(query_heads, first_row, block_len, 0)
    scores = jnp.einsum("qhd,khd->hqk", query_block, key_heads, preferred_element_type=F32)
    scores = scores * (1.0 / math.sqrt(HD))
    key_index = jnp.arange(key_heads.shape[0], dtype=jnp.int32)
    query_index = first_row + jnp.arange(block_len, dtype=jnp.int32)
    allowed = key_index[None, :] <= query_index[:, None]
    return (query_block, jnp.where(allowed[None, :, :], scores, masked_score))


def attend_forward(qkv_heads):
    seq_len = qkv_heads.shape[0]
    head_count = qkv_heads.shape[2] // HD
    block_len = min(512, seq_len)
    block_count = seq_len // block_len
    query_heads = qkv_heads[:, 0].reshape(seq_len, head_count, HD)
    key_heads = qkv_heads[:, 1].reshape(seq_len, head_count, HD)
    value_heads = qkv_heads[:, 2].reshape(seq_len, head_count, HD)

    def one_block(block_index):
        query_block, scores = score_block(
            query_heads, key_heads, block_index * block_len, block_len
        )
        row_max = jnp.max(scores, axis=-1, keepdims=True)
        expo_vals = jnp.exp(scores - row_max)
        row_sums = jnp.sum(expo_vals, axis=-1, keepdims=True)
        soft = (expo_vals / row_sums).astype(BF)
        mixed = jnp.einsum("hqk,khd->qhd", soft, value_heads, preferred_element_type=F32)
        return (mixed.astype(BF), (row_max + jnp.log(row_sums))[:, :, 0])

    head_outs, log_norms = lax.map(one_block, jnp.arange(block_count, dtype=jnp.int32))
    return (head_outs.reshape(seq_len, head_count * HD), log_norms)


def attend_backward(qkv_heads, log_norms, grad_out):
    seq_len = qkv_heads.shape[0]
    head_count = qkv_heads.shape[2] // HD
    block_len = min(512, seq_len)
    block_count = seq_len // block_len
    score_scale = 1.0 / math.sqrt(HD)
    query_heads = qkv_heads[:, 0].reshape(seq_len, head_count, HD)
    key_heads = qkv_heads[:, 1].reshape(seq_len, head_count, HD)
    value_heads = qkv_heads[:, 2].reshape(seq_len, head_count, HD)
    grad_heads = grad_out.reshape(seq_len, head_count, HD)

    def one_block(running_grads, block_item):
        block_index, block_norms = block_item
        first_row = block_index * block_len
        query_block, scores = score_block(query_heads, key_heads, first_row, block_len)
        probs_full = jnp.exp(scores - block_norms[:, :, None])
        soft = probs_full.astype(BF)
        grad_block = lax.dynamic_slice_in_dim(grad_heads, first_row, block_len, 0)
        grad_probs = jnp.einsum(
            "qhd,khd->hqk", grad_block, value_heads, preferred_element_type=F32
        )
        weighted = jnp.sum(probs_full * grad_probs, axis=-1, keepdims=True)
        grad_scores = (probs_full * (grad_probs - weighted)).astype(BF)
        query_grad = (
            jnp.einsum("hqk,khd->qhd", grad_scores, key_heads, preferred_element_type=F32)
            * score_scale
        )
        key_grad = (
            running_grads[0]
            + jnp.einsum("hqk,qhd->khd", grad_scores, query_block, preferred_element_type=F32)
            * score_scale
        )
        value_grad = running_grads[1] + jnp.einsum(
            "hqk,qhd->khd", soft, grad_block, preferred_element_type=F32
        )
        return ((key_grad, value_grad), query_grad)

    zero_grads = jnp.zeros((seq_len, head_count, HD), F32)
    key_value, query_grads = lax.scan(
        one_block, (zero_grads, zero_grads), (jnp.arange(block_count, dtype=jnp.int32), log_norms)
    )
    flat_width = head_count * HD
    return (
        query_grads.reshape(seq_len, flat_width),
        key_value[0].reshape(seq_len, flat_width),
        key_value[1].reshape(seq_len, flat_width),
    )


def body(
    layer_input, attn_gain, qkv_weight, out_weight, ffn_gain, gate_up_weight, down_weight, cotangent
):
    n_f = lax.axis_size("fsdp")
    d_f = D // n_f
    cols = layer_input.shape[1]
    qkv_half = ctx_half(qkv_weight, 2)
    qkv_half = qkv_half.reshape(d_f, -1)
    out_half = ctx_half(out_weight, 0)
    gu_half = ctx_half(gate_up_weight, 2)
    gu_half = gu_half.reshape(d_f, -1)
    down_half = ctx_half(down_weight, 0)
    qkv_full = lax.all_gather(qkv_half, "fsdp", axis=0, tiled=True)
    out_half = after(out_half, qkv_full)
    out_full = lax.all_gather(out_half, "fsdp", axis=0, tiled=False)
    gu_half = after(gu_half, out_full)
    gu_full = lax.all_gather(gu_half, "fsdp", axis=0, tiled=True)
    down_half = after(down_half, gu_full)
    down_full = lax.all_gather(down_half, "fsdp", axis=0, tiled=False)

    input_float = layer_input.astype(F32)
    attn_scale = attn_gain.astype(F32)
    ffn_scale = ffn_gain.astype(F32)
    rms_one = lax.rsqrt(row_total(jnp.sum(input_float * input_float, axis=-1)) / D + rms_epsilon)[
        :, None
    ]
    normed_attn = (input_float * rms_one * attn_scale).astype(BF)
    attn_full = gather_rows(normed_attn)
    seq_len = attn_full.shape[0]
    proj = dot(attn_full, qkv_full)
    width = proj.shape[1] // 3
    positions = jnp.arange(seq_len, dtype=jnp.int32)
    qkv_heads = jnp.stack(
        [
            rotate(proj[:, :width], positions, 1.0),
            rotate(proj[:, width : 2 * width], positions, 1.0),
            proj[:, 2 * width :],
        ],
        axis=1,
    ).astype(BF)
    head_outs, log_norms = attend_forward(qkv_heads)

    def out_blocks(inner, full):
        joined = jnp.swapaxes(full, 0, 1).reshape(full.shape[1], lax.axis_size("tp"), cols)
        return lambda t: dot(inner, lax.dynamic_index_in_dim(joined, t, 1, keepdims=False))

    def in_blocks(grads, full):
        split = full.reshape(lax.axis_size("tp"), cols, full.shape[1])
        return lambda t: contract_cols(
            grads, lax.dynamic_index_in_dim(split, t, 0, keepdims=False)
        )

    resid = input_float + scatter_rows(out_blocks(head_outs, out_full))
    rms_two = lax.rsqrt(row_total(jnp.sum(resid * resid, axis=-1)) / D + rms_epsilon)[:, None]
    normed_ffn = (resid * rms_two * ffn_scale).astype(BF)
    ffn_full = gather_rows(normed_ffn)
    cotan_full = gather_rows(cotangent)
    gate_up = dot(ffn_full, gu_full)
    units = gate_up.shape[1] // 2
    gate = gate_up[:, :units]
    up_value = gate_up[:, units:]
    sigma = jax.nn.sigmoid(gate)
    hidden = (gate * sigma * up_value).astype(BF)
    down_part = contract_rows(hidden, cotan_full).astype(BF)
    down_sum = owners(jnp.swapaxes(down_part.reshape(units, n_f, d_f), 0, 1))

    layer_output = (resid + scatter_rows(out_blocks(hidden, down_full))).astype(BF)
    down_rows = jnp.swapaxes(down_full, 0, 1).reshape(units, D)
    grad_hidden = contract_cols(cotan_full, down_rows)
    grad_gu = jnp.concatenate(
        [grad_hidden * up_value * sigma * (1.0 + gate * (1.0 - sigma)), grad_hidden * gate * sigma],
        axis=1,
    ).astype(BF)
    gu_part = contract_rows(ffn_full, grad_gu).astype(BF)
    gu_part = after(gu_part, down_sum)
    gu_sum = owners(gu_part.reshape(n_f, d_f, -1))
    grad_nffn = scatter_rows(in_blocks(grad_gu, gu_full))
    ffn_term = grad_nffn * ffn_scale
    ffn_dot = row_total(jnp.sum(ffn_term * resid, axis=-1))[:, None]
    grad_resid = cotangent.astype(F32) + rms_two * ffn_term - resid * rms_two**3 * ffn_dot / D
    ffn_gain_part = jnp.sum(grad_nffn * resid * rms_two, axis=0)
    grad_branch = grad_resid.astype(BF)
    branch_full = gather_rows(grad_branch)
    out_rows = jnp.swapaxes(out_full, 0, 1).reshape(out_full.shape[1], D)
    grad_heads = contract_cols(branch_full, out_rows).astype(BF)
    out_part = contract_rows(head_outs, branch_full).astype(BF)
    out_part = after(out_part, gu_sum)
    out_sum = owners(jnp.swapaxes(out_part.reshape(-1, n_f, d_f), 0, 1))
    query_grad, key_grad, value_grad = attend_backward(qkv_heads, log_norms, grad_heads)
    grad_proj = jnp.concatenate(
        [rotate(query_grad, positions, -1.0), rotate(key_grad, positions, -1.0), value_grad],
        axis=1,
    ).astype(BF)
    qkv_part = contract_rows(attn_full, grad_proj).astype(BF)
    qkv_sum = owners(qkv_part.reshape(n_f, d_f, -1))
    grad_nattn = scatter_rows(in_blocks(grad_proj, qkv_full))
    attn_term = grad_nattn * attn_scale
    attn_dot = row_total(jnp.sum(attn_term * input_float, axis=-1))[:, None]
    grad_input = grad_resid + rms_one * attn_term - input_float * rms_one**3 * attn_dot / D
    attn_gain_part = jnp.sum(grad_nattn * input_float * rms_one, axis=0)
    gain_grads = lax.psum((attn_gain_part, ffn_gain_part), ("fsdp", "ctx"))

    def in_grad(block, count):
        first, second = trade_ctx(block, 0)
        rows = first.shape[0]
        return jnp.concatenate(
            [first.reshape(rows, count, -1), second.reshape(rows, count, -1)], axis=2
        ).astype(F32)

    def out_grad(block):
        return jnp.concatenate(trade_ctx(block, 1), axis=0).astype(F32)

    return (
        layer_output,
        grad_input,
        gain_grads[0],
        in_grad(qkv_sum, 3),
        out_grad(out_sum),
        gain_grads[1],
        in_grad(gu_sum, 2),
        out_grad(down_sum),
    )


def solution(mesh):
    return jax.shard_map(
        body,
        mesh=mesh,
        in_specs=(
            P(("fsdp", "ctx"), "tp"),
            P("tp"),
            P("fsdp", None, "tp"),
            P("tp", "fsdp"),
            P("tp"),
            P("fsdp", None, "tp"),
            P("tp", "fsdp"),
            P(("fsdp", "ctx"), "tp"),
        ),
        out_specs=(
            P(("fsdp", "ctx"), "tp"),
            P(("fsdp", "ctx"), "tp"),
            P("tp"),
            P(("fsdp", "ctx"), None, "tp"),
            P("tp", ("fsdp", "ctx")),
            P("tp"),
            P(("fsdp", "ctx"), None, "tp"),
            P("tp", ("fsdp", "ctx")),
        ),
        check_vma=False,
    )
```

time: 4570 us -> 2670 us (0.58)
  waiting for transfers between devices: 3220 us -> 715 us
  other arithmetic: 209 us -> 687 us
  local copies, waits for them, and re-layouts: 272 us -> 381 us
  blocking collectives: 180 us -> 114 us
  matrix products: 640 us -> 697 us
    all_gather x8 -> x4, waiting for transfers between devices: 1680 us -> 7.76 us  [the longest x1 7.74 us: body(): out_full = lax.all_gather(out_half, 'fsdp', axis=0, tiled=False)]
    reduce_scatter x8 -> x4, waiting for transfers between devices: 1420 us -> 35.6 us  [owners(): return lax.psum_scatter(grad, 'fsdp', scatter_dimension=0, tiled=False)]
    ppermute x0 -> x48, waiting for transfers between devices: none -> 672 us  [swap(): return lax.ppermute(values, axis, [(i, i ^ step) for i in range(count)])]
    concatenate x0 -> x8, other arithmetic: none -> 375 us  [the longest x4 373 us: gather_rows(): return jnp.concatenate(ordered, axis=0)]
    all_to_all x2 -> x0, blocking collectives: 132 us -> none  [to_tokens(): lax.all_to_all(values, 'ctx', split_axis=0, concat_axis=2, tiled=True)]
    all_to_all x2 -> x0, waiting for transfers between devices: 117 us -> none  [to_heads(): lax.all_to_all(values, 'ctx', split_axis=2, concat_axis=0, tiled=True)]
    psum x1, blocking collectives: 22.7 us -> 76.7 us  [body(): gain_grads = lax.psum((attn_gain_part, ffn_gain_part), ('fsdp', 'ctx'))]
    another operation x5 -> x35, other arithmetic: 15.5 us -> 68.8 us  [the longest x28 33.5 us: gather_rows(): mine = jnp.stack([jnp.concatenate(p, axis=1) for p in ctx_parts])]
  transfers between devices with their start and end apart: 18 -> 56, of which waited for: 15 -> 23; matrix products, arithmetic and copies ran while one was open for 20% -> 57% of each run, Pallas kernels for 0% -> 0%
where the time goes in v1:
time: 2670 us; the launch traced here: 2660 us
  waiting for transfers between devices  715 us (27%)
  matrix products  697 us (26%)
  other arithmetic  687 us (26%)
  local copies, waits for them, and re-layouts  381 us (14%)
  blocking collectives  114 us (4%)
  starting transfers between devices  41.4 us (2%)
    ppermute x48, waiting for transfers between devices, swap(): return lax.ppermute(values, axis, [(i, i ^ step) for i in range(count)])  672 us
    concatenate x4, other arithmetic, gather_rows(): return jnp.concatenate(ordered, axis=0)  373 us
    dot_general x10, matrix products, contract_cols(): lax.dot_general(left, right, (((1,), (1,)), ((), ())), preferred_element_...  178 us
    dot_general x10, matrix products, dot(): return jnp.dot(left, right, preferred_element_type=F32)  155 us
    dot_general x4, matrix products, contract_rows(): lax.dot_general(left, right, (((0,), (0,)), ((), ())), preferred_element_...  128 us
    dynamic_update_slice x8, local copies, waits for them, and re-layouts, attend_backward(): lax.scan(one_block, (zero_grads, zero_grads), (jnp.arange(block_count, dt...  99.1 us
    psum x1, blocking collectives, body(): gain_grads = lax.psum((attn_gain_part, ffn_gain_part), ('fsdp', 'ctx'))  76.7 us
    dot_general x4, matrix products, one_block(): jnp.einsum('hqk,qhd->khd', soft, grad_block, preferred_element_type=F32)  57.1 us
  transfers between devices with their start and end apart: 56, of which 23 were waited for; matrix products, arithmetic and copies ran while one was open for 57% of the time, Pallas kernels for 0%

profile of v1, /device:TPU:0, one launch (start us, length us, event | category | flops | bytes accessed | tf_op | source)
XLA Modules:
  0.0 2658.2 jit_solution(13829717741534584436)
XLA Ops:
  24.2 22.2 collective-permute-done
  62.4 58.6 %collective-permute-done.3 = bf16[1,512,1024]{2,1,0:T(8,128)(2,1)} collective-permute-done((bf16[1,512,1024]{2,1,0:T(8,128)(2,1)}, bf16[1,512,1024]{2,1,0:T(8,128)(2,1)}, u32[]{:S(2)}, u32[]{:S(2)}) %collective-permute-start.3) | collective-permute-done | bytes 1048608 | tf_op jit(solution)/shard_map/ppermute | solution.py:43
  130.4 46.7 %collective-permute-done.4 = bf16[512,2048]{1,0:T(8,128)(2,1)S(1)} collective-permute-done((bf16[512,2048]{1,0:T(8,128)(2,1)S(1)}, bf16[512,2048]{1,0:T(8,128)(2,1)S(1)}, u32[]{:S(2)}, u32[]{:S(2)}) %collective-permute-start.4) | collective-permute-done | bytes 2097184 | tf_op jit(solution)/shard_map/ppermute | solution.py:43
  205.2 84.8 %maximum_maximum_fusion = bf16[2048,4096]{1,0:T(8,128)(2,1)} fusion(bf16[512,1024]{1,0:T(8,128)(2,1)} %get-tuple-element.477, bf16[512,1024]{1,0:T(8,128)(2,1)} %get-tuple-element.475, bf16[512,1024]{1,0:T(8,128)(2,1)} %get-tuple-element.476, bf16[512,1024]{1,0:T(8,128)(2,1)} %get-tuple-element.474, bf16[512,1024]{1,0:T(8,128)(2,1)} %get-tuple-element.468, ...), kind=kLoop, calls=%fused_computation.44 | loop fusion | flops 268435456 | bytes 33554432 | tf_op jit(solution)/shard_map/concatenate | solution.py:98
  290.0 34.9 %fusion.165 = f32[2048,1536]{0,1:T(8,128)} fusion(bf16[2048,4096]{1,0:T(8,128)(2,1)} %maximum_maximum_fusion, bf16[4096,1536]{0,1:T(8,128)(2,1)} %all-gather.7.cloned.1.call-done), kind=kOutput, calls=%fused_computation.431 | convolution fusion | flops 25769803776 | bytes 41943040 | tf_op jit(solution)/shard_map/dot_general | solution.py:147
  349.0 74.7 %while.27 = (s32[]{:T(128)}, bf16[4,512,4,128]{3,2,1,0:T(4,128)(2,1)}, f32[4,4,512]{2,1,0:T(4,128)}, s32[4]{0:T(128)S(1)}, bf16[2048,4,128]{2,0,1:T(8,128)(2,1)}...) while((s32[]{:T(128)}, ...), condition=%wide.region_5.6_spmd, body=%wide.region_2.5_spmd.sunk | while | flops 2199124480 | bytes 69276872 | solution.py:204
  457.1 24.1 collective-permute-done.22
  485.1 68.0 %collective-permute-done.25 = bf16[1,512,1024]{2,1,0:T(8,128)(2,1)S(1)} collective-permute-done((bf16[1,512,1024]{2,1,0:T(8,128)(2,1)S(1)}, bf16[1,512,1024]{2,1,0:T(8,128)(2,1)S(1)}, u32[]{:S(2)}, u32[]{:S(2)}) %collective-permute-start.25) | collective-permute-done | bytes 1048608 | tf_op jit(solution)/shard_map/ppermute | solution.py:43
  566.0 36.7 %collective-permute-done.26 = bf16[512,2048]{1,0:T(8,128)(2,1)} collective-permute-done((bf16[512,2048]{1,0:T(8,128)(2,1)}, bf16[512,2048]{1,0:T(8,128)(2,1)}, u32[]{:S(2)}, u32[]{:S(2)}) %collective-permute-start.26) | collective-permute-done | bytes 2097184 | tf_op jit(solution)/shard_map/ppermute | solution.py:43
  635.8 40.3 %collective-permute-done.7 = bf16[2,1,512,1024]{3,2,1,0:T(8,128)(2,1)} collective-permute-done((bf16[2,1,512,1024]{3,2,1,0:T(8,128)(2,1)}, bf16[2,1,512,1024]{3,2,1,0:T(8,128)(2,1)}, u32[]{:S(2)}, u32[]{:S(2)}) %collective-permute-start.7) | collective-permute-done | bytes 2097184 | tf_op jit(solution)/shard_map/ppermute | solution.py:43
  689.2 14.6 collective-permute-done.8
  725.8 19.0 collective-permute-done.11
  752.9 60.9 %collective-permute-done.14 = bf16[1,512,1024]{2,1,0:T(8,128)(2,1)S(1)} collective-permute-done((bf16[1,512,1024]{2,1,0:T(8,128)(2,1)S(1)}, bf16[1,512,1024]{2,1,0:T(8,128)(2,1)S(1)}, u32[]{:S(2)}, u32[]{:S(2)}) %collective-permute-start.14) | collective-permute-done | bytes 1048608 | tf_op jit(solution)/shard_map/ppermute | solution.py:43
  820.6 39.0 %collective-permute-done.15 = bf16[512,2048]{1,0:T(8,128)(2,1)S(1)} collective-permute-done((bf16[512,2048]{1,0:T(8,128)(2,1)S(1)}, bf16[512,2048]{1,0:T(8,128)(2,1)S(1)}, u32[]{:S(2)}, u32[]{:S(2)}) %collective-permute-start.15) | collective-permute-done | bytes 2097184 | tf_op jit(solution)/shard_map/ppermute | solution.py:43
  863.6 64.9 %maximum_maximum_fusion.2 = bf16[2048,4096]{1,0:T(8,128)(2,1)} fusion(bf16[512,1024]{1,0:T(8,128)(2,1)} %get-tuple-element.435, bf16[512,1024]{1,0:T(8,128)(2,1)} %get-tuple-element.433, bf16[512,1024]{1,0:T(8,128)(2,1)} %get-tuple-element.434, bf16[512,1024]{1,0:T(8,128)(2,1)} %get-tuple-element.432, bf16[512,1024]{1,0:T(8,128)(2,1)} %get-tuple-element.426, ...), kind=kLoop, calls=%fused_computation.50 | loop fusion | flops 268435456 | bytes 33554432 | tf_op jit(solution)/shard_map/concatenate | solution.py:98
  955.2 120.6 %maximum_maximum_fusion.1 = bf16[2048,4096]{1,0:T(8,128)(2,1)} fusion(bf16[512,1024]{1,0:T(8,128)(2,1)} %get-tuple-element.456, bf16[512,1024]{1,0:T(8,128)(2,1)} %get-tuple-element.454, bf16[512,1024]{1,0:T(8,128)(2,1)} %get-tuple-element.455, bf16[512,1024]{1,0:T(8,128)(2,1)} %get-tuple-element.453, bf16[512,1024]{1,0:T(8,128)(2,1)} %get-tuple-element.447, ...), kind=kLoop, calls=%fused_computation.47 | loop fusion | flops 268435456 | bytes 33554432 | tf_op jit(solution)/shard_map/concatenate | solution.py:98
  1075.8 28.8 %copy.106 = bf16[4096,2752]{1,0:T(8,128)(2,1)} copy(bf16[4096,2752]{0,1:T(8,128)(2,1)} %all-gather.9.cloned.1.call-done) | data formatting | bytes 45088768 | tf_op jit(solution)/shard_map/all_gather | solution.py:273
  1104.6 57.0 %fusion.166 = f32[2048,2752]{0,1:T(8,128)} fusion(bf16[2048,4096]{1,0:T(8,128)(2,1)} %maximum_maximum_fusion.1, bf16[4096,2752]{0,1:T(8,128)(2,1)} %all-gather.9.cloned.1.call-done), kind=kOutput, calls=%fused_computation.432 | convolution fusion | flops 46170898432 | bytes 61865984 | tf_op jit(solution)/shard_map/dot_general | solution.py:147
  1161.6 15.2 copy.105
  1176.8 47.7 %multiply_convert_fusion.2 = (bf16[2048,1376]{0,1:T(8,128)(2,1)}, bf16[2048,1376]{0,1:T(8,128)(2,1)}, bf16[2048,1376]{0,1:T(8,128)(2,1)}) fusion(f32[2048,2752]{0,1:T(8,128)} %fusion.166, bf16[2048,4096]{1,0:T(8,128)(2,1)} %maximum_maximum_fusion.2, bf16[1376,4096]{0,1:T(8,128)(2,1)} %bitcast.528), kind=kOutput, calls=%fused_computation.61 | convolution fusion | flops 23130537984 | bytes 67502080 | tf_op jit(solution)/shard_map/dot_general | solution.py:141
  1224.5 18.2 convert_bitcast_fusion.3
  1242.7 17.5 convert_bitcast_fusion.2
  1277.8 11.3 convert_bitcast_fusion.5
  1295.4 11.7 convolution_bitcast_fusion
  1307.1 11.7 convolution_bitcast_fusion.1
  1318.8 18.2 fusion.45
  1337.0 17.9 fusion.48
  1392.6 25.4 collective-permute-done.29
  1426.9 36.0 %collective-permute-done.18 = bf16[2,1,512,1024]{3,2,1,0:T(8,128)(2,1)} collective-permute-done((bf16[2,1,512,1024]{3,2,1,0:T(8,128)(2,1)}, bf16[2,1,512,1024]{3,2,1,0:T(8,128)(2,1)}, u32[]{:S(2)}, u32[]{:S(2)}) %collective-permute-start.18) | collective-permute-done | bytes 2097184 | tf_op jit(solution)/shard_map/ppermute | solution.py:43
  1473.0 14.1 collective-permute-done.30
  1493.8 17.1 psum.44
  1523.9 23.2 collective-permute-done.33
  1550.7 26.9 %convolution_convert_fusion.2 = bf16[1376,4096]{1,0:T(8,128)(2,1)} fusion(bf16[2048,1376]{0,1:T(8,128)(2,1)} %get-tuple-element.286, bf16[2048,4096]{1,0:T(8,128)(2,1)S(1)} %bitcast.518), kind=kOutput, calls=%fused_computation.57 | convolution fusion | flops 23091085312 | bytes 33685504 | tf_op jit(solution)/shard_map/dot_general | solution.py:135
  1588.9 29.4 %collective-permute-done.36 = bf16[1,512,1024]{2,1,0:T(8,128)(2,1)S(1)} collective-permute-done((bf16[1,512,1024]{2,1,0:T(8,128)(2,1)}, bf16[1,512,1024]{2,1,0:T(8,128)(2,1)S(1)}, u32[]{:S(2)}, u32[]{:S(2)}) %collective-permute-start.36) | collective-permute-done | bytes 1048608 | tf_op jit(solution)/shard_map/ppermute | solution.py:43
  1623.1 47.0 %collective-permute-done.37 = bf16[512,2048]{1,0:T(8,128)(2,1)S(1)} collective-permute-done((bf16[512,2048]{1,0:T(8,128)(2,1)S(1)}, bf16[512,2048]{1,0:T(8,128)(2,1)S(1)}, u32[]{:S(2)}, u32[]{:S(2)}) %collective-permute-start.37) | collective-permute-done | bytes 2097184 | tf_op jit(solution)/shard_map/ppermute | solution.py:43
  1687.5 102.9 %maximum_maximum_fusion.3 = bf16[2048,4096]{1,0:T(8,128)(2,1)} fusion(bf16[512,1024]{1,0:T(8,128)(2,1)} %get-tuple-element.414, bf16[512,1024]{1,0:T(8,128)(2,1)} %get-tuple-element.412, bf16[512,1024]{1,0:T(8,128)(2,1)} %get-tuple-element.413, bf16[512,1024]{1,0:T(8,128)(2,1)} %get-tuple-element.411, bf16[512,1024]{1,0:T(8,128)(2,1)} %get-tuple-element.405, ...), kind=kLoop, calls=%fused_computation.53 | loop fusion | flops 268435456 | bytes 33554432 | tf_op jit(solution)/shard_map/concatenate | solution.py:98
  1790.5 13.6 convolution_convert_fusion.3
  1806.7 55.6 %convolution_convert_fusion = bf16[4096,2752]{0,1:T(8,128)(2,1)} fusion(bf16[2048,4096]{1,0:T(8,128)(2,1)} %maximum_maximum_fusion.1, bf16[2048,1376]{0,1:T(8,128)(2,1)} %get-tuple-element.285, bf16[2048,1376]{0,1:T(8,128)(2,1)} %get-tuple-element.284), kind=kOutput, calls=%fused_computation.42 | convolution fusion | flops 46204715008 | bytes 50593792 | tf_op jit(solution)/shard_map/dot_general | solution.py:135
  1862.3 19.6 copy.186
  1888.2 15.8 convolution_convert_fusion.4
  1904.0 366.1 %while.28 = (s32[]{:T(128)}, f32[2048,4,128]{0,2,1:T(8,128)}, f32[2048,4,128]{0,2,1:T(8,128)}, f32[4,512,4,128]{1,0,3,2:T(4,128)}, s32[4]{0:T(128)S(1)}, /*index...) while((s32[]{:T(128)}, f32[2048,4,128]{0,2,1:T(8,128)}, ...), condition=%wide.region_12.13_spmd.clone, body=%wide.region_10.12_spmd.clone.sunk | while | flops 5438175744 | bytes 202436880 | solution.py:246
  1916.1 13.0 multiply_reduce_fusion.5
  1929.2 12.2 multiply_convert_fusion.6
  1951.8 21.2 dynamic_update_slice.20
  1980.3 13.5 bitcast_add_fusion.13
  2005.7 13.1 multiply_reduce_fusion.5
  2018.8 12.3 multiply_convert_fusion.6
  2041.5 21.2 dynamic_update_slice.20
  2071.2 14.7 bitcast_add_fusion.13
  2097.8 13.0 multiply_reduce_fusion.5
  2110.8 12.3 multiply_convert_fusion.6
  2133.5 21.2 dynamic_update_slice.20
  2163.5 14.7 bitcast_add_fusion.13
  2190.1 13.0 multiply_reduce_fusion.5
  2203.1 12.2 multiply_convert_fusion.6
  2225.7 21.1 dynamic_update_slice.20
  2255.4 14.3 bitcast_add_fusion.13
  2284.2 32.3 %convolution_convert_fusion.1 = bf16[4096,1536]{1,0:T(8,128)(2,1)} fusion(bf16[2048,4096]{1,0:T(8,128)(2,1)} %maximum_maximum_fusion, bf16[2048,512]{0,1:T(8,128)(2,1)S(1)} %bitcast.550, bf16[2048,512]{0,1:T(8,128)(2,1)S(1)} %bitcast.560, bf16[2048,512]{0,1:T(8,128)(2,1)S(1)} %bitcast.555), kind=kOutput, calls=%fused_computation.56 | convolution fusion | flops 25794969600 | bytes 35651584 | tf_op jit(solution)/shard_map/dot_general | solution.py:135
  2316.6 15.7 copy.133
  2358.7 11.6 convolution_bitcast_fusion.5
  2404.2 12.5 collective-permute-done.47
  2422.3 50.1 %collective-permute-done.45 = bf16[512,512]{1,0:T(8,128)(2,1)S(1)} collective-permute-done((bf16[512,512]{1,0:T(8,128)(2,1)S(1)}, bf16[512,512]{1,0:T(8,128)(2,1)S(1)}, u32[]{:S(2)}, u32[]{:S(2)}) %collective-permute-start.45) | collective-permute-done | bytes 524320 | tf_op jit(solution)/shard_map/ppermute | solution.py:43
  2489.4 35.6 %reduce-scatter.5.cloned.1.call-done = bf16[1,1024,1536]{2,1,0:T(8,128)(2,1)} async-done(((bf16[4,1024,1536]{2,1,0:T(8,128)(2,1)}), bf16[1,1024,1536]{2,1,0:T(8,128)(2,1)}) %reduce-scatter.5.cloned.1.call-update) | async-done | bytes 3145744 | tf_op jit(solution)/shard_map/reduce_scatter | solution.py:162
  2538.1 76.7 %all-reduce = (f32[1024]{0:T(1024)}, f32[1024]{0:T(1024)}) all-reduce(f32[1024]{0:T(1024)S(1)} %get-tuple-element.238, f32[1024]{0:T(1024)S(1)} %copy-done.87), channel_id=1, replica_groups=mesh['fsdp'=4,'ctx'=2,'tp'=4] {'fsdp','ctx'}, use_global_device_ids=true, to_apply=%region_16.17 | all-reduce | flops 2048 | bytes 16384 | tf_op jit(solution)/shard_map/psum | solution.py:357
  (617 shorter events, 741.2 us)
Async XLA Ops:
  7.2 174.5 %copy-start = (bf16[1024,1024]{1,0:T(8,128)(2,1)S(1)}, bf16[1024,1024]{1,0:T(8,128)(2,1)}, u32[]{:S(2)}) copy-start(bf16[1024,1024]{1,0:T(8,128)(2,1)} %param.15) | copy-start | bytes 6291460
  7.2 282.8 %all-gather.7.cloned.1.call-start = ((), (), s32[]{:S(2)}) async-start(), calls=%async_computation.4 | async-start | bytes 15728640 | tf_op jit(solution)/shard_map/all_gather | solution.py:269
  22.7 23.7 collective-permute-start
  51.9 70.9 %collective-permute-start.1 = (bf16[2,512,1024]{2,1,0:T(8,128)(2,1)}, bf16[2,512,1024]{2,1,0:T(8,128)(2,1)}, u32[]{:S(2)}, u32[]{:S(2)}) collective-permute-start(bf16[2,512,1024]{2,1,0:T(8,128)(2,1)} %pad_maximum_fusion.16), channel_id=1, source_target_pairs={{0,2},{1,3},{2,0},{3,1},{4,6},{5,7},{6,4},{7,5},{8,10},{9,11},{10,... | collective-permute-start | bytes 6291464 | tf_op jit(solution)/shard_map/ppermute | solution.py:43
  53.6 67.5 %collective-permute-start.3 = (bf16[1,512,1024]{2,1,0:T(8,128)(2,1)}, bf16[1,512,1024]{2,1,0:T(8,128)(2,1)}, u32[]{:S(2)}, u32[]{:S(2)}) collective-permute-start(bf16[1,512,1024]{2,1,0:T(8,128)(2,1)} %get-tuple-element.473), channel_id=1, source_target_pairs={{0,2},{1,3},{2,0},{3,1},{4,6},{5,7},{6,4},{7,5},{8,10},{9,11},{10,... | collective-permute-start | bytes 3145736 | tf_op jit(solution)/shard_map/ppermute | solution.py:43
  62.3 369.1 %all-gather.11.cloned.1.call-start = ((), (), s32[]{:S(2)}) async-start(), calls=%async_computation.10 | async-start | bytes 5242880 | tf_op jit(solution)/shard_map/all_gather | solution.py:271
  62.4 60.4 %copy-start.49 = (bf16[1,512,1024]{2,1,0:T(8,128)(2,1)S(1)}, bf16[1,512,1024]{2,1,0:T(8,128)(2,1)}, u32[]{:S(2)}) copy-start(bf16[1,512,1024]{2,1,0:T(8,128)(2,1)} %copy-done.48) | copy-start | bytes 3145732
  128.8 56.6 %collective-permute-start.2 = (bf16[2,512,2048]{2,1,0:T(8,128)(2,1)}, bf16[2,512,2048]{2,1,0:T(8,128)(2,1)}, u32[]{:S(2)}, u32[]{:S(2)}) collective-permute-start(bf16[2,512,2048]{2,1,0:T(8,128)(2,1)} %pad_maximum_fusion.6), channel_id=1, source_target_pairs={{0,1},{1,0},{2,3},{3,2},{4,5},{5,4},{6,7},{7,6},{8,9},{9,8},{10,11... | collective-permute-start | bytes 12582920 | tf_op jit(solution)/shard_map/ppermute | solution.py:43
  129.0 48.1 %collective-permute-start.4 = (bf16[512,2048]{1,0:T(8,128)(2,1)S(1)}, bf16[512,2048]{1,0:T(8,128)(2,1)S(1)}, u32[]{:S(2)}, u32[]{:S(2)}) collective-permute-start(bf16[512,2048]{1,0:T(8,128)(2,1)S(1)} %pad_maximum_fusion.17), channel_id=1, source_target_pairs={{0,4},{4,0},{1,5},{5,1},{2,6},{6,2},{3,7},{7,3},{8,12},{12,8},{9,1... | collective-permute-start | bytes 6291464 | tf_op jit(solution)/shard_map/ppermute | solution.py:43
  181.6 13.2 collective-permute-start.5
  185.4 146.0 %copy-start.55 = (f32[2048,64]{0,1:T(8,128)}, f32[2048,64]{0,1:T(8,128)S(1)}, u32[]{:S(2)}) copy-start(f32[2048,64]{0,1:T(8,128)S(1)} %get-tuple-element.486) | copy-start | bytes 1572868
  348.9 596.3 %all-gather.9.cloned.1.call-start = ((), (), s32[]{:S(2)}) async-start(), calls=%async_computation.5 | async-start | bytes 28180480 | tf_op jit(solution)/shard_map/all_gather | solution.py:273
  448.2 169.1 %collective-permute-start.6 = (bf16[2,2048,1024]{2,1,0:T(8,128)(2,1)}, bf16[2,2048,1024]{2,1,0:T(8,128)(2,1)}, u32[]{:S(2)}, u32[]{:S(2)}) collective-permute-start(bf16[2,2048,1024]{2,1,0:T(8,128)(2,1)} %pad_maximum_fusion.1), channel_id=1, source_target_pairs={{0,1},{1,0},{2,3},{3,2},{4,5},{5,4},{6,7},{7,6},{8,9},{9,8},{10,11... | collective-permute-start | bytes 25165832 | tf_op jit(solution)/shard_map/ppermute | solution.py:43
  453.9 707.6 %all-gather.13.cloned.1.call-start = ((), (), s32[]{:S(2)}) async-start(), calls=%async_computation.11 | async-start | bytes 14090240 | tf_op jit(solution)/shard_map/all_gather | solution.py:275
  455.6 25.6 collective-permute-start.22
  481.4 71.9 %copy-start.46 = (bf16[1,512,1024]{2,1,0:T(8,128)(2,1)}, bf16[1,512,1024]{2,1,0:T(8,128)(2,1)S(1)}, u32[]{:S(2)}) copy-start(bf16[1,512,1024]{2,1,0:T(8,128)(2,1)S(1)} %get-tuple-element.383) | copy-start | bytes 3145732
  483.1 77.8 %collective-permute-start.23 = (bf16[2,512,1024]{2,1,0:T(8,128)(2,1)}, bf16[2,512,1024]{2,1,0:T(8,128)(2,1)}, u32[]{:S(2)}, u32[]{:S(2)}) collective-permute-start(bf16[2,512,1024]{2,1,0:T(8,128)(2,1)} %pad_maximum_fusion.22), channel_id=1, source_target_pairs={{0,2},{1,3},{2,0},{3,1},{4,6},{5,7},{6,4},{7,5},{8,10},{9,11},{10,... | collective-permute-start | bytes 6291464 | tf_op jit(solution)/shard_map/ppermute | solution.py:43
  484.6 72.7 %copy-start.88 = (bf16[1024]{0:T(1024)(128)(2,1)S(1)}, bf16[1024]{0:T(1024)(128)(2,1)}, u32[]{:S(2)}) copy-start(bf16[1024]{0:T(1024)(128)(2,1)} %param.16) | copy-start | bytes 6148
  484.6 68.5 %collective-permute-start.25 = (bf16[1,512,1024]{2,1,0:T(8,128)(2,1)S(1)}, bf16[1,512,1024]{2,1,0:T(8,128)(2,1)S(1)}, u32[]{:S(2)}, u32[]{:S(2)}) collective-permute-start(bf16[1,512,1024]{2,1,0:T(8,128)(2,1)S(1)} %get-tuple-element.431), channel_id=1, source_target_pairs={{0,2},{1,3},{2,0},{3,1},{4,6},{5,7},{6,4},{7,5},{8,10},{9,11},{10,... | collective-permute-start | bytes 3145736 | tf_op jit(solution)/shard_map/ppermute | solution.py:43
  555.8 46.9 %collective-permute-start.26 = (bf16[512,2048]{1,0:T(8,128)(2,1)}, bf16[512,2048]{1,0:T(8,128)(2,1)}, u32[]{:S(2)}, u32[]{:S(2)}) collective-permute-start(bf16[512,2048]{1,0:T(8,128)(2,1)} %pad_maximum_fusion.23), channel_id=1, source_target_pairs={{0,4},{4,0},{1,5},{5,1},{2,6},{6,2},{3,7},{7,3},{8,12},{12,8},{9,1... | collective-permute-start | bytes 6291464 | tf_op jit(solution)/shard_map/ppermute | solution.py:43
  557.3 160.0 %copy-start.79 = (f32[1024]{0:T(1024)}, f32[1024]{0:T(1024)S(1)}, u32[]{:S(2)}) copy-start(f32[1024]{0:T(1024)S(1)} %convert_element_type.326) | copy-start | bytes 12292
  566.0 65.1 %collective-permute-start.24 = (bf16[2,512,2048]{2,1,0:T(8,128)(2,1)}, bf16[2,512,2048]{2,1,0:T(8,128)(2,1)}, u32[]{:S(2)}, u32[]{:S(2)}) collective-permute-start(bf16[2,512,2048]{2,1,0:T(8,128)(2,1)} %pad_maximum_fusion.10), channel_id=1, source_target_pairs={{0,1},{1,0},{2,3},{3,2},{4,5},{5,4},{6,7},{7,6},{8,9},{9,8},{10,11... | collective-permute-start | bytes 12582920 | tf_op jit(solution)/shard_map/ppermute | solution.py:43
  608.7 114.5 %collective-permute-start.27 = (bf16[2,512,2048]{2,1,0:T(8,128)(2,1)}, bf16[2,512,2048]{2,1,0:T(8,128)(2,1)}, u32[]{:S(2)}, u32[]{:S(2)}) collective-permute-start(bf16[2,512,2048]{2,1,0:T(8,128)(2,1)} %pad_maximum_fusion.11), channel_id=1, source_target_pairs={{0,1},{1,0},{2,3},{3,2},{4,5},{5,4},{6,7},{7,6},{8,9},{9,8},{10,11... | collective-permute-start | bytes 12582920 | tf_op jit(solution)/shard_map/ppermute | solution.py:43
  627.8 48.4 %collective-permute-start.7 = (bf16[2,1,512,1024]{3,2,1,0:T(8,128)(2,1)}, bf16[2,1,512,1024]{3,2,1,0:T(8,128)(2,1)}, u32[]{:S(2)}, u32[]{:S(2)}) collective-permute-start(bf16[2,1,512,1024]{3,2,1,0:T(8,128)(2,1)} %fusion.85), channel_id=1, source_target_pairs={{0,4},{4,0},{1,5},{5,1},{2,6},{6,2},{3,7},{7,3},{8,12},{12,8},{9,1... | collective-permute-start | bytes 6291464 | tf_op jit(solution)/shard_map/ppermute | solution.py:43
  629.6 50.9 %collective-permute-start.9 = (bf16[1,2,512,1024]{3,2,1,0:T(8,128)(2,1)S(1)}, bf16[1,2,512,1024]{3,2,1,0:T(8,128)(2,1)}, u32[]{:S(2)}, u32[]{:S(2)}) collective-permute-start(bf16[1,2,512,1024]{3,2,1,0:T(8,128)(2,1)S(1)} %fusion.86), channel_id=1, source_target_pairs={{0,2},{1,3},{2,0},{3,1},{4,6},{5,7},{6,4},{7,5},{8,10},{9,11},{10,... | collective-permute-start | bytes 6291464 | tf_op jit(solution)/shard_map/ppermute | solution.py:43
  678.9 24.9 collective-permute-start.8
  683.1 24.6 collective-permute-start.10
  720.1 24.6 collective-permute-start.11
  745.2 72.1 %collective-permute-start.12 = (bf16[2,512,1024]{2,1,0:T(8,128)(2,1)S(1)}, bf16[2,512,1024]{2,1,0:T(8,128)(2,1)S(1)}, u32[]{:S(2)}, u32[]{:S(2)}) collective-permute-start(bf16[2,512,1024]{2,1,0:T(8,128)(2,1)S(1)} %pad_maximum_fusion.20), channel_id=1, source_target_pairs={{0,2},{1,3},{2,0},{3,1},{4,6},{5,7},{6,4},{7,5},{8,10},{9,11},{10,... | collective-permute-start | bytes 6291464 | tf_op jit(solution)/shard_map/ppermute | solution.py:43
  745.7 68.1 %collective-permute-start.14 = (bf16[1,512,1024]{2,1,0:T(8,128)(2,1)S(1)}, bf16[1,512,1024]{2,1,0:T(8,128)(2,1)S(1)}, u32[]{:S(2)}, u32[]{:S(2)}) collective-permute-start(bf16[1,512,1024]{2,1,0:T(8,128)(2,1)S(1)} %get-tuple-element.452), channel_id=1, source_target_pairs={{0,2},{1,3},{2,0},{3,1},{4,6},{5,7},{6,4},{7,5},{8,10},{9,11},{10,... | collective-permute-start | bytes 3145736 | tf_op jit(solution)/shard_map/ppermute | solution.py:43
  814.2 45.4 %collective-permute-start.15 = (bf16[512,2048]{1,0:T(8,128)(2,1)S(1)}, bf16[512,2048]{1,0:T(8,128)(2,1)S(1)}, u32[]{:S(2)}, u32[]{:S(2)}) collective-permute-start(bf16[512,2048]{1,0:T(8,128)(2,1)S(1)} %pad_maximum_fusion.21), channel_id=1, source_target_pairs={{0,4},{4,0},{1,5},{5,1},{2,6},{6,2},{3,7},{7,3},{8,12},{12,8},{9,1... | collective-permute-start | bytes 6291464 | tf_op jit(solution)/shard_map/ppermute | solution.py:43
  820.6 107.9 %collective-permute-start.13 = (bf16[2,512,2048]{2,1,0:T(8,128)(2,1)}, bf16[2,512,2048]{2,1,0:T(8,128)(2,1)}, u32[]{:S(2)}, u32[]{:S(2)}) collective-permute-start(bf16[2,512,2048]{2,1,0:T(8,128)(2,1)} %pad_maximum_fusion.8), channel_id=1, source_target_pairs={{0,1},{1,0},{2,3},{3,2},{4,5},{5,4},{6,7},{7,6},{8,9},{9,8},{10,11... | collective-permute-start | bytes 12582920 | tf_op jit(solution)/shard_map/ppermute | solution.py:43
  863.6 74.7 %collective-permute-start.16 = (bf16[2,512,2048]{2,1,0:T(8,128)(2,1)}, bf16[2,512,2048]{2,1,0:T(8,128)(2,1)}, u32[]{:S(2)}, u32[]{:S(2)}) collective-permute-start(bf16[2,512,2048]{2,1,0:T(8,128)(2,1)} %pad_maximum_fusion.9), channel_id=1, source_target_pairs={{0,1},{1,0},{2,3},{3,2},{4,5},{5,4},{6,7},{7,6},{8,9},{9,8},{10,11... | collective-permute-start | bytes 12582920 | tf_op jit(solution)/shard_map/ppermute | solution.py:43
  945.2 1436.2 %reduce-scatter.11.cloned.1.call-start = ((), (), s32[]{:S(2)}) async-start(), calls=%async_computation.9 | async-start | bytes 14090240 | tf_op jit(solution)/shard_map/reduce_scatter | solution.py:162
  1277.3 77.6 %collective-permute-start.28 = (bf16[2,2048,1024]{2,1,0:T(8,128)(2,1)}, bf16[2,2048,1024]{2,1,0:T(8,128)(2,1)}, u32[]{:S(2)}, u32[]{:S(2)}) collective-permute-start(bf16[2,2048,1024]{2,1,0:T(8,128)(2,1)} %pad_maximum_fusion.3), channel_id=1, source_target_pairs={{0,1},{1,0},{2,3},{3,2},{4,5},{5,4},{6,7},{7,6},{8,9},{9,8},{10,11... | collective-permute-start | bytes 25165832 | tf_op jit(solution)/shard_map/ppermute | solution.py:43
  1295.4 76.3 %collective-permute-start.17 = (bf16[2,2048,1024]{2,1,0:T(8,128)(2,1)}, bf16[2,2048,1024]{2,1,0:T(8,128)(2,1)}, u32[]{:S(2)}, u32[]{:S(2)}) collective-permute-start(bf16[2,2048,1024]{2,1,0:T(8,128)(2,1)} %pad_maximum_fusion.2), channel_id=1, source_target_pairs={{0,1},{1,0},{2,3},{3,2},{4,5},{5,4},{6,7},{7,6},{8,9},{9,8},{10,11... | collective-permute-start | bytes 25165832 | tf_op jit(solution)/shard_map/ppermute | solution.py:43
  1369.2 48.7 %collective-permute-start.29 = (bf16[2,1,512,1024]{3,2,1,0:T(8,128)(2,1)}, bf16[2,1,512,1024]{3,2,1,0:T(8,128)(2,1)}, u32[]{:S(2)}, u32[]{:S(2)}) collective-permute-start(bf16[2,1,512,1024]{3,2,1,0:T(8,128)(2,1)} %fusion.89), channel_id=1, source_target_pairs={{0,4},{4,0},{1,5},{5,1},{2,6},{6,2},{3,7},{7,3},{8,12},{12,8},{9,1... | collective-permute-start | bytes 6291464 | tf_op jit(solution)/shard_map/ppermute | solution.py:43
  1371.0 50.5 %collective-permute-start.31 = (bf16[1,2,512,1024]{3,2,1,0:T(8,128)(2,1)S(1)}, bf16[1,2,512,1024]{3,2,1,0:T(8,128)(2,1)}, u32[]{:S(2)}, u32[]{:S(2)}) collective-permute-start(bf16[1,2,512,1024]{3,2,1,0:T(8,128)(2,1)S(1)} %fusion.90), channel_id=1, source_target_pairs={{0,2},{1,3},{2,0},{3,1},{4,6},{5,7},{6,4},{7,5},{8,10},{9,11},{10,... | collective-permute-start | bytes 6291464 | tf_op jit(solution)/shard_map/ppermute | solution.py:43
  1387.7 75.1 %collective-permute-start.18 = (bf16[2,1,512,1024]{3,2,1,0:T(8,128)(2,1)}, bf16[2,1,512,1024]{3,2,1,0:T(8,128)(2,1)}, u32[]{:S(2)}, u32[]{:S(2)}) collective-permute-start(bf16[2,1,512,1024]{3,2,1,0:T(8,128)(2,1)} %fusion.87), channel_id=1, source_target_pairs={{0,4},{4,0},{1,5},{5,1},{2,6},{6,2},{3,7},{7,3},{8,12},{12,8},{9,1... | collective-permute-start | bytes 6291464 | tf_op jit(solution)/shard_map/ppermute | solution.py:43
  1391.2 76.3 %collective-permute-start.20 = (bf16[1,2,512,1024]{3,2,1,0:T(8,128)(2,1)S(1)}, bf16[1,2,512,1024]{3,2,1,0:T(8,128)(2,1)}, u32[]{:S(2)}, u32[]{:S(2)}) collective-permute-start(bf16[1,2,512,1024]{3,2,1,0:T(8,128)(2,1)S(1)} %fusion.88), channel_id=1, source_target_pairs={{0,2},{1,3},{2,0},{3,1},{4,6},{5,7},{6,4},{7,5},{8,10},{9,11},{10,... | collective-permute-start | bytes 6291464 | tf_op jit(solution)/shard_map/ppermute | solution.py:43
  1420.7 66.3 %collective-permute-start.30 = (bf16[1,1,512,1024]{3,2,1,0:T(8,128)(2,1)S(1)}, bf16[1,1,512,1024]{3,2,1,0:T(8,128)(2,1)}, u32[]{:S(2)}, u32[]{:S(2)}) collective-permute-start(bf16[1,1,512,1024]{3,2,1,0:T(8,128)(2,1)S(1)} %dynamic-slice_convert_fusion.11), channel_id=1, source_target_pairs={{0,2},{1,3},{2,0},{3,1},{4,6},{5,7},{6,4},{7,5},{8,10},{9,11},{10,... | collective-permute-start | bytes 3145736 | tf_op jit(solution)/shard_map/ppermute | solution.py:43
  1425.4 63.2 %collective-permute-start.32 = (bf16[1,1,512,1024]{3,2,1,0:T(8,128)(2,1)}, bf16[1,1,512,1024]{3,2,1,0:T(8,128)(2,1)}, u32[]{:S(2)}, u32[]{:S(2)}) collective-permute-start(bf16[1,1,512,1024]{3,2,1,0:T(8,128)(2,1)} %dynamic-slice_convert_fusion.10), channel_id=1, source_target_pairs={{0,4},{4,0},{1,5},{5,1},{2,6},{6,2},{3,7},{7,3},{8,12},{12,8},{9,1... | collective-permute-start | bytes 3145736 | tf_op jit(solution)/shard_map/ppermute | solution.py:43
  1466.9 44.1 %collective-permute-start.19 = (bf16[1,1,512,1024]{3,2,1,0:T(8,128)(2,1)}, bf16[1,1,512,1024]{3,2,1,0:T(8,128)(2,1)}, u32[]{:S(2)}, u32[]{:S(2)}) collective-permute-start(bf16[1,1,512,1024]{3,2,1,0:T(8,128)(2,1)} %dynamic-slice_convert_fusion.13), channel_id=1, source_target_pairs={{0,2},{1,3},{2,0},{3,1},{4,6},{5,7},{6,4},{7,5},{8,10},{9,11},{10,... | collective-permute-start | bytes 3145736 | tf_op jit(solution)/shard_map/ppermute | solution.py:43
  1471.4 42.1 %collective-permute-start.21 = (bf16[1,1,512,1024]{3,2,1,0:T(8,128)(2,1)}, bf16[1,1,512,1024]{3,2,1,0:T(8,128)(2,1)}, u32[]{:S(2)}, u32[]{:S(2)}) collective-permute-start(bf16[1,1,512,1024]{3,2,1,0:T(8,128)(2,1)} %dynamic-slice_convert_fusion.12), channel_id=1, source_target_pairs={{0,4},{4,0},{1,5},{5,1},{2,6},{6,2},{3,7},{7,3},{8,12},{12,8},{9,1... | collective-permute-start | bytes 3145736 | tf_op jit(solution)/shard_map/ppermute | solution.py:43
  1522.8 24.3 collective-permute-start.33
  1550.0 68.6 %collective-permute-start.34 = (bf16[2,512,1024]{2,1,0:T(8,128)(2,1)}, bf16[2,512,1024]{2,1,0:T(8,128)(2,1)}, u32[]{:S(2)}, u32[]{:S(2)}) collective-permute-start(bf16[2,512,1024]{2,1,0:T(8,128)(2,1)} %pad_maximum_fusion.24), channel_id=1, source_target_pairs={{0,2},{1,3},{2,0},{3,1},{4,6},{5,7},{6,4},{7,5},{8,10},{9,11},{10,... | collective-permute-start | bytes 6291464 | tf_op jit(solution)/shard_map/ppermute | solution.py:43
  1587.5 815.6 %reduce-scatter.7.cloned.1.call-start = ((), (), s32[]{:S(2)}) async-start(), calls=%async_computation.7 | async-start | bytes 5242880 | tf_op jit(solution)/shard_map/reduce_scatter | solution.py:162
  1587.6 30.8 %collective-permute-start.36 = (bf16[1,512,1024]{2,1,0:T(8,128)(2,1)}, bf16[1,512,1024]{2,1,0:T(8,128)(2,1)S(1)}, u32[]{:S(2)}, u32[]{:S(2)}) collective-permute-start(bf16[1,512,1024]{2,1,0:T(8,128)(2,1)} %get-tuple-element.410), channel_id=1, source_target_pairs={{0,2},{1,3},{2,0},{3,1},{4,6},{5,7},{6,4},{7,5},{8,10},{9,11},{10,... | collective-permute-start | bytes 3145736 | tf_op jit(solution)/shard_map/ppermute | solution.py:43
  1621.7 50.1 %collective-permute-start.35 = (bf16[2,512,2048]{2,1,0:T(8,128)(2,1)S(1)}, bf16[2,512,2048]{2,1,0:T(8,128)(2,1)S(1)}, u32[]{:S(2)}, u32[]{:S(2)}) collective-permute-start(bf16[2,512,2048]{2,1,0:T(8,128)(2,1)S(1)} %pad_maximum_fusion.13), channel_id=1, source_target_pairs={{0,1},{1,0},{2,3},{3,2},{4,5},{5,4},{6,7},{7,6},{8,9},{9,8},{10,11... | collective-permute-start | bytes 12582920 | tf_op jit(solution)/shard_map/ppermute | solution.py:43
  1622.0 48.1 %collective-permute-start.37 = (bf16[512,2048]{1,0:T(8,128)(2,1)S(1)}, bf16[512,2048]{1,0:T(8,128)(2,1)S(1)}, u32[]{:S(2)}, u32[]{:S(2)}) collective-permute-start(bf16[512,2048]{1,0:T(8,128)(2,1)S(1)} %pad_maximum_fusion.25), channel_id=1, source_target_pairs={{0,4},{4,0},{1,5},{5,1},{2,6},{6,2},{3,7},{7,3},{8,12},{12,8},{9,1... | collective-permute-start | bytes 6291464 | tf_op jit(solution)/shard_map/ppermute | solution.py:43
  1671.7 7.2 collective-permute-start.38
  1806.7 678.7 %reduce-scatter.9.cloned.1.call-start = ((), (), s32[]{:S(2)}) async-start(), calls=%async_computation.8 | async-start | bytes 28180480 | tf_op jit(solution)/shard_map/reduce_scatter | solution.py:162
  1881.9 643.1 %reduce-scatter.5.cloned.1.call-start = ((), (), s32[]{:S(2)}) async-start(), calls=%async_computation.6 | async-start | bytes 15728640 | tf_op jit(solution)/shard_map/reduce_scatter | solution.py:162
  2358.6 26.3 collective-permute-start.39
  2382.9 33.8 %collective-permute-start.47 = (bf16[1376,512]{1,0:T(8,128)(2,1)S(1)}, bf16[1376,512]{1,0:T(8,128)(2,1)S(1)}, u32[]{:S(2)}, u32[]{:S(2)}) collective-permute-start(bf16[1376,512]{1,0:T(8,128)(2,1)S(1)} %dynamic-slice_bitcast_fusion.2), channel_id=1, source_target_pairs={{0,4},{4,0},{1,5},{5,1},{2,6},{6,2},{3,7},{7,3},{8,12},{12,8},{9,1... | collective-permute-start | bytes 4227080 | tf_op jit(solution)/shard_map/ppermute | solution.py:43
  2399.0 75.3 %collective-permute-start.40 = (bf16[2,1,512,1024]{3,2,1,0:T(8,128)(2,1)}, bf16[2,1,512,1024]{3,2,1,0:T(8,128)(2,1)}, u32[]{:S(2)}, u32[]{:S(2)}) collective-permute-start(bf16[2,1,512,1024]{3,2,1,0:T(8,128)(2,1)} %fusion.91), channel_id=1, source_target_pairs={{0,4},{4,0},{1,5},{5,1},{2,6},{6,2},{3,7},{7,3},{8,12},{12,8},{9,1... | collective-permute-start | bytes 6291464 | tf_op jit(solution)/shard_map/ppermute | solution.py:43
  2403.1 74.5 %collective-permute-start.42 = (bf16[1,2,512,1024]{3,2,1,0:T(8,128)(2,1)}, bf16[1,2,512,1024]{3,2,1,0:T(8,128)(2,1)}, u32[]{:S(2)}, u32[]{:S(2)}) collective-permute-start(bf16[1,2,512,1024]{3,2,1,0:T(8,128)(2,1)} %fusion.92), channel_id=1, source_target_pairs={{0,2},{1,3},{2,0},{3,1},{4,6},{5,7},{6,4},{7,5},{8,10},{9,11},{10,... | collective-permute-start | bytes 6291464 | tf_op jit(solution)/shard_map/ppermute | solution.py:43
  2404.1 68.2 %collective-permute-start.45 = (bf16[512,512]{1,0:T(8,128)(2,1)S(1)}, bf16[512,512]{1,0:T(8,128)(2,1)S(1)}, u32[]{:S(2)}, u32[]{:S(2)}) collective-permute-start(bf16[512,512]{1,0:T(8,128)(2,1)S(1)} %dynamic-slice_bitcast_fusion.3), channel_id=1, source_target_pairs={{0,4},{4,0},{1,5},{5,1},{2,6},{6,2},{3,7},{7,3},{8,12},{12,8},{9,1... | collective-permute-start | bytes 1572872 | tf_op jit(solution)/shard_map/ppermute | solution.py:43
  2416.7 57.5 %slice-start = ((s8[8388608]{0:T(1024)(128)(4,1)}), s8[4194304]{0:T(1024)(128)(4,1)S(1)}, s32[]{:S(2)}) async-start(s8[8388608]{0:T(1024)(128)(4,1)} %bitcast.503), calls=%async_computation.12 | async-start | bytes 8388608
  2477.5 54.2 %collective-permute-start.41 = (bf16[1,1,512,1024]{3,2,1,0:T(8,128)(2,1)S(1)}, bf16[1,1,512,1024]{3,2,1,0:T(8,128)(2,1)}, u32[]{:S(2)}, u32[]{:S(2)}) collective-permute-start(bf16[1,1,512,1024]{3,2,1,0:T(8,128)(2,1)S(1)} %dynamic-slice_convert_fusion.9), channel_id=1, source_target_pairs={{0,2},{1,3},{2,0},{3,1},{4,6},{5,7},{6,4},{7,5},{8,10},{9,11},{10,... | collective-permute-start | bytes 3145736 | tf_op jit(solution)/shard_map/ppermute | solution.py:43
  2483.8 50.4 %collective-permute-start.43 = (bf16[1,1,512,1024]{3,2,1,0:T(8,128)(2,1)}, bf16[1,1,512,1024]{3,2,1,0:T(8,128)(2,1)}, u32[]{:S(2)}, u32[]{:S(2)}) collective-permute-start(bf16[1,1,512,1024]{3,2,1,0:T(8,128)(2,1)} %dynamic-slice_convert_fusion.8), channel_id=1, source_target_pairs={{0,4},{4,0},{1,5},{5,1},{2,6},{6,2},{3,7},{7,3},{8,12},{12,8},{9,1... | collective-permute-start | bytes 3145736 | tf_op jit(solution)/shard_map/ppermute | solution.py:43
  2488.9 152.3 %collective-permute-start.46 = (bf16[512,2752]{0,1:T(8,128)(2,1)}, bf16[512,2752]{0,1:T(8,128)(2,1)}, u32[]{:S(2)}, u32[]{:S(2)}) collective-permute-start(bf16[512,2752]{0,1:T(8,128)(2,1)} %dynamic-slice_bitcast_fusion.1), channel_id=1, source_target_pairs={{0,4},{4,0},{1,5},{5,1},{2,6},{6,2},{3,7},{7,3},{8,12},{12,8},{9,1... | collective-permute-start | bytes 8454152 | tf_op jit(solution)/shard_map/ppermute | solution.py:43
  2530.1 98.8 %collective-permute-start.44 = (bf16[512,1536]{0,1:T(8,128)(2,1)}, bf16[512,1536]{0,1:T(8,128)(2,1)}, u32[]{:S(2)}, u32[]{:S(2)}) collective-permute-start(bf16[512,1536]{0,1:T(8,128)(2,1)} %bitcast.565), channel_id=1, source_target_pairs={{0,4},{4,0},{1,5},{5,1},{2,6},{6,2},{3,7},{7,3},{8,12},{12,8},{9,1... | collective-permute-start | bytes 4718600 | tf_op jit(solution)/shard_map/ppermute | solution.py:43
  2536.6 84.1 %copy-start.85 = (f32[1024]{0:T(1024)S(1)}, f32[1024]{0:T(1024)}, u32[]{:S(2)}) copy-start(f32[1024]{0:T(1024)} %get-tuple-element.487) | copy-start | bytes 12292
  (105 other events, 1174.4 us)
Sparse Core Ops, SparseCore 0:
  62.5 219.5 all-gather.6
  349.0 82.3 all-gather.10
  454.1 381.1 all-gather.8
  945.4 194.4 all-gather.12
  1587.6 188.8 reduce-scatter.10
  1806.8 74.4 reduce-scatter.6
  1883.8 372.7 reduce-scatter.8
  2316.7 208.2 reduce-scatter.4

commit v2 on v0

v2 whole, which is shorter than its diff:
```python
import math

import jax
import jax.numpy as jnp
from jax import lax
from jax.experimental import pallas as pl
from jax.experimental.layout import Layout, with_layout_constraint
from jax.experimental.pallas import tpu as pltpu
from jax.sharding import PartitionSpec as P

D = 4096
HD = 128
BF = jnp.bfloat16
F32 = jnp.float32
rms_epsilon = 1e-05
NT = (((1,), (1,)), ((), ()))
LOG2E = 1.4426950408889634


def mm(left, right, dims=(((1,), (0,)), ((), ()))):
    return lax.dot_general(left, right, dims, preferred_element_type=F32)


def turn(values, cosine, sine):
    return values * cosine + pltpu.roll(values, HD // 2, 1) * sine


def rope_tables(seq_len):
    half_width = HD // 2
    inv_freq = jnp.exp(-math.log(10000.0) * jnp.arange(half_width, dtype=F32) * 2.0 / HD)
    angles = jnp.arange(seq_len, dtype=F32)[:, None] * inv_freq[None, :]
    cosine, sine = jnp.cos(angles), jnp.sin(angles)
    return jnp.concatenate([cosine, cosine], axis=1), jnp.concatenate([-sine, sine], axis=1)


def attend_forward(query_proj, key_proj, value_proj, cosine, sine):
    seq_len = query_proj.shape[0]
    heads = query_proj.shape[1] // HD
    block = min(512, seq_len)
    blocks = seq_len // block
    scale = LOG2E / math.sqrt(HD)

    def kernel(q_in, k_in, v_in, cos_q, sin_q, cos_k, sin_k, q_out, k_out, v_out, out, norm, vt):
        i = pl.program_id(1)

        @pl.when(i == 0)
        def _():
            for j in range(blocks):
                rows = pl.ds(j * block, block)
                k_out[rows, :] = turn(k_in[rows, :], cos_k[rows, :], sin_k[rows, :]).astype(BF)
                v_out[rows, :] = v_in[rows, :].astype(BF)
                vt[j] = v_in[rows, :].T.astype(BF)

        q_out[...] = turn(q_in[...], cos_q[...], sin_q[...]).astype(BF)
        query = q_out[...]

        def step(j, carry, diagonal):
            top, total, mixed = carry
            rows = pl.ds(pl.multiple_of(j * block, block), block)
            scores = mm(k_out[rows, :], query, NT) * scale
            if diagonal:
                key_at = lax.broadcasted_iota(jnp.int32, scores.shape, 0)
                query_at = lax.broadcasted_iota(jnp.int32, scores.shape, 1)
                scores = jnp.where(key_at <= query_at, scores, -1e30)
            new_top = jnp.maximum(top, jnp.max(scores, axis=0, keepdims=True))
            expo = jnp.exp2(scores - new_top)
            fade = jnp.exp2(top - new_top)
            total = total * fade + jnp.sum(expo, axis=0, keepdims=True)
            mixed = mixed * fade + mm(vt[j], expo.astype(BF))
            return new_top, total, mixed

        carry = (
            jnp.full((1, block), -1e30, F32),
            jnp.zeros((1, block), F32),
            jnp.zeros((HD, block), F32),
        )
        carry = lax.fori_loop(0, i, lambda j, c: step(j, c, False), carry)
        top, total, mixed = step(i, carry, True)
        out[...] = (mixed / total).T.astype(BF)
        norm[0] = top + jnp.log2(total)

    row = pl.BlockSpec((block, HD), lambda h, i: (i, h))
    col = pl.BlockSpec((seq_len, HD), lambda h, i: (0, h))
    pos = pl.BlockSpec((block, HD), lambda h, i: (i, 0))
    all_pos = pl.BlockSpec((seq_len, HD), lambda h, i: (0, 0))
    wide = jax.ShapeDtypeStruct((seq_len, heads * HD), BF)
    pairs = heads * seq_len * (seq_len + block) // 2
    return pl.pallas_call(
        kernel,
        grid=(heads, blocks),
        in_specs=[row, col, col, pos, pos, all_pos, all_pos],
        out_specs=[row, col, col, row, pl.BlockSpec((1, 1, block), lambda h, i: (h, 0, i))],
        out_shape=[wide, wide, wide, wide, jax.ShapeDtypeStruct((heads, 1, seq_len), F32)],
        scratch_shapes=[pltpu.VMEM((blocks, HD, block), BF)],
        compiler_params=pltpu.CompilerParams(vmem_limit_bytes=48 << 20),
        cost_estimate=pl.CostEstimate(
            flops=4 * pairs * HD,
            transcendentals=pairs,
            bytes_accessed=seq_len * heads * HD * (12 + 8),
        ),
    )(query_proj, key_proj, value_proj, cosine, sine, cosine, sine)


def attend_backward(queries, keys, values, outs, norms, grads, cosine, sine):
    seq_len = queries.shape[0]
    heads = queries.shape[1] // HD
    block = min(512, seq_len)
    blocks = seq_len // block
    root = 1.0 / math.sqrt(HD)
    scale = LOG2E * root

    def kernel(q, k, v, o, g, norm, cos_q, sin_q, cos_k, sin_k, dq, dk, dv, kt, dk_sum, dv_sum):
        i = pl.program_id(1)

        @pl.when(i == 0)
        def _():
            for j in range(blocks):
                rows = pl.ds(j * block, block)
                kt[j] = k[rows, :].astype(F32).T.astype(BF)
            dk_sum[...] = jnp.zeros_like(dk_sum)
            dv_sum[...] = jnp.zeros_like(dv_sum)

        query = q[...]
        grad = g[...]
        dots = (grad.astype(F32) * o[...].astype(F32)).T
        weighted = jnp.sum(dots, axis=0, keepdims=True)
        level = norm[0]

        def step(j, total, diagonal):
            rows = pl.ds(pl.multiple_of(j * block, block), block)
            scores = mm(k[rows, :], query, NT) * scale
            probs = jnp.exp2(scores - level)
            if diagonal:
                key_at = lax.broadcasted_iota(jnp.int32, scores.shape, 0)
                query_at = lax.broadcasted_iota(jnp.int32, scores.shape, 1)
                probs = jnp.where(key_at <= query_at, probs, 0.0)
            dv_sum[rows, :] += mm(probs.astype(BF), grad)
            d_probs = mm(v[rows, :], grad, NT)
            d_scores = (probs * (d_probs - weighted)).astype(BF)
            dk_sum[rows, :] += mm(d_scores, query)
            return total + mm(kt[j], d_scores)

        total = lax.fori_loop(
            0, i, lambda j, c: step(j, c, False), jnp.zeros((HD, block), F32)
        )
        total = step(i, total, True)
        dq[...] = turn(total.T * root, cos_q[...], -sin_q[...]).astype(BF)

        @pl.when(i == blocks - 1)
        def _():
            for j in range(blocks):
                rows = pl.ds(j * block, block)
                dk[rows, :] = turn(
                    dk_sum[rows, :] * root, cos_k[rows, :], -sin_k[rows, :]
                ).astype(BF)
                dv[rows, :] = dv_sum[rows, :].astype(BF)

    row = pl.BlockSpec((block, HD), lambda h, i: (i, h))
    col = pl.BlockSpec((seq_len, HD), lambda h, i: (0, h))
    pos = pl.BlockSpec((block, HD), lambda h, i: (i, 0))
    all_pos = pl.BlockSpec((seq_len, HD), lambda h, i: (0, 0))
    wide = jax.ShapeDtypeStruct((seq_len, heads * HD), BF)
    pairs = heads * seq_len * (seq_len + block) // 2
    return pl.pallas_call(
        kernel,
        grid=(heads, blocks),
        in_specs=[row, col, col, row, row, pl.BlockSpec((1, 1, block), lambda h, i: (h, 0, i)),
                  pos, pos, all_pos, all_pos],
        out_specs=[row, col, col],
        out_shape=[wide, wide, wide],
        scratch_shapes=[
            pltpu.VMEM((blocks, HD, block), BF),
            pltpu.VMEM((seq_len, HD), F32),
            pltpu.VMEM((seq_len, HD), F32),
        ],
        compiler_params=pltpu.CompilerParams(vmem_limit_bytes=48 << 20),
        cost_estimate=pl.CostEstimate(
            flops=10 * pairs * HD,
            transcendentals=pairs,
            bytes_accessed=seq_len * heads * HD * 16,
        ),
    )(queries, keys, values, outs, grads, norms, cosine, sine, cosine, sine)


def row_total(values):
    return lax.psum(values, "tp")


def swap(values, axis, bit):
    step = 1 << bit
    return lax.ppermute(values, axis, [(i, i ^ step) for i in range(lax.axis_size(axis))])


def high_bits():
    return list(range(1, lax.axis_size("tp").bit_length() - 1))[::-1]


def gather_rows(values):
    rows, cols = values.shape
    half = rows // 2
    n_t, n_c = lax.axis_size("tp"), lax.axis_size("ctx")
    me_t, me_c = lax.axis_index("tp"), lax.axis_index("ctx")
    across = [("tp", b) for b in high_bits()]
    full = jnp.zeros((n_t, n_c * rows, cols), values.dtype)
    for part, plan in enumerate(([("ctx", 0)] + across, across + [("ctx", 0)])):
        held = {(0, 0): values[part * half : (part + 1) * half]}
        for axis, bit in plan + [("tp", 0)]:
            for (dc, dt), piece in list(held.items()):
                key = (1, dt) if axis == "ctx" else (dc, dt | (1 << bit))
                held[key] = swap(piece, axis, bit)
        for (dc, dt), piece in held.items():
            start = (me_t ^ dt, (me_c ^ dc) * rows + part * half, 0)
            full = lax.dynamic_update_slice(full, piece[None], start)
    return with_layout_constraint(full, Layout((0, 1, 2)))


def scatter_rows(block_of):
    n_t, n_c = lax.axis_size("tp"), lax.axis_size("ctx")
    me_t, me_c = lax.axis_index("tp"), lax.axis_index("ctx")
    sums = {}
    for dt in range(0, n_t, 2):
        got = swap(block_of(me_t ^ (dt + 1)).astype(BF), "tp", 0)
        sums[dt] = (block_of(me_t ^ dt) + got.astype(F32)).astype(BF)
    rows = sums[0].shape[0] // n_c
    cols = sums[0].shape[1]
    half = rows // 2
    across = [("tp", b) for b in high_bits()]
    done = []
    for part, plan in enumerate(([("ctx", 0)] + across, across + [("ctx", 0)])):
        held = {}
        for dt, total in sums.items():
            split = total.reshape(n_c, rows, cols)[:, part * half : (part + 1) * half]
            for dc in range(n_c):
                held[(dc, dt)] = lax.dynamic_index_in_dim(split, me_c ^ dc, 0, keepdims=False)
        for axis, bit in plan:
            left = {}
            for (dc, dt), piece in held.items():
                give = dc == 1 if axis == "ctx" else (dt >> bit) & 1
                if not give:
                    away = (1, dt) if axis == "ctx" else (dc, dt | (1 << bit))
                    got = swap(held[away].astype(BF), axis, bit)
                    left[(dc, dt)] = piece.astype(F32) + got.astype(F32)
            held = left
        done.append(held[(0, 0)])
    return jnp.concatenate(done, axis=0)


def ctx_half(weight, axis):
    size = weight.shape[axis] // lax.axis_size("ctx")
    return lax.dynamic_slice_in_dim(weight, lax.axis_index("ctx") * size, size, axis)


def after(value, token):
    value, _ = lax.optimization_barrier((value, token))
    return value


def owners(grad):
    return lax.psum_scatter(grad, "fsdp", scatter_dimension=0, tiled=False)


def spread(weight):
    return lax.all_gather(weight, "fsdp", axis=0, tiled=False)


def trade_ctx(block, axis):
    size = block.shape[axis] // lax.axis_size("ctx")
    me = lax.axis_index("ctx")
    own = lax.dynamic_slice_in_dim(block, me * size, size, axis)
    give = lax.dynamic_slice_in_dim(block, (1 - me) * size, size, axis)
    got = swap(give, "ctx", 0)
    return jnp.where(me == 0, own, got), jnp.where(me == 0, got, own)


def out_grad(block):
    return jnp.concatenate(trade_ctx(block, 1), axis=0).astype(F32)


def total_rows(values):
    values = values + swap(values, "ctx", 0)
    for bit in range(lax.axis_size("fsdp").bit_length() - 1):
        values = values + swap(values, "fsdp", bit)
    return values


def body(
    layer_input, attn_gain, qkv_weight, out_weight, ffn_gain, gate_up_weight, down_weight, cotangent
):
    n_f = lax.axis_size("fsdp")
    d_f = D // n_f
    qkv_parts = [spread(ctx_half(qkv_weight[:, i], 1)) for i in range(3)]
    out_full = spread(ctx_half(out_weight, 0))
    gu_full = spread(ctx_half(gate_up_weight, 2).reshape(d_f, -1))
    down_full = spread(ctx_half(down_weight, 0))

    def into(full, weight):
        return mm(full, weight, (((0, 2), (0, 1)), ((), ())))

    def back_out(full, weight):
        return mm(full, weight, (((0, 2), (0, 2)), ((), ())))

    def out_blocks(inner, weight):
        return lambda t: mm(inner, lax.dynamic_index_in_dim(weight, t, 0, keepdims=False))

    def in_blocks(grads, weight):
        return lambda t: mm(grads, lax.dynamic_index_in_dim(weight, t, 0, keepdims=False), NT)

    def in_part(full, grads):
        return mm(full, grads, (((1,), (0,)), ((), ()))).astype(BF)

    def out_part(inner, full):
        return jnp.stack(
            [mm(inner, full[t], (((0,), (0,)), ((), ()))).astype(BF) for t in range(n_f)]
        )

    input_float = layer_input.astype(F32)
    attn_scale = attn_gain.astype(F32)
    ffn_scale = ffn_gain.astype(F32)
    rms_one = lax.rsqrt(row_total(jnp.sum(input_float * input_float, axis=-1)) / D + rms_epsilon)[
        :, None
    ]
    normed_attn = (input_float * rms_one * attn_scale).astype(BF)
    attn_full = gather_rows(normed_attn)
    seq_len = attn_full.shape[1]
    cosine, sine = rope_tables(seq_len)
    cotan_full = gather_rows(after(cotangent, attn_full))
    proj = [into(attn_full, part) for part in qkv_parts]
    queries, keys, values, head_outs, norms = attend_forward(*proj, cosine, sine)
    resid = input_float + scatter_rows(out_blocks(head_outs, out_full))
    rms_two = lax.rsqrt(row_total(jnp.sum(resid * resid, axis=-1)) / D + rms_epsilon)[:, None]
    normed_ffn = (resid * rms_two * ffn_scale).astype(BF)
    ffn_full = gather_rows(normed_ffn)
    gate_up = into(ffn_full, gu_full)
    units = gate_up.shape[1] // 2
    gate = gate_up[:, :units]
    up_value = gate_up[:, units:]
    sigma = jax.nn.sigmoid(gate)
    hidden = (gate * sigma * up_value).astype(BF)
    down_part = out_part(hidden, cotan_full)
    down_sum = owners(down_part)
    down_full = after(down_full, down_part)
    grad_hidden = back_out(cotan_full, down_full)
    grad_gu = jnp.concatenate(
        [grad_hidden * up_value * sigma * (1.0 + gate * (1.0 - sigma)), grad_hidden * gate * sigma],
        axis=1,
    ).astype(BF)
    gu_part = in_part(ffn_full, grad_gu)
    gu_sum = owners(after(gu_part, down_sum))
    grad_nffn = after(scatter_rows(in_blocks(grad_gu, gu_full)), (gu_part, down_sum))
    ffn_term = grad_nffn * ffn_scale
    ffn_dot = row_total(jnp.sum(ffn_term * resid, axis=-1))[:, None]
    grad_resid = cotangent.astype(F32) + rms_two * ffn_term - resid * rms_two**3 * ffn_dot / D
    ffn_gain_part = jnp.sum(grad_nffn * resid * rms_two, axis=0)
    grad_branch = grad_resid.astype(BF)
    branch_full = gather_rows(grad_branch)
    grad_heads = back_out(branch_full, out_full).astype(BF)
    out_sum = owners(out_part(head_outs, branch_full))
    grad_proj = attend_backward(
        queries, keys, values, head_outs, norms, grad_heads, cosine, sine
    )
    qkv_part = [in_part(attn_full, grad) for grad in grad_proj]
    qkv_sum = [owners(part) for part in qkv_part]
    grad_nattn = scatter_rows(
        in_blocks(jnp.concatenate(grad_proj, axis=1), jnp.concatenate(qkv_parts, axis=2))
    )
    hidden = after(hidden, qkv_part)
    layer_output = (resid + scatter_rows(out_blocks(hidden, down_full))).astype(BF)
    attn_term = grad_nattn * attn_scale
    attn_dot = row_total(jnp.sum(attn_term * input_float, axis=-1))[:, None]
    grad_input = grad_resid + rms_one * attn_term - input_float * rms_one**3 * attn_dot / D
    attn_gain_part = jnp.sum(grad_nattn * input_float * rms_one, axis=0)
    gain_grads = total_rows(jnp.stack([attn_gain_part, ffn_gain_part]))

    down_grad = out_grad(down_sum)
    rows, other_rows = trade_ctx(gu_sum, 0)
    gu_grad = jnp.concatenate(
        [v.reshape(v.shape[0], 2, -1) for v in (rows, other_rows)], axis=2
    ).astype(F32)
    out_weight_grad = out_grad(out_sum)
    done = (down_grad, out_weight_grad, gu_grad, grad_input, layer_output, gain_grads)
    qkv_grad = []
    for part in qkv_sum:
        qkv_grad.append(jnp.concatenate(trade_ctx(after(part, done), 0), axis=1).astype(F32))
        done = done + (qkv_grad[-1],)
    qkv_grad = jnp.stack(qkv_grad, axis=1)

    return (
        layer_output,
        grad_input,
        gain_grads[0],
        qkv_grad,
        out_weight_grad,
        gain_grads[1],
        gu_grad,
        down_grad,
    )


def solution(mesh):
    return jax.shard_map(
        body,
        mesh=mesh,
        in_specs=(
            P(("fsdp", "ctx"), "tp"),
            P("tp"),
            P("fsdp", None, "tp"),
            P("tp", "fsdp"),
            P("tp"),
            P("fsdp", None, "tp"),
            P("tp", "fsdp"),
            P(("fsdp", "ctx"), "tp"),
        ),
        out_specs=(
            P(("fsdp", "ctx"), "tp"),
            P(("fsdp", "ctx"), "tp"),
            P("tp"),
            P(("fsdp", "ctx"), None, "tp"),
            P("tp", ("fsdp", "ctx")),
            P("tp"),
            P(("fsdp", "ctx"), None, "tp"),
            P("tp", ("fsdp", "ctx")),
        ),
        check_vma=False,
    )
```

time: 4570 us -> 1840 us (0.40)
  waiting for transfers between devices: 3220 us -> 887 us
  matrix products: 640 us -> 472 us
  local copies, waits for them, and re-layouts: 272 us -> 143 us
  blocking collectives: 180 us -> 53 us
  other arithmetic: 209 us -> 106 us
  Pallas kernels: 0 us -> 79.1 us
  starting transfers between devices: 11.5 us -> 79 us
    all_gather x8 -> x6, waiting for transfers between devices: 1680 us -> 294 us  [spread(): return lax.all_gather(weight, 'fsdp', axis=0, tiled=False)]
    reduce_scatter x8 -> x6, waiting for transfers between devices: 1420 us -> 116 us  [owners(): return lax.psum_scatter(grad, 'fsdp', scatter_dimension=0, tiled=False)]
    ppermute x0 -> x97, waiting for transfers between devices: none -> 477 us  [swap(): lax.ppermute(values, axis, [(i, i ^ step) for i in range(lax.axis_size(ax...]
    dot_general x40 -> x34, matrix products: 640 us -> 472 us  [mm(): return lax.dot_general(left, right, dims, preferred_element_type=F32)]
    all_to_all x2 -> x0, blocking collectives: 132 us -> none  [to_tokens(): lax.all_to_all(values, 'ctx', split_axis=0, concat_axis=2, tiled=True)]
    all_to_all x2 -> x0, waiting for transfers between devices: 117 us -> none  [to_heads(): lax.all_to_all(values, 'ctx', split_axis=2, concat_axis=0, tiled=True)]
    pallas_call x0 -> x2, Pallas kernels: none -> 79.1 us  [the longest x1 44 us: attend_backward(): pl.pallas_call(kernel, grid=(heads, blocks), in_specs=[row, col, col, row...]
    ppermute x0 -> x97, starting transfers between devices: none -> 78.5 us  [swap(): lax.ppermute(values, axis, [(i, i ^ step) for i in range(lax.axis_size(ax...]
  transfers between devices with their start and end apart: 18 -> 109, of which waited for: 15 -> 40; matrix products, arithmetic and copies ran while one was open for 20% -> 38% of each run, Pallas kernels for 0% -> 4%
where the time goes in v2:
time: 1840 us
  waiting for transfers between devices  887 us (48%)
  matrix products  472 us (26%)
  local copies, waits for them, and re-layouts  143 us (8%)
  other arithmetic  106 us (6%)
  Pallas kernels  79.1 us (4%)
  starting transfers between devices  79 us (4%)
  blocking collectives  53 us (3%)
    ppermute x97, waiting for transfers between devices, swap(): lax.ppermute(values, axis, [(i, i ^ step) for i in range(lax.axis_size(ax...  477 us
    dot_general x34, matrix products, mm(): return lax.dot_general(left, right, dims, preferred_element_type=F32)  472 us
    all_gather x6, waiting for transfers between devices, spread(): return lax.all_gather(weight, 'fsdp', axis=0, tiled=False)  294 us
    reduce_scatter x6, waiting for transfers between devices, owners(): return lax.psum_scatter(grad, 'fsdp', scatter_dimension=0, tiled=False)  116 us
    ppermute x97, starting transfers between devices, swap(): lax.ppermute(values, axis, [(i, i ^ step) for i in range(lax.axis_size(ax...  78.5 us
    dynamic_update_slice x64, local copies, waits for them, and re-layouts, gather_rows(): full = lax.dynamic_update_slice(full, piece[None], start)  69.6 us
    psum x4, blocking collectives, row_total(): return lax.psum(values, 'tp')  53 us
    pallas_call x1, Pallas kernels, attend_backward(): pl.pallas_call(kernel, grid=(heads, blocks), in_specs=[row, col, col, row...  44 us
  transfers between devices with their start and end apart: 109, of which 40 were waited for; matrix products, arithmetic and copies ran while one was open for 38% of the time, Pallas kernels for 4%

profile of v2, /device:TPU:0, one launch (start us, length us, event | category | flops | bytes accessed | tf_op | source)
XLA Modules:
  0.0 1835.6 jit_solution(15299160243905954080)
XLA Ops:
  29.3 8.6 psum.28
  50.2 15.4 collective-permute-done
  79.7 12.6 collective-permute-done.7
  95.1 16.7 collective-permute-done.2
  117.2 8.5 collective-permute-done.9
  137.6 14.9 convolution_bitcast_fusion.1.v_in
  152.5 28.0 %all-gather.16.cloned.1.call-done = bf16[4096,1,512]{2,0,1:T(8,128)(2,1)} async-done(((bf16[1024,1,512]{2,0,1:T(8,128)(2,1)}), bf16[4096,1,512]{2,0,1:T(8,128)(2,1)}) %all-gather.16.cloned.1.call-update) | async-done | bytes 4194320 | tf_op jit(solution)/shard_map/all_gather | solution.py:263
  180.5 14.9 convolution_bitcast_fusion.2.k_in
  195.4 66.0 %all-gather.14.cloned.1.call-done = bf16[4096,1,512]{2,0,1:T(8,128)(2,1)} async-done(((bf16[1024,1,512]{2,0,1:T(8,128)(2,1)}), bf16[4096,1,512]{2,0,1:T(8,128)(2,1)}) %all-gather.14.cloned.1.call-update) | async-done | bytes 4194320 | tf_op jit(solution)/shard_map/all_gather | solution.py:263
  261.4 15.1 convolution_bitcast_fusion.3.q_in
  276.5 35.1 %shard_map.143 = (bf16[2048,512]{1,0:T(8,128)(2,1)S(1)}, bf16[2048,512]{1,0:T(8,128)(2,1)}, bf16[2048,512]{1,0:T(8,128)(2,1)}, bf16[2048,512]{1,0:T(8,128)(2,1)}, f32[4,1,2048]{2,1,0:T(1,128)S(1)}) custom-call(f32[2048,512]{1,0:T(8,128)} %convolution_bitcast_fusion.3.q_in, f32[2048,512]{1,0:T(8,128)} %convolution_bitcast_fusion.2.k_in, ...), custom_call_target="tpu_custom_call" | custom-call | flops 5368709120 | bytes 20971520 | tf_op jit(solution)/shard_map/pallas_call | solution.py:88
  312.9 29.3 %all-gather.20.cloned.1.call-done = bf16[2048,1024]{1,0:T(8,128)(2,1)} async-done(((bf16[512,1024]{1,0:T(8,128)(2,1)}), bf16[2048,1024]{1,0:T(8,128)(2,1)}) %all-gather.20.cloned.1.call-update) | async-done | bytes 4194320 | tf_op jit(solution)/shard_map/all_gather | solution.py:263
  359.4 16.5 collective-permute-done.36
  390.4 11.9 collective-permute-done.38
  411.0 12.5 collective-permute-done.43
  441.9 52.8 %collective-permute-done.17 = bf16[512,1024]{1,0:T(8,128)(2,1)S(1)} collective-permute-done((bf16[512,1024]{1,0:T(8,128)(2,1)S(1)}, bf16[512,1024]{1,0:T(8,128)(2,1)S(1)}, u32[]{:S(2)}, u32[]{:S(2)}) %collective-permute-start.17) | collective-permute-done | bytes 1048608 | tf_op jit(solution)/shard_map/ppermute | solution.py:191
  504.9 12.3 collective-permute-done.15
  517.2 20.9 %collective-permute-done.18 = bf16[512,1024]{1,0:T(8,128)(2,1)S(1)} collective-permute-done((bf16[512,1024]{1,0:T(8,128)(2,1)S(1)}, bf16[512,1024]{1,0:T(8,128)(2,1)S(1)}, u32[]{:S(2)}, u32[]{:S(2)}) %collective-permute-start.18) | collective-permute-done | bytes 1048608 | tf_op jit(solution)/shard_map/ppermute | solution.py:191
  565.0 12.0 collective-permute-done.22
  589.7 20.8 %collective-permute-done.29 = bf16[512,1024]{1,0:T(8,128)(2,1)S(1)} collective-permute-done((bf16[512,1024]{1,0:T(8,128)(2,1)S(1)}, bf16[512,1024]{1,0:T(8,128)(2,1)S(1)}, u32[]{:S(2)}, u32[]{:S(2)}) %collective-permute-start.29) | collective-permute-done | bytes 1048608 | tf_op jit(solution)/shard_map/ppermute | solution.py:191
  612.0 17.9 collective-permute-done.24
  646.6 78.6 %all-gather.12.cloned.1.call-done = bf16[4,1024,2752]{1,2,0:T(8,128)(2,1)} async-done(((bf16[1,1024,2752]{1,2,0:T(8,128)(2,1)}), bf16[4,1024,2752]{1,2,0:T(8,128)(2,1)}) %all-gather.12.cloned.1.call-update) | async-done | bytes 22544400 | tf_op jit(solution)/shard_map/all_gather | solution.py:263
  725.2 57.1 %convolution_bitcast_fusion = f32[2048,2752]{0,1:T(8,128)} fusion(bf16[4,2048,1024]{2,1,0:T(8,128)(2,1)} %bitcast_dynamic-update-slice_fusion.32, bf16[4,1024,2752]{1,2,0:T(8,128)(2,1)} %all-gather.12.cloned.1.call-done), kind=kOutput, calls=%fused_computation.1 | convolution fusion | flops 46170898432 | bytes 61865984 | tf_op jit(solution)/shard_map/dot_general | solution.py:21
  782.3 9.0 multiply_convert_fusion
  791.3 9.8 fusion.53
  801.1 7.9 fusion.52
  809.0 7.9 fusion.51
  816.9 7.9 fusion.50
  830.1 91.8 %all-gather.22.cloned.1.call-done = bf16[5504,1024]{1,0:T(8,128)(2,1)} async-done(((bf16[1376,1024]{1,0:T(8,128)(2,1)}), bf16[5504,1024]{1,0:T(8,128)(2,1)}) %all-gather.22.cloned.1.call-update) | async-done | bytes 11272208 | tf_op jit(solution)/shard_map/all_gather | solution.py:263
  921.8 37.3 %fusion.3 = (bf16[2048,1376]{0,1:T(8,128)(2,1)S(1)}, bf16[2048,1376]{0,1:T(8,128)(2,1)}) fusion(f32[2048,2752]{0,1:T(8,128)} %convolution_bitcast_fusion, bf16[4,2048,1024]{2,1,0:T(8,128)(2,1)} %bitcast_dynamic-update-slice_fusion.16, bf16[4,1376,1024]{2,1,0:T(8,128)(2,1)} %bitcast.512), kind=kOutput, calls=%fused_computation.10 | convolution fusion | flops 23122083840 | bytes 61865984 | tf_op jit(solution)/shard_map/dot_general | solution.py:21
  961.7 54.7 %convolution_convert_fusion = bf16[4,1024,2752]{1,2,0:T(8,128)(2,1)} fusion(bf16[4,2048,1024]{2,1,0:T(8,128)(2,1)} %bitcast_dynamic-update-slice_fusion.32, bf16[2048,1376]{0,1:T(8,128)(2,1)} %get-tuple-element.49, bf16[2048,1376]{0,1:T(8,128)(2,1)S(1)} %get-tuple-element.48), kind=kOutput, calls=%fused_computation | convolution fusion | flops 46204715008 | bytes 50593792 | tf_op jit(solution)/shard_map/dot_general | solution.py:21
  1016.3 97.3 %reduce-scatter.7.cloned.1.call-done = bf16[1,1376,1024]{2,1,0:T(8,128)(2,1)} async-done(((bf16[4,1376,1024]{2,1,0:T(8,128)(2,1)}), bf16[1,1376,1024]{2,1,0:T(8,128)(2,1)}) %reduce-scatter.7.cloned.1.call-update) | async-done | bytes 2818064 | tf_op jit(solution)/shard_map/reduce_scatter | solution.py:259
  1113.8 17.1 fusion.39
  1131.0 17.3 fusion.36
  1148.9 17.7 add_convert_fusion.4
  1170.3 17.8 add_convert_fusion.5
  1200.2 15.5 collective-permute-done.51
  1221.7 19.0 %collective-permute-done.55 = bf16[512,1024]{1,0:T(8,128)(2,1)S(1)} collective-permute-done((bf16[512,1024]{1,0:T(8,128)(2,1)S(1)}, bf16[512,1024]{1,0:T(8,128)(2,1)S(1)}, u32[]{:S(2)}, u32[]{:S(2)}) %collective-permute-start.55) | collective-permute-done | bytes 1048608 | tf_op jit(solution)/shard_map/ppermute | solution.py:191
  1259.7 21.0 %collective-permute-done.58 = bf16[512,1024]{1,0:T(8,128)(2,1)S(1)} collective-permute-done((bf16[512,1024]{1,0:T(8,128)(2,1)S(1)}, bf16[512,1024]{1,0:T(8,128)(2,1)S(1)}, u32[]{:S(2)}, u32[]{:S(2)}) %collective-permute-start.58) | collective-permute-done | bytes 1048608 | tf_op jit(solution)/shard_map/ppermute | solution.py:191
  1286.3 19.9 %collective-permute-done.65 = bf16[512,1024]{1,0:T(8,128)(2,1)S(1)} collective-permute-done((bf16[512,1024]{1,0:T(8,128)(2,1)S(1)}, bf16[512,1024]{1,0:T(8,128)(2,1)S(1)}, u32[]{:S(2)}, u32[]{:S(2)}) %collective-permute-start.65) | collective-permute-done | bytes 1048608 | tf_op jit(solution)/shard_map/ppermute | solution.py:191
  1306.9 19.9 %collective-permute-done.60 = bf16[512,1024]{1,0:T(8,128)(2,1)S(1)} collective-permute-done((bf16[512,1024]{1,0:T(8,128)(2,1)S(1)}, bf16[512,1024]{1,0:T(8,128)(2,1)S(1)}, u32[]{:S(2)}, u32[]{:S(2)}) %collective-permute-start.60) | collective-permute-done | bytes 1048608 | tf_op jit(solution)/shard_map/ppermute | solution.py:191
  1347.6 15.3 bitcast_convert_fusion.g
  1362.9 44.0 %shard_map.144 = (bf16[2048,512]{1,0:T(8,128)(2,1)S(1)}, bf16[2048,512]{1,0:T(8,128)(2,1)}, bf16[2048,512]{1,0:T(8,128)(2,1)}) custom-call(bf16[2048,512]{1,0:T(8,128)(2,1)} %copy-done.6, bf16[2048,512]{1,0:T(8,128)(2,1)} %get-tuple-element.26.k, bf16[2048,512]{1,0:T(8,128)(2,1)} %get-tuple-element.27.v, bf16[2048,512]{1,0:T(8,128)(2,1)} %get-tuple-element.24.o, ...), custom_call_target="tpu_custom_call" | custom-call | flops 13421772800 | bytes 16777216 | tf_op jit(solution)/shard_map/pallas_call | solution.py:164
  1406.9 13.8 convolution_convert_fusion.9
  1423.7 10.5 pad_maximum_fusion
  1434.2 21.1 %collective-permute-done.91 = bf16[1376,512]{1,0:T(8,128)(2,1)S(1)} collective-permute-done((bf16[1376,512]{1,0:T(8,128)(2,1)S(1)}, bf16[1376,512]{1,0:T(8,128)(2,1)S(1)}, u32[]{:S(2)}, u32[]{:S(2)}) %collective-permute-start.91) | collective-permute-done | bytes 1409056 | tf_op jit(solution)/shard_map/ppermute | solution.py:191
  1463.6 13.9 convolution_convert_fusion.8
  1477.5 11.6 convolution_convert_fusion.1
  1489.2 11.8 convolution_convert_fusion.2
  1500.9 13.8 convolution_convert_fusion.7
  1515.1 11.7 convolution_convert_fusion.3
  1526.8 10.1 convolution_convert_fusion.4
  1537.5 11.0 add_convert_fusion
  1550.5 11.1 add_convert_fusion.1
  1565.1 9.6 add_convert_fusion.2
  1576.8 10.2 add_convert_fusion.3
  1591.1 28.0 %collective-permute-done.75 = bf16[512,1024]{1,0:T(8,128)(2,1)S(1)} collective-permute-done((bf16[512,1024]{1,0:T(8,128)(2,1)S(1)}, bf16[512,1024]{1,0:T(8,128)(2,1)S(1)}, u32[]{:S(2)}, u32[]{:S(2)}) %collective-permute-start.75) | collective-permute-done | bytes 1048608 | tf_op jit(solution)/shard_map/ppermute | solution.py:191
  1623.6 10.5 collective-permute-done.78
  1637.5 19.1 %collective-permute-done.84 = bf16[512,1024]{1,0:T(8,128)(2,1)S(1)} collective-permute-done((bf16[512,1024]{1,0:T(8,128)(2,1)S(1)}, bf16[512,1024]{1,0:T(8,128)(2,1)S(1)}, u32[]{:S(2)}, u32[]{:S(2)}) %collective-permute-start.84) | collective-permute-done | bytes 1048608 | tf_op jit(solution)/shard_map/ppermute | solution.py:191
  1672.0 30.7 %psum.31 = f32[1024]{0:T(1024)S(1)} all-reduce(f32[1024]{0:T(1024)S(1)} %get-tuple-element.43), channel_id=1, replica_groups=mesh['fsdp'=4,'ctx'=2,'tp'=4] {'tp'}, use_global_device_ids=true, to_apply=%region_8.9 | all-reduce | flops 1024 | bytes 8192 | tf_op jit(solution)/shard_map/psum | solution.py:186
  1716.6 32.4 %collective-permute-done.88 = f32[2,1024]{1,0:T(2,128)S(1)} collective-permute-done((f32[2,1024]{1,0:T(2,128)S(1)}, f32[2,1024]{1,0:T(2,128)S(1)}, u32[]{:S(2)}, u32[]{:S(2)}) %collective-permute-start.88) | collective-permute-done | bytes 8224 | tf_op jit(solution)/shard_map/ppermute | solution.py:191
  1777.0 9.7 collective-permute-done.94
  1790.5 18.7 %reduce-scatter.17.cloned.1.call-done = bf16[1,1024,512]{2,1,0:T(8,128)(2,1)} async-done(((bf16[4,1024,512]{2,1,0:T(8,128)(2,1)}), bf16[1,1024,512]{2,1,0:T(8,128)(2,1)}) %reduce-scatter.17.cloned.1.call-update) | async-done | bytes 1048592 | tf_op jit(solution)/shard_map/reduce_scatter | solution.py:259
  1814.0 10.1 collective-permute-done.96
  (490 shorter events, 374.3 us)
Async XLA Ops:
  7.2 130.4 %all-gather.18.cloned.1.call-start = ((), (), s32[]{:S(2)}) async-start(), calls=%async_computation.15 | async-start | bytes 5242880 | tf_op jit(solution)/shard_map/all_gather | solution.py:263
  15.4 165.1 %all-gather.16.cloned.1.call-start = ((), (), s32[]{:S(2)}) async-start(), calls=%async_computation.14 | async-start | bytes 5242880 | tf_op jit(solution)/shard_map/all_gather | solution.py:263
  17.7 243.6 %all-gather.14.cloned.1.call-start = ((), (), s32[]{:S(2)}) async-start(), calls=%async_computation.13 | async-start | bytes 5242880 | tf_op jit(solution)/shard_map/all_gather | solution.py:263
  20.1 322.1 %all-gather.20.cloned.1.call-start = ((), (), s32[]{:S(2)}) async-start(), calls=%async_computation.16 | async-start | bytes 5242880 | tf_op jit(solution)/shard_map/all_gather | solution.py:263
  21.2 704.0 %all-gather.12.cloned.1.call-start = ((), (), s32[]{:S(2)}) async-start(), calls=%async_computation.6 | async-start | bytes 28180480 | tf_op jit(solution)/shard_map/all_gather | solution.py:263
  27.0 894.8 %all-gather.22.cloned.1.call-start = ((), (), s32[]{:S(2)}) async-start(), calls=%async_computation.17 | async-start | bytes 14090240 | tf_op jit(solution)/shard_map/all_gather | solution.py:263
  43.4 34.8 %collective-permute-start.1 = (bf16[512,1024]{1,0:T(8,128)(2,1)}, bf16[512,1024]{1,0:T(8,128)(2,1)}, u32[]{:S(2)}, u32[]{:S(2)}) collective-permute-start(bf16[512,1024]{1,0:T(8,128)(2,1)} %get-tuple-element.88), channel_id=1, source_target_pairs={{0,2},{1,3},{2,0},{3,1},{4,6},{5,7},{6,4},{7,5},{8,10},{9,11},{10,... | collective-permute-start | bytes 3145736 | tf_op jit(solution)/shard_map/ppermute | solution.py:191
  43.9 35.8 %collective-permute-start.3 = (bf16[512,1024]{1,0:T(8,128)(2,1)}, bf16[512,1024]{1,0:T(8,128)(2,1)}, u32[]{:S(2)}, u32[]{:S(2)}) collective-permute-start(bf16[512,1024]{1,0:T(8,128)(2,1)} %get-tuple-element.88), channel_id=1, source_target_pairs={{0,1},{1,0},{2,3},{3,2},{4,5},{5,4},{6,7},{7,6},{8,9},{9,8},{10,11... | collective-permute-start | bytes 3145736 | tf_op jit(solution)/shard_map/ppermute | solution.py:191
  43.9 48.3 %collective-permute-start.7 = (bf16[512,1024]{1,0:T(8,128)(2,1)}, bf16[512,1024]{1,0:T(8,128)(2,1)}, u32[]{:S(2)}, u32[]{:S(2)}) collective-permute-start(bf16[512,1024]{1,0:T(8,128)(2,1)} %get-tuple-element.87), channel_id=1, source_target_pairs={{0,2},{1,3},{2,0},{3,1},{4,6},{5,7},{6,4},{7,5},{8,10},{9,11},{10,... | collective-permute-start | bytes 3145736 | tf_op jit(solution)/shard_map/ppermute | solution.py:191
  65.6 46.1 %collective-permute-start.2 = (bf16[512,1024]{1,0:T(8,128)(2,1)}, bf16[512,1024]{1,0:T(8,128)(2,1)S(1)}, u32[]{:S(2)}, u32[]{:S(2)}) collective-permute-start(bf16[512,1024]{1,0:T(8,128)(2,1)} %collective-permute-done), channel_id=1, source_target_pairs={{0,2},{1,3},{2,0},{3,1},{4,6},{5,7},{6,4},{7,5},{8,10},{9,11},{10,... | collective-permute-start | bytes 3145736 | tf_op jit(solution)/shard_map/ppermute | solution.py:191
  75.1 40.0 %collective-permute-start.4 = (bf16[512,1024]{1,0:T(8,128)(2,1)}, bf16[512,1024]{1,0:T(8,128)(2,1)S(1)}, u32[]{:S(2)}, u32[]{:S(2)}) collective-permute-start(bf16[512,1024]{1,0:T(8,128)(2,1)} %collective-permute-done), channel_id=1, source_target_pairs={{0,1},{1,0},{2,3},{3,2},{4,5},{5,4},{6,7},{7,6},{8,9},{9,8},{10,11... | collective-permute-start | bytes 3145736 | tf_op jit(solution)/shard_map/ppermute | solution.py:191
  78.2 38.5 %collective-permute-start.8 = (bf16[512,1024]{1,0:T(8,128)(2,1)}, bf16[512,1024]{1,0:T(8,128)(2,1)S(1)}, u32[]{:S(2)}, u32[]{:S(2)}) collective-permute-start(bf16[512,1024]{1,0:T(8,128)(2,1)} %get-tuple-element.87), channel_id=1, source_target_pairs={{0,4},{4,0},{1,5},{5,1},{2,6},{6,2},{3,7},{7,3},{8,12},{12,8},{9,1... | collective-permute-start | bytes 3145736 | tf_op jit(solution)/shard_map/ppermute | solution.py:191
  79.7 37.0 %collective-permute-start.5 = (bf16[512,1024]{1,0:T(8,128)(2,1)}, bf16[512,1024]{1,0:T(8,128)(2,1)S(1)}, u32[]{:S(2)}, u32[]{:S(2)}) collective-permute-start(bf16[512,1024]{1,0:T(8,128)(2,1)} %collective-permute-done.1), channel_id=1, source_target_pairs={{0,1},{1,0},{2,3},{3,2},{4,5},{5,4},{6,7},{7,6},{8,9},{9,8},{10,11... | collective-permute-start | bytes 3145736 | tf_op jit(solution)/shard_map/ppermute | solution.py:191
  92.2 33.5 %collective-permute-start.9 = (bf16[512,1024]{1,0:T(8,128)(2,1)}, bf16[512,1024]{1,0:T(8,128)(2,1)S(1)}, u32[]{:S(2)}, u32[]{:S(2)}) collective-permute-start(bf16[512,1024]{1,0:T(8,128)(2,1)} %collective-permute-done.7), channel_id=1, source_target_pairs={{0,4},{4,0},{1,5},{5,1},{2,6},{6,2},{3,7},{7,3},{8,12},{12,8},{9,1... | collective-permute-start | bytes 3145736 | tf_op jit(solution)/shard_map/ppermute | solution.py:191
  348.5 79.2 %collective-permute-start.16 = (bf16[2048,1024]{1,0:T(8,128)(2,1)}, bf16[2048,1024]{1,0:T(8,128)(2,1)}, u32[]{:S(2)}, u32[]{:S(2)}) collective-permute-start(bf16[2048,1024]{1,0:T(8,128)(2,1)} %convolution_convert_fusion.5), channel_id=1, source_target_pairs={{0,1},{1,0},{2,3},{3,2},{4,5},{5,4},{6,7},{7,6},{8,9},{9,8},{10,11... | collective-permute-start | bytes 12582920 | tf_op jit(solution)/shard_map/ppermute | solution.py:191
  358.9 77.3 %collective-permute-start.14 = (bf16[2048,1024]{1,0:T(8,128)(2,1)}, bf16[2048,1024]{1,0:T(8,128)(2,1)}, u32[]{:S(2)}, u32[]{:S(2)}) collective-permute-start(bf16[2048,1024]{1,0:T(8,128)(2,1)} %convolution_convert_fusion.6), channel_id=1, source_target_pairs={{0,1},{1,0},{2,3},{3,2},{4,5},{5,4},{6,7},{7,6},{8,9},{9,8},{10,11... | collective-permute-start | bytes 12582920 | tf_op jit(solution)/shard_map/ppermute | solution.py:191
  359.4 29.8 %collective-permute-start.39 = (bf16[512,1024]{1,0:T(8,128)(2,1)}, bf16[512,1024]{1,0:T(8,128)(2,1)}, u32[]{:S(2)}, u32[]{:S(2)}) collective-permute-start(bf16[512,1024]{1,0:T(8,128)(2,1)} %get-tuple-element.82), channel_id=1, source_target_pairs={{0,1},{1,0},{2,3},{3,2},{4,5},{5,4},{6,7},{7,6},{8,9},{9,8},{10,11... | collective-permute-start | bytes 3145736 | tf_op jit(solution)/shard_map/ppermute | solution.py:191
  379.3 734.4 %reduce-scatter.7.cloned.1.call-start = ((), (), s32[]{:S(2)}) async-start(), calls=%async_computation.7 | async-start | bytes 14090240 | tf_op jit(solution)/shard_map/reduce_scatter | solution.py:259
  389.3 34.2 %collective-permute-start.43 = (bf16[512,1024]{1,0:T(8,128)(2,1)}, bf16[512,1024]{1,0:T(8,128)(2,1)}, u32[]{:S(2)}, u32[]{:S(2)}) collective-permute-start(bf16[512,1024]{1,0:T(8,128)(2,1)} %get-tuple-element.81), channel_id=1, source_target_pairs={{0,2},{1,3},{2,0},{3,1},{4,6},{5,7},{6,4},{7,5},{8,10},{9,11},{10,... | collective-permute-start | bytes 3145736 | tf_op jit(solution)/shard_map/ppermute | solution.py:191
  423.5 74.2 %collective-permute-start.44 = (bf16[512,1024]{1,0:T(8,128)(2,1)}, bf16[512,1024]{1,0:T(8,128)(2,1)}, u32[]{:S(2)}, u32[]{:S(2)}) collective-permute-start(bf16[512,1024]{1,0:T(8,128)(2,1)} %get-tuple-element.81), channel_id=1, source_target_pairs={{0,4},{4,0},{1,5},{5,1},{2,6},{6,2},{3,7},{7,3},{8,12},{12,8},{9,1... | collective-permute-start | bytes 3145736 | tf_op jit(solution)/shard_map/ppermute | solution.py:191
  425.0 113.7 %collective-permute-start.45 = (bf16[512,1024]{1,0:T(8,128)(2,1)}, bf16[512,1024]{1,0:T(8,128)(2,1)}, u32[]{:S(2)}, u32[]{:S(2)}) collective-permute-start(bf16[512,1024]{1,0:T(8,128)(2,1)} %collective-permute-done.43), channel_id=1, source_target_pairs={{0,4},{4,0},{1,5},{5,1},{2,6},{6,2},{3,7},{7,3},{8,12},{12,8},{9,1... | collective-permute-start | bytes 3145736 | tf_op jit(solution)/shard_map/ppermute | solution.py:191
  432.9 61.9 %collective-permute-start.17 = (bf16[512,1024]{1,0:T(8,128)(2,1)S(1)}, bf16[512,1024]{1,0:T(8,128)(2,1)S(1)}, u32[]{:S(2)}, u32[]{:S(2)}) collective-permute-start(bf16[512,1024]{1,0:T(8,128)(2,1)S(1)} %dynamic-slice_bitcast_fusion.16), channel_id=1, source_target_pairs={{0,4},{4,0},{1,5},{5,1},{2,6},{6,2},{3,7},{7,3},{8,12},{12,8},{9,1... | collective-permute-start | bytes 3145736 | tf_op jit(solution)/shard_map/ppermute | solution.py:191
  434.6 62.0 %collective-permute-start.20 = (bf16[512,1024]{1,0:T(8,128)(2,1)S(1)}, bf16[512,1024]{1,0:T(8,128)(2,1)S(1)}, u32[]{:S(2)}, u32[]{:S(2)}) collective-permute-start(bf16[512,1024]{1,0:T(8,128)(2,1)S(1)} %get-tuple-element.86), channel_id=1, source_target_pairs={{0,2},{1,3},{2,0},{3,1},{4,6},{5,7},{6,4},{7,5},{8,10},{9,11},{10,... | collective-permute-start | bytes 3145736 | tf_op jit(solution)/shard_map/ppermute | solution.py:191
  441.3 75.9 %collective-permute-start.15 = (bf16[512,1024]{1,0:T(8,128)(2,1)S(1)}, bf16[512,1024]{1,0:T(8,128)(2,1)S(1)}, u32[]{:S(2)}, u32[]{:S(2)}) collective-permute-start(bf16[512,1024]{1,0:T(8,128)(2,1)S(1)} %dynamic-slice_bitcast_fusion.17), channel_id=1, source_target_pairs={{0,4},{4,0},{1,5},{5,1},{2,6},{6,2},{3,7},{7,3},{8,12},{12,8},{9,1... | collective-permute-start | bytes 3145736 | tf_op jit(solution)/shard_map/ppermute | solution.py:191
  494.7 44.5 %collective-permute-start.19 = (bf16[512,1024]{1,0:T(8,128)(2,1)S(1)}, bf16[512,1024]{1,0:T(8,128)(2,1)S(1)}, u32[]{:S(2)}, u32[]{:S(2)}) collective-permute-start(bf16[512,1024]{1,0:T(8,128)(2,1)S(1)} %get-tuple-element.85), channel_id=1, source_target_pairs={{0,2},{1,3},{2,0},{3,1},{4,6},{5,7},{6,4},{7,5},{8,10},{9,11},{10,... | collective-permute-start | bytes 3145736 | tf_op jit(solution)/shard_map/ppermute | solution.py:191
  496.7 41.4 %collective-permute-start.18 = (bf16[512,1024]{1,0:T(8,128)(2,1)S(1)}, bf16[512,1024]{1,0:T(8,128)(2,1)S(1)}, u32[]{:S(2)}, u32[]{:S(2)}) collective-permute-start(bf16[512,1024]{1,0:T(8,128)(2,1)S(1)} %fusion.96), channel_id=1, source_target_pairs={{0,2},{1,3},{2,0},{3,1},{4,6},{5,7},{6,4},{7,5},{8,10},{9,11},{10,... | collective-permute-start | bytes 3145736 | tf_op jit(solution)/shard_map/ppermute | solution.py:191
  497.7 41.7 %collective-permute-start.21 = (bf16[512,1024]{1,0:T(8,128)(2,1)S(1)}, bf16[512,1024]{1,0:T(8,128)(2,1)S(1)}, u32[]{:S(2)}, u32[]{:S(2)}) collective-permute-start(bf16[512,1024]{1,0:T(8,128)(2,1)S(1)} %fusion.94), channel_id=1, source_target_pairs={{0,4},{4,0},{1,5},{5,1},{2,6},{6,2},{3,7},{7,3},{8,12},{12,8},{9,1... | collective-permute-start | bytes 3145736 | tf_op jit(solution)/shard_map/ppermute | solution.py:191
  517.2 40.1 %collective-permute-start.46 = (bf16[512,1024]{1,0:T(8,128)(2,1)}, bf16[512,1024]{1,0:T(8,128)(2,1)}, u32[]{:S(2)}, u32[]{:S(2)}) collective-permute-start(bf16[512,1024]{1,0:T(8,128)(2,1)} %get-tuple-element.81), channel_id=1, source_target_pairs={{0,1},{1,0},{2,3},{3,2},{4,5},{5,4},{6,7},{7,6},{8,9},{9,8},{10,11... | collective-permute-start | bytes 3145736 | tf_op jit(solution)/shard_map/ppermute | solution.py:191
  539.3 39.2 %collective-permute-start.49 = (bf16[512,1024]{1,0:T(8,128)(2,1)}, bf16[512,1024]{1,0:T(8,128)(2,1)S(1)}, u32[]{:S(2)}, u32[]{:S(2)}) collective-permute-start(bf16[512,1024]{1,0:T(8,128)(2,1)} %collective-permute-done.45), channel_id=1, source_target_pairs={{0,1},{1,0},{2,3},{3,2},{4,5},{5,4},{6,7},{7,6},{8,9},{9,8},{10,11... | collective-permute-start | bytes 3145736 | tf_op jit(solution)/shard_map/ppermute | solution.py:191
  562.5 48.0 %collective-permute-start.29 = (bf16[512,1024]{1,0:T(8,128)(2,1)S(1)}, bf16[512,1024]{1,0:T(8,128)(2,1)S(1)}, u32[]{:S(2)}, u32[]{:S(2)}) collective-permute-start(bf16[512,1024]{1,0:T(8,128)(2,1)S(1)} %get-tuple-element.83), channel_id=1, source_target_pairs={{0,2},{1,3},{2,0},{3,1},{4,6},{5,7},{6,4},{7,5},{8,10},{9,11},{10,... | collective-permute-start | bytes 3145736 | tf_op jit(solution)/shard_map/ppermute | solution.py:191
  577.0 53.0 %collective-permute-start.24 = (bf16[512,1024]{1,0:T(8,128)(2,1)S(1)}, bf16[512,1024]{1,0:T(8,128)(2,1)S(1)}, u32[]{:S(2)}, u32[]{:S(2)}) collective-permute-start(bf16[512,1024]{1,0:T(8,128)(2,1)S(1)} %collective-permute-done.22), channel_id=1, source_target_pairs={{0,2},{1,3},{2,0},{3,1},{4,6},{5,7},{6,4},{7,5},{8,10},{9,11},{10,... | collective-permute-start | bytes 3145736 | tf_op jit(solution)/shard_map/ppermute | solution.py:191
  586.9 45.3 %collective-permute-start.26 = (bf16[512,1024]{1,0:T(8,128)(2,1)S(1)}, bf16[512,1024]{1,0:T(8,128)(2,1)S(1)}, u32[]{:S(2)}, u32[]{:S(2)}) collective-permute-start(bf16[512,1024]{1,0:T(8,128)(2,1)S(1)} %collective-permute-done.22), channel_id=1, source_target_pairs={{0,1},{1,0},{2,3},{3,2},{4,5},{5,4},{6,7},{7,6},{8,9},{9,8},{10,11... | collective-permute-start | bytes 3145736 | tf_op jit(solution)/shard_map/ppermute | solution.py:191
  588.0 45.7 %collective-permute-start.30 = (bf16[512,1024]{1,0:T(8,128)(2,1)S(1)}, bf16[512,1024]{1,0:T(8,128)(2,1)S(1)}, u32[]{:S(2)}, u32[]{:S(2)}) collective-permute-start(bf16[512,1024]{1,0:T(8,128)(2,1)S(1)} %get-tuple-element.83), channel_id=1, source_target_pairs={{0,4},{4,0},{1,5},{5,1},{2,6},{6,2},{3,7},{7,3},{8,12},{12,8},{9,1... | collective-permute-start | bytes 3145736 | tf_op jit(solution)/shard_map/ppermute | solution.py:191
  589.5 44.2 %collective-permute-start.27 = (bf16[512,1024]{1,0:T(8,128)(2,1)S(1)}, bf16[512,1024]{1,0:T(8,128)(2,1)S(1)}, u32[]{:S(2)}, u32[]{:S(2)}) collective-permute-start(bf16[512,1024]{1,0:T(8,128)(2,1)S(1)} %collective-permute-done.23), channel_id=1, source_target_pairs={{0,1},{1,0},{2,3},{3,2},{4,5},{5,4},{6,7},{7,6},{8,9},{9,8},{10,11... | collective-permute-start | bytes 3145736 | tf_op jit(solution)/shard_map/ppermute | solution.py:191
  830.0 835.0 %reduce-scatter.13.cloned.1.call-start = ((), (), s32[]{:S(2)}) async-start(), calls=%async_computation.10 | async-start | bytes 28180480 | tf_op jit(solution)/shard_map/reduce_scatter | solution.py:259
  1113.7 636.7 %reduce-scatter.11.cloned.1.call-start = ((), (), s32[]{:S(2)}) async-start(), calls=%async_computation.9 | async-start | bytes 5242880 | tf_op jit(solution)/shard_map/reduce_scatter | solution.py:259
  1196.5 44.2 %collective-permute-start.55 = (bf16[512,1024]{1,0:T(8,128)(2,1)S(1)}, bf16[512,1024]{1,0:T(8,128)(2,1)S(1)}, u32[]{:S(2)}, u32[]{:S(2)}) collective-permute-start(bf16[512,1024]{1,0:T(8,128)(2,1)S(1)} %get-tuple-element.79), channel_id=1, source_target_pairs={{0,2},{1,3},{2,0},{3,1},{4,6},{5,7},{6,4},{7,5},{8,10},{9,11},{10,... | collective-permute-start | bytes 3145736 | tf_op jit(solution)/shard_map/ppermute | solution.py:191
  1198.6 42.1 %collective-permute-start.57 = (bf16[512,1024]{1,0:T(8,128)(2,1)S(1)}, bf16[512,1024]{1,0:T(8,128)(2,1)S(1)}, u32[]{:S(2)}, u32[]{:S(2)}) collective-permute-start(bf16[512,1024]{1,0:T(8,128)(2,1)S(1)} %fusion.90), channel_id=1, source_target_pairs={{0,4},{4,0},{1,5},{5,1},{2,6},{6,2},{3,7},{7,3},{8,12},{12,8},{9,1... | collective-permute-start | bytes 3145736 | tf_op jit(solution)/shard_map/ppermute | solution.py:191
  1259.1 47.1 %collective-permute-start.65 = (bf16[512,1024]{1,0:T(8,128)(2,1)S(1)}, bf16[512,1024]{1,0:T(8,128)(2,1)S(1)}, u32[]{:S(2)}, u32[]{:S(2)}) collective-permute-start(bf16[512,1024]{1,0:T(8,128)(2,1)S(1)} %get-tuple-element.77), channel_id=1, source_target_pairs={{0,2},{1,3},{2,0},{3,1},{4,6},{5,7},{6,4},{7,5},{8,10},{9,11},{10,... | collective-permute-start | bytes 3145736 | tf_op jit(solution)/shard_map/ppermute | solution.py:191
  1280.7 46.1 %collective-permute-start.60 = (bf16[512,1024]{1,0:T(8,128)(2,1)S(1)}, bf16[512,1024]{1,0:T(8,128)(2,1)S(1)}, u32[]{:S(2)}, u32[]{:S(2)}) collective-permute-start(bf16[512,1024]{1,0:T(8,128)(2,1)S(1)} %collective-permute-done.58), channel_id=1, source_target_pairs={{0,2},{1,3},{2,0},{3,1},{4,6},{5,7},{6,4},{7,5},{8,10},{9,11},{10,... | collective-permute-start | bytes 3145736 | tf_op jit(solution)/shard_map/ppermute | solution.py:191
  1284.4 42.7 %collective-permute-start.62 = (bf16[512,1024]{1,0:T(8,128)(2,1)S(1)}, bf16[512,1024]{1,0:T(8,128)(2,1)S(1)}, u32[]{:S(2)}, u32[]{:S(2)}) collective-permute-start(bf16[512,1024]{1,0:T(8,128)(2,1)S(1)} %collective-permute-done.58), channel_id=1, source_target_pairs={{0,1},{1,0},{2,3},{3,2},{4,5},{5,4},{6,7},{7,6},{8,9},{9,8},{10,11... | collective-permute-start | bytes 3145736 | tf_op jit(solution)/shard_map/ppermute | solution.py:191
  1284.6 43.1 %collective-permute-start.66 = (bf16[512,1024]{1,0:T(8,128)(2,1)S(1)}, bf16[512,1024]{1,0:T(8,128)(2,1)S(1)}, u32[]{:S(2)}, u32[]{:S(2)}) collective-permute-start(bf16[512,1024]{1,0:T(8,128)(2,1)S(1)} %get-tuple-element.77), channel_id=1, source_target_pairs={{0,4},{4,0},{1,5},{5,1},{2,6},{6,2},{3,7},{7,3},{8,12},{12,8},{9,1... | collective-permute-start | bytes 3145736 | tf_op jit(solution)/shard_map/ppermute | solution.py:191
  1286.1 41.7 %collective-permute-start.63 = (bf16[512,1024]{1,0:T(8,128)(2,1)S(1)}, bf16[512,1024]{1,0:T(8,128)(2,1)S(1)}, u32[]{:S(2)}, u32[]{:S(2)}) collective-permute-start(bf16[512,1024]{1,0:T(8,128)(2,1)S(1)} %collective-permute-done.59), channel_id=1, source_target_pairs={{0,1},{1,0},{2,3},{3,2},{4,5},{5,4},{6,7},{7,6},{8,9},{9,8},{10,11... | collective-permute-start | bytes 3145736 | tf_op jit(solution)/shard_map/ppermute | solution.py:191
  1347.6 426.9 %reduce-scatter.9.cloned.1.call-start = ((), (), s32[]{:S(2)}) async-start(), calls=%async_computation.8 | async-start | bytes 5242880 | tf_op jit(solution)/shard_map/reduce_scatter | solution.py:259
  1420.7 367.2 %reduce-scatter.15.cloned.1.call-start = ((), (), s32[]{:S(2)}) async-start(), calls=%async_computation.11 | async-start | bytes 5242880 | tf_op jit(solution)/shard_map/reduce_scatter | solution.py:259
  1422.3 32.9 %collective-permute-start.91 = (bf16[1376,512]{1,0:T(8,128)(2,1)S(1)}, bf16[1376,512]{1,0:T(8,128)(2,1)S(1)}, u32[]{:S(2)}, u32[]{:S(2)}) collective-permute-start(bf16[1376,512]{1,0:T(8,128)(2,1)S(1)} %dynamic-slice_bitcast_fusion.1), channel_id=1, source_target_pairs={{0,4},{4,0},{1,5},{5,1},{2,6},{6,2},{3,7},{7,3},{8,12},{12,8},{9,1... | collective-permute-start | bytes 4227080 | tf_op jit(solution)/shard_map/ppermute | solution.py:191
  1477.5 331.8 %reduce-scatter.17.cloned.1.call-start = ((), (), s32[]{:S(2)}) async-start(), calls=%async_computation.12 | async-start | bytes 5242880 | tf_op jit(solution)/shard_map/reduce_scatter | solution.py:259
  1489.2 48.3 %collective-permute-start.82 = (bf16[2048,1024]{1,0:T(8,128)(2,1)}, bf16[2048,1024]{1,0:T(8,128)(2,1)}, u32[]{:S(2)}, u32[]{:S(2)}) collective-permute-start(bf16[2048,1024]{1,0:T(8,128)(2,1)} %convolution_convert_fusion.1), channel_id=1, source_target_pairs={{0,1},{1,0},{2,3},{3,2},{4,5},{5,4},{6,7},{7,6},{8,9},{9,8},{10,11... | collective-permute-start | bytes 12582920 | tf_op jit(solution)/shard_map/ppermute | solution.py:191
  1514.7 35.8 %collective-permute-start.80 = (bf16[2048,1024]{1,0:T(8,128)(2,1)}, bf16[2048,1024]{1,0:T(8,128)(2,1)}, u32[]{:S(2)}, u32[]{:S(2)}) collective-permute-start(bf16[2048,1024]{1,0:T(8,128)(2,1)} %convolution_convert_fusion.2), channel_id=1, source_target_pairs={{0,1},{1,0},{2,3},{3,2},{4,5},{5,4},{6,7},{7,6},{8,9},{9,8},{10,11... | collective-permute-start | bytes 12582920 | tf_op jit(solution)/shard_map/ppermute | solution.py:191
  1526.8 37.8 %collective-permute-start.74 = (bf16[2048,1024]{1,0:T(8,128)(2,1)}, bf16[2048,1024]{1,0:T(8,128)(2,1)}, u32[]{:S(2)}, u32[]{:S(2)}) collective-permute-start(bf16[2048,1024]{1,0:T(8,128)(2,1)} %convolution_convert_fusion.3), channel_id=1, source_target_pairs={{0,1},{1,0},{2,3},{3,2},{4,5},{5,4},{6,7},{7,6},{8,9},{9,8},{10,11... | collective-permute-start | bytes 12582920 | tf_op jit(solution)/shard_map/ppermute | solution.py:191
  1536.9 38.4 %collective-permute-start.72 = (bf16[2048,1024]{1,0:T(8,128)(2,1)}, bf16[2048,1024]{1,0:T(8,128)(2,1)}, u32[]{:S(2)}, u32[]{:S(2)}) collective-permute-start(bf16[2048,1024]{1,0:T(8,128)(2,1)} %convolution_convert_fusion.4), channel_id=1, source_target_pairs={{0,1},{1,0},{2,3},{3,2},{4,5},{5,4},{6,7},{7,6},{8,9},{9,8},{10,11... | collective-permute-start | bytes 12582920 | tf_op jit(solution)/shard_map/ppermute | solution.py:191
  1549.0 38.1 %collective-permute-start.83 = (bf16[512,1024]{1,0:T(8,128)(2,1)S(1)}, bf16[512,1024]{1,0:T(8,128)(2,1)S(1)}, u32[]{:S(2)}, u32[]{:S(2)}) collective-permute-start(bf16[512,1024]{1,0:T(8,128)(2,1)S(1)} %dynamic-slice_bitcast_fusion.4), channel_id=1, source_target_pairs={{0,4},{4,0},{1,5},{5,1},{2,6},{6,2},{3,7},{7,3},{8,12},{12,8},{9,1... | collective-permute-start | bytes 3145736 | tf_op jit(solution)/shard_map/ppermute | solution.py:191
  1562.2 74.8 %collective-permute-start.81 = (bf16[512,1024]{1,0:T(8,128)(2,1)S(1)}, bf16[512,1024]{1,0:T(8,128)(2,1)}, u32[]{:S(2)}, u32[]{:S(2)}) collective-permute-start(bf16[512,1024]{1,0:T(8,128)(2,1)S(1)} %dynamic-slice_bitcast_fusion.5), channel_id=1, source_target_pairs={{0,4},{4,0},{1,5},{5,1},{2,6},{6,2},{3,7},{7,3},{8,12},{12,8},{9,1... | collective-permute-start | bytes 3145736 | tf_op jit(solution)/shard_map/ppermute | solution.py:191
  1564.6 97.0 %collective-permute-start.85 = (bf16[512,1024]{1,0:T(8,128)(2,1)S(1)}, bf16[512,1024]{1,0:T(8,128)(2,1)}, u32[]{:S(2)}, u32[]{:S(2)}) collective-permute-start(bf16[512,1024]{1,0:T(8,128)(2,1)S(1)} %get-tuple-element.73), channel_id=1, source_target_pairs={{0,2},{1,3},{2,0},{3,1},{4,6},{5,7},{6,4},{7,5},{8,10},{9,11},{10,... | collective-permute-start | bytes 3145736 | tf_op jit(solution)/shard_map/ppermute | solution.py:191
  1575.3 43.8 %collective-permute-start.75 = (bf16[512,1024]{1,0:T(8,128)(2,1)S(1)}, bf16[512,1024]{1,0:T(8,128)(2,1)S(1)}, u32[]{:S(2)}, u32[]{:S(2)}) collective-permute-start(bf16[512,1024]{1,0:T(8,128)(2,1)S(1)} %dynamic-slice_bitcast_fusion.8), channel_id=1, source_target_pairs={{0,4},{4,0},{1,5},{5,1},{2,6},{6,2},{3,7},{7,3},{8,12},{12,8},{9,1... | collective-permute-start | bytes 3145736 | tf_op jit(solution)/shard_map/ppermute | solution.py:191
  1587.2 46.9 %collective-permute-start.78 = (bf16[512,1024]{1,0:T(8,128)(2,1)S(1)}, bf16[512,1024]{1,0:T(8,128)(2,1)S(1)}, u32[]{:S(2)}, u32[]{:S(2)}) collective-permute-start(bf16[512,1024]{1,0:T(8,128)(2,1)S(1)} %get-tuple-element.76), channel_id=1, source_target_pairs={{0,2},{1,3},{2,0},{3,1},{4,6},{5,7},{6,4},{7,5},{8,10},{9,11},{10,... | collective-permute-start | bytes 3145736 | tf_op jit(solution)/shard_map/ppermute | solution.py:191
  1589.2 67.4 %collective-permute-start.84 = (bf16[512,1024]{1,0:T(8,128)(2,1)S(1)}, bf16[512,1024]{1,0:T(8,128)(2,1)S(1)}, u32[]{:S(2)}, u32[]{:S(2)}) collective-permute-start(bf16[512,1024]{1,0:T(8,128)(2,1)S(1)} %fusion.84), channel_id=1, source_target_pairs={{0,2},{1,3},{2,0},{3,1},{4,6},{5,7},{6,4},{7,5},{8,10},{9,11},{10,... | collective-permute-start | bytes 3145736 | tf_op jit(solution)/shard_map/ppermute | solution.py:191
  1619.1 42.7 %collective-permute-start.87 = (bf16[512,1024]{1,0:T(8,128)(2,1)S(1)}, bf16[512,1024]{1,0:T(8,128)(2,1)S(1)}, u32[]{:S(2)}, u32[]{:S(2)}) collective-permute-start(bf16[512,1024]{1,0:T(8,128)(2,1)S(1)} %fusion.82), channel_id=1, source_target_pairs={{0,4},{4,0},{1,5},{5,1},{2,6},{6,2},{3,7},{7,3},{8,12},{12,8},{9,1... | collective-permute-start | bytes 3145736 | tf_op jit(solution)/shard_map/ppermute | solution.py:191
  1634.1 68.6 %collective-permute-start.73 = (bf16[512,1024]{1,0:T(8,128)(2,1)}, bf16[512,1024]{1,0:T(8,128)(2,1)}, u32[]{:S(2)}, u32[]{:S(2)}) collective-permute-start(bf16[512,1024]{1,0:T(8,128)(2,1)} %dynamic-slice_bitcast_fusion.9), channel_id=1, source_target_pairs={{0,4},{4,0},{1,5},{5,1},{2,6},{6,2},{3,7},{7,3},{8,12},{12,8},{9,1... | collective-permute-start | bytes 3145736 | tf_op jit(solution)/shard_map/ppermute | solution.py:191
  1637.0 76.0 %collective-permute-start.77 = (bf16[512,1024]{1,0:T(8,128)(2,1)S(1)}, bf16[512,1024]{1,0:T(8,128)(2,1)}, u32[]{:S(2)}, u32[]{:S(2)}) collective-permute-start(bf16[512,1024]{1,0:T(8,128)(2,1)S(1)} %get-tuple-element.75), channel_id=1, source_target_pairs={{0,2},{1,3},{2,0},{3,1},{4,6},{5,7},{6,4},{7,5},{8,10},{9,11},{10,... | collective-permute-start | bytes 3145736 | tf_op jit(solution)/shard_map/ppermute | solution.py:191
  1656.6 47.0 %collective-permute-start.76 = (bf16[512,1024]{1,0:T(8,128)(2,1)}, bf16[512,1024]{1,0:T(8,128)(2,1)}, u32[]{:S(2)}, u32[]{:S(2)}) collective-permute-start(bf16[512,1024]{1,0:T(8,128)(2,1)} %fusion.88), channel_id=1, source_target_pairs={{0,2},{1,3},{2,0},{3,1},{4,6},{5,7},{6,4},{7,5},{8,10},{9,11},{10,... | collective-permute-start | bytes 3145736 | tf_op jit(solution)/shard_map/ppermute | solution.py:191
  1661.6 51.4 %collective-permute-start.79 = (bf16[512,1024]{1,0:T(8,128)(2,1)}, bf16[512,1024]{1,0:T(8,128)(2,1)}, u32[]{:S(2)}, u32[]{:S(2)}) collective-permute-start(bf16[512,1024]{1,0:T(8,128)(2,1)} %fusion.86), channel_id=1, source_target_pairs={{0,4},{4,0},{1,5},{5,1},{2,6},{6,2},{3,7},{7,3},{8,12},{12,8},{9,1... | collective-permute-start | bytes 3145736 | tf_op jit(solution)/shard_map/ppermute | solution.py:191
  1668.7 96.7 %collective-permute-start.93 = (bf16[512,2752]{0,1:T(8,128)(2,1)}, bf16[512,2752]{0,1:T(8,128)(2,1)}, u32[]{:S(2)}, u32[]{:S(2)}) collective-permute-start(bf16[512,2752]{0,1:T(8,128)(2,1)} %dynamic-slice_bitcast_fusion), channel_id=1, source_target_pairs={{0,4},{4,0},{1,5},{5,1},{2,6},{6,2},{3,7},{7,3},{8,12},{12,8},{9,1... | collective-permute-start | bytes 8454152 | tf_op jit(solution)/shard_map/ppermute | solution.py:191
  1702.7 46.2 %collective-permute-start.88 = (f32[2,1024]{1,0:T(2,128)S(1)}, f32[2,1024]{1,0:T(2,128)S(1)}, u32[]{:S(2)}, u32[]{:S(2)}) collective-permute-start(f32[2,1024]{1,0:T(2,128)S(1)} %pad_maximum_fusion.8), channel_id=1, source_target_pairs={{0,4},{4,0},{1,5},{5,1},{2,6},{6,2},{3,7},{7,3},{8,12},{12,8},{9,1... | collective-permute-start | bytes 24584 | tf_op jit(solution)/shard_map/ppermute | solution.py:191
  (105 other events, 2255.6 us)
Sparse Core Ops, SparseCore 0:
  15.5 83.4 all-gather.17
  101.1 79.2 all-gather.15
  182.0 79.2 all-gather.13
  262.8 79.2 all-gather.19
  344.1 381.0 all-gather.11
  726.6 195.1 all-gather.21
  924.8 188.8 reduce-scatter.6
  1116.1 373.3 reduce-scatter.12
  1491.7 78.4 reduce-scatter.10
  1572.4 77.2 reduce-scatter.8
  1652.0 77.2 reduce-scatter.14
  1731.6 77.6 reduce-scatter.16

commit v3 on v2

--- a/solution.py
+++ b/solution.py
@@ -94,7 +94,7 @@
         scratch_shapes=[pltpu.VMEM((blocks, HD, block), BF)],
         compiler_params=pltpu.CompilerParams(vmem_limit_bytes=48 << 20),
         cost_estimate=pl.CostEstimate(
-            flops=4 * pairs * HD,
+            flops=30 * pairs * HD,
             transcendentals=pairs,
             bytes_accessed=seq_len * heads * HD * (12 + 8),
         ),
@@ -175,7 +175,7 @@
         ],
         compiler_params=pltpu.CompilerParams(vmem_limit_bytes=48 << 20),
         cost_estimate=pl.CostEstimate(
-            flops=10 * pairs * HD,
+            flops=38 * pairs * HD,
             transcendentals=pairs,
             bytes_accessed=seq_len * heads * HD * 16,
         ),
@@ -186,68 +186,134 @@
     return lax.psum(values, "tp")
 
 
+def flip(axis, bit):
+    step = 1 << bit
+    return [(i, i ^ step) for i in range(lax.axis_size(axis))]
+
+
 def swap(values, axis, bit):
-    step = 1 << bit
-    return lax.ppermute(values, axis, [(i, i ^ step) for i in range(lax.axis_size(axis))])
-
-
-def high_bits():
-    return list(range(1, lax.axis_size("tp").bit_length() - 1))[::-1]
+    return lax.ppermute(values, axis, flip(axis, bit))
+
+
+def at_bit(axis, bit):
+    return (lax.axis_index(axis) >> bit) & 1
+
+
+def tp_high():
+    return [("tp", b) for b in range(1, lax.axis_size("tp").bit_length() - 1)][::-1]
+
+
+def cut(rows, count):
+    step = -(-rows // (16 * count)) * 16
+    edges = [min(i * step, rows) for i in range(count)] + [rows]
+    return list(zip(edges[:-1], edges[1:]))
+
+
+def turns(links):
+    return [links[i:] + links[:i] for i in range(len(links))]
+
+
+def pinned(values):
+    return with_layout_constraint(values, Layout(tuple(range(values.ndim))))
+
+
+def spot(shift):
+    block = lax.axis_index("tp")
+    row = lax.axis_index("ctx")
+    for axis, bit in shift:
+        if axis == "tp":
+            block = block ^ (1 << bit)
+        elif axis == "ctx":
+            row = row ^ 1
+    return block, row
 
 
 def gather_rows(values):
     rows, cols = values.shape
-    half = rows // 2
-    n_t, n_c = lax.axis_size("tp"), lax.axis_size("ctx")
-    me_t, me_c = lax.axis_index("tp"), lax.axis_index("ctx")
-    across = [("tp", b) for b in high_bits()]
-    full = jnp.zeros((n_t, n_c * rows, cols), values.dtype)
-    for part, plan in enumerate(([("ctx", 0)] + across, across + [("ctx", 0)])):
-        held = {(0, 0): values[part * half : (part + 1) * half]}
-        for axis, bit in plan + [("tp", 0)]:
-            for (dc, dt), piece in list(held.items()):
-                key = (1, dt) if axis == "ctx" else (dc, dt | (1 << bit))
-                held[key] = swap(piece, axis, bit)
-        for (dc, dt), piece in held.items():
-            start = (me_t ^ dt, (me_c ^ dc) * rows + part * half, 0)
+    links = [("ctx", 0)] + tp_high()
+    full = jnp.zeros((lax.axis_size("tp"), lax.axis_size("ctx") * rows, cols), values.dtype)
+    orders = turns(links)
+    for (low, high), order in zip(cut(rows, len(orders)), orders):
+        held = {frozenset(): values[low:high]}
+        for link in order + [("tp", 0)]:
+            for shift, piece in list(held.items()):
+                held[shift | {link}] = swap(piece, *link)
+        for shift, piece in held.items():
+            block, row = spot(shift)
+            full = lax.dynamic_update_slice(full, piece[None], (block, row * rows + low, 0))
+    return pinned(full)
+
+
+def gather_pair(values, token=None):
+    rows, cols = values.shape
+    n_c = lax.axis_size("ctx")
+    links = [("ctx", 0)] + tp_high() + [("fsdp", 0)]
+    full = jnp.zeros((lax.axis_size("tp") // 2, 2 * n_c * rows, cols), values.dtype)
+    orders = turns(links)
+    for (low, high), order in zip(cut(rows, len(orders)), orders):
+        held = {frozenset(): values[low:high]}
+        for turn, link in enumerate(order):
+            if turn == 1 and token is not None:
+                held = dict(zip(held, after(list(held.values()), token)))
+            for shift, piece in list(held.items()):
+                held[shift | {link}] = swap(piece, *link)
+        for shift, piece in held.items():
+            block, row = spot(shift)
+            plane = at_bit("fsdp", 0) ^ (("fsdp", 0) in shift)
+            start = (block >> 1, (plane * n_c + row) * rows + low, 0)
             full = lax.dynamic_update_slice(full, piece[None], start)
-    return with_layout_constraint(full, Layout((0, 1, 2)))
+    full = pinned(full)
+    return full, pinned(swap(full, "tp", 0))
+
+
+def lower(values):
+    return values.astype(BF)
+
+
+def scatter_sums(sums, links):
+    high = tp_high()
+    rows = sums[0].shape[-2]
+    n_rows = sums[0].ndim - 2
+    plan = [(link, i) for i, link in enumerate(high)]
+    plan += [(link, len(high) + i) for i, link in enumerate(links)]
+    orders = turns(plan)
+    done = []
+    for (low, top), order in zip(cut(rows, len(orders)), orders):
+        part = jnp.stack([s[..., low:top, :] for s in sums])
+        part = part.reshape((2,) * len(high) + part.shape[1:])
+        for link, dim in order:
+            me = at_bit(*link)
+            give = lax.dynamic_index_in_dim(part, 1 - me, dim, keepdims=True)
+            keep = lax.dynamic_index_in_dim(part, me, dim, keepdims=True)
+            part = keep.astype(F32) + swap(lower(give), *link).astype(F32)
+        done.append(part.reshape(part.shape[-2:]))
+    return jnp.concatenate(done, axis=0)
 
 
 def scatter_rows(block_of):
-    n_t, n_c = lax.axis_size("tp"), lax.axis_size("ctx")
-    me_t, me_c = lax.axis_index("tp"), lax.axis_index("ctx")
-    sums = {}
-    for dt in range(0, n_t, 2):
-        got = swap(block_of(me_t ^ (dt + 1)).astype(BF), "tp", 0)
-        sums[dt] = (block_of(me_t ^ dt) + got.astype(F32)).astype(BF)
-    rows = sums[0].shape[0] // n_c
-    cols = sums[0].shape[1]
-    half = rows // 2
-    across = [("tp", b) for b in high_bits()]
-    done = []
-    for part, plan in enumerate(([("ctx", 0)] + across, across + [("ctx", 0)])):
-        held = {}
-        for dt, total in sums.items():
-            split = total.reshape(n_c, rows, cols)[:, part * half : (part + 1) * half]
-            for dc in range(n_c):
-                held[(dc, dt)] = lax.dynamic_index_in_dim(split, me_c ^ dc, 0, keepdims=False)
-        for axis, bit in plan:
-            left = {}
-            for (dc, dt), piece in held.items():
-                give = dc == 1 if axis == "ctx" else (dt >> bit) & 1
-                if not give:
-                    away = (1, dt) if axis == "ctx" else (dc, dt | (1 << bit))
-                    got = swap(held[away].astype(BF), axis, bit)
-                    left[(dc, dt)] = piece.astype(F32) + got.astype(F32)
-            held = left
-        done.append(held[(0, 0)])
-    return jnp.concatenate(done, axis=0)
-
-
-def ctx_half(weight, axis):
-    size = weight.shape[axis] // lax.axis_size("ctx")
-    return lax.dynamic_slice_in_dim(weight, lax.axis_index("ctx") * size, size, axis)
+    n_c = lax.axis_size("ctx")
+    core = at_bit("tp", 0)
+    sums = []
+    for i in range(lax.axis_size("tp") // 2):
+        got = swap(lower(block_of(2 * i + 1 - core)), "tp", 0)
+        total = lower(block_of(2 * i + core) + got.astype(F32))
+        sums.append(total.reshape(n_c, -1, total.shape[-1]))
+    return scatter_sums(sums, [("ctx", 0)])
+
+
+def scatter_pair(own_block, other_block):
+    n_c = lax.axis_size("ctx")
+    sums = []
+    for i in range(lax.axis_size("tp") // 2):
+        got = swap(lower(other_block(i)), "tp", 0)
+        total = lower(own_block(i) + got.astype(F32))
+        sums.append(total.reshape(2, n_c, -1, total.shape[-1]))
+    return scatter_sums(sums, [("fsdp", 0), ("ctx", 0)])
+
+
+def share(weight, axis, index, count):
+    size = weight.shape[axis] // count
+    return lax.dynamic_slice_in_dim(weight, index * size, size, axis)
 
 
 def after(value, token):
@@ -263,17 +329,49 @@
     return lax.all_gather(weight, "fsdp", axis=0, tiled=False)
 
 
+def far_groups():
+    count = lax.axis_size("fsdp")
+    return [list(range(i, count, 2)) for i in range(2)]
+
+
+def far_owners(grad):
+    return lax.psum_scatter(
+        grad, "fsdp", scatter_dimension=0, tiled=False, axis_index_groups=far_groups()
+    )
+
+
+def far_spread(weight):
+    return lax.all_gather(weight, "fsdp", axis=0, tiled=False, axis_index_groups=far_groups())
+
+
+def pair_share(block, axis, token, hold):
+    n_c = lax.axis_size("ctx")
+    place = lax.axis_index("ctx") * 2
+    plane = at_bit("fsdp", 0)
+    mine = share(block, axis, place + plane, 2 * n_c)
+    near = swap(after(share(block, axis, place + 1 - plane, 2 * n_c), token), "fsdp", 0)
+    near = after(near, hold)
+    same = at_bit("tp", 0) == plane
+    return jnp.where(same, mine, near), jnp.where(same, near, mine)
+
+
+def pair_grad(own, other, axis):
+    plane = at_bit("fsdp", 0)
+    same = at_bit("tp", 0) == plane
+    mine = jnp.where(same, own, other)
+    near = swap(jnp.where(same, other, own), "fsdp", 0)
+    pair = jnp.stack(
+        [jnp.where(plane == 0, mine, near), jnp.where(plane == 0, near, mine)]
+    )
+    return [v[i] for v in trade_ctx(pair, axis + 1) for i in range(2)]
+
+
 def trade_ctx(block, axis):
-    size = block.shape[axis] // lax.axis_size("ctx")
+    n_c = lax.axis_size("ctx")
     me = lax.axis_index("ctx")
-    own = lax.dynamic_slice_in_dim(block, me * size, size, axis)
-    give = lax.dynamic_slice_in_dim(block, (1 - me) * size, size, axis)
-    got = swap(give, "ctx", 0)
+    own = share(block, axis, me, n_c)
+    got = swap(share(block, axis, 1 - me, n_c), "ctx", 0)
     return jnp.where(me == 0, own, got), jnp.where(me == 0, got, own)
-
-
-def out_grad(block):
-    return jnp.concatenate(trade_ctx(block, 1), axis=0).astype(F32)
 
 
 def total_rows(values):
@@ -283,35 +381,37 @@
     return values
 
 
+def into(full, weight):
+    return mm(full, weight, (((0, 2), (0, 1)), ((), ())))
+
+
+def back_out(full, weight):
+    return mm(full, weight, (((0, 2), (0, 2)), ((), ())))
+
+
+def in_part(full, grads):
+    return lower(mm(full, grads, (((1,), (0,)), ((), ()))))
+
+
+def out_part(inner, full):
+    return jnp.stack(
+        [lower(mm(inner, full[i], (((0,), (0,)), ((), ())))) for i in range(full.shape[0])]
+    )
+
+
 def body(
     layer_input, attn_gain, qkv_weight, out_weight, ffn_gain, gate_up_weight, down_weight, cotangent
 ):
-    n_f = lax.axis_size("fsdp")
-    d_f = D // n_f
-    qkv_parts = [spread(ctx_half(qkv_weight[:, i], 1)) for i in range(3)]
-    out_full = spread(ctx_half(out_weight, 0))
-    gu_full = spread(ctx_half(gate_up_weight, 2).reshape(d_f, -1))
-    down_full = spread(ctx_half(down_weight, 0))
-
-    def into(full, weight):
-        return mm(full, weight, (((0, 2), (0, 1)), ((), ())))
-
-    def back_out(full, weight):
-        return mm(full, weight, (((0, 2), (0, 2)), ((), ())))
+    n_c = lax.axis_size("ctx")
+    me_c = lax.axis_index("ctx")
+    qkv_parts = [spread(share(qkv_weight[:, i], 1, me_c, n_c)) for i in range(3)]
+    out_full = spread(share(out_weight, 0, me_c, n_c))
 
     def out_blocks(inner, weight):
         return lambda t: mm(inner, lax.dynamic_index_in_dim(weight, t, 0, keepdims=False))
 
     def in_blocks(grads, weight):
         return lambda t: mm(grads, lax.dynamic_index_in_dim(weight, t, 0, keepdims=False), NT)
-
-    def in_part(full, grads):
-        return mm(full, grads, (((1,), (0,)), ((), ()))).astype(BF)
-
-    def out_part(inner, full):
-        return jnp.stack(
-            [mm(inner, full[t], (((0,), (0,)), ((), ()))).astype(BF) for t in range(n_f)]
-        )
 
     input_float = layer_input.astype(F32)
     attn_scale = attn_gain.astype(F32)
@@ -319,41 +419,57 @@
     rms_one = lax.rsqrt(row_total(jnp.sum(input_float * input_float, axis=-1)) / D + rms_epsilon)[
         :, None
     ]
-    normed_attn = (input_float * rms_one * attn_scale).astype(BF)
+    normed_attn = lower(input_float * rms_one * attn_scale)
     attn_full = gather_rows(normed_attn)
     seq_len = attn_full.shape[1]
     cosine, sine = rope_tables(seq_len)
-    cotan_full = gather_rows(after(cotangent, attn_full))
     proj = [into(attn_full, part) for part in qkv_parts]
+    cotan_full = gather_pair(after(cotangent, attn_full))
+    proj = after(proj, cotan_full)
     queries, keys, values, head_outs, norms = attend_forward(*proj, cosine, sine)
+    gu_share = pair_share(gate_up_weight, 2, tuple(proj), head_outs)
+    gu_wide = far_spread(jnp.stack(gu_share))
+    down_share = jnp.stack(pair_share(down_weight, 0, gu_share, gu_share))
+    down_full = far_spread(down_share)
+    gu_pair = [gu_wide[:, i].reshape(gu_wide.shape[0], gu_wide.shape[2], -1) for i in range(2)]
     resid = input_float + scatter_rows(out_blocks(head_outs, out_full))
+    resid = after(resid, down_share)
     rms_two = lax.rsqrt(row_total(jnp.sum(resid * resid, axis=-1)) / D + rms_epsilon)[:, None]
-    normed_ffn = (resid * rms_two * ffn_scale).astype(BF)
-    ffn_full = gather_rows(normed_ffn)
-    gate_up = into(ffn_full, gu_full)
+    normed_ffn = lower(resid * rms_two * ffn_scale)
+    ffn_full = gather_pair(normed_ffn, gu_wide)
+    gate_up = into(ffn_full[0], gu_pair[0]) + into(ffn_full[1], gu_pair[1])
     units = gate_up.shape[1] // 2
     gate = gate_up[:, :units]
     up_value = gate_up[:, units:]
     sigma = jax.nn.sigmoid(gate)
-    hidden = (gate * sigma * up_value).astype(BF)
-    down_part = out_part(hidden, cotan_full)
-    down_sum = owners(down_part)
+    hidden = lower(gate * sigma * up_value)
+    down_part = [out_part(hidden, full) for full in cotan_full]
+    down_sum = [far_owners(part) for part in down_part]
     down_full = after(down_full, down_part)
-    grad_hidden = back_out(cotan_full, down_full)
-    grad_gu = jnp.concatenate(
-        [grad_hidden * up_value * sigma * (1.0 + gate * (1.0 - sigma)), grad_hidden * gate * sigma],
-        axis=1,
-    ).astype(BF)
-    gu_part = in_part(ffn_full, grad_gu)
-    gu_sum = owners(after(gu_part, down_sum))
-    grad_nffn = after(scatter_rows(in_blocks(grad_gu, gu_full)), (gu_part, down_sum))
+    down_pair = [down_full[:, i] for i in range(2)]
+    grad_hidden = back_out(cotan_full[0], down_pair[0]) + back_out(cotan_full[1], down_pair[1])
+    grad_gu = lower(
+        jnp.concatenate(
+            [
+                grad_hidden * up_value * sigma * (1.0 + gate * (1.0 - sigma)),
+                grad_hidden * gate * sigma,
+            ],
+            axis=1,
+        )
+    )
+    gu_part = [in_part(full, grad_gu) for full in ffn_full]
+    gu_sum = [far_owners(after(part, down_sum)) for part in gu_part]
+    grad_nffn = scatter_pair(
+        lambda i: mm(grad_gu, gu_pair[0][i], NT), lambda i: mm(grad_gu, gu_pair[1][i], NT)
+    )
+    grad_nffn = after(grad_nffn, gu_part)
     ffn_term = grad_nffn * ffn_scale
     ffn_dot = row_total(jnp.sum(ffn_term * resid, axis=-1))[:, None]
     grad_resid = cotangent.astype(F32) + rms_two * ffn_term - resid * rms_two**3 * ffn_dot / D
     ffn_gain_part = jnp.sum(grad_nffn * resid * rms_two, axis=0)
-    grad_branch = grad_resid.astype(BF)
+    grad_branch = lower(grad_resid)
     branch_full = gather_rows(grad_branch)
-    grad_heads = back_out(branch_full, out_full).astype(BF)
+    grad_heads = lower(back_out(branch_full, out_full))
     out_sum = owners(out_part(head_outs, branch_full))
     grad_proj = attend_backward(
         queries, keys, values, head_outs, norms, grad_heads, cosine, sine
@@ -364,19 +480,21 @@
         in_blocks(jnp.concatenate(grad_proj, axis=1), jnp.concatenate(qkv_parts, axis=2))
     )
     hidden = after(hidden, qkv_part)
-    layer_output = (resid + scatter_rows(out_blocks(hidden, down_full))).astype(BF)
+    ffn_out = scatter_pair(
+        lambda i: mm(hidden, down_pair[0][i]), lambda i: mm(hidden, down_pair[1][i])
+    )
+    layer_output = lower(resid + ffn_out)
     attn_term = grad_nattn * attn_scale
     attn_dot = row_total(jnp.sum(attn_term * input_float, axis=-1))[:, None]
     grad_input = grad_resid + rms_one * attn_term - input_float * rms_one**3 * attn_dot / D
     attn_gain_part = jnp.sum(grad_nattn * input_float * rms_one, axis=0)
     gain_grads = total_rows(jnp.stack([attn_gain_part, ffn_gain_part]))
 
-    down_grad = out_grad(down_sum)
-    rows, other_rows = trade_ctx(gu_sum, 0)
+    down_grad = jnp.concatenate(pair_grad(*down_sum, 1), axis=0).astype(F32)
     gu_grad = jnp.concatenate(
-        [v.reshape(v.shape[0], 2, -1) for v in (rows, other_rows)], axis=2
+        [v.reshape(v.shape[0], 2, -1) for v in pair_grad(*gu_sum, 0)], axis=2
     ).astype(F32)
-    out_weight_grad = out_grad(out_sum)
+    out_weight_grad = jnp.concatenate(trade_ctx(out_sum, 1), axis=0).astype(F32)
     done = (down_grad, out_weight_grad, gu_grad, grad_input, layer_output, gain_grads)
     qkv_grad = []
     for part in qkv_sum:

time: 1840 us -> 2360 us (1.28)
  waiting for transfers between devices: 887 us -> 1230 us
  other arithmetic: 106 us -> 191 us
  local copies, waits for them, and re-layouts: 143 us -> 187 us
  matrix products: 472 us -> 511 us
  starting transfers between devices: 79 us -> 109 us
  blocking collectives: 53 us -> 26.3 us
    ppermute x97 -> x119, waiting for transfers between devices: 477 us -> 948 us  [swap(): return lax.ppermute(values, axis, flip(axis, bit))]
    all_gather x6 -> x4, waiting for transfers between devices: 294 us -> 126 us  [spread(): return lax.all_gather(weight, 'fsdp', axis=0, tiled=False)]
    all_gather x0 -> x2, waiting for transfers between devices: none -> 129 us  [far_spread(): lax.all_gather(weight, 'fsdp', axis=0, tiled=False, axis_index_groups=far...]
    reduce_scatter x6 -> x4, waiting for transfers between devices: 116 us -> 0.05 us  [owners(): return lax.psum_scatter(grad, 'fsdp', scatter_dimension=0, tiled=False)]
    dot_general x34 -> x37, matrix products: 472 us -> 511 us  [mm(): return lax.dot_general(left, right, dims, preferred_element_type=F32)]
    another operation x2 -> x20, other arithmetic: 7.49 us -> 43.5 us  [the longest x10 23 us: scatter_sums(): part = jnp.stack([s[..., low:top, :] for s in sums])]
    add x8 -> x17, other arithmetic: 16.8 us -> 49.6 us  [the longest x16 46.8 us: scatter_sums(): part = keep.astype(F32) + swap(lower(give), *link).astype(F32)]
    ppermute x97 -> x119, starting transfers between devices: 78.5 us -> 108 us  [swap(): return lax.ppermute(values, axis, flip(axis, bit))]
  transfers between devices with their start and end apart: 109 -> 133, of which waited for: 40 -> 65; matrix products, arithmetic and copies ran while one was open for 38% -> 36% of each run, Pallas kernels for 4% -> 3%
where the time goes in v3:
time: 2360 us; the launch traced here: 2350 us
  waiting for transfers between devices  1230 us (52%)
  matrix products  511 us (22%)
  other arithmetic  191 us (8%)
  local copies, waits for them, and re-layouts  187 us (8%)
  starting transfers between devices  109 us (5%)
  Pallas kernels  79.4 us (3%)
  blocking collectives  26.3 us (1%)
    ppermute x119, waiting for transfers between devices, swap(): return lax.ppermute(values, axis, flip(axis, bit))  948 us
    dot_general x37, matrix products, mm(): return lax.dot_general(left, right, dims, preferred_element_type=F32)  511 us
    all_gather x2, waiting for transfers between devices, far_spread(): lax.all_gather(weight, 'fsdp', axis=0, tiled=False, axis_index_groups=far...  129 us
    all_gather x4, waiting for transfers between devices, spread(): return lax.all_gather(weight, 'fsdp', axis=0, tiled=False)  126 us
    ppermute x119, starting transfers between devices, swap(): return lax.ppermute(values, axis, flip(axis, bit))  108 us
  transfers between devices with their start and end apart: 133, of which 65 were waited for; matrix products, arithmetic and copies ran while one was open for 36% of the time, Pallas kernels for 3%

profile of v3, /device:TPU:0, one launch (start us, length us, event | category | flops | bytes accessed | tf_op | source)
XLA Modules:
  0.0 2348.0 jit_solution(12811379692853835573)
XLA Ops:
  34.4 13.6 collective-permute-done
  59.3 21.8 collective-permute-done.7
  83.0 18.0 collective-permute-done.2
  124.5 11.6 collective-permute-done.14
  148.2 19.0 collective-permute-done.16
  171.0 66.0 %collective-permute-done.18 = bf16[352,1024]{1,0:T(8,128)(2,1)S(1)} collective-permute-done((bf16[352,1024]{1,0:T(8,128)(2,1)S(1)}, bf16[352,1024]{1,0:T(8,128)(2,1)S(1)}, u32[]{:S(2)}, u32[]{:S(2)}) %collective-permute-start.18) | collective-permute-done | bytes 720928 | tf_op jit(solution)/shard_map/ppermute | solution.py:195
  237.9 14.5 collective-permute-done.19
  256.9 11.0 collective-permute-done.20
  272.2 11.1 collective-permute-done.22
  285.8 11.9 collective-permute-done.23
  301.5 13.6 collective-permute-done.25
  318.4 12.1 collective-permute-done.26
  331.8 10.9 collective-permute-done.27
  348.9 11.4 collective-permute-done.33
  379.0 15.7 convolution_bitcast_fusion.v_in
  394.7 15.0 convolution_bitcast_fusion.1.k_in
  409.6 41.1 %all-gather.13.cloned.1.call-done = bf16[4096,1,512]{2,0,1:T(8,128)(2,1)} async-done(((bf16[1024,1,512]{2,0,1:T(8,128)(2,1)}), bf16[4096,1,512]{2,0,1:T(8,128)(2,1)}) %all-gather.13.cloned.1.call-update) | async-done | bytes 4194320 | tf_op jit(solution)/shard_map/all_gather | solution.py:329
  450.7 14.9 convolution_bitcast_fusion.2.q_in
  465.6 35.5 %shard_map.143 = (bf16[2048,512]{1,0:T(8,128)(2,1)S(1)}, bf16[2048,512]{1,0:T(8,128)(2,1)}, bf16[2048,512]{1,0:T(8,128)(2,1)}, bf16[2048,512]{1,0:T(8,128)(2,1)}, f32[4,1,2048]{2,1,0:T(1,128)S(1)}) custom-call(f32[2048,512]{1,0:T(8,128)} %convolution_bitcast_fusion.2.q_in, f32[2048,512]{1,0:T(8,128)} %convolution_bitcast_fusion.1.k_in, ...), custom_call_target="tpu_custom_call" | custom-call | flops 40265318400 | bytes 20971520 | tf_op jit(solution)/shard_map/pallas_call | solution.py:88
  502.5 85.0 %all-gather.19.cloned.1.call-done = bf16[2048,1024]{1,0:T(8,128)(2,1)} async-done(((bf16[512,1024]{1,0:T(8,128)(2,1)}), bf16[2048,1024]{1,0:T(8,128)(2,1)}) %all-gather.19.cloned.1.call-update) | async-done | bytes 4194320 | tf_op jit(solution)/shard_map/all_gather | solution.py:329
  635.5 36.1 %collective-permute-done.38 = bf16[1,2,512,1024]{3,2,1,0:T(8,128)(2,1)} collective-permute-done((bf16[1,2,512,1024]{3,2,1,0:T(8,128)(2,1)}, bf16[1,2,512,1024]{3,2,1,0:T(8,128)(2,1)}, u32[]{:S(2)}, u32[]{:S(2)}) %collective-permute-start.38) | collective-permute-done | bytes 2097184 | tf_op jit(solution)/shard_map/ppermute | solution.py:195
  683.2 13.6 collective-permute-done.43
  728.9 11.4 collective-permute-done.44
  740.3 129.3 %all-gather.21.cloned.1.call-done = bf16[4,1024,2,688]{1,3,2,0:T(8,128)(2,1)} async-done(((bf16[2,1024,2,688]{1,3,2,0:T(8,128)(2,1)}), bf16[4,1024,2,688]{1,3,2,0:T(8,128)(2,1)}) %all-gather.21.cloned.1.call-update) | async-done | bytes 11272208 | tf_op jit(solution)/shard_map/all_gather | solution.py:344
  891.0 11.9 collective-permute-done.46
  907.8 28.7 %collective-permute-done.49 = bf16[352,1024]{1,0:T(8,128)(2,1)S(1)} collective-permute-done((bf16[352,1024]{1,0:T(8,128)(2,1)S(1)}, bf16[352,1024]{1,0:T(8,128)(2,1)S(1)}, u32[]{:S(2)}, u32[]{:S(2)}) %collective-permute-start.49) | collective-permute-done | bytes 720928 | tf_op jit(solution)/shard_map/ppermute | solution.py:195
  938.8 13.1 collective-permute-done.50
  972.7 11.0 collective-permute-done.60
  984.2 14.9 collective-permute-done.56
  1036.1 10.9 fusion.132
  1053.0 30.6 %fusion.141 = f32[4096,1376,1]{0,1,2:T(8,128)} fusion(bf16[2,4096,1024]{2,1,0:T(8,128)(2,1)} %collective-permute-done.65, bf16[2,1024,1376]{1,2,0:T(8,128)(2,1)} %bitcast.545), kind=kOutput, calls=%fused_computation.430 | convolution fusion | flops 23085449216 | bytes 44957696 | tf_op jit(solution)/shard_map/dot_general | solution.py:21
  1083.6 31.0 %bitcast_add_fusion = f32[4096,1376]{0,1:T(8,128)} fusion(f32[4096,1376,1]{0,1,2:T(8,128)} %fusion.141, bf16[2,4096,1024]{2,1,0:T(8,128)(2,1)} %bitcast_dynamic-update-slice_fusion.64, bf16[2,1024,1376]{1,2,0:T(8,128)(2,1)S(1)} %bitcast.544), kind=kOutput, calls=%fused_computation | convolution fusion | flops 23091085312 | bytes 67502080 | tf_op jit(solution)/shard_map/dot_general | solution.py:21
  1165.3 18.9 fusion.52
  1184.3 29.0 %multiply_convert_fusion.1 = (bf16[4096,688]{0,1:T(8,128)(2,1)}, bf16[4096,688]{0,1:T(8,128)(2,1)}) fusion(f32[4096,1376]{0,1:T(8,128)} %bitcast_add_fusion, f32[4096,688,1]{0,1,2:T(8,128)} %fusion.52, bf16[2,4096,1024]{2,1,0:T(8,128)(2,1)} %bitcast_dynamic-update-slice_fusion.72, bf16[2,2,688,1024]{3,2,1,0:T(8,128)(2,1)} %bitcast.581), kind=kOutput, calls=%fused_computation.13 | convolution fusion | flops 11582177280 | bytes 64684032 | tf_op jit(solution)/shard_map/dot_general | solution.py:21
  1213.3 19.6 convolution_convert_fusion.2
  1233.1 18.6 convolution_convert_fusion.3
  1252.1 30.8 %fusion.11 = bf16[2,1024,1376]{1,2,0:T(8,128)(2,1)} fusion(bf16[2,4096,1024]{2,1,0:T(8,128)(2,1)} %bitcast_dynamic-update-slice_fusion.64, bf16[4096,688]{0,1:T(8,128)(2,1)} %get-tuple-element.77, bf16[4096,688]{0,1:T(8,128)(2,1)} %get-tuple-element.76), kind=kOutput, calls=%fused_computation.73 | convolution fusion | flops 23110811648 | bytes 33685504 | tf_op jit(solution)/shard_map/dot_general | solution.py:21
  1282.9 24.3 %reduce-scatter.11.cloned.1.call-done = bf16[1,688,1024]{2,1,0:T(8,128)(2,1)} async-done(((bf16[2,688,1024]{2,1,0:T(8,128)(2,1)}), bf16[1,688,1024]{2,1,0:T(8,128)(2,1)}) %reduce-scatter.11.cloned.1.call-update) | async-done | bytes 1409040 | tf_op jit(solution)/shard_map/reduce_scatter | solution.py:338
  1307.3 20.6 add_convert_fusion.2
  1327.9 19.9 add_convert_fusion.3
  1368.6 46.0 %collective-permute-done.74 = bf16[2,2,1,320,1024]{4,3,2,1,0:T(8,128)(2,1)} collective-permute-done((bf16[2,2,1,320,1024]{4,3,2,1,0:T(8,128)(2,1)}, bf16[2,2,1,320,1024]{4,3,2,1,0:T(8,128)(2,1)}, u32[]{:S(2)}, u32[]{:S(2)}) %collective-permute-start.74) | collective-permute-done | bytes 2621472 | tf_op jit(solution)/shard_map/ppermute | solution.py:195
  1435.1 42.5 %collective-permute-done.71 = bf16[2,1,2,352,1024]{4,3,2,1,0:T(8,128)(2,1)} collective-permute-done((bf16[2,1,2,352,1024]{4,3,2,1,0:T(8,128)(2,1)}, bf16[2,1,2,352,1024]{4,3,2,1,0:T(8,128)(2,1)}, u32[]{:S(2)}, u32[]{:S(2)}) %collective-permute-start.71) | collective-permute-done | bytes 2883616 | tf_op jit(solution)/shard_map/ppermute | solution.py:195
  1485.1 29.2 %fusion.8 = bf16[2,1024,1376]{1,2,0:T(8,128)(2,1)} fusion(bf16[2,4096,1024]{2,1,0:T(8,128)(2,1)} %collective-permute-done.65, bf16[4096,688]{0,1:T(8,128)(2,1)} %get-tuple-element.77, bf16[4096,688]{0,1:T(8,128)(2,1)S(1)} %bitcast.592), kind=kOutput, calls=%fused_computation.72 | convolution fusion | flops 23110811648 | bytes 33685504 | tf_op jit(solution)/shard_map/dot_general | solution.py:21
  1575.2 15.2 collective-permute-done.77
  1600.4 15.5 collective-permute-done.84
  1616.5 19.9 collective-permute-done.79
  1664.6 15.3 bitcast_convert_fusion.g
  1679.9 43.9 %shard_map.144 = (bf16[2048,512]{1,0:T(8,128)(2,1)S(1)}, bf16[2048,512]{1,0:T(8,128)(2,1)}, bf16[2048,512]{1,0:T(8,128)(2,1)}) custom-call(bf16[2048,512]{1,0:T(8,128)(2,1)} %copy-done.6, bf16[2048,512]{1,0:T(8,128)(2,1)} %get-tuple-element.56.k, bf16[2048,512]{1,0:T(8,128)(2,1)} %get-tuple-element.57.v, bf16[2048,512]{1,0:T(8,128)(2,1)} %get-tuple-element.43.o, ...), custom_call_target="tpu_custom_call" | custom-call | flops 51002736640 | bytes 16777216 | tf_op jit(solution)/shard_map/pallas_call | solution.py:164
  1723.9 13.9 convolution_convert_fusion.10
  1740.2 12.7 convolution_convert_fusion.4
  1774.6 13.9 convolution_convert_fusion.9
  1794.1 11.6 convolution_convert_fusion
  1816.3 102.8 %collective-permute-done.114 = bf16[1024,1376]{0,1:T(8,128)(2,1)S(1)} collective-permute-done((bf16[1024,1376]{0,1:T(8,128)(2,1)S(1)}, bf16[1024,1376]{0,1:T(8,128)(2,1)S(1)}, u32[]{:S(2)}, u32[]{:S(2)}) %collective-permute-start.114) | collective-permute-done | bytes 2818080 | tf_op jit(solution)/shard_map/ppermute | solution.py:195
  1923.2 11.4 add_convert_fusion.4
  1934.6 12.2 add_convert_fusion.5
  1966.3 35.8 %collective-permute-done.104 = bf16[1,2,512,1024]{3,2,1,0:T(8,128)(2,1)} collective-permute-done((bf16[1,2,512,1024]{3,2,1,0:T(8,128)(2,1)}, bf16[1,2,512,1024]{3,2,1,0:T(8,128)(2,1)}, u32[]{:S(2)}, u32[]{:S(2)}) %collective-permute-start.104) | collective-permute-done | bytes 2097184 | tf_op jit(solution)/shard_map/ppermute | solution.py:195
  2007.7 58.5 %collective-permute-done.106 = bf16[2,1,512,1024]{3,2,1,0:T(8,128)(2,1)} collective-permute-done((bf16[2,1,512,1024]{3,2,1,0:T(8,128)(2,1)}, bf16[2,1,512,1024]{3,2,1,0:T(8,128)(2,1)}, u32[]{:S(2)}, u32[]{:S(2)}) %collective-permute-start.106) | collective-permute-done | bytes 2097184 | tf_op jit(solution)/shard_map/ppermute | solution.py:195
  2074.5 14.0 collective-permute-done.105
  2094.4 11.1 add_convert_fusion
  2114.0 13.4 add_convert_fusion.1
  2146.0 49.1 %collective-permute-done.108 = f32[2,1024]{1,0:T(2,128)S(1)} collective-permute-done((f32[2,1024]{1,0:T(2,128)S(1)}, f32[2,1024]{1,0:T(2,128)S(1)}, u32[]{:S(2)}, u32[]{:S(2)}) %collective-permute-start.108) | collective-permute-done | bytes 8224 | tf_op jit(solution)/shard_map/ppermute | solution.py:195
  2195.2 11.3 maximum_convert_fusion
  2281.8 11.7 collective-permute-done.95
  2317.8 11.1 collective-permute-done.117
  (749 shorter events, 731.0 us)
Async XLA Ops:
  7.2 371.8 %all-gather.17.cloned.1.call-start = ((), (), s32[]{:S(2)}) async-start(), calls=%async_computation.18 | async-start | bytes 5242880 | tf_op jit(solution)/shard_map/all_gather | solution.py:329
  32.2 362.4 %all-gather.15.cloned.1.call-start = ((), (), s32[]{:S(2)}) async-start(), calls=%async_computation.17 | async-start | bytes 5242880 | tf_op jit(solution)/shard_map/all_gather | solution.py:329
  32.8 48.3 %collective-permute-start.7 = (bf16[512,1024]{1,0:T(8,128)(2,1)}, bf16[512,1024]{1,0:T(8,128)(2,1)S(1)}, u32[]{:S(2)}, u32[]{:S(2)}) collective-permute-start(bf16[512,1024]{1,0:T(8,128)(2,1)} %get-tuple-element.125), channel_id=1, source_target_pairs={{0,2},{1,3},{2,0},{3,1},{4,6},{5,7},{6,4},{7,5},{8,10},{9,11},{10,... | collective-permute-start | bytes 3145736 | tf_op jit(solution)/shard_map/ppermute | solution.py:195
  48.0 53.1 %collective-permute-start.2 = (bf16[512,1024]{1,0:T(8,128)(2,1)}, bf16[512,1024]{1,0:T(8,128)(2,1)}, u32[]{:S(2)}, u32[]{:S(2)}) collective-permute-start(bf16[512,1024]{1,0:T(8,128)(2,1)} %collective-permute-done), channel_id=1, source_target_pairs={{0,2},{1,3},{2,0},{3,1},{4,6},{5,7},{6,4},{7,5},{8,10},{9,11},{10,... | collective-permute-start | bytes 3145736 | tf_op jit(solution)/shard_map/ppermute | solution.py:195
  51.9 51.8 %collective-permute-start.4 = (bf16[512,1024]{1,0:T(8,128)(2,1)}, bf16[512,1024]{1,0:T(8,128)(2,1)S(1)}, u32[]{:S(2)}, u32[]{:S(2)}) collective-permute-start(bf16[512,1024]{1,0:T(8,128)(2,1)} %collective-permute-done), channel_id=1, source_target_pairs={{0,1},{1,0},{2,3},{3,2},{4,5},{5,4},{6,7},{7,6},{8,9},{9,8},{10,11... | collective-permute-start | bytes 3145736 | tf_op jit(solution)/shard_map/ppermute | solution.py:195
  58.8 45.6 %collective-permute-start.8 = (bf16[512,1024]{1,0:T(8,128)(2,1)S(1)}, bf16[512,1024]{1,0:T(8,128)(2,1)S(1)}, u32[]{:S(2)}, u32[]{:S(2)}) collective-permute-start(bf16[512,1024]{1,0:T(8,128)(2,1)S(1)} %copy-done.88), channel_id=1, source_target_pairs={{0,4},{4,0},{1,5},{5,1},{2,6},{6,2},{3,7},{7,3},{8,12},{12,8},{9,1... | collective-permute-start | bytes 3145736 | tf_op jit(solution)/shard_map/ppermute | solution.py:195
  120.7 330.0 %all-gather.13.cloned.1.call-start = ((), (), s32[]{:S(2)}) async-start(), calls=%async_computation.16 | async-start | bytes 5242880 | tf_op jit(solution)/shard_map/all_gather | solution.py:329
  120.8 48.9 %collective-permute-start.17 = (bf16[352,1024]{1,0:T(8,128)(2,1)}, bf16[352,1024]{1,0:T(8,128)(2,1)S(1)}, u32[]{:S(2)}, u32[]{:S(2)}) collective-permute-start(bf16[352,1024]{1,0:T(8,128)(2,1)} %get-tuple-element.124), channel_id=1, source_target_pairs={{0,8},{8,0},{16,24},{24,16},{1,9},{9,1},{17,25},{25,17},{2,10},{10... | collective-permute-start | bytes 2162696 | tf_op jit(solution)/shard_map/ppermute | solution.py:195
  123.6 131.8 %collective-permute-start.21 = (bf16[352,1024]{1,0:T(8,128)(2,1)}, bf16[352,1024]{1,0:T(8,128)(2,1)S(1)}, u32[]{:S(2)}, u32[]{:S(2)}) collective-permute-start(bf16[352,1024]{1,0:T(8,128)(2,1)} %get-tuple-element.123), channel_id=1, source_target_pairs={{0,2},{1,3},{2,0},{3,1},{4,6},{5,7},{6,4},{7,5},{8,10},{9,11},{10,... | collective-permute-start | bytes 2162696 | tf_op jit(solution)/shard_map/ppermute | solution.py:195
  124.1 130.7 %collective-permute-start.28 = (bf16[320,1024]{1,0:T(8,128)(2,1)S(1)}, bf16[320,1024]{1,0:T(8,128)(2,1)S(1)}, u32[]{:S(2)}, u32[]{:S(2)}) collective-permute-start(bf16[320,1024]{1,0:T(8,128)(2,1)S(1)} %slice.218), channel_id=1, source_target_pairs={{0,8},{8,0},{16,24},{24,16},{1,9},{9,1},{17,25},{25,17},{2,10},{10... | collective-permute-start | bytes 1966088 | tf_op jit(solution)/shard_map/ppermute | solution.py:195
  145.7 91.3 %collective-permute-start.18 = (bf16[352,1024]{1,0:T(8,128)(2,1)S(1)}, bf16[352,1024]{1,0:T(8,128)(2,1)S(1)}, u32[]{:S(2)}, u32[]{:S(2)}) collective-permute-start(bf16[352,1024]{1,0:T(8,128)(2,1)S(1)} %collective-permute-done.14), channel_id=1, source_target_pairs={{0,8},{8,0},{16,24},{24,16},{1,9},{9,1},{17,25},{25,17},{2,10},{10... | collective-permute-start | bytes 2162696 | tf_op jit(solution)/shard_map/ppermute | solution.py:195
  167.1 85.3 %collective-permute-start.19 = (bf16[352,1024]{1,0:T(8,128)(2,1)S(1)}, bf16[352,1024]{1,0:T(8,128)(2,1)S(1)}, u32[]{:S(2)}, u32[]{:S(2)}) collective-permute-start(bf16[352,1024]{1,0:T(8,128)(2,1)S(1)} %collective-permute-done.15), channel_id=1, source_target_pairs={{0,8},{8,0},{16,24},{24,16},{1,9},{9,1},{17,25},{25,17},{2,10},{10... | collective-permute-start | bytes 2162696 | tf_op jit(solution)/shard_map/ppermute | solution.py:195
  169.7 98.2 %collective-permute-start.20 = (bf16[352,1024]{1,0:T(8,128)(2,1)S(1)}, bf16[352,1024]{1,0:T(8,128)(2,1)S(1)}, u32[]{:S(2)}, u32[]{:S(2)}) collective-permute-start(bf16[352,1024]{1,0:T(8,128)(2,1)S(1)} %collective-permute-done.16), channel_id=1, source_target_pairs={{0,8},{8,0},{16,24},{24,16},{1,9},{9,1},{17,25},{25,17},{2,10},{10... | collective-permute-start | bytes 2162696 | tf_op jit(solution)/shard_map/ppermute | solution.py:195
  237.0 46.3 %collective-permute-start.22 = (bf16[352,1024]{1,0:T(8,128)(2,1)S(1)}, bf16[352,1024]{1,0:T(8,128)(2,1)S(1)}, u32[]{:S(2)}, u32[]{:S(2)}) collective-permute-start(bf16[352,1024]{1,0:T(8,128)(2,1)S(1)} %copy-done.89), channel_id=1, source_target_pairs={{0,8},{8,0},{16,24},{24,16},{1,9},{9,1},{17,25},{25,17},{2,10},{10... | collective-permute-start | bytes 2162696 | tf_op jit(solution)/shard_map/ppermute | solution.py:195
  252.5 47.6 %collective-permute-start.24 = (bf16[352,1024]{1,0:T(8,128)(2,1)S(1)}, bf16[352,1024]{1,0:T(8,128)(2,1)S(1)}, u32[]{:S(2)}, u32[]{:S(2)}) collective-permute-start(bf16[352,1024]{1,0:T(8,128)(2,1)S(1)} %copy-done.89), channel_id=1, source_target_pairs={{0,4},{4,0},{1,5},{5,1},{2,6},{6,2},{3,7},{7,3},{8,12},{12,8},{9,1... | collective-permute-start | bytes 2162696 | tf_op jit(solution)/shard_map/ppermute | solution.py:195
  254.9 61.5 %collective-permute-start.29 = (bf16[320,1024]{1,0:T(8,128)(2,1)S(1)}, bf16[320,1024]{1,0:T(8,128)(2,1)S(1)}, u32[]{:S(2)}, u32[]{:S(2)}) collective-permute-start(bf16[320,1024]{1,0:T(8,128)(2,1)S(1)} %slice.218), channel_id=1, source_target_pairs={{0,4},{4,0},{1,5},{5,1},{2,6},{6,2},{3,7},{7,3},{8,12},{12,8},{9,1... | collective-permute-start | bytes 1966088 | tf_op jit(solution)/shard_map/ppermute | solution.py:195
  255.4 62.6 %collective-permute-start.30 = (bf16[320,1024]{1,0:T(8,128)(2,1)S(1)}, bf16[320,1024]{1,0:T(8,128)(2,1)S(1)}, u32[]{:S(2)}, u32[]{:S(2)}) collective-permute-start(bf16[320,1024]{1,0:T(8,128)(2,1)S(1)} %collective-permute-done.28), channel_id=1, source_target_pairs={{0,4},{4,0},{1,5},{5,1},{2,6},{6,2},{3,7},{7,3},{8,12},{12,8},{9,1... | collective-permute-start | bytes 1966088 | tf_op jit(solution)/shard_map/ppermute | solution.py:195
  368.3 97.3 %collective-permute-start.35 = (bf16[2,4096,1024]{2,1,0:T(8,128)(2,1)}, bf16[2,4096,1024]{2,1,0:T(8,128)(2,1)}, u32[]{:S(2)}, u32[]{:S(2)}) collective-permute-start(bf16[2,4096,1024]{2,1,0:T(8,128)(2,1)} %bitcast_dynamic-update-slice_fusion.72), channel_id=1, source_target_pairs={{0,1},{1,0},{2,3},{3,2},{4,5},{5,4},{6,7},{7,6},{8,9},{9,8},{10,11... | collective-permute-start | bytes 50331656 | tf_op jit(solution)/shard_map/ppermute | solution.py:195
  369.4 218.1 %all-gather.19.cloned.1.call-start = ((), (), s32[]{:S(2)}) async-start(), calls=%async_computation.19 | async-start | bytes 5242880 | tf_op jit(solution)/shard_map/all_gather | solution.py:329
  370.5 499.1 %all-gather.21.cloned.1.call-start = ((), (), s32[]{:S(2)}) async-start(), calls=%async_computation.20 | async-start | bytes 16908288 | tf_op jit(solution)/shard_map/all_gather | solution.py:344
  465.6 134.4 %collective-permute-start.42 = (bf16[1024,2,688]{0,2,1:T(8,128)(2,1)}, bf16[1024,2,688]{0,2,1:T(8,128)(2,1)}, u32[]{:S(2)}, u32[]{:S(2)}) collective-permute-start(bf16[1024,2,688]{0,2,1:T(8,128)(2,1)} %constant_dynamic-slice_fusion.3), channel_id=1, source_target_pairs={{0,8},{8,0},{16,24},{24,16},{1,9},{9,1},{17,25},{25,17},{2,10},{10... | collective-permute-start | bytes 8454152 | tf_op jit(solution)/shard_map/ppermute | solution.py:195
  607.2 558.2 %all-gather.23.cloned.1.call-start = ((), (), s32[]{:S(2)}) async-start(), calls=%async_computation.21 | async-start | bytes 8454144 | tf_op jit(solution)/shard_map/all_gather | solution.py:344
  623.7 47.8 %collective-permute-start.38 = (bf16[1,2,512,1024]{3,2,1,0:T(8,128)(2,1)}, bf16[1,2,512,1024]{3,2,1,0:T(8,128)(2,1)}, u32[]{:S(2)}, u32[]{:S(2)}) collective-permute-start(bf16[1,2,512,1024]{3,2,1,0:T(8,128)(2,1)} %fusion.65), channel_id=1, source_target_pairs={{0,2},{1,3},{2,0},{3,1},{4,6},{5,7},{6,4},{7,5},{8,10},{9,11},{10,... | collective-permute-start | bytes 6291464 | tf_op jit(solution)/shard_map/ppermute | solution.py:195
  628.3 48.9 %collective-permute-start.40 = (bf16[2,1,512,1024]{3,2,1,0:T(8,128)(2,1)}, bf16[2,1,512,1024]{3,2,1,0:T(8,128)(2,1)}, u32[]{:S(2)}, u32[]{:S(2)}) collective-permute-start(bf16[2,1,512,1024]{3,2,1,0:T(8,128)(2,1)} %fusion.63), channel_id=1, source_target_pairs={{0,4},{4,0},{1,5},{5,1},{2,6},{6,2},{3,7},{7,3},{8,12},{12,8},{9,1... | collective-permute-start | bytes 6291464 | tf_op jit(solution)/shard_map/ppermute | solution.py:195
  632.5 64.2 %collective-permute-start.43 = (bf16[688,1024]{1,0:T(8,128)(2,1)}, bf16[688,1024]{1,0:T(8,128)(2,1)}, u32[]{:S(2)}, u32[]{:S(2)}) collective-permute-start(bf16[688,1024]{1,0:T(8,128)(2,1)} %constant_dynamic-slice_fusion.4), channel_id=1, source_target_pairs={{0,8},{8,0},{16,24},{24,16},{1,9},{9,1},{17,25},{25,17},{2,10},{10... | collective-permute-start | bytes 4227080 | tf_op jit(solution)/shard_map/ppermute | solution.py:195
  724.2 149.4 %collective-permute-start.51 = (bf16[352,1024]{1,0:T(8,128)(2,1)S(1)}, bf16[352,1024]{1,0:T(8,128)(2,1)S(1)}, u32[]{:S(2)}, u32[]{:S(2)}) collective-permute-start(bf16[352,1024]{1,0:T(8,128)(2,1)S(1)} %get-tuple-element.51), channel_id=1, source_target_pairs={{0,2},{1,3},{2,0},{3,1},{4,6},{5,7},{6,4},{7,5},{8,10},{9,11},{10,... | collective-permute-start | bytes 2162696 | tf_op jit(solution)/shard_map/ppermute | solution.py:195
  725.8 145.9 %collective-permute-start.58 = (bf16[320,1024]{1,0:T(8,128)(2,1)S(1)}, bf16[320,1024]{1,0:T(8,128)(2,1)}, u32[]{:S(2)}, u32[]{:S(2)}) collective-permute-start(bf16[320,1024]{1,0:T(8,128)(2,1)S(1)} %slice.284), channel_id=1, source_target_pairs={{0,8},{8,0},{16,24},{24,16},{1,9},{9,1},{17,25},{25,17},{2,10},{10... | collective-permute-start | bytes 1966088 | tf_op jit(solution)/shard_map/ppermute | solution.py:195
  873.7 82.5 %collective-permute-start.52 = (bf16[352,1024]{1,0:T(8,128)(2,1)S(1)}, bf16[352,1024]{1,0:T(8,128)(2,1)S(1)}, u32[]{:S(2)}, u32[]{:S(2)}) collective-permute-start(bf16[352,1024]{1,0:T(8,128)(2,1)S(1)} %get-tuple-element.51), channel_id=1, source_target_pairs={{0,8},{8,0},{16,24},{24,16},{1,9},{9,1},{17,25},{25,17},{2,10},{10... | collective-permute-start | bytes 2162696 | tf_op jit(solution)/shard_map/ppermute | solution.py:195
  888.6 79.7 %collective-permute-start.54 = (bf16[352,1024]{1,0:T(8,128)(2,1)S(1)}, bf16[352,1024]{1,0:T(8,128)(2,1)S(1)}, u32[]{:S(2)}, u32[]{:S(2)}) collective-permute-start(bf16[352,1024]{1,0:T(8,128)(2,1)S(1)} %get-tuple-element.51), channel_id=1, source_target_pairs={{0,4},{4,0},{1,5},{5,1},{2,6},{6,2},{3,7},{7,3},{8,12},{12,8},{9,1... | collective-permute-start | bytes 2162696 | tf_op jit(solution)/shard_map/ppermute | solution.py:195
  903.8 48.1 %collective-permute-start.50 = (bf16[352,1024]{1,0:T(8,128)(2,1)S(1)}, bf16[352,1024]{1,0:T(8,128)(2,1)S(1)}, u32[]{:S(2)}, u32[]{:S(2)}) collective-permute-start(bf16[352,1024]{1,0:T(8,128)(2,1)S(1)} %collective-permute-done.46), channel_id=1, source_target_pairs={{0,8},{8,0},{16,24},{24,16},{1,9},{9,1},{17,25},{25,17},{2,10},{10... | collective-permute-start | bytes 2162696 | tf_op jit(solution)/shard_map/ppermute | solution.py:195
  906.8 59.1 %collective-permute-start.53 = (bf16[352,1024]{1,0:T(8,128)(2,1)S(1)}, bf16[352,1024]{1,0:T(8,128)(2,1)S(1)}, u32[]{:S(2)}, u32[]{:S(2)}) collective-permute-start(bf16[352,1024]{1,0:T(8,128)(2,1)S(1)} %collective-permute-done.51), channel_id=1, source_target_pairs={{0,8},{8,0},{16,24},{24,16},{1,9},{9,1},{17,25},{25,17},{2,10},{10... | collective-permute-start | bytes 2162696 | tf_op jit(solution)/shard_map/ppermute | solution.py:195
  969.7 46.5 %collective-permute-start.61 = (bf16[320,1024]{1,0:T(8,128)(2,1)S(1)}, bf16[320,1024]{1,0:T(8,128)(2,1)S(1)}, u32[]{:S(2)}, u32[]{:S(2)}) collective-permute-start(bf16[320,1024]{1,0:T(8,128)(2,1)S(1)} %slice.284), channel_id=1, source_target_pairs={{0,2},{1,3},{2,0},{3,1},{4,6},{5,7},{6,4},{7,5},{8,10},{9,11},{10,... | collective-permute-start | bytes 1966088 | tf_op jit(solution)/shard_map/ppermute | solution.py:195
  971.3 45.9 %collective-permute-start.62 = (bf16[320,1024]{1,0:T(8,128)(2,1)}, bf16[320,1024]{1,0:T(8,128)(2,1)S(1)}, u32[]{:S(2)}, u32[]{:S(2)}) collective-permute-start(bf16[320,1024]{1,0:T(8,128)(2,1)} %collective-permute-done.58), channel_id=1, source_target_pairs={{0,2},{1,3},{2,0},{3,1},{4,6},{5,7},{6,4},{7,5},{8,10},{9,11},{10,... | collective-permute-start | bytes 1966088 | tf_op jit(solution)/shard_map/ppermute | solution.py:195
  1027.5 255.4 %reduce-scatter.13.cloned.1.call-start = ((), (), s32[]{:S(2)}) async-start(), calls=%async_computation.10 | async-start | bytes 4227072 | tf_op jit(solution)/shard_map/reduce_scatter | solution.py:338
  1165.3 141.9 %reduce-scatter.11.cloned.1.call-start = ((), (), s32[]{:S(2)}) async-start(), calls=%async_computation.9 | async-start | bytes 4227072 | tf_op jit(solution)/shard_map/reduce_scatter | solution.py:338
  1232.9 74.3 %collective-permute-start.67 = (bf16[4096,1024]{1,0:T(8,128)(2,1)}, bf16[4096,1024]{1,0:T(8,128)(2,1)}, u32[]{:S(2)}, u32[]{:S(2)}) collective-permute-start(bf16[4096,1024]{1,0:T(8,128)(2,1)} %convolution_convert_fusion.2), channel_id=1, source_target_pairs={{0,1},{1,0},{2,3},{3,2},{4,5},{5,4},{6,7},{7,6},{8,9},{9,8},{10,11... | collective-permute-start | bytes 25165832 | tf_op jit(solution)/shard_map/ppermute | solution.py:195
  1233.1 555.5 %reduce-scatter.17.cloned.1.call-start = ((), (), s32[]{:S(2)}) async-start(), calls=%async_computation.12 | async-start | bytes 8454144 | tf_op jit(solution)/shard_map/reduce_scatter | solution.py:338
  1251.7 76.2 %collective-permute-start.66 = (bf16[4096,1024]{1,0:T(8,128)(2,1)}, bf16[4096,1024]{1,0:T(8,128)(2,1)}, u32[]{:S(2)}, u32[]{:S(2)}) collective-permute-start(bf16[4096,1024]{1,0:T(8,128)(2,1)} %convolution_convert_fusion.3), channel_id=1, source_target_pairs={{0,1},{1,0},{2,3},{3,2},{4,5},{5,4},{6,7},{7,6},{8,9},{9,8},{10,11... | collective-permute-start | bytes 25165832 | tf_op jit(solution)/shard_map/ppermute | solution.py:195
  1307.2 481.3 %reduce-scatter.19.cloned.1.call-start = ((), (), s32[]{:S(2)}) async-start(), calls=%async_computation.13 | async-start | bytes 8454144 | tf_op jit(solution)/shard_map/reduce_scatter | solution.py:338
  1355.7 58.9 %collective-permute-start.74 = (bf16[2,2,1,320,1024]{4,3,2,1,0:T(8,128)(2,1)}, bf16[2,2,1,320,1024]{4,3,2,1,0:T(8,128)(2,1)}, u32[]{:S(2)}, u32[]{:S(2)}) collective-permute-start(bf16[2,2,1,320,1024]{4,3,2,1,0:T(8,128)(2,1)} %fusion.57), channel_id=1, source_target_pairs={{0,4},{4,0},{1,5},{5,1},{2,6},{6,2},{3,7},{7,3},{8,12},{12,8},{9,1... | collective-permute-start | bytes 7864328 | tf_op jit(solution)/shard_map/ppermute | solution.py:195
  1363.9 65.7 %collective-permute-start.68 = (bf16[1,2,2,352,1024]{4,3,2,1,0:T(8,128)(2,1)}, bf16[1,2,2,352,1024]{4,3,2,1,0:T(8,128)(2,1)}, u32[]{:S(2)}, u32[]{:S(2)}) collective-permute-start(bf16[1,2,2,352,1024]{4,3,2,1,0:T(8,128)(2,1)} %fusion.48), channel_id=1, source_target_pairs={{0,2},{1,3},{2,0},{3,1},{4,6},{5,7},{6,4},{7,5},{8,10},{9,11},{10,... | collective-permute-start | bytes 8650760 | tf_op jit(solution)/shard_map/ppermute | solution.py:195
  1368.6 109.0 %collective-permute-start.71 = (bf16[2,1,2,352,1024]{4,3,2,1,0:T(8,128)(2,1)}, bf16[2,1,2,352,1024]{4,3,2,1,0:T(8,128)(2,1)}, u32[]{:S(2)}, u32[]{:S(2)}) collective-permute-start(bf16[2,1,2,352,1024]{4,3,2,1,0:T(8,128)(2,1)} %fusion.46), channel_id=1, source_target_pairs={{0,8},{8,0},{16,24},{24,16},{1,9},{9,1},{17,25},{25,17},{2,10},{10... | collective-permute-start | bytes 8650760 | tf_op jit(solution)/shard_map/ppermute | solution.py:195
  1420.0 94.4 %collective-permute-start.75 = (bf16[1,2,1,320,1024]{4,3,2,1,0:T(8,128)(2,1)}, bf16[1,2,1,320,1024]{4,3,2,1,0:T(8,128)(2,1)}, u32[]{:S(2)}, u32[]{:S(2)}) collective-permute-start(bf16[1,2,1,320,1024]{4,3,2,1,0:T(8,128)(2,1)} %dynamic-slice_convert_fusion.5), channel_id=1, source_target_pairs={{0,2},{1,3},{2,0},{3,1},{4,6},{5,7},{6,4},{7,5},{8,10},{9,11},{10,... | collective-permute-start | bytes 3932168 | tf_op jit(solution)/shard_map/ppermute | solution.py:195
  1435.1 84.4 %collective-permute-start.69 = (bf16[1,1,2,352,1024]{4,3,2,1,0:T(8,128)(2,1)}, bf16[1,1,2,352,1024]{4,3,2,1,0:T(8,128)(2,1)}, u32[]{:S(2)}, u32[]{:S(2)}) collective-permute-start(bf16[1,1,2,352,1024]{4,3,2,1,0:T(8,128)(2,1)} %dynamic-slice_convert_fusion.3), channel_id=1, source_target_pairs={{0,8},{8,0},{16,24},{24,16},{1,9},{9,1},{17,25},{25,17},{2,10},{10... | collective-permute-start | bytes 4325384 | tf_op jit(solution)/shard_map/ppermute | solution.py:195
  1530.6 62.1 %collective-permute-start.111 = (bf16[688,1024]{1,0:T(8,128)(2,1)}, bf16[688,1024]{1,0:T(8,128)(2,1)}, u32[]{:S(2)}, u32[]{:S(2)}) collective-permute-start(bf16[688,1024]{1,0:T(8,128)(2,1)} %broadcast_select_fusion.7), channel_id=1, source_target_pairs={{0,8},{8,0},{16,24},{24,16},{1,9},{9,1},{17,25},{25,17},{2,10},{10... | collective-permute-start | bytes 4227080 | tf_op jit(solution)/shard_map/ppermute | solution.py:195
  1532.5 706.3 %reduce-scatter.15.cloned.1.call-start = ((), (), s32[]{:S(2)}) async-start(), calls=%async_computation.11 | async-start | bytes 5242880 | tf_op jit(solution)/shard_map/reduce_scatter | solution.py:325
  1590.5 46.0 %collective-permute-start.79 = (bf16[512,1024]{1,0:T(8,128)(2,1)S(1)}, bf16[512,1024]{1,0:T(8,128)(2,1)S(1)}, u32[]{:S(2)}, u32[]{:S(2)}) collective-permute-start(bf16[512,1024]{1,0:T(8,128)(2,1)S(1)} %collective-permute-done.77), channel_id=1, source_target_pairs={{0,2},{1,3},{2,0},{3,1},{4,6},{5,7},{6,4},{7,5},{8,10},{9,11},{10,... | collective-permute-start | bytes 3145736 | tf_op jit(solution)/shard_map/ppermute | solution.py:195
  1636.7 323.3 %collective-permute-start.112 = (bf16[2,688,512]{2,1,0:T(8,128)(2,1)}, bf16[2,688,512]{2,1,0:T(8,128)(2,1)}, u32[]{:S(2)}, u32[]{:S(2)}) collective-permute-start(bf16[2,688,512]{2,1,0:T(8,128)(2,1)} %fusion.82), channel_id=1, source_target_pairs={{0,4},{4,0},{1,5},{5,1},{2,6},{6,2},{3,7},{7,3},{8,12},{12,8},{9,1... | collective-permute-start | bytes 4227080 | tf_op jit(solution)/shard_map/ppermute | solution.py:195
  1664.5 633.7 %reduce-scatter.9.cloned.1.call-start = ((), (), s32[]{:S(2)}) async-start(), calls=%async_computation.8 | async-start | bytes 5242880 | tf_op jit(solution)/shard_map/reduce_scatter | solution.py:325
  1737.7 575.2 %reduce-scatter.21.cloned.1.call-start = ((), (), s32[]{:S(2)}) async-start(), calls=%async_computation.14 | async-start | bytes 5242880 | tf_op jit(solution)/shard_map/reduce_scatter | solution.py:325
  1752.9 170.2 %collective-permute-start.103 = (bf16[2048,1024]{1,0:T(8,128)(2,1)}, bf16[2048,1024]{1,0:T(8,128)(2,1)}, u32[]{:S(2)}, u32[]{:S(2)}) collective-permute-start(bf16[2048,1024]{1,0:T(8,128)(2,1)} %convolution_convert_fusion.4), channel_id=1, source_target_pairs={{0,1},{1,0},{2,3},{3,2},{4,5},{5,4},{6,7},{7,6},{8,9},{9,8},{10,11... | collective-permute-start | bytes 12582920 | tf_op jit(solution)/shard_map/ppermute | solution.py:195
  1763.2 171.4 %collective-permute-start.102 = (bf16[2048,1024]{1,0:T(8,128)(2,1)}, bf16[2048,1024]{1,0:T(8,128)(2,1)}, u32[]{:S(2)}, u32[]{:S(2)}) collective-permute-start(bf16[2048,1024]{1,0:T(8,128)(2,1)} %convolution_convert_fusion.5), channel_id=1, source_target_pairs={{0,1},{1,0},{2,3},{3,2},{4,5},{5,4},{6,7},{7,6},{8,9},{9,8},{10,11... | collective-permute-start | bytes 12582920 | tf_op jit(solution)/shard_map/ppermute | solution.py:195
  1788.5 526.9 %reduce-scatter.23.cloned.1.call-start = ((), (), s32[]{:S(2)}) async-start(), calls=%async_computation.15 | async-start | bytes 5242880 | tf_op jit(solution)/shard_map/reduce_scatter | solution.py:325
  1790.9 128.1 %collective-permute-start.114 = (bf16[1024,1376]{0,1:T(8,128)(2,1)S(1)}, bf16[1024,1376]{0,1:T(8,128)(2,1)S(1)}, u32[]{:S(2)}, u32[]{:S(2)}) collective-permute-start(bf16[1024,1376]{0,1:T(8,128)(2,1)S(1)} %select_bitcast_fusion), channel_id=1, source_target_pairs={{0,8},{8,0},{16,24},{24,16},{1,9},{9,1},{17,25},{25,17},{2,10},{10... | collective-permute-start | bytes 8454152 | tf_op jit(solution)/shard_map/ppermute | solution.py:195
  1816.3 278.1 %collective-permute-start.92 = (bf16[4096,1024]{1,0:T(8,128)(2,1)}, bf16[4096,1024]{1,0:T(8,128)(2,1)}, u32[]{:S(2)}, u32[]{:S(2)}) collective-permute-start(bf16[4096,1024]{1,0:T(8,128)(2,1)} %convolution_convert_fusion), channel_id=1, source_target_pairs={{0,1},{1,0},{2,3},{3,2},{4,5},{5,4},{6,7},{7,6},{8,9},{9,8},{10,11... | collective-permute-start | bytes 25165832 | tf_op jit(solution)/shard_map/ppermute | solution.py:195
  1920.6 192.9 %collective-permute-start.91 = (bf16[4096,1024]{1,0:T(8,128)(2,1)}, bf16[4096,1024]{1,0:T(8,128)(2,1)}, u32[]{:S(2)}, u32[]{:S(2)}) collective-permute-start(bf16[4096,1024]{1,0:T(8,128)(2,1)} %convolution_convert_fusion.1), channel_id=1, source_target_pairs={{0,1},{1,0},{2,3},{3,2},{4,5},{5,4},{6,7},{7,6},{8,9},{9,8},{10,11... | collective-permute-start | bytes 25165832 | tf_op jit(solution)/shard_map/ppermute | solution.py:195
  1953.6 48.6 %collective-permute-start.104 = (bf16[1,2,512,1024]{3,2,1,0:T(8,128)(2,1)}, bf16[1,2,512,1024]{3,2,1,0:T(8,128)(2,1)}, u32[]{:S(2)}, u32[]{:S(2)}) collective-permute-start(bf16[1,2,512,1024]{3,2,1,0:T(8,128)(2,1)} %fusion.61), channel_id=1, source_target_pairs={{0,2},{1,3},{2,0},{3,1},{4,6},{5,7},{6,4},{7,5},{8,10},{9,11},{10,... | collective-permute-start | bytes 6291464 | tf_op jit(solution)/shard_map/ppermute | solution.py:195
  1957.0 112.5 %collective-permute-start.115 = (bf16[2,512,1376]{1,2,0:T(8,128)(2,1)}, bf16[2,512,1376]{1,2,0:T(8,128)(2,1)}, u32[]{:S(2)}, u32[]{:S(2)}) collective-permute-start(bf16[2,512,1376]{1,2,0:T(8,128)(2,1)} %fusion.50), channel_id=1, source_target_pairs={{0,4},{4,0},{1,5},{5,1},{2,6},{6,2},{3,7},{7,3},{8,12},{12,8},{9,1... | collective-permute-start | bytes 8454152 | tf_op jit(solution)/shard_map/ppermute | solution.py:195
  1960.0 106.2 %collective-permute-start.106 = (bf16[2,1,512,1024]{3,2,1,0:T(8,128)(2,1)}, bf16[2,1,512,1024]{3,2,1,0:T(8,128)(2,1)}, u32[]{:S(2)}, u32[]{:S(2)}) collective-permute-start(bf16[2,1,512,1024]{3,2,1,0:T(8,128)(2,1)} %fusion.59), channel_id=1, source_target_pairs={{0,4},{4,0},{1,5},{5,1},{2,6},{6,2},{3,7},{7,3},{8,12},{12,8},{9,1... | collective-permute-start | bytes 6291464 | tf_op jit(solution)/shard_map/ppermute | solution.py:195
  2006.0 82.5 %collective-permute-start.105 = (bf16[1,1,512,1024]{3,2,1,0:T(8,128)(2,1)S(1)}, bf16[1,1,512,1024]{3,2,1,0:T(8,128)(2,1)S(1)}, u32[]{:S(2)}, u32[]{:S(2)}) collective-permute-start(bf16[1,1,512,1024]{3,2,1,0:T(8,128)(2,1)S(1)} %dynamic-slice_convert_fusion.7), channel_id=1, source_target_pairs={{0,4},{4,0},{1,5},{5,1},{2,6},{6,2},{3,7},{7,3},{8,12},{12,8},{9,1... | collective-permute-start | bytes 3145736 | tf_op jit(solution)/shard_map/ppermute | solution.py:195
  2136.8 77.6 %collective-permute-start.99 = (bf16[2,2,1,320,1024]{4,3,2,1,0:T(8,128)(2,1)}, bf16[2,2,1,320,1024]{4,3,2,1,0:T(8,128)(2,1)}, u32[]{:S(2)}, u32[]{:S(2)}) collective-permute-start(bf16[2,2,1,320,1024]{4,3,2,1,0:T(8,128)(2,1)} %fusion.55), channel_id=1, source_target_pairs={{0,4},{4,0},{1,5},{5,1},{2,6},{6,2},{3,7},{7,3},{8,12},{12,8},{9,1... | collective-permute-start | bytes 7864328 | tf_op jit(solution)/shard_map/ppermute | solution.py:195
  2141.0 80.0 %collective-permute-start.93 = (bf16[1,2,2,352,1024]{4,3,2,1,0:T(8,128)(2,1)}, bf16[1,2,2,352,1024]{4,3,2,1,0:T(8,128)(2,1)}, u32[]{:S(2)}, u32[]{:S(2)}) collective-permute-start(bf16[1,2,2,352,1024]{4,3,2,1,0:T(8,128)(2,1)} %fusion.44), channel_id=1, source_target_pairs={{0,2},{1,3},{2,0},{3,1},{4,6},{5,7},{6,4},{7,5},{8,10},{9,11},{10,... | collective-permute-start | bytes 8650760 | tf_op jit(solution)/shard_map/ppermute | solution.py:195
  2144.8 83.7 %collective-permute-start.96 = (bf16[2,1,2,352,1024]{4,3,2,1,0:T(8,128)(2,1)}, bf16[2,1,2,352,1024]{4,3,2,1,0:T(8,128)(2,1)}, u32[]{:S(2)}, u32[]{:S(2)}) collective-permute-start(bf16[2,1,2,352,1024]{4,3,2,1,0:T(8,128)(2,1)} %fusion.42), channel_id=1, source_target_pairs={{0,8},{8,0},{16,24},{24,16},{1,9},{9,1},{17,25},{25,17},{2,10},{10... | collective-permute-start | bytes 8650760 | tf_op jit(solution)/shard_map/ppermute | solution.py:195
  2144.8 50.3 %collective-permute-start.108 = (f32[2,1024]{1,0:T(2,128)S(1)}, f32[2,1024]{1,0:T(2,128)S(1)}, u32[]{:S(2)}, u32[]{:S(2)}) collective-permute-start(f32[2,1024]{1,0:T(2,128)S(1)} %pad_maximum_fusion.11), channel_id=1, source_target_pairs={{0,4},{4,0},{1,5},{5,1},{2,6},{6,2},{3,7},{7,3},{8,12},{12,8},{9,1... | collective-permute-start | bytes 24584 | tf_op jit(solution)/shard_map/ppermute | solution.py:195
  (198 other events, 4536.3 us)
Sparse Core Ops, SparseCore 0:
  32.4 80.1 all-gather.16
  120.8 144.1 all-gather.14
  369.5 81.1 all-gather.12
  452.1 135.3 all-gather.18
  607.3 262.2 all-gather.20
  1027.6 133.0 all-gather.22
  1165.4 69.5 reduce-scatter.12
  1237.3 69.8 reduce-scatter.10
  1309.5 130.3 reduce-scatter.16
  1532.7 129.1 reduce-scatter.18
  1664.6 75.6 reduce-scatter.14
  1742.6 100.8 reduce-scatter.8
  1845.8 101.8 reduce-scatter.20
  1966.4 76.7 reduce-scatter.22

commit v4 on v2

--- a/solution.py
+++ b/solution.py
@@ -94,7 +94,7 @@
         scratch_shapes=[pltpu.VMEM((blocks, HD, block), BF)],
         compiler_params=pltpu.CompilerParams(vmem_limit_bytes=48 << 20),
         cost_estimate=pl.CostEstimate(
-            flops=4 * pairs * HD,
+            flops=30 * pairs * HD,
             transcendentals=pairs,
             bytes_accessed=seq_len * heads * HD * (12 + 8),
         ),
@@ -175,7 +175,7 @@
         ],
         compiler_params=pltpu.CompilerParams(vmem_limit_bytes=48 << 20),
         cost_estimate=pl.CostEstimate(
-            flops=10 * pairs * HD,
+            flops=38 * pairs * HD,
             transcendentals=pairs,
             bytes_accessed=seq_len * heads * HD * 16,
         ),
@@ -250,6 +250,12 @@
     return lax.dynamic_slice_in_dim(weight, lax.axis_index("ctx") * size, size, axis)
 
 
+def part_of(weight, axis, index):
+    size = weight.shape[axis] // (2 * lax.axis_size("ctx"))
+    start = (2 * lax.axis_index("ctx") + index) * size
+    return lax.dynamic_slice_in_dim(weight, start, size, axis)
+
+
 def after(value, token):
     value, _ = lax.optimization_barrier((value, token))
     return value
@@ -257,6 +263,29 @@
 
 def owners(grad):
     return lax.psum_scatter(grad, "fsdp", scatter_dimension=0, tiled=False)
+
+
+def line_owners(grad):
+    count = lax.axis_size("fsdp")
+    me = lax.axis_index("fsdp")
+
+    def part(owner):
+        owner = jnp.clip(owner, 0, count - 1)
+        return lax.dynamic_index_in_dim(grad, owner, 0, keepdims=False)
+
+    def joined(mine, got):
+        return mine if got is None else (mine.astype(F32) + got.astype(F32)).astype(BF)
+
+    steps = []
+    up = down = None
+    for step in range(count - 1):
+        gap = count - 1 - step
+        up = joined(part(me + gap), up)
+        up = lax.ppermute(up, "fsdp", [(i, i + 1) for i in range(step + 1)])
+        down = joined(part(me - gap), down)
+        down = lax.ppermute(down, "fsdp", [(i, i - 1) for i in range(gap, count)])
+        steps.append((up, down))
+    return steps, part(me).astype(F32) + up.astype(F32) + down.astype(F32)
 
 
 def spread(weight):
@@ -272,6 +301,10 @@
     return jnp.where(me == 0, own, got), jnp.where(me == 0, got, own)
 
 
+def by_ctx(halves):
+    return [half[i] for i in range(lax.axis_size("ctx")) for half in halves]
+
+
 def out_grad(block):
     return jnp.concatenate(trade_ctx(block, 1), axis=0).astype(F32)
 
@@ -288,10 +321,11 @@
 ):
     n_f = lax.axis_size("fsdp")
     d_f = D // n_f
-    qkv_parts = [spread(ctx_half(qkv_weight[:, i], 1)) for i in range(3)]
+    qkv_full = spread(ctx_half(jnp.swapaxes(qkv_weight, 0, 1), 2))
+    qkv_parts = [qkv_full[:, i] for i in range(3)]
     out_full = spread(ctx_half(out_weight, 0))
-    gu_full = spread(ctx_half(gate_up_weight, 2).reshape(d_f, -1))
-    down_full = spread(ctx_half(down_weight, 0))
+    gu_full = [spread(part_of(gate_up_weight, 2, i).reshape(d_f, -1)) for i in range(2)]
+    down_full = [spread(part_of(down_weight, 0, i)) for i in range(2)]
 
     def into(full, weight):
         return mm(full, weight, (((0, 2), (0, 1)), ((), ())))
@@ -324,29 +358,48 @@
     seq_len = attn_full.shape[1]
     cosine, sine = rope_tables(seq_len)
     cotan_full = gather_rows(after(cotangent, attn_full))
-    proj = [into(attn_full, part) for part in qkv_parts]
+    proj = after([into(attn_full, part) for part in qkv_parts], cotan_full)
     queries, keys, values, head_outs, norms = attend_forward(*proj, cosine, sine)
     resid = input_float + scatter_rows(out_blocks(head_outs, out_full))
     rms_two = lax.rsqrt(row_total(jnp.sum(resid * resid, axis=-1)) / D + rms_epsilon)[:, None]
     normed_ffn = (resid * rms_two * ffn_scale).astype(BF)
     ffn_full = gather_rows(normed_ffn)
-    gate_up = into(ffn_full, gu_full)
-    units = gate_up.shape[1] // 2
-    gate = gate_up[:, :units]
-    up_value = gate_up[:, units:]
-    sigma = jax.nn.sigmoid(gate)
-    hidden = (gate * sigma * up_value).astype(BF)
-    down_part = out_part(hidden, cotan_full)
-    down_sum = owners(down_part)
-    down_full = after(down_full, down_part)
-    grad_hidden = back_out(cotan_full, down_full)
-    grad_gu = jnp.concatenate(
-        [grad_hidden * up_value * sigma * (1.0 + gate * (1.0 - sigma)), grad_hidden * gate * sigma],
-        axis=1,
-    ).astype(BF)
-    gu_part = in_part(ffn_full, grad_gu)
-    gu_sum = owners(after(gu_part, down_sum))
-    grad_nffn = after(scatter_rows(in_blocks(grad_gu, gu_full)), (gu_part, down_sum))
+
+    def ffn_hidden(tokens, weight):
+        gate_up = into(tokens, weight)
+        units = gate_up.shape[1] // 2
+        gate = gate_up[:, :units]
+        up_value = gate_up[:, units:]
+        sigma = jax.nn.sigmoid(gate)
+        return gate, up_value, sigma, (gate * sigma * up_value).astype(BF)
+
+    def ffn_grads(cotan, weight, gate, up_value, sigma):
+        grad_hidden = back_out(cotan, weight)
+        return jnp.concatenate(
+            [
+                grad_hidden * up_value * sigma * (1.0 + gate * (1.0 - sigma)),
+                grad_hidden * gate * sigma,
+            ],
+            axis=1,
+        ).astype(BF)
+
+    *inner, hidden_a = ffn_hidden(ffn_full, gu_full[0])
+    down_part_a = out_part(hidden_a, cotan_full)
+    down_steps, down_sum_a = line_owners(down_part_a)
+    weight = after(down_full[0], down_part_a)
+    grad_gu_a = ffn_grads(cotan_full, weight, *inner)
+    gu_part_a = in_part(ffn_full, grad_gu_a)
+    gu_steps, gu_sum_a = line_owners(gu_part_a)
+    tokens = after(ffn_full, (gu_part_a, gu_steps[0], down_steps[-1]))
+    *inner, hidden_b = ffn_hidden(tokens, gu_full[1])
+    down_part_b = out_part(hidden_b, cotan_full)
+    down_sum_b = owners(down_part_b)
+    weight = after(down_full[1], (down_part_b, gu_steps[-1]))
+    grad_gu_b = ffn_grads(cotan_full, weight, *inner)
+    gu_part_b = in_part(ffn_full, grad_gu_b)
+    gu_sum_b = owners(gu_part_b)
+    blocks = [in_blocks(grad_gu_a, gu_full[0]), in_blocks(grad_gu_b, gu_full[1])]
+    grad_nffn = after(scatter_rows(lambda t: blocks[0](t) + blocks[1](t)), gu_part_b)
     ffn_term = grad_nffn * ffn_scale
     ffn_dot = row_total(jnp.sum(ffn_term * resid, axis=-1))[:, None]
     grad_resid = cotangent.astype(F32) + rms_two * ffn_term - resid * rms_two**3 * ffn_dot / D
@@ -358,31 +411,38 @@
     grad_proj = attend_backward(
         queries, keys, values, head_outs, norms, grad_heads, cosine, sine
     )
-    qkv_part = [in_part(attn_full, grad) for grad in grad_proj]
+    qkv_part = [
+        in_part(attn_full, jnp.concatenate(grad_proj[1:], axis=1)),
+        in_part(attn_full, grad_proj[0]),
+    ]
     qkv_sum = [owners(part) for part in qkv_part]
     grad_nattn = scatter_rows(
         in_blocks(jnp.concatenate(grad_proj, axis=1), jnp.concatenate(qkv_parts, axis=2))
     )
-    hidden = after(hidden, qkv_part)
-    layer_output = (resid + scatter_rows(out_blocks(hidden, down_full))).astype(BF)
+    hidden_a, hidden_b = after((hidden_a, hidden_b), qkv_part)
+    outs = [out_blocks(hidden_a, down_full[0]), out_blocks(hidden_b, down_full[1])]
+    layer_output = (resid + scatter_rows(lambda t: outs[0](t) + outs[1](t))).astype(BF)
     attn_term = grad_nattn * attn_scale
     attn_dot = row_total(jnp.sum(attn_term * input_float, axis=-1))[:, None]
     grad_input = grad_resid + rms_one * attn_term - input_float * rms_one**3 * attn_dot / D
     attn_gain_part = jnp.sum(grad_nattn * input_float * rms_one, axis=0)
     gain_grads = total_rows(jnp.stack([attn_gain_part, ffn_gain_part]))
 
-    down_grad = out_grad(down_sum)
-    rows, other_rows = trade_ctx(gu_sum, 0)
-    gu_grad = jnp.concatenate(
-        [v.reshape(v.shape[0], 2, -1) for v in (rows, other_rows)], axis=2
-    ).astype(F32)
+    down_grad = by_ctx([trade_ctx(v, 1) for v in (down_sum_a.astype(BF), down_sum_b)])
+    down_grad = jnp.concatenate(down_grad, axis=0).astype(F32)
+    gu_grad = by_ctx([trade_ctx(v, 0) for v in (gu_sum_a.astype(BF), gu_sum_b)])
+    gu_grad = jnp.concatenate([v.reshape(v.shape[0], 2, -1) for v in gu_grad], axis=2).astype(F32)
     out_weight_grad = out_grad(out_sum)
     done = (down_grad, out_weight_grad, gu_grad, grad_input, layer_output, gain_grads)
     qkv_grad = []
     for part in qkv_sum:
-        qkv_grad.append(jnp.concatenate(trade_ctx(after(part, done), 0), axis=1).astype(F32))
+        first, second = trade_ctx(after(part, done), 0)
+        wide = queries.shape[1]
+        for i in range(0, first.shape[1], wide):
+            both = [first[:, i : i + wide], second[:, i : i + wide]]
+            qkv_grad.append(jnp.concatenate(both, axis=1).astype(F32))
         done = done + (qkv_grad[-1],)
-    qkv_grad = jnp.stack(qkv_grad, axis=1)
+    qkv_grad = jnp.stack([qkv_grad[2], qkv_grad[0], qkv_grad[1]], axis=1)
 
     return (
         layer_output,

time: 1840 us -> 2100 us (1.14); the launches traced: 1840 us -> 2060 us
  starting transfers between devices: 79 us -> 404 us
  waiting for transfers between devices: 887 us -> 730 us
  matrix products: 472 us -> 511 us
  other arithmetic: 106 us -> 138 us
    ppermute x0 -> x12, starting transfers between devices: none -> 286 us  [the longest x6 275 us: line_owners(): up = lax.ppermute(up, 'fsdp', [(i, i + 1) for i in range(step + 1)])]
    all_gather x6, waiting for transfers between devices: 294 us -> 65 us  [spread(): return lax.all_gather(weight, 'fsdp', axis=0, tiled=False)]
    ppermute x0 -> x12, waiting for transfers between devices: none -> 179 us  [the longest x6 179 us: line_owners(): up = lax.ppermute(up, 'fsdp', [(i, i + 1) for i in range(step + 1)])]
    reduce_scatter x6 -> x5, waiting for transfers between devices: 116 us -> 0.01 us  [owners(): return lax.psum_scatter(grad, 'fsdp', scatter_dimension=0, tiled=False)]
    dot_general x34 -> x48, matrix products: 472 us -> 511 us  [mm(): return lax.dot_general(left, right, dims, preferred_element_type=F32)]
    convert_element_type x3 -> x13, other arithmetic: 19.9 us -> 57.7 us  [the longest x6 27 us: joined(): (mine.astype(F32) + got.astype(F32)).astype(BF)]
    ppermute x97 -> x98, starting transfers between devices: 78.5 us -> 116 us  [swap(): lax.ppermute(values, axis, [(i, i ^ step) for i in range(lax.axis_size(ax...]
    dynamic_update_slice x64, local copies, waits for them, and re-layouts: 69.6 us -> 44.9 us  [gather_rows(): full = lax.dynamic_update_slice(full, piece[None], start)]
  transfers between devices with their start and end apart: 109 -> 121, of which waited for: 40 -> 44; matrix products, arithmetic and copies ran while one was open for 38% -> 36% of each run, Pallas kernels for 4% -> 4%
where the time goes in v4:
time: 2100 us; the launch traced here: 2060 us
  waiting for transfers between devices  730 us (35%)
  matrix products  511 us (24%)
  starting transfers between devices  404 us (19%)
  other arithmetic  138 us (7%)
  local copies, waits for them, and re-layouts  128 us (6%)
  Pallas kernels  79 us (4%)
  blocking collectives  57.7 us (3%)
    dot_general x48, matrix products, mm(): return lax.dot_general(left, right, dims, preferred_element_type=F32)  511 us
    ppermute x98, waiting for transfers between devices, swap(): lax.ppermute(values, axis, [(i, i ^ step) for i in range(lax.axis_size(ax...  485 us
    ppermute x6, starting transfers between devices, line_owners(): up = lax.ppermute(up, 'fsdp', [(i, i + 1) for i in range(step + 1)])  275 us
    ppermute x6, waiting for transfers between devices, line_owners(): up = lax.ppermute(up, 'fsdp', [(i, i + 1) for i in range(step + 1)])  179 us
    ppermute x98, starting transfers between devices, swap(): lax.ppermute(values, axis, [(i, i ^ step) for i in range(lax.axis_size(ax...  116 us
    all_gather x6, waiting for transfers between devices, spread(): return lax.all_gather(weight, 'fsdp', axis=0, tiled=False)  65 us
    psum x4, blocking collectives, row_total(): return lax.psum(values, 'tp')  57.7 us
    dynamic_update_slice x64, local copies, waits for them, and re-layouts, gather_rows(): full = lax.dynamic_update_slice(full, piece[None], start)  44.9 us
  transfers between devices with their start and end apart: 121, of which 44 were waited for; matrix products, arithmetic and copies ran while one was open for 36% of the time, Pallas kernels for 4%

profile of v4, /device:TPU:0, one launch (start us, length us, event | category | flops | bytes accessed | tf_op | source)
XLA Modules:
  0.0 2062.7 jit_solution(1722312466143943138)
XLA Ops:
  13.3 8.4 psum.28
  32.3 19.1 collective-permute-done
  58.6 20.5 collective-permute-done.7
  79.7 19.1 collective-permute-done.2
  127.4 12.3 collective-permute-done.14
  151.4 18.8 collective-permute-done.21
  171.8 19.7 collective-permute-done.16
  209.5 22.8 %all-gather.15.cloned.1.call-done = bf16[12,1024,512]{2,1,0:T(8,128)(2,1)} async-done(((bf16[3,1024,512]{2,1,0:T(8,128)(2,1)}), bf16[12,1024,512]{2,1,0:T(8,128)(2,1)}) %all-gather.15.cloned.1.call-update) | async-done | bytes 12582928 | tf_op jit(solution)/shard_map/all_gather | solution.py:292
  232.2 15.0 convolution_bitcast_fusion.2.v_in
  247.3 15.1 convolution_bitcast_fusion.3.k_in
  262.4 12.6 convolution_bitcast_fusion.4.q_in
  274.9 35.1 %shard_map.143 = (bf16[2048,512]{1,0:T(8,128)(2,1)S(1)}, bf16[2048,512]{1,0:T(8,128)(2,1)}, bf16[2048,512]{1,0:T(8,128)(2,1)}, bf16[2048,512]{1,0:T(8,128)(2,1)}, f32[4,1,2048]{2,1,0:T(1,128)S(1)}) custom-call(f32[2048,512]{1,0:T(8,128)} %convolution_bitcast_fusion.4.q_in, f32[2048,512]{1,0:T(8,128)} %convolution_bitcast_fusion.3.k_in, ...), custom_call_target="tpu_custom_call" | custom-call | flops 40265318400 | bytes 20971520 | tf_op jit(solution)/shard_map/pallas_call | solution.py:88
  342.8 16.6 collective-permute-done.31
  364.0 17.9 collective-permute-done.29
  386.5 19.5 collective-permute-done.33
  423.5 21.3 %collective-permute-done.36 = bf16[512,1024]{1,0:T(8,128)(2,1)} collective-permute-done((bf16[512,1024]{1,0:T(8,128)(2,1)}, bf16[512,1024]{1,0:T(8,128)(2,1)}, u32[]{:S(2)}, u32[]{:S(2)}) %collective-permute-start.36) | collective-permute-done | bytes 1048608 | tf_op jit(solution)/shard_map/ppermute | solution.py:191
  458.1 12.2 collective-permute-done.43
  473.1 17.9 collective-permute-done.38
  515.1 28.8 %convolution_bitcast_fusion.1 = f32[2048,1376]{0,1:T(8,128)S(1)} fusion(bf16[4,2048,1024]{2,1,0:T(8,128)(2,1)} %bitcast_dynamic-update-slice_fusion.16, bf16[4,1024,1376]{1,2,0:T(8,128)(2,1)} %all-gather.11.cloned.1.call-done), kind=kOutput, calls=%fused_computation.10 | convolution fusion | flops 23085449216 | bytes 39321600 | tf_op jit(solution)/shard_map/dot_general | solution.py:21
  573.6 40.9 %all-gather.19.cloned.1.call-done = bf16[2752,1024]{1,0:T(8,128)(2,1)} async-done(((bf16[688,1024]{1,0:T(8,128)(2,1)}), bf16[2752,1024]{1,0:T(8,128)(2,1)}) %all-gather.19.cloned.1.call-update) | async-done | bytes 5636112 | tf_op jit(solution)/shard_map/all_gather | solution.py:292
  614.5 20.7 %fusion.15 = (bf16[2048,688]{0,1:T(8,128)(2,1)S(1)}, bf16[2048,688]{0,1:T(8,128)(2,1)S(1)}) fusion(f32[2048,1376]{0,1:T(8,128)} %copy-done.23, bf16[4,2048,1024]{2,1,0:T(8,128)(2,1)} %bitcast_dynamic-update-slice_fusion.32, bf16[4,688,1024]{2,1,0:T(8,128)(2,1)} %bitcast.633), kind=kOutput, calls=%fused_computation.53 | convolution fusion | flops 11561041920 | bytes 39321600 | tf_op jit(solution)/shard_map/dot_general | solution.py:21
  635.2 30.2 %convolution_convert_fusion.1 = bf16[4,1024,1376]{1,2,0:T(8,128)(2,1)} fusion(bf16[4,2048,1024]{2,1,0:T(8,128)(2,1)} %bitcast_dynamic-update-slice_fusion.16, bf16[2048,688]{0,1:T(8,128)(2,1)S(1)} %get-tuple-element.59, bf16[2048,688]{0,1:T(8,128)(2,1)S(1)} %get-tuple-element.58), kind=kOutput, calls=%fused_computation.1 | convolution fusion | flops 23102357504 | bytes 33685504 | tf_op jit(solution)/shard_map/dot_general | solution.py:21
  693.7 46.0 %collective-permute-done.52 = bf16[688,1024]{1,0:T(8,128)(2,1)S(1)} collective-permute-done((bf16[688,1024]{1,0:T(8,128)(2,1)}, bf16[688,1024]{1,0:T(8,128)(2,1)S(1)}, u32[]{:S(2)}, u32[]{:S(2)}) %collective-permute-start.52) | collective-permute-done | bytes 1409056 | tf_op jit(solution)/shard_map/ppermute | solution.py:284
  743.5 166.2 %collective-permute-start.53 = (bf16[688,1024]{1,0:T(8,128)(2,1)S(1)}, bf16[688,1024]{1,0:T(8,128)(2,1)S(1)}, u32[]{:S(2)}, u32[]{:S(2)}) collective-permute-start(bf16[688,1024]{1,0:T(8,128)(2,1)S(1)} %get-tuple-element.72), channel_id=1, source_target_pairs={{0,8},{8,16},{1,9},{9,17},{2,10},{10,18},{3,11},{11,19},{4,12},{12... | collective-permute-start | bytes 4227080 | tf_op jit(solution)/shard_map/ppermute | solution.py:284
  909.7 10.5 fusion.66
  921.5 15.0 collective-permute-done.53
  938.3 79.5 %collective-permute-start.54 = (bf16[688,1024]{1,0:T(8,128)(2,1)}, bf16[688,1024]{1,0:T(8,128)(2,1)}, u32[]{:S(2)}, u32[]{:S(2)}) collective-permute-start(bf16[688,1024]{1,0:T(8,128)(2,1)} %fusion.61), channel_id=1, source_target_pairs={{0,8},{8,16},{16,24},{1,9},{9,17},{17,25},{2,10},{10,18},{18,26},{... | collective-permute-start | bytes 4227080 | tf_op jit(solution)/shard_map/ppermute | solution.py:284
  1017.8 10.5 fusion.63
  1042.9 31.2 %collective-permute-done.54 = bf16[688,1024]{1,0:T(8,128)(2,1)} collective-permute-done((bf16[688,1024]{1,0:T(8,128)(2,1)}, bf16[688,1024]{1,0:T(8,128)(2,1)}, u32[]{:S(2)}, u32[]{:S(2)}) %collective-permute-start.54) | collective-permute-done | bytes 1409056 | tf_op jit(solution)/shard_map/ppermute | solution.py:284
  1074.1 28.0 %convolution_bitcast_fusion = f32[2048,1376]{0,1:T(8,128)S(1)} fusion(bf16[4,2048,1024]{2,1,0:T(8,128)(2,1)} %bitcast_dynamic-update-slice_fusion.16, bf16[4,1024,1376]{1,2,0:T(8,128)(2,1)} %all-gather.13.cloned.1.call-done), kind=kOutput, calls=%fused_computation.9 | convolution fusion | flops 23085449216 | bytes 39321600 | tf_op jit(solution)/shard_map/dot_general | solution.py:21
  1112.8 14.6 collective-permute-done.58
  1132.9 19.6 collective-permute-start.59
  1172.0 72.5 %collective-permute-done.59 = bf16[1024,1376]{0,1:T(8,128)(2,1)} collective-permute-done((bf16[1024,1376]{0,1:T(8,128)(2,1)}, bf16[1024,1376]{0,1:T(8,128)(2,1)}, u32[]{:S(2)}, u32[]{:S(2)}) %collective-permute-start.59) | collective-permute-done | bytes 2818080 | tf_op jit(solution)/shard_map/ppermute | solution.py:284
  1244.4 20.2 fusion.9
  1264.7 13.6 add_convert_fusion.7
  1278.3 28.3 %convolution_convert_fusion = bf16[4,1024,1376]{1,2,0:T(8,128)(2,1)} fusion(bf16[4,2048,1024]{2,1,0:T(8,128)(2,1)} %bitcast_dynamic-update-slice_fusion.16, bf16[2048,688]{0,1:T(8,128)(2,1)S(1)} %get-tuple-element.57, bf16[2048,688]{0,1:T(8,128)(2,1)S(1)} %get-tuple-element.56), kind=kOutput, calls=%fused_computation | convolution fusion | flops 23102357504 | bytes 33685504 | tf_op jit(solution)/shard_map/dot_general | solution.py:21
  1306.6 10.0 fusion.69
  1316.6 10.4 add_convert_fusion.9
  1327.5 11.6 fusion.72
  1339.1 11.3 add_convert_fusion.6
  1353.8 10.9 add_convert_fusion.8
  1366.5 10.7 collective-permute-done.65
  1381.1 18.5 collective-permute-done.63
  1404.3 19.2 collective-permute-done.67
  1443.8 21.5 %collective-permute-done.70 = bf16[512,1024]{1,0:T(8,128)(2,1)S(1)} collective-permute-done((bf16[512,1024]{1,0:T(8,128)(2,1)S(1)}, bf16[512,1024]{1,0:T(8,128)(2,1)S(1)}, u32[]{:S(2)}, u32[]{:S(2)}) %collective-permute-start.70) | collective-permute-done | bytes 1048608 | tf_op jit(solution)/shard_map/ppermute | solution.py:191
  1470.5 19.8 collective-permute-done.77
  1491.4 19.5 collective-permute-done.72
  1531.7 15.0 bitcast_convert_fusion.g
  1546.7 43.9 %shard_map.144 = (bf16[2048,512]{1,0:T(8,128)(2,1)S(1)}, bf16[2048,512]{1,0:T(8,128)(2,1)}, bf16[2048,512]{1,0:T(8,128)(2,1)}) custom-call(bf16[2048,512]{1,0:T(8,128)(2,1)} %copy-done.6, bf16[2048,512]{1,0:T(8,128)(2,1)} %get-tuple-element.36.k, bf16[2048,512]{1,0:T(8,128)(2,1)} %get-tuple-element.37.v, bf16[2048,512]{1,0:T(8,128)(2,1)} %get-tuple-element.32.o, ...), custom_call_target="tpu_custom_call" | custom-call | flops 51002736640 | bytes 16777216 | tf_op jit(solution)/shard_map/pallas_call | solution.py:164
  1590.7 23.2 %convolution_convert_fusion.2 = bf16[4,1024,1024]{2,1,0:T(8,128)(2,1)} fusion(bf16[4,2048,1024]{2,1,0:T(8,128)(2,1)} %copy-done.21, bf16[2048,512]{1,0:T(8,128)(2,1)} %get-tuple-element.42, bf16[2048,512]{1,0:T(8,128)(2,1)} %get-tuple-element.41), kind=kOutput, calls=%fused_computation.23 | convolution fusion | flops 17192452096 | bytes 29360128 | tf_op jit(solution)/shard_map/dot_general | solution.py:21
  1644.4 28.8 %collective-permute-done.106 = bf16[512,1376]{0,1:T(8,128)(2,1)} collective-permute-done((bf16[512,1376]{0,1:T(8,128)(2,1)}, bf16[512,1376]{0,1:T(8,128)(2,1)}, u32[]{:S(2)}, u32[]{:S(2)}) %collective-permute-start.106) | collective-permute-done | bytes 1409056 | tf_op jit(solution)/shard_map/ppermute | solution.py:191
  1676.8 10.5 collective-permute-done.104
  1692.8 12.4 convolution_convert_fusion.3
  1705.2 10.3 convolution_convert_fusion.4
  1716.4 11.0 convolution_convert_fusion.7
  1766.9 10.5 add_convert_fusion
  1779.5 10.9 add_convert_fusion.1
  1821.2 26.9 %collective-permute-done.87 = bf16[512,1024]{1,0:T(8,128)(2,1)} collective-permute-done((bf16[512,1024]{1,0:T(8,128)(2,1)S(1)}, bf16[512,1024]{1,0:T(8,128)(2,1)}, u32[]{:S(2)}, u32[]{:S(2)}) %collective-permute-start.87) | collective-permute-done | bytes 1048608 | tf_op jit(solution)/shard_map/ppermute | solution.py:191
  1853.5 9.3 collective-permute-done.90
  1866.3 19.1 collective-permute-done.96
  1894.3 37.1 %psum.31 = f32[1024]{0:T(1024)S(1)} all-reduce(f32[1024]{0:T(1024)S(1)} %get-tuple-element.51), channel_id=1, replica_groups=mesh['fsdp'=4,'ctx'=2,'tp'=4] {'tp'}, use_global_device_ids=true, to_apply=%region_7.8 | all-reduce | flops 1024 | bytes 8192 | tf_op jit(solution)/shard_map/psum | solution.py:186
  1946.2 37.7 %collective-permute-start.101 = (f32[2,1024]{1,0:T(2,128)S(1)}, f32[2,1024]{1,0:T(2,128)S(1)}, u32[]{:S(2)}, u32[]{:S(2)}) collective-permute-start(f32[2,1024]{1,0:T(2,128)S(1)} %fusion.185), channel_id=1, source_target_pairs={{0,8},{8,0},{16,24},{24,16},{1,9},{9,1},{17,25},{25,17},{2,10},{10... | collective-permute-start | bytes 24584 | tf_op jit(solution)/shard_map/ppermute | solution.py:191
  2003.4 11.4 maximum_convert_fusion
  2020.9 30.0 %collective-permute-done.108 = bf16[512,512]{1,0:T(8,128)(2,1)S(1)} collective-permute-done((bf16[512,512]{1,0:T(8,128)(2,1)S(1)}, bf16[512,512]{1,0:T(8,128)(2,1)S(1)}, u32[]{:S(2)}, u32[]{:S(2)}) %collective-permute-start.108) | collective-permute-done | bytes 524320 | tf_op jit(solution)/shard_map/ppermute | solution.py:191
  (602 shorter events, 535.0 us)
Async XLA Ops:
  7.2 225.1 %all-gather.15.cloned.1.call-start = ((), (), s32[]{:S(2)}) async-start(), calls=%async_computation.12 | async-start | bytes 15728640 | tf_op jit(solution)/shard_map/all_gather | solution.py:292
  11.2 301.6 %all-gather.17.cloned.1.call-start = ((), (), s32[]{:S(2)}) async-start(), calls=%async_computation.13 | async-start | bytes 5242880 | tf_op jit(solution)/shard_map/all_gather | solution.py:292
  30.2 484.9 %all-gather.11.cloned.1.call-start = ((), (), s32[]{:S(2)}) async-start(), calls=%async_computation.5 | async-start | bytes 14090240 | tf_op jit(solution)/shard_map/all_gather | solution.py:292
  30.7 48.3 %collective-permute-start.7 = (bf16[512,1024]{1,0:T(8,128)(2,1)}, bf16[512,1024]{1,0:T(8,128)(2,1)S(1)}, u32[]{:S(2)}, u32[]{:S(2)}) collective-permute-start(bf16[512,1024]{1,0:T(8,128)(2,1)} %get-tuple-element.115), channel_id=1, source_target_pairs={{0,2},{1,3},{2,0},{3,1},{4,6},{5,7},{6,4},{7,5},{8,10},{9,11},{10,... | collective-permute-start | bytes 3145736 | tf_op jit(solution)/shard_map/ppermute | solution.py:191
  51.4 47.3 %collective-permute-start.2 = (bf16[512,1024]{1,0:T(8,128)(2,1)}, bf16[512,1024]{1,0:T(8,128)(2,1)S(1)}, u32[]{:S(2)}, u32[]{:S(2)}) collective-permute-start(bf16[512,1024]{1,0:T(8,128)(2,1)} %collective-permute-done), channel_id=1, source_target_pairs={{0,2},{1,3},{2,0},{3,1},{4,6},{5,7},{6,4},{7,5},{8,10},{9,11},{10,... | collective-permute-start | bytes 3145736 | tf_op jit(solution)/shard_map/ppermute | solution.py:191
  55.4 44.9 %collective-permute-start.4 = (bf16[512,1024]{1,0:T(8,128)(2,1)}, bf16[512,1024]{1,0:T(8,128)(2,1)S(1)}, u32[]{:S(2)}, u32[]{:S(2)}) collective-permute-start(bf16[512,1024]{1,0:T(8,128)(2,1)} %collective-permute-done), channel_id=1, source_target_pairs={{0,1},{1,0},{2,3},{3,2},{4,5},{5,4},{6,7},{7,6},{8,9},{9,8},{10,11... | collective-permute-start | bytes 3145736 | tf_op jit(solution)/shard_map/ppermute | solution.py:191
  56.9 44.0 %collective-permute-start.8 = (bf16[512,1024]{1,0:T(8,128)(2,1)S(1)}, bf16[512,1024]{1,0:T(8,128)(2,1)S(1)}, u32[]{:S(2)}, u32[]{:S(2)}) collective-permute-start(bf16[512,1024]{1,0:T(8,128)(2,1)S(1)} %copy-done.44), channel_id=1, source_target_pairs={{0,4},{4,0},{1,5},{5,1},{2,6},{6,2},{3,7},{7,3},{8,12},{12,8},{9,1... | collective-permute-start | bytes 3145736 | tf_op jit(solution)/shard_map/ppermute | solution.py:191
  58.5 42.5 %collective-permute-start.5 = (bf16[512,1024]{1,0:T(8,128)(2,1)S(1)}, bf16[512,1024]{1,0:T(8,128)(2,1)S(1)}, u32[]{:S(2)}, u32[]{:S(2)}) collective-permute-start(bf16[512,1024]{1,0:T(8,128)(2,1)S(1)} %collective-permute-done.1), channel_id=1, source_target_pairs={{0,1},{1,0},{2,3},{3,2},{4,5},{5,4},{6,7},{7,6},{8,9},{9,8},{10,11... | collective-permute-start | bytes 3145736 | tf_op jit(solution)/shard_map/ppermute | solution.py:191
  121.4 493.1 %all-gather.19.cloned.1.call-start = ((), (), s32[]{:S(2)}) async-start(), calls=%async_computation.14 | async-start | bytes 7045120 | tf_op jit(solution)/shard_map/all_gather | solution.py:292
  122.2 48.1 %collective-permute-start.21 = (bf16[512,1024]{1,0:T(8,128)(2,1)}, bf16[512,1024]{1,0:T(8,128)(2,1)S(1)}, u32[]{:S(2)}, u32[]{:S(2)}) collective-permute-start(bf16[512,1024]{1,0:T(8,128)(2,1)} %get-tuple-element.113), channel_id=1, source_target_pairs={{0,2},{1,3},{2,0},{3,1},{4,6},{5,7},{6,4},{7,5},{8,10},{9,11},{10,... | collective-permute-start | bytes 3145736 | tf_op jit(solution)/shard_map/ppermute | solution.py:191
  139.7 51.8 %collective-permute-start.16 = (bf16[512,1024]{1,0:T(8,128)(2,1)S(1)}, bf16[512,1024]{1,0:T(8,128)(2,1)S(1)}, u32[]{:S(2)}, u32[]{:S(2)}) collective-permute-start(bf16[512,1024]{1,0:T(8,128)(2,1)S(1)} %collective-permute-done.14), channel_id=1, source_target_pairs={{0,2},{1,3},{2,0},{3,1},{4,6},{5,7},{6,4},{7,5},{8,10},{9,11},{10,... | collective-permute-start | bytes 3145736 | tf_op jit(solution)/shard_map/ppermute | solution.py:191
  149.5 44.2 %collective-permute-start.18 = (bf16[512,1024]{1,0:T(8,128)(2,1)S(1)}, bf16[512,1024]{1,0:T(8,128)(2,1)S(1)}, u32[]{:S(2)}, u32[]{:S(2)}) collective-permute-start(bf16[512,1024]{1,0:T(8,128)(2,1)S(1)} %collective-permute-done.14), channel_id=1, source_target_pairs={{0,1},{1,0},{2,3},{3,2},{4,5},{5,4},{6,7},{7,6},{8,9},{9,8},{10,11... | collective-permute-start | bytes 3145736 | tf_op jit(solution)/shard_map/ppermute | solution.py:191
  150.6 44.6 %collective-permute-start.22 = (bf16[512,1024]{1,0:T(8,128)(2,1)}, bf16[512,1024]{1,0:T(8,128)(2,1)S(1)}, u32[]{:S(2)}, u32[]{:S(2)}) collective-permute-start(bf16[512,1024]{1,0:T(8,128)(2,1)} %get-tuple-element.113), channel_id=1, source_target_pairs={{0,4},{4,0},{1,5},{5,1},{2,6},{6,2},{3,7},{7,3},{8,12},{12,8},{9,1... | collective-permute-start | bytes 3145736 | tf_op jit(solution)/shard_map/ppermute | solution.py:191
  151.2 44.1 %collective-permute-start.19 = (bf16[512,1024]{1,0:T(8,128)(2,1)S(1)}, bf16[512,1024]{1,0:T(8,128)(2,1)S(1)}, u32[]{:S(2)}, u32[]{:S(2)}) collective-permute-start(bf16[512,1024]{1,0:T(8,128)(2,1)S(1)} %collective-permute-done.15), channel_id=1, source_target_pairs={{0,1},{1,0},{2,3},{3,2},{4,5},{5,4},{6,7},{7,6},{8,9},{9,8},{10,11... | collective-permute-start | bytes 3145736 | tf_op jit(solution)/shard_map/ppermute | solution.py:191
  327.3 746.8 %all-gather.13.cloned.1.call-start = ((), (), s32[]{:S(2)}) async-start(), calls=%async_computation.6 | async-start | bytes 14090240 | tf_op jit(solution)/shard_map/all_gather | solution.py:292
  361.4 44.6 %collective-permute-start.33 = (bf16[512,1024]{1,0:T(8,128)(2,1)S(1)}, bf16[512,1024]{1,0:T(8,128)(2,1)S(1)}, u32[]{:S(2)}, u32[]{:S(2)}) collective-permute-start(bf16[512,1024]{1,0:T(8,128)(2,1)S(1)} %get-tuple-element.111), channel_id=1, source_target_pairs={{0,2},{1,3},{2,0},{3,1},{4,6},{5,7},{6,4},{7,5},{8,10},{9,11},{10,... | collective-permute-start | bytes 3145736 | tf_op jit(solution)/shard_map/ppermute | solution.py:191
  362.3 43.8 %collective-permute-start.35 = (bf16[512,1024]{1,0:T(8,128)(2,1)S(1)}, bf16[512,1024]{1,0:T(8,128)(2,1)S(1)}, u32[]{:S(2)}, u32[]{:S(2)}) collective-permute-start(bf16[512,1024]{1,0:T(8,128)(2,1)S(1)} %fusion.94), channel_id=1, source_target_pairs={{0,4},{4,0},{1,5},{5,1},{2,6},{6,2},{3,7},{7,3},{8,12},{12,8},{9,1... | collective-permute-start | bytes 3145736 | tf_op jit(solution)/shard_map/ppermute | solution.py:191
  423.0 47.3 %collective-permute-start.43 = (bf16[512,1024]{1,0:T(8,128)(2,1)}, bf16[512,1024]{1,0:T(8,128)(2,1)S(1)}, u32[]{:S(2)}, u32[]{:S(2)}) collective-permute-start(bf16[512,1024]{1,0:T(8,128)(2,1)} %get-tuple-element.109), channel_id=1, source_target_pairs={{0,2},{1,3},{2,0},{3,1},{4,6},{5,7},{6,4},{7,5},{8,10},{9,11},{10,... | collective-permute-start | bytes 3145736 | tf_op jit(solution)/shard_map/ppermute | solution.py:191
  444.8 46.2 %collective-permute-start.38 = (bf16[512,1024]{1,0:T(8,128)(2,1)}, bf16[512,1024]{1,0:T(8,128)(2,1)}, u32[]{:S(2)}, u32[]{:S(2)}) collective-permute-start(bf16[512,1024]{1,0:T(8,128)(2,1)} %collective-permute-done.36), channel_id=1, source_target_pairs={{0,2},{1,3},{2,0},{3,1},{4,6},{5,7},{6,4},{7,5},{8,10},{9,11},{10,... | collective-permute-start | bytes 3145736 | tf_op jit(solution)/shard_map/ppermute | solution.py:191
  446.4 725.6 %all-gather.21.cloned.1.call-start = ((), (), s32[]{:S(2)}) async-start(), calls=%async_computation.15 | async-start | bytes 7045120 | tf_op jit(solution)/shard_map/all_gather | solution.py:292
  454.0 41.6 %collective-permute-start.40 = (bf16[512,1024]{1,0:T(8,128)(2,1)}, bf16[512,1024]{1,0:T(8,128)(2,1)S(1)}, u32[]{:S(2)}, u32[]{:S(2)}) collective-permute-start(bf16[512,1024]{1,0:T(8,128)(2,1)} %collective-permute-done.36), channel_id=1, source_target_pairs={{0,1},{1,0},{2,3},{3,2},{4,5},{5,4},{6,7},{7,6},{8,9},{9,8},{10,11... | collective-permute-start | bytes 3145736 | tf_op jit(solution)/shard_map/ppermute | solution.py:191
  456.3 40.7 %collective-permute-start.44 = (bf16[512,1024]{1,0:T(8,128)(2,1)}, bf16[512,1024]{1,0:T(8,128)(2,1)S(1)}, u32[]{:S(2)}, u32[]{:S(2)}) collective-permute-start(bf16[512,1024]{1,0:T(8,128)(2,1)} %get-tuple-element.109), channel_id=1, source_target_pairs={{0,4},{4,0},{1,5},{5,1},{2,6},{6,2},{3,7},{7,3},{8,12},{12,8},{9,1... | collective-permute-start | bytes 3145736 | tf_op jit(solution)/shard_map/ppermute | solution.py:191
  676.7 63.0 %collective-permute-start.52 = (bf16[688,1024]{1,0:T(8,128)(2,1)}, bf16[688,1024]{1,0:T(8,128)(2,1)S(1)}, u32[]{:S(2)}, u32[]{:S(2)}) collective-permute-start(bf16[688,1024]{1,0:T(8,128)(2,1)} %get-tuple-element.74), channel_id=1, source_target_pairs={{0,8},{1,9},{2,10},{3,11},{4,12},{5,13},{6,14},{7,15}} | collective-permute-start | bytes 4227080 | tf_op jit(solution)/shard_map/ppermute | solution.py:284
  682.2 57.6 %collective-permute-start.56 = (bf16[688,1024]{1,0:T(8,128)(2,1)}, bf16[688,1024]{1,0:T(8,128)(2,1)}, u32[]{:S(2)}, u32[]{:S(2)}) collective-permute-start(bf16[688,1024]{1,0:T(8,128)(2,1)} %fusion.58), channel_id=1, source_target_pairs={{16,8},{24,16},{17,9},{25,17},{18,10},{26,18},{19,11},{27,19},{20,... | collective-permute-start | bytes 4227080 | tf_op jit(solution)/shard_map/ppermute | solution.py:286
  684.0 954.8 %reduce-scatter.8.cloned.1.call-start = ((), (), s32[]{:S(2)}) async-start(), calls=%async_computation.8 | async-start | bytes 7045120 | tf_op jit(solution)/shard_map/reduce_scatter | solution.py:265
  684.0 344.3 %collective-permute-start.50 = (bf16[1024,1376]{0,1:T(8,128)(2,1)}, bf16[1024,1376]{0,1:T(8,128)(2,1)}, u32[]{:S(2)}, u32[]{:S(2)}) collective-permute-start(bf16[1024,1376]{0,1:T(8,128)(2,1)} %get-tuple-element.68), channel_id=1, source_target_pairs={{0,8},{1,9},{2,10},{3,11},{4,12},{5,13},{6,14},{7,15}} | collective-permute-start | bytes 8454152 | tf_op jit(solution)/shard_map/ppermute | solution.py:284
  691.3 337.0 %collective-permute-start.60 = (bf16[1024,1376]{0,1:T(8,128)(2,1)S(1)}, bf16[1024,1376]{0,1:T(8,128)(2,1)}, u32[]{:S(2)}, u32[]{:S(2)}) collective-permute-start(bf16[1024,1376]{0,1:T(8,128)(2,1)S(1)} %fusion.2), channel_id=1, source_target_pairs={{16,8},{24,16},{17,9},{25,17},{18,10},{26,18},{19,11},{27,19},{20,... | collective-permute-start | bytes 8454152 | tf_op jit(solution)/shard_map/ppermute | solution.py:286
  743.5 193.0 %collective-permute-start.53 = (bf16[688,1024]{1,0:T(8,128)(2,1)S(1)}, bf16[688,1024]{1,0:T(8,128)(2,1)S(1)}, u32[]{:S(2)}, u32[]{:S(2)}) collective-permute-start(bf16[688,1024]{1,0:T(8,128)(2,1)S(1)} %get-tuple-element.72), channel_id=1, source_target_pairs={{0,8},{8,16},{1,9},{9,17},{2,10},{10,18},{3,11},{11,19},{4,12},{12... | collective-permute-start | bytes 4227080 | tf_op jit(solution)/shard_map/ppermute | solution.py:284
  920.2 122.7 %collective-permute-start.57 = (bf16[688,1024]{1,0:T(8,128)(2,1)}, bf16[688,1024]{1,0:T(8,128)(2,1)}, u32[]{:S(2)}, u32[]{:S(2)}) collective-permute-start(bf16[688,1024]{1,0:T(8,128)(2,1)} %get-tuple-element.71), channel_id=1, source_target_pairs={{8,0},{16,8},{24,16},{9,1},{17,9},{25,17},{10,2},{18,10},{26,18},{... | collective-permute-start | bytes 4227080 | tf_op jit(solution)/shard_map/ppermute | solution.py:286
  938.3 135.8 %collective-permute-start.54 = (bf16[688,1024]{1,0:T(8,128)(2,1)}, bf16[688,1024]{1,0:T(8,128)(2,1)}, u32[]{:S(2)}, u32[]{:S(2)}) collective-permute-start(bf16[688,1024]{1,0:T(8,128)(2,1)} %fusion.61), channel_id=1, source_target_pairs={{0,8},{8,16},{16,24},{1,9},{9,17},{17,25},{2,10},{10,18},{18,26},{... | collective-permute-start | bytes 4227080 | tf_op jit(solution)/shard_map/ppermute | solution.py:284
  1036.6 90.7 %collective-permute-start.58 = (bf16[1024,1376]{0,1:T(8,128)(2,1)}, bf16[1024,1376]{0,1:T(8,128)(2,1)}, u32[]{:S(2)}, u32[]{:S(2)}) collective-permute-start(bf16[1024,1376]{0,1:T(8,128)(2,1)} %get-tuple-element.64), channel_id=1, source_target_pairs={{0,8},{8,16},{1,9},{9,17},{2,10},{10,18},{3,11},{11,19},{4,12},{12... | collective-permute-start | bytes 8454152 | tf_op jit(solution)/shard_map/ppermute | solution.py:284
  1041.4 130.5 %collective-permute-start.61 = (bf16[1024,1376]{0,1:T(8,128)(2,1)}, bf16[1024,1376]{0,1:T(8,128)(2,1)S(1)}, u32[]{:S(2)}, u32[]{:S(2)}) collective-permute-start(bf16[1024,1376]{0,1:T(8,128)(2,1)} %get-tuple-element.63), channel_id=1, source_target_pairs={{8,0},{16,8},{24,16},{9,1},{17,9},{25,17},{10,2},{18,10},{26,18},{... | collective-permute-start | bytes 8454152 | tf_op jit(solution)/shard_map/ppermute | solution.py:286
  1132.9 111.5 %collective-permute-start.59 = (bf16[1024,1376]{0,1:T(8,128)(2,1)}, bf16[1024,1376]{0,1:T(8,128)(2,1)}, u32[]{:S(2)}, u32[]{:S(2)}) collective-permute-start(bf16[1024,1376]{0,1:T(8,128)(2,1)} %fusion.5), channel_id=1, source_target_pairs={{0,8},{8,16},{16,24},{1,9},{9,17},{17,25},{2,10},{10,18},{18,26},{... | collective-permute-start | bytes 8454152 | tf_op jit(solution)/shard_map/ppermute | solution.py:284
  1171.5 768.9 %reduce-scatter.12.cloned.1.call-start = ((), (), s32[]{:S(2)}) async-start(), calls=%async_computation.10 | async-start | bytes 14090240 | tf_op jit(solution)/shard_map/reduce_scatter | solution.py:265
  1278.3 60.9 %collective-permute-start.64 = (bf16[2048,1024]{1,0:T(8,128)(2,1)}, bf16[2048,1024]{1,0:T(8,128)(2,1)}, u32[]{:S(2)}, u32[]{:S(2)}) collective-permute-start(bf16[2048,1024]{1,0:T(8,128)(2,1)} %add_convert_fusion.7), channel_id=1, source_target_pairs={{0,1},{1,0},{2,3},{3,2},{4,5},{5,4},{6,7},{7,6},{8,9},{9,8},{10,11... | collective-permute-start | bytes 12582920 | tf_op jit(solution)/shard_map/ppermute | solution.py:191
  1306.6 677.3 %reduce-scatter.10.cloned.1.call-start = ((), (), s32[]{:S(2)}) async-start(), calls=%async_computation.9 | async-start | bytes 5242880 | tf_op jit(solution)/shard_map/reduce_scatter | solution.py:265
  1378.5 45.0 %collective-permute-start.67 = (bf16[512,1024]{1,0:T(8,128)(2,1)S(1)}, bf16[512,1024]{1,0:T(8,128)(2,1)S(1)}, u32[]{:S(2)}, u32[]{:S(2)}) collective-permute-start(bf16[512,1024]{1,0:T(8,128)(2,1)S(1)} %get-tuple-element.107), channel_id=1, source_target_pairs={{0,2},{1,3},{2,0},{3,1},{4,6},{5,7},{6,4},{7,5},{8,10},{9,11},{10,... | collective-permute-start | bytes 3145736 | tf_op jit(solution)/shard_map/ppermute | solution.py:191
  1380.1 43.5 %collective-permute-start.69 = (bf16[512,1024]{1,0:T(8,128)(2,1)S(1)}, bf16[512,1024]{1,0:T(8,128)(2,1)S(1)}, u32[]{:S(2)}, u32[]{:S(2)}) collective-permute-start(bf16[512,1024]{1,0:T(8,128)(2,1)S(1)} %fusion.90), channel_id=1, source_target_pairs={{0,4},{4,0},{1,5},{5,1},{2,6},{6,2},{3,7},{7,3},{8,12},{12,8},{9,1... | collective-permute-start | bytes 3145736 | tf_op jit(solution)/shard_map/ppermute | solution.py:191
  1443.3 47.1 %collective-permute-start.77 = (bf16[512,1024]{1,0:T(8,128)(2,1)S(1)}, bf16[512,1024]{1,0:T(8,128)(2,1)S(1)}, u32[]{:S(2)}, u32[]{:S(2)}) collective-permute-start(bf16[512,1024]{1,0:T(8,128)(2,1)S(1)} %get-tuple-element.105), channel_id=1, source_target_pairs={{0,2},{1,3},{2,0},{3,1},{4,6},{5,7},{6,4},{7,5},{8,10},{9,11},{10,... | collective-permute-start | bytes 3145736 | tf_op jit(solution)/shard_map/ppermute | solution.py:191
  1465.2 45.7 %collective-permute-start.72 = (bf16[512,1024]{1,0:T(8,128)(2,1)S(1)}, bf16[512,1024]{1,0:T(8,128)(2,1)S(1)}, u32[]{:S(2)}, u32[]{:S(2)}) collective-permute-start(bf16[512,1024]{1,0:T(8,128)(2,1)S(1)} %collective-permute-done.70), channel_id=1, source_target_pairs={{0,2},{1,3},{2,0},{3,1},{4,6},{5,7},{6,4},{7,5},{8,10},{9,11},{10,... | collective-permute-start | bytes 3145736 | tf_op jit(solution)/shard_map/ppermute | solution.py:191
  1468.5 42.7 %collective-permute-start.74 = (bf16[512,1024]{1,0:T(8,128)(2,1)S(1)}, bf16[512,1024]{1,0:T(8,128)(2,1)S(1)}, u32[]{:S(2)}, u32[]{:S(2)}) collective-permute-start(bf16[512,1024]{1,0:T(8,128)(2,1)S(1)} %collective-permute-done.70), channel_id=1, source_target_pairs={{0,1},{1,0},{2,3},{3,2},{4,5},{5,4},{6,7},{7,6},{8,9},{9,8},{10,11... | collective-permute-start | bytes 3145736 | tf_op jit(solution)/shard_map/ppermute | solution.py:191
  1468.7 43.2 %collective-permute-start.78 = (bf16[512,1024]{1,0:T(8,128)(2,1)S(1)}, bf16[512,1024]{1,0:T(8,128)(2,1)S(1)}, u32[]{:S(2)}, u32[]{:S(2)}) collective-permute-start(bf16[512,1024]{1,0:T(8,128)(2,1)S(1)} %get-tuple-element.105), channel_id=1, source_target_pairs={{0,4},{4,0},{1,5},{5,1},{2,6},{6,2},{3,7},{7,3},{8,12},{12,8},{9,1... | collective-permute-start | bytes 3145736 | tf_op jit(solution)/shard_map/ppermute | solution.py:191
  1470.3 41.7 %collective-permute-start.75 = (bf16[512,1024]{1,0:T(8,128)(2,1)S(1)}, bf16[512,1024]{1,0:T(8,128)(2,1)S(1)}, u32[]{:S(2)}, u32[]{:S(2)}) collective-permute-start(bf16[512,1024]{1,0:T(8,128)(2,1)S(1)} %collective-permute-done.71), channel_id=1, source_target_pairs={{0,1},{1,0},{2,3},{3,2},{4,5},{5,4},{6,7},{7,6},{8,9},{9,8},{10,11... | collective-permute-start | bytes 3145736 | tf_op jit(solution)/shard_map/ppermute | solution.py:191
  1531.6 483.1 %reduce-scatter.14.cloned.1.call-start = ((), (), s32[]{:S(2)}) async-start(), calls=%async_computation.11 | async-start | bytes 10485760 | tf_op jit(solution)/shard_map/reduce_scatter | solution.py:265
  1613.9 404.0 %reduce-scatter.6.cloned.1.call-start = ((), (), s32[]{:S(2)}) async-start(), calls=%async_computation.7 | async-start | bytes 5242880 | tf_op jit(solution)/shard_map/reduce_scatter | solution.py:265
  1632.9 40.2 %collective-permute-start.106 = (bf16[512,1376]{0,1:T(8,128)(2,1)}, bf16[512,1376]{0,1:T(8,128)(2,1)}, u32[]{:S(2)}, u32[]{:S(2)}) collective-permute-start(bf16[512,1376]{0,1:T(8,128)(2,1)} %constant_dynamic-slice_fusion.2), channel_id=1, source_target_pairs={{0,4},{4,0},{1,5},{5,1},{2,6},{6,2},{3,7},{7,3},{8,12},{12,8},{9,1... | collective-permute-start | bytes 4227080 | tf_op jit(solution)/shard_map/ppermute | solution.py:191
  1640.0 47.3 %collective-permute-start.104 = (bf16[688,512]{1,0:T(8,128)(2,1)S(1)}, bf16[688,512]{1,0:T(8,128)(2,1)S(1)}, u32[]{:S(2)}, u32[]{:S(2)}) collective-permute-start(bf16[688,512]{1,0:T(8,128)(2,1)S(1)} %dynamic-slice_bitcast_fusion.22), channel_id=1, source_target_pairs={{0,4},{4,0},{1,5},{5,1},{2,6},{6,2},{3,7},{7,3},{8,12},{12,8},{9,1... | collective-permute-start | bytes 2113544 | tf_op jit(solution)/shard_map/ppermute | solution.py:191
  1705.2 61.7 %collective-permute-start.94 = (bf16[2048,1024]{1,0:T(8,128)(2,1)}, bf16[2048,1024]{1,0:T(8,128)(2,1)}, u32[]{:S(2)}, u32[]{:S(2)}) collective-permute-start(bf16[2048,1024]{1,0:T(8,128)(2,1)} %convolution_convert_fusion.3), channel_id=1, source_target_pairs={{0,1},{1,0},{2,3},{3,2},{4,5},{5,4},{6,7},{7,6},{8,9},{9,8},{10,11... | collective-permute-start | bytes 12582920 | tf_op jit(solution)/shard_map/ppermute | solution.py:191
  1715.5 64.0 %collective-permute-start.92 = (bf16[2048,1024]{1,0:T(8,128)(2,1)}, bf16[2048,1024]{1,0:T(8,128)(2,1)}, u32[]{:S(2)}, u32[]{:S(2)}) collective-permute-start(bf16[2048,1024]{1,0:T(8,128)(2,1)} %convolution_convert_fusion.4), channel_id=1, source_target_pairs={{0,1},{1,0},{2,3},{3,2},{4,5},{5,4},{6,7},{7,6},{8,9},{9,8},{10,11... | collective-permute-start | bytes 12582920 | tf_op jit(solution)/shard_map/ppermute | solution.py:191
  1740.3 53.0 %collective-permute-start.86 = (bf16[2048,1024]{1,0:T(8,128)(2,1)}, bf16[2048,1024]{1,0:T(8,128)(2,1)}, u32[]{:S(2)}, u32[]{:S(2)}) collective-permute-start(bf16[2048,1024]{1,0:T(8,128)(2,1)} %add_convert_fusion.3), channel_id=1, source_target_pairs={{0,1},{1,0},{2,3},{3,2},{4,5},{5,4},{6,7},{7,6},{8,9},{9,8},{10,11... | collective-permute-start | bytes 12582920 | tf_op jit(solution)/shard_map/ppermute | solution.py:191
  1751.9 49.7 %collective-permute-start.84 = (bf16[2048,1024]{1,0:T(8,128)(2,1)}, bf16[2048,1024]{1,0:T(8,128)(2,1)}, u32[]{:S(2)}, u32[]{:S(2)}) collective-permute-start(bf16[2048,1024]{1,0:T(8,128)(2,1)} %add_convert_fusion.5), channel_id=1, source_target_pairs={{0,1},{1,0},{2,3},{3,2},{4,5},{5,4},{6,7},{7,6},{8,9},{9,8},{10,11... | collective-permute-start | bytes 12582920 | tf_op jit(solution)/shard_map/ppermute | solution.py:191
  1790.9 74.8 %collective-permute-start.93 = (bf16[512,1024]{1,0:T(8,128)(2,1)S(1)}, bf16[512,1024]{1,0:T(8,128)(2,1)}, u32[]{:S(2)}, u32[]{:S(2)}) collective-permute-start(bf16[512,1024]{1,0:T(8,128)(2,1)S(1)} %dynamic-slice_bitcast_fusion.9), channel_id=1, source_target_pairs={{0,4},{4,0},{1,5},{5,1},{2,6},{6,2},{3,7},{7,3},{8,12},{12,8},{9,1... | collective-permute-start | bytes 3145736 | tf_op jit(solution)/shard_map/ppermute | solution.py:191
  1793.4 95.3 %collective-permute-start.97 = (bf16[512,1024]{1,0:T(8,128)(2,1)S(1)}, bf16[512,1024]{1,0:T(8,128)(2,1)}, u32[]{:S(2)}, u32[]{:S(2)}) collective-permute-start(bf16[512,1024]{1,0:T(8,128)(2,1)S(1)} %get-tuple-element.101), channel_id=1, source_target_pairs={{0,2},{1,3},{2,0},{3,1},{4,6},{5,7},{6,4},{7,5},{8,10},{9,11},{10,... | collective-permute-start | bytes 3145736 | tf_op jit(solution)/shard_map/ppermute | solution.py:191
  1801.6 46.5 %collective-permute-start.87 = (bf16[512,1024]{1,0:T(8,128)(2,1)S(1)}, bf16[512,1024]{1,0:T(8,128)(2,1)}, u32[]{:S(2)}, u32[]{:S(2)}) collective-permute-start(bf16[512,1024]{1,0:T(8,128)(2,1)S(1)} %dynamic-slice_bitcast_fusion.12), channel_id=1, source_target_pairs={{0,4},{4,0},{1,5},{5,1},{2,6},{6,2},{3,7},{7,3},{8,12},{12,8},{9,1... | collective-permute-start | bytes 3145736 | tf_op jit(solution)/shard_map/ppermute | solution.py:191
  1812.0 50.9 %collective-permute-start.90 = (bf16[512,1024]{1,0:T(8,128)(2,1)S(1)}, bf16[512,1024]{1,0:T(8,128)(2,1)S(1)}, u32[]{:S(2)}, u32[]{:S(2)}) collective-permute-start(bf16[512,1024]{1,0:T(8,128)(2,1)S(1)} %get-tuple-element.104), channel_id=1, source_target_pairs={{0,2},{1,3},{2,0},{3,1},{4,6},{5,7},{6,4},{7,5},{8,10},{9,11},{10,... | collective-permute-start | bytes 3145736 | tf_op jit(solution)/shard_map/ppermute | solution.py:191
  1818.0 67.3 %collective-permute-start.96 = (bf16[512,1024]{1,0:T(8,128)(2,1)S(1)}, bf16[512,1024]{1,0:T(8,128)(2,1)S(1)}, u32[]{:S(2)}, u32[]{:S(2)}) collective-permute-start(bf16[512,1024]{1,0:T(8,128)(2,1)S(1)} %fusion.84), channel_id=1, source_target_pairs={{0,2},{1,3},{2,0},{3,1},{4,6},{5,7},{6,4},{7,5},{8,10},{9,11},{10,... | collective-permute-start | bytes 3145736 | tf_op jit(solution)/shard_map/ppermute | solution.py:191
  1848.1 41.0 %collective-permute-start.99 = (bf16[512,1024]{1,0:T(8,128)(2,1)S(1)}, bf16[512,1024]{1,0:T(8,128)(2,1)S(1)}, u32[]{:S(2)}, u32[]{:S(2)}) collective-permute-start(bf16[512,1024]{1,0:T(8,128)(2,1)S(1)} %fusion.82), channel_id=1, source_target_pairs={{0,4},{4,0},{1,5},{5,1},{2,6},{6,2},{3,7},{7,3},{8,12},{12,8},{9,1... | collective-permute-start | bytes 3145736 | tf_op jit(solution)/shard_map/ppermute | solution.py:191
  1862.9 68.5 %collective-permute-start.85 = (bf16[512,1024]{1,0:T(8,128)(2,1)S(1)}, bf16[512,1024]{1,0:T(8,128)(2,1)}, u32[]{:S(2)}, u32[]{:S(2)}) collective-permute-start(bf16[512,1024]{1,0:T(8,128)(2,1)S(1)} %dynamic-slice_bitcast_fusion.13), channel_id=1, source_target_pairs={{0,4},{4,0},{1,5},{5,1},{2,6},{6,2},{3,7},{7,3},{8,12},{12,8},{9,1... | collective-permute-start | bytes 3145736 | tf_op jit(solution)/shard_map/ppermute | solution.py:191
  1865.8 76.6 %collective-permute-start.89 = (bf16[512,1024]{1,0:T(8,128)(2,1)}, bf16[512,1024]{1,0:T(8,128)(2,1)}, u32[]{:S(2)}, u32[]{:S(2)}) collective-permute-start(bf16[512,1024]{1,0:T(8,128)(2,1)} %get-tuple-element.103), channel_id=1, source_target_pairs={{0,2},{1,3},{2,0},{3,1},{4,6},{5,7},{6,4},{7,5},{8,10},{9,11},{10,... | collective-permute-start | bytes 3145736 | tf_op jit(solution)/shard_map/ppermute | solution.py:191
  1885.4 46.1 %collective-permute-start.88 = (bf16[512,1024]{1,0:T(8,128)(2,1)}, bf16[512,1024]{1,0:T(8,128)(2,1)}, u32[]{:S(2)}, u32[]{:S(2)}) collective-permute-start(bf16[512,1024]{1,0:T(8,128)(2,1)} %fusion.88), channel_id=1, source_target_pairs={{0,2},{1,3},{2,0},{3,1},{4,6},{5,7},{6,4},{7,5},{8,10},{9,11},{10,... | collective-permute-start | bytes 3145736 | tf_op jit(solution)/shard_map/ppermute | solution.py:191
  1888.7 53.7 %collective-permute-start.91 = (bf16[512,1024]{1,0:T(8,128)(2,1)}, bf16[512,1024]{1,0:T(8,128)(2,1)}, u32[]{:S(2)}, u32[]{:S(2)}) collective-permute-start(bf16[512,1024]{1,0:T(8,128)(2,1)} %fusion.86), channel_id=1, source_target_pairs={{0,4},{4,0},{1,5},{5,1},{2,6},{6,2},{3,7},{7,3},{8,12},{12,8},{9,1... | collective-permute-start | bytes 3145736 | tf_op jit(solution)/shard_map/ppermute | solution.py:191
  1892.8 53.4 %collective-permute-start.100 = (f32[2,1024]{1,0:T(2,128)S(1)}, f32[2,1024]{1,0:T(2,128)S(1)}, u32[]{:S(2)}, u32[]{:S(2)}) collective-permute-start(f32[2,1024]{1,0:T(2,128)S(1)} %pad_maximum_fusion.10), channel_id=1, source_target_pairs={{0,4},{4,0},{1,5},{5,1},{2,6},{6,2},{3,7},{7,3},{8,12},{12,8},{9,1... | collective-permute-start | bytes 24584 | tf_op jit(solution)/shard_map/ppermute | solution.py:191
  1941.9 58.9 %collective-permute-start.107 = (bf16[512,1376]{0,1:T(8,128)(2,1)S(1)}, bf16[512,1376]{0,1:T(8,128)(2,1)}, u32[]{:S(2)}, u32[]{:S(2)}) collective-permute-start(bf16[512,1376]{0,1:T(8,128)(2,1)S(1)} %dynamic-slice_bitcast_fusion.3), channel_id=1, source_target_pairs={{0,4},{4,0},{1,5},{5,1},{2,6},{6,2},{3,7},{7,3},{8,12},{12,8},{9,1... | collective-permute-start | bytes 4227080 | tf_op jit(solution)/shard_map/ppermute | solution.py:191
  1946.2 40.5 %collective-permute-start.101 = (f32[2,1024]{1,0:T(2,128)S(1)}, f32[2,1024]{1,0:T(2,128)S(1)}, u32[]{:S(2)}, u32[]{:S(2)}) collective-permute-start(f32[2,1024]{1,0:T(2,128)S(1)} %fusion.185), channel_id=1, source_target_pairs={{0,8},{8,0},{16,24},{24,16},{1,9},{9,1},{17,25},{25,17},{2,10},{10... | collective-permute-start | bytes 24584 | tf_op jit(solution)/shard_map/ppermute | solution.py:191
  (146 other events, 3487.5 us)
Sparse Core Ops, SparseCore 0:
  11.3 220.8 all-gather.14
  233.8 78.9 all-gather.16
  314.9 195.2 all-gather.10
  511.7 102.7 all-gather.18
  615.9 281.1 all-gather.12
  898.5 184.8 all-gather.20
  1171.6 128.6 reduce-scatter.7
  1306.7 230.9 reduce-scatter.11
  1540.0 107.9 reduce-scatter.9
  1650.3 147.5 reduce-scatter.13
  1800.3 77.5 reduce-scatter.5

commit v5 on v2

--- a/solution.py
+++ b/solution.py
@@ -94,7 +94,7 @@
         scratch_shapes=[pltpu.VMEM((blocks, HD, block), BF)],
         compiler_params=pltpu.CompilerParams(vmem_limit_bytes=48 << 20),
         cost_estimate=pl.CostEstimate(
-            flops=4 * pairs * HD,
+            flops=30 * pairs * HD,
             transcendentals=pairs,
             bytes_accessed=seq_len * heads * HD * (12 + 8),
         ),
@@ -175,7 +175,7 @@
         ],
         compiler_params=pltpu.CompilerParams(vmem_limit_bytes=48 << 20),
         cost_estimate=pl.CostEstimate(
-            flops=10 * pairs * HD,
+            flops=38 * pairs * HD,
             transcendentals=pairs,
             bytes_accessed=seq_len * heads * HD * 16,
         ),
@@ -212,6 +212,10 @@
             start = (me_t ^ dt, (me_c ^ dc) * rows + part * half, 0)
             full = lax.dynamic_update_slice(full, piece[None], start)
     return with_layout_constraint(full, Layout((0, 1, 2)))
+
+
+def gather_pair(values):
+    return gather_rows(values), gather_rows(near(values))
 
 
 def scatter_rows(block_of):
@@ -259,6 +263,56 @@
     return lax.psum_scatter(grad, "fsdp", scatter_dimension=0, tiled=False)
 
 
+def far_groups():
+    count = lax.axis_size("fsdp")
+    return [list(range(i, count, 2)) for i in range(2)]
+
+
+def far_owners(grad):
+    grad = grad.reshape((-1, 2) + grad.shape[1:])
+    return lax.psum_scatter(
+        grad, "fsdp", scatter_dimension=0, tiled=False, axis_index_groups=far_groups()
+    )
+
+
+def far_spread(weight):
+    full = lax.all_gather(
+        weight, "fsdp", axis=0, tiled=False, axis_index_groups=far_groups()
+    )
+    return full.reshape((-1,) + full.shape[2:])
+
+
+def plane():
+    return lax.axis_index("fsdp") & 1
+
+
+def near(values):
+    return swap(values, "fsdp", 0)
+
+
+def in_pair(mine, other):
+    return jnp.where(plane() == 0, mine, other), jnp.where(plane() == 0, other, mine)
+
+
+def pair_share(block, axis, token, hold):
+    count = 2 * lax.axis_size("ctx")
+    size = block.shape[axis] // count
+    place = lax.axis_index("ctx") * 2
+
+    def columns(index):
+        return lax.dynamic_slice_in_dim(block, (place + index) * size, size, axis)
+
+    other = near(after(columns(1 - plane()), token))
+    return jnp.stack(in_pair(columns(plane()), after(other, hold)))
+
+
+def pair_grad(block, axis):
+    mine = lax.dynamic_index_in_dim(block, plane(), 0, keepdims=False)
+    give = lax.dynamic_index_in_dim(block, 1 - plane(), 0, keepdims=False)
+    both = trade_ctx(jnp.stack(in_pair(mine, near(give))), axis + 1)
+    return [v[i] for v in both for i in range(2)]
+
+
 def spread(weight):
     return lax.all_gather(weight, "fsdp", axis=0, tiled=False)
 
@@ -288,10 +342,9 @@
 ):
     n_f = lax.axis_size("fsdp")
     d_f = D // n_f
-    qkv_parts = [spread(ctx_half(qkv_weight[:, i], 1)) for i in range(3)]
+    qkv_full = spread(ctx_half(jnp.swapaxes(qkv_weight, 0, 1), 2))
+    qkv_parts = [qkv_full[:, i] for i in range(3)]
     out_full = spread(ctx_half(out_weight, 0))
-    gu_full = spread(ctx_half(gate_up_weight, 2).reshape(d_f, -1))
-    down_full = spread(ctx_half(down_weight, 0))
 
     def into(full, weight):
         return mm(full, weight, (((0, 2), (0, 1)), ((), ())))
@@ -305,13 +358,17 @@
     def in_blocks(grads, weight):
         return lambda t: mm(grads, lax.dynamic_index_in_dim(weight, t, 0, keepdims=False), NT)
 
+    def in_sum(full, grads):
+        return mm(full, grads, (((1,), (0,)), ((), ())))
+
     def in_part(full, grads):
-        return mm(full, grads, (((1,), (0,)), ((), ()))).astype(BF)
+        return in_sum(full, grads).astype(BF)
 
     def out_part(inner, full):
-        return jnp.stack(
-            [mm(inner, full[t], (((0,), (0,)), ((), ()))).astype(BF) for t in range(n_f)]
-        )
+        def block(t):
+            return sum(mm(v, f[t], (((0,), (0,)), ((), ()))) for v, f in zip(inner, full))
+
+        return jnp.stack([block(t).astype(BF) for t in range(n_f)])
 
     input_float = layer_input.astype(F32)
     attn_scale = attn_gain.astype(F32)
@@ -323,30 +380,46 @@
     attn_full = gather_rows(normed_attn)
     seq_len = attn_full.shape[1]
     cosine, sine = rope_tables(seq_len)
-    cotan_full = gather_rows(after(cotangent, attn_full))
-    proj = [into(attn_full, part) for part in qkv_parts]
+    cotans = gather_pair(after(cotangent, attn_full))
+    proj = after([into(attn_full, part) for part in qkv_parts], cotans[0])
     queries, keys, values, head_outs, norms = attend_forward(*proj, cosine, sine)
+    gu_share = pair_share(gate_up_weight, 2, tuple(proj), head_outs)
+    gu_full = far_spread(gu_share.reshape(2, d_f, -1))
+    down_share = pair_share(down_weight, 0, gu_share, gu_share)
+    down_full = far_spread(down_share)
     resid = input_float + scatter_rows(out_blocks(head_outs, out_full))
     rms_two = lax.rsqrt(row_total(jnp.sum(resid * resid, axis=-1)) / D + rms_epsilon)[:, None]
     normed_ffn = (resid * rms_two * ffn_scale).astype(BF)
-    ffn_full = gather_rows(normed_ffn)
-    gate_up = into(ffn_full, gu_full)
-    units = gate_up.shape[1] // 2
-    gate = gate_up[:, :units]
-    up_value = gate_up[:, units:]
-    sigma = jax.nn.sigmoid(gate)
-    hidden = (gate * sigma * up_value).astype(BF)
-    down_part = out_part(hidden, cotan_full)
-    down_sum = owners(down_part)
+    tokens = gather_pair(normed_ffn)
+    inner = []
+    for part in tokens:
+        gate_up = into(part, gu_full)
+        units = gate_up.shape[1] // 2
+        gate = gate_up[:, :units]
+        up_value = gate_up[:, units:]
+        sigma = jax.nn.sigmoid(gate)
+        inner.append((gate, up_value, sigma, (gate * sigma * up_value).astype(BF)))
+    hidden = [v[3] for v in inner]
+    down_part = out_part(hidden, cotans)
+    down_sum = far_owners(down_part)
     down_full = after(down_full, down_part)
-    grad_hidden = back_out(cotan_full, down_full)
-    grad_gu = jnp.concatenate(
-        [grad_hidden * up_value * sigma * (1.0 + gate * (1.0 - sigma)), grad_hidden * gate * sigma],
-        axis=1,
-    ).astype(BF)
-    gu_part = in_part(ffn_full, grad_gu)
-    gu_sum = owners(after(gu_part, down_sum))
-    grad_nffn = after(scatter_rows(in_blocks(grad_gu, gu_full)), (gu_part, down_sum))
+    grad_gu = []
+    for cotan, (gate, up_value, sigma, _) in zip(cotans, inner):
+        grad_hidden = back_out(cotan, down_full)
+        grad_gu.append(
+            jnp.concatenate(
+                [
+                    grad_hidden * up_value * sigma * (1.0 + gate * (1.0 - sigma)),
+                    grad_hidden * gate * sigma,
+                ],
+                axis=1,
+            ).astype(BF)
+        )
+    grad_near = scatter_rows(in_blocks(grad_gu[1], gu_full))
+    gu_part = (in_sum(tokens[0], grad_gu[0]) + in_sum(tokens[1], grad_gu[1])).astype(BF)
+    gu_sum = far_owners(gu_part)
+    grad_own = scatter_rows(in_blocks(grad_gu[0], gu_full))
+    grad_nffn = after(grad_own, gu_part) + near(grad_near.astype(BF)).astype(F32)
     ffn_term = grad_nffn * ffn_scale
     ffn_dot = row_total(jnp.sum(ffn_term * resid, axis=-1))[:, None]
     grad_resid = cotangent.astype(F32) + rms_two * ffn_term - resid * rms_two**3 * ffn_dot / D
@@ -354,35 +427,43 @@
     grad_branch = grad_resid.astype(BF)
     branch_full = gather_rows(grad_branch)
     grad_heads = back_out(branch_full, out_full).astype(BF)
-    out_sum = owners(out_part(head_outs, branch_full))
+    out_sum = owners(out_part([head_outs], [branch_full]))
     grad_proj = attend_backward(
         queries, keys, values, head_outs, norms, grad_heads, cosine, sine
     )
-    qkv_part = [in_part(attn_full, grad) for grad in grad_proj]
+    qkv_part = [
+        in_part(attn_full, jnp.concatenate(grad_proj[1:], axis=1)),
+        in_part(attn_full, grad_proj[0]),
+    ]
     qkv_sum = [owners(part) for part in qkv_part]
     grad_nattn = scatter_rows(
         in_blocks(jnp.concatenate(grad_proj, axis=1), jnp.concatenate(qkv_parts, axis=2))
     )
     hidden = after(hidden, qkv_part)
-    layer_output = (resid + scatter_rows(out_blocks(hidden, down_full))).astype(BF)
+    out_near = scatter_rows(out_blocks(hidden[1], down_full))
+    out_own = scatter_rows(out_blocks(hidden[0], down_full))
+    layer_output = (resid + out_own + near(out_near.astype(BF)).astype(F32)).astype(BF)
     attn_term = grad_nattn * attn_scale
     attn_dot = row_total(jnp.sum(attn_term * input_float, axis=-1))[:, None]
     grad_input = grad_resid + rms_one * attn_term - input_float * rms_one**3 * attn_dot / D
     attn_gain_part = jnp.sum(grad_nattn * input_float * rms_one, axis=0)
     gain_grads = total_rows(jnp.stack([attn_gain_part, ffn_gain_part]))
 
-    down_grad = out_grad(down_sum)
-    rows, other_rows = trade_ctx(gu_sum, 0)
+    down_grad = jnp.concatenate(pair_grad(down_sum, 1), axis=0).astype(F32)
     gu_grad = jnp.concatenate(
-        [v.reshape(v.shape[0], 2, -1) for v in (rows, other_rows)], axis=2
+        [v.reshape(v.shape[0], 2, -1) for v in pair_grad(gu_sum, 0)], axis=2
     ).astype(F32)
     out_weight_grad = out_grad(out_sum)
     done = (down_grad, out_weight_grad, gu_grad, grad_input, layer_output, gain_grads)
     qkv_grad = []
     for part in qkv_sum:
-        qkv_grad.append(jnp.concatenate(trade_ctx(after(part, done), 0), axis=1).astype(F32))
+        first, second = trade_ctx(after(part, done), 0)
+        wide = queries.shape[1]
+        for i in range(0, first.shape[1], wide):
+            both = [first[:, i : i + wide], second[:, i : i + wide]]
+            qkv_grad.append(jnp.concatenate(both, axis=1).astype(F32))
         done = done + (qkv_grad[-1],)
-    qkv_grad = jnp.stack(qkv_grad, axis=1)
+    qkv_grad = jnp.stack([qkv_grad[2], qkv_grad[0], qkv_grad[1]], axis=1)
 
     return (
         layer_output,

time: 1840 us -> 2050 us (1.11)
  waiting for transfers between devices: 887 us -> 986 us
  local copies, waits for them, and re-layouts: 143 us -> 182 us
  matrix products: 472 us -> 509 us
  starting transfers between devices: 79 us -> 107 us
    ppermute x97 -> x148, waiting for transfers between devices: 477 us -> 982 us  [swap(): lax.ppermute(values, axis, [(i, i ^ step) for i in range(lax.axis_size(ax...]
    all_gather x6 -> x2, waiting for transfers between devices: 294 us -> 3.76 us  [spread(): return lax.all_gather(weight, 'fsdp', axis=0, tiled=False)]
    reduce_scatter x6 -> x3, waiting for transfers between devices: 116 us -> 0.01 us  [owners(): return lax.psum_scatter(grad, 'fsdp', scatter_dimension=0, tiled=False)]
    dot_general x34 -> x48, matrix products: 472 us -> 509 us  [mm(): return lax.dot_general(left, right, dims, preferred_element_type=F32)]
    ppermute x97 -> x148, starting transfers between devices: 78.5 us -> 106 us  [swap(): lax.ppermute(values, axis, [(i, i ^ step) for i in range(lax.axis_size(ax...]
    dynamic_update_slice x64 -> x96, local copies, waits for them, and re-layouts: 69.6 us -> 83.3 us  [gather_rows(): full = lax.dynamic_update_slice(full, piece[None], start)]
  transfers between devices with their start and end apart: 109 -> 157, of which waited for: 40 -> 57; matrix products, arithmetic and copies ran while one was open for 38% -> 35% of each run, Pallas kernels for 4% -> 4%
where the time goes in v5:
time: 2050 us; the launch traced here: 2040 us
  waiting for transfers between devices  986 us (48%)
  matrix products  509 us (25%)
  local copies, waits for them, and re-layouts  182 us (9%)
  other arithmetic  121 us (6%)
  starting transfers between devices  107 us (5%)
  Pallas kernels  79.1 us (4%)
  blocking collectives  36 us (2%)
    ppermute x148, waiting for transfers between devices, swap(): lax.ppermute(values, axis, [(i, i ^ step) for i in range(lax.axis_size(ax...  982 us
    dot_general x48, matrix products, mm(): return lax.dot_general(left, right, dims, preferred_element_type=F32)  509 us
    ppermute x148, starting transfers between devices, swap(): lax.ppermute(values, axis, [(i, i ^ step) for i in range(lax.axis_size(ax...  106 us
    dynamic_update_slice x96, local copies, waits for them, and re-layouts, gather_rows(): full = lax.dynamic_update_slice(full, piece[None], start)  83.3 us
    pallas_call x1, Pallas kernels, attend_backward(): pl.pallas_call(kernel, grid=(heads, blocks), in_specs=[row, col, col, row...  44 us
  transfers between devices with their start and end apart: 157, of which 57 were waited for; matrix products, arithmetic and copies ran while one was open for 35% of the time, Pallas kernels for 4%

profile of v5, /device:TPU:0, one launch (start us, length us, event | category | flops | bytes accessed | tf_op | source)
XLA Modules:
  0.0 2037.0 jit_solution(14316914118016263948)
XLA Ops:
  31.1 20.3 collective-permute-done
  58.4 19.6 collective-permute-done.1
  79.9 17.8 collective-permute-done.2
  124.5 16.8 collective-permute-done.14
  156.9 10.5 collective-permute-done.15
  169.7 19.1 collective-permute-done.16
  196.8 18.0 collective-permute-done.22
  214.9 59.6 %collective-permute-done.67 = bf16[1024,1024]{1,0:T(8,128)(2,1)S(1)} collective-permute-done((bf16[1024,1024]{1,0:T(8,128)(2,1)}, bf16[1024,1024]{1,0:T(8,128)(2,1)S(1)}, u32[]{:S(2)}, u32[]{:S(2)}) %collective-permute-start.67) | collective-permute-done | bytes 2097184 | tf_op jit(solution)/shard_map/ppermute | solution.py:191
  290.1 15.1 convolution_bitcast_fusion.2.v_in
  305.2 15.1 convolution_bitcast_fusion.3.k_in
  320.3 12.6 convolution_bitcast_fusion.4.q_in
  332.9 35.1 %shard_map.143 = (bf16[2048,512]{1,0:T(8,128)(2,1)S(1)}, bf16[2048,512]{1,0:T(8,128)(2,1)}, bf16[2048,512]{1,0:T(8,128)(2,1)}, bf16[2048,512]{1,0:T(8,128)(2,1)}, f32[4,1,2048]{2,1,0:T(1,128)S(1)}) custom-call(f32[2048,512]{1,0:T(8,128)} %convolution_bitcast_fusion.4.q_in, f32[2048,512]{1,0:T(8,128)} %convolution_bitcast_fusion.3.k_in, ...), custom_call_target="tpu_custom_call" | custom-call | flops 40265318400 | bytes 20971520 | tf_op jit(solution)/shard_map/pallas_call | solution.py:88
  379.4 36.3 %collective-permute-done.50 = bf16[1024,2,688]{0,2,1:T(8,128)(2,1)} collective-permute-done((bf16[1024,2,688]{0,2,1:T(8,128)(2,1)}, bf16[1024,2,688]{0,2,1:T(8,128)(2,1)}, u32[]{:S(2)}, u32[]{:S(2)}) %collective-permute-start.50) | collective-permute-done | bytes 2818080 | tf_op jit(solution)/shard_map/ppermute | solution.py:191
  453.6 17.7 collective-permute-done.75
  491.8 50.8 %collective-permute-done.31 = bf16[512,1024]{1,0:T(8,128)(2,1)S(1)} collective-permute-done((bf16[512,1024]{1,0:T(8,128)(2,1)S(1)}, bf16[512,1024]{1,0:T(8,128)(2,1)S(1)}, u32[]{:S(2)}, u32[]{:S(2)}) %collective-permute-start.31) | collective-permute-done | bytes 1048608 | tf_op jit(solution)/shard_map/ppermute | solution.py:191
  551.8 13.3 collective-permute-done.29
  565.1 22.3 %collective-permute-done.32 = bf16[512,1024]{1,0:T(8,128)(2,1)S(1)} collective-permute-done((bf16[512,1024]{1,0:T(8,128)(2,1)S(1)}, bf16[512,1024]{1,0:T(8,128)(2,1)S(1)}, u32[]{:S(2)}, u32[]{:S(2)}) %collective-permute-start.32) | collective-permute-done | bytes 1048608 | tf_op jit(solution)/shard_map/ppermute | solution.py:191
  614.7 98.6 %collective-permute-done.66 = bf16[688,1024]{1,0:T(8,128)(2,1)} collective-permute-done((bf16[688,1024]{1,0:T(8,128)(2,1)}, bf16[688,1024]{1,0:T(8,128)(2,1)}, u32[]{:S(2)}, u32[]{:S(2)}) %collective-permute-start.66) | collective-permute-done | bytes 1409056 | tf_op jit(solution)/shard_map/ppermute | solution.py:191
  723.9 15.6 collective-permute-done.37
  743.3 18.8 collective-permute-done.38
  766.5 17.1 collective-permute-done.43
  786.9 11.2 collective-permute-done.51
  813.0 20.9 %collective-permute-done.52 = bf16[512,1024]{1,0:T(8,128)(2,1)S(1)} collective-permute-done((bf16[512,1024]{1,0:T(8,128)(2,1)S(1)}, bf16[512,1024]{1,0:T(8,128)(2,1)S(1)}, u32[]{:S(2)}, u32[]{:S(2)}) %collective-permute-start.52) | collective-permute-done | bytes 1048608 | tf_op jit(solution)/shard_map/ppermute | solution.py:191
  839.7 19.3 collective-permute-done.59
  859.4 21.4 %collective-permute-done.54 = bf16[512,1024]{1,0:T(8,128)(2,1)S(1)} collective-permute-done((bf16[512,1024]{1,0:T(8,128)(2,1)S(1)}, bf16[512,1024]{1,0:T(8,128)(2,1)S(1)}, u32[]{:S(2)}, u32[]{:S(2)}) %collective-permute-start.54) | collective-permute-done | bytes 1048608 | tf_op jit(solution)/shard_map/ppermute | solution.py:191
  898.4 28.0 %convolution_bitcast_fusion = f32[2048,1376]{0,1:T(8,128)S(1)} fusion(bf16[4,2048,1024]{2,1,0:T(8,128)(2,1)} %bitcast_dynamic-update-slice_fusion.32, bf16[4,1024,1376]{1,2,0:T(8,128)(2,1)} %bitcast.730), kind=kOutput, calls=%fused_computation.8 | convolution fusion | flops 23085449216 | bytes 39321600 | tf_op jit(solution)/shard_map/dot_general | solution.py:21
  950.5 28.5 %convolution_bitcast_fusion.1 = f32[2048,1376]{0,1:T(8,128)} fusion(bf16[4,2048,1024]{2,1,0:T(8,128)(2,1)S(1)} %bitcast.688, bf16[4,1024,1376]{1,2,0:T(8,128)(2,1)} %bitcast.731), kind=kOutput, calls=%fused_computation.9 | convolution fusion | flops 23085449216 | bytes 39321600 | tf_op jit(solution)/shard_map/dot_general | solution.py:21
  1011.7 25.8 %fusion.4 = (bf16[2048,688]{0,1:T(8,128)(2,1)}, bf16[2048,688]{0,1:T(8,128)(2,1)}) fusion(f32[2048,1376]{0,1:T(8,128)} %copy-done.26, bf16[4,2048,1024]{2,1,0:T(8,128)(2,1)} %bitcast_dynamic-update-slice_fusion.16, bf16[4,688,1024]{2,1,0:T(8,128)(2,1)} %all-gather.14.cloned.1.call-done), kind=kOutput, calls=%fused_computation.39 | convolution fusion | flops 11561041920 | bytes 39321600 | tf_op jit(solution)/shard_map/dot_general | solution.py:21
  1037.6 19.6 fusion.10
  1057.2 12.4 convolution_convert_fusion.8
  1069.6 10.4 convolution_convert_fusion.7
  1098.3 31.6 %fusion = f32[4,1024,1376]{1,2,0:T(8,128)} fusion(bf16[4,2048,1024]{2,1,0:T(8,128)(2,1)} %bitcast_dynamic-update-slice_fusion.32, bf16[2048,688]{0,1:T(8,128)(2,1)} %get-tuple-element.61, bf16[2048,688]{0,1:T(8,128)(2,1)} %get-tuple-element.60), kind=kOutput, calls=%fused_computation.33 | convolution fusion | flops 23096721408 | bytes 44957696 | tf_op jit(solution)/shard_map/dot_general | solution.py:21
  1129.9 29.6 %add_convert_fusion = bf16[4,1024,1376]{1,2,0:T(8,128)(2,1)} fusion(f32[4,1024,1376]{1,2,0:T(8,128)} %fusion, bf16[4,2048,1024]{2,1,0:T(8,128)(2,1)} %copy-done.25, bf16[2048,688]{0,1:T(8,128)(2,1)S(1)} %copy-done.85, bf16[2048,688]{0,1:T(8,128)(2,1)S(1)} %get-tuple-element.62), kind=kOutput, calls=%fused_computation | convolution fusion | flops 23107993600 | bytes 56229888 | tf_op jit(solution)/shard_map/dot_general | solution.py:21
  1159.7 10.1 add_convert_fusion.9
  1172.4 9.6 add_convert_fusion.7
  1186.0 10.1 add_convert_fusion.8
  1196.6 21.1 %collective-permute-done.93 = bf16[512,1024]{1,0:T(8,128)(2,1)S(1)} collective-permute-done((bf16[512,1024]{1,0:T(8,128)(2,1)S(1)}, bf16[512,1024]{1,0:T(8,128)(2,1)S(1)}, u32[]{:S(2)}, u32[]{:S(2)}) %collective-permute-start.93) | collective-permute-done | bytes 1048608 | tf_op jit(solution)/shard_map/ppermute | solution.py:191
  1219.5 11.9 collective-permute-done.96
  1233.0 11.2 add_convert_fusion.10
  1246.7 10.8 collective-permute-done.94
  1288.8 13.6 collective-permute-done.86
  1303.0 19.8 collective-permute-done.87
  1323.7 34.5 %collective-permute-done.98 = bf16[1024,1024]{1,0:T(8,128)(2,1)S(1)} collective-permute-done((bf16[1024,1024]{1,0:T(8,128)(2,1)S(1)}, bf16[1024,1024]{1,0:T(8,128)(2,1)S(1)}, u32[]{:S(2)}, u32[]{:S(2)}) %collective-permute-start.98) | collective-permute-done | bytes 2097184 | tf_op jit(solution)/shard_map/ppermute | solution.py:191
  1377.4 20.8 %collective-permute-done.99 = bf16[512,1024]{1,0:T(8,128)(2,1)S(1)} collective-permute-done((bf16[512,1024]{1,0:T(8,128)(2,1)S(1)}, bf16[512,1024]{1,0:T(8,128)(2,1)S(1)}, u32[]{:S(2)}, u32[]{:S(2)}) %collective-permute-start.99) | collective-permute-done | bytes 1048608 | tf_op jit(solution)/shard_map/ppermute | solution.py:191
  1403.0 21.0 %collective-permute-done.100 = bf16[512,1024]{1,0:T(8,128)(2,1)S(1)} collective-permute-done((bf16[512,1024]{1,0:T(8,128)(2,1)S(1)}, bf16[512,1024]{1,0:T(8,128)(2,1)S(1)}, u32[]{:S(2)}, u32[]{:S(2)}) %collective-permute-start.100) | collective-permute-done | bytes 1048608 | tf_op jit(solution)/shard_map/ppermute | solution.py:191
  1424.3 20.3 collective-permute-done.101
  1465.8 15.0 bitcast_convert_fusion.g
  1480.8 44.0 %shard_map.144 = (bf16[2048,512]{1,0:T(8,128)(2,1)S(1)}, bf16[2048,512]{1,0:T(8,128)(2,1)}, bf16[2048,512]{1,0:T(8,128)(2,1)}) custom-call(bf16[2048,512]{1,0:T(8,128)(2,1)} %copy-done.6, bf16[2048,512]{1,0:T(8,128)(2,1)} %get-tuple-element.38.k, bf16[2048,512]{1,0:T(8,128)(2,1)} %get-tuple-element.39.v, bf16[2048,512]{1,0:T(8,128)(2,1)} %get-tuple-element.34.o, ...), custom_call_target="tpu_custom_call" | custom-call | flops 51002736640 | bytes 16777216 | tf_op jit(solution)/shard_map/pallas_call | solution.py:164
  1524.7 23.3 %convolution_convert_fusion = bf16[4,1024,1024]{2,1,0:T(8,128)(2,1)} fusion(bf16[4,2048,1024]{2,1,0:T(8,128)(2,1)} %copy-done.24, bf16[2048,512]{1,0:T(8,128)(2,1)} %get-tuple-element.46, bf16[2048,512]{1,0:T(8,128)(2,1)} %get-tuple-element.45), kind=kOutput, calls=%fused_computation.22 | convolution fusion | flops 17192452096 | bytes 29360128 | tf_op jit(solution)/shard_map/dot_general | solution.py:21
  1562.6 12.5 convolution_convert_fusion.1
  1575.0 10.3 convolution_convert_fusion.2
  1585.4 11.1 convolution_convert_fusion.13
  1604.4 38.6 %collective-permute-done.141 = bf16[688,1024]{1,0:T(8,128)(2,1)} collective-permute-done((bf16[688,1024]{1,0:T(8,128)(2,1)S(1)}, bf16[688,1024]{1,0:T(8,128)(2,1)}, u32[]{:S(2)}, u32[]{:S(2)}) %collective-permute-start.141) | collective-permute-done | bytes 1409056 | tf_op jit(solution)/shard_map/ppermute | solution.py:191
  1712.2 10.8 add_convert_fusion.2
  1771.0 15.4 collective-permute-done.131
  1790.9 9.3 collective-permute-done.135
  1812.0 19.2 collective-permute-done.122
  1834.6 10.5 collective-permute-done.126
  1856.9 11.0 collective-permute-done.144
  1875.4 14.8 psum.31
  1901.1 14.3 collective-permute-done.139
  1919.7 39.6 %collective-permute-done.120 = bf16[512,1024]{1,0:T(8,128)(2,1)} collective-permute-done((bf16[512,1024]{1,0:T(8,128)(2,1)}, bf16[512,1024]{1,0:T(8,128)(2,1)}, u32[]{:S(2)}, u32[]{:S(2)}) %collective-permute-start.120) | collective-permute-done | bytes 1048608 | tf_op jit(solution)/shard_map/ppermute | solution.py:191
  1975.1 11.4 maximum_convert_fusion
  1992.6 32.5 %collective-permute-done.146 = bf16[512,512]{1,0:T(8,128)(2,1)S(1)} collective-permute-done((bf16[512,512]{1,0:T(8,128)(2,1)S(1)}, bf16[512,512]{1,0:T(8,128)(2,1)S(1)}, u32[]{:S(2)}, u32[]{:S(2)}) %collective-permute-start.146) | collective-permute-done | bytes 524320 | tf_op jit(solution)/shard_map/ppermute | solution.py:191
  (773 shorter events, 653.1 us)
Async XLA Ops:
  7.2 282.9 %all-gather.10.cloned.1.call-start = ((), (), s32[]{:S(2)}) async-start(), calls=%async_computation.11 | async-start | bytes 15728640 | tf_op jit(solution)/shard_map/all_gather | solution.py:317
  11.2 362.0 %all-gather.12.cloned.1.call-start = ((), (), s32[]{:S(2)}) async-start(), calls=%async_computation.12 | async-start | bytes 5242880 | tf_op jit(solution)/shard_map/all_gather | solution.py:317
  29.5 48.5 %collective-permute-start.1 = (bf16[512,1024]{1,0:T(8,128)(2,1)}, bf16[512,1024]{1,0:T(8,128)(2,1)}, u32[]{:S(2)}, u32[]{:S(2)}) collective-permute-start(bf16[512,1024]{1,0:T(8,128)(2,1)} %get-tuple-element.132), channel_id=1, source_target_pairs={{0,2},{1,3},{2,0},{3,1},{4,6},{5,7},{6,4},{7,5},{8,10},{9,11},{10,... | collective-permute-start | bytes 3145736 | tf_op jit(solution)/shard_map/ppermute | solution.py:191
  31.1 47.4 %collective-permute-start.3 = (bf16[512,1024]{1,0:T(8,128)(2,1)}, bf16[512,1024]{1,0:T(8,128)(2,1)}, u32[]{:S(2)}, u32[]{:S(2)}) collective-permute-start(bf16[512,1024]{1,0:T(8,128)(2,1)} %get-tuple-element.132), channel_id=1, source_target_pairs={{0,1},{1,0},{2,3},{3,2},{4,5},{5,4},{6,7},{7,6},{8,9},{9,8},{10,11... | collective-permute-start | bytes 3145736 | tf_op jit(solution)/shard_map/ppermute | solution.py:191
  118.5 779.9 %all-gather.8.cloned.1.call-start = ((), (), s32[]{:S(2)}) async-start(), calls=%async_computation.5 | async-start | bytes 16908288 | tf_op jit(solution)/shard_map/all_gather | solution.py:279
  119.1 48.3 %collective-permute-start.15 = (bf16[512,1024]{1,0:T(8,128)(2,1)}, bf16[512,1024]{1,0:T(8,128)(2,1)}, u32[]{:S(2)}, u32[]{:S(2)}) collective-permute-start(bf16[512,1024]{1,0:T(8,128)(2,1)} %get-tuple-element.130), channel_id=1, source_target_pairs={{0,2},{1,3},{2,0},{3,1},{4,6},{5,7},{6,4},{7,5},{8,10},{9,11},{10,... | collective-permute-start | bytes 3145736 | tf_op jit(solution)/shard_map/ppermute | solution.py:191
  141.3 47.5 %collective-permute-start.16 = (bf16[512,1024]{1,0:T(8,128)(2,1)S(1)}, bf16[512,1024]{1,0:T(8,128)(2,1)}, u32[]{:S(2)}, u32[]{:S(2)}) collective-permute-start(bf16[512,1024]{1,0:T(8,128)(2,1)S(1)} %collective-permute-done.14), channel_id=1, source_target_pairs={{0,2},{1,3},{2,0},{3,1},{4,6},{5,7},{6,4},{7,5},{8,10},{9,11},{10,... | collective-permute-start | bytes 3145736 | tf_op jit(solution)/shard_map/ppermute | solution.py:191
  142.3 132.2 %collective-permute-start.67 = (bf16[1024,1024]{1,0:T(8,128)(2,1)}, bf16[1024,1024]{1,0:T(8,128)(2,1)S(1)}, u32[]{:S(2)}, u32[]{:S(2)}) collective-permute-start(bf16[1024,1024]{1,0:T(8,128)(2,1)} %param.15), channel_id=1, source_target_pairs={{0,8},{8,0},{16,24},{24,16},{1,9},{9,1},{17,25},{25,17},{2,10},{10... | collective-permute-start | bytes 6291464 | tf_op jit(solution)/shard_map/ppermute | solution.py:191
  191.6 84.7 %collective-permute-start.23 = (bf16[512,1024]{1,0:T(8,128)(2,1)}, bf16[512,1024]{1,0:T(8,128)(2,1)S(1)}, u32[]{:S(2)}, u32[]{:S(2)}) collective-permute-start(bf16[512,1024]{1,0:T(8,128)(2,1)} %collective-permute-done.21), channel_id=1, source_target_pairs={{0,4},{4,0},{1,5},{5,1},{2,6},{6,2},{3,7},{7,3},{8,12},{12,8},{9,1... | collective-permute-start | bytes 3145736 | tf_op jit(solution)/shard_map/ppermute | solution.py:191
  193.1 84.7 %collective-permute-start.20 = (bf16[512,1024]{1,0:T(8,128)(2,1)}, bf16[512,1024]{1,0:T(8,128)(2,1)S(1)}, u32[]{:S(2)}, u32[]{:S(2)}) collective-permute-start(bf16[512,1024]{1,0:T(8,128)(2,1)} %collective-permute-done.16), channel_id=1, source_target_pairs={{0,1},{1,0},{2,3},{3,2},{4,5},{5,4},{6,7},{7,6},{8,9},{9,8},{10,11... | collective-permute-start | bytes 3145736 | tf_op jit(solution)/shard_map/ppermute | solution.py:191
  195.2 89.1 %collective-permute-start.24 = (bf16[512,1024]{1,0:T(8,128)(2,1)S(1)}, bf16[512,1024]{1,0:T(8,128)(2,1)S(1)}, u32[]{:S(2)}, u32[]{:S(2)}) collective-permute-start(bf16[512,1024]{1,0:T(8,128)(2,1)S(1)} %copy-done.61), channel_id=1, source_target_pairs={{0,1},{1,0},{2,3},{3,2},{4,5},{5,4},{6,7},{7,6},{8,9},{9,8},{10,11... | collective-permute-start | bytes 3145736 | tf_op jit(solution)/shard_map/ppermute | solution.py:191
  214.9 72.0 %collective-permute-start.25 = (bf16[512,1024]{1,0:T(8,128)(2,1)}, bf16[512,1024]{1,0:T(8,128)(2,1)S(1)}, u32[]{:S(2)}, u32[]{:S(2)}) collective-permute-start(bf16[512,1024]{1,0:T(8,128)(2,1)} %collective-permute-done.21), channel_id=1, source_target_pairs={{0,1},{1,0},{2,3},{3,2},{4,5},{5,4},{6,7},{7,6},{8,9},{9,8},{10,11... | collective-permute-start | bytes 3145736 | tf_op jit(solution)/shard_map/ppermute | solution.py:191
  276.3 155.2 %collective-permute-start.69 = (bf16[512,1024]{1,0:T(8,128)(2,1)}, bf16[512,1024]{1,0:T(8,128)(2,1)S(1)}, u32[]{:S(2)}, u32[]{:S(2)}) collective-permute-start(bf16[512,1024]{1,0:T(8,128)(2,1)} %get-tuple-element.122), channel_id=1, source_target_pairs={{0,2},{1,3},{2,0},{3,1},{4,6},{5,7},{6,4},{7,5},{8,10},{9,11},{10,... | collective-permute-start | bytes 3145736 | tf_op jit(solution)/shard_map/ppermute | solution.py:191
  284.3 138.7 %collective-permute-start.68 = (bf16[512,1024]{1,0:T(8,128)(2,1)}, bf16[512,1024]{1,0:T(8,128)(2,1)}, u32[]{:S(2)}, u32[]{:S(2)}) collective-permute-start(bf16[512,1024]{1,0:T(8,128)(2,1)} %get-tuple-element.122), channel_id=1, source_target_pairs={{0,4},{4,0},{1,5},{5,1},{2,6},{6,2},{3,7},{7,3},{8,12},{12,8},{9,1... | collective-permute-start | bytes 3145736 | tf_op jit(solution)/shard_map/ppermute | solution.py:191
  332.9 82.8 %collective-permute-start.50 = (bf16[1024,2,688]{0,2,1:T(8,128)(2,1)}, bf16[1024,2,688]{0,2,1:T(8,128)(2,1)}, u32[]{:S(2)}, u32[]{:S(2)}) collective-permute-start(bf16[1024,2,688]{0,2,1:T(8,128)(2,1)} %constant_dynamic-slice_fusion.3), channel_id=1, source_target_pairs={{0,8},{8,0},{16,24},{24,16},{1,9},{9,1},{17,25},{25,17},{2,10},{10... | collective-permute-start | bytes 8454152 | tf_op jit(solution)/shard_map/ppermute | solution.py:191
  379.4 98.3 %collective-permute-start.30 = (bf16[2048,1024]{1,0:T(8,128)(2,1)}, bf16[2048,1024]{1,0:T(8,128)(2,1)}, u32[]{:S(2)}, u32[]{:S(2)}) collective-permute-start(bf16[2048,1024]{1,0:T(8,128)(2,1)} %convolution_convert_fusion.11), channel_id=1, source_target_pairs={{0,1},{1,0},{2,3},{3,2},{4,5},{5,4},{6,7},{7,6},{8,9},{9,8},{10,11... | collective-permute-start | bytes 12582920 | tf_op jit(solution)/shard_map/ppermute | solution.py:191
  422.9 588.8 %all-gather.14.cloned.1.call-start = ((), (), s32[]{:S(2)}) async-start(), calls=%async_computation.13 | async-start | bytes 8454144 | tf_op jit(solution)/shard_map/all_gather | solution.py:279
  431.5 54.6 %collective-permute-start.28 = (bf16[2048,1024]{1,0:T(8,128)(2,1)}, bf16[2048,1024]{1,0:T(8,128)(2,1)}, u32[]{:S(2)}, u32[]{:S(2)}) collective-permute-start(bf16[2048,1024]{1,0:T(8,128)(2,1)} %convolution_convert_fusion.12), channel_id=1, source_target_pairs={{0,1},{1,0},{2,3},{3,2},{4,5},{5,4},{6,7},{7,6},{8,9},{9,8},{10,11... | collective-permute-start | bytes 12582920 | tf_op jit(solution)/shard_map/ppermute | solution.py:191
  471.4 74.2 %collective-permute-start.76 = (bf16[512,1024]{1,0:T(8,128)(2,1)}, bf16[512,1024]{1,0:T(8,128)(2,1)}, u32[]{:S(2)}, u32[]{:S(2)}) collective-permute-start(bf16[512,1024]{1,0:T(8,128)(2,1)} %get-tuple-element.121), channel_id=1, source_target_pairs={{0,4},{4,0},{1,5},{5,1},{2,6},{6,2},{3,7},{7,3},{8,12},{12,8},{9,1... | collective-permute-start | bytes 3145736 | tf_op jit(solution)/shard_map/ppermute | solution.py:191
  472.9 76.6 %collective-permute-start.77 = (bf16[512,1024]{1,0:T(8,128)(2,1)S(1)}, bf16[512,1024]{1,0:T(8,128)(2,1)}, u32[]{:S(2)}, u32[]{:S(2)}) collective-permute-start(bf16[512,1024]{1,0:T(8,128)(2,1)S(1)} %collective-permute-done.75), channel_id=1, source_target_pairs={{0,4},{4,0},{1,5},{5,1},{2,6},{6,2},{3,7},{7,3},{8,12},{12,8},{9,1... | collective-permute-start | bytes 3145736 | tf_op jit(solution)/shard_map/ppermute | solution.py:191
  482.9 59.8 %collective-permute-start.31 = (bf16[512,1024]{1,0:T(8,128)(2,1)S(1)}, bf16[512,1024]{1,0:T(8,128)(2,1)S(1)}, u32[]{:S(2)}, u32[]{:S(2)}) collective-permute-start(bf16[512,1024]{1,0:T(8,128)(2,1)S(1)} %dynamic-slice_bitcast_fusion.25), channel_id=1, source_target_pairs={{0,4},{4,0},{1,5},{5,1},{2,6},{6,2},{3,7},{7,3},{8,12},{12,8},{9,1... | collective-permute-start | bytes 3145736 | tf_op jit(solution)/shard_map/ppermute | solution.py:191
  484.7 59.9 %collective-permute-start.34 = (bf16[512,1024]{1,0:T(8,128)(2,1)S(1)}, bf16[512,1024]{1,0:T(8,128)(2,1)S(1)}, u32[]{:S(2)}, u32[]{:S(2)}) collective-permute-start(bf16[512,1024]{1,0:T(8,128)(2,1)S(1)} %get-tuple-element.128), channel_id=1, source_target_pairs={{0,2},{1,3},{2,0},{3,1},{4,6},{5,7},{6,4},{7,5},{8,10},{9,11},{10,... | collective-permute-start | bytes 3145736 | tf_op jit(solution)/shard_map/ppermute | solution.py:191
  491.3 73.8 %collective-permute-start.29 = (bf16[512,1024]{1,0:T(8,128)(2,1)S(1)}, bf16[512,1024]{1,0:T(8,128)(2,1)S(1)}, u32[]{:S(2)}, u32[]{:S(2)}) collective-permute-start(bf16[512,1024]{1,0:T(8,128)(2,1)S(1)} %dynamic-slice_bitcast_fusion.26), channel_id=1, source_target_pairs={{0,4},{4,0},{1,5},{5,1},{2,6},{6,2},{3,7},{7,3},{8,12},{12,8},{9,1... | collective-permute-start | bytes 3145736 | tf_op jit(solution)/shard_map/ppermute | solution.py:191
  549.5 54.4 %collective-permute-start.78 = (bf16[512,1024]{1,0:T(8,128)(2,1)}, bf16[512,1024]{1,0:T(8,128)(2,1)}, u32[]{:S(2)}, u32[]{:S(2)}) collective-permute-start(bf16[512,1024]{1,0:T(8,128)(2,1)} %get-tuple-element.121), channel_id=1, source_target_pairs={{0,1},{1,0},{2,3},{3,2},{4,5},{5,4},{6,7},{7,6},{8,9},{9,8},{10,11... | collective-permute-start | bytes 3145736 | tf_op jit(solution)/shard_map/ppermute | solution.py:191
  588.6 124.7 %collective-permute-start.66 = (bf16[688,1024]{1,0:T(8,128)(2,1)}, bf16[688,1024]{1,0:T(8,128)(2,1)}, u32[]{:S(2)}, u32[]{:S(2)}) collective-permute-start(bf16[688,1024]{1,0:T(8,128)(2,1)} %constant_dynamic-slice_fusion.2), channel_id=1, source_target_pairs={{0,8},{8,0},{16,24},{24,16},{1,9},{9,1},{17,25},{25,17},{2,10},{10... | collective-permute-start | bytes 4227080 | tf_op jit(solution)/shard_map/ppermute | solution.py:191
  603.9 110.9 %collective-permute-start.36 = (bf16[512,1024]{1,0:T(8,128)(2,1)}, bf16[512,1024]{1,0:T(8,128)(2,1)}, u32[]{:S(2)}, u32[]{:S(2)}) collective-permute-start(bf16[512,1024]{1,0:T(8,128)(2,1)} %get-tuple-element.126), channel_id=1, source_target_pairs={{0,4},{4,0},{1,5},{5,1},{2,6},{6,2},{3,7},{7,3},{8,12},{12,8},{9,1... | collective-permute-start | bytes 3145736 | tf_op jit(solution)/shard_map/ppermute | solution.py:191
  714.8 47.3 %collective-permute-start.38 = (bf16[512,1024]{1,0:T(8,128)(2,1)}, bf16[512,1024]{1,0:T(8,128)(2,1)}, u32[]{:S(2)}, u32[]{:S(2)}) collective-permute-start(bf16[512,1024]{1,0:T(8,128)(2,1)} %collective-permute-done.36), channel_id=1, source_target_pairs={{0,2},{1,3},{2,0},{3,1},{4,6},{5,7},{6,4},{7,5},{8,10},{9,11},{10,... | collective-permute-start | bytes 3145736 | tf_op jit(solution)/shard_map/ppermute | solution.py:191
  717.9 80.2 %collective-permute-start.51 = (bf16[1024,1024]{1,0:T(8,128)(2,1)S(1)}, bf16[1024,1024]{1,0:T(8,128)(2,1)}, u32[]{:S(2)}, u32[]{:S(2)}) collective-permute-start(bf16[1024,1024]{1,0:T(8,128)(2,1)S(1)} %multiply_convert_fusion.2), channel_id=1, source_target_pairs={{0,8},{8,0},{16,24},{24,16},{1,9},{9,1},{17,25},{25,17},{2,10},{10... | collective-permute-start | bytes 6291464 | tf_op jit(solution)/shard_map/ppermute | solution.py:191
  719.8 839.2 %reduce-scatter.8.cloned.1.call-start = ((), (), s32[]{:S(2)}) async-start(), calls=%async_computation.7 | async-start | bytes 8454144 | tf_op jit(solution)/shard_map/reduce_scatter | solution.py:273
  783.6 51.4 %collective-permute-start.47 = (bf16[512,1024]{1,0:T(8,128)(2,1)S(1)}, bf16[512,1024]{1,0:T(8,128)(2,1)S(1)}, u32[]{:S(2)}, u32[]{:S(2)}) collective-permute-start(bf16[512,1024]{1,0:T(8,128)(2,1)S(1)} %collective-permute-done.43), channel_id=1, source_target_pairs={{0,1},{1,0},{2,3},{3,2},{4,5},{5,4},{6,7},{7,6},{8,9},{9,8},{10,11... | collective-permute-start | bytes 3145736 | tf_op jit(solution)/shard_map/ppermute | solution.py:191
  812.1 46.9 %collective-permute-start.55 = (bf16[512,1024]{1,0:T(8,128)(2,1)S(1)}, bf16[512,1024]{1,0:T(8,128)(2,1)S(1)}, u32[]{:S(2)}, u32[]{:S(2)}) collective-permute-start(bf16[512,1024]{1,0:T(8,128)(2,1)S(1)} %get-tuple-element.124), channel_id=1, source_target_pairs={{0,1},{1,0},{2,3},{3,2},{4,5},{5,4},{6,7},{7,6},{8,9},{9,8},{10,11... | collective-permute-start | bytes 3145736 | tf_op jit(solution)/shard_map/ppermute | solution.py:191
  812.4 46.7 %collective-permute-start.59 = (bf16[512,1024]{1,0:T(8,128)(2,1)S(1)}, bf16[512,1024]{1,0:T(8,128)(2,1)S(1)}, u32[]{:S(2)}, u32[]{:S(2)}) collective-permute-start(bf16[512,1024]{1,0:T(8,128)(2,1)S(1)} %get-tuple-element.123), channel_id=1, source_target_pairs={{0,2},{1,3},{2,0},{3,1},{4,6},{5,7},{6,4},{7,5},{8,10},{9,11},{10,... | collective-permute-start | bytes 3145736 | tf_op jit(solution)/shard_map/ppermute | solution.py:191
  838.2 46.3 %collective-permute-start.60 = (bf16[512,1024]{1,0:T(8,128)(2,1)S(1)}, bf16[512,1024]{1,0:T(8,128)(2,1)S(1)}, u32[]{:S(2)}, u32[]{:S(2)}) collective-permute-start(bf16[512,1024]{1,0:T(8,128)(2,1)S(1)} %get-tuple-element.123), channel_id=1, source_target_pairs={{0,4},{4,0},{1,5},{5,1},{2,6},{6,2},{3,7},{7,3},{8,12},{12,8},{9,1... | collective-permute-start | bytes 3145736 | tf_op jit(solution)/shard_map/ppermute | solution.py:191
  1097.2 651.9 %reduce-scatter.12.cloned.1.call-start = ((), (), s32[]{:S(2)}) async-start(), calls=%async_computation.9 | async-start | bytes 16908288 | tf_op jit(solution)/shard_map/reduce_scatter | solution.py:273
  1097.2 62.4 %collective-permute-start.84 = (bf16[2048,1024]{1,0:T(8,128)(2,1)}, bf16[2048,1024]{1,0:T(8,128)(2,1)}, u32[]{:S(2)}, u32[]{:S(2)}) collective-permute-start(bf16[2048,1024]{1,0:T(8,128)(2,1)} %convolution_convert_fusion.9), channel_id=1, source_target_pairs={{0,1},{1,0},{2,3},{3,2},{4,5},{5,4},{6,7},{7,6},{8,9},{9,8},{10,11... | collective-permute-start | bytes 12582920 | tf_op jit(solution)/shard_map/ppermute | solution.py:191
  1097.3 134.7 %collective-permute-start.82 = (bf16[2048,1024]{1,0:T(8,128)(2,1)}, bf16[2048,1024]{1,0:T(8,128)(2,1)}, u32[]{:S(2)}, u32[]{:S(2)}) collective-permute-start(bf16[2048,1024]{1,0:T(8,128)(2,1)} %convolution_convert_fusion.10), channel_id=1, source_target_pairs={{0,1},{1,0},{2,3},{3,2},{4,5},{5,4},{6,7},{7,6},{8,9},{9,8},{10,11... | collective-permute-start | bytes 12582920 | tf_op jit(solution)/shard_map/ppermute | solution.py:191
  1097.8 73.8 %collective-permute-start.92 = (bf16[2048,1024]{1,0:T(8,128)(2,1)}, bf16[2048,1024]{1,0:T(8,128)(2,1)}, u32[]{:S(2)}, u32[]{:S(2)}) collective-permute-start(bf16[2048,1024]{1,0:T(8,128)(2,1)} %convolution_convert_fusion.7), channel_id=1, source_target_pairs={{0,1},{1,0},{2,3},{3,2},{4,5},{5,4},{6,7},{7,6},{8,9},{9,8},{10,11... | collective-permute-start | bytes 12582920 | tf_op jit(solution)/shard_map/ppermute | solution.py:191
  1097.9 86.5 %collective-permute-start.90 = (bf16[2048,1024]{1,0:T(8,128)(2,1)}, bf16[2048,1024]{1,0:T(8,128)(2,1)}, u32[]{:S(2)}, u32[]{:S(2)}) collective-permute-start(bf16[2048,1024]{1,0:T(8,128)(2,1)} %convolution_convert_fusion.8), channel_id=1, source_target_pairs={{0,1},{1,0},{2,3},{3,2},{4,5},{5,4},{6,7},{7,6},{8,9},{9,8},{10,11... | collective-permute-start | bytes 12582920 | tf_op jit(solution)/shard_map/ppermute | solution.py:191
  1159.6 757.1 %reduce-scatter.10.cloned.1.call-start = ((), (), s32[]{:S(2)}) async-start(), calls=%async_computation.8 | async-start | bytes 5242880 | tf_op jit(solution)/shard_map/reduce_scatter | solution.py:263
  1170.3 98.3 %collective-permute-start.85 = (bf16[512,1024]{1,0:T(8,128)(2,1)S(1)}, bf16[512,1024]{1,0:T(8,128)(2,1)S(1)}, u32[]{:S(2)}, u32[]{:S(2)}) collective-permute-start(bf16[512,1024]{1,0:T(8,128)(2,1)S(1)} %dynamic-slice_bitcast_fusion.21), channel_id=1, source_target_pairs={{0,4},{4,0},{1,5},{5,1},{2,6},{6,2},{3,7},{7,3},{8,12},{12,8},{9,1... | collective-permute-start | bytes 3145736 | tf_op jit(solution)/shard_map/ppermute | solution.py:191
  1183.9 74.9 %collective-permute-start.95 = (bf16[512,1024]{1,0:T(8,128)(2,1)S(1)}, bf16[512,1024]{1,0:T(8,128)(2,1)S(1)}, u32[]{:S(2)}, u32[]{:S(2)}) collective-permute-start(bf16[512,1024]{1,0:T(8,128)(2,1)S(1)} %get-tuple-element.117), channel_id=1, source_target_pairs={{0,2},{1,3},{2,0},{3,1},{4,6},{5,7},{6,4},{7,5},{8,10},{9,11},{10,... | collective-permute-start | bytes 3145736 | tf_op jit(solution)/shard_map/ppermute | solution.py:191
  1184.3 47.0 %collective-permute-start.96 = (bf16[512,1024]{1,0:T(8,128)(2,1)S(1)}, bf16[512,1024]{1,0:T(8,128)(2,1)S(1)}, u32[]{:S(2)}, u32[]{:S(2)}) collective-permute-start(bf16[512,1024]{1,0:T(8,128)(2,1)S(1)} %get-tuple-element.118), channel_id=1, source_target_pairs={{0,2},{1,3},{2,0},{3,1},{4,6},{5,7},{6,4},{7,5},{8,10},{9,11},{10,... | collective-permute-start | bytes 3145736 | tf_op jit(solution)/shard_map/ppermute | solution.py:191
  1267.2 91.1 %collective-permute-start.98 = (bf16[1024,1024]{1,0:T(8,128)(2,1)S(1)}, bf16[1024,1024]{1,0:T(8,128)(2,1)S(1)}, u32[]{:S(2)}, u32[]{:S(2)}) collective-permute-start(bf16[1024,1024]{1,0:T(8,128)(2,1)S(1)} %pad_maximum_fusion.10), channel_id=1, source_target_pairs={{0,8},{8,0},{16,24},{24,16},{1,9},{9,1},{17,25},{25,17},{2,10},{10... | collective-permute-start | bytes 6291464 | tf_op jit(solution)/shard_map/ppermute | solution.py:191
  1269.8 52.9 %collective-permute-start.87 = (bf16[512,1024]{1,0:T(8,128)(2,1)S(1)}, bf16[512,1024]{1,0:T(8,128)(2,1)S(1)}, u32[]{:S(2)}, u32[]{:S(2)}) collective-permute-start(bf16[512,1024]{1,0:T(8,128)(2,1)S(1)} %get-tuple-element.119), channel_id=1, source_target_pairs={{0,2},{1,3},{2,0},{3,1},{4,6},{5,7},{6,4},{7,5},{8,10},{9,11},{10,... | collective-permute-start | bytes 3145736 | tf_op jit(solution)/shard_map/ppermute | solution.py:191
  1375.9 48.0 %collective-permute-start.100 = (bf16[512,1024]{1,0:T(8,128)(2,1)S(1)}, bf16[512,1024]{1,0:T(8,128)(2,1)S(1)}, u32[]{:S(2)}, u32[]{:S(2)}) collective-permute-start(bf16[512,1024]{1,0:T(8,128)(2,1)S(1)} %get-tuple-element.116), channel_id=1, source_target_pairs={{0,2},{1,3},{2,0},{3,1},{4,6},{5,7},{6,4},{7,5},{8,10},{9,11},{10,... | collective-permute-start | bytes 3145736 | tf_op jit(solution)/shard_map/ppermute | solution.py:191
  1377.4 46.8 %collective-permute-start.102 = (bf16[512,1024]{1,0:T(8,128)(2,1)S(1)}, bf16[512,1024]{1,0:T(8,128)(2,1)S(1)}, u32[]{:S(2)}, u32[]{:S(2)}) collective-permute-start(bf16[512,1024]{1,0:T(8,128)(2,1)S(1)} %get-tuple-element.116), channel_id=1, source_target_pairs={{0,1},{1,0},{2,3},{3,2},{4,5},{5,4},{6,7},{7,6},{8,9},{9,8},{10,11... | collective-permute-start | bytes 3145736 | tf_op jit(solution)/shard_map/ppermute | solution.py:191
  1398.2 46.4 %collective-permute-start.101 = (bf16[512,1024]{1,0:T(8,128)(2,1)S(1)}, bf16[512,1024]{1,0:T(8,128)(2,1)S(1)}, u32[]{:S(2)}, u32[]{:S(2)}) collective-permute-start(bf16[512,1024]{1,0:T(8,128)(2,1)S(1)} %collective-permute-done.99), channel_id=1, source_target_pairs={{0,2},{1,3},{2,0},{3,1},{4,6},{5,7},{6,4},{7,5},{8,10},{9,11},{10,... | collective-permute-start | bytes 3145736 | tf_op jit(solution)/shard_map/ppermute | solution.py:191
  1465.8 520.7 %reduce-scatter.14.cloned.1.call-start = ((), (), s32[]{:S(2)}) async-start(), calls=%async_computation.10 | async-start | bytes 10485760 | tf_op jit(solution)/shard_map/reduce_scatter | solution.py:263
  1548.0 442.0 %reduce-scatter.6.cloned.1.call-start = ((), (), s32[]{:S(2)}) async-start(), calls=%async_computation.6 | async-start | bytes 5242880 | tf_op jit(solution)/shard_map/reduce_scatter | solution.py:263
  1560.6 82.4 %collective-permute-start.141 = (bf16[688,1024]{1,0:T(8,128)(2,1)S(1)}, bf16[688,1024]{1,0:T(8,128)(2,1)}, u32[]{:S(2)}, u32[]{:S(2)}) collective-permute-start(bf16[688,1024]{1,0:T(8,128)(2,1)S(1)} %dynamic-slice_bitcast_fusion.2), channel_id=1, source_target_pairs={{0,8},{8,0},{16,24},{24,16},{1,9},{9,1},{17,25},{25,17},{2,10},{10... | collective-permute-start | bytes 4227080 | tf_op jit(solution)/shard_map/ppermute | solution.py:191
  1596.5 82.6 %collective-permute-start.132 = (bf16[2048,1024]{1,0:T(8,128)(2,1)}, bf16[2048,1024]{1,0:T(8,128)(2,1)}, u32[]{:S(2)}, u32[]{:S(2)}) collective-permute-start(bf16[2048,1024]{1,0:T(8,128)(2,1)} %convolution_convert_fusion.1), channel_id=1, source_target_pairs={{0,1},{1,0},{2,3},{3,2},{4,5},{5,4},{6,7},{7,6},{8,9},{9,8},{10,11... | collective-permute-start | bytes 12582920 | tf_op jit(solution)/shard_map/ppermute | solution.py:191
  1653.5 58.3 %collective-permute-start.130 = (bf16[2048,1024]{1,0:T(8,128)(2,1)}, bf16[2048,1024]{1,0:T(8,128)(2,1)}, u32[]{:S(2)}, u32[]{:S(2)}) collective-permute-start(bf16[2048,1024]{1,0:T(8,128)(2,1)} %convolution_convert_fusion.2), channel_id=1, source_target_pairs={{0,1},{1,0},{2,3},{3,2},{4,5},{5,4},{6,7},{7,6},{8,9},{9,8},{10,11... | collective-permute-start | bytes 12582920 | tf_op jit(solution)/shard_map/ppermute | solution.py:191
  1653.6 71.3 %collective-permute-start.121 = (bf16[2048,1024]{1,0:T(8,128)(2,1)}, bf16[2048,1024]{1,0:T(8,128)(2,1)}, u32[]{:S(2)}, u32[]{:S(2)}) collective-permute-start(bf16[2048,1024]{1,0:T(8,128)(2,1)} %convolution_convert_fusion.4), channel_id=1, source_target_pairs={{0,1},{1,0},{2,3},{3,2},{4,5},{5,4},{6,7},{7,6},{8,9},{9,8},{10,11... | collective-permute-start | bytes 12582920 | tf_op jit(solution)/shard_map/ppermute | solution.py:191
  1679.0 52.8 %collective-permute-start.113 = (bf16[2048,1024]{1,0:T(8,128)(2,1)}, bf16[2048,1024]{1,0:T(8,128)(2,1)}, u32[]{:S(2)}, u32[]{:S(2)}) collective-permute-start(bf16[2048,1024]{1,0:T(8,128)(2,1)} %convolution_convert_fusion.6), channel_id=1, source_target_pairs={{0,1},{1,0},{2,3},{3,2},{4,5},{5,4},{6,7},{7,6},{8,9},{9,8},{10,11... | collective-permute-start | bytes 12582920 | tf_op jit(solution)/shard_map/ppermute | solution.py:191
  1692.7 53.1 %collective-permute-start.133 = (bf16[512,1024]{1,0:T(8,128)(2,1)}, bf16[512,1024]{1,0:T(8,128)(2,1)}, u32[]{:S(2)}, u32[]{:S(2)}) collective-permute-start(bf16[512,1024]{1,0:T(8,128)(2,1)} %dynamic-slice_bitcast_fusion.5), channel_id=1, source_target_pairs={{0,4},{4,0},{1,5},{5,1},{2,6},{6,2},{3,7},{7,3},{8,12},{12,8},{9,1... | collective-permute-start | bytes 3145736 | tf_op jit(solution)/shard_map/ppermute | solution.py:191
  1700.1 51.3 %collective-permute-start.136 = (bf16[512,1024]{1,0:T(8,128)(2,1)}, bf16[512,1024]{1,0:T(8,128)(2,1)}, u32[]{:S(2)}, u32[]{:S(2)}) collective-permute-start(bf16[512,1024]{1,0:T(8,128)(2,1)} %get-tuple-element.110), channel_id=1, source_target_pairs={{0,2},{1,3},{2,0},{3,1},{4,6},{5,7},{6,4},{7,5},{8,10},{9,11},{10,... | collective-permute-start | bytes 3145736 | tf_op jit(solution)/shard_map/ppermute | solution.py:191
  1752.4 115.6 %collective-permute-start.144 = (bf16[1024,1376]{0,1:T(8,128)(2,1)S(1)}, bf16[1024,1376]{0,1:T(8,128)(2,1)S(1)}, u32[]{:S(2)}, u32[]{:S(2)}) collective-permute-start(bf16[1024,1376]{0,1:T(8,128)(2,1)S(1)} %dynamic-slice_bitcast_fusion.1), channel_id=1, source_target_pairs={{0,8},{8,0},{16,24},{24,16},{1,9},{9,1},{17,25},{25,17},{2,10},{10... | collective-permute-start | bytes 8454152 | tf_op jit(solution)/shard_map/ppermute | solution.py:191
  1831.2 58.9 %collective-permute-start.114 = (bf16[512,1024]{1,0:T(8,128)(2,1)}, bf16[512,1024]{1,0:T(8,128)(2,1)}, u32[]{:S(2)}, u32[]{:S(2)}) collective-permute-start(bf16[512,1024]{1,0:T(8,128)(2,1)} %dynamic-slice_bitcast_fusion.14), channel_id=1, source_target_pairs={{0,4},{4,0},{1,5},{5,1},{2,6},{6,2},{3,7},{7,3},{8,12},{12,8},{9,1... | collective-permute-start | bytes 3145736 | tf_op jit(solution)/shard_map/ppermute | solution.py:191
  1845.2 53.7 %collective-permute-start.117 = (bf16[512,1024]{1,0:T(8,128)(2,1)}, bf16[512,1024]{1,0:T(8,128)(2,1)}, u32[]{:S(2)}, u32[]{:S(2)}) collective-permute-start(bf16[512,1024]{1,0:T(8,128)(2,1)} %fusion.96), channel_id=1, source_target_pairs={{0,2},{1,3},{2,0},{3,1},{4,6},{5,7},{6,4},{7,5},{8,10},{9,11},{10,... | collective-permute-start | bytes 3145736 | tf_op jit(solution)/shard_map/ppermute | solution.py:191
  1868.0 93.8 %collective-permute-start.129 = (bf16[1024,1024]{1,0:T(8,128)(2,1)}, bf16[1024,1024]{1,0:T(8,128)(2,1)}, u32[]{:S(2)}, u32[]{:S(2)}) collective-permute-start(bf16[1024,1024]{1,0:T(8,128)(2,1)} %pad_maximum_fusion.11), channel_id=1, source_target_pairs={{0,8},{8,0},{16,24},{24,16},{1,9},{9,1},{17,25},{25,17},{2,10},{10... | collective-permute-start | bytes 6291464 | tf_op jit(solution)/shard_map/ppermute | solution.py:191
  1872.3 99.7 %collective-permute-start.145 = (bf16[2,512,1376]{1,2,0:T(8,128)(2,1)}, bf16[2,512,1376]{1,2,0:T(8,128)(2,1)}, u32[]{:S(2)}, u32[]{:S(2)}) collective-permute-start(bf16[2,512,1376]{1,2,0:T(8,128)(2,1)} %fusion.52), channel_id=1, source_target_pairs={{0,4},{4,0},{1,5},{5,1},{2,6},{6,2},{3,7},{7,3},{8,12},{12,8},{9,1... | collective-permute-start | bytes 8454152 | tf_op jit(solution)/shard_map/ppermute | solution.py:191
  1891.2 68.1 %collective-permute-start.120 = (bf16[512,1024]{1,0:T(8,128)(2,1)}, bf16[512,1024]{1,0:T(8,128)(2,1)}, u32[]{:S(2)}, u32[]{:S(2)}) collective-permute-start(bf16[512,1024]{1,0:T(8,128)(2,1)} %fusion.94), channel_id=1, source_target_pairs={{0,4},{4,0},{1,5},{5,1},{2,6},{6,2},{3,7},{7,3},{8,12},{12,8},{9,1... | collective-permute-start | bytes 3145736 | tf_op jit(solution)/shard_map/ppermute | solution.py:191
  1915.4 46.4 %collective-permute-start.140 = (f32[2,1024]{1,0:T(2,128)S(1)}, f32[2,1024]{1,0:T(2,128)S(1)}, u32[]{:S(2)}, u32[]{:S(2)}) collective-permute-start(f32[2,1024]{1,0:T(2,128)S(1)} %fusion.267), channel_id=1, source_target_pairs={{0,16},{8,24},{16,0},{24,8},{1,17},{9,25},{17,1},{25,9},{2,18},{10... | collective-permute-start | bytes 24584 | tf_op jit(solution)/shard_map/ppermute | solution.py:191
  1917.9 52.2 %collective-permute-start.143 = (bf16[512,512]{1,0:T(8,128)(2,1)S(1)}, bf16[512,512]{1,0:T(8,128)(2,1)S(1)}, u32[]{:S(2)}, u32[]{:S(2)}) collective-permute-start(bf16[512,512]{1,0:T(8,128)(2,1)S(1)} %dynamic-slice_bitcast_fusion.27), channel_id=1, source_target_pairs={{0,4},{4,0},{1,5},{5,1},{2,6},{6,2},{3,7},{7,3},{8,12},{12,8},{9,1... | collective-permute-start | bytes 1572872 | tf_op jit(solution)/shard_map/ppermute | solution.py:191
  (206 other events, 5280.7 us)
Sparse Core Ops, SparseCore 0:
  11.3 261.4 all-gather.9
  274.3 98.7 all-gather.11
  423.0 260.2 all-gather.7
  720.0 133.9 all-gather.13
  1097.3 129.8 reduce-scatter.7
  1230.0 251.0 reduce-scatter.11
  1483.5 75.7 reduce-scatter.9
  1561.7 168.0 reduce-scatter.13
  1732.1 135.6 reduce-scatter.5

commit v6 on v5

--- a/solution.py
+++ b/solution.py
@@ -195,7 +195,7 @@
     return list(range(1, lax.axis_size("tp").bit_length() - 1))[::-1]
 
 
-def gather_rows(values):
+def gather_rows(values, arrived=None):
     rows, cols = values.shape
     half = rows // 2
     n_t, n_c = lax.axis_size("tp"), lax.axis_size("ctx")
@@ -208,23 +208,27 @@
             for (dc, dt), piece in list(held.items()):
                 key = (1, dt) if axis == "ctx" else (dc, dt | (1 << bit))
                 held[key] = swap(piece, axis, bit)
+            if arrived is not None and len(held) == 2:
+                arrived.append(held[key])
         for (dc, dt), piece in held.items():
             start = (me_t ^ dt, (me_c ^ dc) * rows + part * half, 0)
             full = lax.dynamic_update_slice(full, piece[None], start)
     return with_layout_constraint(full, Layout((0, 1, 2)))
 
 
-def gather_pair(values):
-    return gather_rows(values), gather_rows(near(values))
-
-
-def scatter_rows(block_of):
-    n_t, n_c = lax.axis_size("tp"), lax.axis_size("ctx")
-    me_t, me_c = lax.axis_index("tp"), lax.axis_index("ctx")
+def core_sums(block_of):
+    n_t = lax.axis_size("tp")
+    me_t = lax.axis_index("tp")
     sums = {}
     for dt in range(0, n_t, 2):
         got = swap(block_of(me_t ^ (dt + 1)).astype(BF), "tp", 0)
         sums[dt] = (block_of(me_t ^ dt) + got.astype(F32)).astype(BF)
+    return sums
+
+
+def scatter_sums(sums):
+    n_c = lax.axis_size("ctx")
+    me_c = lax.axis_index("ctx")
     rows = sums[0].shape[0] // n_c
     cols = sums[0].shape[1]
     half = rows // 2
@@ -249,6 +253,10 @@
     return jnp.concatenate(done, axis=0)
 
 
+def scatter_rows(block_of):
+    return scatter_sums(core_sums(block_of))
+
+
 def ctx_half(weight, axis):
     size = weight.shape[axis] // lax.axis_size("ctx")
     return lax.dynamic_slice_in_dim(weight, lax.axis_index("ctx") * size, size, axis)
@@ -380,17 +388,19 @@
     attn_full = gather_rows(normed_attn)
     seq_len = attn_full.shape[1]
     cosine, sine = rope_tables(seq_len)
-    cotans = gather_pair(after(cotangent, attn_full))
+    cotans = [gather_rows(after(cotangent, attn_full))]
     proj = after([into(attn_full, part) for part in qkv_parts], cotans[0])
     queries, keys, values, head_outs, norms = attend_forward(*proj, cosine, sine)
-    gu_share = pair_share(gate_up_weight, 2, tuple(proj), head_outs)
+    sums = core_sums(out_blocks(head_outs, out_full))
+    gu_share = pair_share(gate_up_weight, 2, tuple(proj), tuple(sums.values()))
     gu_full = far_spread(gu_share.reshape(2, d_f, -1))
     down_share = pair_share(down_weight, 0, gu_share, gu_share)
-    down_full = far_spread(down_share)
-    resid = input_float + scatter_rows(out_blocks(head_outs, out_full))
+    resid = after(input_float + scatter_sums(sums), down_share)
     rms_two = lax.rsqrt(row_total(jnp.sum(resid * resid, axis=-1)) / D + rms_epsilon)[:, None]
     normed_ffn = (resid * rms_two * ffn_scale).astype(BF)
-    tokens = gather_pair(normed_ffn)
+    down_full = far_spread(down_share)
+    tokens = [gather_rows(normed_ffn), gather_rows(near(normed_ffn))]
+    cotans.append(gather_rows(after(near(after(cotangent, tokens[0])), tokens[1])))
     inner = []
     for part in tokens:
         gate_up = into(part, gu_full)
@@ -415,18 +425,33 @@
                 axis=1,
             ).astype(BF)
         )
-    grad_near = scatter_rows(in_blocks(grad_gu[1], gu_full))
-    gu_part = (in_sum(tokens[0], grad_gu[0]) + in_sum(tokens[1], grad_gu[1])).astype(BF)
-    gu_sum = far_owners(gu_part)
-    grad_own = scatter_rows(in_blocks(grad_gu[0], gu_full))
-    grad_nffn = after(grad_own, gu_part) + near(grad_near.astype(BF)).astype(F32)
+    sums_near = core_sums(in_blocks(grad_gu[1], gu_full))
+    sums_own = core_sums(in_blocks(after(grad_gu[0], tuple(sums_near.values())), gu_full))
+    grad_gu = after(grad_gu, tuple(sums_own.values()))
+    gu_part = [
+        sum(in_sum(t, g[:, i * units : (i + 1) * units]) for t, g in zip(tokens, grad_gu))
+        for i in range(2)
+    ]
+    gu_part = [part.astype(BF) for part in gu_part]
+    gu_sum = [far_owners(after(part, down_sum)) for part in gu_part]
+    grad_nffn = scatter_sums(sums_own) + near(scatter_sums(sums_near).astype(BF)).astype(F32)
+    grad_nffn = after(grad_nffn, gu_part)
     ffn_term = grad_nffn * ffn_scale
     ffn_dot = row_total(jnp.sum(ffn_term * resid, axis=-1))[:, None]
     grad_resid = cotangent.astype(F32) + rms_two * ffn_term - resid * rms_two**3 * ffn_dot / D
     ffn_gain_part = jnp.sum(grad_nffn * resid * rms_two, axis=0)
     grad_branch = grad_resid.astype(BF)
-    branch_full = gather_rows(grad_branch)
+    arrived = []
+    branch_full = gather_rows(grad_branch, arrived)
+    hidden = after(hidden, arrived)
+    sums_near = core_sums(out_blocks(hidden[1], down_full))
+    sums_own = core_sums(out_blocks(hidden[0], down_full))
+    down_grad = jnp.concatenate(pair_grad(down_sum, 1), axis=0).astype(F32)
     grad_heads = back_out(branch_full, out_full).astype(BF)
+    grad_heads = after(grad_heads, (sums_near, sums_own, down_grad))
+    ffn_out = scatter_sums(sums_own) + near(scatter_sums(sums_near).astype(BF)).astype(F32)
+    layer_output = (resid + ffn_out).astype(BF)
+    gate_grad = pair_grad(gu_sum[0], 0)
     out_sum = owners(out_part([head_outs], [branch_full]))
     grad_proj = attend_backward(
         queries, keys, values, head_outs, norms, grad_heads, cosine, sine
@@ -436,22 +461,18 @@
         in_part(attn_full, grad_proj[0]),
     ]
     qkv_sum = [owners(part) for part in qkv_part]
+    grad_proj = after(grad_proj, (layer_output, gate_grad))
     grad_nattn = scatter_rows(
         in_blocks(jnp.concatenate(grad_proj, axis=1), jnp.concatenate(qkv_parts, axis=2))
     )
-    hidden = after(hidden, qkv_part)
-    out_near = scatter_rows(out_blocks(hidden[1], down_full))
-    out_own = scatter_rows(out_blocks(hidden[0], down_full))
-    layer_output = (resid + out_own + near(out_near.astype(BF)).astype(F32)).astype(BF)
     attn_term = grad_nattn * attn_scale
     attn_dot = row_total(jnp.sum(attn_term * input_float, axis=-1))[:, None]
     grad_input = grad_resid + rms_one * attn_term - input_float * rms_one**3 * attn_dot / D
     attn_gain_part = jnp.sum(grad_nattn * input_float * rms_one, axis=0)
     gain_grads = total_rows(jnp.stack([attn_gain_part, ffn_gain_part]))
 
-    down_grad = jnp.concatenate(pair_grad(down_sum, 1), axis=0).astype(F32)
-    gu_grad = jnp.concatenate(
-        [v.reshape(v.shape[0], 2, -1) for v in pair_grad(gu_sum, 0)], axis=2
+    gu_grad = jnp.stack(
+        [jnp.concatenate(v, axis=1) for v in (gate_grad, pair_grad(gu_sum[1], 0))], axis=1
     ).astype(F32)
     out_weight_grad = out_grad(out_sum)
     done = (down_grad, out_weight_grad, gu_grad, grad_input, layer_output, gain_grads)

time: 2050 us -> 2090 us (1.020)
  other arithmetic: 121 us -> 154 us
  matrix products: 509 us -> 536 us
    ppermute x148 -> x150, waiting for transfers between devices: 982 us -> 945 us  [swap(): lax.ppermute(values, axis, [(i, i ^ step) for i in range(lax.axis_size(ax...]
    dot_general x48 -> x50, matrix products: 509 us -> 536 us  [mm(): return lax.dot_general(left, right, dims, preferred_element_type=F32)]
    reduce_scatter x2 -> x3, waiting for transfers between devices: 0.01 us -> 25.3 us  [far_owners(): lax.psum_scatter(grad, 'fsdp', scatter_dimension=0, tiled=False, axis_ind...]
    ppermute x148 -> x150, starting transfers between devices: 106 us -> 115 us  [swap(): lax.ppermute(values, axis, [(i, i ^ step) for i in range(lax.axis_size(ax...]
  transfers between devices with their start and end apart: 157 -> 160, of which waited for: 57 -> 59; matrix products, arithmetic and copies ran while one was open for 35% -> 37% of each run, Pallas kernels for 4% -> 4%
where the time goes in v6:
time: 2090 us; the launch traced here: 2080 us
  waiting for transfers between devices  981 us (47%)
  matrix products  536 us (26%)
  local copies, waits for them, and re-layouts  175 us (8%)
  other arithmetic  154 us (7%)
  starting transfers between devices  116 us (6%)
  Pallas kernels  79.2 us (4%)
  blocking collectives  26.3 us (1%)
    ppermute x150, waiting for transfers between devices, swap(): lax.ppermute(values, axis, [(i, i ^ step) for i in range(lax.axis_size(ax...  945 us
    dot_general x50, matrix products, mm(): return lax.dot_general(left, right, dims, preferred_element_type=F32)  536 us
    ppermute x150, starting transfers between devices, swap(): lax.ppermute(values, axis, [(i, i ^ step) for i in range(lax.axis_size(ax...  115 us
    dynamic_update_slice x96, local copies, waits for them, and re-layouts, gather_rows(): full = lax.dynamic_update_slice(full, piece[None], start)  73.7 us
    pallas_call x1, Pallas kernels, attend_backward(): pl.pallas_call(kernel, grid=(heads, blocks), in_specs=[row, col, col, row...  43.9 us
  transfers between devices with their start and end apart: 160, of which 59 were waited for; matrix products, arithmetic and copies ran while one was open for 37% of the time, Pallas kernels for 4%

profile of v6, /device:TPU:0, one launch (start us, length us, event | category | flops | bytes accessed | tf_op | source)
XLA Modules:
  0.0 2084.1 jit_solution(11097641655009500991)
XLA Ops:
  31.1 20.3 collective-permute-done
  58.4 19.6 collective-permute-done.1
  79.9 17.8 collective-permute-done.2
  124.4 16.8 collective-permute-done.14
  150.9 16.3 collective-permute-done.21
  170.3 18.2 collective-permute-done.16
  193.3 19.4 collective-permute-done.23
  232.2 15.0 convolution_bitcast_fusion.2.v_in
  247.3 15.1 convolution_bitcast_fusion.3.k_in
  262.4 12.4 convolution_bitcast_fusion.4.q_in
  274.8 35.3 %shard_map.143 = (bf16[2048,512]{1,0:T(8,128)(2,1)S(1)}, bf16[2048,512]{1,0:T(8,128)(2,1)}, bf16[2048,512]{1,0:T(8,128)(2,1)}, bf16[2048,512]{1,0:T(8,128)(2,1)}, f32[4,1,2048]{2,1,0:T(1,128)S(1)}) custom-call(f32[2048,512]{1,0:T(8,128)} %convolution_bitcast_fusion.4.q_in, f32[2048,512]{1,0:T(8,128)} %convolution_bitcast_fusion.3.k_in, ...), custom_call_target="tpu_custom_call" | custom-call | flops 40265318400 | bytes 20971520 | tf_op jit(solution)/shard_map/pallas_call | solution.py:88
  340.7 52.1 %collective-permute-done.36 = bf16[1024,2,688]{0,2,1:T(8,128)(2,1)} collective-permute-done((bf16[1024,2,688]{0,2,1:T(8,128)(2,1)}, bf16[1024,2,688]{0,2,1:T(8,128)(2,1)}, u32[]{:S(2)}, u32[]{:S(2)}) %collective-permute-start.36) | collective-permute-done | bytes 2818080 | tf_op jit(solution)/shard_map/ppermute | solution.py:191
  406.4 13.1 collective-permute-done.31
  449.4 15.7 collective-permute-done.33
  489.7 18.6 collective-permute-done.38
  515.1 18.2 collective-permute-done.39
  533.4 20.9 %collective-permute-done.40 = bf16[512,1024]{1,0:T(8,128)(2,1)S(1)} collective-permute-done((bf16[512,1024]{1,0:T(8,128)(2,1)}, bf16[512,1024]{1,0:T(8,128)(2,1)S(1)}, u32[]{:S(2)}, u32[]{:S(2)}) %collective-permute-start.40) | collective-permute-done | bytes 1048608 | tf_op jit(solution)/shard_map/ppermute | solution.py:191
  557.5 23.1 %collective-permute-done.46 = bf16[512,1024]{1,0:T(8,128)(2,1)S(1)} collective-permute-done((bf16[512,1024]{1,0:T(8,128)(2,1)}, bf16[512,1024]{1,0:T(8,128)(2,1)S(1)}, u32[]{:S(2)}, u32[]{:S(2)}) %collective-permute-start.46) | collective-permute-done | bytes 1048608 | tf_op jit(solution)/shard_map/ppermute | solution.py:191
  580.6 20.2 collective-permute-done.52
  610.5 19.8 collective-permute-done.53
  634.6 22.2 %collective-permute-done.60 = bf16[512,1024]{1,0:T(8,128)(2,1)S(1)} collective-permute-done((bf16[512,1024]{1,0:T(8,128)(2,1)}, bf16[512,1024]{1,0:T(8,128)(2,1)S(1)}, u32[]{:S(2)}, u32[]{:S(2)}) %collective-permute-start.60) | collective-permute-done | bytes 1048608 | tf_op jit(solution)/shard_map/ppermute | solution.py:191
  658.8 19.8 collective-permute-done.55
  683.1 20.4 collective-permute-done.62
  707.7 83.0 %collective-permute-done.67 = bf16[1024,1024]{1,0:T(8,128)(2,1)S(1)} collective-permute-done((bf16[1024,1024]{1,0:T(8,128)(2,1)S(1)}, bf16[1024,1024]{1,0:T(8,128)(2,1)S(1)}, u32[]{:S(2)}, u32[]{:S(2)}) %collective-permute-start.67) | collective-permute-done | bytes 2097184 | tf_op jit(solution)/shard_map/ppermute | solution.py:191
  795.7 21.9 %collective-permute-done.68 = bf16[512,1024]{1,0:T(8,128)(2,1)} collective-permute-done((bf16[512,1024]{1,0:T(8,128)(2,1)}, bf16[512,1024]{1,0:T(8,128)(2,1)}, u32[]{:S(2)}, u32[]{:S(2)}) %collective-permute-start.68) | collective-permute-done | bytes 1048608 | tf_op jit(solution)/shard_map/ppermute | solution.py:191
  831.4 11.1 collective-permute-done.69
  845.3 18.4 collective-permute-done.70
  889.7 28.0 %convolution_bitcast_fusion = f32[2048,1376]{0,1:T(8,128)S(1)} fusion(bf16[4,2048,1024]{2,1,0:T(8,128)(2,1)} %copy-done.22, bf16[4,1024,1376]{1,2,0:T(8,128)(2,1)} %bitcast.764), kind=kOutput, calls=%fused_computation.9 | convolution fusion | flops 23085449216 | bytes 39321600 | tf_op jit(solution)/shard_map/dot_general | solution.py:21
  941.8 28.5 %convolution_bitcast_fusion.1 = f32[2048,1376]{0,1:T(8,128)} fusion(bf16[4,2048,1024]{2,1,0:T(8,128)(2,1)S(1)} %bitcast.723, bf16[4,1024,1376]{1,2,0:T(8,128)(2,1)} %bitcast.765), kind=kOutput, calls=%fused_computation.10 | convolution fusion | flops 23085449216 | bytes 39321600 | tf_op jit(solution)/shard_map/dot_general | solution.py:21
  1002.8 20.5 fusion.2
  1023.4 12.2 convolution_convert_fusion.9
  1046.4 21.9 %fusion.7 = (bf16[2048,688]{0,1:T(8,128)(2,1)}, bf16[2048,688]{0,1:T(8,128)(2,1)}) fusion(f32[2048,1376]{0,1:T(8,128)} %convolution_bitcast_fusion.1, bf16[4,2048,1024]{2,1,0:T(8,128)(2,1)} %bitcast_dynamic-update-slice_fusion.64, bf16[4,688,1024]{2,1,0:T(8,128)(2,1)} %all-gather.14.cloned.1.call-done), kind=kOutput, calls=%fused_computation.41 | convolution fusion | flops 11561041920 | bytes 39321600 | tf_op jit(solution)/shard_map/dot_general | solution.py:21
  1071.5 12.9 add_convert_fusion.10
  1105.7 11.6 convolution_convert_fusion.7
  1126.4 17.2 collective-permute-done.93
  1150.9 11.2 add_convert_fusion.9
  1162.1 11.2 add_convert_fusion.8
  1173.4 16.3 fusion.52
  1189.6 19.4 add_convert_fusion.1
  1209.1 25.3 %reduce-scatter.7.cloned.1.call-done = bf16[1,2,688,1024]{3,2,1,0:T(8,128)(2,1)} async-done(((bf16[2,2,688,1024]{3,2,1,0:T(8,128)(2,1)}), bf16[1,2,688,1024]{3,2,1,0:T(8,128)(2,1)}) %reduce-scatter.7.cloned.1.call-update) | async-done | bytes 2818064 | tf_op jit(solution)/shard_map/reduce_scatter | solution.py:281
  1246.0 17.8 fusion.49
  1275.9 19.4 add_convert_fusion
  1295.3 18.9 collective-permute-done.88
  1318.2 14.7 collective-permute-done.98
  1368.1 13.5 collective-permute-done.100
  1412.3 12.1 collective-permute-done.119
  1435.4 15.3 collective-permute-done.124
  1450.7 19.6 collective-permute-done.125
  1484.0 13.9 bitcast_convert_fusion.g
  1553.0 43.9 %shard_map.144 = (bf16[2048,512]{1,0:T(8,128)(2,1)S(1)}, bf16[2048,512]{1,0:T(8,128)(2,1)}, bf16[2048,512]{1,0:T(8,128)(2,1)}) custom-call(bf16[2048,512]{1,0:T(8,128)(2,1)} %copy-done.6, bf16[2048,512]{1,0:T(8,128)(2,1)} %get-tuple-element.62.k, bf16[2048,512]{1,0:T(8,128)(2,1)} %get-tuple-element.63.v, bf16[2048,512]{1,0:T(8,128)(2,1)} %get-tuple-element.46.o, ...), custom_call_target="tpu_custom_call" | custom-call | flops 51002736640 | bytes 16777216 | tf_op jit(solution)/shard_map/pallas_call | solution.py:164
  1596.9 23.3 %convolution_convert_fusion = bf16[4,1024,1024]{2,1,0:T(8,128)(2,1)} fusion(bf16[4,2048,1024]{2,1,0:T(8,128)(2,1)} %copy-done.20, bf16[2048,512]{1,0:T(8,128)(2,1)} %get-tuple-element.72, bf16[2048,512]{1,0:T(8,128)(2,1)} %get-tuple-element.71), kind=kOutput, calls=%fused_computation.23 | convolution fusion | flops 17192452096 | bytes 29360128 | tf_op jit(solution)/shard_map/dot_general | solution.py:21
  1638.9 17.4 collective-permute-done.112
  1659.6 19.2 collective-permute-done.104
  1681.9 20.4 collective-permute-done.107
  1707.0 17.8 collective-permute-done.113
  1734.3 12.0 collective-permute-done.102
  1759.5 77.7 %collective-permute-done.132 = bf16[1024,688]{0,1:T(8,128)(2,1)} collective-permute-done((bf16[1024,688]{0,1:T(8,128)(2,1)}, bf16[1024,688]{0,1:T(8,128)(2,1)}, u32[]{:S(2)}, u32[]{:S(2)}) %collective-permute-start.132) | collective-permute-done | bytes 1409056 | tf_op jit(solution)/shard_map/ppermute | solution.py:191
  1855.9 14.1 collective-permute-done.146
  1882.1 12.4 convolution_convert_fusion.1
  1905.2 11.2 convolution_convert_fusion.13
  1921.5 11.7 add_convert_fusion.2
  1964.5 17.8 collective-permute-done.135
  1982.4 23.4 %collective-permute-done.138 = bf16[512,1024]{1,0:T(8,128)(2,1)S(1)} collective-permute-done((bf16[512,1024]{1,0:T(8,128)(2,1)S(1)}, bf16[512,1024]{1,0:T(8,128)(2,1)S(1)}, u32[]{:S(2)}, u32[]{:S(2)}) %collective-permute-start.138) | collective-permute-done | bytes 1048608 | tf_op jit(solution)/shard_map/ppermute | solution.py:191
  2039.6 32.3 %collective-permute-done.148 = bf16[512,512]{1,0:T(8,128)(2,1)S(1)} collective-permute-done((bf16[512,512]{1,0:T(8,128)(2,1)S(1)}, bf16[512,512]{1,0:T(8,128)(2,1)S(1)}, u32[]{:S(2)}, u32[]{:S(2)}) %collective-permute-start.148) | collective-permute-done | bytes 524320 | tf_op jit(solution)/shard_map/ppermute | solution.py:191
  (801 shorter events, 726.3 us)
Async XLA Ops:
  7.2 225.1 %all-gather.10.cloned.1.call-start = ((), (), s32[]{:S(2)}) async-start(), calls=%async_computation.13 | async-start | bytes 15728640 | tf_op jit(solution)/shard_map/all_gather | solution.py:325
  11.2 302.2 %all-gather.12.cloned.1.call-start = ((), (), s32[]{:S(2)}) async-start(), calls=%async_computation.14 | async-start | bytes 5242880 | tf_op jit(solution)/shard_map/all_gather | solution.py:325
  29.5 48.5 %collective-permute-start.1 = (bf16[512,1024]{1,0:T(8,128)(2,1)}, bf16[512,1024]{1,0:T(8,128)(2,1)}, u32[]{:S(2)}, u32[]{:S(2)}) collective-permute-start(bf16[512,1024]{1,0:T(8,128)(2,1)} %get-tuple-element.154), channel_id=1, source_target_pairs={{0,2},{1,3},{2,0},{3,1},{4,6},{5,7},{6,4},{7,5},{8,10},{9,11},{10,... | collective-permute-start | bytes 3145736 | tf_op jit(solution)/shard_map/ppermute | solution.py:191
  31.1 47.4 %collective-permute-start.3 = (bf16[512,1024]{1,0:T(8,128)(2,1)}, bf16[512,1024]{1,0:T(8,128)(2,1)}, u32[]{:S(2)}, u32[]{:S(2)}) collective-permute-start(bf16[512,1024]{1,0:T(8,128)(2,1)} %get-tuple-element.154), channel_id=1, source_target_pairs={{0,1},{1,0},{2,3},{3,2},{4,5},{5,4},{6,7},{7,6},{8,9},{9,8},{10,11... | collective-permute-start | bytes 3145736 | tf_op jit(solution)/shard_map/ppermute | solution.py:191
  51.5 46.2 %collective-permute-start.2 = (bf16[512,1024]{1,0:T(8,128)(2,1)}, bf16[512,1024]{1,0:T(8,128)(2,1)}, u32[]{:S(2)}, u32[]{:S(2)}) collective-permute-start(bf16[512,1024]{1,0:T(8,128)(2,1)} %collective-permute-done), channel_id=1, source_target_pairs={{0,2},{1,3},{2,0},{3,1},{4,6},{5,7},{6,4},{7,5},{8,10},{9,11},{10,... | collective-permute-start | bytes 3145736 | tf_op jit(solution)/shard_map/ppermute | solution.py:191
  55.4 45.0 %collective-permute-start.4 = (bf16[512,1024]{1,0:T(8,128)(2,1)}, bf16[512,1024]{1,0:T(8,128)(2,1)S(1)}, u32[]{:S(2)}, u32[]{:S(2)}) collective-permute-start(bf16[512,1024]{1,0:T(8,128)(2,1)} %collective-permute-done), channel_id=1, source_target_pairs={{0,1},{1,0},{2,3},{3,2},{4,5},{5,4},{6,7},{7,6},{8,9},{9,8},{10,11... | collective-permute-start | bytes 3145736 | tf_op jit(solution)/shard_map/ppermute | solution.py:191
  118.3 771.3 %all-gather.8.cloned.1.call-start = ((), (), s32[]{:S(2)}) async-start(), calls=%async_computation.6 | async-start | bytes 16908288 | tf_op jit(solution)/shard_map/all_gather | solution.py:287
  118.4 49.3 %collective-permute-start.15 = (bf16[512,1024]{1,0:T(8,128)(2,1)}, bf16[512,1024]{1,0:T(8,128)(2,1)S(1)}, u32[]{:S(2)}, u32[]{:S(2)}) collective-permute-start(bf16[512,1024]{1,0:T(8,128)(2,1)} %get-tuple-element.152), channel_id=1, source_target_pairs={{0,2},{1,3},{2,0},{3,1},{4,6},{5,7},{6,4},{7,5},{8,10},{9,11},{10,... | collective-permute-start | bytes 3145736 | tf_op jit(solution)/shard_map/ppermute | solution.py:191
  118.9 50.3 %collective-permute-start.17 = (bf16[512,1024]{1,0:T(8,128)(2,1)}, bf16[512,1024]{1,0:T(8,128)(2,1)S(1)}, u32[]{:S(2)}, u32[]{:S(2)}) collective-permute-start(bf16[512,1024]{1,0:T(8,128)(2,1)} %get-tuple-element.152), channel_id=1, source_target_pairs={{0,1},{1,0},{2,3},{3,2},{4,5},{5,4},{6,7},{7,6},{8,9},{9,8},{10,11... | collective-permute-start | bytes 3145736 | tf_op jit(solution)/shard_map/ppermute | solution.py:191
  118.9 48.3 %collective-permute-start.21 = (bf16[512,1024]{1,0:T(8,128)(2,1)}, bf16[512,1024]{1,0:T(8,128)(2,1)S(1)}, u32[]{:S(2)}, u32[]{:S(2)}) collective-permute-start(bf16[512,1024]{1,0:T(8,128)(2,1)} %get-tuple-element.151), channel_id=1, source_target_pairs={{0,2},{1,3},{2,0},{3,1},{4,6},{5,7},{6,4},{7,5},{8,10},{9,11},{10,... | collective-permute-start | bytes 3145736 | tf_op jit(solution)/shard_map/ppermute | solution.py:191
  141.2 47.3 %collective-permute-start.16 = (bf16[512,1024]{1,0:T(8,128)(2,1)S(1)}, bf16[512,1024]{1,0:T(8,128)(2,1)S(1)}, u32[]{:S(2)}, u32[]{:S(2)}) collective-permute-start(bf16[512,1024]{1,0:T(8,128)(2,1)S(1)} %collective-permute-done.14), channel_id=1, source_target_pairs={{0,2},{1,3},{2,0},{3,1},{4,6},{5,7},{6,4},{7,5},{8,10},{9,11},{10,... | collective-permute-start | bytes 3145736 | tf_op jit(solution)/shard_map/ppermute | solution.py:191
  167.7 45.0 %collective-permute-start.23 = (bf16[512,1024]{1,0:T(8,128)(2,1)S(1)}, bf16[512,1024]{1,0:T(8,128)(2,1)S(1)}, u32[]{:S(2)}, u32[]{:S(2)}) collective-permute-start(bf16[512,1024]{1,0:T(8,128)(2,1)S(1)} %collective-permute-done.21), channel_id=1, source_target_pairs={{0,4},{4,0},{1,5},{5,1},{2,6},{6,2},{3,7},{7,3},{8,12},{12,8},{9,1... | collective-permute-start | bytes 3145736 | tf_op jit(solution)/shard_map/ppermute | solution.py:191
  329.4 63.3 %collective-permute-start.36 = (bf16[1024,2,688]{0,2,1:T(8,128)(2,1)}, bf16[1024,2,688]{0,2,1:T(8,128)(2,1)}, u32[]{:S(2)}, u32[]{:S(2)}) collective-permute-start(bf16[1024,2,688]{0,2,1:T(8,128)(2,1)} %constant_dynamic-slice_fusion.2), channel_id=1, source_target_pairs={{0,8},{8,0},{16,24},{24,16},{1,9},{9,1},{17,25},{25,17},{2,10},{10... | collective-permute-start | bytes 8454152 | tf_op jit(solution)/shard_map/ppermute | solution.py:191
  489.2 513.6 %all-gather.14.cloned.1.call-start = ((), (), s32[]{:S(2)}) async-start(), calls=%async_computation.15 | async-start | bytes 8454144 | tf_op jit(solution)/shard_map/all_gather | solution.py:287
  508.3 46.0 %collective-permute-start.40 = (bf16[512,1024]{1,0:T(8,128)(2,1)}, bf16[512,1024]{1,0:T(8,128)(2,1)S(1)}, u32[]{:S(2)}, u32[]{:S(2)}) collective-permute-start(bf16[512,1024]{1,0:T(8,128)(2,1)} %collective-permute-done.38), channel_id=1, source_target_pairs={{0,2},{1,3},{2,0},{3,1},{4,6},{5,7},{6,4},{7,5},{8,10},{9,11},{10,... | collective-permute-start | bytes 3145736 | tf_op jit(solution)/shard_map/ppermute | solution.py:191
  509.8 91.0 %collective-permute-start.52 = (bf16[1024,1024]{1,0:T(8,128)(2,1)S(1)}, bf16[1024,1024]{1,0:T(8,128)(2,1)S(1)}, u32[]{:S(2)}, u32[]{:S(2)}) collective-permute-start(bf16[1024,1024]{1,0:T(8,128)(2,1)S(1)} %multiply_convert_fusion.2), channel_id=1, source_target_pairs={{0,8},{8,0},{16,24},{24,16},{1,9},{9,1},{17,25},{25,17},{2,10},{10... | collective-permute-start | bytes 6291464 | tf_op jit(solution)/shard_map/ppermute | solution.py:191
  555.0 49.6 %collective-permute-start.47 = (bf16[512,1024]{1,0:T(8,128)(2,1)S(1)}, bf16[512,1024]{1,0:T(8,128)(2,1)S(1)}, u32[]{:S(2)}, u32[]{:S(2)}) collective-permute-start(bf16[512,1024]{1,0:T(8,128)(2,1)S(1)} %collective-permute-done.45), channel_id=1, source_target_pairs={{0,4},{4,0},{1,5},{5,1},{2,6},{6,2},{3,7},{7,3},{8,12},{12,8},{9,1... | collective-permute-start | bytes 3145736 | tf_op jit(solution)/shard_map/ppermute | solution.py:191
  556.7 49.3 %collective-permute-start.44 = (bf16[512,1024]{1,0:T(8,128)(2,1)S(1)}, bf16[512,1024]{1,0:T(8,128)(2,1)}, u32[]{:S(2)}, u32[]{:S(2)}) collective-permute-start(bf16[512,1024]{1,0:T(8,128)(2,1)S(1)} %collective-permute-done.40), channel_id=1, source_target_pairs={{0,1},{1,0},{2,3},{3,2},{4,5},{5,4},{6,7},{7,6},{8,9},{9,8},{10,11... | collective-permute-start | bytes 3145736 | tf_op jit(solution)/shard_map/ppermute | solution.py:191
  556.9 51.2 %collective-permute-start.48 = (bf16[512,1024]{1,0:T(8,128)(2,1)}, bf16[512,1024]{1,0:T(8,128)(2,1)S(1)}, u32[]{:S(2)}, u32[]{:S(2)}) collective-permute-start(bf16[512,1024]{1,0:T(8,128)(2,1)} %get-tuple-element.147), channel_id=1, source_target_pairs={{0,1},{1,0},{2,3},{3,2},{4,5},{5,4},{6,7},{7,6},{8,9},{9,8},{10,11... | collective-permute-start | bytes 3145736 | tf_op jit(solution)/shard_map/ppermute | solution.py:191
  608.9 48.5 %collective-permute-start.56 = (bf16[512,1024]{1,0:T(8,128)(2,1)}, bf16[512,1024]{1,0:T(8,128)(2,1)S(1)}, u32[]{:S(2)}, u32[]{:S(2)}) collective-permute-start(bf16[512,1024]{1,0:T(8,128)(2,1)} %get-tuple-element.146), channel_id=1, source_target_pairs={{0,1},{1,0},{2,3},{3,2},{4,5},{5,4},{6,7},{7,6},{8,9},{9,8},{10,11... | collective-permute-start | bytes 3145736 | tf_op jit(solution)/shard_map/ppermute | solution.py:191
  609.1 47.7 %collective-permute-start.60 = (bf16[512,1024]{1,0:T(8,128)(2,1)}, bf16[512,1024]{1,0:T(8,128)(2,1)S(1)}, u32[]{:S(2)}, u32[]{:S(2)}) collective-permute-start(bf16[512,1024]{1,0:T(8,128)(2,1)} %get-tuple-element.145), channel_id=1, source_target_pairs={{0,2},{1,3},{2,0},{3,1},{4,6},{5,7},{6,4},{7,5},{8,10},{9,11},{10,... | collective-permute-start | bytes 3145736 | tf_op jit(solution)/shard_map/ppermute | solution.py:191
  630.3 48.3 %collective-permute-start.55 = (bf16[512,1024]{1,0:T(8,128)(2,1)S(1)}, bf16[512,1024]{1,0:T(8,128)(2,1)S(1)}, u32[]{:S(2)}, u32[]{:S(2)}) collective-permute-start(bf16[512,1024]{1,0:T(8,128)(2,1)S(1)} %collective-permute-done.53), channel_id=1, source_target_pairs={{0,2},{1,3},{2,0},{3,1},{4,6},{5,7},{6,4},{7,5},{8,10},{9,11},{10,... | collective-permute-start | bytes 3145736 | tf_op jit(solution)/shard_map/ppermute | solution.py:191
  631.2 47.7 %collective-permute-start.57 = (bf16[512,1024]{1,0:T(8,128)(2,1)S(1)}, bf16[512,1024]{1,0:T(8,128)(2,1)S(1)}, u32[]{:S(2)}, u32[]{:S(2)}) collective-permute-start(bf16[512,1024]{1,0:T(8,128)(2,1)S(1)} %collective-permute-done.53), channel_id=1, source_target_pairs={{0,1},{1,0},{2,3},{3,2},{4,5},{5,4},{6,7},{7,6},{8,9},{9,8},{10,11... | collective-permute-start | bytes 3145736 | tf_op jit(solution)/shard_map/ppermute | solution.py:191
  634.3 45.2 %collective-permute-start.58 = (bf16[512,1024]{1,0:T(8,128)(2,1)S(1)}, bf16[512,1024]{1,0:T(8,128)(2,1)S(1)}, u32[]{:S(2)}, u32[]{:S(2)}) collective-permute-start(bf16[512,1024]{1,0:T(8,128)(2,1)S(1)} %collective-permute-done.54), channel_id=1, source_target_pairs={{0,1},{1,0},{2,3},{3,2},{4,5},{5,4},{6,7},{7,6},{8,9},{9,8},{10,11... | collective-permute-start | bytes 3145736 | tf_op jit(solution)/shard_map/ppermute | solution.py:191
  657.4 46.1 %collective-permute-start.62 = (bf16[512,1024]{1,0:T(8,128)(2,1)S(1)}, bf16[512,1024]{1,0:T(8,128)(2,1)S(1)}, u32[]{:S(2)}, u32[]{:S(2)}) collective-permute-start(bf16[512,1024]{1,0:T(8,128)(2,1)S(1)} %collective-permute-done.60), channel_id=1, source_target_pairs={{0,4},{4,0},{1,5},{5,1},{2,6},{6,2},{3,7},{7,3},{8,12},{12,8},{9,1... | collective-permute-start | bytes 3145736 | tf_op jit(solution)/shard_map/ppermute | solution.py:191
  679.6 111.1 %collective-permute-start.67 = (bf16[1024,1024]{1,0:T(8,128)(2,1)S(1)}, bf16[1024,1024]{1,0:T(8,128)(2,1)S(1)}, u32[]{:S(2)}, u32[]{:S(2)}) collective-permute-start(bf16[1024,1024]{1,0:T(8,128)(2,1)S(1)} %copy-done.12), channel_id=1, source_target_pairs={{0,8},{8,0},{16,24},{24,16},{1,9},{9,1},{17,25},{25,17},{2,10},{10... | collective-permute-start | bytes 6291464 | tf_op jit(solution)/shard_map/ppermute | solution.py:191
  795.1 47.4 %collective-permute-start.69 = (bf16[512,1024]{1,0:T(8,128)(2,1)}, bf16[512,1024]{1,0:T(8,128)(2,1)}, u32[]{:S(2)}, u32[]{:S(2)}) collective-permute-start(bf16[512,1024]{1,0:T(8,128)(2,1)} %get-tuple-element.144), channel_id=1, source_target_pairs={{0,2},{1,3},{2,0},{3,1},{4,6},{5,7},{6,4},{7,5},{8,10},{9,11},{10,... | collective-permute-start | bytes 3145736 | tf_op jit(solution)/shard_map/ppermute | solution.py:191
  795.7 47.4 %collective-permute-start.71 = (bf16[512,1024]{1,0:T(8,128)(2,1)}, bf16[512,1024]{1,0:T(8,128)(2,1)}, u32[]{:S(2)}, u32[]{:S(2)}) collective-permute-start(bf16[512,1024]{1,0:T(8,128)(2,1)} %get-tuple-element.144), channel_id=1, source_target_pairs={{0,1},{1,0},{2,3},{3,2},{4,5},{5,4},{6,7},{7,6},{8,9},{9,8},{10,11... | collective-permute-start | bytes 3145736 | tf_op jit(solution)/shard_map/ppermute | solution.py:191
  817.6 46.1 %collective-permute-start.70 = (bf16[512,1024]{1,0:T(8,128)(2,1)}, bf16[512,1024]{1,0:T(8,128)(2,1)}, u32[]{:S(2)}, u32[]{:S(2)}) collective-permute-start(bf16[512,1024]{1,0:T(8,128)(2,1)} %collective-permute-done.68), channel_id=1, source_target_pairs={{0,2},{1,3},{2,0},{3,1},{4,6},{5,7},{6,4},{7,5},{8,10},{9,11},{10,... | collective-permute-start | bytes 3145736 | tf_op jit(solution)/shard_map/ppermute | solution.py:191
  819.1 415.3 %reduce-scatter.7.cloned.1.call-start = ((), (), s32[]{:S(2)}) async-start(), calls=%async_computation.7 | async-start | bytes 8454144 | tf_op jit(solution)/shard_map/reduce_scatter | solution.py:281
  1105.6 626.1 %reduce-scatter.9.cloned.1.call-start = ((), (), s32[]{:S(2)}) async-start(), calls=%async_computation.8 | async-start | bytes 8454144 | tf_op jit(solution)/shard_map/reduce_scatter | solution.py:281
  1123.9 113.5 %collective-permute-start.95 = (bf16[512,1024]{1,0:T(8,128)(2,1)S(1)}, bf16[512,1024]{1,0:T(8,128)(2,1)}, u32[]{:S(2)}, u32[]{:S(2)}) collective-permute-start(bf16[512,1024]{1,0:T(8,128)(2,1)S(1)} %get-tuple-element.139), channel_id=1, source_target_pairs={{0,2},{1,3},{2,0},{3,1},{4,6},{5,7},{6,4},{7,5},{8,10},{9,11},{10,... | collective-permute-start | bytes 3145736 | tf_op jit(solution)/shard_map/ppermute | solution.py:191
  1143.6 91.3 %collective-permute-start.92 = (bf16[512,1024]{1,0:T(8,128)(2,1)}, bf16[512,1024]{1,0:T(8,128)(2,1)}, u32[]{:S(2)}, u32[]{:S(2)}) collective-permute-start(bf16[512,1024]{1,0:T(8,128)(2,1)} %dynamic-slice_bitcast_fusion.19), channel_id=1, source_target_pairs={{0,4},{4,0},{1,5},{5,1},{2,6},{6,2},{3,7},{7,3},{8,12},{12,8},{9,1... | collective-permute-start | bytes 3145736 | tf_op jit(solution)/shard_map/ppermute | solution.py:191
  1147.3 87.6 %collective-permute-start.94 = (bf16[512,1024]{1,0:T(8,128)(2,1)}, bf16[512,1024]{1,0:T(8,128)(2,1)}, u32[]{:S(2)}, u32[]{:S(2)}) collective-permute-start(bf16[512,1024]{1,0:T(8,128)(2,1)} %fusion.104), channel_id=1, source_target_pairs={{0,2},{1,3},{2,0},{3,1},{4,6},{5,7},{6,4},{7,5},{8,10},{9,11},{10,... | collective-permute-start | bytes 3145736 | tf_op jit(solution)/shard_map/ppermute | solution.py:191
  1150.1 87.3 %collective-permute-start.97 = (bf16[512,1024]{1,0:T(8,128)(2,1)}, bf16[512,1024]{1,0:T(8,128)(2,1)}, u32[]{:S(2)}, u32[]{:S(2)}) collective-permute-start(bf16[512,1024]{1,0:T(8,128)(2,1)} %fusion.101), channel_id=1, source_target_pairs={{0,4},{4,0},{1,5},{5,1},{2,6},{6,2},{3,7},{7,3},{8,12},{12,8},{9,1... | collective-permute-start | bytes 3145736 | tf_op jit(solution)/shard_map/ppermute | solution.py:191
  1234.4 523.6 %reduce-scatter.15.cloned.1.call-start = ((), (), s32[]{:S(2)}) async-start(), calls=%async_computation.11 | async-start | bytes 8454144 | tf_op jit(solution)/shard_map/reduce_scatter | solution.py:281
  1241.3 91.5 %collective-permute-start.98 = (bf16[1024,1024]{1,0:T(8,128)(2,1)}, bf16[1024,1024]{1,0:T(8,128)(2,1)S(1)}, u32[]{:S(2)}, u32[]{:S(2)}) collective-permute-start(bf16[1024,1024]{1,0:T(8,128)(2,1)} %pad_maximum_fusion.9), channel_id=1, source_target_pairs={{0,8},{8,0},{16,24},{24,16},{1,9},{9,1},{17,25},{25,17},{2,10},{10... | collective-permute-start | bytes 6291464 | tf_op jit(solution)/shard_map/ppermute | solution.py:191
  1266.0 50.4 %collective-permute-start.89 = (bf16[512,1024]{1,0:T(8,128)(2,1)S(1)}, bf16[512,1024]{1,0:T(8,128)(2,1)}, u32[]{:S(2)}, u32[]{:S(2)}) collective-permute-start(bf16[512,1024]{1,0:T(8,128)(2,1)S(1)} %get-tuple-element.141), channel_id=1, source_target_pairs={{0,2},{1,3},{2,0},{3,1},{4,6},{5,7},{6,4},{7,5},{8,10},{9,11},{10,... | collective-permute-start | bytes 3145736 | tf_op jit(solution)/shard_map/ppermute | solution.py:191
  1357.8 49.6 %collective-permute-start.118 = (bf16[512,1024]{1,0:T(8,128)(2,1)}, bf16[512,1024]{1,0:T(8,128)(2,1)}, u32[]{:S(2)}, u32[]{:S(2)}) collective-permute-start(bf16[512,1024]{1,0:T(8,128)(2,1)} %get-tuple-element.138), channel_id=1, source_target_pairs={{0,2},{1,3},{2,0},{3,1},{4,6},{5,7},{6,4},{7,5},{8,10},{9,11},{10,... | collective-permute-start | bytes 3145736 | tf_op jit(solution)/shard_map/ppermute | solution.py:191
  1358.8 68.3 %collective-permute-start.120 = (bf16[512,1024]{1,0:T(8,128)(2,1)}, bf16[512,1024]{1,0:T(8,128)(2,1)}, u32[]{:S(2)}, u32[]{:S(2)}) collective-permute-start(bf16[512,1024]{1,0:T(8,128)(2,1)} %get-tuple-element.138), channel_id=1, source_target_pairs={{0,1},{1,0},{2,3},{3,2},{4,5},{5,4},{6,7},{7,6},{8,9},{9,8},{10,11... | collective-permute-start | bytes 3145736 | tf_op jit(solution)/shard_map/ppermute | solution.py:191
  1366.1 66.4 %collective-permute-start.130 = (bf16[688,1024]{1,0:T(8,128)(2,1)S(1)}, bf16[688,1024]{1,0:T(8,128)(2,1)}, u32[]{:S(2)}, u32[]{:S(2)}) collective-permute-start(bf16[688,1024]{1,0:T(8,128)(2,1)S(1)} %dynamic-slice_bitcast_fusion.3), channel_id=1, source_target_pairs={{0,8},{8,0},{16,24},{24,16},{1,9},{9,1},{17,25},{25,17},{2,10},{10... | collective-permute-start | bytes 4227080 | tf_op jit(solution)/shard_map/ppermute | solution.py:191
  1368.1 485.1 %reduce-scatter.13.cloned.1.call-start = ((), (), s32[]{:S(2)}) async-start(), calls=%async_computation.10 | async-start | bytes 5242880 | tf_op jit(solution)/shard_map/reduce_scatter | solution.py:271
  1430.8 46.6 %collective-permute-start.126 = (bf16[512,1024]{1,0:T(8,128)(2,1)}, bf16[512,1024]{1,0:T(8,128)(2,1)S(1)}, u32[]{:S(2)}, u32[]{:S(2)}) collective-permute-start(bf16[512,1024]{1,0:T(8,128)(2,1)} %get-tuple-element.137), channel_id=1, source_target_pairs={{0,1},{1,0},{2,3},{3,2},{4,5},{5,4},{6,7},{7,6},{8,9},{9,8},{10,11... | collective-permute-start | bytes 3145736 | tf_op jit(solution)/shard_map/ppermute | solution.py:191
  1432.5 92.9 %collective-permute-start.109 = (bf16[2048,1024]{1,0:T(8,128)(2,1)}, bf16[2048,1024]{1,0:T(8,128)(2,1)}, u32[]{:S(2)}, u32[]{:S(2)}) collective-permute-start(bf16[2048,1024]{1,0:T(8,128)(2,1)} %convolution_convert_fusion.4), channel_id=1, source_target_pairs={{0,1},{1,0},{2,3},{3,2},{4,5},{5,4},{6,7},{7,6},{8,9},{9,8},{10,11... | collective-permute-start | bytes 12582920 | tf_op jit(solution)/shard_map/ppermute | solution.py:191
  1477.4 55.2 %collective-permute-start.111 = (bf16[2048,1024]{1,0:T(8,128)(2,1)}, bf16[2048,1024]{1,0:T(8,128)(2,1)}, u32[]{:S(2)}, u32[]{:S(2)}) collective-permute-start(bf16[2048,1024]{1,0:T(8,128)(2,1)} %convolution_convert_fusion.3), channel_id=1, source_target_pairs={{0,1},{1,0},{2,3},{3,2},{4,5},{5,4},{6,7},{7,6},{8,9},{9,8},{10,11... | collective-permute-start | bytes 12582920 | tf_op jit(solution)/shard_map/ppermute | solution.py:191
  1478.5 61.0 %collective-permute-start.101 = (bf16[2048,1024]{1,0:T(8,128)(2,1)}, bf16[2048,1024]{1,0:T(8,128)(2,1)}, u32[]{:S(2)}, u32[]{:S(2)}) collective-permute-start(bf16[2048,1024]{1,0:T(8,128)(2,1)} %convolution_convert_fusion.6), channel_id=1, source_target_pairs={{0,1},{1,0},{2,3},{3,2},{4,5},{5,4},{6,7},{7,6},{8,9},{9,8},{10,11... | collective-permute-start | bytes 12582920 | tf_op jit(solution)/shard_map/ppermute | solution.py:191
  1480.1 66.1 %collective-permute-start.103 = (bf16[2048,1024]{1,0:T(8,128)(2,1)}, bf16[2048,1024]{1,0:T(8,128)(2,1)}, u32[]{:S(2)}, u32[]{:S(2)}) collective-permute-start(bf16[2048,1024]{1,0:T(8,128)(2,1)} %convolution_convert_fusion.5), channel_id=1, source_target_pairs={{0,1},{1,0},{2,3},{3,2},{4,5},{5,4},{6,7},{7,6},{8,9},{9,8},{10,11... | collective-permute-start | bytes 12582920 | tf_op jit(solution)/shard_map/ppermute | solution.py:191
  1518.4 515.0 %reduce-scatter.17.cloned.1.call-start = ((), (), s32[]{:S(2)}) async-start(), calls=%async_computation.12 | async-start | bytes 10485760 | tf_op jit(solution)/shard_map/reduce_scatter | solution.py:271
  1620.2 416.0 %reduce-scatter.11.cloned.1.call-start = ((), (), s32[]{:S(2)}) async-start(), calls=%async_computation.9 | async-start | bytes 5242880 | tf_op jit(solution)/shard_map/reduce_scatter | solution.py:271
  1633.7 45.1 %collective-permute-start.104 = (bf16[512,1024]{1,0:T(8,128)(2,1)S(1)}, bf16[512,1024]{1,0:T(8,128)(2,1)S(1)}, u32[]{:S(2)}, u32[]{:S(2)}) collective-permute-start(bf16[512,1024]{1,0:T(8,128)(2,1)S(1)} %dynamic-slice_bitcast_fusion.14), channel_id=1, source_target_pairs={{0,4},{4,0},{1,5},{5,1},{2,6},{6,2},{3,7},{7,3},{8,12},{12,8},{9,1... | collective-permute-start | bytes 3145736 | tf_op jit(solution)/shard_map/ppermute | solution.py:191
  1636.0 68.9 %collective-permute-start.110 = (bf16[512,1024]{1,0:T(8,128)(2,1)S(1)}, bf16[512,1024]{1,0:T(8,128)(2,1)S(1)}, u32[]{:S(2)}, u32[]{:S(2)}) collective-permute-start(bf16[512,1024]{1,0:T(8,128)(2,1)S(1)} %dynamic-slice_bitcast_fusion.11), channel_id=1, source_target_pairs={{0,4},{4,0},{1,5},{5,1},{2,6},{6,2},{3,7},{7,3},{8,12},{12,8},{9,1... | collective-permute-start | bytes 3145736 | tf_op jit(solution)/shard_map/ppermute | solution.py:191
  1637.5 89.8 %collective-permute-start.114 = (bf16[512,1024]{1,0:T(8,128)(2,1)S(1)}, bf16[512,1024]{1,0:T(8,128)(2,1)S(1)}, u32[]{:S(2)}, u32[]{:S(2)}) collective-permute-start(bf16[512,1024]{1,0:T(8,128)(2,1)S(1)} %get-tuple-element.133), channel_id=1, source_target_pairs={{0,2},{1,3},{2,0},{3,1},{4,6},{5,7},{6,4},{7,5},{8,10},{9,11},{10,... | collective-permute-start | bytes 3145736 | tf_op jit(solution)/shard_map/ppermute | solution.py:191
  1656.4 46.0 %collective-permute-start.107 = (bf16[512,1024]{1,0:T(8,128)(2,1)S(1)}, bf16[512,1024]{1,0:T(8,128)(2,1)S(1)}, u32[]{:S(2)}, u32[]{:S(2)}) collective-permute-start(bf16[512,1024]{1,0:T(8,128)(2,1)S(1)} %get-tuple-element.136), channel_id=1, source_target_pairs={{0,2},{1,3},{2,0},{3,1},{4,6},{5,7},{6,4},{7,5},{8,10},{9,11},{10,... | collective-permute-start | bytes 3145736 | tf_op jit(solution)/shard_map/ppermute | solution.py:191
  1658.8 66.0 %collective-permute-start.113 = (bf16[512,1024]{1,0:T(8,128)(2,1)S(1)}, bf16[512,1024]{1,0:T(8,128)(2,1)S(1)}, u32[]{:S(2)}, u32[]{:S(2)}) collective-permute-start(bf16[512,1024]{1,0:T(8,128)(2,1)S(1)} %fusion.94), channel_id=1, source_target_pairs={{0,2},{1,3},{2,0},{3,1},{4,6},{5,7},{6,4},{7,5},{8,10},{9,11},{10,... | collective-permute-start | bytes 3145736 | tf_op jit(solution)/shard_map/ppermute | solution.py:191
  1678.8 50.0 %collective-permute-start.116 = (bf16[512,1024]{1,0:T(8,128)(2,1)S(1)}, bf16[512,1024]{1,0:T(8,128)(2,1)S(1)}, u32[]{:S(2)}, u32[]{:S(2)}) collective-permute-start(bf16[512,1024]{1,0:T(8,128)(2,1)S(1)} %fusion.91), channel_id=1, source_target_pairs={{0,4},{4,0},{1,5},{5,1},{2,6},{6,2},{3,7},{7,3},{8,12},{12,8},{9,1... | collective-permute-start | bytes 3145736 | tf_op jit(solution)/shard_map/ppermute | solution.py:191
  1704.9 140.5 %collective-permute-start.106 = (bf16[512,1024]{1,0:T(8,128)(2,1)}, bf16[512,1024]{1,0:T(8,128)(2,1)}, u32[]{:S(2)}, u32[]{:S(2)}) collective-permute-start(bf16[512,1024]{1,0:T(8,128)(2,1)} %get-tuple-element.135), channel_id=1, source_target_pairs={{0,2},{1,3},{2,0},{3,1},{4,6},{5,7},{6,4},{7,5},{8,10},{9,11},{10,... | collective-permute-start | bytes 3145736 | tf_op jit(solution)/shard_map/ppermute | solution.py:191
  1724.8 116.8 %collective-permute-start.105 = (bf16[512,1024]{1,0:T(8,128)(2,1)}, bf16[512,1024]{1,0:T(8,128)(2,1)}, u32[]{:S(2)}, u32[]{:S(2)}) collective-permute-start(bf16[512,1024]{1,0:T(8,128)(2,1)} %fusion.99), channel_id=1, source_target_pairs={{0,2},{1,3},{2,0},{3,1},{4,6},{5,7},{6,4},{7,5},{8,10},{9,11},{10,... | collective-permute-start | bytes 3145736 | tf_op jit(solution)/shard_map/ppermute | solution.py:191
  1727.3 118.2 %collective-permute-start.108 = (bf16[512,1024]{1,0:T(8,128)(2,1)}, bf16[512,1024]{1,0:T(8,128)(2,1)}, u32[]{:S(2)}, u32[]{:S(2)}) collective-permute-start(bf16[512,1024]{1,0:T(8,128)(2,1)} %fusion.97), channel_id=1, source_target_pairs={{0,4},{4,0},{1,5},{5,1},{2,6},{6,2},{3,7},{7,3},{8,12},{12,8},{9,1... | collective-permute-start | bytes 3145736 | tf_op jit(solution)/shard_map/ppermute | solution.py:191
  1730.9 116.7 %collective-permute-start.117 = (bf16[1024,1024]{1,0:T(8,128)(2,1)}, bf16[1024,1024]{1,0:T(8,128)(2,1)}, u32[]{:S(2)}, u32[]{:S(2)}) collective-permute-start(bf16[1024,1024]{1,0:T(8,128)(2,1)} %pad_maximum_fusion.10), channel_id=1, source_target_pairs={{0,8},{8,0},{16,24},{24,16},{1,9},{9,1},{17,25},{25,17},{2,10},{10... | collective-permute-start | bytes 6291464 | tf_op jit(solution)/shard_map/ppermute | solution.py:191
  1746.3 90.9 %collective-permute-start.132 = (bf16[1024,688]{0,1:T(8,128)(2,1)}, bf16[1024,688]{0,1:T(8,128)(2,1)}, u32[]{:S(2)}, u32[]{:S(2)}) collective-permute-start(bf16[1024,688]{0,1:T(8,128)(2,1)} %dynamic-slice_bitcast_fusion.2), channel_id=1, source_target_pairs={{0,8},{8,0},{16,24},{24,16},{1,9},{9,1},{17,25},{25,17},{2,10},{10... | collective-permute-start | bytes 4227080 | tf_op jit(solution)/shard_map/ppermute | solution.py:191
  1855.0 61.4 %collective-permute-start.145 = (bf16[512,512]{1,0:T(8,128)(2,1)}, bf16[512,512]{1,0:T(8,128)(2,1)}, u32[]{:S(2)}, u32[]{:S(2)}) collective-permute-start(bf16[512,512]{1,0:T(8,128)(2,1)} %dynamic-slice_bitcast_fusion.28), channel_id=1, source_target_pairs={{0,4},{4,0},{1,5},{5,1},{2,6},{6,2},{3,7},{7,3},{8,12},{12,8},{9,1... | collective-permute-start | bytes 1572872 | tf_op jit(solution)/shard_map/ppermute | solution.py:191
  1874.3 45.2 %collective-permute-start.147 = (bf16[2,512,688]{1,2,0:T(8,128)(2,1)}, bf16[2,512,688]{1,2,0:T(8,128)(2,1)}, u32[]{:S(2)}, u32[]{:S(2)}) collective-permute-start(bf16[2,512,688]{1,2,0:T(8,128)(2,1)} %fusion.124), channel_id=1, source_target_pairs={{0,4},{4,0},{1,5},{5,1},{2,6},{6,2},{3,7},{7,3},{8,12},{12,8},{9,1... | collective-permute-start | bytes 4227080 | tf_op jit(solution)/shard_map/ppermute | solution.py:191
  1948.2 58.2 %collective-permute-start.139 = (bf16[512,1024]{1,0:T(8,128)(2,1)S(1)}, bf16[512,1024]{1,0:T(8,128)(2,1)S(1)}, u32[]{:S(2)}, u32[]{:S(2)}) collective-permute-start(bf16[512,1024]{1,0:T(8,128)(2,1)S(1)} %get-tuple-element.131), channel_id=1, source_target_pairs={{0,2},{1,3},{2,0},{3,1},{4,6},{5,7},{6,4},{7,5},{8,10},{9,11},{10,... | collective-permute-start | bytes 3145736 | tf_op jit(solution)/shard_map/ppermute | solution.py:191
  1960.3 45.4 %collective-permute-start.138 = (bf16[512,1024]{1,0:T(8,128)(2,1)S(1)}, bf16[512,1024]{1,0:T(8,128)(2,1)S(1)}, u32[]{:S(2)}, u32[]{:S(2)}) collective-permute-start(bf16[512,1024]{1,0:T(8,128)(2,1)S(1)} %fusion.89), channel_id=1, source_target_pairs={{0,2},{1,3},{2,0},{3,1},{4,6},{5,7},{6,4},{7,5},{8,10},{9,11},{10,... | collective-permute-start | bytes 3145736 | tf_op jit(solution)/shard_map/ppermute | solution.py:191
  (212 other events, 4726.2 us)
Sparse Core Ops, SparseCore 0:
  11.3 220.8 all-gather.9
  234.4 78.9 all-gather.11
  489.4 256.6 all-gather.7
  819.2 132.3 all-gather.13
  1105.7 128.6 reduce-scatter.6
  1236.7 130.3 reduce-scatter.8
  1369.9 130.2 reduce-scatter.14
  1518.5 75.6 reduce-scatter.12
  1620.3 172.1 reduce-scatter.16
  1916.6 77.8 reduce-scatter.10

commit v7 on v2

--- a/solution.py
+++ b/solution.py
@@ -288,7 +288,8 @@
 ):
     n_f = lax.axis_size("fsdp")
     d_f = D // n_f
-    qkv_parts = [spread(ctx_half(qkv_weight[:, i], 1)) for i in range(3)]
+    qkv_full = spread(ctx_half(jnp.swapaxes(qkv_weight, 0, 1), 2))
+    qkv_parts = [qkv_full[:, i] for i in range(3)]
     out_full = spread(ctx_half(out_weight, 0))
     gu_full = spread(ctx_half(gate_up_weight, 2).reshape(d_f, -1))
     down_full = spread(ctx_half(down_weight, 0))
@@ -358,7 +359,10 @@
     grad_proj = attend_backward(
         queries, keys, values, head_outs, norms, grad_heads, cosine, sine
     )
-    qkv_part = [in_part(attn_full, grad) for grad in grad_proj]
+    qkv_part = [
+        in_part(attn_full, jnp.concatenate(grad_proj[1:], axis=1)),
+        in_part(attn_full, grad_proj[0]),
+    ]
     qkv_sum = [owners(part) for part in qkv_part]
     grad_nattn = scatter_rows(
         in_blocks(jnp.concatenate(grad_proj, axis=1), jnp.concatenate(qkv_parts, axis=2))
@@ -380,9 +384,13 @@
     done = (down_grad, out_weight_grad, gu_grad, grad_input, layer_output, gain_grads)
     qkv_grad = []
     for part in qkv_sum:
-        qkv_grad.append(jnp.concatenate(trade_ctx(after(part, done), 0), axis=1).astype(F32))
+        first, second = trade_ctx(after(part, done), 0)
+        wide = queries.shape[1]
+        for i in range(0, first.shape[1], wide):
+            both = [first[:, i : i + wide], second[:, i : i + wide]]
+            qkv_grad.append(jnp.concatenate(both, axis=1).astype(F32))
         done = done + (qkv_grad[-1],)
-    qkv_grad = jnp.stack(qkv_grad, axis=1)
+    qkv_grad = jnp.stack([qkv_grad[2], qkv_grad[0], qkv_grad[1]], axis=1)
 
     return (
         layer_output,

time: 1840 us -> 1810 us (0.984)
    all_gather x6 -> x4, waiting for transfers between devices: 294 us -> 276 us  [spread(): return lax.all_gather(weight, 'fsdp', axis=0, tiled=False)]
    dot_general x34 -> x33, matrix products: 472 us -> 458 us  [mm(): return lax.dot_general(left, right, dims, preferred_element_type=F32)]
    reduce_scatter x6 -> x5, waiting for transfers between devices: 116 us -> 123 us  [owners(): return lax.psum_scatter(grad, 'fsdp', scatter_dimension=0, tiled=False)]
    ppermute x97 -> x96, starting transfers between devices: 78.5 us -> 77.1 us  [swap(): lax.ppermute(values, axis, [(i, i ^ step) for i in range(lax.axis_size(ax...]
    ppermute x97 -> x96, waiting for transfers between devices: 477 us -> 476 us  [swap(): lax.ppermute(values, axis, [(i, i ^ step) for i in range(lax.axis_size(ax...]
  transfers between devices with their start and end apart: 109 -> 105, of which waited for: 40 -> 38; matrix products, arithmetic and copies ran while one was open for 38% -> 38% of each run, Pallas kernels for 4% -> 4%
where the time goes in v7:
time: 1810 us; the launch traced here: 1800 us
  waiting for transfers between devices  875 us (48%)
  matrix products  458 us (25%)
  local copies, waits for them, and re-layouts  139 us (8%)
  other arithmetic  98.5 us (5%)
  Pallas kernels  79 us (4%)
  starting transfers between devices  77.4 us (4%)
  blocking collectives  52.9 us (3%)
    ppermute x96, waiting for transfers between devices, swap(): lax.ppermute(values, axis, [(i, i ^ step) for i in range(lax.axis_size(ax...  476 us
    dot_general x33, matrix products, mm(): return lax.dot_general(left, right, dims, preferred_element_type=F32)  458 us
    all_gather x4, waiting for transfers between devices, spread(): return lax.all_gather(weight, 'fsdp', axis=0, tiled=False)  276 us
    reduce_scatter x5, waiting for transfers between devices, owners(): return lax.psum_scatter(grad, 'fsdp', scatter_dimension=0, tiled=False)  123 us
    ppermute x96, starting transfers between devices, swap(): lax.ppermute(values, axis, [(i, i ^ step) for i in range(lax.axis_size(ax...  77.1 us
    dynamic_update_slice x64, local copies, waits for them, and re-layouts, gather_rows(): full = lax.dynamic_update_slice(full, piece[None], start)  69.8 us
    psum x4, blocking collectives, row_total(): return lax.psum(values, 'tp')  52.9 us
    pallas_call x1, Pallas kernels, attend_backward(): pl.pallas_call(kernel, grid=(heads, blocks), in_specs=[row, col, col, row...  43.9 us
  transfers between devices with their start and end apart: 105, of which 38 were waited for; matrix products, arithmetic and copies ran while one was open for 38% of the time, Pallas kernels for 4%

profile of v7, /device:TPU:0, one launch (start us, length us, event | category | flops | bytes accessed | tf_op | source)
XLA Modules:
  0.0 1795.4 jit_solution(5993964152854521709)
XLA Ops:
  20.2 8.1 psum.28
  40.6 16.0 collective-permute-done
  70.6 12.0 collective-permute-done.7
  85.5 17.3 collective-permute-done.2
  108.2 8.5 collective-permute-done.9
  128.5 103.7 %all-gather.10.cloned.1.call-done = bf16[12,1024,512]{2,1,0:T(8,128)(2,1)} async-done(((bf16[3,1024,512]{2,1,0:T(8,128)(2,1)}), bf16[12,1024,512]{2,1,0:T(8,128)(2,1)}) %all-gather.10.cloned.1.call-update) | async-done | bytes 12582928 | tf_op jit(solution)/shard_map/all_gather | solution.py:263
  232.2 15.0 convolution_bitcast_fusion.1.v_in
  247.2 13.7 convolution_bitcast_fusion.2.k_in
  260.9 13.9 convolution_bitcast_fusion.3.q_in
  274.8 35.1 %shard_map.143 = (bf16[2048,512]{1,0:T(8,128)(2,1)S(1)}, bf16[2048,512]{1,0:T(8,128)(2,1)}, bf16[2048,512]{1,0:T(8,128)(2,1)}, bf16[2048,512]{1,0:T(8,128)(2,1)}, f32[4,1,2048]{2,1,0:T(1,128)S(1)}) custom-call(f32[2048,512]{1,0:T(8,128)} %convolution_bitcast_fusion.3.q_in, f32[2048,512]{1,0:T(8,128)} %convolution_bitcast_fusion.2.k_in, ...), custom_call_target="tpu_custom_call" | custom-call | flops 5368709120 | bytes 20971520 | tf_op jit(solution)/shard_map/pallas_call | solution.py:88
  312.8 6.4 convolution_convert_fusion.6
  330.0 16.5 collective-permute-done.36
  350.1 6.4 broadcast.35.clone.2
  360.9 12.0 collective-permute-done.38
  381.7 12.5 collective-permute-done.43
  412.6 52.8 %collective-permute-done.17 = bf16[512,1024]{1,0:T(8,128)(2,1)S(1)} collective-permute-done((bf16[512,1024]{1,0:T(8,128)(2,1)S(1)}, bf16[512,1024]{1,0:T(8,128)(2,1)S(1)}, u32[]{:S(2)}, u32[]{:S(2)}) %collective-permute-start.17) | collective-permute-done | bytes 1048608 | tf_op jit(solution)/shard_map/ppermute | solution.py:191
  475.5 12.3 collective-permute-done.15
  487.9 20.9 %collective-permute-done.18 = bf16[512,1024]{1,0:T(8,128)(2,1)S(1)} collective-permute-done((bf16[512,1024]{1,0:T(8,128)(2,1)S(1)}, bf16[512,1024]{1,0:T(8,128)(2,1)S(1)}, u32[]{:S(2)}, u32[]{:S(2)}) %collective-permute-start.18) | collective-permute-done | bytes 1048608 | tf_op jit(solution)/shard_map/ppermute | solution.py:191
  513.1 7.6 psum.29
  535.6 12.0 collective-permute-done.22
  550.2 6.5 broadcast.35.clone.1
  560.5 20.5 %collective-permute-done.29 = bf16[512,1024]{1,0:T(8,128)(2,1)S(1)} collective-permute-done((bf16[512,1024]{1,0:T(8,128)(2,1)S(1)}, bf16[512,1024]{1,0:T(8,128)(2,1)S(1)}, u32[]{:S(2)}, u32[]{:S(2)}) %collective-permute-start.29) | collective-permute-done | bytes 1048608 | tf_op jit(solution)/shard_map/ppermute | solution.py:191
  582.7 17.9 collective-permute-done.24
  617.6 78.4 %all-gather.8.cloned.1.call-done = bf16[4,1024,2752]{1,2,0:T(8,128)(2,1)} async-done(((bf16[1,1024,2752]{1,2,0:T(8,128)(2,1)}), bf16[4,1024,2752]{1,2,0:T(8,128)(2,1)}) %all-gather.8.cloned.1.call-update) | async-done | bytes 22544400 | tf_op jit(solution)/shard_map/all_gather | solution.py:263
  696.0 57.0 %convolution_bitcast_fusion = f32[2048,2752]{0,1:T(8,128)} fusion(bf16[4,2048,1024]{2,1,0:T(8,128)(2,1)} %bitcast_dynamic-update-slice_fusion.32, bf16[4,1024,2752]{1,2,0:T(8,128)(2,1)} %all-gather.8.cloned.1.call-done), kind=kOutput, calls=%fused_computation.1 | convolution fusion | flops 46170898432 | bytes 61865984 | tf_op jit(solution)/shard_map/dot_general | solution.py:21
  753.0 9.0 multiply_convert_fusion
  762.0 9.7 fusion.55
  771.7 7.9 fusion.54
  779.6 7.9 fusion.53
  787.5 7.9 fusion.52
  800.7 91.9 %all-gather.14.cloned.1.call-done = bf16[5504,1024]{1,0:T(8,128)(2,1)} async-done(((bf16[1376,1024]{1,0:T(8,128)(2,1)}), bf16[5504,1024]{1,0:T(8,128)(2,1)}) %all-gather.14.cloned.1.call-update) | async-done | bytes 11272208 | tf_op jit(solution)/shard_map/all_gather | solution.py:263
  892.6 37.1 %fusion.3 = (bf16[2048,1376]{0,1:T(8,128)(2,1)S(1)}, bf16[2048,1376]{0,1:T(8,128)(2,1)}) fusion(f32[2048,2752]{0,1:T(8,128)} %convolution_bitcast_fusion, bf16[4,2048,1024]{2,1,0:T(8,128)(2,1)} %bitcast_dynamic-update-slice_fusion.16, bf16[4,1376,1024]{2,1,0:T(8,128)(2,1)} %bitcast.517), kind=kOutput, calls=%fused_computation.10 | convolution fusion | flops 23122083840 | bytes 61865984 | tf_op jit(solution)/shard_map/dot_general | solution.py:21
  932.2 54.7 %convolution_convert_fusion = bf16[4,1024,2752]{1,2,0:T(8,128)(2,1)} fusion(bf16[4,2048,1024]{2,1,0:T(8,128)(2,1)} %bitcast_dynamic-update-slice_fusion.32, bf16[2048,1376]{0,1:T(8,128)(2,1)} %get-tuple-element.47, bf16[2048,1376]{0,1:T(8,128)(2,1)S(1)} %get-tuple-element.46), kind=kOutput, calls=%fused_computation | convolution fusion | flops 46204715008 | bytes 50593792 | tf_op jit(solution)/shard_map/dot_general | solution.py:21
  986.9 97.4 %reduce-scatter.6.cloned.1.call-done = bf16[1,1376,1024]{2,1,0:T(8,128)(2,1)} async-done(((bf16[4,1376,1024]{2,1,0:T(8,128)(2,1)}), bf16[1,1376,1024]{2,1,0:T(8,128)(2,1)}) %reduce-scatter.6.cloned.1.call-update) | async-done | bytes 2818064 | tf_op jit(solution)/shard_map/reduce_scatter | solution.py:259
  1084.4 17.4 fusion.41
  1101.9 17.4 fusion.38
  1119.8 17.6 add_convert_fusion.4
  1141.2 17.6 add_convert_fusion.5
  1171.1 15.4 collective-permute-done.51
  1192.6 19.0 %collective-permute-done.55 = bf16[512,1024]{1,0:T(8,128)(2,1)S(1)} collective-permute-done((bf16[512,1024]{1,0:T(8,128)(2,1)S(1)}, bf16[512,1024]{1,0:T(8,128)(2,1)S(1)}, u32[]{:S(2)}, u32[]{:S(2)}) %collective-permute-start.55) | collective-permute-done | bytes 1048608 | tf_op jit(solution)/shard_map/ppermute | solution.py:191
  1215.0 6.2 psum.30
  1230.9 21.0 %collective-permute-done.58 = bf16[512,1024]{1,0:T(8,128)(2,1)S(1)} collective-permute-done((bf16[512,1024]{1,0:T(8,128)(2,1)S(1)}, bf16[512,1024]{1,0:T(8,128)(2,1)S(1)}, u32[]{:S(2)}, u32[]{:S(2)}) %collective-permute-start.58) | collective-permute-done | bytes 1048608 | tf_op jit(solution)/shard_map/ppermute | solution.py:191
  1257.6 19.8 %collective-permute-done.65 = bf16[512,1024]{1,0:T(8,128)(2,1)S(1)} collective-permute-done((bf16[512,1024]{1,0:T(8,128)(2,1)S(1)}, bf16[512,1024]{1,0:T(8,128)(2,1)S(1)}, u32[]{:S(2)}, u32[]{:S(2)}) %collective-permute-start.65) | collective-permute-done | bytes 1048608 | tf_op jit(solution)/shard_map/ppermute | solution.py:191
  1278.1 19.9 %collective-permute-done.60 = bf16[512,1024]{1,0:T(8,128)(2,1)S(1)} collective-permute-done((bf16[512,1024]{1,0:T(8,128)(2,1)S(1)}, bf16[512,1024]{1,0:T(8,128)(2,1)S(1)}, u32[]{:S(2)}, u32[]{:S(2)}) %collective-permute-start.60) | collective-permute-done | bytes 1048608 | tf_op jit(solution)/shard_map/ppermute | solution.py:191
  1318.8 15.0 bitcast_convert_fusion.g
  1333.9 43.9 %shard_map.144 = (bf16[2048,512]{1,0:T(8,128)(2,1)S(1)}, bf16[2048,512]{1,0:T(8,128)(2,1)}, bf16[2048,512]{1,0:T(8,128)(2,1)}) custom-call(bf16[2048,512]{1,0:T(8,128)(2,1)} %copy-done.6, bf16[2048,512]{1,0:T(8,128)(2,1)} %get-tuple-element.25.k, bf16[2048,512]{1,0:T(8,128)(2,1)} %get-tuple-element.26.v, bf16[2048,512]{1,0:T(8,128)(2,1)} %get-tuple-element.23.o, ...), custom_call_target="tpu_custom_call" | custom-call | flops 13421772800 | bytes 16777216 | tf_op jit(solution)/shard_map/pallas_call | solution.py:164
  1377.7 23.1 %convolution_convert_fusion.1 = bf16[4,1024,1024]{2,1,0:T(8,128)(2,1)} fusion(bf16[4,2048,1024]{2,1,0:T(8,128)(2,1)} %bitcast_dynamic-update-slice_fusion.48, bf16[2048,512]{1,0:T(8,128)(2,1)} %get-tuple-element.32, bf16[2048,512]{1,0:T(8,128)(2,1)} %get-tuple-element.31), kind=kOutput, calls=%fused_computation.29 | convolution fusion | flops 17192452096 | bytes 29360128 | tf_op jit(solution)/shard_map/dot_general | solution.py:21
  1413.6 26.3 %collective-permute-done.91 = bf16[1376,512]{1,0:T(8,128)(2,1)S(1)} collective-permute-done((bf16[1376,512]{1,0:T(8,128)(2,1)S(1)}, bf16[1376,512]{1,0:T(8,128)(2,1)S(1)}, u32[]{:S(2)}, u32[]{:S(2)}) %collective-permute-start.91) | collective-permute-done | bytes 1409056 | tf_op jit(solution)/shard_map/ppermute | solution.py:191
  1447.9 8.3 convolution_convert_fusion.2
  1456.3 8.3 convolution_convert_fusion.3
  1464.6 14.3 convolution_convert_fusion.8
  1479.4 11.2 convolution_convert_fusion.4
  1490.6 10.1 convolution_convert_fusion.5
  1501.3 11.2 add_convert_fusion
  1514.4 11.0 add_convert_fusion.1
  1529.0 9.7 add_convert_fusion.2
  1540.6 9.8 add_convert_fusion.3
  1554.9 28.2 %collective-permute-done.75 = bf16[512,1024]{1,0:T(8,128)(2,1)S(1)} collective-permute-done((bf16[512,1024]{1,0:T(8,128)(2,1)S(1)}, bf16[512,1024]{1,0:T(8,128)(2,1)S(1)}, u32[]{:S(2)}, u32[]{:S(2)}) %collective-permute-start.75) | collective-permute-done | bytes 1048608 | tf_op jit(solution)/shard_map/ppermute | solution.py:191
  1587.5 10.4 collective-permute-done.78
  1601.3 19.1 %collective-permute-done.84 = bf16[512,1024]{1,0:T(8,128)(2,1)S(1)} collective-permute-done((bf16[512,1024]{1,0:T(8,128)(2,1)S(1)}, bf16[512,1024]{1,0:T(8,128)(2,1)S(1)}, u32[]{:S(2)}, u32[]{:S(2)}) %collective-permute-start.84) | collective-permute-done | bytes 1048608 | tf_op jit(solution)/shard_map/ppermute | solution.py:191
  1635.5 31.0 %psum.31 = f32[1024]{0:T(1024)S(1)} all-reduce(f32[1024]{0:T(1024)S(1)} %get-tuple-element.41), channel_id=1, replica_groups=mesh['fsdp'=4,'ctx'=2,'tp'=4] {'tp'}, use_global_device_ids=true, to_apply=%region_8.9 | all-reduce | flops 1024 | bytes 8192 | tf_op jit(solution)/shard_map/psum | solution.py:186
  1680.2 32.8 %collective-permute-done.88 = f32[2,1024]{1,0:T(2,128)S(1)} collective-permute-done((f32[2,1024]{1,0:T(2,128)S(1)}, f32[2,1024]{1,0:T(2,128)S(1)}, u32[]{:S(2)}, u32[]{:S(2)}) %collective-permute-start.88) | collective-permute-done | bytes 8224 | tf_op jit(solution)/shard_map/ppermute | solution.py:191
  1742.5 25.9 %reduce-scatter.8.cloned.1.call-done = bf16[1,1024,512]{2,1,0:T(8,128)(2,1)} async-done(((bf16[4,1024,512]{2,1,0:T(8,128)(2,1)}), bf16[1,1024,512]{2,1,0:T(8,128)(2,1)}) %reduce-scatter.8.cloned.1.call-update) | async-done | bytes 1048592 | tf_op jit(solution)/shard_map/reduce_scatter | solution.py:259
  1771.7 11.6 collective-permute-done.94
  (487 shorter events, 340.6 us)
Async XLA Ops:
  7.2 225.0 %all-gather.10.cloned.1.call-start = ((), (), s32[]{:S(2)}) async-start(), calls=%async_computation.11 | async-start | bytes 15728640 | tf_op jit(solution)/shard_map/all_gather | solution.py:263
  11.2 301.6 %all-gather.12.cloned.1.call-start = ((), (), s32[]{:S(2)}) async-start(), calls=%async_computation.12 | async-start | bytes 5242880 | tf_op jit(solution)/shard_map/all_gather | solution.py:263
  12.3 683.7 %all-gather.8.cloned.1.call-start = ((), (), s32[]{:S(2)}) async-start(), calls=%async_computation.5 | async-start | bytes 28180480 | tf_op jit(solution)/shard_map/all_gather | solution.py:263
  18.1 874.5 %all-gather.14.cloned.1.call-start = ((), (), s32[]{:S(2)}) async-start(), calls=%async_computation.13 | async-start | bytes 14090240 | tf_op jit(solution)/shard_map/all_gather | solution.py:263
  33.7 35.4 %collective-permute-start.1 = (bf16[512,1024]{1,0:T(8,128)(2,1)}, bf16[512,1024]{1,0:T(8,128)(2,1)}, u32[]{:S(2)}, u32[]{:S(2)}) collective-permute-start(bf16[512,1024]{1,0:T(8,128)(2,1)} %get-tuple-element.88), channel_id=1, source_target_pairs={{0,2},{1,3},{2,0},{3,1},{4,6},{5,7},{6,4},{7,5},{8,10},{9,11},{10,... | collective-permute-start | bytes 3145736 | tf_op jit(solution)/shard_map/ppermute | solution.py:191
  34.7 36.0 %collective-permute-start.3 = (bf16[512,1024]{1,0:T(8,128)(2,1)}, bf16[512,1024]{1,0:T(8,128)(2,1)}, u32[]{:S(2)}, u32[]{:S(2)}) collective-permute-start(bf16[512,1024]{1,0:T(8,128)(2,1)} %get-tuple-element.88), channel_id=1, source_target_pairs={{0,1},{1,0},{2,3},{3,2},{4,5},{5,4},{6,7},{7,6},{8,9},{9,8},{10,11... | collective-permute-start | bytes 3145736 | tf_op jit(solution)/shard_map/ppermute | solution.py:191
  34.7 47.9 %collective-permute-start.7 = (bf16[512,1024]{1,0:T(8,128)(2,1)}, bf16[512,1024]{1,0:T(8,128)(2,1)}, u32[]{:S(2)}, u32[]{:S(2)}) collective-permute-start(bf16[512,1024]{1,0:T(8,128)(2,1)} %get-tuple-element.87), channel_id=1, source_target_pairs={{0,2},{1,3},{2,0},{3,1},{4,6},{5,7},{6,4},{7,5},{8,10},{9,11},{10,... | collective-permute-start | bytes 3145736 | tf_op jit(solution)/shard_map/ppermute | solution.py:191
  56.6 46.1 %collective-permute-start.2 = (bf16[512,1024]{1,0:T(8,128)(2,1)}, bf16[512,1024]{1,0:T(8,128)(2,1)S(1)}, u32[]{:S(2)}, u32[]{:S(2)}) collective-permute-start(bf16[512,1024]{1,0:T(8,128)(2,1)} %collective-permute-done), channel_id=1, source_target_pairs={{0,2},{1,3},{2,0},{3,1},{4,6},{5,7},{6,4},{7,5},{8,10},{9,11},{10,... | collective-permute-start | bytes 3145736 | tf_op jit(solution)/shard_map/ppermute | solution.py:191
  66.1 40.0 %collective-permute-start.4 = (bf16[512,1024]{1,0:T(8,128)(2,1)}, bf16[512,1024]{1,0:T(8,128)(2,1)S(1)}, u32[]{:S(2)}, u32[]{:S(2)}) collective-permute-start(bf16[512,1024]{1,0:T(8,128)(2,1)} %collective-permute-done), channel_id=1, source_target_pairs={{0,1},{1,0},{2,3},{3,2},{4,5},{5,4},{6,7},{7,6},{8,9},{9,8},{10,11... | collective-permute-start | bytes 3145736 | tf_op jit(solution)/shard_map/ppermute | solution.py:191
  69.1 38.5 %collective-permute-start.8 = (bf16[512,1024]{1,0:T(8,128)(2,1)}, bf16[512,1024]{1,0:T(8,128)(2,1)S(1)}, u32[]{:S(2)}, u32[]{:S(2)}) collective-permute-start(bf16[512,1024]{1,0:T(8,128)(2,1)} %get-tuple-element.87), channel_id=1, source_target_pairs={{0,4},{4,0},{1,5},{5,1},{2,6},{6,2},{3,7},{7,3},{8,12},{12,8},{9,1... | collective-permute-start | bytes 3145736 | tf_op jit(solution)/shard_map/ppermute | solution.py:191
  70.6 37.0 %collective-permute-start.5 = (bf16[512,1024]{1,0:T(8,128)(2,1)}, bf16[512,1024]{1,0:T(8,128)(2,1)S(1)}, u32[]{:S(2)}, u32[]{:S(2)}) collective-permute-start(bf16[512,1024]{1,0:T(8,128)(2,1)} %collective-permute-done.1), channel_id=1, source_target_pairs={{0,1},{1,0},{2,3},{3,2},{4,5},{5,4},{6,7},{7,6},{8,9},{9,8},{10,11... | collective-permute-start | bytes 3145736 | tf_op jit(solution)/shard_map/ppermute | solution.py:191
  82.6 34.0 %collective-permute-start.9 = (bf16[512,1024]{1,0:T(8,128)(2,1)}, bf16[512,1024]{1,0:T(8,128)(2,1)S(1)}, u32[]{:S(2)}, u32[]{:S(2)}) collective-permute-start(bf16[512,1024]{1,0:T(8,128)(2,1)} %collective-permute-done.7), channel_id=1, source_target_pairs={{0,4},{4,0},{1,5},{5,1},{2,6},{6,2},{3,7},{7,3},{8,12},{12,8},{9,1... | collective-permute-start | bytes 3145736 | tf_op jit(solution)/shard_map/ppermute | solution.py:191
  319.1 79.2 %collective-permute-start.16 = (bf16[2048,1024]{1,0:T(8,128)(2,1)}, bf16[2048,1024]{1,0:T(8,128)(2,1)}, u32[]{:S(2)}, u32[]{:S(2)}) collective-permute-start(bf16[2048,1024]{1,0:T(8,128)(2,1)} %convolution_convert_fusion.6), channel_id=1, source_target_pairs={{0,1},{1,0},{2,3},{3,2},{4,5},{5,4},{6,7},{7,6},{8,9},{9,8},{10,11... | collective-permute-start | bytes 12582920 | tf_op jit(solution)/shard_map/ppermute | solution.py:191
  329.5 77.3 %collective-permute-start.14 = (bf16[2048,1024]{1,0:T(8,128)(2,1)}, bf16[2048,1024]{1,0:T(8,128)(2,1)}, u32[]{:S(2)}, u32[]{:S(2)}) collective-permute-start(bf16[2048,1024]{1,0:T(8,128)(2,1)} %convolution_convert_fusion.7), channel_id=1, source_target_pairs={{0,1},{1,0},{2,3},{3,2},{4,5},{5,4},{6,7},{7,6},{8,9},{9,8},{10,11... | collective-permute-start | bytes 12582920 | tf_op jit(solution)/shard_map/ppermute | solution.py:191
  330.0 29.7 %collective-permute-start.39 = (bf16[512,1024]{1,0:T(8,128)(2,1)}, bf16[512,1024]{1,0:T(8,128)(2,1)}, u32[]{:S(2)}, u32[]{:S(2)}) collective-permute-start(bf16[512,1024]{1,0:T(8,128)(2,1)} %get-tuple-element.82), channel_id=1, source_target_pairs={{0,1},{1,0},{2,3},{3,2},{4,5},{5,4},{6,7},{7,6},{8,9},{9,8},{10,11... | collective-permute-start | bytes 3145736 | tf_op jit(solution)/shard_map/ppermute | solution.py:191
  350.0 734.4 %reduce-scatter.6.cloned.1.call-start = ((), (), s32[]{:S(2)}) async-start(), calls=%async_computation.6 | async-start | bytes 14090240 | tf_op jit(solution)/shard_map/reduce_scatter | solution.py:259
  359.7 34.4 %collective-permute-start.43 = (bf16[512,1024]{1,0:T(8,128)(2,1)}, bf16[512,1024]{1,0:T(8,128)(2,1)}, u32[]{:S(2)}, u32[]{:S(2)}) collective-permute-start(bf16[512,1024]{1,0:T(8,128)(2,1)} %get-tuple-element.81), channel_id=1, source_target_pairs={{0,2},{1,3},{2,0},{3,1},{4,6},{5,7},{6,4},{7,5},{8,10},{9,11},{10,... | collective-permute-start | bytes 3145736 | tf_op jit(solution)/shard_map/ppermute | solution.py:191
  394.1 74.2 %collective-permute-start.44 = (bf16[512,1024]{1,0:T(8,128)(2,1)}, bf16[512,1024]{1,0:T(8,128)(2,1)}, u32[]{:S(2)}, u32[]{:S(2)}) collective-permute-start(bf16[512,1024]{1,0:T(8,128)(2,1)} %get-tuple-element.81), channel_id=1, source_target_pairs={{0,4},{4,0},{1,5},{5,1},{2,6},{6,2},{3,7},{7,3},{8,12},{12,8},{9,1... | collective-permute-start | bytes 3145736 | tf_op jit(solution)/shard_map/ppermute | solution.py:191
  395.6 113.7 %collective-permute-start.45 = (bf16[512,1024]{1,0:T(8,128)(2,1)}, bf16[512,1024]{1,0:T(8,128)(2,1)}, u32[]{:S(2)}, u32[]{:S(2)}) collective-permute-start(bf16[512,1024]{1,0:T(8,128)(2,1)} %collective-permute-done.43), channel_id=1, source_target_pairs={{0,4},{4,0},{1,5},{5,1},{2,6},{6,2},{3,7},{7,3},{8,12},{12,8},{9,1... | collective-permute-start | bytes 3145736 | tf_op jit(solution)/shard_map/ppermute | solution.py:191
  403.6 61.8 %collective-permute-start.17 = (bf16[512,1024]{1,0:T(8,128)(2,1)S(1)}, bf16[512,1024]{1,0:T(8,128)(2,1)S(1)}, u32[]{:S(2)}, u32[]{:S(2)}) collective-permute-start(bf16[512,1024]{1,0:T(8,128)(2,1)S(1)} %dynamic-slice_bitcast_fusion.17), channel_id=1, source_target_pairs={{0,4},{4,0},{1,5},{5,1},{2,6},{6,2},{3,7},{7,3},{8,12},{12,8},{9,1... | collective-permute-start | bytes 3145736 | tf_op jit(solution)/shard_map/ppermute | solution.py:191
  405.3 62.0 %collective-permute-start.20 = (bf16[512,1024]{1,0:T(8,128)(2,1)S(1)}, bf16[512,1024]{1,0:T(8,128)(2,1)S(1)}, u32[]{:S(2)}, u32[]{:S(2)}) collective-permute-start(bf16[512,1024]{1,0:T(8,128)(2,1)S(1)} %get-tuple-element.86), channel_id=1, source_target_pairs={{0,2},{1,3},{2,0},{3,1},{4,6},{5,7},{6,4},{7,5},{8,10},{9,11},{10,... | collective-permute-start | bytes 3145736 | tf_op jit(solution)/shard_map/ppermute | solution.py:191
  412.0 75.9 %collective-permute-start.15 = (bf16[512,1024]{1,0:T(8,128)(2,1)S(1)}, bf16[512,1024]{1,0:T(8,128)(2,1)S(1)}, u32[]{:S(2)}, u32[]{:S(2)}) collective-permute-start(bf16[512,1024]{1,0:T(8,128)(2,1)S(1)} %dynamic-slice_bitcast_fusion.18), channel_id=1, source_target_pairs={{0,4},{4,0},{1,5},{5,1},{2,6},{6,2},{3,7},{7,3},{8,12},{12,8},{9,1... | collective-permute-start | bytes 3145736 | tf_op jit(solution)/shard_map/ppermute | solution.py:191
  465.4 44.5 %collective-permute-start.19 = (bf16[512,1024]{1,0:T(8,128)(2,1)S(1)}, bf16[512,1024]{1,0:T(8,128)(2,1)S(1)}, u32[]{:S(2)}, u32[]{:S(2)}) collective-permute-start(bf16[512,1024]{1,0:T(8,128)(2,1)S(1)} %get-tuple-element.85), channel_id=1, source_target_pairs={{0,2},{1,3},{2,0},{3,1},{4,6},{5,7},{6,4},{7,5},{8,10},{9,11},{10,... | collective-permute-start | bytes 3145736 | tf_op jit(solution)/shard_map/ppermute | solution.py:191
  467.3 41.4 %collective-permute-start.18 = (bf16[512,1024]{1,0:T(8,128)(2,1)S(1)}, bf16[512,1024]{1,0:T(8,128)(2,1)S(1)}, u32[]{:S(2)}, u32[]{:S(2)}) collective-permute-start(bf16[512,1024]{1,0:T(8,128)(2,1)S(1)} %fusion.98), channel_id=1, source_target_pairs={{0,2},{1,3},{2,0},{3,1},{4,6},{5,7},{6,4},{7,5},{8,10},{9,11},{10,... | collective-permute-start | bytes 3145736 | tf_op jit(solution)/shard_map/ppermute | solution.py:191
  468.3 41.7 %collective-permute-start.21 = (bf16[512,1024]{1,0:T(8,128)(2,1)S(1)}, bf16[512,1024]{1,0:T(8,128)(2,1)S(1)}, u32[]{:S(2)}, u32[]{:S(2)}) collective-permute-start(bf16[512,1024]{1,0:T(8,128)(2,1)S(1)} %fusion.96), channel_id=1, source_target_pairs={{0,4},{4,0},{1,5},{5,1},{2,6},{6,2},{3,7},{7,3},{8,12},{12,8},{9,1... | collective-permute-start | bytes 3145736 | tf_op jit(solution)/shard_map/ppermute | solution.py:191
  487.9 40.1 %collective-permute-start.46 = (bf16[512,1024]{1,0:T(8,128)(2,1)}, bf16[512,1024]{1,0:T(8,128)(2,1)}, u32[]{:S(2)}, u32[]{:S(2)}) collective-permute-start(bf16[512,1024]{1,0:T(8,128)(2,1)} %get-tuple-element.81), channel_id=1, source_target_pairs={{0,1},{1,0},{2,3},{3,2},{4,5},{5,4},{6,7},{7,6},{8,9},{9,8},{10,11... | collective-permute-start | bytes 3145736 | tf_op jit(solution)/shard_map/ppermute | solution.py:191
  509.9 39.2 %collective-permute-start.49 = (bf16[512,1024]{1,0:T(8,128)(2,1)}, bf16[512,1024]{1,0:T(8,128)(2,1)S(1)}, u32[]{:S(2)}, u32[]{:S(2)}) collective-permute-start(bf16[512,1024]{1,0:T(8,128)(2,1)} %collective-permute-done.45), channel_id=1, source_target_pairs={{0,1},{1,0},{2,3},{3,2},{4,5},{5,4},{6,7},{7,6},{8,9},{9,8},{10,11... | collective-permute-start | bytes 3145736 | tf_op jit(solution)/shard_map/ppermute | solution.py:191
  533.1 27.2 %collective-permute-start.25 = (bf16[512,1024]{1,0:T(8,128)(2,1)S(1)}, bf16[512,1024]{1,0:T(8,128)(2,1)S(1)}, u32[]{:S(2)}, u32[]{:S(2)}) collective-permute-start(bf16[512,1024]{1,0:T(8,128)(2,1)S(1)} %get-tuple-element.84), channel_id=1, source_target_pairs={{0,1},{1,0},{2,3},{3,2},{4,5},{5,4},{6,7},{7,6},{8,9},{9,8},{10,11... | collective-permute-start | bytes 3145736 | tf_op jit(solution)/shard_map/ppermute | solution.py:191
  533.1 48.0 %collective-permute-start.29 = (bf16[512,1024]{1,0:T(8,128)(2,1)S(1)}, bf16[512,1024]{1,0:T(8,128)(2,1)S(1)}, u32[]{:S(2)}, u32[]{:S(2)}) collective-permute-start(bf16[512,1024]{1,0:T(8,128)(2,1)S(1)} %get-tuple-element.83), channel_id=1, source_target_pairs={{0,2},{1,3},{2,0},{3,1},{4,6},{5,7},{6,4},{7,5},{8,10},{9,11},{10,... | collective-permute-start | bytes 3145736 | tf_op jit(solution)/shard_map/ppermute | solution.py:191
  547.6 53.0 %collective-permute-start.24 = (bf16[512,1024]{1,0:T(8,128)(2,1)S(1)}, bf16[512,1024]{1,0:T(8,128)(2,1)S(1)}, u32[]{:S(2)}, u32[]{:S(2)}) collective-permute-start(bf16[512,1024]{1,0:T(8,128)(2,1)S(1)} %collective-permute-done.22), channel_id=1, source_target_pairs={{0,2},{1,3},{2,0},{3,1},{4,6},{5,7},{6,4},{7,5},{8,10},{9,11},{10,... | collective-permute-start | bytes 3145736 | tf_op jit(solution)/shard_map/ppermute | solution.py:191
  557.8 45.0 %collective-permute-start.26 = (bf16[512,1024]{1,0:T(8,128)(2,1)S(1)}, bf16[512,1024]{1,0:T(8,128)(2,1)S(1)}, u32[]{:S(2)}, u32[]{:S(2)}) collective-permute-start(bf16[512,1024]{1,0:T(8,128)(2,1)S(1)} %collective-permute-done.22), channel_id=1, source_target_pairs={{0,1},{1,0},{2,3},{3,2},{4,5},{5,4},{6,7},{7,6},{8,9},{9,8},{10,11... | collective-permute-start | bytes 3145736 | tf_op jit(solution)/shard_map/ppermute | solution.py:191
  558.8 45.6 %collective-permute-start.30 = (bf16[512,1024]{1,0:T(8,128)(2,1)S(1)}, bf16[512,1024]{1,0:T(8,128)(2,1)S(1)}, u32[]{:S(2)}, u32[]{:S(2)}) collective-permute-start(bf16[512,1024]{1,0:T(8,128)(2,1)S(1)} %get-tuple-element.83), channel_id=1, source_target_pairs={{0,4},{4,0},{1,5},{5,1},{2,6},{6,2},{3,7},{7,3},{8,12},{12,8},{9,1... | collective-permute-start | bytes 3145736 | tf_op jit(solution)/shard_map/ppermute | solution.py:191
  560.3 44.1 %collective-permute-start.27 = (bf16[512,1024]{1,0:T(8,128)(2,1)S(1)}, bf16[512,1024]{1,0:T(8,128)(2,1)S(1)}, u32[]{:S(2)}, u32[]{:S(2)}) collective-permute-start(bf16[512,1024]{1,0:T(8,128)(2,1)S(1)} %collective-permute-done.23), channel_id=1, source_target_pairs={{0,1},{1,0},{2,3},{3,2},{4,5},{5,4},{6,7},{7,6},{8,9},{9,8},{10,11... | collective-permute-start | bytes 3145736 | tf_op jit(solution)/shard_map/ppermute | solution.py:191
  800.7 828.2 %reduce-scatter.12.cloned.1.call-start = ((), (), s32[]{:S(2)}) async-start(), calls=%async_computation.9 | async-start | bytes 28180480 | tf_op jit(solution)/shard_map/reduce_scatter | solution.py:259
  1084.4 630.1 %reduce-scatter.10.cloned.1.call-start = ((), (), s32[]{:S(2)}) async-start(), calls=%async_computation.8 | async-start | bytes 5242880 | tf_op jit(solution)/shard_map/reduce_scatter | solution.py:259
  1139.7 28.3 %collective-permute-start.56 = (bf16[512,1024]{1,0:T(8,128)(2,1)S(1)}, bf16[512,1024]{1,0:T(8,128)(2,1)}, u32[]{:S(2)}, u32[]{:S(2)}) collective-permute-start(bf16[512,1024]{1,0:T(8,128)(2,1)S(1)} %get-tuple-element.80), channel_id=1, source_target_pairs={{0,2},{1,3},{2,0},{3,1},{4,6},{5,7},{6,4},{7,5},{8,10},{9,11},{10,... | collective-permute-start | bytes 3145736 | tf_op jit(solution)/shard_map/ppermute | solution.py:191
  1167.4 44.2 %collective-permute-start.55 = (bf16[512,1024]{1,0:T(8,128)(2,1)S(1)}, bf16[512,1024]{1,0:T(8,128)(2,1)S(1)}, u32[]{:S(2)}, u32[]{:S(2)}) collective-permute-start(bf16[512,1024]{1,0:T(8,128)(2,1)S(1)} %get-tuple-element.79), channel_id=1, source_target_pairs={{0,2},{1,3},{2,0},{3,1},{4,6},{5,7},{6,4},{7,5},{8,10},{9,11},{10,... | collective-permute-start | bytes 3145736 | tf_op jit(solution)/shard_map/ppermute | solution.py:191
  1169.6 42.0 %collective-permute-start.57 = (bf16[512,1024]{1,0:T(8,128)(2,1)S(1)}, bf16[512,1024]{1,0:T(8,128)(2,1)S(1)}, u32[]{:S(2)}, u32[]{:S(2)}) collective-permute-start(bf16[512,1024]{1,0:T(8,128)(2,1)S(1)} %fusion.92), channel_id=1, source_target_pairs={{0,4},{4,0},{1,5},{5,1},{2,6},{6,2},{3,7},{7,3},{8,12},{12,8},{9,1... | collective-permute-start | bytes 3145736 | tf_op jit(solution)/shard_map/ppermute | solution.py:191
  1230.4 47.1 %collective-permute-start.65 = (bf16[512,1024]{1,0:T(8,128)(2,1)S(1)}, bf16[512,1024]{1,0:T(8,128)(2,1)S(1)}, u32[]{:S(2)}, u32[]{:S(2)}) collective-permute-start(bf16[512,1024]{1,0:T(8,128)(2,1)S(1)} %get-tuple-element.77), channel_id=1, source_target_pairs={{0,2},{1,3},{2,0},{3,1},{4,6},{5,7},{6,4},{7,5},{8,10},{9,11},{10,... | collective-permute-start | bytes 3145736 | tf_op jit(solution)/shard_map/ppermute | solution.py:191
  1251.9 46.1 %collective-permute-start.60 = (bf16[512,1024]{1,0:T(8,128)(2,1)S(1)}, bf16[512,1024]{1,0:T(8,128)(2,1)S(1)}, u32[]{:S(2)}, u32[]{:S(2)}) collective-permute-start(bf16[512,1024]{1,0:T(8,128)(2,1)S(1)} %collective-permute-done.58), channel_id=1, source_target_pairs={{0,2},{1,3},{2,0},{3,1},{4,6},{5,7},{6,4},{7,5},{8,10},{9,11},{10,... | collective-permute-start | bytes 3145736 | tf_op jit(solution)/shard_map/ppermute | solution.py:191
  1255.6 42.6 %collective-permute-start.62 = (bf16[512,1024]{1,0:T(8,128)(2,1)S(1)}, bf16[512,1024]{1,0:T(8,128)(2,1)S(1)}, u32[]{:S(2)}, u32[]{:S(2)}) collective-permute-start(bf16[512,1024]{1,0:T(8,128)(2,1)S(1)} %collective-permute-done.58), channel_id=1, source_target_pairs={{0,1},{1,0},{2,3},{3,2},{4,5},{5,4},{6,7},{7,6},{8,9},{9,8},{10,11... | collective-permute-start | bytes 3145736 | tf_op jit(solution)/shard_map/ppermute | solution.py:191
  1255.8 43.1 %collective-permute-start.66 = (bf16[512,1024]{1,0:T(8,128)(2,1)S(1)}, bf16[512,1024]{1,0:T(8,128)(2,1)S(1)}, u32[]{:S(2)}, u32[]{:S(2)}) collective-permute-start(bf16[512,1024]{1,0:T(8,128)(2,1)S(1)} %get-tuple-element.77), channel_id=1, source_target_pairs={{0,4},{4,0},{1,5},{5,1},{2,6},{6,2},{3,7},{7,3},{8,12},{12,8},{9,1... | collective-permute-start | bytes 3145736 | tf_op jit(solution)/shard_map/ppermute | solution.py:191
  1257.4 41.7 %collective-permute-start.63 = (bf16[512,1024]{1,0:T(8,128)(2,1)S(1)}, bf16[512,1024]{1,0:T(8,128)(2,1)S(1)}, u32[]{:S(2)}, u32[]{:S(2)}) collective-permute-start(bf16[512,1024]{1,0:T(8,128)(2,1)S(1)} %collective-permute-done.59), channel_id=1, source_target_pairs={{0,1},{1,0},{2,3},{3,2},{4,5},{5,4},{6,7},{7,6},{8,9},{9,8},{10,11... | collective-permute-start | bytes 3145736 | tf_op jit(solution)/shard_map/ppermute | solution.py:191
  1318.7 420.0 %reduce-scatter.14.cloned.1.call-start = ((), (), s32[]{:S(2)}) async-start(), calls=%async_computation.10 | async-start | bytes 10485760 | tf_op jit(solution)/shard_map/reduce_scatter | solution.py:259
  1400.9 367.6 %reduce-scatter.8.cloned.1.call-start = ((), (), s32[]{:S(2)}) async-start(), calls=%async_computation.7 | async-start | bytes 5242880 | tf_op jit(solution)/shard_map/reduce_scatter | solution.py:259
  1406.9 33.0 %collective-permute-start.91 = (bf16[1376,512]{1,0:T(8,128)(2,1)S(1)}, bf16[1376,512]{1,0:T(8,128)(2,1)S(1)}, u32[]{:S(2)}, u32[]{:S(2)}) collective-permute-start(bf16[1376,512]{1,0:T(8,128)(2,1)S(1)} %dynamic-slice_bitcast_fusion.2), channel_id=1, source_target_pairs={{0,4},{4,0},{1,5},{5,1},{2,6},{6,2},{3,7},{7,3},{8,12},{12,8},{9,1... | collective-permute-start | bytes 4227080 | tf_op jit(solution)/shard_map/ppermute | solution.py:191
  1456.3 45.0 %collective-permute-start.82 = (bf16[2048,1024]{1,0:T(8,128)(2,1)}, bf16[2048,1024]{1,0:T(8,128)(2,1)}, u32[]{:S(2)}, u32[]{:S(2)}) collective-permute-start(bf16[2048,1024]{1,0:T(8,128)(2,1)} %convolution_convert_fusion.2), channel_id=1, source_target_pairs={{0,1},{1,0},{2,3},{3,2},{4,5},{5,4},{6,7},{7,6},{8,9},{9,8},{10,11... | collective-permute-start | bytes 12582920 | tf_op jit(solution)/shard_map/ppermute | solution.py:191
  1478.9 35.5 %collective-permute-start.80 = (bf16[2048,1024]{1,0:T(8,128)(2,1)}, bf16[2048,1024]{1,0:T(8,128)(2,1)}, u32[]{:S(2)}, u32[]{:S(2)}) collective-permute-start(bf16[2048,1024]{1,0:T(8,128)(2,1)} %convolution_convert_fusion.3), channel_id=1, source_target_pairs={{0,1},{1,0},{2,3},{3,2},{4,5},{5,4},{6,7},{7,6},{8,9},{9,8},{10,11... | collective-permute-start | bytes 12582920 | tf_op jit(solution)/shard_map/ppermute | solution.py:191
  1490.6 37.7 %collective-permute-start.74 = (bf16[2048,1024]{1,0:T(8,128)(2,1)}, bf16[2048,1024]{1,0:T(8,128)(2,1)}, u32[]{:S(2)}, u32[]{:S(2)}) collective-permute-start(bf16[2048,1024]{1,0:T(8,128)(2,1)} %convolution_convert_fusion.4), channel_id=1, source_target_pairs={{0,1},{1,0},{2,3},{3,2},{4,5},{5,4},{6,7},{7,6},{8,9},{9,8},{10,11... | collective-permute-start | bytes 12582920 | tf_op jit(solution)/shard_map/ppermute | solution.py:191
  1500.8 38.5 %collective-permute-start.72 = (bf16[2048,1024]{1,0:T(8,128)(2,1)}, bf16[2048,1024]{1,0:T(8,128)(2,1)}, u32[]{:S(2)}, u32[]{:S(2)}) collective-permute-start(bf16[2048,1024]{1,0:T(8,128)(2,1)} %convolution_convert_fusion.5), channel_id=1, source_target_pairs={{0,1},{1,0},{2,3},{3,2},{4,5},{5,4},{6,7},{7,6},{8,9},{9,8},{10,11... | collective-permute-start | bytes 12582920 | tf_op jit(solution)/shard_map/ppermute | solution.py:191
  1513.0 37.7 %collective-permute-start.83 = (bf16[512,1024]{1,0:T(8,128)(2,1)S(1)}, bf16[512,1024]{1,0:T(8,128)(2,1)S(1)}, u32[]{:S(2)}, u32[]{:S(2)}) collective-permute-start(bf16[512,1024]{1,0:T(8,128)(2,1)S(1)} %dynamic-slice_bitcast_fusion.5), channel_id=1, source_target_pairs={{0,4},{4,0},{1,5},{5,1},{2,6},{6,2},{3,7},{7,3},{8,12},{12,8},{9,1... | collective-permute-start | bytes 3145736 | tf_op jit(solution)/shard_map/ppermute | solution.py:191
  1525.9 74.8 %collective-permute-start.81 = (bf16[512,1024]{1,0:T(8,128)(2,1)S(1)}, bf16[512,1024]{1,0:T(8,128)(2,1)}, u32[]{:S(2)}, u32[]{:S(2)}) collective-permute-start(bf16[512,1024]{1,0:T(8,128)(2,1)S(1)} %dynamic-slice_bitcast_fusion.6), channel_id=1, source_target_pairs={{0,4},{4,0},{1,5},{5,1},{2,6},{6,2},{3,7},{7,3},{8,12},{12,8},{9,1... | collective-permute-start | bytes 3145736 | tf_op jit(solution)/shard_map/ppermute | solution.py:191
  1528.4 96.7 %collective-permute-start.85 = (bf16[512,1024]{1,0:T(8,128)(2,1)S(1)}, bf16[512,1024]{1,0:T(8,128)(2,1)}, u32[]{:S(2)}, u32[]{:S(2)}) collective-permute-start(bf16[512,1024]{1,0:T(8,128)(2,1)S(1)} %get-tuple-element.73), channel_id=1, source_target_pairs={{0,2},{1,3},{2,0},{3,1},{4,6},{5,7},{6,4},{7,5},{8,10},{9,11},{10,... | collective-permute-start | bytes 3145736 | tf_op jit(solution)/shard_map/ppermute | solution.py:191
  1539.2 43.8 %collective-permute-start.75 = (bf16[512,1024]{1,0:T(8,128)(2,1)S(1)}, bf16[512,1024]{1,0:T(8,128)(2,1)S(1)}, u32[]{:S(2)}, u32[]{:S(2)}) collective-permute-start(bf16[512,1024]{1,0:T(8,128)(2,1)S(1)} %dynamic-slice_bitcast_fusion.9), channel_id=1, source_target_pairs={{0,4},{4,0},{1,5},{5,1},{2,6},{6,2},{3,7},{7,3},{8,12},{12,8},{9,1... | collective-permute-start | bytes 3145736 | tf_op jit(solution)/shard_map/ppermute | solution.py:191
  1550.6 47.3 %collective-permute-start.78 = (bf16[512,1024]{1,0:T(8,128)(2,1)S(1)}, bf16[512,1024]{1,0:T(8,128)(2,1)S(1)}, u32[]{:S(2)}, u32[]{:S(2)}) collective-permute-start(bf16[512,1024]{1,0:T(8,128)(2,1)S(1)} %get-tuple-element.76), channel_id=1, source_target_pairs={{0,2},{1,3},{2,0},{3,1},{4,6},{5,7},{6,4},{7,5},{8,10},{9,11},{10,... | collective-permute-start | bytes 3145736 | tf_op jit(solution)/shard_map/ppermute | solution.py:191
  1553.0 67.4 %collective-permute-start.84 = (bf16[512,1024]{1,0:T(8,128)(2,1)S(1)}, bf16[512,1024]{1,0:T(8,128)(2,1)S(1)}, u32[]{:S(2)}, u32[]{:S(2)}) collective-permute-start(bf16[512,1024]{1,0:T(8,128)(2,1)S(1)} %fusion.86), channel_id=1, source_target_pairs={{0,2},{1,3},{2,0},{3,1},{4,6},{5,7},{6,4},{7,5},{8,10},{9,11},{10,... | collective-permute-start | bytes 3145736 | tf_op jit(solution)/shard_map/ppermute | solution.py:191
  1583.1 42.6 %collective-permute-start.87 = (bf16[512,1024]{1,0:T(8,128)(2,1)S(1)}, bf16[512,1024]{1,0:T(8,128)(2,1)S(1)}, u32[]{:S(2)}, u32[]{:S(2)}) collective-permute-start(bf16[512,1024]{1,0:T(8,128)(2,1)S(1)} %fusion.84), channel_id=1, source_target_pairs={{0,4},{4,0},{1,5},{5,1},{2,6},{6,2},{3,7},{7,3},{8,12},{12,8},{9,1... | collective-permute-start | bytes 3145736 | tf_op jit(solution)/shard_map/ppermute | solution.py:191
  1598.0 68.6 %collective-permute-start.73 = (bf16[512,1024]{1,0:T(8,128)(2,1)}, bf16[512,1024]{1,0:T(8,128)(2,1)}, u32[]{:S(2)}, u32[]{:S(2)}) collective-permute-start(bf16[512,1024]{1,0:T(8,128)(2,1)} %dynamic-slice_bitcast_fusion.10), channel_id=1, source_target_pairs={{0,4},{4,0},{1,5},{5,1},{2,6},{6,2},{3,7},{7,3},{8,12},{12,8},{9,1... | collective-permute-start | bytes 3145736 | tf_op jit(solution)/shard_map/ppermute | solution.py:191
  1600.7 75.9 %collective-permute-start.77 = (bf16[512,1024]{1,0:T(8,128)(2,1)S(1)}, bf16[512,1024]{1,0:T(8,128)(2,1)}, u32[]{:S(2)}, u32[]{:S(2)}) collective-permute-start(bf16[512,1024]{1,0:T(8,128)(2,1)S(1)} %get-tuple-element.75), channel_id=1, source_target_pairs={{0,2},{1,3},{2,0},{3,1},{4,6},{5,7},{6,4},{7,5},{8,10},{9,11},{10,... | collective-permute-start | bytes 3145736 | tf_op jit(solution)/shard_map/ppermute | solution.py:191
  1620.4 46.8 %collective-permute-start.76 = (bf16[512,1024]{1,0:T(8,128)(2,1)}, bf16[512,1024]{1,0:T(8,128)(2,1)}, u32[]{:S(2)}, u32[]{:S(2)}) collective-permute-start(bf16[512,1024]{1,0:T(8,128)(2,1)} %fusion.90), channel_id=1, source_target_pairs={{0,2},{1,3},{2,0},{3,1},{4,6},{5,7},{6,4},{7,5},{8,10},{9,11},{10,... | collective-permute-start | bytes 3145736 | tf_op jit(solution)/shard_map/ppermute | solution.py:191
  1625.0 51.5 %collective-permute-start.79 = (bf16[512,1024]{1,0:T(8,128)(2,1)}, bf16[512,1024]{1,0:T(8,128)(2,1)}, u32[]{:S(2)}, u32[]{:S(2)}) collective-permute-start(bf16[512,1024]{1,0:T(8,128)(2,1)} %fusion.88), channel_id=1, source_target_pairs={{0,4},{4,0},{1,5},{5,1},{2,6},{6,2},{3,7},{7,3},{8,12},{12,8},{9,1... | collective-permute-start | bytes 3145736 | tf_op jit(solution)/shard_map/ppermute | solution.py:191
  1632.6 97.0 %collective-permute-start.93 = (bf16[512,2752]{0,1:T(8,128)(2,1)}, bf16[512,2752]{0,1:T(8,128)(2,1)}, u32[]{:S(2)}, u32[]{:S(2)}) collective-permute-start(bf16[512,2752]{0,1:T(8,128)(2,1)} %dynamic-slice_bitcast_fusion.1), channel_id=1, source_target_pairs={{0,4},{4,0},{1,5},{5,1},{2,6},{6,2},{3,7},{7,3},{8,12},{12,8},{9,1... | collective-permute-start | bytes 8454152 | tf_op jit(solution)/shard_map/ppermute | solution.py:191
  1666.6 46.4 %collective-permute-start.88 = (f32[2,1024]{1,0:T(2,128)S(1)}, f32[2,1024]{1,0:T(2,128)S(1)}, u32[]{:S(2)}, u32[]{:S(2)}) collective-permute-start(f32[2,1024]{1,0:T(2,128)S(1)} %pad_maximum_fusion.8), channel_id=1, source_target_pairs={{0,4},{4,0},{1,5},{5,1},{2,6},{6,2},{3,7},{7,3},{8,12},{12,8},{9,1... | collective-permute-start | bytes 24584 | tf_op jit(solution)/shard_map/ppermute | solution.py:191
  1741.1 43.4 %collective-permute-start.95 = (bf16[512,1024]{1,0:T(8,128)(2,1)}, bf16[512,1024]{1,0:T(8,128)(2,1)S(1)}, u32[]{:S(2)}, u32[]{:S(2)}) collective-permute-start(bf16[512,1024]{1,0:T(8,128)(2,1)} %constant_dynamic-slice_fusion), channel_id=1, source_target_pairs={{0,4},{4,0},{1,5},{5,1},{2,6},{6,2},{3,7},{7,3},{8,12},{12,8},{9,1... | collective-permute-start | bytes 3145736 | tf_op jit(solution)/shard_map/ppermute | solution.py:191
  (106 other events, 2205.1 us)
Sparse Core Ops, SparseCore 0:
  11.3 220.8 all-gather.9
  233.8 78.9 all-gather.11
  314.9 381.0 all-gather.7
  697.4 195.1 all-gather.13
  895.4 188.8 reduce-scatter.5
  1086.6 373.3 reduce-scatter.11
  1462.2 78.4 reduce-scatter.9
  1543.2 144.9 reduce-scatter.13
  1690.6 77.8 reduce-scatter.7

commit v8 on v6

--- a/solution.py
+++ b/solution.py
@@ -302,7 +302,7 @@
     return jnp.where(plane() == 0, mine, other), jnp.where(plane() == 0, other, mine)
 
 
-def pair_share(block, axis, token, hold):
+def pair_share(block, axis):
     count = 2 * lax.axis_size("ctx")
     size = block.shape[axis] // count
     place = lax.axis_index("ctx") * 2
@@ -310,8 +310,7 @@
     def columns(index):
         return lax.dynamic_slice_in_dim(block, (place + index) * size, size, axis)
 
-    other = near(after(columns(1 - plane()), token))
-    return jnp.stack(in_pair(columns(plane()), after(other, hold)))
+    return jnp.stack(in_pair(columns(plane()), near(columns(1 - plane()))))
 
 
 def pair_grad(block, axis):
@@ -378,6 +377,9 @@
 
         return jnp.stack([block(t).astype(BF) for t in range(n_f)])
 
+    shares = (pair_share(gate_up_weight, 2).reshape(2, d_f, -1), pair_share(down_weight, 0))
+    gu_full = far_spread(shares[0])
+    down_full = far_spread(shares[1])
     input_float = layer_input.astype(F32)
     attn_scale = attn_gain.astype(F32)
     ffn_scale = ffn_gain.astype(F32)
@@ -389,21 +391,18 @@
     seq_len = attn_full.shape[1]
     cosine, sine = rope_tables(seq_len)
     cotans = [gather_rows(after(cotangent, attn_full))]
-    proj = after([into(attn_full, part) for part in qkv_parts], cotans[0])
+    full = after(attn_full, (cotans[0], shares))
+    proj = [into(full, part) for part in qkv_parts]
     queries, keys, values, head_outs, norms = attend_forward(*proj, cosine, sine)
     sums = core_sums(out_blocks(head_outs, out_full))
-    gu_share = pair_share(gate_up_weight, 2, tuple(proj), tuple(sums.values()))
-    gu_full = far_spread(gu_share.reshape(2, d_f, -1))
-    down_share = pair_share(down_weight, 0, gu_share, gu_share)
-    resid = after(input_float + scatter_sums(sums), down_share)
+    resid = input_float + scatter_sums(sums)
     rms_two = lax.rsqrt(row_total(jnp.sum(resid * resid, axis=-1)) / D + rms_epsilon)[:, None]
     normed_ffn = (resid * rms_two * ffn_scale).astype(BF)
-    down_full = far_spread(down_share)
     tokens = [gather_rows(normed_ffn), gather_rows(near(normed_ffn))]
-    cotans.append(gather_rows(after(near(after(cotangent, tokens[0])), tokens[1])))
+    gate_ups = [into(part, gu_full) for part in tokens]
+    cotans.append(gather_rows(after(near(after(cotangent, normed_ffn)), gate_ups[0])))
     inner = []
-    for part in tokens:
-        gate_up = into(part, gu_full)
+    for gate_up in gate_ups:
         units = gate_up.shape[1] // 2
         gate = gate_up[:, :units]
         up_value = gate_up[:, units:]
@@ -456,15 +455,11 @@
     grad_proj = attend_backward(
         queries, keys, values, head_outs, norms, grad_heads, cosine, sine
     )
-    qkv_part = [
-        in_part(attn_full, jnp.concatenate(grad_proj[1:], axis=1)),
-        in_part(attn_full, grad_proj[0]),
-    ]
-    qkv_sum = [owners(part) for part in qkv_part]
-    grad_proj = after(grad_proj, (layer_output, gate_grad))
-    grad_nattn = scatter_rows(
-        in_blocks(jnp.concatenate(grad_proj, axis=1), jnp.concatenate(qkv_parts, axis=2))
-    )
+    joined = jnp.concatenate(grad_proj, axis=1)
+    qkv_part = in_part(attn_full, joined)
+    qkv_sum = owners(qkv_part)
+    joined = after(joined, (layer_output, gate_grad, qkv_part))
+    grad_nattn = scatter_rows(in_blocks(joined, jnp.concatenate(qkv_parts, axis=2)))
     attn_term = grad_nattn * attn_scale
     attn_dot = row_total(jnp.sum(attn_term * input_float, axis=-1))[:, None]
     grad_input = grad_resid + rms_one * attn_term - input_float * rms_one**3 * attn_dot / D
@@ -476,15 +471,15 @@
     ).astype(F32)
     out_weight_grad = out_grad(out_sum)
     done = (down_grad, out_weight_grad, gu_grad, grad_input, layer_output, gain_grads)
-    qkv_grad = []
-    for part in qkv_sum:
-        first, second = trade_ctx(after(part, done), 0)
-        wide = queries.shape[1]
-        for i in range(0, first.shape[1], wide):
-            both = [first[:, i : i + wide], second[:, i : i + wide]]
-            qkv_grad.append(jnp.concatenate(both, axis=1).astype(F32))
-        done = done + (qkv_grad[-1],)
-    qkv_grad = jnp.stack([qkv_grad[2], qkv_grad[0], qkv_grad[1]], axis=1)
+    halves = trade_ctx(after(qkv_sum, done), 0)
+    wide = queries.shape[1]
+    qkv_grad = jnp.stack(
+        [
+            jnp.concatenate([v[:, i * wide : (i + 1) * wide] for v in halves], axis=1)
+            for i in range(3)
+        ],
+        axis=1,
+    ).astype(F32)
 
     return (
         layer_output,

time: 2090 us -> 2260 us (1.081)
  waiting for transfers between devices: 981 us -> 1140 us
  local copies, waits for them, and re-layouts: 175 us -> 231 us
    ppermute x150 -> x149, waiting for transfers between devices: 945 us -> 1110 us  [swap(): lax.ppermute(values, axis, [(i, i ^ step) for i in range(lax.axis_size(ax...]
    dynamic_update_slice x96, local copies, waits for them, and re-layouts: 73.7 us -> 111 us  [gather_rows(): full = lax.dynamic_update_slice(full, piece[None], start)]
    dot_general x50 -> x49, matrix products: 536 us -> 518 us  [mm(): return lax.dot_general(left, right, dims, preferred_element_type=F32)]
    ppermute x150 -> x149, starting transfers between devices: 115 us -> 103 us  [swap(): lax.ppermute(values, axis, [(i, i ^ step) for i in range(lax.axis_size(ax...]
  transfers between devices with their start and end apart: 160 -> 158, of which waited for: 59 -> 48; matrix products, arithmetic and copies ran while one was open for 37% -> 35% of each run, Pallas kernels for 4% -> 4%
where the time goes in v8:
time: 2260 us; the launch traced here: 2250 us
  waiting for transfers between devices  1140 us (50%)
  matrix products  518 us (23%)
  local copies, waits for them, and re-layouts  231 us (10%)
  other arithmetic  139 us (6%)
  starting transfers between devices  105 us (5%)
  Pallas kernels  79 us (3%)
  blocking collectives  26.2 us (1%)
    ppermute x149, waiting for transfers between devices, swap(): lax.ppermute(values, axis, [(i, i ^ step) for i in range(lax.axis_size(ax...  1110 us
    dot_general x49, matrix products, mm(): return lax.dot_general(left, right, dims, preferred_element_type=F32)  518 us
    dynamic_update_slice x96, local copies, waits for them, and re-layouts, gather_rows(): full = lax.dynamic_update_slice(full, piece[None], start)  111 us
    ppermute x149, starting transfers between devices, swap(): lax.ppermute(values, axis, [(i, i ^ step) for i in range(lax.axis_size(ax...  103 us
  transfers between devices with their start and end apart: 158, of which 48 were waited for; matrix products, arithmetic and copies ran while one was open for 35% of the time, Pallas kernels for 4%

profile of v8, /device:TPU:0, one launch (start us, length us, event | category | flops | bytes accessed | tf_op | source)
XLA Modules:
  0.0 2251.5 jit_solution(34126843742801497)
XLA Ops:
  36.2 16.1 collective-permute-done
  79.3 19.3 collective-permute-done.2
  107.3 10.3 collective-permute-done.9
  141.0 180.1 %collective-permute-done.28 = bf16[688,1024]{1,0:T(8,128)(2,1)} collective-permute-done((bf16[688,1024]{1,0:T(8,128)(2,1)}, bf16[688,1024]{1,0:T(8,128)(2,1)}, u32[]{:S(2)}, u32[]{:S(2)}) %collective-permute-start.28) | collective-permute-done | bytes 1409056 | tf_op jit(solution)/shard_map/ppermute | solution.py:191
  351.5 20.9 collective-permute-done.21
  376.1 17.9 collective-permute-done.16
  411.4 15.2 convolution_bitcast_fusion.2.v_in
  426.6 13.7 convolution_bitcast_fusion.3.k_in
  440.3 13.7 convolution_bitcast_fusion.4.q_in
  453.9 35.1 %shard_map.143 = (bf16[2048,512]{1,0:T(8,128)(2,1)S(1)}, bf16[2048,512]{1,0:T(8,128)(2,1)}, bf16[2048,512]{1,0:T(8,128)(2,1)}, bf16[2048,512]{1,0:T(8,128)(2,1)}, f32[4,1,2048]{2,1,0:T(1,128)S(1)}) custom-call(f32[2048,512]{1,0:T(8,128)} %convolution_bitcast_fusion.4.q_in, f32[2048,512]{1,0:T(8,128)} %convolution_bitcast_fusion.3.k_in, ...), custom_call_target="tpu_custom_call" | custom-call | flops 40265318400 | bytes 20971520 | tf_op jit(solution)/shard_map/pallas_call | solution.py:88
  524.3 16.2 collective-permute-done.32
  544.9 18.1 collective-permute-done.30
  567.7 20.1 collective-permute-done.34
  607.5 21.9 collective-permute-done.37
  642.9 12.8 collective-permute-done.39
  660.5 15.2 collective-permute-done.44
  680.7 117.0 %collective-permute-done.52 = bf16[1024,1024]{1,0:T(8,128)(2,1)} collective-permute-done((bf16[1024,1024]{1,0:T(8,128)(2,1)}, bf16[1024,1024]{1,0:T(8,128)(2,1)}, u32[]{:S(2)}, u32[]{:S(2)}) %collective-permute-start.52) | collective-permute-done | bytes 2097184 | tf_op jit(solution)/shard_map/ppermute | solution.py:191
  823.8 28.0 %convolution_bitcast_fusion.1 = f32[2048,1376]{0,1:T(8,128)S(1)} fusion(bf16[4,2048,1024]{2,1,0:T(8,128)(2,1)} %bitcast_dynamic-update-slice_fusion.48, bf16[4,1024,1376]{1,2,0:T(8,128)(2,1)} %bitcast.745), kind=kOutput, calls=%fused_computation.11 | convolution fusion | flops 23085449216 | bytes 39321600 | tf_op jit(solution)/shard_map/dot_general | solution.py:21
  851.8 51.2 %collective-permute-done.67 = bf16[1024,1024]{1,0:T(8,128)(2,1)} collective-permute-done((bf16[1024,1024]{1,0:T(8,128)(2,1)}, bf16[1024,1024]{1,0:T(8,128)(2,1)}, u32[]{:S(2)}, u32[]{:S(2)}) %collective-permute-start.67) | collective-permute-done | bytes 2097184 | tf_op jit(solution)/shard_map/ppermute | solution.py:191
  938.8 15.8 collective-permute-done.69
  962.9 22.0 collective-permute-done.62
  999.2 19.1 collective-permute-done.70
  1019.9 31.2 %convolution_bitcast_fusion = f32[2048,1376]{0,1:T(8,128)} fusion(bf16[4,2048,1024]{2,1,0:T(8,128)(2,1)} %bitcast_dynamic-update-slice_fusion.32, bf16[4,1024,1376]{1,2,0:T(8,128)(2,1)} %bitcast.746), kind=kOutput, calls=%fused_computation.10 | convolution fusion | flops 23085449216 | bytes 39321600 | tf_op jit(solution)/shard_map/dot_general | solution.py:21
  1107.3 20.3 fusion.3
  1127.6 12.2 convolution_convert_fusion.9
  1140.3 10.2 convolution_convert_fusion.10
  1150.6 22.0 fusion.8
  1175.8 12.9 add_convert_fusion.10
  1188.7 11.0 add_convert_fusion.11
  1199.6 10.3 convolution_convert_fusion.8
  1210.5 11.3 convolution_convert_fusion.7
  1233.9 15.8 collective-permute-done.93
  1258.4 11.1 add_convert_fusion.9
  1269.5 11.1 add_convert_fusion.8
  1280.6 17.9 fusion.51
  1298.5 20.9 add_convert_fusion.1
  1319.3 22.3 reduce-scatter.6.cloned.1.call-done
  1352.1 18.3 fusion.48
  1382.2 19.7 add_convert_fusion
  1402.0 20.5 collective-permute-done.88
  1426.7 12.6 collective-permute-done.98
  1471.0 11.3 collective-permute-done.99
  1514.8 13.7 collective-permute-done.119
  1535.9 19.0 collective-permute-done.124
  1554.8 18.9 collective-permute-done.125
  1578.4 13.0 bitcast_convert_fusion.g
  1645.6 43.9 %shard_map.144 = (bf16[2048,512]{1,0:T(8,128)(2,1)S(1)}, bf16[2048,512]{1,0:T(8,128)(2,1)}, bf16[2048,512]{1,0:T(8,128)(2,1)}) custom-call(bf16[2048,512]{1,0:T(8,128)(2,1)} %copy-done.2, bf16[2048,512]{1,0:T(8,128)(2,1)} %get-tuple-element.45.k, bf16[2048,512]{1,0:T(8,128)(2,1)} %get-tuple-element.46.v, bf16[2048,512]{1,0:T(8,128)(2,1)} %get-tuple-element.34.o, ...), custom_call_target="tpu_custom_call" | custom-call | flops 51002736640 | bytes 16777216 | tf_op jit(solution)/shard_map/pallas_call | solution.py:164
  1694.6 30.8 %convolution_convert_fusion = bf16[4,1024,1536]{2,1,0:T(8,128)(2,1)} fusion(bf16[4,2048,1024]{2,1,0:T(8,128)(2,1)} %bitcast_dynamic-update-slice_fusion.80, bf16[2048,1536]{1,0:T(8,128)(2,1)S(1)} %constant_dynamic-update-slice_fusion), kind=kOutput, calls=%fused_computation | convolution fusion | flops 25776095232 | bytes 35651584 | tf_op jit(solution)/shard_map/dot_general | solution.py:21
  1725.4 9.8 slice_bitcast_fusion.26
  1749.0 12.9 collective-permute-done.112
  1769.8 35.5 %collective-permute-done.104 = bf16[512,1024]{1,0:T(8,128)(2,1)S(1)} collective-permute-done((bf16[512,1024]{1,0:T(8,128)(2,1)S(1)}, bf16[512,1024]{1,0:T(8,128)(2,1)S(1)}, u32[]{:S(2)}, u32[]{:S(2)}) %collective-permute-start.104) | collective-permute-done | bytes 1048608 | tf_op jit(solution)/shard_map/ppermute | solution.py:191
  1816.7 15.8 collective-permute-done.113
  1840.4 64.1 %collective-permute-done.132 = bf16[1024,688]{0,1:T(8,128)(2,1)S(1)} collective-permute-done((bf16[1024,688]{0,1:T(8,128)(2,1)S(1)}, bf16[1024,688]{0,1:T(8,128)(2,1)S(1)}, u32[]{:S(2)}, u32[]{:S(2)}) %collective-permute-start.132) | collective-permute-done | bytes 1409056 | tf_op jit(solution)/shard_map/ppermute | solution.py:191
  1912.4 97.1 %collective-permute-done.117 = bf16[1024,1024]{1,0:T(8,128)(2,1)S(1)} collective-permute-done((bf16[1024,1024]{1,0:T(8,128)(2,1)S(1)}, bf16[1024,1024]{1,0:T(8,128)(2,1)S(1)}, u32[]{:S(2)}, u32[]{:S(2)}) %collective-permute-start.117) | collective-permute-done | bytes 2097184 | tf_op jit(solution)/shard_map/ppermute | solution.py:191
  2018.4 10.4 convolution_convert_fusion.1
  2028.8 16.6 collective-permute-done.146
  2049.6 10.1 convolution_convert_fusion.2
  2060.8 30.3 %collective-permute-done.145 = bf16[512,512]{1,0:T(8,128)(2,1)S(1)} collective-permute-done((bf16[512,512]{1,0:T(8,128)(2,1)S(1)}, bf16[512,512]{1,0:T(8,128)(2,1)S(1)}, u32[]{:S(2)}, u32[]{:S(2)}) %collective-permute-start.145) | collective-permute-done | bytes 524320 | tf_op jit(solution)/shard_map/ppermute | solution.py:191
  2095.9 10.9 add_convert_fusion.2
  2109.7 9.7 add_convert_fusion.3
  2122.2 11.4 collective-permute-done.137
  2137.6 18.4 collective-permute-done.135
  2156.1 21.3 collective-permute-done.138
  2204.4 34.9 %collective-permute-done.148 = bf16[512,1536]{1,0:T(8,128)(2,1)S(1)} collective-permute-done((bf16[512,1536]{1,0:T(8,128)(2,1)S(1)}, bf16[512,1536]{1,0:T(8,128)(2,1)S(1)}, u32[]{:S(2)}, u32[]{:S(2)}) %collective-permute-start.148) | collective-permute-done | bytes 1572896 | tf_op jit(solution)/shard_map/ppermute | solution.py:191
  (759 shorter events, 662.3 us)
Async XLA Ops:
  8.0 403.4 %all-gather.10.cloned.1.call-start = ((), (), s32[]{:S(2)}) async-start(), calls=%async_computation.11 | async-start | bytes 15728640 | tf_op jit(solution)/shard_map/all_gather | solution.py:324
  12.0 478.3 %all-gather.12.cloned.1.call-start = ((), (), s32[]{:S(2)}) async-start(), calls=%async_computation.12 | async-start | bytes 5242880 | tf_op jit(solution)/shard_map/all_gather | solution.py:324
  30.4 48.4 %collective-permute-start.7 = (bf16[512,1024]{1,0:T(8,128)(2,1)}, bf16[512,1024]{1,0:T(8,128)(2,1)S(1)}, u32[]{:S(2)}, u32[]{:S(2)}) collective-permute-start(bf16[512,1024]{1,0:T(8,128)(2,1)} %get-tuple-element.135), channel_id=1, source_target_pairs={{0,2},{1,3},{2,0},{3,1},{4,6},{5,7},{6,4},{7,5},{8,10},{9,11},{10,... | collective-permute-start | bytes 3145736 | tf_op jit(solution)/shard_map/ppermute | solution.py:191
  33.1 790.7 %all-gather.8.cloned.1.call-start = ((), (), s32[]{:S(2)}) async-start(), calls=%async_computation.5 | async-start | bytes 16908288 | tf_op jit(solution)/shard_map/all_gather | solution.py:287
  104.7 224.4 %collective-permute-start.51 = (bf16[1024,2,688]{0,2,1:T(8,128)(2,1)}, bf16[1024,2,688]{0,2,1:T(8,128)(2,1)}, u32[]{:S(2)}, u32[]{:S(2)}) collective-permute-start(bf16[1024,2,688]{0,2,1:T(8,128)(2,1)} %constant_dynamic-slice_fusion.1), channel_id=1, source_target_pairs={{0,8},{8,0},{16,24},{24,16},{1,9},{9,1},{17,25},{25,17},{2,10},{10... | collective-permute-start | bytes 8454152 | tf_op jit(solution)/shard_map/ppermute | solution.py:191
  123.5 197.6 %collective-permute-start.28 = (bf16[688,1024]{1,0:T(8,128)(2,1)}, bf16[688,1024]{1,0:T(8,128)(2,1)}, u32[]{:S(2)}, u32[]{:S(2)}) collective-permute-start(bf16[688,1024]{1,0:T(8,128)(2,1)} %constant_dynamic-slice_fusion.3), channel_id=1, source_target_pairs={{0,8},{8,0},{16,24},{24,16},{1,9},{9,1},{17,25},{25,17},{2,10},{10... | collective-permute-start | bytes 4227080 | tf_op jit(solution)/shard_map/ppermute | solution.py:191
  132.3 195.3 %collective-permute-start.14 = (bf16[512,1024]{1,0:T(8,128)(2,1)}, bf16[512,1024]{1,0:T(8,128)(2,1)}, u32[]{:S(2)}, u32[]{:S(2)}) collective-permute-start(bf16[512,1024]{1,0:T(8,128)(2,1)} %get-tuple-element.134), channel_id=1, source_target_pairs={{0,4},{4,0},{1,5},{5,1},{2,6},{6,2},{3,7},{7,3},{8,12},{12,8},{9,1... | collective-permute-start | bytes 3145736 | tf_op jit(solution)/shard_map/ppermute | solution.py:191
  325.2 47.2 %collective-permute-start.21 = (bf16[512,1024]{1,0:T(8,128)(2,1)}, bf16[512,1024]{1,0:T(8,128)(2,1)S(1)}, u32[]{:S(2)}, u32[]{:S(2)}) collective-permute-start(bf16[512,1024]{1,0:T(8,128)(2,1)} %get-tuple-element.133), channel_id=1, source_target_pairs={{0,2},{1,3},{2,0},{3,1},{4,6},{5,7},{6,4},{7,5},{8,10},{9,11},{10,... | collective-permute-start | bytes 3145736 | tf_op jit(solution)/shard_map/ppermute | solution.py:191
  327.7 66.4 %collective-permute-start.16 = (bf16[512,1024]{1,0:T(8,128)(2,1)}, bf16[512,1024]{1,0:T(8,128)(2,1)S(1)}, u32[]{:S(2)}, u32[]{:S(2)}) collective-permute-start(bf16[512,1024]{1,0:T(8,128)(2,1)} %collective-permute-done.14), channel_id=1, source_target_pairs={{0,2},{1,3},{2,0},{3,1},{4,6},{5,7},{6,4},{7,5},{8,10},{9,11},{10,... | collective-permute-start | bytes 3145736 | tf_op jit(solution)/shard_map/ppermute | solution.py:191
  344.9 52.5 %collective-permute-start.18 = (bf16[512,1024]{1,0:T(8,128)(2,1)}, bf16[512,1024]{1,0:T(8,128)(2,1)S(1)}, u32[]{:S(2)}, u32[]{:S(2)}) collective-permute-start(bf16[512,1024]{1,0:T(8,128)(2,1)} %collective-permute-done.14), channel_id=1, source_target_pairs={{0,1},{1,0},{2,3},{3,2},{4,5},{5,4},{6,7},{7,6},{8,9},{9,8},{10,11... | collective-permute-start | bytes 3145736 | tf_op jit(solution)/shard_map/ppermute | solution.py:191
  350.0 48.9 %collective-permute-start.22 = (bf16[512,1024]{1,0:T(8,128)(2,1)}, bf16[512,1024]{1,0:T(8,128)(2,1)S(1)}, u32[]{:S(2)}, u32[]{:S(2)}) collective-permute-start(bf16[512,1024]{1,0:T(8,128)(2,1)} %get-tuple-element.133), channel_id=1, source_target_pairs={{0,4},{4,0},{1,5},{5,1},{2,6},{6,2},{3,7},{7,3},{8,12},{12,8},{9,1... | collective-permute-start | bytes 3145736 | tf_op jit(solution)/shard_map/ppermute | solution.py:191
  351.5 47.5 %collective-permute-start.19 = (bf16[512,1024]{1,0:T(8,128)(2,1)}, bf16[512,1024]{1,0:T(8,128)(2,1)S(1)}, u32[]{:S(2)}, u32[]{:S(2)}) collective-permute-start(bf16[512,1024]{1,0:T(8,128)(2,1)} %collective-permute-done.15), channel_id=1, source_target_pairs={{0,1},{1,0},{2,3},{3,2},{4,5},{5,4},{6,7},{7,6},{8,9},{9,8},{10,11... | collective-permute-start | bytes 3145736 | tf_op jit(solution)/shard_map/ppermute | solution.py:191
  500.1 607.3 %all-gather.14.cloned.1.call-start = ((), (), s32[]{:S(2)}) async-start(), calls=%async_computation.13 | async-start | bytes 8454144 | tf_op jit(solution)/shard_map/all_gather | solution.py:287
  630.9 166.9 %collective-permute-start.52 = (bf16[1024,1024]{1,0:T(8,128)(2,1)}, bf16[1024,1024]{1,0:T(8,128)(2,1)}, u32[]{:S(2)}, u32[]{:S(2)}) collective-permute-start(bf16[1024,1024]{1,0:T(8,128)(2,1)} %multiply_convert_fusion.2), channel_id=1, source_target_pairs={{0,8},{8,0},{16,24},{24,16},{1,9},{9,1},{17,25},{25,17},{2,10},{10... | collective-permute-start | bytes 6291464 | tf_op jit(solution)/shard_map/ppermute | solution.py:191
  630.9 710.7 %reduce-scatter.6.cloned.1.call-start = ((), (), s32[]{:S(2)}) async-start(), calls=%async_computation.6 | async-start | bytes 8454144 | tf_op jit(solution)/shard_map/reduce_scatter | solution.py:281
  659.1 150.0 %collective-permute-start.45 = (bf16[512,1024]{1,0:T(8,128)(2,1)S(1)}, bf16[512,1024]{1,0:T(8,128)(2,1)S(1)}, u32[]{:S(2)}, u32[]{:S(2)}) collective-permute-start(bf16[512,1024]{1,0:T(8,128)(2,1)S(1)} %copy-done.66), channel_id=1, source_target_pairs={{0,4},{4,0},{1,5},{5,1},{2,6},{6,2},{3,7},{7,3},{8,12},{12,8},{9,1... | collective-permute-start | bytes 3145736 | tf_op jit(solution)/shard_map/ppermute | solution.py:191
  675.7 133.4 %collective-permute-start.46 = (bf16[512,1024]{1,0:T(8,128)(2,1)S(1)}, bf16[512,1024]{1,0:T(8,128)(2,1)S(1)}, u32[]{:S(2)}, u32[]{:S(2)}) collective-permute-start(bf16[512,1024]{1,0:T(8,128)(2,1)S(1)} %collective-permute-done.44), channel_id=1, source_target_pairs={{0,4},{4,0},{1,5},{5,1},{2,6},{6,2},{3,7},{7,3},{8,12},{12,8},{9,1... | collective-permute-start | bytes 3145736 | tf_op jit(solution)/shard_map/ppermute | solution.py:191
  678.1 131.4 %collective-permute-start.43 = (bf16[512,1024]{1,0:T(8,128)(2,1)S(1)}, bf16[512,1024]{1,0:T(8,128)(2,1)S(1)}, u32[]{:S(2)}, u32[]{:S(2)}) collective-permute-start(bf16[512,1024]{1,0:T(8,128)(2,1)S(1)} %collective-permute-done.39), channel_id=1, source_target_pairs={{0,1},{1,0},{2,3},{3,2},{4,5},{5,4},{6,7},{7,6},{8,9},{9,8},{10,11... | collective-permute-start | bytes 3145736 | tf_op jit(solution)/shard_map/ppermute | solution.py:191
  679.2 137.0 %collective-permute-start.47 = (bf16[512,1024]{1,0:T(8,128)(2,1)S(1)}, bf16[512,1024]{1,0:T(8,128)(2,1)S(1)}, u32[]{:S(2)}, u32[]{:S(2)}) collective-permute-start(bf16[512,1024]{1,0:T(8,128)(2,1)S(1)} %copy-done.66), channel_id=1, source_target_pairs={{0,1},{1,0},{2,3},{3,2},{4,5},{5,4},{6,7},{7,6},{8,9},{9,8},{10,11... | collective-permute-start | bytes 3145736 | tf_op jit(solution)/shard_map/ppermute | solution.py:191
  797.8 105.3 %collective-permute-start.67 = (bf16[1024,1024]{1,0:T(8,128)(2,1)}, bf16[1024,1024]{1,0:T(8,128)(2,1)}, u32[]{:S(2)}, u32[]{:S(2)}) collective-permute-start(bf16[1024,1024]{1,0:T(8,128)(2,1)} %param.15), channel_id=1, source_target_pairs={{0,8},{8,0},{16,24},{24,16},{1,9},{9,1},{17,25},{25,17},{2,10},{10... | collective-permute-start | bytes 6291464 | tf_op jit(solution)/shard_map/ppermute | solution.py:191
  816.2 93.1 %collective-permute-start.53 = (bf16[512,1024]{1,0:T(8,128)(2,1)}, bf16[512,1024]{1,0:T(8,128)(2,1)}, u32[]{:S(2)}, u32[]{:S(2)}) collective-permute-start(bf16[512,1024]{1,0:T(8,128)(2,1)} %get-tuple-element.128), channel_id=1, source_target_pairs={{0,4},{4,0},{1,5},{5,1},{2,6},{6,2},{3,7},{7,3},{8,12},{12,8},{9,1... | collective-permute-start | bytes 3145736 | tf_op jit(solution)/shard_map/ppermute | solution.py:191
  818.6 94.9 %collective-permute-start.54 = (bf16[512,1024]{1,0:T(8,128)(2,1)}, bf16[512,1024]{1,0:T(8,128)(2,1)}, u32[]{:S(2)}, u32[]{:S(2)}) collective-permute-start(bf16[512,1024]{1,0:T(8,128)(2,1)} %get-tuple-element.128), channel_id=1, source_target_pairs={{0,2},{1,3},{2,0},{3,1},{4,6},{5,7},{6,4},{7,5},{8,10},{9,11},{10,... | collective-permute-start | bytes 3145736 | tf_op jit(solution)/shard_map/ppermute | solution.py:191
  820.2 116.5 %collective-permute-start.56 = (bf16[512,1024]{1,0:T(8,128)(2,1)}, bf16[512,1024]{1,0:T(8,128)(2,1)}, u32[]{:S(2)}, u32[]{:S(2)}) collective-permute-start(bf16[512,1024]{1,0:T(8,128)(2,1)} %get-tuple-element.128), channel_id=1, source_target_pairs={{0,1},{1,0},{2,3},{3,2},{4,5},{5,4},{6,7},{7,6},{8,9},{9,8},{10,11... | collective-permute-start | bytes 3145736 | tf_op jit(solution)/shard_map/ppermute | solution.py:191
  821.3 116.0 %collective-permute-start.60 = (bf16[512,1024]{1,0:T(8,128)(2,1)}, bf16[512,1024]{1,0:T(8,128)(2,1)}, u32[]{:S(2)}, u32[]{:S(2)}) collective-permute-start(bf16[512,1024]{1,0:T(8,128)(2,1)} %get-tuple-element.127), channel_id=1, source_target_pairs={{0,2},{1,3},{2,0},{3,1},{4,6},{5,7},{6,4},{7,5},{8,10},{9,11},{10,... | collective-permute-start | bytes 3145736 | tf_op jit(solution)/shard_map/ppermute | solution.py:191
  937.4 47.6 %collective-permute-start.62 = (bf16[512,1024]{1,0:T(8,128)(2,1)}, bf16[512,1024]{1,0:T(8,128)(2,1)S(1)}, u32[]{:S(2)}, u32[]{:S(2)}) collective-permute-start(bf16[512,1024]{1,0:T(8,128)(2,1)} %collective-permute-done.60), channel_id=1, source_target_pairs={{0,4},{4,0},{1,5},{5,1},{2,6},{6,2},{3,7},{7,3},{8,12},{12,8},{9,1... | collective-permute-start | bytes 3145736 | tf_op jit(solution)/shard_map/ppermute | solution.py:191
  994.8 57.8 %collective-permute-start.71 = (bf16[512,1024]{1,0:T(8,128)(2,1)}, bf16[512,1024]{1,0:T(8,128)(2,1)}, u32[]{:S(2)}, u32[]{:S(2)}) collective-permute-start(bf16[512,1024]{1,0:T(8,128)(2,1)} %get-tuple-element.126), channel_id=1, source_target_pairs={{0,1},{1,0},{2,3},{3,2},{4,5},{5,4},{6,7},{7,6},{8,9},{9,8},{10,11... | collective-permute-start | bytes 3145736 | tf_op jit(solution)/shard_map/ppermute | solution.py:191
  995.8 58.2 %collective-permute-start.76 = (bf16[512,1024]{1,0:T(8,128)(2,1)}, bf16[512,1024]{1,0:T(8,128)(2,1)}, u32[]{:S(2)}, u32[]{:S(2)}) collective-permute-start(bf16[512,1024]{1,0:T(8,128)(2,1)} %get-tuple-element.125), channel_id=1, source_target_pairs={{0,4},{4,0},{1,5},{5,1},{2,6},{6,2},{3,7},{7,3},{8,12},{12,8},{9,1... | collective-permute-start | bytes 3145736 | tf_op jit(solution)/shard_map/ppermute | solution.py:191
  997.6 57.0 %collective-permute-start.72 = (bf16[512,1024]{1,0:T(8,128)(2,1)S(1)}, bf16[512,1024]{1,0:T(8,128)(2,1)}, u32[]{:S(2)}, u32[]{:S(2)}) collective-permute-start(bf16[512,1024]{1,0:T(8,128)(2,1)S(1)} %collective-permute-done.68), channel_id=1, source_target_pairs={{0,1},{1,0},{2,3},{3,2},{4,5},{5,4},{6,7},{7,6},{8,9},{9,8},{10,11... | collective-permute-start | bytes 3145736 | tf_op jit(solution)/shard_map/ppermute | solution.py:191
  998.9 57.1 %collective-permute-start.73 = (bf16[512,1024]{1,0:T(8,128)(2,1)S(1)}, bf16[512,1024]{1,0:T(8,128)(2,1)}, u32[]{:S(2)}, u32[]{:S(2)}) collective-permute-start(bf16[512,1024]{1,0:T(8,128)(2,1)S(1)} %collective-permute-done.69), channel_id=1, source_target_pairs={{0,1},{1,0},{2,3},{3,2},{4,5},{5,4},{6,7},{7,6},{8,9},{9,8},{10,11... | collective-permute-start | bytes 3145736 | tf_op jit(solution)/shard_map/ppermute | solution.py:191
  1210.0 46.9 %collective-permute-start.84 = (bf16[2048,1024]{1,0:T(8,128)(2,1)}, bf16[2048,1024]{1,0:T(8,128)(2,1)}, u32[]{:S(2)}, u32[]{:S(2)}) collective-permute-start(bf16[2048,1024]{1,0:T(8,128)(2,1)} %convolution_convert_fusion.8), channel_id=1, source_target_pairs={{0,1},{1,0},{2,3},{3,2},{4,5},{5,4},{6,7},{7,6},{8,9},{9,8},{10,11... | collective-permute-start | bytes 12582920 | tf_op jit(solution)/shard_map/ppermute | solution.py:191
  1210.4 596.3 %reduce-scatter.8.cloned.1.call-start = ((), (), s32[]{:S(2)}) async-start(), calls=%async_computation.7 | async-start | bytes 8454144 | tf_op jit(solution)/shard_map/reduce_scatter | solution.py:281
  1221.8 47.7 %collective-permute-start.86 = (bf16[2048,1024]{1,0:T(8,128)(2,1)}, bf16[2048,1024]{1,0:T(8,128)(2,1)}, u32[]{:S(2)}, u32[]{:S(2)}) collective-permute-start(bf16[2048,1024]{1,0:T(8,128)(2,1)} %convolution_convert_fusion.7), channel_id=1, source_target_pairs={{0,1},{1,0},{2,3},{3,2},{4,5},{5,4},{6,7},{7,6},{8,9},{9,8},{10,11... | collective-permute-start | bytes 12582920 | tf_op jit(solution)/shard_map/ppermute | solution.py:191
  1233.2 108.5 %collective-permute-start.92 = (bf16[512,1024]{1,0:T(8,128)(2,1)}, bf16[512,1024]{1,0:T(8,128)(2,1)}, u32[]{:S(2)}, u32[]{:S(2)}) collective-permute-start(bf16[512,1024]{1,0:T(8,128)(2,1)} %dynamic-slice_bitcast_fusion.19), channel_id=1, source_target_pairs={{0,4},{4,0},{1,5},{5,1},{2,6},{6,2},{3,7},{7,3},{8,12},{12,8},{9,1... | collective-permute-start | bytes 3145736 | tf_op jit(solution)/shard_map/ppermute | solution.py:191
  1249.7 94.7 %collective-permute-start.95 = (bf16[512,1024]{1,0:T(8,128)(2,1)S(1)}, bf16[512,1024]{1,0:T(8,128)(2,1)}, u32[]{:S(2)}, u32[]{:S(2)}) collective-permute-start(bf16[512,1024]{1,0:T(8,128)(2,1)S(1)} %get-tuple-element.121), channel_id=1, source_target_pairs={{0,2},{1,3},{2,0},{3,1},{4,6},{5,7},{6,4},{7,5},{8,10},{9,11},{10,... | collective-permute-start | bytes 3145736 | tf_op jit(solution)/shard_map/ppermute | solution.py:191
  1252.8 88.9 %collective-permute-start.94 = (bf16[512,1024]{1,0:T(8,128)(2,1)}, bf16[512,1024]{1,0:T(8,128)(2,1)}, u32[]{:S(2)}, u32[]{:S(2)}) collective-permute-start(bf16[512,1024]{1,0:T(8,128)(2,1)} %fusion.103), channel_id=1, source_target_pairs={{0,2},{1,3},{2,0},{3,1},{4,6},{5,7},{6,4},{7,5},{8,10},{9,11},{10,... | collective-permute-start | bytes 3145736 | tf_op jit(solution)/shard_map/ppermute | solution.py:191
  1256.9 87.5 %collective-permute-start.97 = (bf16[512,1024]{1,0:T(8,128)(2,1)}, bf16[512,1024]{1,0:T(8,128)(2,1)}, u32[]{:S(2)}, u32[]{:S(2)}) collective-permute-start(bf16[512,1024]{1,0:T(8,128)(2,1)} %fusion.100), channel_id=1, source_target_pairs={{0,4},{4,0},{1,5},{5,1},{2,6},{6,2},{3,7},{7,3},{8,12},{12,8},{9,1... | collective-permute-start | bytes 3145736 | tf_op jit(solution)/shard_map/ppermute | solution.py:191
  1341.7 670.5 %reduce-scatter.14.cloned.1.call-start = ((), (), s32[]{:S(2)}) async-start(), calls=%async_computation.10 | async-start | bytes 8454144 | tf_op jit(solution)/shard_map/reduce_scatter | solution.py:281
  1348.3 91.0 %collective-permute-start.98 = (bf16[1024,1024]{1,0:T(8,128)(2,1)}, bf16[1024,1024]{1,0:T(8,128)(2,1)S(1)}, u32[]{:S(2)}, u32[]{:S(2)}) collective-permute-start(bf16[1024,1024]{1,0:T(8,128)(2,1)} %pad_maximum_fusion.8), channel_id=1, source_target_pairs={{0,8},{8,0},{16,24},{24,16},{1,9},{9,1},{17,25},{25,17},{2,10},{10... | collective-permute-start | bytes 6291464 | tf_op jit(solution)/shard_map/ppermute | solution.py:191
  1375.4 49.2 %collective-permute-start.89 = (bf16[512,1024]{1,0:T(8,128)(2,1)S(1)}, bf16[512,1024]{1,0:T(8,128)(2,1)}, u32[]{:S(2)}, u32[]{:S(2)}) collective-permute-start(bf16[512,1024]{1,0:T(8,128)(2,1)S(1)} %get-tuple-element.123), channel_id=1, source_target_pairs={{0,2},{1,3},{2,0},{3,1},{4,6},{5,7},{6,4},{7,5},{8,10},{9,11},{10,... | collective-permute-start | bytes 3145736 | tf_op jit(solution)/shard_map/ppermute | solution.py:191
  1460.6 52.3 %collective-permute-start.118 = (bf16[512,1024]{1,0:T(8,128)(2,1)}, bf16[512,1024]{1,0:T(8,128)(2,1)}, u32[]{:S(2)}, u32[]{:S(2)}) collective-permute-start(bf16[512,1024]{1,0:T(8,128)(2,1)} %get-tuple-element.120), channel_id=1, source_target_pairs={{0,2},{1,3},{2,0},{3,1},{4,6},{5,7},{6,4},{7,5},{8,10},{9,11},{10,... | collective-permute-start | bytes 3145736 | tf_op jit(solution)/shard_map/ppermute | solution.py:191
  1461.2 67.9 %collective-permute-start.120 = (bf16[512,1024]{1,0:T(8,128)(2,1)}, bf16[512,1024]{1,0:T(8,128)(2,1)}, u32[]{:S(2)}, u32[]{:S(2)}) collective-permute-start(bf16[512,1024]{1,0:T(8,128)(2,1)} %get-tuple-element.120), channel_id=1, source_target_pairs={{0,1},{1,0},{2,3},{3,2},{4,5},{5,4},{6,7},{7,6},{8,9},{9,8},{10,11... | collective-permute-start | bytes 3145736 | tf_op jit(solution)/shard_map/ppermute | solution.py:191
  1469.3 63.6 %collective-permute-start.130 = (bf16[688,1024]{1,0:T(8,128)(2,1)S(1)}, bf16[688,1024]{1,0:T(8,128)(2,1)}, u32[]{:S(2)}, u32[]{:S(2)}) collective-permute-start(bf16[688,1024]{1,0:T(8,128)(2,1)S(1)} %dynamic-slice_bitcast_fusion.3), channel_id=1, source_target_pairs={{0,8},{8,0},{16,24},{24,16},{1,9},{9,1},{17,25},{25,17},{2,10},{10... | collective-permute-start | bytes 4227080 | tf_op jit(solution)/shard_map/ppermute | solution.py:191
  1471.0 588.7 %reduce-scatter.12.cloned.1.call-start = ((), (), s32[]{:S(2)}) async-start(), calls=%async_computation.9 | async-start | bytes 5242880 | tf_op jit(solution)/shard_map/reduce_scatter | solution.py:271
  1532.9 84.1 %collective-permute-start.109 = (bf16[2048,1024]{1,0:T(8,128)(2,1)}, bf16[2048,1024]{1,0:T(8,128)(2,1)}, u32[]{:S(2)}, u32[]{:S(2)}) collective-permute-start(bf16[2048,1024]{1,0:T(8,128)(2,1)} %convolution_convert_fusion.4), channel_id=1, source_target_pairs={{0,1},{1,0},{2,3},{3,2},{4,5},{5,4},{6,7},{7,6},{8,9},{9,8},{10,11... | collective-permute-start | bytes 12582920 | tf_op jit(solution)/shard_map/ppermute | solution.py:191
  1576.1 49.0 %collective-permute-start.111 = (bf16[2048,1024]{1,0:T(8,128)(2,1)}, bf16[2048,1024]{1,0:T(8,128)(2,1)}, u32[]{:S(2)}, u32[]{:S(2)}) collective-permute-start(bf16[2048,1024]{1,0:T(8,128)(2,1)} %convolution_convert_fusion.3), channel_id=1, source_target_pairs={{0,1},{1,0},{2,3},{3,2},{4,5},{5,4},{6,7},{7,6},{8,9},{9,8},{10,11... | collective-permute-start | bytes 12582920 | tf_op jit(solution)/shard_map/ppermute | solution.py:191
  1576.3 55.8 %collective-permute-start.101 = (bf16[2048,1024]{1,0:T(8,128)(2,1)}, bf16[2048,1024]{1,0:T(8,128)(2,1)}, u32[]{:S(2)}, u32[]{:S(2)}) collective-permute-start(bf16[2048,1024]{1,0:T(8,128)(2,1)} %convolution_convert_fusion.6), channel_id=1, source_target_pairs={{0,1},{1,0},{2,3},{3,2},{4,5},{5,4},{6,7},{7,6},{8,9},{9,8},{10,11... | collective-permute-start | bytes 12582920 | tf_op jit(solution)/shard_map/ppermute | solution.py:191
  1576.9 61.9 %collective-permute-start.103 = (bf16[2048,1024]{1,0:T(8,128)(2,1)}, bf16[2048,1024]{1,0:T(8,128)(2,1)}, u32[]{:S(2)}, u32[]{:S(2)}) collective-permute-start(bf16[2048,1024]{1,0:T(8,128)(2,1)} %convolution_convert_fusion.5), channel_id=1, source_target_pairs={{0,1},{1,0},{2,3},{3,2},{4,5},{5,4},{6,7},{7,6},{8,9},{9,8},{10,11... | collective-permute-start | bytes 12582920 | tf_op jit(solution)/shard_map/ppermute | solution.py:191
  1605.1 596.4 %reduce-scatter.10.cloned.1.call-start = ((), (), s32[]{:S(2)}) async-start(), calls=%async_computation.8 | async-start | bytes 15728640 | tf_op jit(solution)/shard_map/reduce_scatter | solution.py:271
  1739.0 76.1 %collective-permute-start.110 = (bf16[512,1024]{1,0:T(8,128)(2,1)}, bf16[512,1024]{1,0:T(8,128)(2,1)S(1)}, u32[]{:S(2)}, u32[]{:S(2)}) collective-permute-start(bf16[512,1024]{1,0:T(8,128)(2,1)} %dynamic-slice_bitcast_fusion.11), channel_id=1, source_target_pairs={{0,4},{4,0},{1,5},{5,1},{2,6},{6,2},{3,7},{7,3},{8,12},{12,8},{9,1... | collective-permute-start | bytes 3145736 | tf_op jit(solution)/shard_map/ppermute | solution.py:191
  1742.9 62.4 %collective-permute-start.104 = (bf16[512,1024]{1,0:T(8,128)(2,1)S(1)}, bf16[512,1024]{1,0:T(8,128)(2,1)S(1)}, u32[]{:S(2)}, u32[]{:S(2)}) collective-permute-start(bf16[512,1024]{1,0:T(8,128)(2,1)S(1)} %dynamic-slice_bitcast_fusion.14), channel_id=1, source_target_pairs={{0,4},{4,0},{1,5},{5,1},{2,6},{6,2},{3,7},{7,3},{8,12},{12,8},{9,1... | collective-permute-start | bytes 3145736 | tf_op jit(solution)/shard_map/ppermute | solution.py:191
  1745.9 62.5 %collective-permute-start.107 = (bf16[512,1024]{1,0:T(8,128)(2,1)}, bf16[512,1024]{1,0:T(8,128)(2,1)}, u32[]{:S(2)}, u32[]{:S(2)}) collective-permute-start(bf16[512,1024]{1,0:T(8,128)(2,1)} %get-tuple-element.118), channel_id=1, source_target_pairs={{0,2},{1,3},{2,0},{3,1},{4,6},{5,7},{6,4},{7,5},{8,10},{9,11},{10,... | collective-permute-start | bytes 3145736 | tf_op jit(solution)/shard_map/ppermute | solution.py:191
  1761.9 73.9 %collective-permute-start.114 = (bf16[512,1024]{1,0:T(8,128)(2,1)}, bf16[512,1024]{1,0:T(8,128)(2,1)}, u32[]{:S(2)}, u32[]{:S(2)}) collective-permute-start(bf16[512,1024]{1,0:T(8,128)(2,1)} %get-tuple-element.115), channel_id=1, source_target_pairs={{0,2},{1,3},{2,0},{3,1},{4,6},{5,7},{6,4},{7,5},{8,10},{9,11},{10,... | collective-permute-start | bytes 3145736 | tf_op jit(solution)/shard_map/ppermute | solution.py:191
  1766.9 65.5 %collective-permute-start.113 = (bf16[512,1024]{1,0:T(8,128)(2,1)}, bf16[512,1024]{1,0:T(8,128)(2,1)}, u32[]{:S(2)}, u32[]{:S(2)}) collective-permute-start(bf16[512,1024]{1,0:T(8,128)(2,1)} %fusion.93), channel_id=1, source_target_pairs={{0,2},{1,3},{2,0},{3,1},{4,6},{5,7},{6,4},{7,5},{8,10},{9,11},{10,... | collective-permute-start | bytes 3145736 | tf_op jit(solution)/shard_map/ppermute | solution.py:191
  1808.4 96.1 %collective-permute-start.132 = (bf16[1024,688]{0,1:T(8,128)(2,1)S(1)}, bf16[1024,688]{0,1:T(8,128)(2,1)S(1)}, u32[]{:S(2)}, u32[]{:S(2)}) collective-permute-start(bf16[1024,688]{0,1:T(8,128)(2,1)S(1)} %dynamic-slice_bitcast_fusion.2), channel_id=1, source_target_pairs={{0,8},{8,0},{16,24},{24,16},{1,9},{9,1},{17,25},{25,17},{2,10},{10... | collective-permute-start | bytes 4227080 | tf_op jit(solution)/shard_map/ppermute | solution.py:191
  1815.1 90.8 %collective-permute-start.102 = (bf16[512,1024]{1,0:T(8,128)(2,1)S(1)}, bf16[512,1024]{1,0:T(8,128)(2,1)S(1)}, u32[]{:S(2)}, u32[]{:S(2)}) collective-permute-start(bf16[512,1024]{1,0:T(8,128)(2,1)S(1)} %dynamic-slice_bitcast_fusion.15), channel_id=1, source_target_pairs={{0,4},{4,0},{1,5},{5,1},{2,6},{6,2},{3,7},{7,3},{8,12},{12,8},{9,1... | collective-permute-start | bytes 3145736 | tf_op jit(solution)/shard_map/ppermute | solution.py:191
  1832.4 79.4 %collective-permute-start.106 = (bf16[512,1024]{1,0:T(8,128)(2,1)}, bf16[512,1024]{1,0:T(8,128)(2,1)S(1)}, u32[]{:S(2)}, u32[]{:S(2)}) collective-permute-start(bf16[512,1024]{1,0:T(8,128)(2,1)} %get-tuple-element.117), channel_id=1, source_target_pairs={{0,2},{1,3},{2,0},{3,1},{4,6},{5,7},{6,4},{7,5},{8,10},{9,11},{10,... | collective-permute-start | bytes 3145736 | tf_op jit(solution)/shard_map/ppermute | solution.py:191
  1835.9 75.4 %collective-permute-start.105 = (bf16[512,1024]{1,0:T(8,128)(2,1)S(1)}, bf16[512,1024]{1,0:T(8,128)(2,1)S(1)}, u32[]{:S(2)}, u32[]{:S(2)}) collective-permute-start(bf16[512,1024]{1,0:T(8,128)(2,1)S(1)} %fusion.98), channel_id=1, source_target_pairs={{0,2},{1,3},{2,0},{3,1},{4,6},{5,7},{6,4},{7,5},{8,10},{9,11},{10,... | collective-permute-start | bytes 3145736 | tf_op jit(solution)/shard_map/ppermute | solution.py:191
  1836.4 75.4 %collective-permute-start.108 = (bf16[512,1024]{1,0:T(8,128)(2,1)S(1)}, bf16[512,1024]{1,0:T(8,128)(2,1)S(1)}, u32[]{:S(2)}, u32[]{:S(2)}) collective-permute-start(bf16[512,1024]{1,0:T(8,128)(2,1)S(1)} %fusion.96), channel_id=1, source_target_pairs={{0,4},{4,0},{1,5},{5,1},{2,6},{6,2},{3,7},{7,3},{8,12},{12,8},{9,1... | collective-permute-start | bytes 3145736 | tf_op jit(solution)/shard_map/ppermute | solution.py:191
  1904.5 105.0 %collective-permute-start.117 = (bf16[1024,1024]{1,0:T(8,128)(2,1)S(1)}, bf16[1024,1024]{1,0:T(8,128)(2,1)S(1)}, u32[]{:S(2)}, u32[]{:S(2)}) collective-permute-start(bf16[1024,1024]{1,0:T(8,128)(2,1)S(1)} %pad_maximum_fusion.9), channel_id=1, source_target_pairs={{0,8},{8,0},{16,24},{24,16},{1,9},{9,1},{17,25},{25,17},{2,10},{10... | collective-permute-start | bytes 6291464 | tf_op jit(solution)/shard_map/ppermute | solution.py:191
  1905.9 107.9 %collective-permute-start.133 = (bf16[2,512,688]{1,2,0:T(8,128)(2,1)}, bf16[2,512,688]{1,2,0:T(8,128)(2,1)}, u32[]{:S(2)}, u32[]{:S(2)}) collective-permute-start(bf16[2,512,688]{1,2,0:T(8,128)(2,1)} %fusion.124), channel_id=1, source_target_pairs={{0,4},{4,0},{1,5},{5,1},{2,6},{6,2},{3,7},{7,3},{8,12},{12,8},{9,1... | collective-permute-start | bytes 4227080 | tf_op jit(solution)/shard_map/ppermute | solution.py:191
  2028.8 67.1 %collective-permute-start.136 = (bf16[2048,1024]{1,0:T(8,128)(2,1)}, bf16[2048,1024]{1,0:T(8,128)(2,1)}, u32[]{:S(2)}, u32[]{:S(2)}) collective-permute-start(bf16[2048,1024]{1,0:T(8,128)(2,1)} %convolution_convert_fusion.1), channel_id=1, source_target_pairs={{0,1},{1,0},{2,3},{3,2},{4,5},{5,4},{6,7},{7,6},{8,9},{9,8},{10,11... | collective-permute-start | bytes 12582920 | tf_op jit(solution)/shard_map/ppermute | solution.py:191
  2047.0 46.9 %collective-permute-start.147 = (bf16[2,512,688]{1,2,0:T(8,128)(2,1)}, bf16[2,512,688]{1,2,0:T(8,128)(2,1)}, u32[]{:S(2)}, u32[]{:S(2)}) collective-permute-start(bf16[2,512,688]{1,2,0:T(8,128)(2,1)} %fusion.122), channel_id=1, source_target_pairs={{0,4},{4,0},{1,5},{5,1},{2,6},{6,2},{3,7},{7,3},{8,12},{12,8},{9,1... | collective-permute-start | bytes 4227080 | tf_op jit(solution)/shard_map/ppermute | solution.py:191
  2059.7 49.9 %collective-permute-start.134 = (bf16[2048,1024]{1,0:T(8,128)(2,1)}, bf16[2048,1024]{1,0:T(8,128)(2,1)}, u32[]{:S(2)}, u32[]{:S(2)}) collective-permute-start(bf16[2048,1024]{1,0:T(8,128)(2,1)} %convolution_convert_fusion.2), channel_id=1, source_target_pairs={{0,1},{1,0},{2,3},{3,2},{4,5},{5,4},{6,7},{7,6},{8,9},{9,8},{10,11... | collective-permute-start | bytes 12582920 | tf_op jit(solution)/shard_map/ppermute | solution.py:191
  2121.9 56.1 %collective-permute-start.139 = (bf16[512,1024]{1,0:T(8,128)(2,1)S(1)}, bf16[512,1024]{1,0:T(8,128)(2,1)S(1)}, u32[]{:S(2)}, u32[]{:S(2)}) collective-permute-start(bf16[512,1024]{1,0:T(8,128)(2,1)S(1)} %get-tuple-element.113), channel_id=1, source_target_pairs={{0,2},{1,3},{2,0},{3,1},{4,6},{5,7},{6,4},{7,5},{8,10},{9,11},{10,... | collective-permute-start | bytes 3145736 | tf_op jit(solution)/shard_map/ppermute | solution.py:191
  (193 other events, 4264.1 us)
Sparse Core Ops, SparseCore 0:
  12.1 306.9 all-gather.9
  320.7 83.1 all-gather.11
Sparse Core Ops, SparseCore 1:
  500.2 259.7 all-gather.7
  761.3 133.2 all-gather.13
  1210.5 131.1 reduce-scatter.5
  1344.1 130.2 reduce-scatter.7
  1476.7 130.2 reduce-scatter.13
  1609.4 75.7 reduce-scatter.11
  1725.5 284.1 reduce-scatter.9

commit v9 on v7

--- a/solution.py
+++ b/solution.py
@@ -355,18 +355,14 @@
     grad_branch = grad_resid.astype(BF)
     branch_full = gather_rows(grad_branch)
     grad_heads = back_out(branch_full, out_full).astype(BF)
-    out_sum = owners(out_part(head_outs, branch_full))
     grad_proj = attend_backward(
         queries, keys, values, head_outs, norms, grad_heads, cosine, sine
     )
-    qkv_part = [
-        in_part(attn_full, jnp.concatenate(grad_proj[1:], axis=1)),
-        in_part(attn_full, grad_proj[0]),
-    ]
-    qkv_sum = [owners(part) for part in qkv_part]
-    grad_nattn = scatter_rows(
-        in_blocks(jnp.concatenate(grad_proj, axis=1), jnp.concatenate(qkv_parts, axis=2))
-    )
+    joined = jnp.concatenate(grad_proj, axis=1)
+    qkv_part = in_part(attn_full, joined)
+    qkv_sum = [owners(qkv_part)]
+    grad_nattn = scatter_rows(in_blocks(joined, jnp.concatenate(qkv_parts, axis=2)))
+    out_sum = owners(out_part(after(head_outs, qkv_part), branch_full))
     hidden = after(hidden, qkv_part)
     layer_output = (resid + scatter_rows(out_blocks(hidden, down_full))).astype(BF)
     attn_term = grad_nattn * attn_scale
@@ -380,8 +376,7 @@
     gu_grad = jnp.concatenate(
         [v.reshape(v.shape[0], 2, -1) for v in (rows, other_rows)], axis=2
     ).astype(F32)
-    out_weight_grad = out_grad(out_sum)
-    done = (down_grad, out_weight_grad, gu_grad, grad_input, layer_output, gain_grads)
+    done = (down_grad, gu_grad, grad_input, layer_output, gain_grads)
     qkv_grad = []
     for part in qkv_sum:
         first, second = trade_ctx(after(part, done), 0)
@@ -390,7 +385,8 @@
             both = [first[:, i : i + wide], second[:, i : i + wide]]
             qkv_grad.append(jnp.concatenate(both, axis=1).astype(F32))
         done = done + (qkv_grad[-1],)
-    qkv_grad = jnp.stack([qkv_grad[2], qkv_grad[0], qkv_grad[1]], axis=1)
+    qkv_grad = jnp.stack(qkv_grad, axis=1)
+    out_weight_grad = out_grad(after(out_sum, done))
 
     return (
         layer_output,

time: 1810 us -> 1800 us (level)
    dot_general x33 -> x32, matrix products: 458 us -> 452 us  [mm(): return lax.dot_general(left, right, dims, preferred_element_type=F32)]
    reduce_scatter x5 -> x4, waiting for transfers between devices: 123 us -> 119 us  [owners(): return lax.psum_scatter(grad, 'fsdp', scatter_dimension=0, tiled=False)]
    ppermute x96 -> x95, starting transfers between devices: 77.1 us -> 74 us  [swap(): lax.ppermute(values, axis, [(i, i ^ step) for i in range(lax.axis_size(ax...]
    ppermute x96 -> x95, waiting for transfers between devices: 476 us -> 478 us  [swap(): lax.ppermute(values, axis, [(i, i ^ step) for i in range(lax.axis_size(ax...]
  transfers between devices with their start and end apart: 105 -> 103, of which waited for: 38 -> 38; matrix products, arithmetic and copies ran while one was open for 38% -> 37% of each run, Pallas kernels for 4% -> 4%
where the time goes in v9:
time: 1800 us; the launch traced here: 1790 us
  waiting for transfers between devices  872 us (48%)
  matrix products  452 us (25%)
  local copies, waits for them, and re-layouts  145 us (8%)
  other arithmetic  90.9 us (5%)
  Pallas kernels  79 us (4%)
  starting transfers between devices  74.3 us (4%)
  blocking collectives  61.7 us (3%)
    ppermute x95, waiting for transfers between devices, swap(): lax.ppermute(values, axis, [(i, i ^ step) for i in range(lax.axis_size(ax...  478 us
    dot_general x32, matrix products, mm(): return lax.dot_general(left, right, dims, preferred_element_type=F32)  452 us
    all_gather x4, waiting for transfers between devices, spread(): return lax.all_gather(weight, 'fsdp', axis=0, tiled=False)  274 us
    reduce_scatter x4, waiting for transfers between devices, owners(): return lax.psum_scatter(grad, 'fsdp', scatter_dimension=0, tiled=False)  119 us
    ppermute x95, starting transfers between devices, swap(): lax.ppermute(values, axis, [(i, i ^ step) for i in range(lax.axis_size(ax...  74 us
    dynamic_update_slice x64, local copies, waits for them, and re-layouts, gather_rows(): full = lax.dynamic_update_slice(full, piece[None], start)  71.4 us
    psum x4, blocking collectives, row_total(): return lax.psum(values, 'tp')  61.7 us
    pallas_call x1, Pallas kernels, attend_backward(): pl.pallas_call(kernel, grid=(heads, blocks), in_specs=[row, col, col, row...  43.9 us
  transfers between devices with their start and end apart: 103, of which 38 were waited for; matrix products, arithmetic and copies ran while one was open for 37% of the time, Pallas kernels for 4%

profile of v9, /device:TPU:0, one launch (start us, length us, event | category | flops | bytes accessed | tf_op | source)
XLA Modules:
  0.0 1790.9 jit_solution(7873913823833238859)
XLA Ops:
  20.2 8.1 psum.28
  40.6 16.0 collective-permute-done
  58.3 6.1 broadcast.35.clone
  70.1 12.5 collective-permute-done.7
  85.5 17.3 collective-permute-done.2
  108.2 8.4 collective-permute-done.9
  128.5 103.7 %all-gather.10.cloned.1.call-done = bf16[12,1024,512]{2,1,0:T(8,128)(2,1)} async-done(((bf16[3,1024,512]{2,1,0:T(8,128)(2,1)}), bf16[12,1024,512]{2,1,0:T(8,128)(2,1)}) %all-gather.10.cloned.1.call-update) | async-done | bytes 12582928 | tf_op jit(solution)/shard_map/all_gather | solution.py:263
  232.2 15.0 convolution_bitcast_fusion.1.v_in
  247.3 13.7 convolution_bitcast_fusion.2.k_in
  261.0 13.9 convolution_bitcast_fusion.3.q_in
  274.9 35.1 %shard_map.143 = (bf16[2048,512]{1,0:T(8,128)(2,1)S(1)}, bf16[2048,512]{1,0:T(8,128)(2,1)}, bf16[2048,512]{1,0:T(8,128)(2,1)}, bf16[2048,512]{1,0:T(8,128)(2,1)}, f32[4,1,2048]{2,1,0:T(1,128)S(1)}) custom-call(f32[2048,512]{1,0:T(8,128)} %convolution_bitcast_fusion.3.q_in, f32[2048,512]{1,0:T(8,128)} %convolution_bitcast_fusion.2.k_in, ...), custom_call_target="tpu_custom_call" | custom-call | flops 5368709120 | bytes 20971520 | tf_op jit(solution)/shard_map/pallas_call | solution.py:88
  312.8 6.4 convolution_convert_fusion.6
  330.0 16.5 collective-permute-done.36
  350.2 6.6 broadcast.35.clone.2
  362.3 10.6 collective-permute-done.38
  383.0 11.0 collective-permute-done.43
  412.5 52.8 %collective-permute-done.17 = bf16[512,1024]{1,0:T(8,128)(2,1)S(1)} collective-permute-done((bf16[512,1024]{1,0:T(8,128)(2,1)S(1)}, bf16[512,1024]{1,0:T(8,128)(2,1)S(1)}, u32[]{:S(2)}, u32[]{:S(2)}) %collective-permute-start.17) | collective-permute-done | bytes 1048608 | tf_op jit(solution)/shard_map/ppermute | solution.py:191
  474.2 13.5 collective-permute-done.15
  487.7 21.1 %collective-permute-done.18 = bf16[512,1024]{1,0:T(8,128)(2,1)S(1)} collective-permute-done((bf16[512,1024]{1,0:T(8,128)(2,1)S(1)}, bf16[512,1024]{1,0:T(8,128)(2,1)S(1)}, u32[]{:S(2)}, u32[]{:S(2)}) %collective-permute-start.18) | collective-permute-done | bytes 1048608 | tf_op jit(solution)/shard_map/ppermute | solution.py:191
  513.2 7.6 psum.29
  537.6 10.7 collective-permute-done.22
  552.1 6.2 broadcast.35.clone.1
  562.2 19.6 %collective-permute-done.29 = bf16[512,1024]{1,0:T(8,128)(2,1)S(1)} collective-permute-done((bf16[512,1024]{1,0:T(8,128)(2,1)S(1)}, bf16[512,1024]{1,0:T(8,128)(2,1)S(1)}, u32[]{:S(2)}, u32[]{:S(2)}) %collective-permute-start.29) | collective-permute-done | bytes 1048608 | tf_op jit(solution)/shard_map/ppermute | solution.py:191
  583.4 17.9 collective-permute-done.24
  619.0 77.0 %all-gather.8.cloned.1.call-done = bf16[4,1024,2752]{1,2,0:T(8,128)(2,1)} async-done(((bf16[1,1024,2752]{1,2,0:T(8,128)(2,1)}), bf16[4,1024,2752]{1,2,0:T(8,128)(2,1)}) %all-gather.8.cloned.1.call-update) | async-done | bytes 22544400 | tf_op jit(solution)/shard_map/all_gather | solution.py:263
  696.0 56.8 %convolution_bitcast_fusion = f32[2048,2752]{0,1:T(8,128)} fusion(bf16[4,2048,1024]{2,1,0:T(8,128)(2,1)} %bitcast_dynamic-update-slice_fusion.32, bf16[4,1024,2752]{1,2,0:T(8,128)(2,1)} %all-gather.8.cloned.1.call-done), kind=kOutput, calls=%fused_computation.2 | convolution fusion | flops 46170898432 | bytes 61865984 | tf_op jit(solution)/shard_map/dot_general | solution.py:21
  752.8 9.0 multiply_convert_fusion
  761.8 9.7 fusion.54
  771.5 7.9 fusion.53
  779.4 7.9 fusion.52
  787.4 7.9 fusion.51
  800.5 92.1 %all-gather.14.cloned.1.call-done = bf16[5504,1024]{1,0:T(8,128)(2,1)} async-done(((bf16[1376,1024]{1,0:T(8,128)(2,1)}), bf16[5504,1024]{1,0:T(8,128)(2,1)}) %all-gather.14.cloned.1.call-update) | async-done | bytes 11272208 | tf_op jit(solution)/shard_map/all_gather | solution.py:263
  892.6 37.5 %fusion.3 = (bf16[2048,1376]{0,1:T(8,128)(2,1)S(1)}, bf16[2048,1376]{0,1:T(8,128)(2,1)}) fusion(f32[2048,2752]{0,1:T(8,128)} %convolution_bitcast_fusion, bf16[4,2048,1024]{2,1,0:T(8,128)(2,1)} %bitcast_dynamic-update-slice_fusion.16, bf16[4,1376,1024]{2,1,0:T(8,128)(2,1)} %bitcast.510), kind=kOutput, calls=%fused_computation.11 | convolution fusion | flops 23122083840 | bytes 61865984 | tf_op jit(solution)/shard_map/dot_general | solution.py:21
  932.6 54.7 %convolution_convert_fusion = bf16[4,1024,2752]{1,2,0:T(8,128)(2,1)} fusion(bf16[4,2048,1024]{2,1,0:T(8,128)(2,1)} %bitcast_dynamic-update-slice_fusion.32, bf16[2048,1376]{0,1:T(8,128)(2,1)} %get-tuple-element.49, bf16[2048,1376]{0,1:T(8,128)(2,1)S(1)} %get-tuple-element.48), kind=kOutput, calls=%fused_computation | convolution fusion | flops 46204715008 | bytes 50593792 | tf_op jit(solution)/shard_map/dot_general | solution.py:21
  987.3 97.1 %reduce-scatter.5.cloned.1.call-done = bf16[1,1376,1024]{2,1,0:T(8,128)(2,1)} async-done(((bf16[4,1376,1024]{2,1,0:T(8,128)(2,1)}), bf16[1,1376,1024]{2,1,0:T(8,128)(2,1)}) %reduce-scatter.5.cloned.1.call-update) | async-done | bytes 2818064 | tf_op jit(solution)/shard_map/reduce_scatter | solution.py:259
  1084.4 17.1 fusion.40
  1101.6 17.3 fusion.37
  1119.5 17.7 add_convert_fusion.4
  1142.8 17.9 add_convert_fusion.5
  1172.0 15.4 collective-permute-done.51
  1193.3 19.2 %collective-permute-done.55 = bf16[512,1024]{1,0:T(8,128)(2,1)S(1)} collective-permute-done((bf16[512,1024]{1,0:T(8,128)(2,1)S(1)}, bf16[512,1024]{1,0:T(8,128)(2,1)S(1)}, u32[]{:S(2)}, u32[]{:S(2)}) %collective-permute-start.55) | collective-permute-done | bytes 1048608 | tf_op jit(solution)/shard_map/ppermute | solution.py:191
  1221.7 6.3 fusion.141
  1231.8 21.0 %collective-permute-done.58 = bf16[512,1024]{1,0:T(8,128)(2,1)S(1)} collective-permute-done((bf16[512,1024]{1,0:T(8,128)(2,1)S(1)}, bf16[512,1024]{1,0:T(8,128)(2,1)S(1)}, u32[]{:S(2)}, u32[]{:S(2)}) %collective-permute-start.58) | collective-permute-done | bytes 1048608 | tf_op jit(solution)/shard_map/ppermute | solution.py:191
  1258.5 19.8 %collective-permute-done.65 = bf16[512,1024]{1,0:T(8,128)(2,1)S(1)} collective-permute-done((bf16[512,1024]{1,0:T(8,128)(2,1)S(1)}, bf16[512,1024]{1,0:T(8,128)(2,1)S(1)}, u32[]{:S(2)}, u32[]{:S(2)}) %collective-permute-start.65) | collective-permute-done | bytes 1048608 | tf_op jit(solution)/shard_map/ppermute | solution.py:191
  1279.0 19.9 %collective-permute-done.60 = bf16[512,1024]{1,0:T(8,128)(2,1)S(1)} collective-permute-done((bf16[512,1024]{1,0:T(8,128)(2,1)S(1)}, bf16[512,1024]{1,0:T(8,128)(2,1)S(1)}, u32[]{:S(2)}, u32[]{:S(2)}) %collective-permute-start.60) | collective-permute-done | bytes 1048608 | tf_op jit(solution)/shard_map/ppermute | solution.py:191
  1307.7 14.1 bitcast_convert_fusion.g
  1321.8 43.9 %shard_map.144 = (bf16[2048,512]{1,0:T(8,128)(2,1)S(1)}, bf16[2048,512]{1,0:T(8,128)(2,1)}, bf16[2048,512]{1,0:T(8,128)(2,1)}) custom-call(bf16[2048,512]{1,0:T(8,128)(2,1)} %copy-done.2, bf16[2048,512]{1,0:T(8,128)(2,1)} %get-tuple-element.26.k, bf16[2048,512]{1,0:T(8,128)(2,1)} %get-tuple-element.27.v, bf16[2048,512]{1,0:T(8,128)(2,1)} %get-tuple-element.38.o, ...), custom_call_target="tpu_custom_call" | custom-call | flops 13421772800 | bytes 16777216 | tf_op jit(solution)/shard_map/pallas_call | solution.py:164
  1370.8 31.2 %convolution_convert_fusion.1 = bf16[4,1024,1536]{2,1,0:T(8,128)(2,1)} fusion(bf16[4,2048,1024]{2,1,0:T(8,128)(2,1)} %bitcast_dynamic-update-slice_fusion.48, bf16[2048,1536]{1,0:T(8,128)(2,1)S(1)} %constant_dynamic-update-slice_fusion), kind=kOutput, calls=%fused_computation.1 | convolution fusion | flops 25776095232 | bytes 35651584 | tf_op jit(solution)/shard_map/dot_general | solution.py:21
  1410.4 30.6 %collective-permute-done.91 = bf16[1376,512]{1,0:T(8,128)(2,1)S(1)} collective-permute-done((bf16[1376,512]{1,0:T(8,128)(2,1)S(1)}, bf16[1376,512]{1,0:T(8,128)(2,1)S(1)}, u32[]{:S(2)}, u32[]{:S(2)}) %collective-permute-start.91) | collective-permute-done | bytes 1409056 | tf_op jit(solution)/shard_map/ppermute | solution.py:191
  1445.0 8.8 convolution_convert_fusion.2
  1453.7 8.8 convolution_convert_fusion.3
  1463.0 10.4 convolution_convert_fusion.4
  1473.4 11.3 convolution_convert_fusion.5
  1497.1 11.3 add_convert_fusion
  1510.4 11.0 add_convert_fusion.1
  1525.2 9.6 add_convert_fusion.2
  1537.7 10.0 add_convert_fusion.3
  1553.3 25.7 %collective-permute-done.75 = bf16[512,1024]{1,0:T(8,128)(2,1)S(1)} collective-permute-done((bf16[512,1024]{1,0:T(8,128)(2,1)S(1)}, bf16[512,1024]{1,0:T(8,128)(2,1)S(1)}, u32[]{:S(2)}, u32[]{:S(2)}) %collective-permute-start.75) | collective-permute-done | bytes 1048608 | tf_op jit(solution)/shard_map/ppermute | solution.py:191
  1585.4 9.3 collective-permute-done.84
  1603.2 14.1 collective-permute-done.85
  1623.3 40.0 %psum.31 = f32[1024]{0:T(1024)S(1)} all-reduce(f32[1024]{0:T(1024)S(1)} %get-tuple-element.43), channel_id=1, replica_groups=mesh['fsdp'=4,'ctx'=2,'tp'=4] {'tp'}, use_global_device_ids=true, to_apply=%region_8.9 | all-reduce | flops 1024 | bytes 8192 | tf_op jit(solution)/shard_map/psum | solution.py:186
  1672.2 36.8 %collective-permute-done.88 = f32[2,1024]{1,0:T(2,128)S(1)} collective-permute-done((f32[2,1024]{1,0:T(2,128)S(1)}, f32[2,1024]{1,0:T(2,128)S(1)}, u32[]{:S(2)}, u32[]{:S(2)}) %collective-permute-start.88) | collective-permute-done | bytes 8224 | tf_op jit(solution)/shard_map/ppermute | solution.py:191
  1734.3 22.1 %reduce-scatter.11.cloned.1.call-done = bf16[1,512,1024]{2,1,0:T(8,128)(2,1)} async-done(((bf16[4,512,1024]{2,1,0:T(8,128)(2,1)}), bf16[1,512,1024]{2,1,0:T(8,128)(2,1)}) %reduce-scatter.11.cloned.1.call-update) | async-done | bytes 1048592 | tf_op jit(solution)/shard_map/reduce_scatter | solution.py:259
  1759.7 15.8 collective-permute-done.94
  (482 shorter events, 331.0 us)
Async XLA Ops:
  7.2 225.0 %all-gather.10.cloned.1.call-start = ((), (), s32[]{:S(2)}) async-start(), calls=%async_computation.9 | async-start | bytes 15728640 | tf_op jit(solution)/shard_map/all_gather | solution.py:263
  11.2 301.6 %all-gather.12.cloned.1.call-start = ((), (), s32[]{:S(2)}) async-start(), calls=%async_computation.10 | async-start | bytes 5242880 | tf_op jit(solution)/shard_map/all_gather | solution.py:263
  12.3 683.7 %all-gather.8.cloned.1.call-start = ((), (), s32[]{:S(2)}) async-start(), calls=%async_computation.4 | async-start | bytes 28180480 | tf_op jit(solution)/shard_map/all_gather | solution.py:263
  18.1 874.5 %all-gather.14.cloned.1.call-start = ((), (), s32[]{:S(2)}) async-start(), calls=%async_computation.11 | async-start | bytes 14090240 | tf_op jit(solution)/shard_map/all_gather | solution.py:263
  33.8 34.6 %collective-permute-start.1 = (bf16[512,1024]{1,0:T(8,128)(2,1)}, bf16[512,1024]{1,0:T(8,128)(2,1)}, u32[]{:S(2)}, u32[]{:S(2)}) collective-permute-start(bf16[512,1024]{1,0:T(8,128)(2,1)} %get-tuple-element.90), channel_id=1, source_target_pairs={{0,2},{1,3},{2,0},{3,1},{4,6},{5,7},{6,4},{7,5},{8,10},{9,11},{10,... | collective-permute-start | bytes 3145736 | tf_op jit(solution)/shard_map/ppermute | solution.py:191
  34.7 35.2 %collective-permute-start.3 = (bf16[512,1024]{1,0:T(8,128)(2,1)}, bf16[512,1024]{1,0:T(8,128)(2,1)}, u32[]{:S(2)}, u32[]{:S(2)}) collective-permute-start(bf16[512,1024]{1,0:T(8,128)(2,1)} %get-tuple-element.90), channel_id=1, source_target_pairs={{0,1},{1,0},{2,3},{3,2},{4,5},{5,4},{6,7},{7,6},{8,9},{9,8},{10,11... | collective-permute-start | bytes 3145736 | tf_op jit(solution)/shard_map/ppermute | solution.py:191
  34.7 47.9 %collective-permute-start.7 = (bf16[512,1024]{1,0:T(8,128)(2,1)}, bf16[512,1024]{1,0:T(8,128)(2,1)}, u32[]{:S(2)}, u32[]{:S(2)}) collective-permute-start(bf16[512,1024]{1,0:T(8,128)(2,1)} %get-tuple-element.89), channel_id=1, source_target_pairs={{0,2},{1,3},{2,0},{3,1},{4,6},{5,7},{6,4},{7,5},{8,10},{9,11},{10,... | collective-permute-start | bytes 3145736 | tf_op jit(solution)/shard_map/ppermute | solution.py:191
  56.6 46.1 %collective-permute-start.2 = (bf16[512,1024]{1,0:T(8,128)(2,1)}, bf16[512,1024]{1,0:T(8,128)(2,1)S(1)}, u32[]{:S(2)}, u32[]{:S(2)}) collective-permute-start(bf16[512,1024]{1,0:T(8,128)(2,1)} %collective-permute-done), channel_id=1, source_target_pairs={{0,2},{1,3},{2,0},{3,1},{4,6},{5,7},{6,4},{7,5},{8,10},{9,11},{10,... | collective-permute-start | bytes 3145736 | tf_op jit(solution)/shard_map/ppermute | solution.py:191
  66.0 40.1 %collective-permute-start.4 = (bf16[512,1024]{1,0:T(8,128)(2,1)}, bf16[512,1024]{1,0:T(8,128)(2,1)S(1)}, u32[]{:S(2)}, u32[]{:S(2)}) collective-permute-start(bf16[512,1024]{1,0:T(8,128)(2,1)} %collective-permute-done), channel_id=1, source_target_pairs={{0,1},{1,0},{2,3},{3,2},{4,5},{5,4},{6,7},{7,6},{8,9},{9,8},{10,11... | collective-permute-start | bytes 3145736 | tf_op jit(solution)/shard_map/ppermute | solution.py:191
  68.4 39.3 %collective-permute-start.8 = (bf16[512,1024]{1,0:T(8,128)(2,1)}, bf16[512,1024]{1,0:T(8,128)(2,1)S(1)}, u32[]{:S(2)}, u32[]{:S(2)}) collective-permute-start(bf16[512,1024]{1,0:T(8,128)(2,1)} %get-tuple-element.89), channel_id=1, source_target_pairs={{0,4},{4,0},{1,5},{5,1},{2,6},{6,2},{3,7},{7,3},{8,12},{12,8},{9,1... | collective-permute-start | bytes 3145736 | tf_op jit(solution)/shard_map/ppermute | solution.py:191
  69.9 37.8 %collective-permute-start.5 = (bf16[512,1024]{1,0:T(8,128)(2,1)}, bf16[512,1024]{1,0:T(8,128)(2,1)S(1)}, u32[]{:S(2)}, u32[]{:S(2)}) collective-permute-start(bf16[512,1024]{1,0:T(8,128)(2,1)} %collective-permute-done.1), channel_id=1, source_target_pairs={{0,1},{1,0},{2,3},{3,2},{4,5},{5,4},{6,7},{7,6},{8,9},{9,8},{10,11... | collective-permute-start | bytes 3145736 | tf_op jit(solution)/shard_map/ppermute | solution.py:191
  82.7 33.9 %collective-permute-start.9 = (bf16[512,1024]{1,0:T(8,128)(2,1)}, bf16[512,1024]{1,0:T(8,128)(2,1)S(1)}, u32[]{:S(2)}, u32[]{:S(2)}) collective-permute-start(bf16[512,1024]{1,0:T(8,128)(2,1)} %collective-permute-done.7), channel_id=1, source_target_pairs={{0,4},{4,0},{1,5},{5,1},{2,6},{6,2},{3,7},{7,3},{8,12},{12,8},{9,1... | collective-permute-start | bytes 3145736 | tf_op jit(solution)/shard_map/ppermute | solution.py:191
  319.1 79.1 %collective-permute-start.16 = (bf16[2048,1024]{1,0:T(8,128)(2,1)}, bf16[2048,1024]{1,0:T(8,128)(2,1)}, u32[]{:S(2)}, u32[]{:S(2)}) collective-permute-start(bf16[2048,1024]{1,0:T(8,128)(2,1)} %convolution_convert_fusion.6), channel_id=1, source_target_pairs={{0,1},{1,0},{2,3},{3,2},{4,5},{5,4},{6,7},{7,6},{8,9},{9,8},{10,11... | collective-permute-start | bytes 12582920 | tf_op jit(solution)/shard_map/ppermute | solution.py:191
  329.5 77.2 %collective-permute-start.14 = (bf16[2048,1024]{1,0:T(8,128)(2,1)}, bf16[2048,1024]{1,0:T(8,128)(2,1)}, u32[]{:S(2)}, u32[]{:S(2)}) collective-permute-start(bf16[2048,1024]{1,0:T(8,128)(2,1)} %convolution_convert_fusion.7), channel_id=1, source_target_pairs={{0,1},{1,0},{2,3},{3,2},{4,5},{5,4},{6,7},{7,6},{8,9},{9,8},{10,11... | collective-permute-start | bytes 12582920 | tf_op jit(solution)/shard_map/ppermute | solution.py:191
  330.0 30.1 %collective-permute-start.39 = (bf16[512,1024]{1,0:T(8,128)(2,1)}, bf16[512,1024]{1,0:T(8,128)(2,1)S(1)}, u32[]{:S(2)}, u32[]{:S(2)}) collective-permute-start(bf16[512,1024]{1,0:T(8,128)(2,1)} %get-tuple-element.84), channel_id=1, source_target_pairs={{0,1},{1,0},{2,3},{3,2},{4,5},{5,4},{6,7},{7,6},{8,9},{9,8},{10,11... | collective-permute-start | bytes 3145736 | tf_op jit(solution)/shard_map/ppermute | solution.py:191
  350.1 734.3 %reduce-scatter.5.cloned.1.call-start = ((), (), s32[]{:S(2)}) async-start(), calls=%async_computation.5 | async-start | bytes 14090240 | tf_op jit(solution)/shard_map/reduce_scatter | solution.py:259
  361.0 33.0 %collective-permute-start.43 = (bf16[512,1024]{1,0:T(8,128)(2,1)}, bf16[512,1024]{1,0:T(8,128)(2,1)S(1)}, u32[]{:S(2)}, u32[]{:S(2)}) collective-permute-start(bf16[512,1024]{1,0:T(8,128)(2,1)} %get-tuple-element.83), channel_id=1, source_target_pairs={{0,2},{1,3},{2,0},{3,1},{4,6},{5,7},{6,4},{7,5},{8,10},{9,11},{10,... | collective-permute-start | bytes 3145736 | tf_op jit(solution)/shard_map/ppermute | solution.py:191
  394.0 74.2 %collective-permute-start.44 = (bf16[512,1024]{1,0:T(8,128)(2,1)}, bf16[512,1024]{1,0:T(8,128)(2,1)}, u32[]{:S(2)}, u32[]{:S(2)}) collective-permute-start(bf16[512,1024]{1,0:T(8,128)(2,1)} %get-tuple-element.83), channel_id=1, source_target_pairs={{0,4},{4,0},{1,5},{5,1},{2,6},{6,2},{3,7},{7,3},{8,12},{12,8},{9,1... | collective-permute-start | bytes 3145736 | tf_op jit(solution)/shard_map/ppermute | solution.py:191
  395.5 113.9 %collective-permute-start.45 = (bf16[512,1024]{1,0:T(8,128)(2,1)S(1)}, bf16[512,1024]{1,0:T(8,128)(2,1)}, u32[]{:S(2)}, u32[]{:S(2)}) collective-permute-start(bf16[512,1024]{1,0:T(8,128)(2,1)S(1)} %collective-permute-done.43), channel_id=1, source_target_pairs={{0,4},{4,0},{1,5},{5,1},{2,6},{6,2},{3,7},{7,3},{8,12},{12,8},{9,1... | collective-permute-start | bytes 3145736 | tf_op jit(solution)/shard_map/ppermute | solution.py:191
  403.4 61.8 %collective-permute-start.17 = (bf16[512,1024]{1,0:T(8,128)(2,1)S(1)}, bf16[512,1024]{1,0:T(8,128)(2,1)S(1)}, u32[]{:S(2)}, u32[]{:S(2)}) collective-permute-start(bf16[512,1024]{1,0:T(8,128)(2,1)S(1)} %dynamic-slice_bitcast_fusion.17), channel_id=1, source_target_pairs={{0,4},{4,0},{1,5},{5,1},{2,6},{6,2},{3,7},{7,3},{8,12},{12,8},{9,1... | collective-permute-start | bytes 3145736 | tf_op jit(solution)/shard_map/ppermute | solution.py:191
  405.2 62.0 %collective-permute-start.20 = (bf16[512,1024]{1,0:T(8,128)(2,1)S(1)}, bf16[512,1024]{1,0:T(8,128)(2,1)S(1)}, u32[]{:S(2)}, u32[]{:S(2)}) collective-permute-start(bf16[512,1024]{1,0:T(8,128)(2,1)S(1)} %get-tuple-element.88), channel_id=1, source_target_pairs={{0,2},{1,3},{2,0},{3,1},{4,6},{5,7},{6,4},{7,5},{8,10},{9,11},{10,... | collective-permute-start | bytes 3145736 | tf_op jit(solution)/shard_map/ppermute | solution.py:191
  411.9 75.9 %collective-permute-start.15 = (bf16[512,1024]{1,0:T(8,128)(2,1)S(1)}, bf16[512,1024]{1,0:T(8,128)(2,1)S(1)}, u32[]{:S(2)}, u32[]{:S(2)}) collective-permute-start(bf16[512,1024]{1,0:T(8,128)(2,1)S(1)} %dynamic-slice_bitcast_fusion.18), channel_id=1, source_target_pairs={{0,4},{4,0},{1,5},{5,1},{2,6},{6,2},{3,7},{7,3},{8,12},{12,8},{9,1... | collective-permute-start | bytes 3145736 | tf_op jit(solution)/shard_map/ppermute | solution.py:191
  465.3 44.7 %collective-permute-start.19 = (bf16[512,1024]{1,0:T(8,128)(2,1)S(1)}, bf16[512,1024]{1,0:T(8,128)(2,1)S(1)}, u32[]{:S(2)}, u32[]{:S(2)}) collective-permute-start(bf16[512,1024]{1,0:T(8,128)(2,1)S(1)} %get-tuple-element.87), channel_id=1, source_target_pairs={{0,2},{1,3},{2,0},{3,1},{4,6},{5,7},{6,4},{7,5},{8,10},{9,11},{10,... | collective-permute-start | bytes 3145736 | tf_op jit(solution)/shard_map/ppermute | solution.py:191
  467.2 41.6 %collective-permute-start.18 = (bf16[512,1024]{1,0:T(8,128)(2,1)S(1)}, bf16[512,1024]{1,0:T(8,128)(2,1)S(1)}, u32[]{:S(2)}, u32[]{:S(2)}) collective-permute-start(bf16[512,1024]{1,0:T(8,128)(2,1)S(1)} %fusion.97), channel_id=1, source_target_pairs={{0,2},{1,3},{2,0},{3,1},{4,6},{5,7},{6,4},{7,5},{8,10},{9,11},{10,... | collective-permute-start | bytes 3145736 | tf_op jit(solution)/shard_map/ppermute | solution.py:191
  468.2 41.9 %collective-permute-start.21 = (bf16[512,1024]{1,0:T(8,128)(2,1)S(1)}, bf16[512,1024]{1,0:T(8,128)(2,1)S(1)}, u32[]{:S(2)}, u32[]{:S(2)}) collective-permute-start(bf16[512,1024]{1,0:T(8,128)(2,1)S(1)} %fusion.95), channel_id=1, source_target_pairs={{0,4},{4,0},{1,5},{5,1},{2,6},{6,2},{3,7},{7,3},{8,12},{12,8},{9,1... | collective-permute-start | bytes 3145736 | tf_op jit(solution)/shard_map/ppermute | solution.py:191
  487.7 40.9 %collective-permute-start.46 = (bf16[512,1024]{1,0:T(8,128)(2,1)}, bf16[512,1024]{1,0:T(8,128)(2,1)}, u32[]{:S(2)}, u32[]{:S(2)}) collective-permute-start(bf16[512,1024]{1,0:T(8,128)(2,1)} %get-tuple-element.83), channel_id=1, source_target_pairs={{0,1},{1,0},{2,3},{3,2},{4,5},{5,4},{6,7},{7,6},{8,9},{9,8},{10,11... | collective-permute-start | bytes 3145736 | tf_op jit(solution)/shard_map/ppermute | solution.py:191
  510.0 39.8 %collective-permute-start.49 = (bf16[512,1024]{1,0:T(8,128)(2,1)}, bf16[512,1024]{1,0:T(8,128)(2,1)}, u32[]{:S(2)}, u32[]{:S(2)}) collective-permute-start(bf16[512,1024]{1,0:T(8,128)(2,1)} %collective-permute-done.45), channel_id=1, source_target_pairs={{0,1},{1,0},{2,3},{3,2},{4,5},{5,4},{6,7},{7,6},{8,9},{9,8},{10,11... | collective-permute-start | bytes 3145736 | tf_op jit(solution)/shard_map/ppermute | solution.py:191
  533.2 27.3 %collective-permute-start.23 = (bf16[512,1024]{1,0:T(8,128)(2,1)S(1)}, bf16[512,1024]{1,0:T(8,128)(2,1)S(1)}, u32[]{:S(2)}, u32[]{:S(2)}) collective-permute-start(bf16[512,1024]{1,0:T(8,128)(2,1)S(1)} %get-tuple-element.86), channel_id=1, source_target_pairs={{0,2},{1,3},{2,0},{3,1},{4,6},{5,7},{6,4},{7,5},{8,10},{9,11},{10,... | collective-permute-start | bytes 3145736 | tf_op jit(solution)/shard_map/ppermute | solution.py:191
  533.8 28.2 %collective-permute-start.25 = (bf16[512,1024]{1,0:T(8,128)(2,1)S(1)}, bf16[512,1024]{1,0:T(8,128)(2,1)S(1)}, u32[]{:S(2)}, u32[]{:S(2)}) collective-permute-start(bf16[512,1024]{1,0:T(8,128)(2,1)S(1)} %get-tuple-element.86), channel_id=1, source_target_pairs={{0,1},{1,0},{2,3},{3,2},{4,5},{5,4},{6,7},{7,6},{8,9},{9,8},{10,11... | collective-permute-start | bytes 3145736 | tf_op jit(solution)/shard_map/ppermute | solution.py:191
  533.8 47.9 %collective-permute-start.29 = (bf16[512,1024]{1,0:T(8,128)(2,1)S(1)}, bf16[512,1024]{1,0:T(8,128)(2,1)S(1)}, u32[]{:S(2)}, u32[]{:S(2)}) collective-permute-start(bf16[512,1024]{1,0:T(8,128)(2,1)S(1)} %get-tuple-element.85), channel_id=1, source_target_pairs={{0,2},{1,3},{2,0},{3,1},{4,6},{5,7},{6,4},{7,5},{8,10},{9,11},{10,... | collective-permute-start | bytes 3145736 | tf_op jit(solution)/shard_map/ppermute | solution.py:191
  548.3 53.0 %collective-permute-start.24 = (bf16[512,1024]{1,0:T(8,128)(2,1)S(1)}, bf16[512,1024]{1,0:T(8,128)(2,1)S(1)}, u32[]{:S(2)}, u32[]{:S(2)}) collective-permute-start(bf16[512,1024]{1,0:T(8,128)(2,1)S(1)} %collective-permute-done.22), channel_id=1, source_target_pairs={{0,2},{1,3},{2,0},{3,1},{4,6},{5,7},{6,4},{7,5},{8,10},{9,11},{10,... | collective-permute-start | bytes 3145736 | tf_op jit(solution)/shard_map/ppermute | solution.py:191
  559.4 44.0 %collective-permute-start.26 = (bf16[512,1024]{1,0:T(8,128)(2,1)S(1)}, bf16[512,1024]{1,0:T(8,128)(2,1)S(1)}, u32[]{:S(2)}, u32[]{:S(2)}) collective-permute-start(bf16[512,1024]{1,0:T(8,128)(2,1)S(1)} %collective-permute-done.22), channel_id=1, source_target_pairs={{0,1},{1,0},{2,3},{3,2},{4,5},{5,4},{6,7},{7,6},{8,9},{9,8},{10,11... | collective-permute-start | bytes 3145736 | tf_op jit(solution)/shard_map/ppermute | solution.py:191
  560.5 44.5 %collective-permute-start.30 = (bf16[512,1024]{1,0:T(8,128)(2,1)S(1)}, bf16[512,1024]{1,0:T(8,128)(2,1)S(1)}, u32[]{:S(2)}, u32[]{:S(2)}) collective-permute-start(bf16[512,1024]{1,0:T(8,128)(2,1)S(1)} %get-tuple-element.85), channel_id=1, source_target_pairs={{0,4},{4,0},{1,5},{5,1},{2,6},{6,2},{3,7},{7,3},{8,12},{12,8},{9,1... | collective-permute-start | bytes 3145736 | tf_op jit(solution)/shard_map/ppermute | solution.py:191
  562.0 43.0 %collective-permute-start.27 = (bf16[512,1024]{1,0:T(8,128)(2,1)S(1)}, bf16[512,1024]{1,0:T(8,128)(2,1)S(1)}, u32[]{:S(2)}, u32[]{:S(2)}) collective-permute-start(bf16[512,1024]{1,0:T(8,128)(2,1)S(1)} %collective-permute-done.23), channel_id=1, source_target_pairs={{0,1},{1,0},{2,3},{3,2},{4,5},{5,4},{6,7},{7,6},{8,9},{9,8},{10,11... | collective-permute-start | bytes 3145736 | tf_op jit(solution)/shard_map/ppermute | solution.py:191
  800.5 798.9 %reduce-scatter.9.cloned.1.call-start = ((), (), s32[]{:S(2)}) async-start(), calls=%async_computation.7 | async-start | bytes 28180480 | tf_op jit(solution)/shard_map/reduce_scatter | solution.py:259
  1084.4 645.8 %reduce-scatter.7.cloned.1.call-start = ((), (), s32[]{:S(2)}) async-start(), calls=%async_computation.6 | async-start | bytes 15728640 | tf_op jit(solution)/shard_map/reduce_scatter | solution.py:259
  1141.3 27.3 %collective-permute-start.56 = (bf16[512,1024]{1,0:T(8,128)(2,1)}, bf16[512,1024]{1,0:T(8,128)(2,1)}, u32[]{:S(2)}, u32[]{:S(2)}) collective-permute-start(bf16[512,1024]{1,0:T(8,128)(2,1)} %get-tuple-element.82), channel_id=1, source_target_pairs={{0,2},{1,3},{2,0},{3,1},{4,6},{5,7},{6,4},{7,5},{8,10},{9,11},{10,... | collective-permute-start | bytes 3145736 | tf_op jit(solution)/shard_map/ppermute | solution.py:191
  1168.3 44.2 %collective-permute-start.55 = (bf16[512,1024]{1,0:T(8,128)(2,1)S(1)}, bf16[512,1024]{1,0:T(8,128)(2,1)S(1)}, u32[]{:S(2)}, u32[]{:S(2)}) collective-permute-start(bf16[512,1024]{1,0:T(8,128)(2,1)S(1)} %get-tuple-element.81), channel_id=1, source_target_pairs={{0,2},{1,3},{2,0},{3,1},{4,6},{5,7},{6,4},{7,5},{8,10},{9,11},{10,... | collective-permute-start | bytes 3145736 | tf_op jit(solution)/shard_map/ppermute | solution.py:191
  1170.2 42.2 %collective-permute-start.57 = (bf16[512,1024]{1,0:T(8,128)(2,1)S(1)}, bf16[512,1024]{1,0:T(8,128)(2,1)S(1)}, u32[]{:S(2)}, u32[]{:S(2)}) collective-permute-start(bf16[512,1024]{1,0:T(8,128)(2,1)S(1)} %fusion.91), channel_id=1, source_target_pairs={{0,4},{4,0},{1,5},{5,1},{2,6},{6,2},{3,7},{7,3},{8,12},{12,8},{9,1... | collective-permute-start | bytes 3145736 | tf_op jit(solution)/shard_map/ppermute | solution.py:191
  1231.2 47.1 %collective-permute-start.65 = (bf16[512,1024]{1,0:T(8,128)(2,1)S(1)}, bf16[512,1024]{1,0:T(8,128)(2,1)S(1)}, u32[]{:S(2)}, u32[]{:S(2)}) collective-permute-start(bf16[512,1024]{1,0:T(8,128)(2,1)S(1)} %get-tuple-element.79), channel_id=1, source_target_pairs={{0,2},{1,3},{2,0},{3,1},{4,6},{5,7},{6,4},{7,5},{8,10},{9,11},{10,... | collective-permute-start | bytes 3145736 | tf_op jit(solution)/shard_map/ppermute | solution.py:191
  1252.8 46.1 %collective-permute-start.60 = (bf16[512,1024]{1,0:T(8,128)(2,1)S(1)}, bf16[512,1024]{1,0:T(8,128)(2,1)S(1)}, u32[]{:S(2)}, u32[]{:S(2)}) collective-permute-start(bf16[512,1024]{1,0:T(8,128)(2,1)S(1)} %collective-permute-done.58), channel_id=1, source_target_pairs={{0,2},{1,3},{2,0},{3,1},{4,6},{5,7},{6,4},{7,5},{8,10},{9,11},{10,... | collective-permute-start | bytes 3145736 | tf_op jit(solution)/shard_map/ppermute | solution.py:191
  1256.5 42.7 %collective-permute-start.62 = (bf16[512,1024]{1,0:T(8,128)(2,1)S(1)}, bf16[512,1024]{1,0:T(8,128)(2,1)S(1)}, u32[]{:S(2)}, u32[]{:S(2)}) collective-permute-start(bf16[512,1024]{1,0:T(8,128)(2,1)S(1)} %collective-permute-done.58), channel_id=1, source_target_pairs={{0,1},{1,0},{2,3},{3,2},{4,5},{5,4},{6,7},{7,6},{8,9},{9,8},{10,11... | collective-permute-start | bytes 3145736 | tf_op jit(solution)/shard_map/ppermute | solution.py:191
  1256.7 43.1 %collective-permute-start.66 = (bf16[512,1024]{1,0:T(8,128)(2,1)S(1)}, bf16[512,1024]{1,0:T(8,128)(2,1)S(1)}, u32[]{:S(2)}, u32[]{:S(2)}) collective-permute-start(bf16[512,1024]{1,0:T(8,128)(2,1)S(1)} %get-tuple-element.79), channel_id=1, source_target_pairs={{0,4},{4,0},{1,5},{5,1},{2,6},{6,2},{3,7},{7,3},{8,12},{12,8},{9,1... | collective-permute-start | bytes 3145736 | tf_op jit(solution)/shard_map/ppermute | solution.py:191
  1258.3 41.7 %collective-permute-start.63 = (bf16[512,1024]{1,0:T(8,128)(2,1)S(1)}, bf16[512,1024]{1,0:T(8,128)(2,1)S(1)}, u32[]{:S(2)}, u32[]{:S(2)}) collective-permute-start(bf16[512,1024]{1,0:T(8,128)(2,1)S(1)} %collective-permute-done.59), channel_id=1, source_target_pairs={{0,1},{1,0},{2,3},{3,2},{4,5},{5,4},{6,7},{7,6},{8,9},{9,8},{10,11... | collective-permute-start | bytes 3145736 | tf_op jit(solution)/shard_map/ppermute | solution.py:191
  1402.0 354.3 %reduce-scatter.11.cloned.1.call-start = ((), (), s32[]{:S(2)}) async-start(), calls=%async_computation.8 | async-start | bytes 5242880 | tf_op jit(solution)/shard_map/reduce_scatter | solution.py:259
  1408.0 33.0 %collective-permute-start.91 = (bf16[1376,512]{1,0:T(8,128)(2,1)S(1)}, bf16[1376,512]{1,0:T(8,128)(2,1)S(1)}, u32[]{:S(2)}, u32[]{:S(2)}) collective-permute-start(bf16[1376,512]{1,0:T(8,128)(2,1)S(1)} %dynamic-slice_bitcast_fusion.2), channel_id=1, source_target_pairs={{0,4},{4,0},{1,5},{5,1},{2,6},{6,2},{3,7},{7,3},{8,12},{12,8},{9,1... | collective-permute-start | bytes 4227080 | tf_op jit(solution)/shard_map/ppermute | solution.py:191
  1453.7 43.4 %collective-permute-start.82 = (bf16[2048,1024]{1,0:T(8,128)(2,1)}, bf16[2048,1024]{1,0:T(8,128)(2,1)}, u32[]{:S(2)}, u32[]{:S(2)}) collective-permute-start(bf16[2048,1024]{1,0:T(8,128)(2,1)} %convolution_convert_fusion.2), channel_id=1, source_target_pairs={{0,1},{1,0},{2,3},{3,2},{4,5},{5,4},{6,7},{7,6},{8,9},{9,8},{10,11... | collective-permute-start | bytes 12582920 | tf_op jit(solution)/shard_map/ppermute | solution.py:191
  1462.5 47.9 %collective-permute-start.80 = (bf16[2048,1024]{1,0:T(8,128)(2,1)}, bf16[2048,1024]{1,0:T(8,128)(2,1)}, u32[]{:S(2)}, u32[]{:S(2)}) collective-permute-start(bf16[2048,1024]{1,0:T(8,128)(2,1)} %convolution_convert_fusion.3), channel_id=1, source_target_pairs={{0,1},{1,0},{2,3},{3,2},{4,5},{5,4},{6,7},{7,6},{8,9},{9,8},{10,11... | collective-permute-start | bytes 12582920 | tf_op jit(solution)/shard_map/ppermute | solution.py:191
  1473.4 51.8 %collective-permute-start.74 = (bf16[2048,1024]{1,0:T(8,128)(2,1)}, bf16[2048,1024]{1,0:T(8,128)(2,1)}, u32[]{:S(2)}, u32[]{:S(2)}) collective-permute-start(bf16[2048,1024]{1,0:T(8,128)(2,1)} %convolution_convert_fusion.4), channel_id=1, source_target_pairs={{0,1},{1,0},{2,3},{3,2},{4,5},{5,4},{6,7},{7,6},{8,9},{9,8},{10,11... | collective-permute-start | bytes 12582920 | tf_op jit(solution)/shard_map/ppermute | solution.py:191
  1484.7 51.3 %collective-permute-start.72 = (bf16[2048,1024]{1,0:T(8,128)(2,1)}, bf16[2048,1024]{1,0:T(8,128)(2,1)}, u32[]{:S(2)}, u32[]{:S(2)}) collective-permute-start(bf16[2048,1024]{1,0:T(8,128)(2,1)} %convolution_convert_fusion.5), channel_id=1, source_target_pairs={{0,1},{1,0},{2,3},{3,2},{4,5},{5,4},{6,7},{7,6},{8,9},{9,8},{10,11... | collective-permute-start | bytes 12582920 | tf_op jit(solution)/shard_map/ppermute | solution.py:191
  1508.9 38.9 %collective-permute-start.83 = (bf16[512,1024]{1,0:T(8,128)(2,1)S(1)}, bf16[512,1024]{1,0:T(8,128)(2,1)S(1)}, u32[]{:S(2)}, u32[]{:S(2)}) collective-permute-start(bf16[512,1024]{1,0:T(8,128)(2,1)S(1)} %dynamic-slice_bitcast_fusion.5), channel_id=1, source_target_pairs={{0,4},{4,0},{1,5},{5,1},{2,6},{6,2},{3,7},{7,3},{8,12},{12,8},{9,1... | collective-permute-start | bytes 3145736 | tf_op jit(solution)/shard_map/ppermute | solution.py:191
  1522.0 61.9 %collective-permute-start.81 = (bf16[512,1024]{1,0:T(8,128)(2,1)S(1)}, bf16[512,1024]{1,0:T(8,128)(2,1)}, u32[]{:S(2)}, u32[]{:S(2)}) collective-permute-start(bf16[512,1024]{1,0:T(8,128)(2,1)S(1)} %dynamic-slice_bitcast_fusion.6), channel_id=1, source_target_pairs={{0,4},{4,0},{1,5},{5,1},{2,6},{6,2},{3,7},{7,3},{8,12},{12,8},{9,1... | collective-permute-start | bytes 3145736 | tf_op jit(solution)/shard_map/ppermute | solution.py:191
  1535.3 43.7 %collective-permute-start.75 = (bf16[512,1024]{1,0:T(8,128)(2,1)S(1)}, bf16[512,1024]{1,0:T(8,128)(2,1)S(1)}, u32[]{:S(2)}, u32[]{:S(2)}) collective-permute-start(bf16[512,1024]{1,0:T(8,128)(2,1)S(1)} %dynamic-slice_bitcast_fusion.9), channel_id=1, source_target_pairs={{0,4},{4,0},{1,5},{5,1},{2,6},{6,2},{3,7},{7,3},{8,12},{12,8},{9,1... | collective-permute-start | bytes 3145736 | tf_op jit(solution)/shard_map/ppermute | solution.py:191
  1536.0 45.8 %collective-permute-start.78 = (bf16[512,1024]{1,0:T(8,128)(2,1)S(1)}, bf16[512,1024]{1,0:T(8,128)(2,1)S(1)}, u32[]{:S(2)}, u32[]{:S(2)}) collective-permute-start(bf16[512,1024]{1,0:T(8,128)(2,1)S(1)} %get-tuple-element.78), channel_id=1, source_target_pairs={{0,2},{1,3},{2,0},{3,1},{4,6},{5,7},{6,4},{7,5},{8,10},{9,11},{10,... | collective-permute-start | bytes 3145736 | tf_op jit(solution)/shard_map/ppermute | solution.py:191
  1548.2 46.6 %collective-permute-start.84 = (bf16[512,1024]{1,0:T(8,128)(2,1)S(1)}, bf16[512,1024]{1,0:T(8,128)(2,1)S(1)}, u32[]{:S(2)}, u32[]{:S(2)}) collective-permute-start(bf16[512,1024]{1,0:T(8,128)(2,1)S(1)} %fusion.85), channel_id=1, source_target_pairs={{0,2},{1,3},{2,0},{3,1},{4,6},{5,7},{6,4},{7,5},{8,10},{9,11},{10,... | collective-permute-start | bytes 3145736 | tf_op jit(solution)/shard_map/ppermute | solution.py:191
  1550.2 67.1 %collective-permute-start.85 = (bf16[512,1024]{1,0:T(8,128)(2,1)}, bf16[512,1024]{1,0:T(8,128)(2,1)}, u32[]{:S(2)}, u32[]{:S(2)}) collective-permute-start(bf16[512,1024]{1,0:T(8,128)(2,1)} %get-tuple-element.75), channel_id=1, source_target_pairs={{0,2},{1,3},{2,0},{3,1},{4,6},{5,7},{6,4},{7,5},{8,10},{9,11},{10,... | collective-permute-start | bytes 3145736 | tf_op jit(solution)/shard_map/ppermute | solution.py:191
  1579.0 39.9 %collective-permute-start.87 = (bf16[512,1024]{1,0:T(8,128)(2,1)}, bf16[512,1024]{1,0:T(8,128)(2,1)}, u32[]{:S(2)}, u32[]{:S(2)}) collective-permute-start(bf16[512,1024]{1,0:T(8,128)(2,1)} %fusion.83), channel_id=1, source_target_pairs={{0,4},{4,0},{1,5},{5,1},{2,6},{6,2},{3,7},{7,3},{8,12},{12,8},{9,1... | collective-permute-start | bytes 3145736 | tf_op jit(solution)/shard_map/ppermute | solution.py:191
  1581.9 87.5 %collective-permute-start.73 = (bf16[512,1024]{1,0:T(8,128)(2,1)}, bf16[512,1024]{1,0:T(8,128)(2,1)}, u32[]{:S(2)}, u32[]{:S(2)}) collective-permute-start(bf16[512,1024]{1,0:T(8,128)(2,1)} %dynamic-slice_bitcast_fusion.10), channel_id=1, source_target_pairs={{0,4},{4,0},{1,5},{5,1},{2,6},{6,2},{3,7},{7,3},{8,12},{12,8},{9,1... | collective-permute-start | bytes 3145736 | tf_op jit(solution)/shard_map/ppermute | solution.py:191
  1583.9 126.6 %collective-permute-start.77 = (bf16[512,1024]{1,0:T(8,128)(2,1)S(1)}, bf16[512,1024]{1,0:T(8,128)(2,1)}, u32[]{:S(2)}, u32[]{:S(2)}) collective-permute-start(bf16[512,1024]{1,0:T(8,128)(2,1)S(1)} %get-tuple-element.77), channel_id=1, source_target_pairs={{0,2},{1,3},{2,0},{3,1},{4,6},{5,7},{6,4},{7,5},{8,10},{9,11},{10,... | collective-permute-start | bytes 3145736 | tf_op jit(solution)/shard_map/ppermute | solution.py:191
  1594.7 75.1 %collective-permute-start.76 = (bf16[512,1024]{1,0:T(8,128)(2,1)}, bf16[512,1024]{1,0:T(8,128)(2,1)}, u32[]{:S(2)}, u32[]{:S(2)}) collective-permute-start(bf16[512,1024]{1,0:T(8,128)(2,1)} %fusion.89), channel_id=1, source_target_pairs={{0,2},{1,3},{2,0},{3,1},{4,6},{5,7},{6,4},{7,5},{8,10},{9,11},{10,... | collective-permute-start | bytes 3145736 | tf_op jit(solution)/shard_map/ppermute | solution.py:191
  1617.3 93.2 %collective-permute-start.79 = (bf16[512,1024]{1,0:T(8,128)(2,1)}, bf16[512,1024]{1,0:T(8,128)(2,1)}, u32[]{:S(2)}, u32[]{:S(2)}) collective-permute-start(bf16[512,1024]{1,0:T(8,128)(2,1)} %fusion.87), channel_id=1, source_target_pairs={{0,4},{4,0},{1,5},{5,1},{2,6},{6,2},{3,7},{7,3},{8,12},{12,8},{9,1... | collective-permute-start | bytes 3145736 | tf_op jit(solution)/shard_map/ppermute | solution.py:191
  1618.9 102.2 %collective-permute-start.92 = (bf16[512,2752]{0,1:T(8,128)(2,1)}, bf16[512,2752]{0,1:T(8,128)(2,1)}, u32[]{:S(2)}, u32[]{:S(2)}) collective-permute-start(bf16[512,2752]{0,1:T(8,128)(2,1)} %dynamic-slice_bitcast_fusion.1), channel_id=1, source_target_pairs={{0,4},{4,0},{1,5},{5,1},{2,6},{6,2},{3,7},{7,3},{8,12},{12,8},{9,1... | collective-permute-start | bytes 8454152 | tf_op jit(solution)/shard_map/ppermute | solution.py:191
  1669.3 39.7 %collective-permute-start.88 = (f32[2,1024]{1,0:T(2,128)S(1)}, f32[2,1024]{1,0:T(2,128)S(1)}, u32[]{:S(2)}, u32[]{:S(2)}) collective-permute-start(f32[2,1024]{1,0:T(2,128)S(1)} %pad_maximum_fusion.8), channel_id=1, source_target_pairs={{0,4},{4,0},{1,5},{5,1},{2,6},{6,2},{3,7},{7,3},{8,12},{12,8},{9,1... | collective-permute-start | bytes 24584 | tf_op jit(solution)/shard_map/ppermute | solution.py:191
  1732.8 45.6 %collective-permute-start.93 = (bf16[512,1536]{1,0:T(8,128)(2,1)}, bf16[512,1536]{1,0:T(8,128)(2,1)}, u32[]{:S(2)}, u32[]{:S(2)}) collective-permute-start(bf16[512,1536]{1,0:T(8,128)(2,1)} %constant_dynamic-slice_fusion.1), channel_id=1, source_target_pairs={{0,4},{4,0},{1,5},{5,1},{2,6},{6,2},{3,7},{7,3},{8,12},{12,8},{9,1... | collective-permute-start | bytes 4718600 | tf_op jit(solution)/shard_map/ppermute | solution.py:191
  (105 other events, 1978.4 us)
Sparse Core Ops, SparseCore 0:
  11.3 220.8 all-gather.9
  233.8 78.9 all-gather.11
  314.9 381.0 all-gather.7
  697.4 195.1 all-gather.13
  895.4 188.8 reduce-scatter.4
  1086.6 373.3 reduce-scatter.8
  1462.3 213.5 reduce-scatter.6
  1678.2 78.1 reduce-scatter.10

commit v10 on v9

--- a/solution.py
+++ b/solution.py
@@ -288,9 +288,13 @@
 ):
     n_f = lax.axis_size("fsdp")
     d_f = D // n_f
-    qkv_full = spread(ctx_half(jnp.swapaxes(qkv_weight, 0, 1), 2))
-    qkv_parts = [qkv_full[:, i] for i in range(3)]
-    out_full = spread(ctx_half(out_weight, 0))
+    attn_weights = spread(
+        jnp.concatenate(
+            [ctx_half(jnp.swapaxes(qkv_weight, 0, 1), 2), ctx_half(out_weight, 0).T[None]]
+        )
+    )
+    qkv_parts = [attn_weights[:, i] for i in range(3)]
+    out_full = attn_weights[:, 3]
     gu_full = spread(ctx_half(gate_up_weight, 2).reshape(d_f, -1))
     down_full = spread(ctx_half(down_weight, 0))
 
@@ -325,9 +329,9 @@
     seq_len = attn_full.shape[1]
     cosine, sine = rope_tables(seq_len)
     cotan_full = gather_rows(after(cotangent, attn_full))
-    proj = [into(attn_full, part) for part in qkv_parts]
+    proj = after([into(attn_full, part) for part in qkv_parts], cotan_full)
     queries, keys, values, head_outs, norms = attend_forward(*proj, cosine, sine)
-    resid = input_float + scatter_rows(out_blocks(head_outs, out_full))
+    resid = input_float + scatter_rows(in_blocks(head_outs, out_full))
     rms_two = lax.rsqrt(row_total(jnp.sum(resid * resid, axis=-1)) / D + rms_epsilon)[:, None]
     normed_ffn = (resid * rms_two * ffn_scale).astype(BF)
     ffn_full = gather_rows(normed_ffn)
@@ -354,15 +358,18 @@
     ffn_gain_part = jnp.sum(grad_nffn * resid * rms_two, axis=0)
     grad_branch = grad_resid.astype(BF)
     branch_full = gather_rows(grad_branch)
-    grad_heads = back_out(branch_full, out_full).astype(BF)
+    grad_heads = into(branch_full, out_full).astype(BF)
     grad_proj = attend_backward(
         queries, keys, values, head_outs, norms, grad_heads, cosine, sine
     )
     joined = jnp.concatenate(grad_proj, axis=1)
     qkv_part = in_part(attn_full, joined)
     qkv_sum = [owners(qkv_part)]
+    gu_halves = trade_ctx(gu_sum, 0)
     grad_nattn = scatter_rows(in_blocks(joined, jnp.concatenate(qkv_parts, axis=2)))
-    out_sum = owners(out_part(after(head_outs, qkv_part), branch_full))
+    grad_nattn = after(grad_nattn, gu_halves)
+    part = out_part(after(head_outs, qkv_part), branch_full)
+    out_sum = owners(jnp.concatenate(trade_ctx(part, 2), axis=1))
     hidden = after(hidden, qkv_part)
     layer_output = (resid + scatter_rows(out_blocks(hidden, down_full))).astype(BF)
     attn_term = grad_nattn * attn_scale
@@ -372,9 +379,8 @@
     gain_grads = total_rows(jnp.stack([attn_gain_part, ffn_gain_part]))
 
     down_grad = out_grad(down_sum)
-    rows, other_rows = trade_ctx(gu_sum, 0)
     gu_grad = jnp.concatenate(
-        [v.reshape(v.shape[0], 2, -1) for v in (rows, other_rows)], axis=2
+        [v.reshape(v.shape[0], 2, -1) for v in gu_halves], axis=2
     ).astype(F32)
     done = (down_grad, gu_grad, grad_input, layer_output, gain_grads)
     qkv_grad = []
@@ -386,7 +392,7 @@
             qkv_grad.append(jnp.concatenate(both, axis=1).astype(F32))
         done = done + (qkv_grad[-1],)
     qkv_grad = jnp.stack(qkv_grad, axis=1)
-    out_weight_grad = out_grad(after(out_sum, done))
+    out_weight_grad = after(out_sum, done).astype(F32)
 
     return (
         layer_output,

time: 1800 us -> 1810 us (level)
  waiting for transfers between devices: 872 us -> 935 us
  blocking collectives: 61.7 us -> 26.2 us
  local copies, waits for them, and re-layouts: 145 us -> 125 us
    ppermute x95, waiting for transfers between devices: 478 us -> 563 us  [swap(): lax.ppermute(values, axis, [(i, i ^ step) for i in range(lax.axis_size(ax...]
    psum x4, blocking collectives: 61.7 us -> 26.2 us  [row_total(): return lax.psum(values, 'tp')]
    dynamic_update_slice x64, local copies, waits for them, and re-layouts: 71.4 us -> 47.1 us  [gather_rows(): full = lax.dynamic_update_slice(full, piece[None], start)]
    reduce_scatter x4, waiting for transfers between devices: 119 us -> 97.6 us  [owners(): return lax.psum_scatter(grad, 'fsdp', scatter_dimension=0, tiled=False)]
    all_gather x4 -> x3, waiting for transfers between devices: 274 us -> 274 us  [spread(): return lax.all_gather(weight, 'fsdp', axis=0, tiled=False)]
  transfers between devices with their start and end apart: 103 -> 102, of which waited for: 38 -> 43; matrix products, arithmetic and copies ran while one was open for 37% -> 36% of each run, Pallas kernels for 4% -> 4%
where the time goes in v10:
time: 1810 us
  waiting for transfers between devices  935 us (52%)
  matrix products  455 us (25%)
  local copies, waits for them, and re-layouts  125 us (7%)
  other arithmetic  99.7 us (6%)
  Pallas kernels  79 us (4%)
  starting transfers between devices  74.5 us (4%)
  blocking collectives  26.2 us (1%)
    ppermute x95, waiting for transfers between devices, swap(): lax.ppermute(values, axis, [(i, i ^ step) for i in range(lax.axis_size(ax...  563 us
    dot_general x32, matrix products, mm(): return lax.dot_general(left, right, dims, preferred_element_type=F32)  455 us
    all_gather x3, waiting for transfers between devices, spread(): return lax.all_gather(weight, 'fsdp', axis=0, tiled=False)  274 us
    reduce_scatter x4, waiting for transfers between devices, owners(): return lax.psum_scatter(grad, 'fsdp', scatter_dimension=0, tiled=False)  97.6 us
    ppermute x95, starting transfers between devices, swap(): lax.ppermute(values, axis, [(i, i ^ step) for i in range(lax.axis_size(ax...  74.2 us
    dynamic_update_slice x64, local copies, waits for them, and re-layouts, gather_rows(): full = lax.dynamic_update_slice(full, piece[None], start)  47.1 us
    pallas_call x1, Pallas kernels, attend_backward(): pl.pallas_call(kernel, grid=(heads, blocks), in_specs=[row, col, col, row...  43.9 us
  transfers between devices with their start and end apart: 102, of which 43 were waited for; matrix products, arithmetic and copies ran while one was open for 36% of the time, Pallas kernels for 4%

profile of v10, /device:TPU:0, one launch (start us, length us, event | category | flops | bytes accessed | tf_op | source)
XLA Modules:
  0.0 1810.7 jit_solution(10755603007753950938)
XLA Ops:
  23.9 8.5 psum.28
  40.0 20.3 %collective-permute-done = bf16[512,1024]{1,0:T(8,128)(2,1)} collective-permute-done((bf16[512,1024]{1,0:T(8,128)(2,1)}, bf16[512,1024]{1,0:T(8,128)(2,1)}, u32[]{:S(2)}, u32[]{:S(2)}) %collective-permute-start) | collective-permute-done | bytes 1048608 | tf_op jit(solution)/shard_map/ppermute | solution.py:191
  67.4 19.3 %collective-permute-done.7 = bf16[512,1024]{1,0:T(8,128)(2,1)S(1)} collective-permute-done((bf16[512,1024]{1,0:T(8,128)(2,1)}, bf16[512,1024]{1,0:T(8,128)(2,1)S(1)}, u32[]{:S(2)}, u32[]{:S(2)}) %collective-permute-start.7) | collective-permute-done | bytes 1048608 | tf_op jit(solution)/shard_map/ppermute | solution.py:191
  88.6 18.0 collective-permute-done.2
  124.4 18.0 collective-permute-done.14
  153.6 13.4 collective-permute-done.21
  168.6 19.7 %collective-permute-done.16 = bf16[512,1024]{1,0:T(8,128)(2,1)S(1)} collective-permute-done((bf16[512,1024]{1,0:T(8,128)(2,1)S(1)}, bf16[512,1024]{1,0:T(8,128)(2,1)S(1)}, u32[]{:S(2)}, u32[]{:S(2)}) %collective-permute-start.16) | collective-permute-done | bytes 1048608 | tf_op jit(solution)/shard_map/ppermute | solution.py:191
  192.5 8.4 collective-permute-done.23
  211.5 94.2 %all-gather.8.cloned.1.call-done = bf16[16,1024,512]{2,1,0:T(8,128)(2,1)} async-done(((bf16[4,1024,512]{2,1,0:T(8,128)(2,1)}), bf16[16,1024,512]{2,1,0:T(8,128)(2,1)}) %all-gather.8.cloned.1.call-update) | async-done | bytes 16777232 | tf_op jit(solution)/shard_map/all_gather | solution.py:263
  305.7 15.2 convolution_bitcast_fusion.1.v_in
  320.9 16.1 convolution_bitcast_fusion.2.k_in
  337.1 12.4 convolution_bitcast_fusion.3.q_in
  349.4 35.1 %shard_map.143 = (bf16[2048,512]{1,0:T(8,128)(2,1)S(1)}, bf16[2048,512]{1,0:T(8,128)(2,1)}, bf16[2048,512]{1,0:T(8,128)(2,1)}, bf16[2048,512]{1,0:T(8,128)(2,1)}, f32[4,1,2048]{2,1,0:T(1,128)S(1)}) custom-call(f32[2048,512]{1,0:T(8,128)} %convolution_bitcast_fusion.3.q_in, f32[2048,512]{1,0:T(8,128)} %convolution_bitcast_fusion.2.k_in, ...), custom_call_target="tpu_custom_call" | custom-call | flops 5368709120 | bytes 20971520 | tf_op jit(solution)/shard_map/pallas_call | solution.py:88
  384.5 12.4 slice_bitcast_fusion.18
  424.4 16.7 collective-permute-done.31
  445.4 18.1 collective-permute-done.29
  468.2 19.5 %collective-permute-done.33 = bf16[512,1024]{1,0:T(8,128)(2,1)S(1)} collective-permute-done((bf16[512,1024]{1,0:T(8,128)(2,1)S(1)}, bf16[512,1024]{1,0:T(8,128)(2,1)S(1)}, u32[]{:S(2)}, u32[]{:S(2)}) %collective-permute-start.33) | collective-permute-done | bytes 1048608 | tf_op jit(solution)/shard_map/ppermute | solution.py:191
  506.5 21.4 %collective-permute-done.36 = bf16[512,1024]{1,0:T(8,128)(2,1)} collective-permute-done((bf16[512,1024]{1,0:T(8,128)(2,1)}, bf16[512,1024]{1,0:T(8,128)(2,1)}, u32[]{:S(2)}, u32[]{:S(2)}) %collective-permute-start.36) | collective-permute-done | bytes 1048608 | tf_op jit(solution)/shard_map/ppermute | solution.py:191
  533.0 6.2 broadcast.35.clone.2
  544.2 9.0 collective-permute-done.43
  556.1 17.8 collective-permute-done.38
  580.6 10.1 collective-permute-done.45
  601.4 87.2 %all-gather.6.cloned.1.call-done = bf16[4,1024,2752]{1,2,0:T(8,128)(2,1)} async-done(((bf16[1,1024,2752]{1,2,0:T(8,128)(2,1)}), bf16[4,1024,2752]{1,2,0:T(8,128)(2,1)}) %all-gather.6.cloned.1.call-update) | async-done | bytes 22544400 | tf_op jit(solution)/shard_map/all_gather | solution.py:263
  688.6 56.8 %convolution_bitcast_fusion = f32[2048,2752]{0,1:T(8,128)} fusion(bf16[4,2048,1024]{2,1,0:T(8,128)(2,1)} %bitcast_dynamic-update-slice_fusion.16, bf16[4,1024,2752]{1,2,0:T(8,128)(2,1)} %all-gather.6.cloned.1.call-done), kind=kOutput, calls=%fused_computation.2 | convolution fusion | flops 46170898432 | bytes 61865984 | tf_op jit(solution)/shard_map/dot_general | solution.py:21
  745.4 8.9 multiply_convert_fusion
  754.4 9.9 fusion.57
  764.3 7.9 fusion.56
  772.2 7.9 fusion.55
  780.1 7.9 fusion.54
  793.2 92.7 %all-gather.10.cloned.1.call-done = bf16[5504,1024]{1,0:T(8,128)(2,1)} async-done(((bf16[1376,1024]{1,0:T(8,128)(2,1)}), bf16[5504,1024]{1,0:T(8,128)(2,1)}) %all-gather.10.cloned.1.call-update) | async-done | bytes 11272208 | tf_op jit(solution)/shard_map/all_gather | solution.py:263
  885.9 37.0 %fusion.3 = (bf16[2048,1376]{0,1:T(8,128)(2,1)S(1)}, bf16[2048,1376]{0,1:T(8,128)(2,1)}) fusion(f32[2048,2752]{0,1:T(8,128)} %convolution_bitcast_fusion, bf16[4,2048,1024]{2,1,0:T(8,128)(2,1)} %bitcast_dynamic-update-slice_fusion.32, bf16[4,1376,1024]{2,1,0:T(8,128)(2,1)} %bitcast.518), kind=kOutput, calls=%fused_computation.11 | convolution fusion | flops 23122083840 | bytes 61865984 | tf_op jit(solution)/shard_map/dot_general | solution.py:21
  925.4 54.7 %convolution_convert_fusion = bf16[4,1024,2752]{1,2,0:T(8,128)(2,1)} fusion(bf16[4,2048,1024]{2,1,0:T(8,128)(2,1)} %bitcast_dynamic-update-slice_fusion.16, bf16[2048,1376]{0,1:T(8,128)(2,1)} %get-tuple-element.57, bf16[2048,1376]{0,1:T(8,128)(2,1)S(1)} %get-tuple-element.56), kind=kOutput, calls=%fused_computation | convolution fusion | flops 46204715008 | bytes 50593792 | tf_op jit(solution)/shard_map/dot_general | solution.py:21
  980.1 97.5 %reduce-scatter.5.cloned.1.call-done = bf16[1,1376,1024]{2,1,0:T(8,128)(2,1)} async-done(((bf16[4,1376,1024]{2,1,0:T(8,128)(2,1)}), bf16[1,1376,1024]{2,1,0:T(8,128)(2,1)}) %reduce-scatter.5.cloned.1.call-update) | async-done | bytes 2818064 | tf_op jit(solution)/shard_map/reduce_scatter | solution.py:259
  1077.7 17.2 fusion.42
  1095.0 17.3 fusion.39
  1112.9 17.8 add_convert_fusion.4
  1136.4 17.7 add_convert_fusion.5
  1165.5 15.3 collective-permute-done.51
  1186.9 19.1 %collective-permute-done.55 = bf16[512,1024]{1,0:T(8,128)(2,1)S(1)} collective-permute-done((bf16[512,1024]{1,0:T(8,128)(2,1)S(1)}, bf16[512,1024]{1,0:T(8,128)(2,1)S(1)}, u32[]{:S(2)}, u32[]{:S(2)}) %collective-permute-start.55) | collective-permute-done | bytes 1048608 | tf_op jit(solution)/shard_map/ppermute | solution.py:191
  1215.3 6.6 fusion.146
  1225.6 21.0 %collective-permute-done.58 = bf16[512,1024]{1,0:T(8,128)(2,1)S(1)} collective-permute-done((bf16[512,1024]{1,0:T(8,128)(2,1)S(1)}, bf16[512,1024]{1,0:T(8,128)(2,1)S(1)}, u32[]{:S(2)}, u32[]{:S(2)}) %collective-permute-start.58) | collective-permute-done | bytes 1048608 | tf_op jit(solution)/shard_map/ppermute | solution.py:191
  1252.3 19.8 %collective-permute-done.65 = bf16[512,1024]{1,0:T(8,128)(2,1)S(1)} collective-permute-done((bf16[512,1024]{1,0:T(8,128)(2,1)S(1)}, bf16[512,1024]{1,0:T(8,128)(2,1)S(1)}, u32[]{:S(2)}, u32[]{:S(2)}) %collective-permute-start.65) | collective-permute-done | bytes 1048608 | tf_op jit(solution)/shard_map/ppermute | solution.py:191
  1272.8 20.0 %collective-permute-done.60 = bf16[512,1024]{1,0:T(8,128)(2,1)S(1)} collective-permute-done((bf16[512,1024]{1,0:T(8,128)(2,1)S(1)}, bf16[512,1024]{1,0:T(8,128)(2,1)S(1)}, u32[]{:S(2)}, u32[]{:S(2)}) %collective-permute-start.60) | collective-permute-done | bytes 1048608 | tf_op jit(solution)/shard_map/ppermute | solution.py:191
  1301.6 13.7 bitcast_convert_fusion.g
  1315.2 43.9 %shard_map.144 = (bf16[2048,512]{1,0:T(8,128)(2,1)S(1)}, bf16[2048,512]{1,0:T(8,128)(2,1)}, bf16[2048,512]{1,0:T(8,128)(2,1)}) custom-call(bf16[2048,512]{1,0:T(8,128)(2,1)} %copy-done.2, bf16[2048,512]{1,0:T(8,128)(2,1)} %get-tuple-element.34.k, bf16[2048,512]{1,0:T(8,128)(2,1)} %get-tuple-element.35.v, bf16[2048,512]{1,0:T(8,128)(2,1)} %get-tuple-element.46.o, ...), custom_call_target="tpu_custom_call" | custom-call | flops 13421772800 | bytes 16777216 | tf_op jit(solution)/shard_map/pallas_call | solution.py:164
  1364.2 31.0 %convolution_convert_fusion.1 = bf16[4,1024,1536]{2,1,0:T(8,128)(2,1)} fusion(bf16[4,2048,1024]{2,1,0:T(8,128)(2,1)} %copy-done.16, bf16[2048,1536]{1,0:T(8,128)(2,1)S(1)} %constant_dynamic-update-slice_fusion), kind=kOutput, calls=%fused_computation.1 | convolution fusion | flops 25776095232 | bytes 35651584 | tf_op jit(solution)/shard_map/dot_general | solution.py:21
  1398.2 6.3 pad_maximum_fusion
  1404.6 25.2 %collective-permute-done.92 = bf16[1376,512]{1,0:T(8,128)(2,1)S(1)} collective-permute-done((bf16[1376,512]{1,0:T(8,128)(2,1)S(1)}, bf16[1376,512]{1,0:T(8,128)(2,1)S(1)}, u32[]{:S(2)}, u32[]{:S(2)}) %collective-permute-start.92) | collective-permute-done | bytes 1409056 | tf_op jit(solution)/shard_map/ppermute | solution.py:191
  1433.8 11.3 convolution_convert_fusion.2
  1455.1 12.1 convolution_convert_fusion.3
  1469.1 10.2 convolution_convert_fusion.4
  1479.7 10.2 convolution_convert_fusion.5
  1490.1 25.4 %collective-permute-done.94 = bf16[4,512,512]{2,1,0:T(8,128)(2,1)S(1)} collective-permute-done((bf16[4,512,512]{2,1,0:T(8,128)(2,1)S(1)}, bf16[4,512,512]{2,1,0:T(8,128)(2,1)S(1)}, u32[]{:S(2)}, u32[]{:S(2)}) %collective-permute-start.94) | collective-permute-done | bytes 2097184 | tf_op jit(solution)/shard_map/ppermute | solution.py:191
  1518.9 11.1 add_convert_fusion
  1532.0 11.6 add_convert_fusion.1
  1550.7 9.0 add_convert_fusion.2
  1563.9 10.3 add_convert_fusion.3
  1583.5 18.3 %collective-permute-done.75 = bf16[512,1024]{1,0:T(8,128)(2,1)} collective-permute-done((bf16[512,1024]{1,0:T(8,128)(2,1)}, bf16[512,1024]{1,0:T(8,128)(2,1)}, u32[]{:S(2)}, u32[]{:S(2)}) %collective-permute-start.75) | collective-permute-done | bytes 1048608 | tf_op jit(solution)/shard_map/ppermute | solution.py:191
  1606.2 13.8 collective-permute-done.78
  1623.3 19.1 %collective-permute-done.84 = bf16[512,1024]{1,0:T(8,128)(2,1)S(1)} collective-permute-done((bf16[512,1024]{1,0:T(8,128)(2,1)S(1)}, bf16[512,1024]{1,0:T(8,128)(2,1)S(1)}, u32[]{:S(2)}, u32[]{:S(2)}) %collective-permute-start.84) | collective-permute-done | bytes 1048608 | tf_op jit(solution)/shard_map/ppermute | solution.py:191
  1644.0 40.5 %collective-permute-done.87 = bf16[512,1024]{1,0:T(8,128)(2,1)S(1)} collective-permute-done((bf16[512,1024]{1,0:T(8,128)(2,1)S(1)}, bf16[512,1024]{1,0:T(8,128)(2,1)S(1)}, u32[]{:S(2)}, u32[]{:S(2)}) %collective-permute-start.87) | collective-permute-done | bytes 1048608 | tf_op jit(solution)/shard_map/ppermute | solution.py:191
  1690.1 16.9 collective-permute-done.73
  1707.6 20.8 %collective-permute-done.79 = bf16[512,1024]{1,0:T(8,128)(2,1)} collective-permute-done((bf16[512,1024]{1,0:T(8,128)(2,1)S(1)}, bf16[512,1024]{1,0:T(8,128)(2,1)}, u32[]{:S(2)}, u32[]{:S(2)}) %collective-permute-start.79) | collective-permute-done | bytes 1048608 | tf_op jit(solution)/shard_map/ppermute | solution.py:191
  1766.5 31.3 %collective-permute-done.93 = bf16[512,1536]{1,0:T(8,128)(2,1)} collective-permute-done((bf16[512,1536]{1,0:T(8,128)(2,1)S(1)}, bf16[512,1536]{1,0:T(8,128)(2,1)}, u32[]{:S(2)}, u32[]{:S(2)}) %collective-permute-start.93) | collective-permute-done | bytes 1572896 | tf_op jit(solution)/shard_map/ppermute | solution.py:191
  (485 shorter events, 332.6 us)
Async XLA Ops:
  7.2 298.5 %all-gather.8.cloned.1.call-start = ((), (), s32[]{:S(2)}) async-start(), calls=%async_computation.9 | async-start | bytes 20971520 | tf_op jit(solution)/shard_map/all_gather | solution.py:263
  16.1 672.5 %all-gather.6.cloned.1.call-start = ((), (), s32[]{:S(2)}) async-start(), calls=%async_computation.4 | async-start | bytes 28180480 | tf_op jit(solution)/shard_map/all_gather | solution.py:263
  21.9 864.1 %all-gather.10.cloned.1.call-start = ((), (), s32[]{:S(2)}) async-start(), calls=%async_computation.10 | async-start | bytes 14090240 | tf_op jit(solution)/shard_map/all_gather | solution.py:263
  37.9 27.7 %collective-permute-start.1 = (bf16[512,1024]{1,0:T(8,128)(2,1)}, bf16[512,1024]{1,0:T(8,128)(2,1)}, u32[]{:S(2)}, u32[]{:S(2)}) collective-permute-start(bf16[512,1024]{1,0:T(8,128)(2,1)} %get-tuple-element.101), channel_id=1, source_target_pairs={{0,2},{1,3},{2,0},{3,1},{4,6},{5,7},{6,4},{7,5},{8,10},{9,11},{10,... | collective-permute-start | bytes 3145736 | tf_op jit(solution)/shard_map/ppermute | solution.py:191
  38.4 28.8 %collective-permute-start.3 = (bf16[512,1024]{1,0:T(8,128)(2,1)}, bf16[512,1024]{1,0:T(8,128)(2,1)}, u32[]{:S(2)}, u32[]{:S(2)}) collective-permute-start(bf16[512,1024]{1,0:T(8,128)(2,1)} %get-tuple-element.101), channel_id=1, source_target_pairs={{0,1},{1,0},{2,3},{3,2},{4,5},{5,4},{6,7},{7,6},{8,9},{9,8},{10,11... | collective-permute-start | bytes 3145736 | tf_op jit(solution)/shard_map/ppermute | solution.py:191
  38.4 48.3 %collective-permute-start.7 = (bf16[512,1024]{1,0:T(8,128)(2,1)}, bf16[512,1024]{1,0:T(8,128)(2,1)S(1)}, u32[]{:S(2)}, u32[]{:S(2)}) collective-permute-start(bf16[512,1024]{1,0:T(8,128)(2,1)} %get-tuple-element.100), channel_id=1, source_target_pairs={{0,2},{1,3},{2,0},{3,1},{4,6},{5,7},{6,4},{7,5},{8,10},{9,11},{10,... | collective-permute-start | bytes 3145736 | tf_op jit(solution)/shard_map/ppermute | solution.py:191
  60.3 46.2 %collective-permute-start.2 = (bf16[512,1024]{1,0:T(8,128)(2,1)}, bf16[512,1024]{1,0:T(8,128)(2,1)}, u32[]{:S(2)}, u32[]{:S(2)}) collective-permute-start(bf16[512,1024]{1,0:T(8,128)(2,1)} %collective-permute-done), channel_id=1, source_target_pairs={{0,2},{1,3},{2,0},{3,1},{4,6},{5,7},{6,4},{7,5},{8,10},{9,11},{10,... | collective-permute-start | bytes 3145736 | tf_op jit(solution)/shard_map/ppermute | solution.py:191
  64.2 45.0 %collective-permute-start.4 = (bf16[512,1024]{1,0:T(8,128)(2,1)}, bf16[512,1024]{1,0:T(8,128)(2,1)S(1)}, u32[]{:S(2)}, u32[]{:S(2)}) collective-permute-start(bf16[512,1024]{1,0:T(8,128)(2,1)} %collective-permute-done), channel_id=1, source_target_pairs={{0,1},{1,0},{2,3},{3,2},{4,5},{5,4},{6,7},{7,6},{8,9},{9,8},{10,11... | collective-permute-start | bytes 3145736 | tf_op jit(solution)/shard_map/ppermute | solution.py:191
  65.6 44.3 %collective-permute-start.8 = (bf16[512,1024]{1,0:T(8,128)(2,1)}, bf16[512,1024]{1,0:T(8,128)(2,1)S(1)}, u32[]{:S(2)}, u32[]{:S(2)}) collective-permute-start(bf16[512,1024]{1,0:T(8,128)(2,1)} %get-tuple-element.100), channel_id=1, source_target_pairs={{0,4},{4,0},{1,5},{5,1},{2,6},{6,2},{3,7},{7,3},{8,12},{12,8},{9,1... | collective-permute-start | bytes 3145736 | tf_op jit(solution)/shard_map/ppermute | solution.py:191
  67.2 42.8 %collective-permute-start.5 = (bf16[512,1024]{1,0:T(8,128)(2,1)}, bf16[512,1024]{1,0:T(8,128)(2,1)S(1)}, u32[]{:S(2)}, u32[]{:S(2)}) collective-permute-start(bf16[512,1024]{1,0:T(8,128)(2,1)} %collective-permute-done.1), channel_id=1, source_target_pairs={{0,1},{1,0},{2,3},{3,2},{4,5},{5,4},{6,7},{7,6},{8,9},{9,8},{10,11... | collective-permute-start | bytes 3145736 | tf_op jit(solution)/shard_map/ppermute | solution.py:191
  86.7 27.3 %collective-permute-start.9 = (bf16[512,1024]{1,0:T(8,128)(2,1)S(1)}, bf16[512,1024]{1,0:T(8,128)(2,1)S(1)}, u32[]{:S(2)}, u32[]{:S(2)}) collective-permute-start(bf16[512,1024]{1,0:T(8,128)(2,1)S(1)} %collective-permute-done.7), channel_id=1, source_target_pairs={{0,4},{4,0},{1,5},{5,1},{2,6},{6,2},{3,7},{7,3},{8,12},{12,8},{9,1... | collective-permute-start | bytes 3145736 | tf_op jit(solution)/shard_map/ppermute | solution.py:191
  118.5 34.3 %collective-permute-start.15 = (bf16[512,1024]{1,0:T(8,128)(2,1)S(1)}, bf16[512,1024]{1,0:T(8,128)(2,1)S(1)}, u32[]{:S(2)}, u32[]{:S(2)}) collective-permute-start(bf16[512,1024]{1,0:T(8,128)(2,1)S(1)} %get-tuple-element.99), channel_id=1, source_target_pairs={{0,2},{1,3},{2,0},{3,1},{4,6},{5,7},{6,4},{7,5},{8,10},{9,11},{10,... | collective-permute-start | bytes 3145736 | tf_op jit(solution)/shard_map/ppermute | solution.py:191
  119.1 34.2 %collective-permute-start.17 = (bf16[512,1024]{1,0:T(8,128)(2,1)S(1)}, bf16[512,1024]{1,0:T(8,128)(2,1)S(1)}, u32[]{:S(2)}, u32[]{:S(2)}) collective-permute-start(bf16[512,1024]{1,0:T(8,128)(2,1)S(1)} %get-tuple-element.99), channel_id=1, source_target_pairs={{0,1},{1,0},{2,3},{3,2},{4,5},{5,4},{6,7},{7,6},{8,9},{9,8},{10,11... | collective-permute-start | bytes 3145736 | tf_op jit(solution)/shard_map/ppermute | solution.py:191
  119.1 47.9 %collective-permute-start.21 = (bf16[512,1024]{1,0:T(8,128)(2,1)S(1)}, bf16[512,1024]{1,0:T(8,128)(2,1)S(1)}, u32[]{:S(2)}, u32[]{:S(2)}) collective-permute-start(bf16[512,1024]{1,0:T(8,128)(2,1)S(1)} %get-tuple-element.98), channel_id=1, source_target_pairs={{0,2},{1,3},{2,0},{3,1},{4,6},{5,7},{6,4},{7,5},{8,10},{9,11},{10,... | collective-permute-start | bytes 3145736 | tf_op jit(solution)/shard_map/ppermute | solution.py:191
  142.4 45.9 %collective-permute-start.16 = (bf16[512,1024]{1,0:T(8,128)(2,1)S(1)}, bf16[512,1024]{1,0:T(8,128)(2,1)S(1)}, u32[]{:S(2)}, u32[]{:S(2)}) collective-permute-start(bf16[512,1024]{1,0:T(8,128)(2,1)S(1)} %collective-permute-done.14), channel_id=1, source_target_pairs={{0,2},{1,3},{2,0},{3,1},{4,6},{5,7},{6,4},{7,5},{8,10},{9,11},{10,... | collective-permute-start | bytes 3145736 | tf_op jit(solution)/shard_map/ppermute | solution.py:191
  151.8 38.7 %collective-permute-start.18 = (bf16[512,1024]{1,0:T(8,128)(2,1)S(1)}, bf16[512,1024]{1,0:T(8,128)(2,1)S(1)}, u32[]{:S(2)}, u32[]{:S(2)}) collective-permute-start(bf16[512,1024]{1,0:T(8,128)(2,1)S(1)} %collective-permute-done.14), channel_id=1, source_target_pairs={{0,1},{1,0},{2,3},{3,2},{4,5},{5,4},{6,7},{7,6},{8,9},{9,8},{10,11... | collective-permute-start | bytes 3145736 | tf_op jit(solution)/shard_map/ppermute | solution.py:191
  152.8 39.2 %collective-permute-start.22 = (bf16[512,1024]{1,0:T(8,128)(2,1)S(1)}, bf16[512,1024]{1,0:T(8,128)(2,1)S(1)}, u32[]{:S(2)}, u32[]{:S(2)}) collective-permute-start(bf16[512,1024]{1,0:T(8,128)(2,1)S(1)} %get-tuple-element.98), channel_id=1, source_target_pairs={{0,4},{4,0},{1,5},{5,1},{2,6},{6,2},{3,7},{7,3},{8,12},{12,8},{9,1... | collective-permute-start | bytes 3145736 | tf_op jit(solution)/shard_map/ppermute | solution.py:191
  153.3 38.7 %collective-permute-start.19 = (bf16[512,1024]{1,0:T(8,128)(2,1)S(1)}, bf16[512,1024]{1,0:T(8,128)(2,1)S(1)}, u32[]{:S(2)}, u32[]{:S(2)}) collective-permute-start(bf16[512,1024]{1,0:T(8,128)(2,1)S(1)} %collective-permute-done.15), channel_id=1, source_target_pairs={{0,1},{1,0},{2,3},{3,2},{4,5},{5,4},{6,7},{7,6},{8,9},{9,8},{10,11... | collective-permute-start | bytes 3145736 | tf_op jit(solution)/shard_map/ppermute | solution.py:191
  167.0 33.9 %collective-permute-start.23 = (bf16[512,1024]{1,0:T(8,128)(2,1)S(1)}, bf16[512,1024]{1,0:T(8,128)(2,1)S(1)}, u32[]{:S(2)}, u32[]{:S(2)}) collective-permute-start(bf16[512,1024]{1,0:T(8,128)(2,1)S(1)} %collective-permute-done.21), channel_id=1, source_target_pairs={{0,4},{4,0},{1,5},{5,1},{2,6},{6,2},{3,7},{7,3},{8,12},{12,8},{9,1... | collective-permute-start | bytes 3145736 | tf_op jit(solution)/shard_map/ppermute | solution.py:191
  423.8 39.7 %collective-permute-start.29 = (bf16[512,1024]{1,0:T(8,128)(2,1)S(1)}, bf16[512,1024]{1,0:T(8,128)(2,1)S(1)}, u32[]{:S(2)}, u32[]{:S(2)}) collective-permute-start(bf16[512,1024]{1,0:T(8,128)(2,1)S(1)} %dynamic-slice_bitcast_fusion.18), channel_id=1, source_target_pairs={{0,4},{4,0},{1,5},{5,1},{2,6},{6,2},{3,7},{7,3},{8,12},{12,8},{9,1... | collective-permute-start | bytes 3145736 | tf_op jit(solution)/shard_map/ppermute | solution.py:191
  442.9 44.7 %collective-permute-start.33 = (bf16[512,1024]{1,0:T(8,128)(2,1)S(1)}, bf16[512,1024]{1,0:T(8,128)(2,1)S(1)}, u32[]{:S(2)}, u32[]{:S(2)}) collective-permute-start(bf16[512,1024]{1,0:T(8,128)(2,1)S(1)} %get-tuple-element.96), channel_id=1, source_target_pairs={{0,2},{1,3},{2,0},{3,1},{4,6},{5,7},{6,4},{7,5},{8,10},{9,11},{10,... | collective-permute-start | bytes 3145736 | tf_op jit(solution)/shard_map/ppermute | solution.py:191
  444.0 43.7 %collective-permute-start.35 = (bf16[512,1024]{1,0:T(8,128)(2,1)S(1)}, bf16[512,1024]{1,0:T(8,128)(2,1)S(1)}, u32[]{:S(2)}, u32[]{:S(2)}) collective-permute-start(bf16[512,1024]{1,0:T(8,128)(2,1)S(1)} %fusion.100), channel_id=1, source_target_pairs={{0,4},{4,0},{1,5},{5,1},{2,6},{6,2},{3,7},{7,3},{8,12},{12,8},{9,1... | collective-permute-start | bytes 3145736 | tf_op jit(solution)/shard_map/ppermute | solution.py:191
  504.4 38.1 %collective-permute-start.37 = (bf16[512,1024]{1,0:T(8,128)(2,1)}, bf16[512,1024]{1,0:T(8,128)(2,1)}, u32[]{:S(2)}, u32[]{:S(2)}) collective-permute-start(bf16[512,1024]{1,0:T(8,128)(2,1)} %get-tuple-element.95), channel_id=1, source_target_pairs={{0,2},{1,3},{2,0},{3,1},{4,6},{5,7},{6,4},{7,5},{8,10},{9,11},{10,... | collective-permute-start | bytes 3145736 | tf_op jit(solution)/shard_map/ppermute | solution.py:191
  505.9 38.0 %collective-permute-start.39 = (bf16[512,1024]{1,0:T(8,128)(2,1)}, bf16[512,1024]{1,0:T(8,128)(2,1)}, u32[]{:S(2)}, u32[]{:S(2)}) collective-permute-start(bf16[512,1024]{1,0:T(8,128)(2,1)} %get-tuple-element.95), channel_id=1, source_target_pairs={{0,1},{1,0},{2,3},{3,2},{4,5},{5,4},{6,7},{7,6},{8,9},{9,8},{10,11... | collective-permute-start | bytes 3145736 | tf_op jit(solution)/shard_map/ppermute | solution.py:191
  506.0 47.3 %collective-permute-start.43 = (bf16[512,1024]{1,0:T(8,128)(2,1)}, bf16[512,1024]{1,0:T(8,128)(2,1)S(1)}, u32[]{:S(2)}, u32[]{:S(2)}) collective-permute-start(bf16[512,1024]{1,0:T(8,128)(2,1)} %get-tuple-element.94), channel_id=1, source_target_pairs={{0,2},{1,3},{2,0},{3,1},{4,6},{5,7},{6,4},{7,5},{8,10},{9,11},{10,... | collective-permute-start | bytes 3145736 | tf_op jit(solution)/shard_map/ppermute | solution.py:191
  527.9 46.0 %collective-permute-start.38 = (bf16[512,1024]{1,0:T(8,128)(2,1)}, bf16[512,1024]{1,0:T(8,128)(2,1)}, u32[]{:S(2)}, u32[]{:S(2)}) collective-permute-start(bf16[512,1024]{1,0:T(8,128)(2,1)} %collective-permute-done.36), channel_id=1, source_target_pairs={{0,2},{1,3},{2,0},{3,1},{4,6},{5,7},{6,4},{7,5},{8,10},{9,11},{10,... | collective-permute-start | bytes 3145736 | tf_op jit(solution)/shard_map/ppermute | solution.py:191
  532.9 544.7 %reduce-scatter.5.cloned.1.call-start = ((), (), s32[]{:S(2)}) async-start(), calls=%async_computation.5 | async-start | bytes 14090240 | tf_op jit(solution)/shard_map/reduce_scatter | solution.py:259
  540.2 38.4 %collective-permute-start.40 = (bf16[512,1024]{1,0:T(8,128)(2,1)}, bf16[512,1024]{1,0:T(8,128)(2,1)S(1)}, u32[]{:S(2)}, u32[]{:S(2)}) collective-permute-start(bf16[512,1024]{1,0:T(8,128)(2,1)} %collective-permute-done.36), channel_id=1, source_target_pairs={{0,1},{1,0},{2,3},{3,2},{4,5},{5,4},{6,7},{7,6},{8,9},{9,8},{10,11... | collective-permute-start | bytes 3145736 | tf_op jit(solution)/shard_map/ppermute | solution.py:191
  542.5 37.6 %collective-permute-start.44 = (bf16[512,1024]{1,0:T(8,128)(2,1)}, bf16[512,1024]{1,0:T(8,128)(2,1)S(1)}, u32[]{:S(2)}, u32[]{:S(2)}) collective-permute-start(bf16[512,1024]{1,0:T(8,128)(2,1)} %get-tuple-element.94), channel_id=1, source_target_pairs={{0,4},{4,0},{1,5},{5,1},{2,6},{6,2},{3,7},{7,3},{8,12},{12,8},{9,1... | collective-permute-start | bytes 3145736 | tf_op jit(solution)/shard_map/ppermute | solution.py:191
  544.0 36.1 %collective-permute-start.41 = (bf16[512,1024]{1,0:T(8,128)(2,1)}, bf16[512,1024]{1,0:T(8,128)(2,1)S(1)}, u32[]{:S(2)}, u32[]{:S(2)}) collective-permute-start(bf16[512,1024]{1,0:T(8,128)(2,1)} %collective-permute-done.37), channel_id=1, source_target_pairs={{0,1},{1,0},{2,3},{3,2},{4,5},{5,4},{6,7},{7,6},{8,9},{9,8},{10,11... | collective-permute-start | bytes 3145736 | tf_op jit(solution)/shard_map/ppermute | solution.py:191
  553.2 37.5 %collective-permute-start.45 = (bf16[512,1024]{1,0:T(8,128)(2,1)S(1)}, bf16[512,1024]{1,0:T(8,128)(2,1)S(1)}, u32[]{:S(2)}, u32[]{:S(2)}) collective-permute-start(bf16[512,1024]{1,0:T(8,128)(2,1)S(1)} %collective-permute-done.43), channel_id=1, source_target_pairs={{0,4},{4,0},{1,5},{5,1},{2,6},{6,2},{3,7},{7,3},{8,12},{12,8},{9,1... | collective-permute-start | bytes 3145736 | tf_op jit(solution)/shard_map/ppermute | solution.py:191
  793.2 784.3 %reduce-scatter.7.cloned.1.call-start = ((), (), s32[]{:S(2)}) async-start(), calls=%async_computation.6 | async-start | bytes 28180480 | tf_op jit(solution)/shard_map/reduce_scatter | solution.py:259
  1077.7 682.5 %reduce-scatter.9.cloned.1.call-start = ((), (), s32[]{:S(2)}) async-start(), calls=%async_computation.7 | async-start | bytes 15728640 | tf_op jit(solution)/shard_map/reduce_scatter | solution.py:259
  1134.9 27.3 %collective-permute-start.56 = (bf16[512,1024]{1,0:T(8,128)(2,1)}, bf16[512,1024]{1,0:T(8,128)(2,1)}, u32[]{:S(2)}, u32[]{:S(2)}) collective-permute-start(bf16[512,1024]{1,0:T(8,128)(2,1)} %get-tuple-element.93), channel_id=1, source_target_pairs={{0,2},{1,3},{2,0},{3,1},{4,6},{5,7},{6,4},{7,5},{8,10},{9,11},{10,... | collective-permute-start | bytes 3145736 | tf_op jit(solution)/shard_map/ppermute | solution.py:191
  1161.8 44.3 %collective-permute-start.55 = (bf16[512,1024]{1,0:T(8,128)(2,1)S(1)}, bf16[512,1024]{1,0:T(8,128)(2,1)S(1)}, u32[]{:S(2)}, u32[]{:S(2)}) collective-permute-start(bf16[512,1024]{1,0:T(8,128)(2,1)S(1)} %get-tuple-element.92), channel_id=1, source_target_pairs={{0,2},{1,3},{2,0},{3,1},{4,6},{5,7},{6,4},{7,5},{8,10},{9,11},{10,... | collective-permute-start | bytes 3145736 | tf_op jit(solution)/shard_map/ppermute | solution.py:191
  1163.9 42.2 %collective-permute-start.57 = (bf16[512,1024]{1,0:T(8,128)(2,1)S(1)}, bf16[512,1024]{1,0:T(8,128)(2,1)S(1)}, u32[]{:S(2)}, u32[]{:S(2)}) collective-permute-start(bf16[512,1024]{1,0:T(8,128)(2,1)S(1)} %fusion.96), channel_id=1, source_target_pairs={{0,4},{4,0},{1,5},{5,1},{2,6},{6,2},{3,7},{7,3},{8,12},{12,8},{9,1... | collective-permute-start | bytes 3145736 | tf_op jit(solution)/shard_map/ppermute | solution.py:191
  1223.6 27.0 %collective-permute-start.59 = (bf16[512,1024]{1,0:T(8,128)(2,1)S(1)}, bf16[512,1024]{1,0:T(8,128)(2,1)S(1)}, u32[]{:S(2)}, u32[]{:S(2)}) collective-permute-start(bf16[512,1024]{1,0:T(8,128)(2,1)S(1)} %get-tuple-element.91), channel_id=1, source_target_pairs={{0,2},{1,3},{2,0},{3,1},{4,6},{5,7},{6,4},{7,5},{8,10},{9,11},{10,... | collective-permute-start | bytes 3145736 | tf_op jit(solution)/shard_map/ppermute | solution.py:191
  1225.1 27.0 %collective-permute-start.61 = (bf16[512,1024]{1,0:T(8,128)(2,1)S(1)}, bf16[512,1024]{1,0:T(8,128)(2,1)S(1)}, u32[]{:S(2)}, u32[]{:S(2)}) collective-permute-start(bf16[512,1024]{1,0:T(8,128)(2,1)S(1)} %get-tuple-element.91), channel_id=1, source_target_pairs={{0,1},{1,0},{2,3},{3,2},{4,5},{5,4},{6,7},{7,6},{8,9},{9,8},{10,11... | collective-permute-start | bytes 3145736 | tf_op jit(solution)/shard_map/ppermute | solution.py:191
  1225.1 47.1 %collective-permute-start.65 = (bf16[512,1024]{1,0:T(8,128)(2,1)S(1)}, bf16[512,1024]{1,0:T(8,128)(2,1)S(1)}, u32[]{:S(2)}, u32[]{:S(2)}) collective-permute-start(bf16[512,1024]{1,0:T(8,128)(2,1)S(1)} %get-tuple-element.90), channel_id=1, source_target_pairs={{0,2},{1,3},{2,0},{3,1},{4,6},{5,7},{6,4},{7,5},{8,10},{9,11},{10,... | collective-permute-start | bytes 3145736 | tf_op jit(solution)/shard_map/ppermute | solution.py:191
  1246.6 46.1 %collective-permute-start.60 = (bf16[512,1024]{1,0:T(8,128)(2,1)S(1)}, bf16[512,1024]{1,0:T(8,128)(2,1)S(1)}, u32[]{:S(2)}, u32[]{:S(2)}) collective-permute-start(bf16[512,1024]{1,0:T(8,128)(2,1)S(1)} %collective-permute-done.58), channel_id=1, source_target_pairs={{0,2},{1,3},{2,0},{3,1},{4,6},{5,7},{6,4},{7,5},{8,10},{9,11},{10,... | collective-permute-start | bytes 3145736 | tf_op jit(solution)/shard_map/ppermute | solution.py:191
  1250.4 42.6 %collective-permute-start.62 = (bf16[512,1024]{1,0:T(8,128)(2,1)S(1)}, bf16[512,1024]{1,0:T(8,128)(2,1)S(1)}, u32[]{:S(2)}, u32[]{:S(2)}) collective-permute-start(bf16[512,1024]{1,0:T(8,128)(2,1)S(1)} %collective-permute-done.58), channel_id=1, source_target_pairs={{0,1},{1,0},{2,3},{3,2},{4,5},{5,4},{6,7},{7,6},{8,9},{9,8},{10,11... | collective-permute-start | bytes 3145736 | tf_op jit(solution)/shard_map/ppermute | solution.py:191
  1250.6 43.1 %collective-permute-start.66 = (bf16[512,1024]{1,0:T(8,128)(2,1)S(1)}, bf16[512,1024]{1,0:T(8,128)(2,1)S(1)}, u32[]{:S(2)}, u32[]{:S(2)}) collective-permute-start(bf16[512,1024]{1,0:T(8,128)(2,1)S(1)} %get-tuple-element.90), channel_id=1, source_target_pairs={{0,4},{4,0},{1,5},{5,1},{2,6},{6,2},{3,7},{7,3},{8,12},{12,8},{9,1... | collective-permute-start | bytes 3145736 | tf_op jit(solution)/shard_map/ppermute | solution.py:191
  1252.1 41.7 %collective-permute-start.63 = (bf16[512,1024]{1,0:T(8,128)(2,1)S(1)}, bf16[512,1024]{1,0:T(8,128)(2,1)S(1)}, u32[]{:S(2)}, u32[]{:S(2)}) collective-permute-start(bf16[512,1024]{1,0:T(8,128)(2,1)S(1)} %collective-permute-done.59), channel_id=1, source_target_pairs={{0,1},{1,0},{2,3},{3,2},{4,5},{5,4},{6,7},{7,6},{8,9},{9,8},{10,11... | collective-permute-start | bytes 3145736 | tf_op jit(solution)/shard_map/ppermute | solution.py:191
  1395.3 367.8 %reduce-scatter.11.cloned.1.call-start = ((), (), s32[]{:S(2)}) async-start(), calls=%async_computation.8 | async-start | bytes 5242880 | tf_op jit(solution)/shard_map/reduce_scatter | solution.py:259
  1396.8 33.0 %collective-permute-start.92 = (bf16[1376,512]{1,0:T(8,128)(2,1)S(1)}, bf16[1376,512]{1,0:T(8,128)(2,1)S(1)}, u32[]{:S(2)}, u32[]{:S(2)}) collective-permute-start(bf16[1376,512]{1,0:T(8,128)(2,1)S(1)} %dynamic-slice_bitcast_fusion.2), channel_id=1, source_target_pairs={{0,4},{4,0},{1,5},{5,1},{2,6},{6,2},{3,7},{7,3},{8,12},{12,8},{9,1... | collective-permute-start | bytes 4227080 | tf_op jit(solution)/shard_map/ppermute | solution.py:191
  1445.1 73.8 %collective-permute-start.82 = (bf16[2048,1024]{1,0:T(8,128)(2,1)}, bf16[2048,1024]{1,0:T(8,128)(2,1)}, u32[]{:S(2)}, u32[]{:S(2)}) collective-permute-start(bf16[2048,1024]{1,0:T(8,128)(2,1)} %convolution_convert_fusion.2), channel_id=1, source_target_pairs={{0,1},{1,0},{2,3},{3,2},{4,5},{5,4},{6,7},{7,6},{8,9},{9,8},{10,11... | collective-permute-start | bytes 12582920 | tf_op jit(solution)/shard_map/ppermute | solution.py:191
  1467.5 48.1 %collective-permute-start.94 = (bf16[4,512,512]{2,1,0:T(8,128)(2,1)S(1)}, bf16[4,512,512]{2,1,0:T(8,128)(2,1)S(1)}, u32[]{:S(2)}, u32[]{:S(2)}) collective-permute-start(bf16[4,512,512]{2,1,0:T(8,128)(2,1)S(1)} %constant_dynamic-slice_fusion), channel_id=1, source_target_pairs={{0,4},{4,0},{1,5},{5,1},{2,6},{6,2},{3,7},{7,3},{8,12},{12,8},{9,1... | collective-permute-start | bytes 6291464 | tf_op jit(solution)/shard_map/ppermute | solution.py:191
  1468.9 63.0 %collective-permute-start.80 = (bf16[2048,1024]{1,0:T(8,128)(2,1)}, bf16[2048,1024]{1,0:T(8,128)(2,1)}, u32[]{:S(2)}, u32[]{:S(2)}) collective-permute-start(bf16[2048,1024]{1,0:T(8,128)(2,1)} %convolution_convert_fusion.3), channel_id=1, source_target_pairs={{0,1},{1,0},{2,3},{3,2},{4,5},{5,4},{6,7},{7,6},{8,9},{9,8},{10,11... | collective-permute-start | bytes 12582920 | tf_op jit(solution)/shard_map/ppermute | solution.py:191
  1479.4 70.9 %collective-permute-start.74 = (bf16[2048,1024]{1,0:T(8,128)(2,1)}, bf16[2048,1024]{1,0:T(8,128)(2,1)}, u32[]{:S(2)}, u32[]{:S(2)}) collective-permute-start(bf16[2048,1024]{1,0:T(8,128)(2,1)} %convolution_convert_fusion.4), channel_id=1, source_target_pairs={{0,1},{1,0},{2,3},{3,2},{4,5},{5,4},{6,7},{7,6},{8,9},{9,8},{10,11... | collective-permute-start | bytes 12582920 | tf_op jit(solution)/shard_map/ppermute | solution.py:191
  1489.9 72.7 %collective-permute-start.72 = (bf16[2048,1024]{1,0:T(8,128)(2,1)}, bf16[2048,1024]{1,0:T(8,128)(2,1)}, u32[]{:S(2)}, u32[]{:S(2)}) collective-permute-start(bf16[2048,1024]{1,0:T(8,128)(2,1)} %convolution_convert_fusion.5), channel_id=1, source_target_pairs={{0,1},{1,0},{2,3},{3,2},{4,5},{5,4},{6,7},{7,6},{8,9},{9,8},{10,11... | collective-permute-start | bytes 12582920 | tf_op jit(solution)/shard_map/ppermute | solution.py:191
  1530.6 44.9 %collective-permute-start.83 = (bf16[512,1024]{1,0:T(8,128)(2,1)S(1)}, bf16[512,1024]{1,0:T(8,128)(2,1)S(1)}, u32[]{:S(2)}, u32[]{:S(2)}) collective-permute-start(bf16[512,1024]{1,0:T(8,128)(2,1)S(1)} %dynamic-slice_bitcast_fusion.5), channel_id=1, source_target_pairs={{0,4},{4,0},{1,5},{5,1},{2,6},{6,2},{3,7},{7,3},{8,12},{12,8},{9,1... | collective-permute-start | bytes 3145736 | tf_op jit(solution)/shard_map/ppermute | solution.py:191
  1546.5 36.5 %collective-permute-start.81 = (bf16[512,1024]{1,0:T(8,128)(2,1)}, bf16[512,1024]{1,0:T(8,128)(2,1)}, u32[]{:S(2)}, u32[]{:S(2)}) collective-permute-start(bf16[512,1024]{1,0:T(8,128)(2,1)} %dynamic-slice_bitcast_fusion.6), channel_id=1, source_target_pairs={{0,4},{4,0},{1,5},{5,1},{2,6},{6,2},{3,7},{7,3},{8,12},{12,8},{9,1... | collective-permute-start | bytes 3145736 | tf_op jit(solution)/shard_map/ppermute | solution.py:191
  1548.7 31.0 %collective-permute-start.86 = (bf16[512,1024]{1,0:T(8,128)(2,1)}, bf16[512,1024]{1,0:T(8,128)(2,1)}, u32[]{:S(2)}, u32[]{:S(2)}) collective-permute-start(bf16[512,1024]{1,0:T(8,128)(2,1)} %get-tuple-element.87), channel_id=1, source_target_pairs={{0,2},{1,3},{2,0},{3,1},{4,6},{5,7},{6,4},{7,5},{8,10},{9,11},{10,... | collective-permute-start | bytes 3145736 | tf_op jit(solution)/shard_map/ppermute | solution.py:191
  1550.3 55.1 %collective-permute-start.85 = (bf16[512,1024]{1,0:T(8,128)(2,1)}, bf16[512,1024]{1,0:T(8,128)(2,1)}, u32[]{:S(2)}, u32[]{:S(2)}) collective-permute-start(bf16[512,1024]{1,0:T(8,128)(2,1)} %get-tuple-element.86), channel_id=1, source_target_pairs={{0,2},{1,3},{2,0},{3,1},{4,6},{5,7},{6,4},{7,5},{8,10},{9,11},{10,... | collective-permute-start | bytes 3145736 | tf_op jit(solution)/shard_map/ppermute | solution.py:191
  1562.5 39.2 %collective-permute-start.75 = (bf16[512,1024]{1,0:T(8,128)(2,1)}, bf16[512,1024]{1,0:T(8,128)(2,1)}, u32[]{:S(2)}, u32[]{:S(2)}) collective-permute-start(bf16[512,1024]{1,0:T(8,128)(2,1)} %dynamic-slice_bitcast_fusion.9), channel_id=1, source_target_pairs={{0,4},{4,0},{1,5},{5,1},{2,6},{6,2},{3,7},{7,3},{8,12},{12,8},{9,1... | collective-permute-start | bytes 3145736 | tf_op jit(solution)/shard_map/ppermute | solution.py:191
  1575.4 44.6 %collective-permute-start.78 = (bf16[512,1024]{1,0:T(8,128)(2,1)}, bf16[512,1024]{1,0:T(8,128)(2,1)}, u32[]{:S(2)}, u32[]{:S(2)}) collective-permute-start(bf16[512,1024]{1,0:T(8,128)(2,1)} %get-tuple-element.89), channel_id=1, source_target_pairs={{0,2},{1,3},{2,0},{3,1},{4,6},{5,7},{6,4},{7,5},{8,10},{9,11},{10,... | collective-permute-start | bytes 3145736 | tf_op jit(solution)/shard_map/ppermute | solution.py:191
  1579.7 150.5 %collective-permute-start.88 = (bf16[512,2752]{0,1:T(8,128)(2,1)S(1)}, bf16[512,2752]{0,1:T(8,128)(2,1)}, u32[]{:S(2)}, u32[]{:S(2)}) collective-permute-start(bf16[512,2752]{0,1:T(8,128)(2,1)S(1)} %dynamic-slice_bitcast_fusion.1), channel_id=1, source_target_pairs={{0,4},{4,0},{1,5},{5,1},{2,6},{6,2},{3,7},{7,3},{8,12},{12,8},{9,1... | collective-permute-start | bytes 8454152 | tf_op jit(solution)/shard_map/ppermute | solution.py:191
  1583.0 59.4 %collective-permute-start.84 = (bf16[512,1024]{1,0:T(8,128)(2,1)S(1)}, bf16[512,1024]{1,0:T(8,128)(2,1)S(1)}, u32[]{:S(2)}, u32[]{:S(2)}) collective-permute-start(bf16[512,1024]{1,0:T(8,128)(2,1)S(1)} %copy-done.30), channel_id=1, source_target_pairs={{0,2},{1,3},{2,0},{3,1},{4,6},{5,7},{6,4},{7,5},{8,10},{9,11},{10,... | collective-permute-start | bytes 3145736 | tf_op jit(solution)/shard_map/ppermute | solution.py:191
  1601.7 82.8 %collective-permute-start.87 = (bf16[512,1024]{1,0:T(8,128)(2,1)S(1)}, bf16[512,1024]{1,0:T(8,128)(2,1)S(1)}, u32[]{:S(2)}, u32[]{:S(2)}) collective-permute-start(bf16[512,1024]{1,0:T(8,128)(2,1)S(1)} %fusion.88), channel_id=1, source_target_pairs={{0,4},{4,0},{1,5},{5,1},{2,6},{6,2},{3,7},{7,3},{8,12},{12,8},{9,1... | collective-permute-start | bytes 3145736 | tf_op jit(solution)/shard_map/ppermute | solution.py:191
  1605.4 101.5 %collective-permute-start.73 = (bf16[512,1024]{1,0:T(8,128)(2,1)S(1)}, bf16[512,1024]{1,0:T(8,128)(2,1)S(1)}, u32[]{:S(2)}, u32[]{:S(2)}) collective-permute-start(bf16[512,1024]{1,0:T(8,128)(2,1)S(1)} %dynamic-slice_bitcast_fusion.10), channel_id=1, source_target_pairs={{0,4},{4,0},{1,5},{5,1},{2,6},{6,2},{3,7},{7,3},{8,12},{12,8},{9,1... | collective-permute-start | bytes 3145736 | tf_op jit(solution)/shard_map/ppermute | solution.py:191
  1620.0 86.9 %collective-permute-start.76 = (bf16[512,1024]{1,0:T(8,128)(2,1)S(1)}, bf16[512,1024]{1,0:T(8,128)(2,1)S(1)}, u32[]{:S(2)}, u32[]{:S(2)}) collective-permute-start(bf16[512,1024]{1,0:T(8,128)(2,1)S(1)} %fusion.94), channel_id=1, source_target_pairs={{0,2},{1,3},{2,0},{3,1},{4,6},{5,7},{6,4},{7,5},{8,10},{9,11},{10,... | collective-permute-start | bytes 3145736 | tf_op jit(solution)/shard_map/ppermute | solution.py:191
  1642.4 65.2 %collective-permute-start.77 = (bf16[512,1024]{1,0:T(8,128)(2,1)S(1)}, bf16[512,1024]{1,0:T(8,128)(2,1)S(1)}, u32[]{:S(2)}, u32[]{:S(2)}) collective-permute-start(bf16[512,1024]{1,0:T(8,128)(2,1)S(1)} %get-tuple-element.88), channel_id=1, source_target_pairs={{0,2},{1,3},{2,0},{3,1},{4,6},{5,7},{6,4},{7,5},{8,10},{9,11},{10,... | collective-permute-start | bytes 3145736 | tf_op jit(solution)/shard_map/ppermute | solution.py:191
  1684.5 43.9 %collective-permute-start.79 = (bf16[512,1024]{1,0:T(8,128)(2,1)S(1)}, bf16[512,1024]{1,0:T(8,128)(2,1)}, u32[]{:S(2)}, u32[]{:S(2)}) collective-permute-start(bf16[512,1024]{1,0:T(8,128)(2,1)S(1)} %fusion.92), channel_id=1, source_target_pairs={{0,4},{4,0},{1,5},{5,1},{2,6},{6,2},{3,7},{7,3},{8,12},{12,8},{9,1... | collective-permute-start | bytes 3145736 | tf_op jit(solution)/shard_map/ppermute | solution.py:191
  1761.7 36.1 %collective-permute-start.93 = (bf16[512,1536]{1,0:T(8,128)(2,1)S(1)}, bf16[512,1536]{1,0:T(8,128)(2,1)}, u32[]{:S(2)}, u32[]{:S(2)}) collective-permute-start(bf16[512,1536]{1,0:T(8,128)(2,1)S(1)} %constant_dynamic-slice_fusion.1), channel_id=1, source_target_pairs={{0,4},{4,0},{1,5},{5,1},{2,6},{6,2},{3,7},{7,3},{8,12},{12,8},{9,1... | collective-permute-start | bytes 4718600 | tf_op jit(solution)/shard_map/ppermute | solution.py:191
  (105 other events, 1693.4 us)
Sparse Core Ops, SparseCore 0:
  16.2 289.4 all-gather.7
  307.8 380.7 all-gather.5
  690.7 195.1 all-gather.9
  888.7 188.8 reduce-scatter.4
  1079.9 373.3 reduce-scatter.6
  1455.4 213.5 reduce-scatter.8
  1671.3 77.9 reduce-scatter.10

commit v11 on v10

--- a/solution.py
+++ b/solution.py
@@ -214,13 +214,18 @@
     return with_layout_constraint(full, Layout((0, 1, 2)))
 
 
-def scatter_rows(block_of):
-    n_t, n_c = lax.axis_size("tp"), lax.axis_size("ctx")
-    me_t, me_c = lax.axis_index("tp"), lax.axis_index("ctx")
+def core_sums(block_of):
+    me_t = lax.axis_index("tp")
     sums = {}
-    for dt in range(0, n_t, 2):
+    for dt in range(0, lax.axis_size("tp"), 2):
         got = swap(block_of(me_t ^ (dt + 1)).astype(BF), "tp", 0)
         sums[dt] = (block_of(me_t ^ dt) + got.astype(F32)).astype(BF)
+    return sums
+
+
+def scatter_sums(sums):
+    n_c = lax.axis_size("ctx")
+    me_c = lax.axis_index("ctx")
     rows = sums[0].shape[0] // n_c
     cols = sums[0].shape[1]
     half = rows // 2
@@ -243,6 +248,10 @@
             held = left
         done.append(held[(0, 0)])
     return jnp.concatenate(done, axis=0)
+
+
+def scatter_rows(block_of):
+    return scatter_sums(core_sums(block_of))
 
 
 def ctx_half(weight, axis):
@@ -350,8 +359,12 @@
         axis=1,
     ).astype(BF)
     gu_part = in_part(ffn_full, grad_gu)
-    gu_sum = owners(after(gu_part, down_sum))
-    grad_nffn = after(scatter_rows(in_blocks(grad_gu, gu_full)), (gu_part, down_sum))
+    sums = core_sums(out_blocks(after(hidden, gu_part), down_full))
+    gu_sum = owners(after(gu_part, (down_sum, tuple(sums.values()))))
+    layer_output = (resid + scatter_sums(sums)).astype(BF)
+    grad_gu = after(grad_gu, tuple(sums.values()))
+    grad_nffn = scatter_rows(in_blocks(grad_gu, gu_full))
+    grad_nffn = after(grad_nffn, (gu_part, down_sum, layer_output))
     ffn_term = grad_nffn * ffn_scale
     ffn_dot = row_total(jnp.sum(ffn_term * resid, axis=-1))[:, None]
     grad_resid = cotangent.astype(F32) + rms_two * ffn_term - resid * rms_two**3 * ffn_dot / D
@@ -370,8 +383,6 @@
     grad_nattn = after(grad_nattn, gu_halves)
     part = out_part(after(head_outs, qkv_part), branch_full)
     out_sum = owners(jnp.concatenate(trade_ctx(part, 2), axis=1))
-    hidden = after(hidden, qkv_part)
-    layer_output = (resid + scatter_rows(out_blocks(hidden, down_full))).astype(BF)
     attn_term = grad_nattn * attn_scale
     attn_dot = row_total(jnp.sum(attn_term * input_float, axis=-1))[:, None]
     grad_input = grad_resid + rms_one * attn_term - input_float * rms_one**3 * attn_dot / D

time: 1810 us -> 1770 us (0.978)
  waiting for transfers between devices: 935 us -> 873 us
    ppermute x95, waiting for transfers between devices: 563 us -> 508 us  [swap(): lax.ppermute(values, axis, [(i, i ^ step) for i in range(lax.axis_size(ax...]
  transfers between devices with their start and end apart: 102 -> 102, of which waited for: 43 -> 42; matrix products, arithmetic and copies ran while one was open for 36% -> 38% of each run, Pallas kernels for 4% -> 4%
where the time goes in v11:
time: 1770 us
  waiting for transfers between devices  873 us (49%)
  matrix products  452 us (26%)
  local copies, waits for them, and re-layouts  134 us (8%)
  other arithmetic  115 us (6%)
  Pallas kernels  79 us (4%)
  starting transfers between devices  71.5 us (4%)
  blocking collectives  27 us (2%)
    ppermute x95, waiting for transfers between devices, swap(): lax.ppermute(values, axis, [(i, i ^ step) for i in range(lax.axis_size(ax...  508 us
    dot_general x32, matrix products, mm(): return lax.dot_general(left, right, dims, preferred_element_type=F32)  452 us
    all_gather x3, waiting for transfers between devices, spread(): return lax.all_gather(weight, 'fsdp', axis=0, tiled=False)  276 us
    reduce_scatter x4, waiting for transfers between devices, owners(): return lax.psum_scatter(grad, 'fsdp', scatter_dimension=0, tiled=False)  89.5 us
    ppermute x95, starting transfers between devices, swap(): lax.ppermute(values, axis, [(i, i ^ step) for i in range(lax.axis_size(ax...  71.2 us
    dynamic_update_slice x64, local copies, waits for them, and re-layouts, gather_rows(): full = lax.dynamic_update_slice(full, piece[None], start)  47.1 us
    pallas_call x1, Pallas kernels, attend_backward(): pl.pallas_call(kernel, grid=(heads, blocks), in_specs=[row, col, col, row...  44 us
  transfers between devices with their start and end apart: 102, of which 42 were waited for; matrix products, arithmetic and copies ran while one was open for 38% of the time, Pallas kernels for 4%

profile of v11, /device:TPU:0, one launch (start us, length us, event | category | flops | bytes accessed | tf_op | source)
XLA Modules:
  0.0 1767.4 jit_solution(17974895649100072118)
XLA Ops:
  23.9 8.8 psum.28
  40.2 20.4 %collective-permute-done = bf16[512,1024]{1,0:T(8,128)(2,1)} collective-permute-done((bf16[512,1024]{1,0:T(8,128)(2,1)}, bf16[512,1024]{1,0:T(8,128)(2,1)}, u32[]{:S(2)}, u32[]{:S(2)}) %collective-permute-start) | collective-permute-done | bytes 1048608 | tf_op jit(solution)/shard_map/ppermute | solution.py:191
  67.7 19.3 %collective-permute-done.7 = bf16[512,1024]{1,0:T(8,128)(2,1)S(1)} collective-permute-done((bf16[512,1024]{1,0:T(8,128)(2,1)}, bf16[512,1024]{1,0:T(8,128)(2,1)S(1)}, u32[]{:S(2)}, u32[]{:S(2)}) %collective-permute-start.7) | collective-permute-done | bytes 1048608 | tf_op jit(solution)/shard_map/ppermute | solution.py:191
  88.8 18.0 %collective-permute-done.2 = bf16[512,1024]{1,0:T(8,128)(2,1)} collective-permute-done((bf16[512,1024]{1,0:T(8,128)(2,1)}, bf16[512,1024]{1,0:T(8,128)(2,1)}, u32[]{:S(2)}, u32[]{:S(2)}) %collective-permute-start.2) | collective-permute-done | bytes 1048608 | tf_op jit(solution)/shard_map/ppermute | solution.py:191
  124.7 18.0 %collective-permute-done.14 = bf16[512,1024]{1,0:T(8,128)(2,1)S(1)} collective-permute-done((bf16[512,1024]{1,0:T(8,128)(2,1)S(1)}, bf16[512,1024]{1,0:T(8,128)(2,1)S(1)}, u32[]{:S(2)}, u32[]{:S(2)}) %collective-permute-start.14) | collective-permute-done | bytes 1048608 | tf_op jit(solution)/shard_map/ppermute | solution.py:191
  144.9 6.1 broadcast.35.clone.1
  153.9 13.4 collective-permute-done.21
  168.9 19.8 %collective-permute-done.16 = bf16[512,1024]{1,0:T(8,128)(2,1)S(1)} collective-permute-done((bf16[512,1024]{1,0:T(8,128)(2,1)S(1)}, bf16[512,1024]{1,0:T(8,128)(2,1)S(1)}, u32[]{:S(2)}, u32[]{:S(2)}) %collective-permute-start.16) | collective-permute-done | bytes 1048608 | tf_op jit(solution)/shard_map/ppermute | solution.py:191
  192.8 8.3 collective-permute-done.23
  211.7 94.0 %all-gather.8.cloned.1.call-done = bf16[16,1024,512]{2,1,0:T(8,128)(2,1)} async-done(((bf16[4,1024,512]{2,1,0:T(8,128)(2,1)}), bf16[16,1024,512]{2,1,0:T(8,128)(2,1)}) %all-gather.8.cloned.1.call-update) | async-done | bytes 16777232 | tf_op jit(solution)/shard_map/all_gather | solution.py:272
  305.7 15.2 convolution_bitcast_fusion.1.v_in
  320.9 16.1 convolution_bitcast_fusion.2.k_in
  337.0 12.4 convolution_bitcast_fusion.3.q_in
  349.4 35.1 %shard_map.143 = (bf16[2048,512]{1,0:T(8,128)(2,1)S(1)}, bf16[2048,512]{1,0:T(8,128)(2,1)}, bf16[2048,512]{1,0:T(8,128)(2,1)}, bf16[2048,512]{1,0:T(8,128)(2,1)}, f32[4,1,2048]{2,1,0:T(1,128)S(1)}) custom-call(f32[2048,512]{1,0:T(8,128)} %convolution_bitcast_fusion.3.q_in, f32[2048,512]{1,0:T(8,128)} %convolution_bitcast_fusion.2.k_in, ...), custom_call_target="tpu_custom_call" | custom-call | flops 5368709120 | bytes 20971520 | tf_op jit(solution)/shard_map/pallas_call | solution.py:88
  384.5 12.3 slice_bitcast_fusion.18
  424.2 16.7 collective-permute-done.31
  445.3 18.1 %collective-permute-done.29 = bf16[512,1024]{1,0:T(8,128)(2,1)S(1)} collective-permute-done((bf16[512,1024]{1,0:T(8,128)(2,1)S(1)}, bf16[512,1024]{1,0:T(8,128)(2,1)S(1)}, u32[]{:S(2)}, u32[]{:S(2)}) %collective-permute-start.29) | collective-permute-done | bytes 1048608 | tf_op jit(solution)/shard_map/ppermute | solution.py:191
  468.0 19.5 %collective-permute-done.33 = bf16[512,1024]{1,0:T(8,128)(2,1)S(1)} collective-permute-done((bf16[512,1024]{1,0:T(8,128)(2,1)S(1)}, bf16[512,1024]{1,0:T(8,128)(2,1)S(1)}, u32[]{:S(2)}, u32[]{:S(2)}) %collective-permute-start.33) | collective-permute-done | bytes 1048608 | tf_op jit(solution)/shard_map/ppermute | solution.py:191
  506.4 21.4 %collective-permute-done.36 = bf16[512,1024]{1,0:T(8,128)(2,1)} collective-permute-done((bf16[512,1024]{1,0:T(8,128)(2,1)}, bf16[512,1024]{1,0:T(8,128)(2,1)}, u32[]{:S(2)}, u32[]{:S(2)}) %collective-permute-start.36) | collective-permute-done | bytes 1048608 | tf_op jit(solution)/shard_map/ppermute | solution.py:191
  531.2 6.2 broadcast.35.clone.2
  542.4 10.8 collective-permute-done.43
  556.1 17.8 %collective-permute-done.38 = bf16[512,1024]{1,0:T(8,128)(2,1)} collective-permute-done((bf16[512,1024]{1,0:T(8,128)(2,1)}, bf16[512,1024]{1,0:T(8,128)(2,1)}, u32[]{:S(2)}, u32[]{:S(2)}) %collective-permute-start.38) | collective-permute-done | bytes 1048608 | tf_op jit(solution)/shard_map/ppermute | solution.py:191
  580.6 8.3 collective-permute-done.45
  599.5 89.1 %all-gather.6.cloned.1.call-done = bf16[4,1024,2752]{1,2,0:T(8,128)(2,1)} async-done(((bf16[1,1024,2752]{1,2,0:T(8,128)(2,1)}), bf16[4,1024,2752]{1,2,0:T(8,128)(2,1)}) %all-gather.6.cloned.1.call-update) | async-done | bytes 22544400 | tf_op jit(solution)/shard_map/all_gather | solution.py:272
  688.6 57.0 %convolution_bitcast_fusion = f32[2048,2752]{0,1:T(8,128)} fusion(bf16[4,2048,1024]{2,1,0:T(8,128)(2,1)} %bitcast_dynamic-update-slice_fusion.16, bf16[4,1024,2752]{1,2,0:T(8,128)(2,1)} %all-gather.6.cloned.1.call-done), kind=kOutput, calls=%fused_computation.2 | convolution fusion | flops 46170898432 | bytes 61865984 | tf_op jit(solution)/shard_map/dot_general | solution.py:21
  745.6 9.0 multiply_convert_fusion
  754.5 9.7 fusion.57
  764.3 7.9 fusion.56
  772.2 7.9 fusion.55
  780.1 7.9 fusion.54
  793.2 92.7 %all-gather.10.cloned.1.call-done = bf16[5504,1024]{1,0:T(8,128)(2,1)} async-done(((bf16[1376,1024]{1,0:T(8,128)(2,1)}), bf16[5504,1024]{1,0:T(8,128)(2,1)}) %all-gather.10.cloned.1.call-update) | async-done | bytes 11272208 | tf_op jit(solution)/shard_map/all_gather | solution.py:272
  885.9 37.5 %fusion.3 = (bf16[2048,1376]{0,1:T(8,128)(2,1)S(1)}, bf16[2048,1376]{0,1:T(8,128)(2,1)}) fusion(f32[2048,2752]{0,1:T(8,128)} %convolution_bitcast_fusion, bf16[4,2048,1024]{2,1,0:T(8,128)(2,1)} %bitcast_dynamic-update-slice_fusion.32, bf16[4,1376,1024]{2,1,0:T(8,128)(2,1)} %bitcast.520), kind=kOutput, calls=%fused_computation.11 | convolution fusion | flops 23122083840 | bytes 61865984 | tf_op jit(solution)/shard_map/dot_general | solution.py:21
  925.8 54.8 %convolution_convert_fusion = bf16[4,1024,2752]{1,2,0:T(8,128)(2,1)} fusion(bf16[4,2048,1024]{2,1,0:T(8,128)(2,1)} %bitcast_dynamic-update-slice_fusion.16, bf16[2048,1376]{0,1:T(8,128)(2,1)} %get-tuple-element.59, bf16[2048,1376]{0,1:T(8,128)(2,1)S(1)} %get-tuple-element.58), kind=kOutput, calls=%fused_computation | convolution fusion | flops 46204715008 | bytes 50593792 | tf_op jit(solution)/shard_map/dot_general | solution.py:21
  980.7 9.8 convolution_convert_fusion.5
  990.6 8.7 convolution_convert_fusion.4
  999.8 8.6 add_convert_fusion.5
  1008.4 8.6 add_convert_fusion.4
  1017.0 60.6 %reduce-scatter.5.cloned.1.call-done = bf16[1,1376,1024]{2,1,0:T(8,128)(2,1)} async-done(((bf16[4,1376,1024]{2,1,0:T(8,128)(2,1)}), bf16[1,1376,1024]{2,1,0:T(8,128)(2,1)}) %reduce-scatter.5.cloned.1.call-update) | async-done | bytes 2818064 | tf_op jit(solution)/shard_map/reduce_scatter | solution.py:268
  1077.7 7.9 pad_maximum_fusion.2
  1085.6 16.8 fusion.42
  1108.0 16.6 fusion.39
  1138.2 17.0 add_convert_fusion.2
  1163.2 17.2 add_convert_fusion.3
  1190.2 10.5 collective-permute-done.64
  1213.5 18.7 %collective-permute-done.59 = bf16[512,1024]{1,0:T(8,128)(2,1)} collective-permute-done((bf16[512,1024]{1,0:T(8,128)(2,1)S(1)}, bf16[512,1024]{1,0:T(8,128)(2,1)}, u32[]{:S(2)}, u32[]{:S(2)}) %collective-permute-start.59) | collective-permute-done | bytes 1048608 | tf_op jit(solution)/shard_map/ppermute | solution.py:191
  1234.3 12.8 collective-permute-done.63
  1262.5 6.9 fusion.146
  1272.7 21.4 %collective-permute-done.66 = bf16[512,1024]{1,0:T(8,128)(2,1)S(1)} collective-permute-done((bf16[512,1024]{1,0:T(8,128)(2,1)S(1)}, bf16[512,1024]{1,0:T(8,128)(2,1)S(1)}, u32[]{:S(2)}, u32[]{:S(2)}) %collective-permute-start.66) | collective-permute-done | bytes 1048608 | tf_op jit(solution)/shard_map/ppermute | solution.py:191
  1299.4 19.9 %collective-permute-done.73 = bf16[512,1024]{1,0:T(8,128)(2,1)S(1)} collective-permute-done((bf16[512,1024]{1,0:T(8,128)(2,1)S(1)}, bf16[512,1024]{1,0:T(8,128)(2,1)S(1)}, u32[]{:S(2)}, u32[]{:S(2)}) %collective-permute-start.73) | collective-permute-done | bytes 1048608 | tf_op jit(solution)/shard_map/ppermute | solution.py:191
  1320.3 19.6 %collective-permute-done.68 = bf16[512,1024]{1,0:T(8,128)(2,1)S(1)} collective-permute-done((bf16[512,1024]{1,0:T(8,128)(2,1)S(1)}, bf16[512,1024]{1,0:T(8,128)(2,1)S(1)}, u32[]{:S(2)}, u32[]{:S(2)}) %collective-permute-start.68) | collective-permute-done | bytes 1048608 | tf_op jit(solution)/shard_map/ppermute | solution.py:191
  1348.7 13.7 bitcast_convert_fusion.g
  1362.4 44.0 %shard_map.144 = (bf16[2048,512]{1,0:T(8,128)(2,1)S(1)}, bf16[2048,512]{1,0:T(8,128)(2,1)}, bf16[2048,512]{1,0:T(8,128)(2,1)}) custom-call(bf16[2048,512]{1,0:T(8,128)(2,1)} %copy-done.2, bf16[2048,512]{1,0:T(8,128)(2,1)} %get-tuple-element.39.k, bf16[2048,512]{1,0:T(8,128)(2,1)} %get-tuple-element.40.v, bf16[2048,512]{1,0:T(8,128)(2,1)} %get-tuple-element.48.o, ...), custom_call_target="tpu_custom_call" | custom-call | flops 13421772800 | bytes 16777216 | tf_op jit(solution)/shard_map/pallas_call | solution.py:164
  1411.4 31.0 %convolution_convert_fusion.1 = bf16[4,1024,1536]{2,1,0:T(8,128)(2,1)} fusion(bf16[4,2048,1024]{2,1,0:T(8,128)(2,1)} %copy-done.15, bf16[2048,1536]{1,0:T(8,128)(2,1)S(1)} %constant_dynamic-update-slice_fusion), kind=kOutput, calls=%fused_computation.1 | convolution fusion | flops 25776095232 | bytes 35651584 | tf_op jit(solution)/shard_map/dot_general | solution.py:21
  1442.6 7.4 pad_maximum_fusion
  1450.1 15.7 convolution_convert_fusion.2
  1479.5 11.5 convolution_convert_fusion.3
  1493.3 33.4 %collective-permute-done.94 = bf16[4,512,512]{2,1,0:T(8,128)(2,1)} collective-permute-done((bf16[4,512,512]{2,1,0:T(8,128)(2,1)S(1)}, bf16[4,512,512]{2,1,0:T(8,128)(2,1)}, u32[]{:S(2)}, u32[]{:S(2)}) %collective-permute-start.94) | collective-permute-done | bytes 2097184 | tf_op jit(solution)/shard_map/ppermute | solution.py:191
  1532.2 10.9 add_convert_fusion
  1551.7 11.1 add_convert_fusion.1
  1564.5 14.8 collective-permute-done.83
  1588.1 74.0 %collective-permute-done.81 = bf16[512,1024]{1,0:T(8,128)(2,1)S(1)} collective-permute-done((bf16[512,1024]{1,0:T(8,128)(2,1)S(1)}, bf16[512,1024]{1,0:T(8,128)(2,1)S(1)}, u32[]{:S(2)}, u32[]{:S(2)}) %collective-permute-start.81) | collective-permute-done | bytes 1048608 | tf_op jit(solution)/shard_map/ppermute | solution.py:191
  1662.7 21.4 %collective-permute-done.87 = bf16[512,1024]{1,0:T(8,128)(2,1)S(1)} collective-permute-done((bf16[512,1024]{1,0:T(8,128)(2,1)S(1)}, bf16[512,1024]{1,0:T(8,128)(2,1)S(1)}, u32[]{:S(2)}, u32[]{:S(2)}) %collective-permute-start.87) | collective-permute-done | bytes 1048608 | tf_op jit(solution)/shard_map/ppermute | solution.py:191
  1703.1 6.1 psum.31
  1720.6 28.9 %reduce-scatter.11.cloned.1.call-done = bf16[1,1024,512]{2,1,0:T(8,128)(2,1)} async-done(((bf16[4,1024,512]{2,1,0:T(8,128)(2,1)}), bf16[1,1024,512]{2,1,0:T(8,128)(2,1)}) %reduce-scatter.11.cloned.1.call-update) | async-done | bytes 1048592 | tf_op jit(solution)/shard_map/reduce_scatter | solution.py:268
  (480 shorter events, 337.0 us)
Async XLA Ops:
  7.2 298.5 %all-gather.8.cloned.1.call-start = ((), (), s32[]{:S(2)}) async-start(), calls=%async_computation.9 | async-start | bytes 20971520 | tf_op jit(solution)/shard_map/all_gather | solution.py:272
  16.1 672.5 %all-gather.6.cloned.1.call-start = ((), (), s32[]{:S(2)}) async-start(), calls=%async_computation.4 | async-start | bytes 28180480 | tf_op jit(solution)/shard_map/all_gather | solution.py:272
  21.9 864.1 %all-gather.10.cloned.1.call-start = ((), (), s32[]{:S(2)}) async-start(), calls=%async_computation.10 | async-start | bytes 14090240 | tf_op jit(solution)/shard_map/all_gather | solution.py:272
  38.2 27.7 %collective-permute-start.1 = (bf16[512,1024]{1,0:T(8,128)(2,1)}, bf16[512,1024]{1,0:T(8,128)(2,1)}, u32[]{:S(2)}, u32[]{:S(2)}) collective-permute-start(bf16[512,1024]{1,0:T(8,128)(2,1)} %get-tuple-element.103), channel_id=1, source_target_pairs={{0,2},{1,3},{2,0},{3,1},{4,6},{5,7},{6,4},{7,5},{8,10},{9,11},{10,... | collective-permute-start | bytes 3145736 | tf_op jit(solution)/shard_map/ppermute | solution.py:191
  38.7 28.8 %collective-permute-start.3 = (bf16[512,1024]{1,0:T(8,128)(2,1)}, bf16[512,1024]{1,0:T(8,128)(2,1)}, u32[]{:S(2)}, u32[]{:S(2)}) collective-permute-start(bf16[512,1024]{1,0:T(8,128)(2,1)} %get-tuple-element.103), channel_id=1, source_target_pairs={{0,1},{1,0},{2,3},{3,2},{4,5},{5,4},{6,7},{7,6},{8,9},{9,8},{10,11... | collective-permute-start | bytes 3145736 | tf_op jit(solution)/shard_map/ppermute | solution.py:191
  38.7 48.3 %collective-permute-start.7 = (bf16[512,1024]{1,0:T(8,128)(2,1)}, bf16[512,1024]{1,0:T(8,128)(2,1)S(1)}, u32[]{:S(2)}, u32[]{:S(2)}) collective-permute-start(bf16[512,1024]{1,0:T(8,128)(2,1)} %get-tuple-element.102), channel_id=1, source_target_pairs={{0,2},{1,3},{2,0},{3,1},{4,6},{5,7},{6,4},{7,5},{8,10},{9,11},{10,... | collective-permute-start | bytes 3145736 | tf_op jit(solution)/shard_map/ppermute | solution.py:191
  60.6 46.3 %collective-permute-start.2 = (bf16[512,1024]{1,0:T(8,128)(2,1)}, bf16[512,1024]{1,0:T(8,128)(2,1)}, u32[]{:S(2)}, u32[]{:S(2)}) collective-permute-start(bf16[512,1024]{1,0:T(8,128)(2,1)} %collective-permute-done), channel_id=1, source_target_pairs={{0,2},{1,3},{2,0},{3,1},{4,6},{5,7},{6,4},{7,5},{8,10},{9,11},{10,... | collective-permute-start | bytes 3145736 | tf_op jit(solution)/shard_map/ppermute | solution.py:191
  64.5 45.0 %collective-permute-start.4 = (bf16[512,1024]{1,0:T(8,128)(2,1)}, bf16[512,1024]{1,0:T(8,128)(2,1)S(1)}, u32[]{:S(2)}, u32[]{:S(2)}) collective-permute-start(bf16[512,1024]{1,0:T(8,128)(2,1)} %collective-permute-done), channel_id=1, source_target_pairs={{0,1},{1,0},{2,3},{3,2},{4,5},{5,4},{6,7},{7,6},{8,9},{9,8},{10,11... | collective-permute-start | bytes 3145736 | tf_op jit(solution)/shard_map/ppermute | solution.py:191
  65.9 44.3 %collective-permute-start.8 = (bf16[512,1024]{1,0:T(8,128)(2,1)}, bf16[512,1024]{1,0:T(8,128)(2,1)S(1)}, u32[]{:S(2)}, u32[]{:S(2)}) collective-permute-start(bf16[512,1024]{1,0:T(8,128)(2,1)} %get-tuple-element.102), channel_id=1, source_target_pairs={{0,4},{4,0},{1,5},{5,1},{2,6},{6,2},{3,7},{7,3},{8,12},{12,8},{9,1... | collective-permute-start | bytes 3145736 | tf_op jit(solution)/shard_map/ppermute | solution.py:191
  67.5 42.8 %collective-permute-start.5 = (bf16[512,1024]{1,0:T(8,128)(2,1)}, bf16[512,1024]{1,0:T(8,128)(2,1)S(1)}, u32[]{:S(2)}, u32[]{:S(2)}) collective-permute-start(bf16[512,1024]{1,0:T(8,128)(2,1)} %collective-permute-done.1), channel_id=1, source_target_pairs={{0,1},{1,0},{2,3},{3,2},{4,5},{5,4},{6,7},{7,6},{8,9},{9,8},{10,11... | collective-permute-start | bytes 3145736 | tf_op jit(solution)/shard_map/ppermute | solution.py:191
  87.0 27.2 %collective-permute-start.9 = (bf16[512,1024]{1,0:T(8,128)(2,1)S(1)}, bf16[512,1024]{1,0:T(8,128)(2,1)S(1)}, u32[]{:S(2)}, u32[]{:S(2)}) collective-permute-start(bf16[512,1024]{1,0:T(8,128)(2,1)S(1)} %collective-permute-done.7), channel_id=1, source_target_pairs={{0,4},{4,0},{1,5},{5,1},{2,6},{6,2},{3,7},{7,3},{8,12},{12,8},{9,1... | collective-permute-start | bytes 3145736 | tf_op jit(solution)/shard_map/ppermute | solution.py:191
  118.8 34.3 %collective-permute-start.15 = (bf16[512,1024]{1,0:T(8,128)(2,1)S(1)}, bf16[512,1024]{1,0:T(8,128)(2,1)S(1)}, u32[]{:S(2)}, u32[]{:S(2)}) collective-permute-start(bf16[512,1024]{1,0:T(8,128)(2,1)S(1)} %get-tuple-element.101), channel_id=1, source_target_pairs={{0,2},{1,3},{2,0},{3,1},{4,6},{5,7},{6,4},{7,5},{8,10},{9,11},{10,... | collective-permute-start | bytes 3145736 | tf_op jit(solution)/shard_map/ppermute | solution.py:191
  119.4 34.2 %collective-permute-start.17 = (bf16[512,1024]{1,0:T(8,128)(2,1)S(1)}, bf16[512,1024]{1,0:T(8,128)(2,1)S(1)}, u32[]{:S(2)}, u32[]{:S(2)}) collective-permute-start(bf16[512,1024]{1,0:T(8,128)(2,1)S(1)} %get-tuple-element.101), channel_id=1, source_target_pairs={{0,1},{1,0},{2,3},{3,2},{4,5},{5,4},{6,7},{7,6},{8,9},{9,8},{10,11... | collective-permute-start | bytes 3145736 | tf_op jit(solution)/shard_map/ppermute | solution.py:191
  119.4 47.9 %collective-permute-start.21 = (bf16[512,1024]{1,0:T(8,128)(2,1)S(1)}, bf16[512,1024]{1,0:T(8,128)(2,1)S(1)}, u32[]{:S(2)}, u32[]{:S(2)}) collective-permute-start(bf16[512,1024]{1,0:T(8,128)(2,1)S(1)} %get-tuple-element.100), channel_id=1, source_target_pairs={{0,2},{1,3},{2,0},{3,1},{4,6},{5,7},{6,4},{7,5},{8,10},{9,11},{10,... | collective-permute-start | bytes 3145736 | tf_op jit(solution)/shard_map/ppermute | solution.py:191
  142.7 45.9 %collective-permute-start.16 = (bf16[512,1024]{1,0:T(8,128)(2,1)S(1)}, bf16[512,1024]{1,0:T(8,128)(2,1)S(1)}, u32[]{:S(2)}, u32[]{:S(2)}) collective-permute-start(bf16[512,1024]{1,0:T(8,128)(2,1)S(1)} %collective-permute-done.14), channel_id=1, source_target_pairs={{0,2},{1,3},{2,0},{3,1},{4,6},{5,7},{6,4},{7,5},{8,10},{9,11},{10,... | collective-permute-start | bytes 3145736 | tf_op jit(solution)/shard_map/ppermute | solution.py:191
  152.0 38.8 %collective-permute-start.18 = (bf16[512,1024]{1,0:T(8,128)(2,1)S(1)}, bf16[512,1024]{1,0:T(8,128)(2,1)S(1)}, u32[]{:S(2)}, u32[]{:S(2)}) collective-permute-start(bf16[512,1024]{1,0:T(8,128)(2,1)S(1)} %collective-permute-done.14), channel_id=1, source_target_pairs={{0,1},{1,0},{2,3},{3,2},{4,5},{5,4},{6,7},{7,6},{8,9},{9,8},{10,11... | collective-permute-start | bytes 3145736 | tf_op jit(solution)/shard_map/ppermute | solution.py:191
  153.1 39.2 %collective-permute-start.22 = (bf16[512,1024]{1,0:T(8,128)(2,1)S(1)}, bf16[512,1024]{1,0:T(8,128)(2,1)S(1)}, u32[]{:S(2)}, u32[]{:S(2)}) collective-permute-start(bf16[512,1024]{1,0:T(8,128)(2,1)S(1)} %get-tuple-element.100), channel_id=1, source_target_pairs={{0,4},{4,0},{1,5},{5,1},{2,6},{6,2},{3,7},{7,3},{8,12},{12,8},{9,1... | collective-permute-start | bytes 3145736 | tf_op jit(solution)/shard_map/ppermute | solution.py:191
  153.6 38.7 %collective-permute-start.19 = (bf16[512,1024]{1,0:T(8,128)(2,1)S(1)}, bf16[512,1024]{1,0:T(8,128)(2,1)S(1)}, u32[]{:S(2)}, u32[]{:S(2)}) collective-permute-start(bf16[512,1024]{1,0:T(8,128)(2,1)S(1)} %collective-permute-done.15), channel_id=1, source_target_pairs={{0,1},{1,0},{2,3},{3,2},{4,5},{5,4},{6,7},{7,6},{8,9},{9,8},{10,11... | collective-permute-start | bytes 3145736 | tf_op jit(solution)/shard_map/ppermute | solution.py:191
  167.3 33.8 %collective-permute-start.23 = (bf16[512,1024]{1,0:T(8,128)(2,1)S(1)}, bf16[512,1024]{1,0:T(8,128)(2,1)S(1)}, u32[]{:S(2)}, u32[]{:S(2)}) collective-permute-start(bf16[512,1024]{1,0:T(8,128)(2,1)S(1)} %collective-permute-done.21), channel_id=1, source_target_pairs={{0,4},{4,0},{1,5},{5,1},{2,6},{6,2},{3,7},{7,3},{8,12},{12,8},{9,1... | collective-permute-start | bytes 3145736 | tf_op jit(solution)/shard_map/ppermute | solution.py:191
  423.6 39.8 %collective-permute-start.29 = (bf16[512,1024]{1,0:T(8,128)(2,1)S(1)}, bf16[512,1024]{1,0:T(8,128)(2,1)S(1)}, u32[]{:S(2)}, u32[]{:S(2)}) collective-permute-start(bf16[512,1024]{1,0:T(8,128)(2,1)S(1)} %dynamic-slice_bitcast_fusion.18), channel_id=1, source_target_pairs={{0,4},{4,0},{1,5},{5,1},{2,6},{6,2},{3,7},{7,3},{8,12},{12,8},{9,1... | collective-permute-start | bytes 3145736 | tf_op jit(solution)/shard_map/ppermute | solution.py:191
  442.8 44.7 %collective-permute-start.33 = (bf16[512,1024]{1,0:T(8,128)(2,1)S(1)}, bf16[512,1024]{1,0:T(8,128)(2,1)S(1)}, u32[]{:S(2)}, u32[]{:S(2)}) collective-permute-start(bf16[512,1024]{1,0:T(8,128)(2,1)S(1)} %get-tuple-element.98), channel_id=1, source_target_pairs={{0,2},{1,3},{2,0},{3,1},{4,6},{5,7},{6,4},{7,5},{8,10},{9,11},{10,... | collective-permute-start | bytes 3145736 | tf_op jit(solution)/shard_map/ppermute | solution.py:191
  443.8 43.7 %collective-permute-start.35 = (bf16[512,1024]{1,0:T(8,128)(2,1)S(1)}, bf16[512,1024]{1,0:T(8,128)(2,1)S(1)}, u32[]{:S(2)}, u32[]{:S(2)}) collective-permute-start(bf16[512,1024]{1,0:T(8,128)(2,1)S(1)} %fusion.100), channel_id=1, source_target_pairs={{0,4},{4,0},{1,5},{5,1},{2,6},{6,2},{3,7},{7,3},{8,12},{12,8},{9,1... | collective-permute-start | bytes 3145736 | tf_op jit(solution)/shard_map/ppermute | solution.py:191
  504.4 36.3 %collective-permute-start.37 = (bf16[512,1024]{1,0:T(8,128)(2,1)}, bf16[512,1024]{1,0:T(8,128)(2,1)}, u32[]{:S(2)}, u32[]{:S(2)}) collective-permute-start(bf16[512,1024]{1,0:T(8,128)(2,1)} %get-tuple-element.97), channel_id=1, source_target_pairs={{0,2},{1,3},{2,0},{3,1},{4,6},{5,7},{6,4},{7,5},{8,10},{9,11},{10,... | collective-permute-start | bytes 3145736 | tf_op jit(solution)/shard_map/ppermute | solution.py:191
  505.9 36.3 %collective-permute-start.39 = (bf16[512,1024]{1,0:T(8,128)(2,1)}, bf16[512,1024]{1,0:T(8,128)(2,1)}, u32[]{:S(2)}, u32[]{:S(2)}) collective-permute-start(bf16[512,1024]{1,0:T(8,128)(2,1)} %get-tuple-element.97), channel_id=1, source_target_pairs={{0,1},{1,0},{2,3},{3,2},{4,5},{5,4},{6,7},{7,6},{8,9},{9,8},{10,11... | collective-permute-start | bytes 3145736 | tf_op jit(solution)/shard_map/ppermute | solution.py:191
  505.9 47.3 %collective-permute-start.43 = (bf16[512,1024]{1,0:T(8,128)(2,1)}, bf16[512,1024]{1,0:T(8,128)(2,1)S(1)}, u32[]{:S(2)}, u32[]{:S(2)}) collective-permute-start(bf16[512,1024]{1,0:T(8,128)(2,1)} %get-tuple-element.96), channel_id=1, source_target_pairs={{0,2},{1,3},{2,0},{3,1},{4,6},{5,7},{6,4},{7,5},{8,10},{9,11},{10,... | collective-permute-start | bytes 3145736 | tf_op jit(solution)/shard_map/ppermute | solution.py:191
  527.9 46.0 %collective-permute-start.38 = (bf16[512,1024]{1,0:T(8,128)(2,1)}, bf16[512,1024]{1,0:T(8,128)(2,1)}, u32[]{:S(2)}, u32[]{:S(2)}) collective-permute-start(bf16[512,1024]{1,0:T(8,128)(2,1)} %collective-permute-done.36), channel_id=1, source_target_pairs={{0,2},{1,3},{2,0},{3,1},{4,6},{5,7},{6,4},{7,5},{8,10},{9,11},{10,... | collective-permute-start | bytes 3145736 | tf_op jit(solution)/shard_map/ppermute | solution.py:191
  531.1 546.5 %reduce-scatter.5.cloned.1.call-start = ((), (), s32[]{:S(2)}) async-start(), calls=%async_computation.5 | async-start | bytes 14090240 | tf_op jit(solution)/shard_map/reduce_scatter | solution.py:268
  538.4 40.2 %collective-permute-start.40 = (bf16[512,1024]{1,0:T(8,128)(2,1)}, bf16[512,1024]{1,0:T(8,128)(2,1)S(1)}, u32[]{:S(2)}, u32[]{:S(2)}) collective-permute-start(bf16[512,1024]{1,0:T(8,128)(2,1)} %collective-permute-done.36), channel_id=1, source_target_pairs={{0,1},{1,0},{2,3},{3,2},{4,5},{5,4},{6,7},{7,6},{8,9},{9,8},{10,11... | collective-permute-start | bytes 3145736 | tf_op jit(solution)/shard_map/ppermute | solution.py:191
  540.7 39.4 %collective-permute-start.44 = (bf16[512,1024]{1,0:T(8,128)(2,1)}, bf16[512,1024]{1,0:T(8,128)(2,1)S(1)}, u32[]{:S(2)}, u32[]{:S(2)}) collective-permute-start(bf16[512,1024]{1,0:T(8,128)(2,1)} %get-tuple-element.96), channel_id=1, source_target_pairs={{0,4},{4,0},{1,5},{5,1},{2,6},{6,2},{3,7},{7,3},{8,12},{12,8},{9,1... | collective-permute-start | bytes 3145736 | tf_op jit(solution)/shard_map/ppermute | solution.py:191
  542.2 38.0 %collective-permute-start.41 = (bf16[512,1024]{1,0:T(8,128)(2,1)}, bf16[512,1024]{1,0:T(8,128)(2,1)S(1)}, u32[]{:S(2)}, u32[]{:S(2)}) collective-permute-start(bf16[512,1024]{1,0:T(8,128)(2,1)} %collective-permute-done.37), channel_id=1, source_target_pairs={{0,1},{1,0},{2,3},{3,2},{4,5},{5,4},{6,7},{7,6},{8,9},{9,8},{10,11... | collective-permute-start | bytes 3145736 | tf_op jit(solution)/shard_map/ppermute | solution.py:191
  553.2 35.7 %collective-permute-start.45 = (bf16[512,1024]{1,0:T(8,128)(2,1)S(1)}, bf16[512,1024]{1,0:T(8,128)(2,1)S(1)}, u32[]{:S(2)}, u32[]{:S(2)}) collective-permute-start(bf16[512,1024]{1,0:T(8,128)(2,1)S(1)} %collective-permute-done.43), channel_id=1, source_target_pairs={{0,4},{4,0},{1,5},{5,1},{2,6},{6,2},{3,7},{7,3},{8,12},{12,8},{9,1... | collective-permute-start | bytes 3145736 | tf_op jit(solution)/shard_map/ppermute | solution.py:191
  793.2 755.5 %reduce-scatter.7.cloned.1.call-start = ((), (), s32[]{:S(2)}) async-start(), calls=%async_computation.6 | async-start | bytes 28180480 | tf_op jit(solution)/shard_map/reduce_scatter | solution.py:268
  1077.7 640.4 %reduce-scatter.9.cloned.1.call-start = ((), (), s32[]{:S(2)}) async-start(), calls=%async_computation.7 | async-start | bytes 15728640 | tf_op jit(solution)/shard_map/reduce_scatter | solution.py:268
  1102.4 35.8 %collective-permute-start.60 = (bf16[2048,1024]{1,0:T(8,128)(2,1)}, bf16[2048,1024]{1,0:T(8,128)(2,1)}, u32[]{:S(2)}, u32[]{:S(2)}) collective-permute-start(bf16[2048,1024]{1,0:T(8,128)(2,1)} %fusion.42), channel_id=1, source_target_pairs={{0,1},{1,0},{2,3},{3,2},{4,5},{5,4},{6,7},{7,6},{8,9},{9,8},{10,11... | collective-permute-start | bytes 12582920 | tf_op jit(solution)/shard_map/ppermute | solution.py:191
  1106.5 28.1 %collective-permute-start.56 = (bf16[512,1024]{1,0:T(8,128)(2,1)S(1)}, bf16[512,1024]{1,0:T(8,128)(2,1)}, u32[]{:S(2)}, u32[]{:S(2)}) collective-permute-start(bf16[512,1024]{1,0:T(8,128)(2,1)S(1)} %get-tuple-element.95), channel_id=1, source_target_pairs={{0,2},{1,3},{2,0},{3,1},{4,6},{5,7},{6,4},{7,5},{8,10},{9,11},{10,... | collective-permute-start | bytes 3145736 | tf_op jit(solution)/shard_map/ppermute | solution.py:191
  1124.6 37.0 %collective-permute-start.58 = (bf16[2048,1024]{1,0:T(8,128)(2,1)}, bf16[2048,1024]{1,0:T(8,128)(2,1)}, u32[]{:S(2)}, u32[]{:S(2)}) collective-permute-start(bf16[2048,1024]{1,0:T(8,128)(2,1)} %fusion.39), channel_id=1, source_target_pairs={{0,1},{1,0},{2,3},{3,2},{4,5},{5,4},{6,7},{7,6},{8,9},{9,8},{10,11... | collective-permute-start | bytes 12582920 | tf_op jit(solution)/shard_map/ppermute | solution.py:191
  1128.5 60.7 %collective-permute-start.51 = (bf16[512,1024]{1,0:T(8,128)(2,1)}, bf16[512,1024]{1,0:T(8,128)(2,1)}, u32[]{:S(2)}, u32[]{:S(2)}) collective-permute-start(bf16[512,1024]{1,0:T(8,128)(2,1)} %dynamic-slice_bitcast_fusion.14), channel_id=1, source_target_pairs={{0,4},{4,0},{1,5},{5,1},{2,6},{6,2},{3,7},{7,3},{8,12},{12,8},{9,1... | collective-permute-start | bytes 3145736 | tf_op jit(solution)/shard_map/ppermute | solution.py:191
  1130.9 72.7 %collective-permute-start.55 = (bf16[512,1024]{1,0:T(8,128)(2,1)S(1)}, bf16[512,1024]{1,0:T(8,128)(2,1)}, u32[]{:S(2)}, u32[]{:S(2)}) collective-permute-start(bf16[512,1024]{1,0:T(8,128)(2,1)S(1)} %get-tuple-element.94), channel_id=1, source_target_pairs={{0,2},{1,3},{2,0},{3,1},{4,6},{5,7},{6,4},{7,5},{8,10},{9,11},{10,... | collective-permute-start | bytes 3145736 | tf_op jit(solution)/shard_map/ppermute | solution.py:191
  1134.6 70.1 %collective-permute-start.54 = (bf16[512,1024]{1,0:T(8,128)(2,1)}, bf16[512,1024]{1,0:T(8,128)(2,1)}, u32[]{:S(2)}, u32[]{:S(2)}) collective-permute-start(bf16[512,1024]{1,0:T(8,128)(2,1)} %fusion.98), channel_id=1, source_target_pairs={{0,2},{1,3},{2,0},{3,1},{4,6},{5,7},{6,4},{7,5},{8,10},{9,11},{10,... | collective-permute-start | bytes 3145736 | tf_op jit(solution)/shard_map/ppermute | solution.py:191
  1161.6 39.1 %collective-permute-start.64 = (bf16[512,1024]{1,0:T(8,128)(2,1)}, bf16[512,1024]{1,0:T(8,128)(2,1)}, u32[]{:S(2)}, u32[]{:S(2)}) collective-permute-start(bf16[512,1024]{1,0:T(8,128)(2,1)} %get-tuple-element.93), channel_id=1, source_target_pairs={{0,2},{1,3},{2,0},{3,1},{4,6},{5,7},{6,4},{7,5},{8,10},{9,11},{10,... | collective-permute-start | bytes 3145736 | tf_op jit(solution)/shard_map/ppermute | solution.py:191
  1189.2 43.0 %collective-permute-start.59 = (bf16[512,1024]{1,0:T(8,128)(2,1)S(1)}, bf16[512,1024]{1,0:T(8,128)(2,1)}, u32[]{:S(2)}, u32[]{:S(2)}) collective-permute-start(bf16[512,1024]{1,0:T(8,128)(2,1)S(1)} %dynamic-slice_bitcast_fusion.10), channel_id=1, source_target_pairs={{0,4},{4,0},{1,5},{5,1},{2,6},{6,2},{3,7},{7,3},{8,12},{12,8},{9,1... | collective-permute-start | bytes 3145736 | tf_op jit(solution)/shard_map/ppermute | solution.py:191
  1200.7 31.5 %collective-permute-start.62 = (bf16[512,1024]{1,0:T(8,128)(2,1)S(1)}, bf16[512,1024]{1,0:T(8,128)(2,1)}, u32[]{:S(2)}, u32[]{:S(2)}) collective-permute-start(bf16[512,1024]{1,0:T(8,128)(2,1)S(1)} %fusion.94), channel_id=1, source_target_pairs={{0,2},{1,3},{2,0},{3,1},{4,6},{5,7},{6,4},{7,5},{8,10},{9,11},{10,... | collective-permute-start | bytes 3145736 | tf_op jit(solution)/shard_map/ppermute | solution.py:191
  1203.6 43.5 %collective-permute-start.63 = (bf16[512,1024]{1,0:T(8,128)(2,1)S(1)}, bf16[512,1024]{1,0:T(8,128)(2,1)S(1)}, u32[]{:S(2)}, u32[]{:S(2)}) collective-permute-start(bf16[512,1024]{1,0:T(8,128)(2,1)S(1)} %copy-done.32), channel_id=1, source_target_pairs={{0,2},{1,3},{2,0},{3,1},{4,6},{5,7},{6,4},{7,5},{8,10},{9,11},{10,... | collective-permute-start | bytes 3145736 | tf_op jit(solution)/shard_map/ppermute | solution.py:191
  1204.6 47.2 %collective-permute-start.65 = (bf16[512,1024]{1,0:T(8,128)(2,1)S(1)}, bf16[512,1024]{1,0:T(8,128)(2,1)}, u32[]{:S(2)}, u32[]{:S(2)}) collective-permute-start(bf16[512,1024]{1,0:T(8,128)(2,1)S(1)} %fusion.92), channel_id=1, source_target_pairs={{0,4},{4,0},{1,5},{5,1},{2,6},{6,2},{3,7},{7,3},{8,12},{12,8},{9,1... | collective-permute-start | bytes 3145736 | tf_op jit(solution)/shard_map/ppermute | solution.py:191
  1270.7 27.0 %collective-permute-start.67 = (bf16[512,1024]{1,0:T(8,128)(2,1)S(1)}, bf16[512,1024]{1,0:T(8,128)(2,1)S(1)}, u32[]{:S(2)}, u32[]{:S(2)}) collective-permute-start(bf16[512,1024]{1,0:T(8,128)(2,1)S(1)} %get-tuple-element.91), channel_id=1, source_target_pairs={{0,2},{1,3},{2,0},{3,1},{4,6},{5,7},{6,4},{7,5},{8,10},{9,11},{10,... | collective-permute-start | bytes 3145736 | tf_op jit(solution)/shard_map/ppermute | solution.py:191
  1272.2 27.0 %collective-permute-start.69 = (bf16[512,1024]{1,0:T(8,128)(2,1)S(1)}, bf16[512,1024]{1,0:T(8,128)(2,1)S(1)}, u32[]{:S(2)}, u32[]{:S(2)}) collective-permute-start(bf16[512,1024]{1,0:T(8,128)(2,1)S(1)} %get-tuple-element.91), channel_id=1, source_target_pairs={{0,1},{1,0},{2,3},{3,2},{4,5},{5,4},{6,7},{7,6},{8,9},{9,8},{10,11... | collective-permute-start | bytes 3145736 | tf_op jit(solution)/shard_map/ppermute | solution.py:191
  1272.2 47.1 %collective-permute-start.73 = (bf16[512,1024]{1,0:T(8,128)(2,1)S(1)}, bf16[512,1024]{1,0:T(8,128)(2,1)S(1)}, u32[]{:S(2)}, u32[]{:S(2)}) collective-permute-start(bf16[512,1024]{1,0:T(8,128)(2,1)S(1)} %get-tuple-element.90), channel_id=1, source_target_pairs={{0,2},{1,3},{2,0},{3,1},{4,6},{5,7},{6,4},{7,5},{8,10},{9,11},{10,... | collective-permute-start | bytes 3145736 | tf_op jit(solution)/shard_map/ppermute | solution.py:191
  1294.2 45.8 %collective-permute-start.68 = (bf16[512,1024]{1,0:T(8,128)(2,1)S(1)}, bf16[512,1024]{1,0:T(8,128)(2,1)S(1)}, u32[]{:S(2)}, u32[]{:S(2)}) collective-permute-start(bf16[512,1024]{1,0:T(8,128)(2,1)S(1)} %collective-permute-done.66), channel_id=1, source_target_pairs={{0,2},{1,3},{2,0},{3,1},{4,6},{5,7},{6,4},{7,5},{8,10},{9,11},{10,... | collective-permute-start | bytes 3145736 | tf_op jit(solution)/shard_map/ppermute | solution.py:191
  1297.5 42.7 %collective-permute-start.70 = (bf16[512,1024]{1,0:T(8,128)(2,1)S(1)}, bf16[512,1024]{1,0:T(8,128)(2,1)S(1)}, u32[]{:S(2)}, u32[]{:S(2)}) collective-permute-start(bf16[512,1024]{1,0:T(8,128)(2,1)S(1)} %collective-permute-done.66), channel_id=1, source_target_pairs={{0,1},{1,0},{2,3},{3,2},{4,5},{5,4},{6,7},{7,6},{8,9},{9,8},{10,11... | collective-permute-start | bytes 3145736 | tf_op jit(solution)/shard_map/ppermute | solution.py:191
  1297.7 43.2 %collective-permute-start.74 = (bf16[512,1024]{1,0:T(8,128)(2,1)S(1)}, bf16[512,1024]{1,0:T(8,128)(2,1)S(1)}, u32[]{:S(2)}, u32[]{:S(2)}) collective-permute-start(bf16[512,1024]{1,0:T(8,128)(2,1)S(1)} %get-tuple-element.90), channel_id=1, source_target_pairs={{0,4},{4,0},{1,5},{5,1},{2,6},{6,2},{3,7},{7,3},{8,12},{12,8},{9,1... | collective-permute-start | bytes 3145736 | tf_op jit(solution)/shard_map/ppermute | solution.py:191
  1299.2 41.7 %collective-permute-start.71 = (bf16[512,1024]{1,0:T(8,128)(2,1)S(1)}, bf16[512,1024]{1,0:T(8,128)(2,1)S(1)}, u32[]{:S(2)}, u32[]{:S(2)}) collective-permute-start(bf16[512,1024]{1,0:T(8,128)(2,1)S(1)} %collective-permute-done.67), channel_id=1, source_target_pairs={{0,1},{1,0},{2,3},{3,2},{4,5},{5,4},{6,7},{7,6},{8,9},{9,8},{10,11... | collective-permute-start | bytes 3145736 | tf_op jit(solution)/shard_map/ppermute | solution.py:191
  1442.5 307.0 %reduce-scatter.11.cloned.1.call-start = ((), (), s32[]{:S(2)}) async-start(), calls=%async_computation.8 | async-start | bytes 5242880 | tf_op jit(solution)/shard_map/reduce_scatter | solution.py:268
  1465.7 66.4 %collective-permute-start.82 = (bf16[2048,1024]{1,0:T(8,128)(2,1)}, bf16[2048,1024]{1,0:T(8,128)(2,1)}, u32[]{:S(2)}, u32[]{:S(2)}) collective-permute-start(bf16[2048,1024]{1,0:T(8,128)(2,1)} %convolution_convert_fusion.2), channel_id=1, source_target_pairs={{0,1},{1,0},{2,3},{3,2},{4,5},{5,4},{6,7},{7,6},{8,9},{9,8},{10,11... | collective-permute-start | bytes 12582920 | tf_op jit(solution)/shard_map/ppermute | solution.py:191
  1478.1 48.6 %collective-permute-start.94 = (bf16[4,512,512]{2,1,0:T(8,128)(2,1)S(1)}, bf16[4,512,512]{2,1,0:T(8,128)(2,1)}, u32[]{:S(2)}, u32[]{:S(2)}) collective-permute-start(bf16[4,512,512]{2,1,0:T(8,128)(2,1)S(1)} %constant_dynamic-slice_fusion), channel_id=1, source_target_pairs={{0,4},{4,0},{1,5},{5,1},{2,6},{6,2},{3,7},{7,3},{8,12},{12,8},{9,1... | collective-permute-start | bytes 6291464 | tf_op jit(solution)/shard_map/ppermute | solution.py:191
  1491.0 60.7 %collective-permute-start.80 = (bf16[2048,1024]{1,0:T(8,128)(2,1)}, bf16[2048,1024]{1,0:T(8,128)(2,1)}, u32[]{:S(2)}, u32[]{:S(2)}) collective-permute-start(bf16[2048,1024]{1,0:T(8,128)(2,1)} %convolution_convert_fusion.3), channel_id=1, source_target_pairs={{0,1},{1,0},{2,3},{3,2},{4,5},{5,4},{6,7},{7,6},{8,9},{9,8},{10,11... | collective-permute-start | bytes 12582920 | tf_op jit(solution)/shard_map/ppermute | solution.py:191
  1492.7 92.1 %collective-permute-start.92 = (bf16[1376,512]{1,0:T(8,128)(2,1)S(1)}, bf16[1376,512]{1,0:T(8,128)(2,1)}, u32[]{:S(2)}, u32[]{:S(2)}) collective-permute-start(bf16[1376,512]{1,0:T(8,128)(2,1)S(1)} %dynamic-slice_bitcast_fusion.2), channel_id=1, source_target_pairs={{0,4},{4,0},{1,5},{5,1},{2,6},{6,2},{3,7},{7,3},{8,12},{12,8},{9,1... | collective-permute-start | bytes 4227080 | tf_op jit(solution)/shard_map/ppermute | solution.py:191
  1544.7 34.7 %collective-permute-start.83 = (bf16[512,1024]{1,0:T(8,128)(2,1)}, bf16[512,1024]{1,0:T(8,128)(2,1)}, u32[]{:S(2)}, u32[]{:S(2)}) collective-permute-start(bf16[512,1024]{1,0:T(8,128)(2,1)} %dynamic-slice_bitcast_fusion.5), channel_id=1, source_target_pairs={{0,4},{4,0},{1,5},{5,1},{2,6},{6,2},{3,7},{7,3},{8,12},{12,8},{9,1... | collective-permute-start | bytes 3145736 | tf_op jit(solution)/shard_map/ppermute | solution.py:191
  1547.5 35.0 %collective-permute-start.86 = (bf16[512,1024]{1,0:T(8,128)(2,1)}, bf16[512,1024]{1,0:T(8,128)(2,1)}, u32[]{:S(2)}, u32[]{:S(2)}) collective-permute-start(bf16[512,1024]{1,0:T(8,128)(2,1)} %get-tuple-element.89), channel_id=1, source_target_pairs={{0,2},{1,3},{2,0},{3,1},{4,6},{5,7},{6,4},{7,5},{8,10},{9,11},{10,... | collective-permute-start | bytes 3145736 | tf_op jit(solution)/shard_map/ppermute | solution.py:191
  1550.7 134.7 %collective-permute-start.88 = (bf16[512,2752]{0,1:T(8,128)(2,1)S(1)}, bf16[512,2752]{0,1:T(8,128)(2,1)S(1)}, u32[]{:S(2)}, u32[]{:S(2)}) collective-permute-start(bf16[512,2752]{0,1:T(8,128)(2,1)S(1)} %dynamic-slice_bitcast_fusion.1), channel_id=1, source_target_pairs={{0,4},{4,0},{1,5},{5,1},{2,6},{6,2},{3,7},{7,3},{8,12},{12,8},{9,1... | collective-permute-start | bytes 8454152 | tf_op jit(solution)/shard_map/ppermute | solution.py:191
  1563.4 98.8 %collective-permute-start.81 = (bf16[512,1024]{1,0:T(8,128)(2,1)S(1)}, bf16[512,1024]{1,0:T(8,128)(2,1)S(1)}, u32[]{:S(2)}, u32[]{:S(2)}) collective-permute-start(bf16[512,1024]{1,0:T(8,128)(2,1)S(1)} %dynamic-slice_bitcast_fusion.6), channel_id=1, source_target_pairs={{0,4},{4,0},{1,5},{5,1},{2,6},{6,2},{3,7},{7,3},{8,12},{12,8},{9,1... | collective-permute-start | bytes 3145736 | tf_op jit(solution)/shard_map/ppermute | solution.py:191
  1581.0 81.1 %collective-permute-start.84 = (bf16[512,1024]{1,0:T(8,128)(2,1)S(1)}, bf16[512,1024]{1,0:T(8,128)(2,1)S(1)}, u32[]{:S(2)}, u32[]{:S(2)}) collective-permute-start(bf16[512,1024]{1,0:T(8,128)(2,1)S(1)} %fusion.90), channel_id=1, source_target_pairs={{0,2},{1,3},{2,0},{3,1},{4,6},{5,7},{6,4},{7,5},{8,10},{9,11},{10,... | collective-permute-start | bytes 3145736 | tf_op jit(solution)/shard_map/ppermute | solution.py:191
  1582.5 80.2 %collective-permute-start.85 = (bf16[512,1024]{1,0:T(8,128)(2,1)S(1)}, bf16[512,1024]{1,0:T(8,128)(2,1)S(1)}, u32[]{:S(2)}, u32[]{:S(2)}) collective-permute-start(bf16[512,1024]{1,0:T(8,128)(2,1)S(1)} %copy-done.33), channel_id=1, source_target_pairs={{0,2},{1,3},{2,0},{3,1},{4,6},{5,7},{6,4},{7,5},{8,10},{9,11},{10,... | collective-permute-start | bytes 3145736 | tf_op jit(solution)/shard_map/ppermute | solution.py:191
  1584.7 99.4 %collective-permute-start.87 = (bf16[512,1024]{1,0:T(8,128)(2,1)S(1)}, bf16[512,1024]{1,0:T(8,128)(2,1)S(1)}, u32[]{:S(2)}, u32[]{:S(2)}) collective-permute-start(bf16[512,1024]{1,0:T(8,128)(2,1)S(1)} %fusion.88), channel_id=1, source_target_pairs={{0,4},{4,0},{1,5},{5,1},{2,6},{6,2},{3,7},{7,3},{8,12},{12,8},{9,1... | collective-permute-start | bytes 3145736 | tf_op jit(solution)/shard_map/ppermute | solution.py:191
  1719.6 35.3 %collective-permute-start.93 = (bf16[512,1536]{1,0:T(8,128)(2,1)S(1)}, bf16[512,1536]{1,0:T(8,128)(2,1)}, u32[]{:S(2)}, u32[]{:S(2)}) collective-permute-start(bf16[512,1536]{1,0:T(8,128)(2,1)S(1)} %constant_dynamic-slice_fusion.1), channel_id=1, source_target_pairs={{0,4},{4,0},{1,5},{5,1},{2,6},{6,2},{3,7},{7,3},{8,12},{12,8},{9,1... | collective-permute-start | bytes 4718600 | tf_op jit(solution)/shard_map/ppermute | solution.py:191
  (103 other events, 1318.4 us)
Sparse Core Ops, SparseCore 0:
  16.2 289.4 all-gather.7
  307.8 380.7 all-gather.5
  690.7 195.1 all-gather.9
  888.7 188.8 reduce-scatter.4
  1079.9 373.3 reduce-scatter.6
  1455.4 213.5 reduce-scatter.8
  1671.3 78.1 reduce-scatter.10

commit v12 on v11

--- a/solution.py
+++ b/solution.py
@@ -393,7 +393,7 @@
     gu_grad = jnp.concatenate(
         [v.reshape(v.shape[0], 2, -1) for v in gu_halves], axis=2
     ).astype(F32)
-    done = (down_grad, gu_grad, grad_input, layer_output, gain_grads)
+    done = (down_grad, gu_grad)
     qkv_grad = []
     for part in qkv_sum:
         first, second = trade_ctx(after(part, done), 0)
@@ -403,6 +403,7 @@
             qkv_grad.append(jnp.concatenate(both, axis=1).astype(F32))
         done = done + (qkv_grad[-1],)
     qkv_grad = jnp.stack(qkv_grad, axis=1)
+    done = (down_grad, gu_grad, grad_input, layer_output, gain_grads, qkv_grad)
     out_weight_grad = after(out_sum, done).astype(F32)
 
     return (

time: 1770 us -> 1770 us (level)
    reduce_scatter x4, waiting for transfers between devices: 89.5 us -> 60.6 us  [owners(): return lax.psum_scatter(grad, 'fsdp', scatter_dimension=0, tiled=False)]
    ppermute x95, waiting for transfers between devices: 508 us -> 533 us  [swap(): lax.ppermute(values, axis, [(i, i ^ step) for i in range(lax.axis_size(ax...]
  transfers between devices with their start and end apart: 102 -> 102, of which waited for: 42 -> 41; matrix products, arithmetic and copies ran while one was open for 38% -> 38% of each run, Pallas kernels for 4% -> 4%
where the time goes in v12:
time: 1770 us
  waiting for transfers between devices  869 us (49%)
  matrix products  452 us (26%)
  local copies, waits for them, and re-layouts  133 us (8%)
  other arithmetic  119 us (7%)
  Pallas kernels  79 us (4%)
  starting transfers between devices  71.4 us (4%)
  blocking collectives  26.9 us (2%)
    ppermute x95, waiting for transfers between devices, swap(): lax.ppermute(values, axis, [(i, i ^ step) for i in range(lax.axis_size(ax...  533 us
    dot_general x32, matrix products, mm(): return lax.dot_general(left, right, dims, preferred_element_type=F32)  452 us
    all_gather x3, waiting for transfers between devices, spread(): return lax.all_gather(weight, 'fsdp', axis=0, tiled=False)  276 us
    ppermute x95, starting transfers between devices, swap(): lax.ppermute(values, axis, [(i, i ^ step) for i in range(lax.axis_size(ax...  71.1 us
    reduce_scatter x4, waiting for transfers between devices, owners(): return lax.psum_scatter(grad, 'fsdp', scatter_dimension=0, tiled=False)  60.6 us
    dynamic_update_slice x64, local copies, waits for them, and re-layouts, gather_rows(): full = lax.dynamic_update_slice(full, piece[None], start)  47.3 us
    pallas_call x1, Pallas kernels, attend_backward(): pl.pallas_call(kernel, grid=(heads, blocks), in_specs=[row, col, col, row...  44 us
  transfers between devices with their start and end apart: 102, of which 41 were waited for; matrix products, arithmetic and copies ran while one was open for 38% of the time, Pallas kernels for 4%

profile of v12, /device:TPU:0, one launch (start us, length us, event | category | flops | bytes accessed | tf_op | source)
XLA Modules:
  0.0 1766.7 jit_solution(2264541318756378860)
XLA Ops:
  23.9 8.8 psum.28
  40.2 20.4 %collective-permute-done = bf16[512,1024]{1,0:T(8,128)(2,1)} collective-permute-done((bf16[512,1024]{1,0:T(8,128)(2,1)}, bf16[512,1024]{1,0:T(8,128)(2,1)}, u32[]{:S(2)}, u32[]{:S(2)}) %collective-permute-start) | collective-permute-done | bytes 1048608 | tf_op jit(solution)/shard_map/ppermute | solution.py:191
  67.7 19.3 %collective-permute-done.7 = bf16[512,1024]{1,0:T(8,128)(2,1)S(1)} collective-permute-done((bf16[512,1024]{1,0:T(8,128)(2,1)}, bf16[512,1024]{1,0:T(8,128)(2,1)S(1)}, u32[]{:S(2)}, u32[]{:S(2)}) %collective-permute-start.7) | collective-permute-done | bytes 1048608 | tf_op jit(solution)/shard_map/ppermute | solution.py:191
  88.8 18.0 %collective-permute-done.2 = bf16[512,1024]{1,0:T(8,128)(2,1)} collective-permute-done((bf16[512,1024]{1,0:T(8,128)(2,1)}, bf16[512,1024]{1,0:T(8,128)(2,1)}, u32[]{:S(2)}, u32[]{:S(2)}) %collective-permute-start.2) | collective-permute-done | bytes 1048608 | tf_op jit(solution)/shard_map/ppermute | solution.py:191
  124.7 18.0 %collective-permute-done.14 = bf16[512,1024]{1,0:T(8,128)(2,1)S(1)} collective-permute-done((bf16[512,1024]{1,0:T(8,128)(2,1)S(1)}, bf16[512,1024]{1,0:T(8,128)(2,1)S(1)}, u32[]{:S(2)}, u32[]{:S(2)}) %collective-permute-start.14) | collective-permute-done | bytes 1048608 | tf_op jit(solution)/shard_map/ppermute | solution.py:191
  144.9 6.1 broadcast.35.clone.1
  153.9 13.4 collective-permute-done.21
  168.9 19.8 %collective-permute-done.16 = bf16[512,1024]{1,0:T(8,128)(2,1)S(1)} collective-permute-done((bf16[512,1024]{1,0:T(8,128)(2,1)S(1)}, bf16[512,1024]{1,0:T(8,128)(2,1)S(1)}, u32[]{:S(2)}, u32[]{:S(2)}) %collective-permute-start.16) | collective-permute-done | bytes 1048608 | tf_op jit(solution)/shard_map/ppermute | solution.py:191
  192.8 8.4 collective-permute-done.23
  211.8 93.9 %all-gather.8.cloned.1.call-done = bf16[16,1024,512]{2,1,0:T(8,128)(2,1)} async-done(((bf16[4,1024,512]{2,1,0:T(8,128)(2,1)}), bf16[16,1024,512]{2,1,0:T(8,128)(2,1)}) %all-gather.8.cloned.1.call-update) | async-done | bytes 16777232 | tf_op jit(solution)/shard_map/all_gather | solution.py:272
  305.7 15.2 convolution_bitcast_fusion.1.v_in
  320.9 16.1 convolution_bitcast_fusion.2.k_in
  337.0 12.4 convolution_bitcast_fusion.3.q_in
  349.4 35.1 %shard_map.143 = (bf16[2048,512]{1,0:T(8,128)(2,1)S(1)}, bf16[2048,512]{1,0:T(8,128)(2,1)}, bf16[2048,512]{1,0:T(8,128)(2,1)}, bf16[2048,512]{1,0:T(8,128)(2,1)}, f32[4,1,2048]{2,1,0:T(1,128)S(1)}) custom-call(f32[2048,512]{1,0:T(8,128)} %convolution_bitcast_fusion.3.q_in, f32[2048,512]{1,0:T(8,128)} %convolution_bitcast_fusion.2.k_in, ...), custom_call_target="tpu_custom_call" | custom-call | flops 5368709120 | bytes 20971520 | tf_op jit(solution)/shard_map/pallas_call | solution.py:88
  384.5 12.3 slice_bitcast_fusion.18
  424.2 16.7 collective-permute-done.31
  445.3 18.1 %collective-permute-done.29 = bf16[512,1024]{1,0:T(8,128)(2,1)S(1)} collective-permute-done((bf16[512,1024]{1,0:T(8,128)(2,1)S(1)}, bf16[512,1024]{1,0:T(8,128)(2,1)S(1)}, u32[]{:S(2)}, u32[]{:S(2)}) %collective-permute-start.29) | collective-permute-done | bytes 1048608 | tf_op jit(solution)/shard_map/ppermute | solution.py:191
  468.0 19.5 %collective-permute-done.33 = bf16[512,1024]{1,0:T(8,128)(2,1)S(1)} collective-permute-done((bf16[512,1024]{1,0:T(8,128)(2,1)S(1)}, bf16[512,1024]{1,0:T(8,128)(2,1)S(1)}, u32[]{:S(2)}, u32[]{:S(2)}) %collective-permute-start.33) | collective-permute-done | bytes 1048608 | tf_op jit(solution)/shard_map/ppermute | solution.py:191
  506.5 21.4 %collective-permute-done.36 = bf16[512,1024]{1,0:T(8,128)(2,1)} collective-permute-done((bf16[512,1024]{1,0:T(8,128)(2,1)}, bf16[512,1024]{1,0:T(8,128)(2,1)}, u32[]{:S(2)}, u32[]{:S(2)}) %collective-permute-start.36) | collective-permute-done | bytes 1048608 | tf_op jit(solution)/shard_map/ppermute | solution.py:191
  531.2 6.1 broadcast.35.clone.2
  542.4 10.8 collective-permute-done.43
  556.1 17.8 %collective-permute-done.38 = bf16[512,1024]{1,0:T(8,128)(2,1)} collective-permute-done((bf16[512,1024]{1,0:T(8,128)(2,1)}, bf16[512,1024]{1,0:T(8,128)(2,1)}, u32[]{:S(2)}, u32[]{:S(2)}) %collective-permute-start.38) | collective-permute-done | bytes 1048608 | tf_op jit(solution)/shard_map/ppermute | solution.py:191
  580.7 8.3 collective-permute-done.45
  599.7 88.9 %all-gather.6.cloned.1.call-done = bf16[4,1024,2752]{1,2,0:T(8,128)(2,1)} async-done(((bf16[1,1024,2752]{1,2,0:T(8,128)(2,1)}), bf16[4,1024,2752]{1,2,0:T(8,128)(2,1)}) %all-gather.6.cloned.1.call-update) | async-done | bytes 22544400 | tf_op jit(solution)/shard_map/all_gather | solution.py:272
  688.6 56.9 %convolution_bitcast_fusion = f32[2048,2752]{0,1:T(8,128)} fusion(bf16[4,2048,1024]{2,1,0:T(8,128)(2,1)} %bitcast_dynamic-update-slice_fusion.16, bf16[4,1024,2752]{1,2,0:T(8,128)(2,1)} %all-gather.6.cloned.1.call-done), kind=kOutput, calls=%fused_computation.2 | convolution fusion | flops 46170898432 | bytes 61865984 | tf_op jit(solution)/shard_map/dot_general | solution.py:21
  745.5 9.0 multiply_convert_fusion
  754.5 9.7 fusion.57
  764.2 7.9 fusion.56
  772.1 7.9 fusion.55
  780.0 7.9 fusion.54
  793.2 92.7 %all-gather.10.cloned.1.call-done = bf16[5504,1024]{1,0:T(8,128)(2,1)} async-done(((bf16[1376,1024]{1,0:T(8,128)(2,1)}), bf16[5504,1024]{1,0:T(8,128)(2,1)}) %all-gather.10.cloned.1.call-update) | async-done | bytes 11272208 | tf_op jit(solution)/shard_map/all_gather | solution.py:272
  885.9 37.5 %fusion.3 = (bf16[2048,1376]{0,1:T(8,128)(2,1)S(1)}, bf16[2048,1376]{0,1:T(8,128)(2,1)}) fusion(f32[2048,2752]{0,1:T(8,128)} %convolution_bitcast_fusion, bf16[4,2048,1024]{2,1,0:T(8,128)(2,1)} %bitcast_dynamic-update-slice_fusion.32, bf16[4,1376,1024]{2,1,0:T(8,128)(2,1)} %bitcast.522), kind=kOutput, calls=%fused_computation.11 | convolution fusion | flops 23122083840 | bytes 61865984 | tf_op jit(solution)/shard_map/dot_general | solution.py:21
  925.9 54.8 %convolution_convert_fusion = bf16[4,1024,2752]{1,2,0:T(8,128)(2,1)} fusion(bf16[4,2048,1024]{2,1,0:T(8,128)(2,1)} %bitcast_dynamic-update-slice_fusion.16, bf16[2048,1376]{0,1:T(8,128)(2,1)} %get-tuple-element.59, bf16[2048,1376]{0,1:T(8,128)(2,1)S(1)} %get-tuple-element.58), kind=kOutput, calls=%fused_computation | convolution fusion | flops 46204715008 | bytes 50593792 | tf_op jit(solution)/shard_map/dot_general | solution.py:21
  980.7 9.8 convolution_convert_fusion.5
  990.6 8.7 convolution_convert_fusion.4
  999.8 8.6 add_convert_fusion.5
  1008.5 8.6 add_convert_fusion.4
  1017.0 60.6 %reduce-scatter.5.cloned.1.call-done = bf16[1,1376,1024]{2,1,0:T(8,128)(2,1)} async-done(((bf16[4,1376,1024]{2,1,0:T(8,128)(2,1)}), bf16[1,1376,1024]{2,1,0:T(8,128)(2,1)}) %reduce-scatter.5.cloned.1.call-update) | async-done | bytes 2818064 | tf_op jit(solution)/shard_map/reduce_scatter | solution.py:268
  1077.7 7.9 pad_maximum_fusion.2
  1085.6 16.8 fusion.42
  1108.0 16.6 fusion.39
  1138.2 17.0 add_convert_fusion.2
  1163.2 17.2 add_convert_fusion.3
  1190.2 10.5 collective-permute-done.64
  1213.4 18.7 %collective-permute-done.59 = bf16[512,1024]{1,0:T(8,128)(2,1)} collective-permute-done((bf16[512,1024]{1,0:T(8,128)(2,1)S(1)}, bf16[512,1024]{1,0:T(8,128)(2,1)}, u32[]{:S(2)}, u32[]{:S(2)}) %collective-permute-start.59) | collective-permute-done | bytes 1048608 | tf_op jit(solution)/shard_map/ppermute | solution.py:191
  1234.3 12.8 collective-permute-done.63
  1262.5 6.9 fusion.146
  1272.8 21.4 %collective-permute-done.66 = bf16[512,1024]{1,0:T(8,128)(2,1)S(1)} collective-permute-done((bf16[512,1024]{1,0:T(8,128)(2,1)S(1)}, bf16[512,1024]{1,0:T(8,128)(2,1)S(1)}, u32[]{:S(2)}, u32[]{:S(2)}) %collective-permute-start.66) | collective-permute-done | bytes 1048608 | tf_op jit(solution)/shard_map/ppermute | solution.py:191
  1299.4 19.9 %collective-permute-done.73 = bf16[512,1024]{1,0:T(8,128)(2,1)S(1)} collective-permute-done((bf16[512,1024]{1,0:T(8,128)(2,1)S(1)}, bf16[512,1024]{1,0:T(8,128)(2,1)S(1)}, u32[]{:S(2)}, u32[]{:S(2)}) %collective-permute-start.73) | collective-permute-done | bytes 1048608 | tf_op jit(solution)/shard_map/ppermute | solution.py:191
  1320.3 19.6 %collective-permute-done.68 = bf16[512,1024]{1,0:T(8,128)(2,1)S(1)} collective-permute-done((bf16[512,1024]{1,0:T(8,128)(2,1)S(1)}, bf16[512,1024]{1,0:T(8,128)(2,1)S(1)}, u32[]{:S(2)}, u32[]{:S(2)}) %collective-permute-start.68) | collective-permute-done | bytes 1048608 | tf_op jit(solution)/shard_map/ppermute | solution.py:191
  1348.7 13.7 bitcast_convert_fusion.g
  1362.4 44.0 %shard_map.144 = (bf16[2048,512]{1,0:T(8,128)(2,1)S(1)}, bf16[2048,512]{1,0:T(8,128)(2,1)}, bf16[2048,512]{1,0:T(8,128)(2,1)}) custom-call(bf16[2048,512]{1,0:T(8,128)(2,1)} %copy-done.2, bf16[2048,512]{1,0:T(8,128)(2,1)} %get-tuple-element.39.k, bf16[2048,512]{1,0:T(8,128)(2,1)} %get-tuple-element.40.v, bf16[2048,512]{1,0:T(8,128)(2,1)} %get-tuple-element.48.o, ...), custom_call_target="tpu_custom_call" | custom-call | flops 13421772800 | bytes 16777216 | tf_op jit(solution)/shard_map/pallas_call | solution.py:164
  1411.5 31.1 %convolution_convert_fusion.1 = bf16[4,1024,1536]{2,1,0:T(8,128)(2,1)} fusion(bf16[4,2048,1024]{2,1,0:T(8,128)(2,1)} %copy-done.14, bf16[2048,1536]{1,0:T(8,128)(2,1)S(1)} %constant_dynamic-update-slice_fusion), kind=kOutput, calls=%fused_computation.1 | convolution fusion | flops 25776095232 | bytes 35651584 | tf_op jit(solution)/shard_map/dot_general | solution.py:21
  1442.6 7.4 pad_maximum_fusion
  1450.1 15.7 convolution_convert_fusion.2
  1479.5 11.5 convolution_convert_fusion.3
  1493.4 33.4 %collective-permute-done.94 = bf16[4,512,512]{2,1,0:T(8,128)(2,1)} collective-permute-done((bf16[4,512,512]{2,1,0:T(8,128)(2,1)S(1)}, bf16[4,512,512]{2,1,0:T(8,128)(2,1)}, u32[]{:S(2)}, u32[]{:S(2)}) %collective-permute-start.94) | collective-permute-done | bytes 2097184 | tf_op jit(solution)/shard_map/ppermute | solution.py:191
  1532.2 10.9 add_convert_fusion
  1548.6 10.8 add_convert_fusion.1
  1564.4 14.9 collective-permute-done.83
  1591.5 70.7 %collective-permute-done.81 = bf16[512,1024]{1,0:T(8,128)(2,1)S(1)} collective-permute-done((bf16[512,1024]{1,0:T(8,128)(2,1)S(1)}, bf16[512,1024]{1,0:T(8,128)(2,1)S(1)}, u32[]{:S(2)}, u32[]{:S(2)}) %collective-permute-start.81) | collective-permute-done | bytes 1048608 | tf_op jit(solution)/shard_map/ppermute | solution.py:191
  1662.7 21.4 %collective-permute-done.87 = bf16[512,1024]{1,0:T(8,128)(2,1)S(1)} collective-permute-done((bf16[512,1024]{1,0:T(8,128)(2,1)S(1)}, bf16[512,1024]{1,0:T(8,128)(2,1)S(1)}, u32[]{:S(2)}, u32[]{:S(2)}) %collective-permute-start.87) | collective-permute-done | bytes 1048608 | tf_op jit(solution)/shard_map/ppermute | solution.py:191
  1703.6 30.8 %collective-permute-done.89 = f32[2,1024]{1,0:T(2,128)S(1)} collective-permute-done((f32[2,1024]{1,0:T(2,128)S(1)}, f32[2,1024]{1,0:T(2,128)S(1)}, u32[]{:S(2)}, u32[]{:S(2)}) %collective-permute-start.89) | collective-permute-done | bytes 8224 | tf_op jit(solution)/shard_map/ppermute | solution.py:191
  1735.9 6.0 psum.31
  (485 shorter events, 338.0 us)
Async XLA Ops:
  7.2 298.5 %all-gather.8.cloned.1.call-start = ((), (), s32[]{:S(2)}) async-start(), calls=%async_computation.9 | async-start | bytes 20971520 | tf_op jit(solution)/shard_map/all_gather | solution.py:272
  16.1 672.5 %all-gather.6.cloned.1.call-start = ((), (), s32[]{:S(2)}) async-start(), calls=%async_computation.4 | async-start | bytes 28180480 | tf_op jit(solution)/shard_map/all_gather | solution.py:272
  21.9 864.1 %all-gather.10.cloned.1.call-start = ((), (), s32[]{:S(2)}) async-start(), calls=%async_computation.10 | async-start | bytes 14090240 | tf_op jit(solution)/shard_map/all_gather | solution.py:272
  38.2 27.7 %collective-permute-start.1 = (bf16[512,1024]{1,0:T(8,128)(2,1)}, bf16[512,1024]{1,0:T(8,128)(2,1)}, u32[]{:S(2)}, u32[]{:S(2)}) collective-permute-start(bf16[512,1024]{1,0:T(8,128)(2,1)} %get-tuple-element.103), channel_id=1, source_target_pairs={{0,2},{1,3},{2,0},{3,1},{4,6},{5,7},{6,4},{7,5},{8,10},{9,11},{10,... | collective-permute-start | bytes 3145736 | tf_op jit(solution)/shard_map/ppermute | solution.py:191
  38.7 28.8 %collective-permute-start.3 = (bf16[512,1024]{1,0:T(8,128)(2,1)}, bf16[512,1024]{1,0:T(8,128)(2,1)}, u32[]{:S(2)}, u32[]{:S(2)}) collective-permute-start(bf16[512,1024]{1,0:T(8,128)(2,1)} %get-tuple-element.103), channel_id=1, source_target_pairs={{0,1},{1,0},{2,3},{3,2},{4,5},{5,4},{6,7},{7,6},{8,9},{9,8},{10,11... | collective-permute-start | bytes 3145736 | tf_op jit(solution)/shard_map/ppermute | solution.py:191
  38.7 48.3 %collective-permute-start.7 = (bf16[512,1024]{1,0:T(8,128)(2,1)}, bf16[512,1024]{1,0:T(8,128)(2,1)S(1)}, u32[]{:S(2)}, u32[]{:S(2)}) collective-permute-start(bf16[512,1024]{1,0:T(8,128)(2,1)} %get-tuple-element.102), channel_id=1, source_target_pairs={{0,2},{1,3},{2,0},{3,1},{4,6},{5,7},{6,4},{7,5},{8,10},{9,11},{10,... | collective-permute-start | bytes 3145736 | tf_op jit(solution)/shard_map/ppermute | solution.py:191
  60.6 46.3 %collective-permute-start.2 = (bf16[512,1024]{1,0:T(8,128)(2,1)}, bf16[512,1024]{1,0:T(8,128)(2,1)}, u32[]{:S(2)}, u32[]{:S(2)}) collective-permute-start(bf16[512,1024]{1,0:T(8,128)(2,1)} %collective-permute-done), channel_id=1, source_target_pairs={{0,2},{1,3},{2,0},{3,1},{4,6},{5,7},{6,4},{7,5},{8,10},{9,11},{10,... | collective-permute-start | bytes 3145736 | tf_op jit(solution)/shard_map/ppermute | solution.py:191
  64.5 45.0 %collective-permute-start.4 = (bf16[512,1024]{1,0:T(8,128)(2,1)}, bf16[512,1024]{1,0:T(8,128)(2,1)S(1)}, u32[]{:S(2)}, u32[]{:S(2)}) collective-permute-start(bf16[512,1024]{1,0:T(8,128)(2,1)} %collective-permute-done), channel_id=1, source_target_pairs={{0,1},{1,0},{2,3},{3,2},{4,5},{5,4},{6,7},{7,6},{8,9},{9,8},{10,11... | collective-permute-start | bytes 3145736 | tf_op jit(solution)/shard_map/ppermute | solution.py:191
  65.9 44.3 %collective-permute-start.8 = (bf16[512,1024]{1,0:T(8,128)(2,1)}, bf16[512,1024]{1,0:T(8,128)(2,1)S(1)}, u32[]{:S(2)}, u32[]{:S(2)}) collective-permute-start(bf16[512,1024]{1,0:T(8,128)(2,1)} %get-tuple-element.102), channel_id=1, source_target_pairs={{0,4},{4,0},{1,5},{5,1},{2,6},{6,2},{3,7},{7,3},{8,12},{12,8},{9,1... | collective-permute-start | bytes 3145736 | tf_op jit(solution)/shard_map/ppermute | solution.py:191
  67.5 42.8 %collective-permute-start.5 = (bf16[512,1024]{1,0:T(8,128)(2,1)}, bf16[512,1024]{1,0:T(8,128)(2,1)S(1)}, u32[]{:S(2)}, u32[]{:S(2)}) collective-permute-start(bf16[512,1024]{1,0:T(8,128)(2,1)} %collective-permute-done.1), channel_id=1, source_target_pairs={{0,1},{1,0},{2,3},{3,2},{4,5},{5,4},{6,7},{7,6},{8,9},{9,8},{10,11... | collective-permute-start | bytes 3145736 | tf_op jit(solution)/shard_map/ppermute | solution.py:191
  87.0 27.2 %collective-permute-start.9 = (bf16[512,1024]{1,0:T(8,128)(2,1)S(1)}, bf16[512,1024]{1,0:T(8,128)(2,1)S(1)}, u32[]{:S(2)}, u32[]{:S(2)}) collective-permute-start(bf16[512,1024]{1,0:T(8,128)(2,1)S(1)} %collective-permute-done.7), channel_id=1, source_target_pairs={{0,4},{4,0},{1,5},{5,1},{2,6},{6,2},{3,7},{7,3},{8,12},{12,8},{9,1... | collective-permute-start | bytes 3145736 | tf_op jit(solution)/shard_map/ppermute | solution.py:191
  118.8 34.4 %collective-permute-start.15 = (bf16[512,1024]{1,0:T(8,128)(2,1)S(1)}, bf16[512,1024]{1,0:T(8,128)(2,1)S(1)}, u32[]{:S(2)}, u32[]{:S(2)}) collective-permute-start(bf16[512,1024]{1,0:T(8,128)(2,1)S(1)} %get-tuple-element.101), channel_id=1, source_target_pairs={{0,2},{1,3},{2,0},{3,1},{4,6},{5,7},{6,4},{7,5},{8,10},{9,11},{10,... | collective-permute-start | bytes 3145736 | tf_op jit(solution)/shard_map/ppermute | solution.py:191
  119.4 34.3 %collective-permute-start.17 = (bf16[512,1024]{1,0:T(8,128)(2,1)S(1)}, bf16[512,1024]{1,0:T(8,128)(2,1)S(1)}, u32[]{:S(2)}, u32[]{:S(2)}) collective-permute-start(bf16[512,1024]{1,0:T(8,128)(2,1)S(1)} %get-tuple-element.101), channel_id=1, source_target_pairs={{0,1},{1,0},{2,3},{3,2},{4,5},{5,4},{6,7},{7,6},{8,9},{9,8},{10,11... | collective-permute-start | bytes 3145736 | tf_op jit(solution)/shard_map/ppermute | solution.py:191
  119.4 47.9 %collective-permute-start.21 = (bf16[512,1024]{1,0:T(8,128)(2,1)S(1)}, bf16[512,1024]{1,0:T(8,128)(2,1)S(1)}, u32[]{:S(2)}, u32[]{:S(2)}) collective-permute-start(bf16[512,1024]{1,0:T(8,128)(2,1)S(1)} %get-tuple-element.100), channel_id=1, source_target_pairs={{0,2},{1,3},{2,0},{3,1},{4,6},{5,7},{6,4},{7,5},{8,10},{9,11},{10,... | collective-permute-start | bytes 3145736 | tf_op jit(solution)/shard_map/ppermute | solution.py:191
  142.7 45.9 %collective-permute-start.16 = (bf16[512,1024]{1,0:T(8,128)(2,1)S(1)}, bf16[512,1024]{1,0:T(8,128)(2,1)S(1)}, u32[]{:S(2)}, u32[]{:S(2)}) collective-permute-start(bf16[512,1024]{1,0:T(8,128)(2,1)S(1)} %collective-permute-done.14), channel_id=1, source_target_pairs={{0,2},{1,3},{2,0},{3,1},{4,6},{5,7},{6,4},{7,5},{8,10},{9,11},{10,... | collective-permute-start | bytes 3145736 | tf_op jit(solution)/shard_map/ppermute | solution.py:191
  152.1 38.7 %collective-permute-start.18 = (bf16[512,1024]{1,0:T(8,128)(2,1)S(1)}, bf16[512,1024]{1,0:T(8,128)(2,1)S(1)}, u32[]{:S(2)}, u32[]{:S(2)}) collective-permute-start(bf16[512,1024]{1,0:T(8,128)(2,1)S(1)} %collective-permute-done.14), channel_id=1, source_target_pairs={{0,1},{1,0},{2,3},{3,2},{4,5},{5,4},{6,7},{7,6},{8,9},{9,8},{10,11... | collective-permute-start | bytes 3145736 | tf_op jit(solution)/shard_map/ppermute | solution.py:191
  153.1 39.2 %collective-permute-start.22 = (bf16[512,1024]{1,0:T(8,128)(2,1)S(1)}, bf16[512,1024]{1,0:T(8,128)(2,1)S(1)}, u32[]{:S(2)}, u32[]{:S(2)}) collective-permute-start(bf16[512,1024]{1,0:T(8,128)(2,1)S(1)} %get-tuple-element.100), channel_id=1, source_target_pairs={{0,4},{4,0},{1,5},{5,1},{2,6},{6,2},{3,7},{7,3},{8,12},{12,8},{9,1... | collective-permute-start | bytes 3145736 | tf_op jit(solution)/shard_map/ppermute | solution.py:191
  153.7 38.6 %collective-permute-start.19 = (bf16[512,1024]{1,0:T(8,128)(2,1)S(1)}, bf16[512,1024]{1,0:T(8,128)(2,1)S(1)}, u32[]{:S(2)}, u32[]{:S(2)}) collective-permute-start(bf16[512,1024]{1,0:T(8,128)(2,1)S(1)} %collective-permute-done.15), channel_id=1, source_target_pairs={{0,1},{1,0},{2,3},{3,2},{4,5},{5,4},{6,7},{7,6},{8,9},{9,8},{10,11... | collective-permute-start | bytes 3145736 | tf_op jit(solution)/shard_map/ppermute | solution.py:191
  167.3 33.9 %collective-permute-start.23 = (bf16[512,1024]{1,0:T(8,128)(2,1)S(1)}, bf16[512,1024]{1,0:T(8,128)(2,1)S(1)}, u32[]{:S(2)}, u32[]{:S(2)}) collective-permute-start(bf16[512,1024]{1,0:T(8,128)(2,1)S(1)} %collective-permute-done.21), channel_id=1, source_target_pairs={{0,4},{4,0},{1,5},{5,1},{2,6},{6,2},{3,7},{7,3},{8,12},{12,8},{9,1... | collective-permute-start | bytes 3145736 | tf_op jit(solution)/shard_map/ppermute | solution.py:191
  423.6 39.7 %collective-permute-start.29 = (bf16[512,1024]{1,0:T(8,128)(2,1)S(1)}, bf16[512,1024]{1,0:T(8,128)(2,1)S(1)}, u32[]{:S(2)}, u32[]{:S(2)}) collective-permute-start(bf16[512,1024]{1,0:T(8,128)(2,1)S(1)} %dynamic-slice_bitcast_fusion.18), channel_id=1, source_target_pairs={{0,4},{4,0},{1,5},{5,1},{2,6},{6,2},{3,7},{7,3},{8,12},{12,8},{9,1... | collective-permute-start | bytes 3145736 | tf_op jit(solution)/shard_map/ppermute | solution.py:191
  442.8 44.7 %collective-permute-start.33 = (bf16[512,1024]{1,0:T(8,128)(2,1)S(1)}, bf16[512,1024]{1,0:T(8,128)(2,1)S(1)}, u32[]{:S(2)}, u32[]{:S(2)}) collective-permute-start(bf16[512,1024]{1,0:T(8,128)(2,1)S(1)} %get-tuple-element.98), channel_id=1, source_target_pairs={{0,2},{1,3},{2,0},{3,1},{4,6},{5,7},{6,4},{7,5},{8,10},{9,11},{10,... | collective-permute-start | bytes 3145736 | tf_op jit(solution)/shard_map/ppermute | solution.py:191
  443.8 43.7 %collective-permute-start.35 = (bf16[512,1024]{1,0:T(8,128)(2,1)S(1)}, bf16[512,1024]{1,0:T(8,128)(2,1)S(1)}, u32[]{:S(2)}, u32[]{:S(2)}) collective-permute-start(bf16[512,1024]{1,0:T(8,128)(2,1)S(1)} %fusion.100), channel_id=1, source_target_pairs={{0,4},{4,0},{1,5},{5,1},{2,6},{6,2},{3,7},{7,3},{8,12},{12,8},{9,1... | collective-permute-start | bytes 3145736 | tf_op jit(solution)/shard_map/ppermute | solution.py:191
  504.4 36.3 %collective-permute-start.37 = (bf16[512,1024]{1,0:T(8,128)(2,1)}, bf16[512,1024]{1,0:T(8,128)(2,1)}, u32[]{:S(2)}, u32[]{:S(2)}) collective-permute-start(bf16[512,1024]{1,0:T(8,128)(2,1)} %get-tuple-element.97), channel_id=1, source_target_pairs={{0,2},{1,3},{2,0},{3,1},{4,6},{5,7},{6,4},{7,5},{8,10},{9,11},{10,... | collective-permute-start | bytes 3145736 | tf_op jit(solution)/shard_map/ppermute | solution.py:191
  505.9 36.2 %collective-permute-start.39 = (bf16[512,1024]{1,0:T(8,128)(2,1)}, bf16[512,1024]{1,0:T(8,128)(2,1)}, u32[]{:S(2)}, u32[]{:S(2)}) collective-permute-start(bf16[512,1024]{1,0:T(8,128)(2,1)} %get-tuple-element.97), channel_id=1, source_target_pairs={{0,1},{1,0},{2,3},{3,2},{4,5},{5,4},{6,7},{7,6},{8,9},{9,8},{10,11... | collective-permute-start | bytes 3145736 | tf_op jit(solution)/shard_map/ppermute | solution.py:191
  505.9 47.3 %collective-permute-start.43 = (bf16[512,1024]{1,0:T(8,128)(2,1)}, bf16[512,1024]{1,0:T(8,128)(2,1)S(1)}, u32[]{:S(2)}, u32[]{:S(2)}) collective-permute-start(bf16[512,1024]{1,0:T(8,128)(2,1)} %get-tuple-element.96), channel_id=1, source_target_pairs={{0,2},{1,3},{2,0},{3,1},{4,6},{5,7},{6,4},{7,5},{8,10},{9,11},{10,... | collective-permute-start | bytes 3145736 | tf_op jit(solution)/shard_map/ppermute | solution.py:191
  527.9 46.0 %collective-permute-start.38 = (bf16[512,1024]{1,0:T(8,128)(2,1)}, bf16[512,1024]{1,0:T(8,128)(2,1)}, u32[]{:S(2)}, u32[]{:S(2)}) collective-permute-start(bf16[512,1024]{1,0:T(8,128)(2,1)} %collective-permute-done.36), channel_id=1, source_target_pairs={{0,2},{1,3},{2,0},{3,1},{4,6},{5,7},{6,4},{7,5},{8,10},{9,11},{10,... | collective-permute-start | bytes 3145736 | tf_op jit(solution)/shard_map/ppermute | solution.py:191
  531.2 546.5 %reduce-scatter.5.cloned.1.call-start = ((), (), s32[]{:S(2)}) async-start(), calls=%async_computation.5 | async-start | bytes 14090240 | tf_op jit(solution)/shard_map/reduce_scatter | solution.py:268
  538.4 40.2 %collective-permute-start.40 = (bf16[512,1024]{1,0:T(8,128)(2,1)}, bf16[512,1024]{1,0:T(8,128)(2,1)S(1)}, u32[]{:S(2)}, u32[]{:S(2)}) collective-permute-start(bf16[512,1024]{1,0:T(8,128)(2,1)} %collective-permute-done.36), channel_id=1, source_target_pairs={{0,1},{1,0},{2,3},{3,2},{4,5},{5,4},{6,7},{7,6},{8,9},{9,8},{10,11... | collective-permute-start | bytes 3145736 | tf_op jit(solution)/shard_map/ppermute | solution.py:191
  540.7 39.5 %collective-permute-start.44 = (bf16[512,1024]{1,0:T(8,128)(2,1)}, bf16[512,1024]{1,0:T(8,128)(2,1)S(1)}, u32[]{:S(2)}, u32[]{:S(2)}) collective-permute-start(bf16[512,1024]{1,0:T(8,128)(2,1)} %get-tuple-element.96), channel_id=1, source_target_pairs={{0,4},{4,0},{1,5},{5,1},{2,6},{6,2},{3,7},{7,3},{8,12},{12,8},{9,1... | collective-permute-start | bytes 3145736 | tf_op jit(solution)/shard_map/ppermute | solution.py:191
  542.2 38.0 %collective-permute-start.41 = (bf16[512,1024]{1,0:T(8,128)(2,1)}, bf16[512,1024]{1,0:T(8,128)(2,1)S(1)}, u32[]{:S(2)}, u32[]{:S(2)}) collective-permute-start(bf16[512,1024]{1,0:T(8,128)(2,1)} %collective-permute-done.37), channel_id=1, source_target_pairs={{0,1},{1,0},{2,3},{3,2},{4,5},{5,4},{6,7},{7,6},{8,9},{9,8},{10,11... | collective-permute-start | bytes 3145736 | tf_op jit(solution)/shard_map/ppermute | solution.py:191
  553.2 35.7 %collective-permute-start.45 = (bf16[512,1024]{1,0:T(8,128)(2,1)S(1)}, bf16[512,1024]{1,0:T(8,128)(2,1)S(1)}, u32[]{:S(2)}, u32[]{:S(2)}) collective-permute-start(bf16[512,1024]{1,0:T(8,128)(2,1)S(1)} %collective-permute-done.43), channel_id=1, source_target_pairs={{0,4},{4,0},{1,5},{5,1},{2,6},{6,2},{3,7},{7,3},{8,12},{12,8},{9,1... | collective-permute-start | bytes 3145736 | tf_op jit(solution)/shard_map/ppermute | solution.py:191
  793.1 766.4 %reduce-scatter.7.cloned.1.call-start = ((), (), s32[]{:S(2)}) async-start(), calls=%async_computation.6 | async-start | bytes 28180480 | tf_op jit(solution)/shard_map/reduce_scatter | solution.py:268
  1077.7 617.5 %reduce-scatter.9.cloned.1.call-start = ((), (), s32[]{:S(2)}) async-start(), calls=%async_computation.7 | async-start | bytes 15728640 | tf_op jit(solution)/shard_map/reduce_scatter | solution.py:268
  1102.4 35.8 %collective-permute-start.60 = (bf16[2048,1024]{1,0:T(8,128)(2,1)}, bf16[2048,1024]{1,0:T(8,128)(2,1)}, u32[]{:S(2)}, u32[]{:S(2)}) collective-permute-start(bf16[2048,1024]{1,0:T(8,128)(2,1)} %fusion.42), channel_id=1, source_target_pairs={{0,1},{1,0},{2,3},{3,2},{4,5},{5,4},{6,7},{7,6},{8,9},{9,8},{10,11... | collective-permute-start | bytes 12582920 | tf_op jit(solution)/shard_map/ppermute | solution.py:191
  1106.5 28.1 %collective-permute-start.56 = (bf16[512,1024]{1,0:T(8,128)(2,1)S(1)}, bf16[512,1024]{1,0:T(8,128)(2,1)}, u32[]{:S(2)}, u32[]{:S(2)}) collective-permute-start(bf16[512,1024]{1,0:T(8,128)(2,1)S(1)} %get-tuple-element.95), channel_id=1, source_target_pairs={{0,2},{1,3},{2,0},{3,1},{4,6},{5,7},{6,4},{7,5},{8,10},{9,11},{10,... | collective-permute-start | bytes 3145736 | tf_op jit(solution)/shard_map/ppermute | solution.py:191
  1124.6 37.0 %collective-permute-start.58 = (bf16[2048,1024]{1,0:T(8,128)(2,1)}, bf16[2048,1024]{1,0:T(8,128)(2,1)}, u32[]{:S(2)}, u32[]{:S(2)}) collective-permute-start(bf16[2048,1024]{1,0:T(8,128)(2,1)} %fusion.39), channel_id=1, source_target_pairs={{0,1},{1,0},{2,3},{3,2},{4,5},{5,4},{6,7},{7,6},{8,9},{9,8},{10,11... | collective-permute-start | bytes 12582920 | tf_op jit(solution)/shard_map/ppermute | solution.py:191
  1128.5 60.7 %collective-permute-start.51 = (bf16[512,1024]{1,0:T(8,128)(2,1)}, bf16[512,1024]{1,0:T(8,128)(2,1)}, u32[]{:S(2)}, u32[]{:S(2)}) collective-permute-start(bf16[512,1024]{1,0:T(8,128)(2,1)} %dynamic-slice_bitcast_fusion.14), channel_id=1, source_target_pairs={{0,4},{4,0},{1,5},{5,1},{2,6},{6,2},{3,7},{7,3},{8,12},{12,8},{9,1... | collective-permute-start | bytes 3145736 | tf_op jit(solution)/shard_map/ppermute | solution.py:191
  1130.9 72.7 %collective-permute-start.55 = (bf16[512,1024]{1,0:T(8,128)(2,1)S(1)}, bf16[512,1024]{1,0:T(8,128)(2,1)}, u32[]{:S(2)}, u32[]{:S(2)}) collective-permute-start(bf16[512,1024]{1,0:T(8,128)(2,1)S(1)} %get-tuple-element.94), channel_id=1, source_target_pairs={{0,2},{1,3},{2,0},{3,1},{4,6},{5,7},{6,4},{7,5},{8,10},{9,11},{10,... | collective-permute-start | bytes 3145736 | tf_op jit(solution)/shard_map/ppermute | solution.py:191
  1134.6 70.0 %collective-permute-start.54 = (bf16[512,1024]{1,0:T(8,128)(2,1)}, bf16[512,1024]{1,0:T(8,128)(2,1)}, u32[]{:S(2)}, u32[]{:S(2)}) collective-permute-start(bf16[512,1024]{1,0:T(8,128)(2,1)} %fusion.98), channel_id=1, source_target_pairs={{0,2},{1,3},{2,0},{3,1},{4,6},{5,7},{6,4},{7,5},{8,10},{9,11},{10,... | collective-permute-start | bytes 3145736 | tf_op jit(solution)/shard_map/ppermute | solution.py:191
  1161.6 39.1 %collective-permute-start.64 = (bf16[512,1024]{1,0:T(8,128)(2,1)}, bf16[512,1024]{1,0:T(8,128)(2,1)}, u32[]{:S(2)}, u32[]{:S(2)}) collective-permute-start(bf16[512,1024]{1,0:T(8,128)(2,1)} %get-tuple-element.93), channel_id=1, source_target_pairs={{0,2},{1,3},{2,0},{3,1},{4,6},{5,7},{6,4},{7,5},{8,10},{9,11},{10,... | collective-permute-start | bytes 3145736 | tf_op jit(solution)/shard_map/ppermute | solution.py:191
  1189.2 42.9 %collective-permute-start.59 = (bf16[512,1024]{1,0:T(8,128)(2,1)S(1)}, bf16[512,1024]{1,0:T(8,128)(2,1)}, u32[]{:S(2)}, u32[]{:S(2)}) collective-permute-start(bf16[512,1024]{1,0:T(8,128)(2,1)S(1)} %dynamic-slice_bitcast_fusion.10), channel_id=1, source_target_pairs={{0,4},{4,0},{1,5},{5,1},{2,6},{6,2},{3,7},{7,3},{8,12},{12,8},{9,1... | collective-permute-start | bytes 3145736 | tf_op jit(solution)/shard_map/ppermute | solution.py:191
  1200.7 31.4 %collective-permute-start.62 = (bf16[512,1024]{1,0:T(8,128)(2,1)S(1)}, bf16[512,1024]{1,0:T(8,128)(2,1)}, u32[]{:S(2)}, u32[]{:S(2)}) collective-permute-start(bf16[512,1024]{1,0:T(8,128)(2,1)S(1)} %fusion.94), channel_id=1, source_target_pairs={{0,2},{1,3},{2,0},{3,1},{4,6},{5,7},{6,4},{7,5},{8,10},{9,11},{10,... | collective-permute-start | bytes 3145736 | tf_op jit(solution)/shard_map/ppermute | solution.py:191
  1203.6 43.5 %collective-permute-start.63 = (bf16[512,1024]{1,0:T(8,128)(2,1)S(1)}, bf16[512,1024]{1,0:T(8,128)(2,1)S(1)}, u32[]{:S(2)}, u32[]{:S(2)}) collective-permute-start(bf16[512,1024]{1,0:T(8,128)(2,1)S(1)} %copy-done.32), channel_id=1, source_target_pairs={{0,2},{1,3},{2,0},{3,1},{4,6},{5,7},{6,4},{7,5},{8,10},{9,11},{10,... | collective-permute-start | bytes 3145736 | tf_op jit(solution)/shard_map/ppermute | solution.py:191
  1204.6 47.2 %collective-permute-start.65 = (bf16[512,1024]{1,0:T(8,128)(2,1)S(1)}, bf16[512,1024]{1,0:T(8,128)(2,1)}, u32[]{:S(2)}, u32[]{:S(2)}) collective-permute-start(bf16[512,1024]{1,0:T(8,128)(2,1)S(1)} %fusion.92), channel_id=1, source_target_pairs={{0,4},{4,0},{1,5},{5,1},{2,6},{6,2},{3,7},{7,3},{8,12},{12,8},{9,1... | collective-permute-start | bytes 3145736 | tf_op jit(solution)/shard_map/ppermute | solution.py:191
  1272.2 27.0 %collective-permute-start.69 = (bf16[512,1024]{1,0:T(8,128)(2,1)S(1)}, bf16[512,1024]{1,0:T(8,128)(2,1)S(1)}, u32[]{:S(2)}, u32[]{:S(2)}) collective-permute-start(bf16[512,1024]{1,0:T(8,128)(2,1)S(1)} %get-tuple-element.91), channel_id=1, source_target_pairs={{0,1},{1,0},{2,3},{3,2},{4,5},{5,4},{6,7},{7,6},{8,9},{9,8},{10,11... | collective-permute-start | bytes 3145736 | tf_op jit(solution)/shard_map/ppermute | solution.py:191
  1272.2 47.1 %collective-permute-start.73 = (bf16[512,1024]{1,0:T(8,128)(2,1)S(1)}, bf16[512,1024]{1,0:T(8,128)(2,1)S(1)}, u32[]{:S(2)}, u32[]{:S(2)}) collective-permute-start(bf16[512,1024]{1,0:T(8,128)(2,1)S(1)} %get-tuple-element.90), channel_id=1, source_target_pairs={{0,2},{1,3},{2,0},{3,1},{4,6},{5,7},{6,4},{7,5},{8,10},{9,11},{10,... | collective-permute-start | bytes 3145736 | tf_op jit(solution)/shard_map/ppermute | solution.py:191
  1294.1 45.8 %collective-permute-start.68 = (bf16[512,1024]{1,0:T(8,128)(2,1)S(1)}, bf16[512,1024]{1,0:T(8,128)(2,1)S(1)}, u32[]{:S(2)}, u32[]{:S(2)}) collective-permute-start(bf16[512,1024]{1,0:T(8,128)(2,1)S(1)} %collective-permute-done.66), channel_id=1, source_target_pairs={{0,2},{1,3},{2,0},{3,1},{4,6},{5,7},{6,4},{7,5},{8,10},{9,11},{10,... | collective-permute-start | bytes 3145736 | tf_op jit(solution)/shard_map/ppermute | solution.py:191
  1297.5 42.7 %collective-permute-start.70 = (bf16[512,1024]{1,0:T(8,128)(2,1)S(1)}, bf16[512,1024]{1,0:T(8,128)(2,1)S(1)}, u32[]{:S(2)}, u32[]{:S(2)}) collective-permute-start(bf16[512,1024]{1,0:T(8,128)(2,1)S(1)} %collective-permute-done.66), channel_id=1, source_target_pairs={{0,1},{1,0},{2,3},{3,2},{4,5},{5,4},{6,7},{7,6},{8,9},{9,8},{10,11... | collective-permute-start | bytes 3145736 | tf_op jit(solution)/shard_map/ppermute | solution.py:191
  1297.7 43.2 %collective-permute-start.74 = (bf16[512,1024]{1,0:T(8,128)(2,1)S(1)}, bf16[512,1024]{1,0:T(8,128)(2,1)S(1)}, u32[]{:S(2)}, u32[]{:S(2)}) collective-permute-start(bf16[512,1024]{1,0:T(8,128)(2,1)S(1)} %get-tuple-element.90), channel_id=1, source_target_pairs={{0,4},{4,0},{1,5},{5,1},{2,6},{6,2},{3,7},{7,3},{8,12},{12,8},{9,1... | collective-permute-start | bytes 3145736 | tf_op jit(solution)/shard_map/ppermute | solution.py:191
  1299.2 41.8 %collective-permute-start.71 = (bf16[512,1024]{1,0:T(8,128)(2,1)S(1)}, bf16[512,1024]{1,0:T(8,128)(2,1)S(1)}, u32[]{:S(2)}, u32[]{:S(2)}) collective-permute-start(bf16[512,1024]{1,0:T(8,128)(2,1)S(1)} %collective-permute-done.67), channel_id=1, source_target_pairs={{0,1},{1,0},{2,3},{3,2},{4,5},{5,4},{6,7},{7,6},{8,9},{9,8},{10,11... | collective-permute-start | bytes 3145736 | tf_op jit(solution)/shard_map/ppermute | solution.py:191
  1442.6 314.2 %reduce-scatter.11.cloned.1.call-start = ((), (), s32[]{:S(2)}) async-start(), calls=%async_computation.8 | async-start | bytes 5242880 | tf_op jit(solution)/shard_map/reduce_scatter | solution.py:268
  1465.8 66.4 %collective-permute-start.82 = (bf16[2048,1024]{1,0:T(8,128)(2,1)}, bf16[2048,1024]{1,0:T(8,128)(2,1)}, u32[]{:S(2)}, u32[]{:S(2)}) collective-permute-start(bf16[2048,1024]{1,0:T(8,128)(2,1)} %convolution_convert_fusion.2), channel_id=1, source_target_pairs={{0,1},{1,0},{2,3},{3,2},{4,5},{5,4},{6,7},{7,6},{8,9},{9,8},{10,11... | collective-permute-start | bytes 12582920 | tf_op jit(solution)/shard_map/ppermute | solution.py:191
  1478.1 48.6 %collective-permute-start.94 = (bf16[4,512,512]{2,1,0:T(8,128)(2,1)S(1)}, bf16[4,512,512]{2,1,0:T(8,128)(2,1)}, u32[]{:S(2)}, u32[]{:S(2)}) collective-permute-start(bf16[4,512,512]{2,1,0:T(8,128)(2,1)S(1)} %constant_dynamic-slice_fusion), channel_id=1, source_target_pairs={{0,4},{4,0},{1,5},{5,1},{2,6},{6,2},{3,7},{7,3},{8,12},{12,8},{9,1... | collective-permute-start | bytes 6291464 | tf_op jit(solution)/shard_map/ppermute | solution.py:191
  1491.0 57.6 %collective-permute-start.80 = (bf16[2048,1024]{1,0:T(8,128)(2,1)}, bf16[2048,1024]{1,0:T(8,128)(2,1)}, u32[]{:S(2)}, u32[]{:S(2)}) collective-permute-start(bf16[2048,1024]{1,0:T(8,128)(2,1)} %convolution_convert_fusion.3), channel_id=1, source_target_pairs={{0,1},{1,0},{2,3},{3,2},{4,5},{5,4},{6,7},{7,6},{8,9},{9,8},{10,11... | collective-permute-start | bytes 12582920 | tf_op jit(solution)/shard_map/ppermute | solution.py:191
  1492.7 92.1 %collective-permute-start.92 = (bf16[1376,512]{1,0:T(8,128)(2,1)S(1)}, bf16[1376,512]{1,0:T(8,128)(2,1)}, u32[]{:S(2)}, u32[]{:S(2)}) collective-permute-start(bf16[1376,512]{1,0:T(8,128)(2,1)S(1)} %dynamic-slice_bitcast_fusion.2), channel_id=1, source_target_pairs={{0,4},{4,0},{1,5},{5,1},{2,6},{6,2},{3,7},{7,3},{8,12},{12,8},{9,1... | collective-permute-start | bytes 4227080 | tf_op jit(solution)/shard_map/ppermute | solution.py:191
  1544.6 34.8 %collective-permute-start.83 = (bf16[512,1024]{1,0:T(8,128)(2,1)}, bf16[512,1024]{1,0:T(8,128)(2,1)}, u32[]{:S(2)}, u32[]{:S(2)}) collective-permute-start(bf16[512,1024]{1,0:T(8,128)(2,1)} %dynamic-slice_bitcast_fusion.5), channel_id=1, source_target_pairs={{0,4},{4,0},{1,5},{5,1},{2,6},{6,2},{3,7},{7,3},{8,12},{12,8},{9,1... | collective-permute-start | bytes 3145736 | tf_op jit(solution)/shard_map/ppermute | solution.py:191
  1547.5 35.0 %collective-permute-start.86 = (bf16[512,1024]{1,0:T(8,128)(2,1)}, bf16[512,1024]{1,0:T(8,128)(2,1)}, u32[]{:S(2)}, u32[]{:S(2)}) collective-permute-start(bf16[512,1024]{1,0:T(8,128)(2,1)} %get-tuple-element.89), channel_id=1, source_target_pairs={{0,2},{1,3},{2,0},{3,1},{4,6},{5,7},{6,4},{7,5},{8,10},{9,11},{10,... | collective-permute-start | bytes 3145736 | tf_op jit(solution)/shard_map/ppermute | solution.py:191
  1561.7 125.8 %collective-permute-start.88 = (bf16[512,2752]{0,1:T(8,128)(2,1)S(1)}, bf16[512,2752]{0,1:T(8,128)(2,1)S(1)}, u32[]{:S(2)}, u32[]{:S(2)}) collective-permute-start(bf16[512,2752]{0,1:T(8,128)(2,1)S(1)} %dynamic-slice_bitcast_fusion.1), channel_id=1, source_target_pairs={{0,4},{4,0},{1,5},{5,1},{2,6},{6,2},{3,7},{7,3},{8,12},{12,8},{9,1... | collective-permute-start | bytes 8454152 | tf_op jit(solution)/shard_map/ppermute | solution.py:191
  1563.4 98.7 %collective-permute-start.81 = (bf16[512,1024]{1,0:T(8,128)(2,1)S(1)}, bf16[512,1024]{1,0:T(8,128)(2,1)S(1)}, u32[]{:S(2)}, u32[]{:S(2)}) collective-permute-start(bf16[512,1024]{1,0:T(8,128)(2,1)S(1)} %dynamic-slice_bitcast_fusion.6), channel_id=1, source_target_pairs={{0,4},{4,0},{1,5},{5,1},{2,6},{6,2},{3,7},{7,3},{8,12},{12,8},{9,1... | collective-permute-start | bytes 3145736 | tf_op jit(solution)/shard_map/ppermute | solution.py:191
  1579.4 83.3 %collective-permute-start.85 = (bf16[512,1024]{1,0:T(8,128)(2,1)S(1)}, bf16[512,1024]{1,0:T(8,128)(2,1)S(1)}, u32[]{:S(2)}, u32[]{:S(2)}) collective-permute-start(bf16[512,1024]{1,0:T(8,128)(2,1)S(1)} %copy-done.33), channel_id=1, source_target_pairs={{0,2},{1,3},{2,0},{3,1},{4,6},{5,7},{6,4},{7,5},{8,10},{9,11},{10,... | collective-permute-start | bytes 3145736 | tf_op jit(solution)/shard_map/ppermute | solution.py:191
  1582.5 79.7 %collective-permute-start.84 = (bf16[512,1024]{1,0:T(8,128)(2,1)S(1)}, bf16[512,1024]{1,0:T(8,128)(2,1)S(1)}, u32[]{:S(2)}, u32[]{:S(2)}) collective-permute-start(bf16[512,1024]{1,0:T(8,128)(2,1)S(1)} %fusion.90), channel_id=1, source_target_pairs={{0,2},{1,3},{2,0},{3,1},{4,6},{5,7},{6,4},{7,5},{8,10},{9,11},{10,... | collective-permute-start | bytes 3145736 | tf_op jit(solution)/shard_map/ppermute | solution.py:191
  1584.8 99.4 %collective-permute-start.87 = (bf16[512,1024]{1,0:T(8,128)(2,1)S(1)}, bf16[512,1024]{1,0:T(8,128)(2,1)S(1)}, u32[]{:S(2)}, u32[]{:S(2)}) collective-permute-start(bf16[512,1024]{1,0:T(8,128)(2,1)S(1)} %fusion.88), channel_id=1, source_target_pairs={{0,4},{4,0},{1,5},{5,1},{2,6},{6,2},{3,7},{7,3},{8,12},{12,8},{9,1... | collective-permute-start | bytes 3145736 | tf_op jit(solution)/shard_map/ppermute | solution.py:191
  1697.9 53.4 %collective-permute-start.93 = (bf16[512,1536]{1,0:T(8,128)(2,1)}, bf16[512,1536]{1,0:T(8,128)(2,1)}, u32[]{:S(2)}, u32[]{:S(2)}) collective-permute-start(bf16[512,1536]{1,0:T(8,128)(2,1)} %constant_dynamic-slice_fusion.1), channel_id=1, source_target_pairs={{0,4},{4,0},{1,5},{5,1},{2,6},{6,2},{3,7},{7,3},{8,12},{12,8},{9,1... | collective-permute-start | bytes 4718600 | tf_op jit(solution)/shard_map/ppermute | solution.py:191
  1702.8 31.6 %collective-permute-start.89 = (f32[2,1024]{1,0:T(2,128)S(1)}, f32[2,1024]{1,0:T(2,128)S(1)}, u32[]{:S(2)}, u32[]{:S(2)}) collective-permute-start(f32[2,1024]{1,0:T(2,128)S(1)} %pad_maximum_fusion.10), channel_id=1, source_target_pairs={{0,4},{4,0},{1,5},{5,1},{2,6},{6,2},{3,7},{7,3},{8,12},{12,8},{9,1... | collective-permute-start | bytes 24584 | tf_op jit(solution)/shard_map/ppermute | solution.py:191
  (105 other events, 1400.4 us)
Sparse Core Ops, SparseCore 0:
  16.2 289.4 all-gather.7
  307.8 380.7 all-gather.5
  690.7 195.1 all-gather.9
  888.7 188.8 reduce-scatter.4
  1079.9 373.3 reduce-scatter.6
  1455.4 213.5 reduce-scatter.8
  1671.3 78.0 reduce-scatter.10

commit v13 on v12

--- a/solution.py
+++ b/solution.py
@@ -286,7 +286,6 @@
 
 
 def total_rows(values):
-    values = values + swap(values, "ctx", 0)
     for bit in range(lax.axis_size("fsdp").bit_length() - 1):
         values = values + swap(values, "fsdp", bit)
     return values
@@ -387,13 +386,15 @@
     attn_dot = row_total(jnp.sum(attn_term * input_float, axis=-1))[:, None]
     grad_input = grad_resid + rms_one * attn_term - input_float * rms_one**3 * attn_dot / D
     attn_gain_part = jnp.sum(grad_nattn * input_float * rms_one, axis=0)
-    gain_grads = total_rows(jnp.stack([attn_gain_part, ffn_gain_part]))
+    gain_parts = jnp.stack([attn_gain_part, ffn_gain_part])
+    gain_parts = gain_parts + swap(gain_parts, "ctx", 0)
+    gain_grads = total_rows(gain_parts)
 
     down_grad = out_grad(down_sum)
     gu_grad = jnp.concatenate(
         [v.reshape(v.shape[0], 2, -1) for v in gu_halves], axis=2
     ).astype(F32)
-    done = (down_grad, gu_grad)
+    done = (down_grad, gu_grad, gain_parts)
     qkv_grad = []
     for part in qkv_sum:
         first, second = trade_ctx(after(part, done), 0)

time: 1770 us -> 1760 us (level)
  transfers between devices with their start and end apart: 102 -> 102, of which waited for: 41 -> 42; matrix products, arithmetic and copies ran while one was open for 38% -> 38% of each run, Pallas kernels for 4% -> 4%
where the time goes in v13:
time: 1760 us
  waiting for transfers between devices  864 us (49%)
  matrix products  452 us (26%)
  local copies, waits for them, and re-layouts  136 us (8%)
  other arithmetic  115 us (7%)
  Pallas kernels  79 us (4%)
  starting transfers between devices  71.2 us (4%)
  blocking collectives  26.9 us (2%)
    ppermute x95, waiting for transfers between devices, swap(): lax.ppermute(values, axis, [(i, i ^ step) for i in range(lax.axis_size(ax...  521 us
    dot_general x32, matrix products, mm(): return lax.dot_general(left, right, dims, preferred_element_type=F32)  452 us
    all_gather x3, waiting for transfers between devices, spread(): return lax.all_gather(weight, 'fsdp', axis=0, tiled=False)  276 us
    ppermute x95, starting transfers between devices, swap(): lax.ppermute(values, axis, [(i, i ^ step) for i in range(lax.axis_size(ax...  71 us
    reduce_scatter x4, waiting for transfers between devices, owners(): return lax.psum_scatter(grad, 'fsdp', scatter_dimension=0, tiled=False)  67.2 us
    dynamic_update_slice x64, local copies, waits for them, and re-layouts, gather_rows(): full = lax.dynamic_update_slice(full, piece[None], start)  47.2 us
    pallas_call x1, Pallas kernels, attend_backward(): pl.pallas_call(kernel, grid=(heads, blocks), in_specs=[row, col, col, row...  44 us
  transfers between devices with their start and end apart: 102, of which 42 were waited for; matrix products, arithmetic and copies ran while one was open for 38% of the time, Pallas kernels for 4%

profile of v13, /device:TPU:0, one launch (start us, length us, event | category | flops | bytes accessed | tf_op | source)
XLA Modules:
  0.0 1759.3 jit_solution(11900666873526560301)
XLA Ops:
  23.9 8.8 psum.28
  40.2 20.4 %collective-permute-done = bf16[512,1024]{1,0:T(8,128)(2,1)} collective-permute-done((bf16[512,1024]{1,0:T(8,128)(2,1)}, bf16[512,1024]{1,0:T(8,128)(2,1)}, u32[]{:S(2)}, u32[]{:S(2)}) %collective-permute-start) | collective-permute-done | bytes 1048608 | tf_op jit(solution)/shard_map/ppermute | solution.py:191
  67.7 19.3 %collective-permute-done.7 = bf16[512,1024]{1,0:T(8,128)(2,1)S(1)} collective-permute-done((bf16[512,1024]{1,0:T(8,128)(2,1)}, bf16[512,1024]{1,0:T(8,128)(2,1)S(1)}, u32[]{:S(2)}, u32[]{:S(2)}) %collective-permute-start.7) | collective-permute-done | bytes 1048608 | tf_op jit(solution)/shard_map/ppermute | solution.py:191
  88.8 18.0 %collective-permute-done.2 = bf16[512,1024]{1,0:T(8,128)(2,1)} collective-permute-done((bf16[512,1024]{1,0:T(8,128)(2,1)}, bf16[512,1024]{1,0:T(8,128)(2,1)}, u32[]{:S(2)}, u32[]{:S(2)}) %collective-permute-start.2) | collective-permute-done | bytes 1048608 | tf_op jit(solution)/shard_map/ppermute | solution.py:191
  124.7 18.0 %collective-permute-done.14 = bf16[512,1024]{1,0:T(8,128)(2,1)S(1)} collective-permute-done((bf16[512,1024]{1,0:T(8,128)(2,1)S(1)}, bf16[512,1024]{1,0:T(8,128)(2,1)S(1)}, u32[]{:S(2)}, u32[]{:S(2)}) %collective-permute-start.14) | collective-permute-done | bytes 1048608 | tf_op jit(solution)/shard_map/ppermute | solution.py:191
  144.9 6.1 broadcast.35.clone.1
  153.9 13.4 collective-permute-done.21
  168.9 19.8 %collective-permute-done.16 = bf16[512,1024]{1,0:T(8,128)(2,1)S(1)} collective-permute-done((bf16[512,1024]{1,0:T(8,128)(2,1)S(1)}, bf16[512,1024]{1,0:T(8,128)(2,1)S(1)}, u32[]{:S(2)}, u32[]{:S(2)}) %collective-permute-start.16) | collective-permute-done | bytes 1048608 | tf_op jit(solution)/shard_map/ppermute | solution.py:191
  192.8 8.4 collective-permute-done.23
  211.8 93.9 %all-gather.8.cloned.1.call-done = bf16[16,1024,512]{2,1,0:T(8,128)(2,1)} async-done(((bf16[4,1024,512]{2,1,0:T(8,128)(2,1)}), bf16[16,1024,512]{2,1,0:T(8,128)(2,1)}) %all-gather.8.cloned.1.call-update) | async-done | bytes 16777232 | tf_op jit(solution)/shard_map/all_gather | solution.py:272
  305.7 15.2 convolution_bitcast_fusion.1.v_in
  320.9 16.1 convolution_bitcast_fusion.2.k_in
  337.0 12.4 convolution_bitcast_fusion.3.q_in
  349.4 35.1 %shard_map.143 = (bf16[2048,512]{1,0:T(8,128)(2,1)S(1)}, bf16[2048,512]{1,0:T(8,128)(2,1)}, bf16[2048,512]{1,0:T(8,128)(2,1)}, bf16[2048,512]{1,0:T(8,128)(2,1)}, f32[4,1,2048]{2,1,0:T(1,128)S(1)}) custom-call(f32[2048,512]{1,0:T(8,128)} %convolution_bitcast_fusion.3.q_in, f32[2048,512]{1,0:T(8,128)} %convolution_bitcast_fusion.2.k_in, ...), custom_call_target="tpu_custom_call" | custom-call | flops 5368709120 | bytes 20971520 | tf_op jit(solution)/shard_map/pallas_call | solution.py:88
  384.5 12.3 slice_bitcast_fusion.18
  424.2 16.7 collective-permute-done.31
  445.3 18.1 %collective-permute-done.29 = bf16[512,1024]{1,0:T(8,128)(2,1)S(1)} collective-permute-done((bf16[512,1024]{1,0:T(8,128)(2,1)S(1)}, bf16[512,1024]{1,0:T(8,128)(2,1)S(1)}, u32[]{:S(2)}, u32[]{:S(2)}) %collective-permute-start.29) | collective-permute-done | bytes 1048608 | tf_op jit(solution)/shard_map/ppermute | solution.py:191
  468.1 19.5 %collective-permute-done.33 = bf16[512,1024]{1,0:T(8,128)(2,1)S(1)} collective-permute-done((bf16[512,1024]{1,0:T(8,128)(2,1)S(1)}, bf16[512,1024]{1,0:T(8,128)(2,1)S(1)}, u32[]{:S(2)}, u32[]{:S(2)}) %collective-permute-start.33) | collective-permute-done | bytes 1048608 | tf_op jit(solution)/shard_map/ppermute | solution.py:191
  506.5 21.4 %collective-permute-done.36 = bf16[512,1024]{1,0:T(8,128)(2,1)} collective-permute-done((bf16[512,1024]{1,0:T(8,128)(2,1)}, bf16[512,1024]{1,0:T(8,128)(2,1)}, u32[]{:S(2)}, u32[]{:S(2)}) %collective-permute-start.36) | collective-permute-done | bytes 1048608 | tf_op jit(solution)/shard_map/ppermute | solution.py:191
  531.2 6.2 broadcast.35.clone.2
  542.4 10.8 collective-permute-done.43
  556.1 17.8 %collective-permute-done.38 = bf16[512,1024]{1,0:T(8,128)(2,1)} collective-permute-done((bf16[512,1024]{1,0:T(8,128)(2,1)}, bf16[512,1024]{1,0:T(8,128)(2,1)}, u32[]{:S(2)}, u32[]{:S(2)}) %collective-permute-start.38) | collective-permute-done | bytes 1048608 | tf_op jit(solution)/shard_map/ppermute | solution.py:191
  580.7 8.3 collective-permute-done.45
  599.6 89.0 %all-gather.6.cloned.1.call-done = bf16[4,1024,2752]{1,2,0:T(8,128)(2,1)} async-done(((bf16[1,1024,2752]{1,2,0:T(8,128)(2,1)}), bf16[4,1024,2752]{1,2,0:T(8,128)(2,1)}) %all-gather.6.cloned.1.call-update) | async-done | bytes 22544400 | tf_op jit(solution)/shard_map/all_gather | solution.py:272
  688.6 56.9 %convolution_bitcast_fusion = f32[2048,2752]{0,1:T(8,128)} fusion(bf16[4,2048,1024]{2,1,0:T(8,128)(2,1)} %bitcast_dynamic-update-slice_fusion.16, bf16[4,1024,2752]{1,2,0:T(8,128)(2,1)} %all-gather.6.cloned.1.call-done), kind=kOutput, calls=%fused_computation.2 | convolution fusion | flops 46170898432 | bytes 61865984 | tf_op jit(solution)/shard_map/dot_general | solution.py:21
  745.5 8.9 multiply_convert_fusion
  754.4 9.7 fusion.57
  764.1 7.9 fusion.56
  772.1 7.9 fusion.55
  780.0 7.9 fusion.54
  793.1 92.8 %all-gather.10.cloned.1.call-done = bf16[5504,1024]{1,0:T(8,128)(2,1)} async-done(((bf16[1376,1024]{1,0:T(8,128)(2,1)}), bf16[5504,1024]{1,0:T(8,128)(2,1)}) %all-gather.10.cloned.1.call-update) | async-done | bytes 11272208 | tf_op jit(solution)/shard_map/all_gather | solution.py:272
  885.9 37.5 %fusion.3 = (bf16[2048,1376]{0,1:T(8,128)(2,1)S(1)}, bf16[2048,1376]{0,1:T(8,128)(2,1)}) fusion(f32[2048,2752]{0,1:T(8,128)} %convolution_bitcast_fusion, bf16[4,2048,1024]{2,1,0:T(8,128)(2,1)} %bitcast_dynamic-update-slice_fusion.32, bf16[4,1376,1024]{2,1,0:T(8,128)(2,1)} %bitcast.522), kind=kOutput, calls=%fused_computation.11 | convolution fusion | flops 23122083840 | bytes 61865984 | tf_op jit(solution)/shard_map/dot_general | solution.py:21
  925.9 54.8 %convolution_convert_fusion = bf16[4,1024,2752]{1,2,0:T(8,128)(2,1)} fusion(bf16[4,2048,1024]{2,1,0:T(8,128)(2,1)} %bitcast_dynamic-update-slice_fusion.16, bf16[2048,1376]{0,1:T(8,128)(2,1)} %get-tuple-element.59, bf16[2048,1376]{0,1:T(8,128)(2,1)S(1)} %get-tuple-element.58), kind=kOutput, calls=%fused_computation | convolution fusion | flops 46204715008 | bytes 50593792 | tf_op jit(solution)/shard_map/dot_general | solution.py:21
  980.7 9.8 convolution_convert_fusion.5
  990.6 8.7 convolution_convert_fusion.4
  999.8 8.6 add_convert_fusion.5
  1008.4 8.6 add_convert_fusion.4
  1017.0 60.6 %reduce-scatter.5.cloned.1.call-done = bf16[1,1376,1024]{2,1,0:T(8,128)(2,1)} async-done(((bf16[4,1376,1024]{2,1,0:T(8,128)(2,1)}), bf16[1,1376,1024]{2,1,0:T(8,128)(2,1)}) %reduce-scatter.5.cloned.1.call-update) | async-done | bytes 2818064 | tf_op jit(solution)/shard_map/reduce_scatter | solution.py:268
  1077.7 7.9 pad_maximum_fusion.2
  1085.6 16.8 fusion.42
  1108.0 16.6 fusion.39
  1138.2 17.0 add_convert_fusion.2
  1163.2 17.2 add_convert_fusion.3
  1190.2 10.5 collective-permute-done.64
  1213.4 18.7 %collective-permute-done.59 = bf16[512,1024]{1,0:T(8,128)(2,1)} collective-permute-done((bf16[512,1024]{1,0:T(8,128)(2,1)S(1)}, bf16[512,1024]{1,0:T(8,128)(2,1)}, u32[]{:S(2)}, u32[]{:S(2)}) %collective-permute-start.59) | collective-permute-done | bytes 1048608 | tf_op jit(solution)/shard_map/ppermute | solution.py:191
  1234.3 12.8 collective-permute-done.63
  1262.5 6.9 fusion.146
  1272.7 21.4 %collective-permute-done.66 = bf16[512,1024]{1,0:T(8,128)(2,1)S(1)} collective-permute-done((bf16[512,1024]{1,0:T(8,128)(2,1)S(1)}, bf16[512,1024]{1,0:T(8,128)(2,1)S(1)}, u32[]{:S(2)}, u32[]{:S(2)}) %collective-permute-start.66) | collective-permute-done | bytes 1048608 | tf_op jit(solution)/shard_map/ppermute | solution.py:191
  1299.4 19.9 %collective-permute-done.73 = bf16[512,1024]{1,0:T(8,128)(2,1)S(1)} collective-permute-done((bf16[512,1024]{1,0:T(8,128)(2,1)S(1)}, bf16[512,1024]{1,0:T(8,128)(2,1)S(1)}, u32[]{:S(2)}, u32[]{:S(2)}) %collective-permute-start.73) | collective-permute-done | bytes 1048608 | tf_op jit(solution)/shard_map/ppermute | solution.py:191
  1320.3 19.6 %collective-permute-done.68 = bf16[512,1024]{1,0:T(8,128)(2,1)S(1)} collective-permute-done((bf16[512,1024]{1,0:T(8,128)(2,1)S(1)}, bf16[512,1024]{1,0:T(8,128)(2,1)S(1)}, u32[]{:S(2)}, u32[]{:S(2)}) %collective-permute-start.68) | collective-permute-done | bytes 1048608 | tf_op jit(solution)/shard_map/ppermute | solution.py:191
  1348.7 13.7 bitcast_convert_fusion.g
  1362.4 44.0 %shard_map.144 = (bf16[2048,512]{1,0:T(8,128)(2,1)S(1)}, bf16[2048,512]{1,0:T(8,128)(2,1)}, bf16[2048,512]{1,0:T(8,128)(2,1)}) custom-call(bf16[2048,512]{1,0:T(8,128)(2,1)} %copy-done.2, bf16[2048,512]{1,0:T(8,128)(2,1)} %get-tuple-element.39.k, bf16[2048,512]{1,0:T(8,128)(2,1)} %get-tuple-element.40.v, bf16[2048,512]{1,0:T(8,128)(2,1)} %get-tuple-element.48.o, ...), custom_call_target="tpu_custom_call" | custom-call | flops 13421772800 | bytes 16777216 | tf_op jit(solution)/shard_map/pallas_call | solution.py:164
  1411.5 31.0 %convolution_convert_fusion.1 = bf16[4,1024,1536]{2,1,0:T(8,128)(2,1)} fusion(bf16[4,2048,1024]{2,1,0:T(8,128)(2,1)} %copy-done.15, bf16[2048,1536]{1,0:T(8,128)(2,1)S(1)} %constant_dynamic-update-slice_fusion), kind=kOutput, calls=%fused_computation.1 | convolution fusion | flops 25776095232 | bytes 35651584 | tf_op jit(solution)/shard_map/dot_general | solution.py:21
  1442.6 7.4 pad_maximum_fusion
  1450.1 15.7 convolution_convert_fusion.2
  1479.5 11.5 convolution_convert_fusion.3
  1493.3 33.4 %collective-permute-done.94 = bf16[4,512,512]{2,1,0:T(8,128)(2,1)} collective-permute-done((bf16[4,512,512]{2,1,0:T(8,128)(2,1)S(1)}, bf16[4,512,512]{2,1,0:T(8,128)(2,1)}, u32[]{:S(2)}, u32[]{:S(2)}) %collective-permute-start.94) | collective-permute-done | bytes 2097184 | tf_op jit(solution)/shard_map/ppermute | solution.py:191
  1532.2 10.9 add_convert_fusion
  1548.6 10.8 add_convert_fusion.1
  1564.4 14.9 collective-permute-done.83
  1591.4 70.7 %collective-permute-done.81 = bf16[512,1024]{1,0:T(8,128)(2,1)S(1)} collective-permute-done((bf16[512,1024]{1,0:T(8,128)(2,1)S(1)}, bf16[512,1024]{1,0:T(8,128)(2,1)S(1)}, u32[]{:S(2)}, u32[]{:S(2)}) %collective-permute-start.81) | collective-permute-done | bytes 1048608 | tf_op jit(solution)/shard_map/ppermute | solution.py:191
  1662.7 21.4 %collective-permute-done.87 = bf16[512,1024]{1,0:T(8,128)(2,1)S(1)} collective-permute-done((bf16[512,1024]{1,0:T(8,128)(2,1)S(1)}, bf16[512,1024]{1,0:T(8,128)(2,1)S(1)}, u32[]{:S(2)}, u32[]{:S(2)}) %collective-permute-start.87) | collective-permute-done | bytes 1048608 | tf_op jit(solution)/shard_map/ppermute | solution.py:191
  1718.8 18.6 %collective-permute-done.93 = bf16[512,1536]{1,0:T(8,128)(2,1)} collective-permute-done((bf16[512,1536]{1,0:T(8,128)(2,1)}, bf16[512,1536]{1,0:T(8,128)(2,1)}, u32[]{:S(2)}, u32[]{:S(2)}) %collective-permute-start.93) | collective-permute-done | bytes 1572896 | tf_op jit(solution)/shard_map/ppermute | solution.py:191
  1742.9 6.5 reduce-scatter.11.cloned.1.call-done
  (487 shorter events, 342.3 us)
Async XLA Ops:
  7.2 298.5 %all-gather.8.cloned.1.call-start = ((), (), s32[]{:S(2)}) async-start(), calls=%async_computation.9 | async-start | bytes 20971520 | tf_op jit(solution)/shard_map/all_gather | solution.py:272
  16.1 672.5 %all-gather.6.cloned.1.call-start = ((), (), s32[]{:S(2)}) async-start(), calls=%async_computation.4 | async-start | bytes 28180480 | tf_op jit(solution)/shard_map/all_gather | solution.py:272
  21.9 864.1 %all-gather.10.cloned.1.call-start = ((), (), s32[]{:S(2)}) async-start(), calls=%async_computation.10 | async-start | bytes 14090240 | tf_op jit(solution)/shard_map/all_gather | solution.py:272
  38.2 27.7 %collective-permute-start.1 = (bf16[512,1024]{1,0:T(8,128)(2,1)}, bf16[512,1024]{1,0:T(8,128)(2,1)}, u32[]{:S(2)}, u32[]{:S(2)}) collective-permute-start(bf16[512,1024]{1,0:T(8,128)(2,1)} %get-tuple-element.103), channel_id=1, source_target_pairs={{0,2},{1,3},{2,0},{3,1},{4,6},{5,7},{6,4},{7,5},{8,10},{9,11},{10,... | collective-permute-start | bytes 3145736 | tf_op jit(solution)/shard_map/ppermute | solution.py:191
  38.7 28.8 %collective-permute-start.3 = (bf16[512,1024]{1,0:T(8,128)(2,1)}, bf16[512,1024]{1,0:T(8,128)(2,1)}, u32[]{:S(2)}, u32[]{:S(2)}) collective-permute-start(bf16[512,1024]{1,0:T(8,128)(2,1)} %get-tuple-element.103), channel_id=1, source_target_pairs={{0,1},{1,0},{2,3},{3,2},{4,5},{5,4},{6,7},{7,6},{8,9},{9,8},{10,11... | collective-permute-start | bytes 3145736 | tf_op jit(solution)/shard_map/ppermute | solution.py:191
  38.7 48.3 %collective-permute-start.7 = (bf16[512,1024]{1,0:T(8,128)(2,1)}, bf16[512,1024]{1,0:T(8,128)(2,1)S(1)}, u32[]{:S(2)}, u32[]{:S(2)}) collective-permute-start(bf16[512,1024]{1,0:T(8,128)(2,1)} %get-tuple-element.102), channel_id=1, source_target_pairs={{0,2},{1,3},{2,0},{3,1},{4,6},{5,7},{6,4},{7,5},{8,10},{9,11},{10,... | collective-permute-start | bytes 3145736 | tf_op jit(solution)/shard_map/ppermute | solution.py:191
  60.6 46.3 %collective-permute-start.2 = (bf16[512,1024]{1,0:T(8,128)(2,1)}, bf16[512,1024]{1,0:T(8,128)(2,1)}, u32[]{:S(2)}, u32[]{:S(2)}) collective-permute-start(bf16[512,1024]{1,0:T(8,128)(2,1)} %collective-permute-done), channel_id=1, source_target_pairs={{0,2},{1,3},{2,0},{3,1},{4,6},{5,7},{6,4},{7,5},{8,10},{9,11},{10,... | collective-permute-start | bytes 3145736 | tf_op jit(solution)/shard_map/ppermute | solution.py:191
  64.5 45.0 %collective-permute-start.4 = (bf16[512,1024]{1,0:T(8,128)(2,1)}, bf16[512,1024]{1,0:T(8,128)(2,1)S(1)}, u32[]{:S(2)}, u32[]{:S(2)}) collective-permute-start(bf16[512,1024]{1,0:T(8,128)(2,1)} %collective-permute-done), channel_id=1, source_target_pairs={{0,1},{1,0},{2,3},{3,2},{4,5},{5,4},{6,7},{7,6},{8,9},{9,8},{10,11... | collective-permute-start | bytes 3145736 | tf_op jit(solution)/shard_map/ppermute | solution.py:191
  65.9 44.3 %collective-permute-start.8 = (bf16[512,1024]{1,0:T(8,128)(2,1)}, bf16[512,1024]{1,0:T(8,128)(2,1)S(1)}, u32[]{:S(2)}, u32[]{:S(2)}) collective-permute-start(bf16[512,1024]{1,0:T(8,128)(2,1)} %get-tuple-element.102), channel_id=1, source_target_pairs={{0,4},{4,0},{1,5},{5,1},{2,6},{6,2},{3,7},{7,3},{8,12},{12,8},{9,1... | collective-permute-start | bytes 3145736 | tf_op jit(solution)/shard_map/ppermute | solution.py:191
  67.5 42.8 %collective-permute-start.5 = (bf16[512,1024]{1,0:T(8,128)(2,1)}, bf16[512,1024]{1,0:T(8,128)(2,1)S(1)}, u32[]{:S(2)}, u32[]{:S(2)}) collective-permute-start(bf16[512,1024]{1,0:T(8,128)(2,1)} %collective-permute-done.1), channel_id=1, source_target_pairs={{0,1},{1,0},{2,3},{3,2},{4,5},{5,4},{6,7},{7,6},{8,9},{9,8},{10,11... | collective-permute-start | bytes 3145736 | tf_op jit(solution)/shard_map/ppermute | solution.py:191
  87.0 27.2 %collective-permute-start.9 = (bf16[512,1024]{1,0:T(8,128)(2,1)S(1)}, bf16[512,1024]{1,0:T(8,128)(2,1)S(1)}, u32[]{:S(2)}, u32[]{:S(2)}) collective-permute-start(bf16[512,1024]{1,0:T(8,128)(2,1)S(1)} %collective-permute-done.7), channel_id=1, source_target_pairs={{0,4},{4,0},{1,5},{5,1},{2,6},{6,2},{3,7},{7,3},{8,12},{12,8},{9,1... | collective-permute-start | bytes 3145736 | tf_op jit(solution)/shard_map/ppermute | solution.py:191
  118.8 34.3 %collective-permute-start.15 = (bf16[512,1024]{1,0:T(8,128)(2,1)S(1)}, bf16[512,1024]{1,0:T(8,128)(2,1)S(1)}, u32[]{:S(2)}, u32[]{:S(2)}) collective-permute-start(bf16[512,1024]{1,0:T(8,128)(2,1)S(1)} %get-tuple-element.101), channel_id=1, source_target_pairs={{0,2},{1,3},{2,0},{3,1},{4,6},{5,7},{6,4},{7,5},{8,10},{9,11},{10,... | collective-permute-start | bytes 3145736 | tf_op jit(solution)/shard_map/ppermute | solution.py:191
  119.4 34.2 %collective-permute-start.17 = (bf16[512,1024]{1,0:T(8,128)(2,1)S(1)}, bf16[512,1024]{1,0:T(8,128)(2,1)S(1)}, u32[]{:S(2)}, u32[]{:S(2)}) collective-permute-start(bf16[512,1024]{1,0:T(8,128)(2,1)S(1)} %get-tuple-element.101), channel_id=1, source_target_pairs={{0,1},{1,0},{2,3},{3,2},{4,5},{5,4},{6,7},{7,6},{8,9},{9,8},{10,11... | collective-permute-start | bytes 3145736 | tf_op jit(solution)/shard_map/ppermute | solution.py:191
  119.4 47.9 %collective-permute-start.21 = (bf16[512,1024]{1,0:T(8,128)(2,1)S(1)}, bf16[512,1024]{1,0:T(8,128)(2,1)S(1)}, u32[]{:S(2)}, u32[]{:S(2)}) collective-permute-start(bf16[512,1024]{1,0:T(8,128)(2,1)S(1)} %get-tuple-element.100), channel_id=1, source_target_pairs={{0,2},{1,3},{2,0},{3,1},{4,6},{5,7},{6,4},{7,5},{8,10},{9,11},{10,... | collective-permute-start | bytes 3145736 | tf_op jit(solution)/shard_map/ppermute | solution.py:191
  142.7 45.9 %collective-permute-start.16 = (bf16[512,1024]{1,0:T(8,128)(2,1)S(1)}, bf16[512,1024]{1,0:T(8,128)(2,1)S(1)}, u32[]{:S(2)}, u32[]{:S(2)}) collective-permute-start(bf16[512,1024]{1,0:T(8,128)(2,1)S(1)} %collective-permute-done.14), channel_id=1, source_target_pairs={{0,2},{1,3},{2,0},{3,1},{4,6},{5,7},{6,4},{7,5},{8,10},{9,11},{10,... | collective-permute-start | bytes 3145736 | tf_op jit(solution)/shard_map/ppermute | solution.py:191
  152.1 38.7 %collective-permute-start.18 = (bf16[512,1024]{1,0:T(8,128)(2,1)S(1)}, bf16[512,1024]{1,0:T(8,128)(2,1)S(1)}, u32[]{:S(2)}, u32[]{:S(2)}) collective-permute-start(bf16[512,1024]{1,0:T(8,128)(2,1)S(1)} %collective-permute-done.14), channel_id=1, source_target_pairs={{0,1},{1,0},{2,3},{3,2},{4,5},{5,4},{6,7},{7,6},{8,9},{9,8},{10,11... | collective-permute-start | bytes 3145736 | tf_op jit(solution)/shard_map/ppermute | solution.py:191
  153.1 39.2 %collective-permute-start.22 = (bf16[512,1024]{1,0:T(8,128)(2,1)S(1)}, bf16[512,1024]{1,0:T(8,128)(2,1)S(1)}, u32[]{:S(2)}, u32[]{:S(2)}) collective-permute-start(bf16[512,1024]{1,0:T(8,128)(2,1)S(1)} %get-tuple-element.100), channel_id=1, source_target_pairs={{0,4},{4,0},{1,5},{5,1},{2,6},{6,2},{3,7},{7,3},{8,12},{12,8},{9,1... | collective-permute-start | bytes 3145736 | tf_op jit(solution)/shard_map/ppermute | solution.py:191
  153.7 38.7 %collective-permute-start.19 = (bf16[512,1024]{1,0:T(8,128)(2,1)S(1)}, bf16[512,1024]{1,0:T(8,128)(2,1)S(1)}, u32[]{:S(2)}, u32[]{:S(2)}) collective-permute-start(bf16[512,1024]{1,0:T(8,128)(2,1)S(1)} %collective-permute-done.15), channel_id=1, source_target_pairs={{0,1},{1,0},{2,3},{3,2},{4,5},{5,4},{6,7},{7,6},{8,9},{9,8},{10,11... | collective-permute-start | bytes 3145736 | tf_op jit(solution)/shard_map/ppermute | solution.py:191
  167.3 33.9 %collective-permute-start.23 = (bf16[512,1024]{1,0:T(8,128)(2,1)S(1)}, bf16[512,1024]{1,0:T(8,128)(2,1)S(1)}, u32[]{:S(2)}, u32[]{:S(2)}) collective-permute-start(bf16[512,1024]{1,0:T(8,128)(2,1)S(1)} %collective-permute-done.21), channel_id=1, source_target_pairs={{0,4},{4,0},{1,5},{5,1},{2,6},{6,2},{3,7},{7,3},{8,12},{12,8},{9,1... | collective-permute-start | bytes 3145736 | tf_op jit(solution)/shard_map/ppermute | solution.py:191
  423.6 39.7 %collective-permute-start.29 = (bf16[512,1024]{1,0:T(8,128)(2,1)S(1)}, bf16[512,1024]{1,0:T(8,128)(2,1)S(1)}, u32[]{:S(2)}, u32[]{:S(2)}) collective-permute-start(bf16[512,1024]{1,0:T(8,128)(2,1)S(1)} %dynamic-slice_bitcast_fusion.18), channel_id=1, source_target_pairs={{0,4},{4,0},{1,5},{5,1},{2,6},{6,2},{3,7},{7,3},{8,12},{12,8},{9,1... | collective-permute-start | bytes 3145736 | tf_op jit(solution)/shard_map/ppermute | solution.py:191
  442.8 44.7 %collective-permute-start.33 = (bf16[512,1024]{1,0:T(8,128)(2,1)S(1)}, bf16[512,1024]{1,0:T(8,128)(2,1)S(1)}, u32[]{:S(2)}, u32[]{:S(2)}) collective-permute-start(bf16[512,1024]{1,0:T(8,128)(2,1)S(1)} %get-tuple-element.98), channel_id=1, source_target_pairs={{0,2},{1,3},{2,0},{3,1},{4,6},{5,7},{6,4},{7,5},{8,10},{9,11},{10,... | collective-permute-start | bytes 3145736 | tf_op jit(solution)/shard_map/ppermute | solution.py:191
  443.8 43.7 %collective-permute-start.35 = (bf16[512,1024]{1,0:T(8,128)(2,1)S(1)}, bf16[512,1024]{1,0:T(8,128)(2,1)S(1)}, u32[]{:S(2)}, u32[]{:S(2)}) collective-permute-start(bf16[512,1024]{1,0:T(8,128)(2,1)S(1)} %fusion.100), channel_id=1, source_target_pairs={{0,4},{4,0},{1,5},{5,1},{2,6},{6,2},{3,7},{7,3},{8,12},{12,8},{9,1... | collective-permute-start | bytes 3145736 | tf_op jit(solution)/shard_map/ppermute | solution.py:191
  504.4 36.3 %collective-permute-start.37 = (bf16[512,1024]{1,0:T(8,128)(2,1)}, bf16[512,1024]{1,0:T(8,128)(2,1)}, u32[]{:S(2)}, u32[]{:S(2)}) collective-permute-start(bf16[512,1024]{1,0:T(8,128)(2,1)} %get-tuple-element.97), channel_id=1, source_target_pairs={{0,2},{1,3},{2,0},{3,1},{4,6},{5,7},{6,4},{7,5},{8,10},{9,11},{10,... | collective-permute-start | bytes 3145736 | tf_op jit(solution)/shard_map/ppermute | solution.py:191
  505.9 36.3 %collective-permute-start.39 = (bf16[512,1024]{1,0:T(8,128)(2,1)}, bf16[512,1024]{1,0:T(8,128)(2,1)}, u32[]{:S(2)}, u32[]{:S(2)}) collective-permute-start(bf16[512,1024]{1,0:T(8,128)(2,1)} %get-tuple-element.97), channel_id=1, source_target_pairs={{0,1},{1,0},{2,3},{3,2},{4,5},{5,4},{6,7},{7,6},{8,9},{9,8},{10,11... | collective-permute-start | bytes 3145736 | tf_op jit(solution)/shard_map/ppermute | solution.py:191
  505.9 47.3 %collective-permute-start.43 = (bf16[512,1024]{1,0:T(8,128)(2,1)}, bf16[512,1024]{1,0:T(8,128)(2,1)S(1)}, u32[]{:S(2)}, u32[]{:S(2)}) collective-permute-start(bf16[512,1024]{1,0:T(8,128)(2,1)} %get-tuple-element.96), channel_id=1, source_target_pairs={{0,2},{1,3},{2,0},{3,1},{4,6},{5,7},{6,4},{7,5},{8,10},{9,11},{10,... | collective-permute-start | bytes 3145736 | tf_op jit(solution)/shard_map/ppermute | solution.py:191
  527.9 46.0 %collective-permute-start.38 = (bf16[512,1024]{1,0:T(8,128)(2,1)}, bf16[512,1024]{1,0:T(8,128)(2,1)}, u32[]{:S(2)}, u32[]{:S(2)}) collective-permute-start(bf16[512,1024]{1,0:T(8,128)(2,1)} %collective-permute-done.36), channel_id=1, source_target_pairs={{0,2},{1,3},{2,0},{3,1},{4,6},{5,7},{6,4},{7,5},{8,10},{9,11},{10,... | collective-permute-start | bytes 3145736 | tf_op jit(solution)/shard_map/ppermute | solution.py:191
  531.1 546.5 %reduce-scatter.5.cloned.1.call-start = ((), (), s32[]{:S(2)}) async-start(), calls=%async_computation.5 | async-start | bytes 14090240 | tf_op jit(solution)/shard_map/reduce_scatter | solution.py:268
  538.4 40.2 %collective-permute-start.40 = (bf16[512,1024]{1,0:T(8,128)(2,1)}, bf16[512,1024]{1,0:T(8,128)(2,1)S(1)}, u32[]{:S(2)}, u32[]{:S(2)}) collective-permute-start(bf16[512,1024]{1,0:T(8,128)(2,1)} %collective-permute-done.36), channel_id=1, source_target_pairs={{0,1},{1,0},{2,3},{3,2},{4,5},{5,4},{6,7},{7,6},{8,9},{9,8},{10,11... | collective-permute-start | bytes 3145736 | tf_op jit(solution)/shard_map/ppermute | solution.py:191
  540.7 39.5 %collective-permute-start.44 = (bf16[512,1024]{1,0:T(8,128)(2,1)}, bf16[512,1024]{1,0:T(8,128)(2,1)S(1)}, u32[]{:S(2)}, u32[]{:S(2)}) collective-permute-start(bf16[512,1024]{1,0:T(8,128)(2,1)} %get-tuple-element.96), channel_id=1, source_target_pairs={{0,4},{4,0},{1,5},{5,1},{2,6},{6,2},{3,7},{7,3},{8,12},{12,8},{9,1... | collective-permute-start | bytes 3145736 | tf_op jit(solution)/shard_map/ppermute | solution.py:191
  542.2 38.0 %collective-permute-start.41 = (bf16[512,1024]{1,0:T(8,128)(2,1)}, bf16[512,1024]{1,0:T(8,128)(2,1)S(1)}, u32[]{:S(2)}, u32[]{:S(2)}) collective-permute-start(bf16[512,1024]{1,0:T(8,128)(2,1)} %collective-permute-done.37), channel_id=1, source_target_pairs={{0,1},{1,0},{2,3},{3,2},{4,5},{5,4},{6,7},{7,6},{8,9},{9,8},{10,11... | collective-permute-start | bytes 3145736 | tf_op jit(solution)/shard_map/ppermute | solution.py:191
  553.2 35.8 %collective-permute-start.45 = (bf16[512,1024]{1,0:T(8,128)(2,1)S(1)}, bf16[512,1024]{1,0:T(8,128)(2,1)S(1)}, u32[]{:S(2)}, u32[]{:S(2)}) collective-permute-start(bf16[512,1024]{1,0:T(8,128)(2,1)S(1)} %collective-permute-done.43), channel_id=1, source_target_pairs={{0,4},{4,0},{1,5},{5,1},{2,6},{6,2},{3,7},{7,3},{8,12},{12,8},{9,1... | collective-permute-start | bytes 3145736 | tf_op jit(solution)/shard_map/ppermute | solution.py:191
  793.1 766.4 %reduce-scatter.7.cloned.1.call-start = ((), (), s32[]{:S(2)}) async-start(), calls=%async_computation.6 | async-start | bytes 28180480 | tf_op jit(solution)/shard_map/reduce_scatter | solution.py:268
  1077.7 620.9 %reduce-scatter.9.cloned.1.call-start = ((), (), s32[]{:S(2)}) async-start(), calls=%async_computation.7 | async-start | bytes 15728640 | tf_op jit(solution)/shard_map/reduce_scatter | solution.py:268
  1102.4 35.8 %collective-permute-start.60 = (bf16[2048,1024]{1,0:T(8,128)(2,1)}, bf16[2048,1024]{1,0:T(8,128)(2,1)}, u32[]{:S(2)}, u32[]{:S(2)}) collective-permute-start(bf16[2048,1024]{1,0:T(8,128)(2,1)} %fusion.42), channel_id=1, source_target_pairs={{0,1},{1,0},{2,3},{3,2},{4,5},{5,4},{6,7},{7,6},{8,9},{9,8},{10,11... | collective-permute-start | bytes 12582920 | tf_op jit(solution)/shard_map/ppermute | solution.py:191
  1106.5 28.1 %collective-permute-start.56 = (bf16[512,1024]{1,0:T(8,128)(2,1)S(1)}, bf16[512,1024]{1,0:T(8,128)(2,1)}, u32[]{:S(2)}, u32[]{:S(2)}) collective-permute-start(bf16[512,1024]{1,0:T(8,128)(2,1)S(1)} %get-tuple-element.95), channel_id=1, source_target_pairs={{0,2},{1,3},{2,0},{3,1},{4,6},{5,7},{6,4},{7,5},{8,10},{9,11},{10,... | collective-permute-start | bytes 3145736 | tf_op jit(solution)/shard_map/ppermute | solution.py:191
  1124.6 37.0 %collective-permute-start.58 = (bf16[2048,1024]{1,0:T(8,128)(2,1)}, bf16[2048,1024]{1,0:T(8,128)(2,1)}, u32[]{:S(2)}, u32[]{:S(2)}) collective-permute-start(bf16[2048,1024]{1,0:T(8,128)(2,1)} %fusion.39), channel_id=1, source_target_pairs={{0,1},{1,0},{2,3},{3,2},{4,5},{5,4},{6,7},{7,6},{8,9},{9,8},{10,11... | collective-permute-start | bytes 12582920 | tf_op jit(solution)/shard_map/ppermute | solution.py:191
  1128.5 60.6 %collective-permute-start.51 = (bf16[512,1024]{1,0:T(8,128)(2,1)}, bf16[512,1024]{1,0:T(8,128)(2,1)}, u32[]{:S(2)}, u32[]{:S(2)}) collective-permute-start(bf16[512,1024]{1,0:T(8,128)(2,1)} %dynamic-slice_bitcast_fusion.14), channel_id=1, source_target_pairs={{0,4},{4,0},{1,5},{5,1},{2,6},{6,2},{3,7},{7,3},{8,12},{12,8},{9,1... | collective-permute-start | bytes 3145736 | tf_op jit(solution)/shard_map/ppermute | solution.py:191
  1130.9 72.7 %collective-permute-start.55 = (bf16[512,1024]{1,0:T(8,128)(2,1)S(1)}, bf16[512,1024]{1,0:T(8,128)(2,1)}, u32[]{:S(2)}, u32[]{:S(2)}) collective-permute-start(bf16[512,1024]{1,0:T(8,128)(2,1)S(1)} %get-tuple-element.94), channel_id=1, source_target_pairs={{0,2},{1,3},{2,0},{3,1},{4,6},{5,7},{6,4},{7,5},{8,10},{9,11},{10,... | collective-permute-start | bytes 3145736 | tf_op jit(solution)/shard_map/ppermute | solution.py:191
  1134.6 70.0 %collective-permute-start.54 = (bf16[512,1024]{1,0:T(8,128)(2,1)}, bf16[512,1024]{1,0:T(8,128)(2,1)}, u32[]{:S(2)}, u32[]{:S(2)}) collective-permute-start(bf16[512,1024]{1,0:T(8,128)(2,1)} %fusion.98), channel_id=1, source_target_pairs={{0,2},{1,3},{2,0},{3,1},{4,6},{5,7},{6,4},{7,5},{8,10},{9,11},{10,... | collective-permute-start | bytes 3145736 | tf_op jit(solution)/shard_map/ppermute | solution.py:191
  1161.6 39.1 %collective-permute-start.64 = (bf16[512,1024]{1,0:T(8,128)(2,1)}, bf16[512,1024]{1,0:T(8,128)(2,1)}, u32[]{:S(2)}, u32[]{:S(2)}) collective-permute-start(bf16[512,1024]{1,0:T(8,128)(2,1)} %get-tuple-element.93), channel_id=1, source_target_pairs={{0,2},{1,3},{2,0},{3,1},{4,6},{5,7},{6,4},{7,5},{8,10},{9,11},{10,... | collective-permute-start | bytes 3145736 | tf_op jit(solution)/shard_map/ppermute | solution.py:191
  1189.2 43.0 %collective-permute-start.59 = (bf16[512,1024]{1,0:T(8,128)(2,1)S(1)}, bf16[512,1024]{1,0:T(8,128)(2,1)}, u32[]{:S(2)}, u32[]{:S(2)}) collective-permute-start(bf16[512,1024]{1,0:T(8,128)(2,1)S(1)} %dynamic-slice_bitcast_fusion.10), channel_id=1, source_target_pairs={{0,4},{4,0},{1,5},{5,1},{2,6},{6,2},{3,7},{7,3},{8,12},{12,8},{9,1... | collective-permute-start | bytes 3145736 | tf_op jit(solution)/shard_map/ppermute | solution.py:191
  1200.7 31.4 %collective-permute-start.62 = (bf16[512,1024]{1,0:T(8,128)(2,1)S(1)}, bf16[512,1024]{1,0:T(8,128)(2,1)}, u32[]{:S(2)}, u32[]{:S(2)}) collective-permute-start(bf16[512,1024]{1,0:T(8,128)(2,1)S(1)} %fusion.94), channel_id=1, source_target_pairs={{0,2},{1,3},{2,0},{3,1},{4,6},{5,7},{6,4},{7,5},{8,10},{9,11},{10,... | collective-permute-start | bytes 3145736 | tf_op jit(solution)/shard_map/ppermute | solution.py:191
  1203.6 43.5 %collective-permute-start.63 = (bf16[512,1024]{1,0:T(8,128)(2,1)S(1)}, bf16[512,1024]{1,0:T(8,128)(2,1)S(1)}, u32[]{:S(2)}, u32[]{:S(2)}) collective-permute-start(bf16[512,1024]{1,0:T(8,128)(2,1)S(1)} %copy-done.33), channel_id=1, source_target_pairs={{0,2},{1,3},{2,0},{3,1},{4,6},{5,7},{6,4},{7,5},{8,10},{9,11},{10,... | collective-permute-start | bytes 3145736 | tf_op jit(solution)/shard_map/ppermute | solution.py:191
  1204.6 47.2 %collective-permute-start.65 = (bf16[512,1024]{1,0:T(8,128)(2,1)S(1)}, bf16[512,1024]{1,0:T(8,128)(2,1)}, u32[]{:S(2)}, u32[]{:S(2)}) collective-permute-start(bf16[512,1024]{1,0:T(8,128)(2,1)S(1)} %fusion.92), channel_id=1, source_target_pairs={{0,4},{4,0},{1,5},{5,1},{2,6},{6,2},{3,7},{7,3},{8,12},{12,8},{9,1... | collective-permute-start | bytes 3145736 | tf_op jit(solution)/shard_map/ppermute | solution.py:191
  1270.7 27.0 %collective-permute-start.67 = (bf16[512,1024]{1,0:T(8,128)(2,1)S(1)}, bf16[512,1024]{1,0:T(8,128)(2,1)S(1)}, u32[]{:S(2)}, u32[]{:S(2)}) collective-permute-start(bf16[512,1024]{1,0:T(8,128)(2,1)S(1)} %get-tuple-element.91), channel_id=1, source_target_pairs={{0,2},{1,3},{2,0},{3,1},{4,6},{5,7},{6,4},{7,5},{8,10},{9,11},{10,... | collective-permute-start | bytes 3145736 | tf_op jit(solution)/shard_map/ppermute | solution.py:191
  1272.2 27.0 %collective-permute-start.69 = (bf16[512,1024]{1,0:T(8,128)(2,1)S(1)}, bf16[512,1024]{1,0:T(8,128)(2,1)S(1)}, u32[]{:S(2)}, u32[]{:S(2)}) collective-permute-start(bf16[512,1024]{1,0:T(8,128)(2,1)S(1)} %get-tuple-element.91), channel_id=1, source_target_pairs={{0,1},{1,0},{2,3},{3,2},{4,5},{5,4},{6,7},{7,6},{8,9},{9,8},{10,11... | collective-permute-start | bytes 3145736 | tf_op jit(solution)/shard_map/ppermute | solution.py:191
  1272.2 47.1 %collective-permute-start.73 = (bf16[512,1024]{1,0:T(8,128)(2,1)S(1)}, bf16[512,1024]{1,0:T(8,128)(2,1)S(1)}, u32[]{:S(2)}, u32[]{:S(2)}) collective-permute-start(bf16[512,1024]{1,0:T(8,128)(2,1)S(1)} %get-tuple-element.90), channel_id=1, source_target_pairs={{0,2},{1,3},{2,0},{3,1},{4,6},{5,7},{6,4},{7,5},{8,10},{9,11},{10,... | collective-permute-start | bytes 3145736 | tf_op jit(solution)/shard_map/ppermute | solution.py:191
  1294.1 45.8 %collective-permute-start.68 = (bf16[512,1024]{1,0:T(8,128)(2,1)S(1)}, bf16[512,1024]{1,0:T(8,128)(2,1)S(1)}, u32[]{:S(2)}, u32[]{:S(2)}) collective-permute-start(bf16[512,1024]{1,0:T(8,128)(2,1)S(1)} %collective-permute-done.66), channel_id=1, source_target_pairs={{0,2},{1,3},{2,0},{3,1},{4,6},{5,7},{6,4},{7,5},{8,10},{9,11},{10,... | collective-permute-start | bytes 3145736 | tf_op jit(solution)/shard_map/ppermute | solution.py:191
  1297.5 42.7 %collective-permute-start.70 = (bf16[512,1024]{1,0:T(8,128)(2,1)S(1)}, bf16[512,1024]{1,0:T(8,128)(2,1)S(1)}, u32[]{:S(2)}, u32[]{:S(2)}) collective-permute-start(bf16[512,1024]{1,0:T(8,128)(2,1)S(1)} %collective-permute-done.66), channel_id=1, source_target_pairs={{0,1},{1,0},{2,3},{3,2},{4,5},{5,4},{6,7},{7,6},{8,9},{9,8},{10,11... | collective-permute-start | bytes 3145736 | tf_op jit(solution)/shard_map/ppermute | solution.py:191
  1297.7 43.2 %collective-permute-start.74 = (bf16[512,1024]{1,0:T(8,128)(2,1)S(1)}, bf16[512,1024]{1,0:T(8,128)(2,1)S(1)}, u32[]{:S(2)}, u32[]{:S(2)}) collective-permute-start(bf16[512,1024]{1,0:T(8,128)(2,1)S(1)} %get-tuple-element.90), channel_id=1, source_target_pairs={{0,4},{4,0},{1,5},{5,1},{2,6},{6,2},{3,7},{7,3},{8,12},{12,8},{9,1... | collective-permute-start | bytes 3145736 | tf_op jit(solution)/shard_map/ppermute | solution.py:191
  1299.2 41.8 %collective-permute-start.71 = (bf16[512,1024]{1,0:T(8,128)(2,1)S(1)}, bf16[512,1024]{1,0:T(8,128)(2,1)S(1)}, u32[]{:S(2)}, u32[]{:S(2)}) collective-permute-start(bf16[512,1024]{1,0:T(8,128)(2,1)S(1)} %collective-permute-done.67), channel_id=1, source_target_pairs={{0,1},{1,0},{2,3},{3,2},{4,5},{5,4},{6,7},{7,6},{8,9},{9,8},{10,11... | collective-permute-start | bytes 3145736 | tf_op jit(solution)/shard_map/ppermute | solution.py:191
  1442.5 306.9 %reduce-scatter.11.cloned.1.call-start = ((), (), s32[]{:S(2)}) async-start(), calls=%async_computation.8 | async-start | bytes 5242880 | tf_op jit(solution)/shard_map/reduce_scatter | solution.py:268
  1465.7 66.4 %collective-permute-start.82 = (bf16[2048,1024]{1,0:T(8,128)(2,1)}, bf16[2048,1024]{1,0:T(8,128)(2,1)}, u32[]{:S(2)}, u32[]{:S(2)}) collective-permute-start(bf16[2048,1024]{1,0:T(8,128)(2,1)} %convolution_convert_fusion.2), channel_id=1, source_target_pairs={{0,1},{1,0},{2,3},{3,2},{4,5},{5,4},{6,7},{7,6},{8,9},{9,8},{10,11... | collective-permute-start | bytes 12582920 | tf_op jit(solution)/shard_map/ppermute | solution.py:191
  1478.1 48.6 %collective-permute-start.94 = (bf16[4,512,512]{2,1,0:T(8,128)(2,1)S(1)}, bf16[4,512,512]{2,1,0:T(8,128)(2,1)}, u32[]{:S(2)}, u32[]{:S(2)}) collective-permute-start(bf16[4,512,512]{2,1,0:T(8,128)(2,1)S(1)} %constant_dynamic-slice_fusion), channel_id=1, source_target_pairs={{0,4},{4,0},{1,5},{5,1},{2,6},{6,2},{3,7},{7,3},{8,12},{12,8},{9,1... | collective-permute-start | bytes 6291464 | tf_op jit(solution)/shard_map/ppermute | solution.py:191
  1490.9 57.7 %collective-permute-start.80 = (bf16[2048,1024]{1,0:T(8,128)(2,1)}, bf16[2048,1024]{1,0:T(8,128)(2,1)}, u32[]{:S(2)}, u32[]{:S(2)}) collective-permute-start(bf16[2048,1024]{1,0:T(8,128)(2,1)} %convolution_convert_fusion.3), channel_id=1, source_target_pairs={{0,1},{1,0},{2,3},{3,2},{4,5},{5,4},{6,7},{7,6},{8,9},{9,8},{10,11... | collective-permute-start | bytes 12582920 | tf_op jit(solution)/shard_map/ppermute | solution.py:191
  1492.6 92.1 %collective-permute-start.92 = (bf16[1376,512]{1,0:T(8,128)(2,1)S(1)}, bf16[1376,512]{1,0:T(8,128)(2,1)}, u32[]{:S(2)}, u32[]{:S(2)}) collective-permute-start(bf16[1376,512]{1,0:T(8,128)(2,1)S(1)} %dynamic-slice_bitcast_fusion.2), channel_id=1, source_target_pairs={{0,4},{4,0},{1,5},{5,1},{2,6},{6,2},{3,7},{7,3},{8,12},{12,8},{9,1... | collective-permute-start | bytes 4227080 | tf_op jit(solution)/shard_map/ppermute | solution.py:191
  1544.6 34.8 %collective-permute-start.83 = (bf16[512,1024]{1,0:T(8,128)(2,1)}, bf16[512,1024]{1,0:T(8,128)(2,1)}, u32[]{:S(2)}, u32[]{:S(2)}) collective-permute-start(bf16[512,1024]{1,0:T(8,128)(2,1)} %dynamic-slice_bitcast_fusion.5), channel_id=1, source_target_pairs={{0,4},{4,0},{1,5},{5,1},{2,6},{6,2},{3,7},{7,3},{8,12},{12,8},{9,1... | collective-permute-start | bytes 3145736 | tf_op jit(solution)/shard_map/ppermute | solution.py:191
  1547.4 35.0 %collective-permute-start.86 = (bf16[512,1024]{1,0:T(8,128)(2,1)}, bf16[512,1024]{1,0:T(8,128)(2,1)}, u32[]{:S(2)}, u32[]{:S(2)}) collective-permute-start(bf16[512,1024]{1,0:T(8,128)(2,1)} %get-tuple-element.89), channel_id=1, source_target_pairs={{0,2},{1,3},{2,0},{3,1},{4,6},{5,7},{6,4},{7,5},{8,10},{9,11},{10,... | collective-permute-start | bytes 3145736 | tf_op jit(solution)/shard_map/ppermute | solution.py:191
  1561.7 123.6 %collective-permute-start.88 = (bf16[512,2752]{0,1:T(8,128)(2,1)S(1)}, bf16[512,2752]{0,1:T(8,128)(2,1)S(1)}, u32[]{:S(2)}, u32[]{:S(2)}) collective-permute-start(bf16[512,2752]{0,1:T(8,128)(2,1)S(1)} %dynamic-slice_bitcast_fusion.1), channel_id=1, source_target_pairs={{0,4},{4,0},{1,5},{5,1},{2,6},{6,2},{3,7},{7,3},{8,12},{12,8},{9,1... | collective-permute-start | bytes 8454152 | tf_op jit(solution)/shard_map/ppermute | solution.py:191
  1563.4 98.7 %collective-permute-start.81 = (bf16[512,1024]{1,0:T(8,128)(2,1)S(1)}, bf16[512,1024]{1,0:T(8,128)(2,1)S(1)}, u32[]{:S(2)}, u32[]{:S(2)}) collective-permute-start(bf16[512,1024]{1,0:T(8,128)(2,1)S(1)} %dynamic-slice_bitcast_fusion.6), channel_id=1, source_target_pairs={{0,4},{4,0},{1,5},{5,1},{2,6},{6,2},{3,7},{7,3},{8,12},{12,8},{9,1... | collective-permute-start | bytes 3145736 | tf_op jit(solution)/shard_map/ppermute | solution.py:191
  1579.4 83.3 %collective-permute-start.85 = (bf16[512,1024]{1,0:T(8,128)(2,1)S(1)}, bf16[512,1024]{1,0:T(8,128)(2,1)S(1)}, u32[]{:S(2)}, u32[]{:S(2)}) collective-permute-start(bf16[512,1024]{1,0:T(8,128)(2,1)S(1)} %copy-done.34), channel_id=1, source_target_pairs={{0,2},{1,3},{2,0},{3,1},{4,6},{5,7},{6,4},{7,5},{8,10},{9,11},{10,... | collective-permute-start | bytes 3145736 | tf_op jit(solution)/shard_map/ppermute | solution.py:191
  1582.4 79.7 %collective-permute-start.84 = (bf16[512,1024]{1,0:T(8,128)(2,1)S(1)}, bf16[512,1024]{1,0:T(8,128)(2,1)S(1)}, u32[]{:S(2)}, u32[]{:S(2)}) collective-permute-start(bf16[512,1024]{1,0:T(8,128)(2,1)S(1)} %fusion.90), channel_id=1, source_target_pairs={{0,2},{1,3},{2,0},{3,1},{4,6},{5,7},{6,4},{7,5},{8,10},{9,11},{10,... | collective-permute-start | bytes 3145736 | tf_op jit(solution)/shard_map/ppermute | solution.py:191
  1584.8 99.4 %collective-permute-start.87 = (bf16[512,1024]{1,0:T(8,128)(2,1)S(1)}, bf16[512,1024]{1,0:T(8,128)(2,1)S(1)}, u32[]{:S(2)}, u32[]{:S(2)}) collective-permute-start(bf16[512,1024]{1,0:T(8,128)(2,1)S(1)} %fusion.88), channel_id=1, source_target_pairs={{0,4},{4,0},{1,5},{5,1},{2,6},{6,2},{3,7},{7,3},{8,12},{12,8},{9,1... | collective-permute-start | bytes 3145736 | tf_op jit(solution)/shard_map/ppermute | solution.py:191
  1701.2 36.2 %collective-permute-start.93 = (bf16[512,1536]{1,0:T(8,128)(2,1)}, bf16[512,1536]{1,0:T(8,128)(2,1)}, u32[]{:S(2)}, u32[]{:S(2)}) collective-permute-start(bf16[512,1536]{1,0:T(8,128)(2,1)} %constant_dynamic-slice_fusion.1), channel_id=1, source_target_pairs={{0,4},{4,0},{1,5},{5,1},{2,6},{6,2},{3,7},{7,3},{8,12},{12,8},{9,1... | collective-permute-start | bytes 4718600 | tf_op jit(solution)/shard_map/ppermute | solution.py:191
  (106 other events, 1362.0 us)
Sparse Core Ops, SparseCore 0:
  16.2 289.4 all-gather.7
  307.8 380.7 all-gather.5
  690.7 195.1 all-gather.9
  888.7 188.8 reduce-scatter.4
  1079.9 373.3 reduce-scatter.6
  1455.4 213.5 reduce-scatter.8
  1671.3 78.1 reduce-scatter.10
